TPU v7x, 32 devices: a whole 2x2x4 slice. The times are simulated.
32 devices in a mesh: seq: 8 (over z, y), head: 4 (over x, core).
Axes of the slice: x: 2, y: 2, z: 4, core: 2. Of those that a mesh axis runs over, the one named last changes fastest.
Arguments:
- tokens: bfloat16 [8192, 1024], P('seq'), may hold values from -6 to 6
- w_query: bfloat16 [1024, 1024], P(None, 'head'), may hold values from -0.375 to 0.375
- w_key: bfloat16 [1024, 1024], P(None, 'head'), may hold values from -0.1875 to 0.1875
- w_value: bfloat16 [1024, 1024], P(None, 'head'), may hold values from -0.1875 to 0.1875
- w_out: bfloat16 [1024, 1024], P(None, 'head'), may hold values from -0.1875 to 0.1875
- level_mix: float32 [4, 16], P(None, 'head'), may hold values from 0.25 to 2
- fine_blocks: int32 [64, 4], P('seq'), may hold values from 0 to 15, as said below
- order: int32 [8, 1024], P('seq'), may hold values from 0 to 1023, each once within a row
- mask_ids: int32 [8, 512], P('seq'), may hold values from 0 to 1023, as said below
Outputs:
- layer_out: bfloat16 [8192, 1024], P('seq', 'head')
Inputs may be any that keep to these rules, and one draw needn't show every extreme that they name: `fine_blocks`: row g names 4 distinct blocks of a window of 16 blocks: ids below 8 stand for the previous time shard's blocks, ids from 8 up for the query block's own shard's blocks, and the first entry is always the query block's own block. `order`: each row is a permutation of the positions of one time shard. `mask_ids`: each row lists exactly 512 distinct positions of its time shard.
All inputs are finite; a program needn't handle non-finite values.
Results may differ from a plain program's by a relative error of at most 0.0098.
Values may be sent and summed in bfloat16 or wider, within the bound.
No kernel may reach another device: no remote copies, remote signals or barrier semaphores. Data moves between devices by JAX's collectives and lax.ppermute only.
A program may use at most 64 MiB of HBM per device.

v0:
```python
import math

import jax
import jax.numpy as jnp
from jax import lax
from jax.sharding import PartitionSpec as P

FBLK = 128
FINE_K = 4
POOL1 = 8


def from_behind(block, axis, distance):
    devices = range(lax.axis_size(axis))
    route = [(i - distance, i) for i in devices if i - distance in devices]
    return lax.ppermute(block, axis, route)


def with_halo(block, sides, width):
    for axis, dim in sides:
        count = lax.axis_size(axis)
        forward = [(i, i + 1) for i in range(count - 1)]
        backward = [(target, source) for source, target in forward]
        low = lax.ppermute(
            lax.slice_in_dim(block, block.shape[dim] - width, None, axis=dim), axis, forward
        )
        high = lax.ppermute(lax.slice_in_dim(block, 0, width, axis=dim), axis, backward)
        block = jnp.concatenate([low, block, high], axis=dim)
    return block


def summarize(key_sums, value_sums, counts):
    factor = 1.0 / jnp.sqrt(jnp.maximum(counts, 1.0))
    return (
        (key_sums * factor[:, None]).astype(jnp.bfloat16),
        (value_sums * factor[:, None]).astype(jnp.bfloat16),
    )


def coarser(key_sums, value_sums, counts):
    groups = key_sums.shape[0] // POOL1
    return (
        jnp.sum(key_sums.reshape(groups, POOL1, -1), axis=1),
        jnp.sum(value_sums.reshape(groups, POOL1, -1), axis=1),
        jnp.sum(counts.reshape(groups, POOL1), axis=1),
    )


def level_scores(queries, key_rows, scaling):
    return (
        jnp.einsum("qhd,khd->hqk", queries, key_rows, preferred_element_type=jnp.float32) * scaling
    )


def weighted_terms(scores, top, value_rows):
    weights = jnp.exp(scores - top[:, :, None])
    numerator = jnp.einsum(
        "hqk,khd->qhd", weights.astype(jnp.bfloat16), value_rows, preferred_element_type=jnp.float32
    )
    return (numerator, jnp.sum(weights, axis=2))


def coarse_level(queries, key_rows, value_rows, scaling):
    scores = level_scores(queries, key_rows, scaling)
    numerator, denominator = weighted_terms(scores, jnp.max(scores, axis=2), value_rows)
    return normalized(numerator, denominator)


def normalized(numerator, denominator):
    return numerator / jnp.transpose(denominator)[:, :, None]


def local(tokens, w_query, w_key, w_value, w_out, level_mix, fine_blocks, order, mask_ids):
    tok_rows, model_width = tokens.shape
    slab_count = lax.axis_size("seq")
    piece_rows = tok_rows // slab_count
    group_width = w_query.shape[1]
    heads_local = level_mix.shape[1]
    head_dim = group_width // heads_local
    blocks_local = tok_rows // FBLK
    scaling = 1.0 / math.sqrt(head_dim)
    joined = jnp.concatenate([w_query, w_key, w_value], axis=1)
    split_rows = tokens.reshape(slab_count, piece_rows, model_width)
    exchanged = jnp.einsum(
        "spd,dc->spc",
        lax.all_to_all(split_rows, "seq", split_axis=0, concat_axis=0, tiled=True),
        joined,
        preferred_element_type=jnp.float32,
    ).astype(jnp.bfloat16)
    projected = jnp.take(exchanged.reshape(tok_rows, 3 * group_width), order[0], axis=0)
    queries = projected[:, :group_width]
    key_rows = projected[:, group_width : 2 * group_width]
    value_rows = projected[:, 2 * group_width :]
    positions = jnp.arange(tok_rows, dtype=jnp.int32)
    masked_here = jnp.any(mask_ids[0][:, None] == positions[None, :], axis=0)
    visible = jnp.where(masked_here, 0.0, 1.0).astype(jnp.float32)
    visible_half = visible.astype(jnp.bfloat16)
    prev_keys, prev_values, prev_visible = from_behind(
        (key_rows, value_rows, visible_half), "seq", 1
    )
    prev_visible = prev_visible.astype(jnp.float32)
    window_keys = jnp.concatenate([prev_keys, key_rows], axis=0).reshape(
        2 * blocks_local, FBLK, heads_local, head_dim
    )
    window_values = jnp.concatenate([prev_values, value_rows], axis=0).reshape(
        2 * blocks_local, FBLK, heads_local, head_dim
    )
    window_visible = jnp.concatenate([prev_visible, visible], axis=0).reshape(
        2 * blocks_local, FBLK
    )
    chosen_keys = window_keys[fine_blocks].reshape(
        blocks_local, FINE_K * FBLK, heads_local, head_dim
    )
    chosen_values = window_values[fine_blocks].reshape(
        blocks_local, FINE_K * FBLK, heads_local, head_dim
    )
    selected_visible = window_visible[fine_blocks].reshape(blocks_local, FINE_K * FBLK)
    own_block = fine_blocks == (blocks_local + jnp.arange(blocks_local, dtype=jnp.int32))[:, None]
    inside = jnp.arange(FBLK, dtype=jnp.int32)
    same_row = inside[:, None] == inside[None, :]
    is_self = (own_block[:, None, :, None] & same_row[None, :, None, :]).reshape(
        blocks_local, FBLK, FINE_K * FBLK
    )
    allowed = is_self | (selected_visible[:, None, :] > 0.5)
    block_queries = queries.reshape(blocks_local, FBLK, heads_local, head_dim)
    scores = (
        jnp.einsum(
            "bqhd,bkhd->bhqk", block_queries, chosen_keys, preferred_element_type=jnp.float32
        )
        * scaling
    )
    top = jnp.max(jnp.where(allowed[:, None], scores, -jnp.inf), axis=3, keepdims=True)
    weights = jnp.where(allowed[:, None], jnp.exp(scores - top), 0.0)
    numerator = jnp.einsum(
        "bhqk,bkhd->bqhd",
        weights.astype(jnp.bfloat16),
        chosen_values,
        preferred_element_type=jnp.float32,
    )
    denominator = jnp.transpose(jnp.sum(weights, axis=3), (0, 2, 1))
    fine_out = (numerator / denominator[..., None]).reshape(tok_rows, heads_local, head_dim)
    flat_queries = queries.reshape(tok_rows, heads_local, head_dim)
    groups_one = tok_rows // POOL1
    masked_keys = key_rows * visible_half[:, None]
    hidden_value_rows = value_rows * visible_half[:, None]
    key_one = jnp.sum(
        masked_keys.reshape(groups_one, POOL1, group_width), axis=1, dtype=jnp.float32
    )
    value_one = jnp.sum(
        hidden_value_rows.reshape(groups_one, POOL1, group_width), axis=1, dtype=jnp.float32
    )
    count_one = jnp.sum(visible.reshape(groups_one, POOL1), axis=1)
    key_two, value_two, count_two = coarser(key_one, value_one, count_one)
    key_three, value_three, count_three = coarser(key_two, value_two, count_two)
    near_keys, near_values = summarize(key_one, value_one, count_one)
    mid_keys, mid_values = summarize(key_two, value_two, count_two)
    far_keys, far_values = summarize(key_three, value_three, count_three)
    near_out = coarse_level(
        flat_queries,
        near_keys.reshape(-1, heads_local, head_dim),
        near_values.reshape(-1, heads_local, head_dim),
        scaling,
    )
    stacked = jnp.stack([mid_keys, mid_values])
    widened = with_halo(stacked, (("seq", 1),), mid_keys.shape[0])
    mid_out = coarse_level(
        flat_queries,
        widened[0].reshape(-1, heads_local, head_dim),
        widened[1].reshape(-1, heads_local, head_dim),
        scaling,
    )
    start_sums = (
        jnp.zeros((tok_rows, heads_local, head_dim), jnp.float32),
        jnp.zeros((heads_local, tok_rows), jnp.float32),
        jnp.full((heads_local, tok_rows), -1e30, jnp.float32),
    )
    piece_scores = level_scores(
        flat_queries,
        lax.all_gather(far_keys, "seq", axis=0, tiled=True).reshape(-1, heads_local, head_dim),
        scaling,
    )
    new_top = jnp.maximum(start_sums[2], jnp.max(piece_scores, axis=2))
    more_num, more_den = weighted_terms(
        piece_scores,
        new_top,
        lax.all_gather(far_values, "seq", axis=0, tiled=True).reshape(-1, heads_local, head_dim),
    )
    blended = (
        level_mix[0][None, :, None] * fine_out
        + level_mix[1][None, :, None] * near_out
        + level_mix[2][None, :, None] * mid_out
        + level_mix[3][None, :, None] * normalized(more_num, more_den)
    )
    attended = blended.reshape(tok_rows, group_width).astype(jnp.bfloat16)
    layer_sum = jnp.dot(
        lax.all_gather(attended, "head", axis=1, tiled=True),
        w_out,
        preferred_element_type=jnp.float32,
    )
    return layer_sum.astype(jnp.bfloat16)


def solution(mesh):
    placed = (
        P("seq", None),
        P(None, "head"),
        P(None, "head"),
        P(None, "head"),
        P(None, "head"),
        P(None, "head"),
        P("seq", None),
        P("seq", None),
        P("seq", None),
    )
    return jax.shard_map(
        local, mesh=mesh, in_specs=placed, out_specs=P("seq", "head"), check_vma=False
    )
```

profile of v0, /device:TPU:0, one launch (start us, length us, event | category | flops | bytes accessed | tf_op | source)
XLA Modules:
  0.0 207.1 jit_solution(17218822086034012465)
XLA Ops:
  6.6 7.4 %all-to-all-start = ((bf16[8,128,1024]{2,1,0:T(8,128)(2,1)}), bf16[8,128,1024]{2,1,0:T(8,128)(2,1)}, u32[]{:S(2)}, u32[]{:S(2)}) async-start(bf16[8,128,1024]{2,1,0:T(8,128)(2,1)} %bitcast.122), calls=%async_computation | async-start | bytes 4194304 | tf_op jit(solution)/shard_map/all_to_all | solution.py:86
  14.4 3.9 %collective-permute-start.1 = (bf16[1024]{0:T(1024)(128)(2,1)S(1)}, bf16[1024]{0:T(1024)(128)(2,1)S(1)}, u32[]{:S(2)}, u32[]{:S(2)}) collective-permute-start(bf16[1024]{0:T(1024)(128)(2,1)S(1)} %get-tuple-element.17), channel_id=1, source_target_pairs={{0,4},{4,8},{8,12},{12,16},{16,20},{20,24},{24,28},{1,5},{5,9},{9,... | collective-permute-start | bytes 6152 | tf_op jit(solution)/shard_map/ppermute | solution.py:16
  19.5 11.7 %collective-permute-done.1 = bf16[1024]{0:T(1024)(128)(2,1)S(1)} collective-permute-done((bf16[1024]{0:T(1024)(128)(2,1)S(1)}, bf16[1024]{0:T(1024)(128)(2,1)S(1)}, u32[]{:S(2)}, u32[]{:S(2)}) %collective-permute-start.1) | collective-permute-done | bytes 2080 | tf_op jit(solution)/shard_map/ppermute | solution.py:16
  32.9 29.5 %all-to-all-done = bf16[8,128,1024]{2,1,0:T(8,128)(2,1)} async-done(((bf16[8,128,1024]{2,1,0:T(8,128)(2,1)}), bf16[8,128,1024]{2,1,0:T(8,128)(2,1)}, u32[]{:S(2)}, u32[]{:S(2)}) %all-to-all-start) | async-done | bytes 2097184 | tf_op jit(solution)/shard_map/all_to_all | solution.py:86
  62.3 3.6 %convolution_convert_fusion = bf16[768,8,128]{0,2,1:T(8,128)(2,1)S(1)} fusion(bf16[8,128,1024]{2,1,0:T(8,128)(2,1)} %all-to-all-done, bf16[1024,256]{1,0:T(8,128)(2,1)S(1)} %copy-done.8, bf16[1024,256]{1,0:T(8,128)(2,1)S(1)} %copy-done.9, bf16[1024,256]{1,0:T(8,128)(2,1)} %param.10), kind=kOutput, calls=%fused_computation.24 | convolution fusion | flops 1616117760 | bytes 5242880 | tf_op jit(solution)/shard_map/spd,dc->spc/dot_general | solution.py:84
  65.9 5.2 %gather_fusion = bf16[1024,768]{1,0:T(8,128)(2,1)} fusion(bf16[1024,768]{1,0:T(8,128)(2,1)S(1)} %bitcast.118, s32[1024]{0:T(1024)S(1)} %broadcast_clamp_fusion), kind=kCustom, calls=%fused_computation | custom fusion | bytes 3149824 | tf_op jit(solution)/shard_map/jit(_take)/gather | solution.py:90
  71.2 1.6 broadcast_select_fusion
  73.6 3.4 %collective-permute-start.3 = (bf16[2,16,256]{2,1,0:T(8,128)(2,1)S(1)}, bf16[2,16,256]{2,1,0:T(8,128)(2,1)S(1)}, u32[]{:S(2)}, u32[]{:S(2)}) collective-permute-start(bf16[2,16,256]{2,1,0:T(8,128)(2,1)S(1)} %pad_maximum_fusion.3), channel_id=1, source_target_pairs={{0,4},{4,8},{8,12},{12,16},{16,20},{20,24},{24,28},{1,5},{5,9},{9,... | collective-permute-start | bytes 49160 | tf_op jit(solution)/shard_map/ppermute | solution.py:24
  77.0 1.3 collective-permute-start.4
  78.8 19.8 %all-gather.1 = bf16[8,2,256]{2,1,0:T(2,128)(2,1)S(1)} all-gather(bf16[1,2,256]{2,1,0:T(2,128)(2,1)S(1)} %get-tuple-element.22), channel_id=1, replica_groups=mesh['seq'=8,'head'=4] {'seq'}, dimensions={0}, use_global_device_ids=true | all-gather | bytes 9216 | tf_op jit(solution)/shard_map/all_gather | solution.py:179
  99.0 16.3 %all-gather = bf16[8,2,256]{2,1,0:T(2,128)(2,1)S(1)} all-gather(bf16[1,2,256]{2,1,0:T(2,128)(2,1)S(1)} %get-tuple-element.21), channel_id=1, replica_groups=mesh['seq'=8,'head'=4] {'seq'}, dimensions={0}, use_global_device_ids=true | all-gather | bytes 9216 | tf_op jit(solution)/shard_map/all_gather | solution.py:186
  115.3 4.8 %collective-permute-start.2 = (bf16[1024,256]{1,0:T(8,128)(2,1)S(1)}, bf16[1024,256]{1,0:T(8,128)(2,1)}, u32[]{:S(2)}, u32[]{:S(2)}) collective-permute-start(bf16[1024,256]{1,0:T(8,128)(2,1)S(1)} %get-tuple-element.8), channel_id=1, source_target_pairs={{0,4},{4,8},{8,12},{12,16},{16,20},{20,24},{24,28},{1,5},{5,9},{9,... | collective-permute-start | bytes 1572872 | tf_op jit(solution)/shard_map/ppermute | solution.py:16
  120.7 1.7 fusion.26
  122.9 1.4 reshape.311
  124.3 2.1 %collective-permute-start = (bf16[1024,256]{1,0:T(8,128)(2,1)S(1)}, bf16[1024,256]{1,0:T(8,128)(2,1)}, u32[]{:S(2)}, u32[]{:S(2)}) collective-permute-start(bf16[1024,256]{1,0:T(8,128)(2,1)S(1)} %get-tuple-element.7), channel_id=1, source_target_pairs={{0,4},{4,8},{8,12},{12,16},{16,20},{20,24},{24,28},{1,5},{5,9},{9,... | collective-permute-start | bytes 1572872 | tf_op jit(solution)/shard_map/ppermute | solution.py:16
  127.1 1.3 fusion.33
  130.4 2.1 reshape.312
  132.5 2.8 %copy.75 = bf16[16,128,4,64]{1,3,2,0:T(8,128)(2,1)S(1)} copy(bf16[16,128,4,64]{3,2,1,0:T(4,128)(2,1)} %reshape.312) | data formatting | bytes 2097152 | tf_op jit(solution)/shard_map/reshape | solution.py:102
  135.3 2.2 %gather_fusion.3 = bf16[32,128,4,64]{1,3,2,0:T(8,128)(2,1)} fusion(bf16[16,128,4,64]{1,3,2,0:T(8,128)(2,1)S(1)} %copy.75, s32[1024]{0:T(1024)S(1)} %pad_clamp_fusion), kind=kCustom, calls=%fused_computation.3 | custom fusion | bytes 4194432 | tf_op jit(solution)/shard_map/gather | solution.py:111
  137.5 2.9 %copy.76 = bf16[32,128,4,64]{1,0,3,2:T(8,128)(2,1)S(1)} copy(bf16[32,128,4,64]{1,3,2,0:T(8,128)(2,1)} %gather_fusion.3) | data formatting | bytes 4194304 | tf_op jit(solution)/shard_map/gather | solution.py:111
  140.4 2.6 %reshape.246 = bf16[8,512,4,64]{1,0,3,2:T(8,128)(2,1)} reshape(bf16[32,128,4,64]{1,0,3,2:T(8,128)(2,1)S(1)} %copy.76) | data formatting | bytes 4194304 | tf_op jit(solution)/shard_map/reshape | solution.py:111
  144.1 1.8 reshape.310
  145.9 2.8 %copy.71 = bf16[16,128,4,64]{1,3,2,0:T(8,128)(2,1)S(1)} copy(bf16[16,128,4,64]{3,2,1,0:T(4,128)(2,1)} %reshape.310) | data formatting | bytes 2097152 | tf_op jit(solution)/shard_map/reshape | solution.py:105
  148.8 2.2 %gather_fusion.1 = bf16[32,128,4,64]{1,3,2,0:T(8,128)(2,1)} fusion(bf16[16,128,4,64]{1,3,2,0:T(8,128)(2,1)S(1)} %copy.71, s32[1024]{0:T(1024)S(1)} %pad_clamp_fusion), kind=kCustom, calls=%fused_computation.1 | custom fusion | bytes 4194432 | tf_op jit(solution)/shard_map/gather | solution.py:114
  150.9 4.2 %copy.72 = bf16[32,128,4,64]{1,0,3,2:T(8,128)(2,1)} copy(bf16[32,128,4,64]{1,3,2,0:T(8,128)(2,1)} %gather_fusion.1) | data formatting | bytes 4194304 | tf_op jit(solution)/shard_map/gather | solution.py:114
  155.2 4.5 %reshape.243 = bf16[8,512,4,64]{1,0,3,2:T(8,128)(2,1)} reshape(bf16[32,128,4,64]{1,0,3,2:T(8,128)(2,1)} %copy.72) | data formatting | bytes 4194304 | tf_op jit(solution)/shard_map/reshape | solution.py:114
  159.7 3.0 %fusion.11 = f32[8,4,128,512]{3,2,1,0:T(8,128)S(1)} fusion(bf16[8,512,4,64]{1,0,3,2:T(8,128)(2,1)S(1)} %copy-done.1, bf16[8,128,4,64]{3,2,1,0:T(4,128)(2,1)} %reshape.311), kind=kOutput, calls=%fused_computation.15 | convolution fusion | flops 268435456 | bytes 11010048 | tf_op jit(solution)/shard_map/bqhd,bkhd->bhqk/dot_general | solution.py:127
  162.7 6.0 %fusion.76 = (f32[8,4,128]{2,1,0:T(4,128)S(1)}, bf16[8,4,128,512]{3,2,1,0:T(8,128)(2,1)}) fusion(f32[8,4,128,512]{3,2,1,0:T(8,128)S(1)} %fusion.11, pred[8,128,512]{2,1,0:T(8,128)(4,1)} %and_or_fusion), kind=kOutput, calls=%fused_computation.122 | output fusion | flops 14680575 | bytes 13123584 | tf_op jit(solution)/shard_map/sub | solution.py:133
  168.7 4.0 %fusion.40 = f32[8,4,8,8,128]{4,3,2,1,0:T(8,128)S(1)} fusion(bf16[8,4,128,512]{3,2,1,0:T(8,128)(2,1)} %get-tuple-element.28, bf16[8,512,4,64]{1,0,3,2:T(8,128)(2,1)S(1)} %copy-done.4, f32[8,128,4]{1,2,0:T(4,128)S(1)} %bitcast.134), kind=kOutput, calls=%fused_computation.49 | convolution fusion | flops 268697600 | bytes 7356416 | tf_op jit(solution)/shard_map/bhqk,bkhd->bqhd/dot_general | solution.py:134
  172.7 1.5 fusion.34
  174.2 22.9 %all-gather.4.cloned.1.call-done = bf16[1024,1024]{0,1:T(8,128)(2,1)} async-done(((bf16[1024,256]{0,1:T(8,128)(2,1)}), bf16[1024,1024]{0,1:T(8,128)(2,1)}) %all-gather.4.cloned.1.call-update) | async-done | bytes 2097168 | tf_op jit(solution)/shard_map/all_gather | solution.py:196
  197.1 3.1 %convolution_convert_fusion.1 = bf16[1024,256]{1,0:T(8,128)(2,1)} fusion(bf16[1024,1024]{0,1:T(8,128)(2,1)} %all-gather.4.cloned.1.call-done, bf16[1024,256]{1,0:T(8,128)(2,1)S(1)} %copy-done), kind=kOutput, calls=%fused_computation.45 | convolution fusion | flops 537133056 | bytes 3145728 | tf_op jit(solution)/shard_map/dot_general | solution.py:195
  (89 shorter events, 9.8 us)
Async XLA Ops:
  6.5 190.6 %copy-start = (bf16[1024,256]{1,0:T(8,128)(2,1)S(1)}, bf16[1024,256]{1,0:T(8,128)(2,1)}, u32[]{:S(2)}) copy-start(bf16[1024,256]{1,0:T(8,128)(2,1)} %param.13) | copy-start | bytes 1572868
  6.5 7.5 %copy-start.10 = (s32[1,512]{1,0:T(1,128)S(1)}, s32[1,512]{1,0:T(1,128)}, u32[]{:S(2)}) copy-start(s32[1,512]{1,0:T(1,128)} %param.17) | copy-start | bytes 6148
  6.5 12.4 %copy-start.6 = (s32[8,4]{0,1:T(4,128)S(1)}, s32[8,4]{0,1:T(4,128)}, u32[]{:S(2)}) copy-start(s32[8,4]{0,1:T(4,128)} %param.15) | copy-start | bytes 388
  6.5 12.6 %copy-start.7 = (f32[4,4]{1,0:T(4,128)S(1)}, f32[4,4]{1,0:T(4,128)}, u32[]{:S(2)}) copy-start(f32[4,4]{1,0:T(4,128)} %param.14) | copy-start | bytes 196
  6.5 12.7 %copy-start.5 = (s32[1,1024]{1,0:T(1,128)S(1)}, s32[1,1024]{1,0:T(1,128)}, u32[]{:S(2)}) copy-start(s32[1,1024]{1,0:T(1,128)} %param.16) | copy-start | bytes 12292
  6.5 55.8 %copy-start.8 = (bf16[1024,256]{1,0:T(8,128)(2,1)S(1)}, bf16[1024,256]{1,0:T(8,128)(2,1)}, u32[]{:S(2)}) copy-start(bf16[1024,256]{1,0:T(8,128)(2,1)} %param.12) | copy-start | bytes 1572868
  6.6 55.8 %copy-start.9 = (bf16[1024,256]{1,0:T(8,128)(2,1)S(1)}, bf16[1024,256]{1,0:T(8,128)(2,1)}, u32[]{:S(2)}) copy-start(bf16[1024,256]{1,0:T(8,128)(2,1)} %param.11) | copy-start | bytes 1572868
  6.6 55.8 %all-to-all-start = ((bf16[8,128,1024]{2,1,0:T(8,128)(2,1)}), bf16[8,128,1024]{2,1,0:T(8,128)(2,1)}, u32[]{:S(2)}, u32[]{:S(2)}) async-start(bf16[8,128,1024]{2,1,0:T(8,128)(2,1)} %bitcast.122), calls=%async_computation | async-start | bytes 4194304 | tf_op jit(solution)/shard_map/all_to_all | solution.py:86
  14.0 183.1 %all-gather.4.cloned.1.call-start = ((), (), s32[]{:S(2)}) async-start(), calls=%async_computation.1 | async-start | bytes 2621440 | tf_op jit(solution)/shard_map/all_gather | solution.py:196
  14.4 16.7 %collective-permute-start.1 = (bf16[1024]{0:T(1024)(128)(2,1)S(1)}, bf16[1024]{0:T(1024)(128)(2,1)S(1)}, u32[]{:S(2)}, u32[]{:S(2)}) collective-permute-start(bf16[1024]{0:T(1024)(128)(2,1)S(1)} %get-tuple-element.17), channel_id=1, source_target_pairs={{0,4},{4,8},{8,12},{12,16},{16,20},{20,24},{24,28},{1,5},{5,9},{9,... | collective-permute-start | bytes 6152 | tf_op jit(solution)/shard_map/ppermute | solution.py:16
  73.6 52.8 %collective-permute-start.3 = (bf16[2,16,256]{2,1,0:T(8,128)(2,1)S(1)}, bf16[2,16,256]{2,1,0:T(8,128)(2,1)S(1)}, u32[]{:S(2)}, u32[]{:S(2)}) collective-permute-start(bf16[2,16,256]{2,1,0:T(8,128)(2,1)S(1)} %pad_maximum_fusion.3), channel_id=1, source_target_pairs={{0,4},{4,8},{8,12},{12,16},{16,20},{20,24},{24,28},{1,5},{5,9},{9,... | collective-permute-start | bytes 49160 | tf_op jit(solution)/shard_map/ppermute | solution.py:24
  77.0 49.5 %collective-permute-start.4 = (bf16[2,16,256]{2,1,0:T(8,128)(2,1)S(1)}, bf16[2,16,256]{2,1,0:T(8,128)(2,1)S(1)}, u32[]{:S(2)}, u32[]{:S(2)}) collective-permute-start(bf16[2,16,256]{2,1,0:T(8,128)(2,1)S(1)} %pad_maximum_fusion.3), channel_id=1, source_target_pairs={{4,0},{8,4},{12,8},{16,12},{20,16},{24,20},{28,24},{5,1},{9,5},{13... | collective-permute-start | bytes 49160 | tf_op jit(solution)/shard_map/ppermute | solution.py:27
  115.3 14.0 %collective-permute-start.2 = (bf16[1024,256]{1,0:T(8,128)(2,1)S(1)}, bf16[1024,256]{1,0:T(8,128)(2,1)}, u32[]{:S(2)}, u32[]{:S(2)}) collective-permute-start(bf16[1024,256]{1,0:T(8,128)(2,1)S(1)} %get-tuple-element.8), channel_id=1, source_target_pairs={{0,4},{4,8},{8,12},{12,16},{16,20},{20,24},{24,28},{1,5},{5,9},{9,... | collective-permute-start | bytes 1572872 | tf_op jit(solution)/shard_map/ppermute | solution.py:16
  120.7 1.8 copy-start.2
  124.3 18.7 %collective-permute-start = (bf16[1024,256]{1,0:T(8,128)(2,1)S(1)}, bf16[1024,256]{1,0:T(8,128)(2,1)}, u32[]{:S(2)}, u32[]{:S(2)}) collective-permute-start(bf16[1024,256]{1,0:T(8,128)(2,1)S(1)} %get-tuple-element.7), channel_id=1, source_target_pairs={{0,4},{4,8},{8,12},{12,16},{16,20},{20,24},{24,28},{1,5},{5,9},{9,... | collective-permute-start | bytes 1572872 | tf_op jit(solution)/shard_map/ppermute | solution.py:16
  155.2 4.5 %copy-start.1 = (bf16[8,512,4,64]{1,0,3,2:T(8,128)(2,1)S(1)}, bf16[8,512,4,64]{1,0,3,2:T(8,128)(2,1)}, u32[]{:S(2)}) copy-start(bf16[8,512,4,64]{1,0,3,2:T(8,128)(2,1)} %reshape.246) | copy-start | bytes 6291460
  162.7 6.0 %copy-start.4 = (bf16[8,512,4,64]{1,0,3,2:T(8,128)(2,1)S(1)}, bf16[8,512,4,64]{1,0,3,2:T(8,128)(2,1)}, u32[]{:S(2)}) copy-start(bf16[8,512,4,64]{1,0,3,2:T(8,128)(2,1)} %reshape.243) | copy-start | bytes 6291460
  168.7 4.0 %copy-start.3 = (f32[4,1024,128]{1,2,0:T(8,128)S(1)}, f32[4,1024,128]{1,2,0:T(8,128)}, u32[]{:S(2)}) copy-start(f32[4,1024,128]{1,2,0:T(8,128)} %copy-done.2) | copy-start | bytes 6291460
  168.7 4.0 %copy-start.11 = (f32[1024,4,64]{0,2,1:T(8,128)S(1)}, f32[1024,4,64]{0,2,1:T(8,128)}, u32[]{:S(2)}) copy-start(f32[1024,4,64]{0,2,1:T(8,128)} %fusion.26) | copy-start | bytes 3145732
  168.7 4.0 %copy-start.12 = (f32[1024,4,64]{0,2,1:T(8,128)S(1)}, f32[1024,4,64]{0,2,1:T(8,128)}, u32[]{:S(2)}) copy-start(f32[1024,4,64]{0,2,1:T(8,128)} %fusion.33) | copy-start | bytes 3145732
Sparse Core Ops, SparseCore 0:
  174.4 22.7 all-gather.3
where the time goes:
time: 208 us; the launch traced here: 207 us
  waiting for transfers between devices  65 us (31%)
  local copies, waits for them, and re-layouts  36.9 us (18%)
  blocking collectives  36.1 us (17%)
  starting transfers between devices  22.9 us (11%)
  matrix products  19.2 us (9%)
  between operations  13.8 us (7%)
  other arithmetic  13.3 us (6%)
    all_to_all x1, waiting for transfers between devices, local(): lax.all_to_all(split_rows, 'seq', split_axis=0, concat_axis=0, tiled=True)  29.5 us
    all_gather x1, waiting for transfers between devices, local(): lax.all_gather(attended, 'head', axis=1, tiled=True)  22.9 us
    all_gather x1, blocking collectives, local(): lax.all_gather(far_keys, 'seq', axis=0, tiled=True)  19.8 us
    all_gather x1, blocking collectives, local(): lax.all_gather(far_values, 'seq', axis=0, tiled=True)  16.3 us
    ppermute x3, waiting for transfers between devices, from_behind(): return lax.ppermute(block, axis, route)  12.6 us
    ppermute x3, starting transfers between devices, from_behind(): return lax.ppermute(block, axis, route)  10.8 us
    all_to_all x1, starting transfers between devices, local(): lax.all_to_all(split_rows, 'seq', split_axis=0, concat_axis=0, tiled=True)  7.42 us
    gather x2, local copies, waits for them, and re-layouts, local(): window_values[fine_blocks]  6.4 us
  transfers between devices with their start and end apart: 7, of which 4 were waited for; matrix products, arithmetic and copies ran while one was open for 11% of the time, Pallas kernels for 0%

commit v1 on v0

v1 whole, which is shorter than its diff:
```python
import functools

import jax
import jax.numpy as jnp
from jax import lax
from jax.experimental import pallas as pl
from jax.experimental.pallas import tpu as pltpu
from jax.sharding import PartitionSpec as P

FBLK = 128
FINE_K = 4
POOL1 = 8
POOL2 = 64
POOL3 = 512
SUMM_ROWS = 32
BF = jnp.bfloat16
F32 = jnp.float32
HIDE = -1e30
VMEM_LIMIT = 56 * 1024 * 1024

X_PAIRS = [(0, 2), (2, 0), (1, 3), (3, 1)]
CORE_PAIRS = [(0, 1), (1, 0), (2, 3), (3, 2)]


def nn(a, b):
    return lax.dot_general(a, b, (((1,), (0,)), ((), ())), preferred_element_type=F32)


def nt(a, b):
    return lax.dot_general(a, b, (((1,), (1,)), ((), ())), preferred_element_type=F32)


def vmem_specs(count):
    return [pl.BlockSpec(memory_space=pltpu.VMEM)] * count


def over_head(block, pairs):
    return lax.ppermute(block, "head", pairs)


def exchange_tokens(tokens):
    tok_rows, width = tokens.shape
    slabs = lax.axis_size("seq")
    rows = tok_rows // slabs
    quarter = width // 4
    slab, head = lax.axis_index("seq"), lax.axis_index("head")
    split = tokens.reshape(slabs, rows, width)

    def columns(other):
        return lax.dynamic_slice_in_dim(split, (head ^ other) * quarter, quarter, axis=2)

    mine = columns(0)
    if slabs != 8:
        first = lax.all_to_all(mine, "seq", split_axis=0, concat_axis=0, tiled=True).reshape(
            tok_rows, quarter
        )
        third = over_head(first, X_PAIRS)
        second = over_head(first, CORE_PAIRS)
        fourth = over_head(third, CORE_PAIRS)
        return [(first, 0, 0), (third, 0, 1), (second, 0, 2), (fourth, 0, 3)], 0
    partner = columns(2)

    def to_peer(source, distance):
        block = lax.dynamic_index_in_dim(source, slab ^ distance, axis=0, keepdims=False)
        return lax.ppermute(block, "seq", [(i, i ^ distance) for i in range(slabs)])

    far = jnp.concatenate([to_peer(mine, d) for d in (7, 6, 5, 4)], axis=0)
    both = jnp.concatenate([mine, partner], axis=2)
    near = jnp.concatenate([to_peer(both, d) for d in (3, 2, 1)], axis=0)
    far_x = over_head(far, X_PAIRS)
    near_core = over_head(near, CORE_PAIRS)
    far_core = over_head(far, CORE_PAIRS)
    far_last = over_head(far_x, CORE_PAIRS)
    own = jnp.concatenate(
        [
            lax.dynamic_index_in_dim(part, slab, axis=0, keepdims=False)
            for part in (mine, partner, columns(1), columns(3))
        ],
        axis=1,
    )
    pieces = [(far, 0, 0), (far_x, 0, 1), (far_core, 0, 2), (far_last, 0, 3)]
    pieces += [(near, 4 * rows, 0), (near_core, 4 * rows, 2), (own, 7 * rows, 0)]
    return pieces, (slab ^ 7) * rows


def project_kernel(places, *refs):
    count = len(places)
    piece_refs, refs = refs[:count], refs[count:]
    wqv_ref, wk_ref, p_ref, pt_ref, ac_ref, fcol_ref, frow_ref = refs[:7]
    qt_ref, vt_ref, k_ref, nk_ref, nvt_ref, summ_ref, comp_ref, x_ref = refs[7:]
    quarter = x_ref.shape[1] // 4
    for piece, (row, column) in zip(piece_refs, places):
        height, width = piece.shape
        x_ref[row : row + height, column * quarter : column * quarter + width] = piece[...]
    group = wk_ref.shape[1]
    x = x_ref[...]
    qv = nt(wqv_ref[...], x).astype(BF)
    k0 = nn(x, wk_ref[...]).astype(BF)
    k = nn(p_ref[...], k0).astype(BF)
    k_ref[...] = k
    qvt = nn(qv, pt_ref[...]).astype(BF)
    qt_ref[...] = qvt[:group] * jnp.asarray(0.125, BF)
    vt = qvt[group:]
    vt_ref[...] = vt
    ac = ac_ref[...]
    near = nk_ref.shape[0]
    lead = near + SUMM_ROWS
    kl = nn(ac, k)
    vl = nt(vt, ac)
    kf = (kl[:lead] * fcol_ref[...]).astype(BF)
    vf = vl[:, :lead] * frow_ref[...]
    nk_ref[...] = kf[:near]
    nvt_ref[...] = vf[:, :near].astype(BF)
    summ_ref[:SUMM_ROWS] = kf[near:]
    summ_ref[SUMM_ROWS:] = jnp.transpose(vf[:, near:]).astype(BF)
    packed = kl.shape[0] - lead
    comp_ref[:packed] = kl[lead:].astype(BF)
    vc = vl[:, lead:].astype(BF)
    for part in range(packed // group):
        comp_ref[packed + part * group : packed + (part + 1) * group] = vc[
            :, part * group : (part + 1) * group
        ]


def attend_kernel(
    lists_ref, mix_ref, qt_ref, k_ref, vt_ref, comp_ref, e_ref, et_ref, bias_ref, nk_ref, nvt_ref,
    summ_ref, selk_ref, selv_ref, out_ref, kw_ref, vw_ref, kc_ref, vc_ref, q4_ref, p_ref,
):
    tok_rows, group = k_ref.shape
    heads = mix_ref.shape[1]
    width = group // heads
    fine = FINE_K * FBLK
    near = nk_ref.shape[0]
    mid_at = fine + near
    mid = 3 * (tok_rows // POOL2)
    far_at = mid_at + mid
    total = kc_ref.shape[0]
    packed = e_ref.shape[1]
    kw_ref[:tok_rows] = nn(e_ref[...], comp_ref[:packed]).astype(BF)
    kw_ref[tok_rows:] = k_ref[...]
    prev = None
    for part in range(packed // group):
        term = nn(
            comp_ref[packed + part * group : packed + (part + 1) * group],
            et_ref[part * group : (part + 1) * group],
        )
        prev = term if prev is None else prev + term
    vw_ref[:, :tok_rows] = prev.astype(BF)
    vw_ref[:, tok_rows:] = vt_ref[...]
    summ = summ_ref[...]
    kc_ref[fine:mid_at] = nk_ref[...]
    vc_ref[:, fine:mid_at] = nvt_ref[...]
    kc_ref[mid_at:] = nn(selk_ref[...], summ).astype(BF)
    vc_ref[:, mid_at:] = jnp.transpose(nn(selv_ref[...], summ)).astype(BF)
    q4_ref[...] = jnp.zeros_like(q4_ref)
    same = lax.broadcasted_iota(jnp.int32, (FBLK, FBLK), 0) == lax.broadcasted_iota(
        jnp.int32, (FBLK, FBLK), 1
    )

    def block(g, carry):
        at = pl.multiple_of(g * FBLK, FBLK)
        biases = []
        for entry in range(FINE_K):
            start = pl.multiple_of(lists_ref[g, entry] * FBLK, FBLK)
            kc_ref[entry * FBLK : (entry + 1) * FBLK] = kw_ref[pl.ds(start, FBLK)]
            vc_ref[:, entry * FBLK : (entry + 1) * FBLK] = vw_ref[:, pl.ds(start, FBLK)]
            bias = bias_ref[pl.ds(start, FBLK)]
            biases.append(jnp.where(same, 0.0, bias) if entry == 0 else bias)
        for h in range(heads):
            q4_ref[h * width : (h + 1) * width, h * FBLK : (h + 1) * FBLK] = qt_ref[
                h * width : (h + 1) * width, pl.ds(at, FBLK)
            ]
        scores = nn(kc_ref[...], q4_ref[...])
        scales = []
        for h in range(heads):
            lanes = slice(h * FBLK, (h + 1) * FBLK)
            parts = [scores[e * FBLK : (e + 1) * FBLK, lanes] + biases[e] for e in range(FINE_K)]
            top = functools.reduce(
                jnp.maximum, [jnp.max(part, axis=0, keepdims=True) for part in parts]
            )
            den = jnp.zeros_like(top)
            for e, part in enumerate(parts):
                weight = jnp.exp(part - top)
                den = den + jnp.sum(weight, axis=0, keepdims=True)
                p_ref[e * FBLK : (e + 1) * FBLK, lanes] = weight.astype(BF)
            scales.append(mix_ref[0, h] / den)
            for level, (low, high) in enumerate(((fine, mid_at), (mid_at, far_at), (far_at, total))):
                part = scores[low:high, lanes]
                weight = jnp.exp(part - jnp.max(part, axis=0, keepdims=True))
                scale = mix_ref[level + 1, h] / jnp.sum(weight, axis=0, keepdims=True)
                p_ref[low:high, lanes] = (weight * scale).astype(BF)
        fine_out = nn(vc_ref[:, :fine], p_ref[:fine])
        coarse_out = nn(vc_ref[:, fine:], p_ref[fine:])
        rows = []
        for h in range(heads):
            pick = (slice(h * width, (h + 1) * width), slice(h * FBLK, (h + 1) * FBLK))
            rows.append(fine_out[pick] * scales[h] + coarse_out[pick])
        out_ref[pl.ds(at, FBLK)] = jnp.transpose(jnp.concatenate(rows, axis=0)).astype(BF)
        return carry

    lax.fori_loop(0, tok_rows // FBLK, block, 0)


def output_kernel(a_ref, b_ref, c_ref, d_ref, w_ref, out_ref):
    group = a_ref.shape[1]
    total = None
    for index, part in enumerate((a_ref, b_ref, c_ref, d_ref)):
        term = nn(part[...], w_ref[index * group : (index + 1) * group])
        total = term if total is None else total + term
    out_ref[...] = total.astype(BF)


def visibility(mask_ids, tok_rows):
    position = jnp.arange(tok_rows, dtype=jnp.int32)
    hidden = jnp.sum((mask_ids[:, None] == position[None, :]).astype(jnp.int32), axis=0)
    before = jnp.sum((mask_ids[:, None] < position[None, :]).astype(jnp.int32), axis=0)
    return hidden == 0, position - before


def local(tokens, w_query, w_key, w_value, w_out, level_mix, fine_blocks, order, mask_ids):
    tok_rows, width = tokens.shape
    slabs = lax.axis_size("seq")
    slab, head = lax.axis_index("seq"), lax.axis_index("head")
    group = w_query.shape[1]
    heads = level_mix.shape[1]
    packed = tok_rows - mask_ids.shape[1]
    near, mids, fars = tok_rows // POOL1, tok_rows // POOL2, tok_rows // POOL3
    quarter = width // 4

    before_mask = lax.ppermute(mask_ids, "seq", [(i, i + 1) for i in range(slabs - 1)])
    pieces, flip = exchange_tokens(tokens)

    place = order[0] ^ flip
    index = jnp.arange(tok_rows, dtype=jnp.int32)
    permute = (place[:, None] == index[None, :]).astype(BF)
    permute_t = (index[:, None] == place[None, :]).astype(BF)
    seen, rank = visibility(mask_ids[0], tok_rows)
    lead = near + SUMM_ROWS
    row = jnp.arange(lead + packed, dtype=jnp.int32)[:, None]
    target = jnp.where(
        row < near,
        index // POOL1,
        jnp.where(
            row < near + mids,
            index // POOL2 + near,
            jnp.where(row < lead, index // POOL3 + near + mids, rank + lead),
        ),
    )
    member = (target == row) & seen[None, :]
    pool = member.astype(BF)
    counts = jnp.sum(member[:lead].astype(F32), axis=1)
    factor = 1.0 / jnp.sqrt(jnp.maximum(counts, 1.0))
    seen_before, rank_before = visibility(before_mask[0], tok_rows)
    seen_before = seen_before & (slab > 0)
    slot = jnp.arange(packed, dtype=jnp.int32)
    expand = ((rank_before[:, None] == slot[None, :]) & seen_before[:, None]).astype(BF)
    expand_t = ((slot[:, None] == rank_before[None, :]) & seen_before[None, :]).astype(BF)
    bias = jnp.where(jnp.concatenate([seen_before, seen]), 0.0, HIDE).astype(F32)
    bias = jnp.broadcast_to(bias[:, None], (2 * tok_rows, FBLK))
    line = jnp.arange(3 * mids + fars * slabs, dtype=jnp.int32)
    mid_shard = slab - 1 + line // mids
    far_line = line - 3 * mids
    step = 2 * SUMM_ROWS
    source = jnp.where(
        line < 3 * mids,
        mid_shard * step + line % mids,
        far_line // fars * step + mids + far_line % fars,
    )
    inside = (line >= 3 * mids) | ((mid_shard >= 0) & (mid_shard < slabs))
    column = jnp.arange(step * slabs, dtype=jnp.int32)[None, :]
    select_k = ((source[:, None] == column) & inside[:, None]).astype(BF)
    select_v = ((source[:, None] + SUMM_ROWS == column) & inside[:, None]).astype(BF)

    def by_quarter(weight):
        parts = [
            lax.dynamic_slice_in_dim(weight, (head ^ other) * quarter, quarter, axis=0)
            for other in (0, 2, 1, 3)
        ]
        return jnp.concatenate(parts, axis=0)

    wqv_t = by_quarter(jnp.concatenate([w_query, w_value], axis=1)).T
    wk = by_quarter(w_key)
    wo = by_quarter(w_out)

    shape = jax.ShapeDtypeStruct
    params = pltpu.CompilerParams(vmem_limit_bytes=VMEM_LIMIT)
    places = tuple((r, c) for _, r, c in pieces)
    q_t, v_t, keys, near_k, near_vt, summ, comp = pl.pallas_call(
        functools.partial(project_kernel, places),
        out_shape=(
            shape((group, tok_rows), BF),
            shape((group, tok_rows), BF),
            shape((tok_rows, group), BF),
            shape((near, group), BF),
            shape((group, near), BF),
            shape((step, group), BF),
            shape((2 * packed, group), BF),
        ),
        in_specs=vmem_specs(len(pieces) + 7),
        out_specs=vmem_specs(7),
        scratch_shapes=[pltpu.VMEM((tok_rows, width), BF)],
        compiler_params=params,
        name="project",
    )(
        *[piece for piece, _, _ in pieces],
        wqv_t,
        wk,
        permute,
        permute_t,
        pool,
        factor[:, None],
        factor[None, :],
    )
    comp_before = lax.ppermute(comp, "seq", [(i, i + 1) for i in range(slabs - 1)])
    summ_all = lax.all_to_all(
        jnp.broadcast_to(summ[None], (slabs, step, group)), "seq", split_axis=0, concat_axis=0, tiled=True
    ).reshape(slabs * step, group)

    total = FINE_K * FBLK + near + line.shape[0]
    smem = pl.BlockSpec(memory_space=pltpu.SMEM)
    attended = pl.pallas_call(
        attend_kernel,
        out_shape=shape((tok_rows, group), BF),
        in_specs=[smem, smem] + vmem_specs(12),
        out_specs=pl.BlockSpec(memory_space=pltpu.VMEM),
        scratch_shapes=[
            pltpu.VMEM((2 * tok_rows, group), BF),
            pltpu.VMEM((group, 2 * tok_rows), BF),
            pltpu.VMEM((total, group), BF),
            pltpu.VMEM((group, total), BF),
            pltpu.VMEM((group, heads * FBLK), BF),
            pltpu.VMEM((total, heads * FBLK), BF),
        ],
        compiler_params=params,
        name="attend",
    )(
        fine_blocks, level_mix, q_t, keys, v_t, comp_before, expand, expand_t, bias, near_k, near_vt,
        summ_all, select_k, select_v,
    )
    third = over_head(attended, X_PAIRS)
    second = over_head(attended, CORE_PAIRS)
    fourth = over_head(third, CORE_PAIRS)
    steps = 4
    tile = pl.BlockSpec((tok_rows // steps, group), lambda i: (i, 0))
    return pl.pallas_call(
        output_kernel,
        grid=(steps,),
        out_shape=shape((tok_rows, group), BF),
        in_specs=[tile] * 4 + [pl.BlockSpec((width, group), lambda i: (0, 0))],
        out_specs=tile,
        compiler_params=params,
        name="output",
    )(attended, third, second, fourth, wo)


def solution(mesh):
    placed = (
        P("seq", None),
        P(None, "head"),
        P(None, "head"),
        P(None, "head"),
        P(None, "head"),
        P(None, "head"),
        P("seq", None),
        P("seq", None),
        P("seq", None),
    )
    return jax.shard_map(
        local, mesh=mesh, in_specs=placed, out_specs=P("seq", "head"), check_vma=False
    )
```

time: 208 us -> 112 us (0.54)
  the two profiles are of different devices: /device:TPU:0 before, /device:TPU:17 now
where the time goes in v1:
time: 112 us; the launch traced here: 111 us
  starting transfers between devices  37 us (33%)
  Pallas kernels  26.6 us (24%)
  waiting for transfers between devices  23.5 us (21%)
  other arithmetic  14.5 us (13%)
  local copies, waits for them, and re-layouts  9.17 us (8%)
    ppermute x7, starting transfers between devices, over_head(): return lax.ppermute(block, 'head', pairs)  15.4 us
    pallas_call x1, Pallas kernels, local(): pl.pallas_call(attend_kernel, out_shape=shape((tok_rows, group), BF), in_...  12.2 us
    ppermute x7, starting transfers between devices, to_peer(): return lax.ppermute(block, 'seq', [(i, i ^ distance) for i in range(slabs)])  11.6 us
    ppermute x7, waiting for transfers between devices, over_head(): return lax.ppermute(block, 'head', pairs)  11 us
    all_to_all x1, waiting for transfers between devices, local(): lax.all_to_all(jnp.broadcast_to(summ[None], (slabs, step, group)), 'seq',...  10.1 us
    pallas_call x1, Pallas kernels, local(): pl.pallas_call(functools.partial(project_kernel, places), out_shape=(shap...  9.98 us
    all_to_all x1, starting transfers between devices, local(): lax.all_to_all(jnp.broadcast_to(summ[None], (slabs, step, group)), 'seq',...  5.67 us
    pallas_call x1, Pallas kernels, local(): pl.pallas_call(output_kernel, grid=(steps,), out_shape=shape((tok_rows, g...  4.39 us
  transfers between devices with their start and end apart: 17, of which 5 were waited for; matrix products, arithmetic and copies ran while one was open for 17% of the time, Pallas kernels for 0%

profile of v1, /device:TPU:17, one launch (start us, length us, event | category | flops | bytes accessed | tf_op | source)
XLA Modules:
  0.0 111.1 jit_solution(13075463281367601511)
XLA Ops:
  0.0 1.3 %constant_dynamic-slice_fusion.9 = (bf16[8,128,256]{2,1,0:T(8,128)(2,1)S(1)}, bf16[8,128,256]{2,1,0:T(8,128)(2,1)S(1)}) fusion(bf16[8,128,1024]{2,1,0:T(8,128)(2,1)} %bitcast.31, s32[]{:T(128)S(6)} %select_n.163, s32[]{:T(128)S(6)} %select_n.171), kind=kLoop, calls=%fused_computation.82 | loop fusion | bytes 2097160 | tf_op jit(solution)/shard_map/dynamic_slice | solution.py:50
  1.4 2.3 %collective-permute-start.7 = (bf16[128,512]{1,0:T(8,128)(2,1)S(1)}, bf16[128,512]{1,0:T(8,128)(2,1)S(1)}, u32[]{:S(2)}, u32[]{:S(2)}) collective-permute-start(bf16[128,512]{1,0:T(8,128)(2,1)S(1)} %get-tuple-element.40), channel_id=1, source_target_pairs={{0,12},{4,8},{8,4},{12,0},{16,28},{20,24},{24,20},{28,16},{1,13},{... | collective-permute-start | bytes 393224 | tf_op jit(solution)/shard_map/ppermute | solution.py:65
  4.1 1.4 %dynamic-slice_bitcast_fusion.3 = (bf16[128,256]{1,0:T(8,128)(2,1)S(1)}, bf16[128,256]{1,0:T(8,128)(2,1)S(1)}, bf16[128,256]{1,0:T(8,128)(2,1)S(1)}, bf16[128,25...) fusion(bf16[8,128,1024]{2,1,0:T(8,128)(2,1)} %bitcast.32, ...), kind=kLoop, calls=%fused_computation.58 | loop fusion | bytes 1048612 | tf_op jit(solution)/shard_map/jit(dynamic_index_in_dim)/squeeze | solution.py:76
  5.6 1.2 %collective-permute-start = (bf16[128,256]{1,0:T(8,128)(2,1)S(1)}, bf16[128,256]{1,0:T(8,128)(2,1)S(1)}, u32[]{:S(2)}, u32[]{:S(2)}) collective-permute-start(bf16[128,256]{1,0:T(8,128)(2,1)S(1)} %get-tuple-element.32), channel_id=1, source_target_pairs={{0,28},{4,24},{8,20},{12,16},{16,12},{20,8},{24,4},{28,0},{1,29},{... | collective-permute-start | bytes 196616 | tf_op jit(solution)/shard_map/ppermute | solution.py:65
  6.8 2.1 %collective-permute-start.12 = (s32[1,512]{1,0:T(1,128)S(1)}, s32[1,512]{1,0:T(1,128)S(1)}, u32[]{:S(2)}, u32[]{:S(2)}) collective-permute-start(s32[1,512]{1,0:T(1,128)S(1)} %copy-done.18), channel_id=1, source_target_pairs={{0,4},{4,8},{8,12},{12,16},{16,20},{20,24},{24,28},{1,5},{5,9},{9,... | collective-permute-start | bytes 6152 | tf_op jit(solution)/shard_map/ppermute | solution.py:230
  9.4 2.6 %fusion.1 = (bf16[1024,1024]{1,0:T(8,128)(2,1)}, bf16[1024,1024]{1,0:T(8,128)(2,1)}) fusion(s32[1024]{0:T(1024)S(1)} %bitcast.34), kind=kLoop, calls=%fused_computation.3 | loop fusion | flops 4194304 | bytes 4198400 | tf_op jit(solution)/shard_map/convert_element_type | solution.py:236
  12.7 3.2 %fusion.33 = (bf16[672,1024]{1,0:T(8,128)(2,1)}, pred[672,1024]{1,0:T(8,128)(4,1)S(1)}) fusion(pred[1024]{0:T(1024)(128)(4,1)S(1)} %broadcast_compare_fusion, s32[1024]{0:T(1024)S(1)} %get-tuple-element.63, s32[1024]{0:T(1024)S(1)} %get-tuple-element.62, pred[672]{0:T(1024)(128)(4,1)S(1)} %get-tuple-element.64, s32[1024]{0:T(1024)S(1)} %get-tuple-element.55, ...), kind=kLoop, calls=%fused_computation.125 | loop fusion | flops 4128768 | bytes 2083808 | tf_op jit(solution)/shard_map/convert_element_type | solution.py:250
  17.1 1.1 %maximum_bitcast_fusion.refs_7_ = bf16[512,1024]{1,0:T(8,128)(2,1)} fusion(bf16[256,512]{0,1:T(8,128)(2,1)S(1)} %get-tuple-element.38, bf16[256,512]{0,1:T(8,128)(2,1)S(1)} %get-tuple-element.37, bf16[256,512]{0,1:T(8,128)(2,1)S(1)} %get-tuple-element.36, bf16[256,512]{0,1:T(8,128)(2,1)S(1)} %get-tuple-element.35), kind=kLoop, calls=%fused_computation.34 | loop fusion | flops 4194304 | bytes 2097152 | tf_op jit(solution)/shard_map/transpose | solution.py:281
  18.2 0.8 pad_maximum_fusion.refs_8_
  21.2 1.3 %collective-permute-start.1 = (bf16[128,256]{1,0:T(8,128)(2,1)S(1)}, bf16[128,256]{1,0:T(8,128)(2,1)S(1)}, u32[]{:S(2)}, u32[]{:S(2)}) collective-permute-start(bf16[128,256]{1,0:T(8,128)(2,1)S(1)} %get-tuple-element.31), channel_id=1, source_target_pairs={{0,24},{4,28},{8,16},{12,20},{16,8},{20,12},{24,0},{28,4},{1,25},{... | collective-permute-start | bytes 196616 | tf_op jit(solution)/shard_map/ppermute | solution.py:65
  23.0 1.9 %collective-permute-start.2 = (bf16[128,256]{1,0:T(8,128)(2,1)S(1)}, bf16[128,256]{1,0:T(8,128)(2,1)S(1)}, u32[]{:S(2)}, u32[]{:S(2)}) collective-permute-start(bf16[128,256]{1,0:T(8,128)(2,1)S(1)} %get-tuple-element.30), channel_id=1, source_target_pairs={{0,20},{4,16},{8,28},{12,24},{16,4},{20,0},{24,12},{28,8},{1,21},{... | collective-permute-start | bytes 196616 | tf_op jit(solution)/shard_map/ppermute | solution.py:65
  24.9 4.5 %collective-permute-start.3 = (bf16[128,256]{1,0:T(8,128)(2,1)S(1)}, bf16[128,256]{1,0:T(8,128)(2,1)S(1)}, u32[]{:S(2)}, u32[]{:S(2)}) collective-permute-start(bf16[128,256]{1,0:T(8,128)(2,1)S(1)} %get-tuple-element.29), channel_id=1, source_target_pairs={{0,16},{4,20},{8,24},{12,28},{16,0},{20,4},{24,8},{28,12},{1,17},{... | collective-permute-start | bytes 196616 | tf_op jit(solution)/shard_map/ppermute | solution.py:65
  29.4 2.3 %collective-permute-done.3 = bf16[128,256]{1,0:T(8,128)(2,1)S(1)} collective-permute-done((bf16[128,256]{1,0:T(8,128)(2,1)S(1)}, bf16[128,256]{1,0:T(8,128)(2,1)S(1)}, u32[]{:S(2)}, u32[]{:S(2)}) %collective-permute-start.3) | collective-permute-done | bytes 65568 | tf_op jit(solution)/shard_map/ppermute | solution.py:65
  31.8 1.3 %collective-permute-start.4 = (bf16[512,256]{1,0:T(8,128)(2,1)S(1)}, bf16[512,256]{1,0:T(8,128)(2,1)S(1)}, u32[]{:S(2)}, u32[]{:S(2)}) collective-permute-start(bf16[512,256]{1,0:T(8,128)(2,1)S(1)} %constant_dynamic-update-slice_fusion.refs_0_), channel_id=1, source_target_pairs={{0,2},{2,0},{1,3},{3,1},{4,6},{6,4},{5,7},{7,5},{8,10},{10,8},{9,1... | collective-permute-start | bytes 786440 | tf_op jit(solution)/shard_map/ppermute | solution.py:38
  33.0 4.1 %collective-permute-start.5 = (bf16[512,256]{1,0:T(8,128)(2,1)S(1)}, bf16[512,256]{1,0:T(8,128)(2,1)S(1)}, u32[]{:S(2)}, u32[]{:S(2)}) collective-permute-start(bf16[512,256]{1,0:T(8,128)(2,1)S(1)} %constant_dynamic-update-slice_fusion.refs_0_), channel_id=1, source_target_pairs={{0,1},{1,0},{2,3},{3,2},{4,5},{5,4},{6,7},{7,6},{8,9},{9,8},{10,11... | collective-permute-start | bytes 786440 | tf_op jit(solution)/shard_map/ppermute | solution.py:38
  37.3 4.6 %collective-permute-start.6 = (bf16[512,256]{1,0:T(8,128)(2,1)S(1)}, bf16[512,256]{1,0:T(8,128)(2,1)S(1)}, u32[]{:S(2)}, u32[]{:S(2)}) collective-permute-start(bf16[512,256]{1,0:T(8,128)(2,1)S(1)} %collective-permute-done.4.refs_1_), channel_id=1, source_target_pairs={{0,1},{1,0},{2,3},{3,2},{4,5},{5,4},{6,7},{7,6},{8,9},{9,8},{10,11... | collective-permute-start | bytes 786440 | tf_op jit(solution)/shard_map/ppermute | solution.py:38
  42.0 1.1 collective-permute-done.6.refs_3_
  43.8 10.0 %project.1 = (bf16[256,1024]{1,0:T(8,128)(2,1)}, bf16[256,1024]{1,0:T(8,128)(2,1)}, bf16[1024,256]{1,0:T(8,128)(2,1)}, bf16[128,256]{1,0:T(8,128)(2,1)}, bf16[25...) custom-call(bf16[512,256]{1,0:T(8,128)(2,1)} %copy-done.10, bf16[512,256]{1,0:T(8,128)(2,1)} %copy-done.12, ...), custom_call_target="tpu_custom_call" | custom-call | tf_op jit(solution)/shard_map/project/pallas_call | solution.py:288
  53.8 2.1 %collective-permute-start.11 = (bf16[1024,256]{1,0:T(8,128)(2,1)}, bf16[1024,256]{1,0:T(8,128)(2,1)S(1)}, u32[]{:S(2)}, u32[]{:S(2)}) collective-permute-start(bf16[1024,256]{1,0:T(8,128)(2,1)} %get-tuple-element.15), channel_id=1, source_target_pairs={{0,4},{4,8},{8,12},{12,16},{16,20},{20,24},{24,28},{1,5},{5,9},{9,... | collective-permute-start | bytes 1572872 | tf_op jit(solution)/shard_map/ppermute | solution.py:314
  55.9 1.5 %broadcast_in_dim.89 = bf16[8,64,256]{2,1,0:T(8,128)(2,1)} broadcast(bf16[64,256]{1,0:T(8,128)(2,1)} %get-tuple-element.18), dimensions={1,2} | broadcast | bytes 294912 | tf_op jit(solution)/shard_map/broadcast_in_dim | solution.py:316
  57.4 5.7 %all-to-all-start = ((bf16[8,64,256]{2,1,0:T(8,128)(2,1)}), bf16[8,64,256]{2,1,0:T(8,128)(2,1)S(1)}, u32[]{:S(2)}, u32[]{:S(2)}) async-start(bf16[8,64,256]{2,1,0:T(8,128)(2,1)} %broadcast_in_dim.89), calls=%async_computation | async-start | bytes 524288 | tf_op jit(solution)/shard_map/all_to_all | solution.py:315
  63.1 1.6 %fusion.4.e_ref = bf16[1024,512]{1,0:T(8,128)(2,1)} fusion(s32[1024]{0:T(1024)S(1)} %iota_subtract_fusion, pred[1024]{0:T(1024)(128)(4,1)S(1)} %compare_and_fusion), kind=kLoop, calls=%fused_computation.17 | loop fusion | flops 1572864 | bytes 1053696 | tf_op jit(solution)/shard_map/convert_element_type | solution.py:256
  64.6 1.4 %fusion.6.et_ref = bf16[512,1024]{1,0:T(8,128)(2,1)} fusion(s32[1024]{0:T(1024)S(1)} %iota_subtract_fusion, pred[1024]{0:T(1024)(128)(4,1)S(1)} %compare_and_fusion), kind=kLoop, calls=%fused_computation.19 | loop fusion | flops 1572864 | bytes 1053696 | tf_op jit(solution)/shard_map/convert_element_type | solution.py:257
  66.0 10.1 %all-to-all-done = bf16[8,64,256]{2,1,0:T(8,128)(2,1)S(1)} async-done(((bf16[8,64,256]{2,1,0:T(8,128)(2,1)}), bf16[8,64,256]{2,1,0:T(8,128)(2,1)S(1)}, u32[]{:S(2)}, u32[]{:S(2)}) %all-to-all-start) | async-done | bytes 262176 | tf_op jit(solution)/shard_map/all_to_all | solution.py:315
  76.2 1.3 %broadcast_in_dim.88.bias_ref = f32[2048,128]{1,0:T(8,128)} broadcast(f32[2048]{0:T(1024)S(1)} %add_select_fusion), dimensions={0} | broadcast | bytes 1056768 | tf_op jit(solution)/shard_map/broadcast_in_dim | solution.py:259
  77.5 12.2 %attend.1.a_ref = bf16[1024,256]{1,0:T(8,128)(2,1)} custom-call(s32[8,4]{1,0:T(8,128)} %copy.20.lists_ref, f32[4,4]{1,0:T(4,128)} %mix_ref.1, bf16[256,1024]{1,0:T(8,128)(2,1)} %get-tuple-element.12.qt_ref, bf16[1024,256]{1,0:T(8,128)(2,1)} %get-tuple-element.13.k_ref, bf16[256,1024]{1,0:T(8,128)(2,1)} %get-tuple-element.14.vt_ref, ...), custom_call_target="tpu_custom_call" | custom-call | tf_op jit(solution)/shard_map/attend/pallas_call | solution.py:321
  89.7 1.1 %collective-permute-start.13 = (bf16[1024,256]{1,0:T(8,128)(2,1)}, bf16[1024,256]{1,0:T(8,128)(2,1)S(1)}, u32[]{:S(2)}, u32[]{:S(2)}) collective-permute-start(bf16[1024,256]{1,0:T(8,128)(2,1)} %attend.1.a_ref), channel_id=1, source_target_pairs={{0,2},{2,0},{1,3},{3,1},{4,6},{6,4},{5,7},{7,5},{8,10},{10,8},{9,1... | collective-permute-start | bytes 1572872 | tf_op jit(solution)/shard_map/ppermute | solution.py:38
  90.8 1.8 %collective-permute-start.14 = (bf16[1024,256]{1,0:T(8,128)(2,1)}, bf16[1024,256]{1,0:T(8,128)(2,1)S(1)}, u32[]{:S(2)}, u32[]{:S(2)}) collective-permute-start(bf16[1024,256]{1,0:T(8,128)(2,1)} %attend.1.a_ref), channel_id=1, source_target_pairs={{0,1},{1,0},{2,3},{3,2},{4,5},{5,4},{6,7},{7,6},{8,9},{9,8},{10,11... | collective-permute-start | bytes 1572872 | tf_op jit(solution)/shard_map/ppermute | solution.py:38
  92.7 9.1 %collective-permute-done.13.b_ref = bf16[1024,256]{1,0:T(8,128)(2,1)S(1)} collective-permute-done((bf16[1024,256]{1,0:T(8,128)(2,1)}, bf16[1024,256]{1,0:T(8,128)(2,1)S(1)}, u32[]{:S(2)}, u32[]{:S(2)}) %collective-permute-start.13) | collective-permute-done | bytes 524320 | tf_op jit(solution)/shard_map/ppermute | solution.py:38
  101.8 2.5 %collective-permute-start.15 = (bf16[1024,256]{1,0:T(8,128)(2,1)S(1)}, bf16[1024,256]{1,0:T(8,128)(2,1)S(1)}, u32[]{:S(2)}, u32[]{:S(2)}) collective-permute-start(bf16[1024,256]{1,0:T(8,128)(2,1)S(1)} %collective-permute-done.13.b_ref), channel_id=1, source_target_pairs={{0,1},{1,0},{2,3},{3,2},{4,5},{5,4},{6,7},{7,6},{8,9},{9,8},{10,11... | collective-permute-start | bytes 1572872 | tf_op jit(solution)/shard_map/ppermute | solution.py:38
  104.3 0.8 pad_maximum_fusion.1.w_ref
  106.7 4.4 %output.1 = bf16[1024,256]{1,0:T(8,128)(2,1)} custom-call(bf16[1024,256]{1,0:T(8,128)(2,1)} %attend.1.a_ref, bf16[1024,256]{1,0:T(8,128)(2,1)} %copy-done.7, bf16[1024,256]{1,0:T(8,128)(2,1)} %copy-done.8, bf16[1024,256]{1,0:T(8,128)(2,1)} %copy-done.9, bf16[1024,256]{1,0:T(8,128)(2,1)} %pad_maximum_fusion.1.w_ref), custom_call_target="tpu_custom_call" | custom-call | tf_op jit(solution)/shard_map/output/pallas_call | solution.py:345
  (85 shorter events, 7.7 us)
Async XLA Ops:
  0.0 6.8 %copy-start.18 = (s32[1,512]{1,0:T(1,128)S(1)}, s32[1,512]{1,0:T(1,128)}, u32[]{:S(2)}) copy-start(s32[1,512]{1,0:T(1,128)} %param.17) | copy-start | bytes 6148
  0.0 9.0 %copy-start.5 = (bf16[1024,256]{1,0:T(8,128)(2,1)S(1)}, bf16[1024,256]{1,0:T(8,128)(2,1)}, u32[]{:S(2)}) copy-start(bf16[1024,256]{1,0:T(8,128)(2,1)} %param.10) | copy-start | bytes 1572868
  1.3 7.8 %copy-start.6 = (bf16[1024,256]{1,0:T(8,128)(2,1)S(1)}, bf16[1024,256]{1,0:T(8,128)(2,1)}, u32[]{:S(2)}) copy-start(bf16[1024,256]{1,0:T(8,128)(2,1)} %param.12) | copy-start | bytes 1572868
  1.4 8.1 %copy-start.16 = (s32[1,1024]{1,0:T(1,128)S(1)}, s32[1,1024]{1,0:T(1,128)}, u32[]{:S(2)}) copy-start(s32[1,1024]{1,0:T(1,128)} %param.16) | copy-start | bytes 12292
  1.4 35.7 %collective-permute-start.7 = (bf16[128,512]{1,0:T(8,128)(2,1)S(1)}, bf16[128,512]{1,0:T(8,128)(2,1)S(1)}, u32[]{:S(2)}, u32[]{:S(2)}) collective-permute-start(bf16[128,512]{1,0:T(8,128)(2,1)S(1)} %get-tuple-element.40), channel_id=1, source_target_pairs={{0,12},{4,8},{8,4},{12,0},{16,28},{20,24},{24,20},{28,16},{1,13},{... | collective-permute-start | bytes 393224 | tf_op jit(solution)/shard_map/ppermute | solution.py:65
  3.7 33.4 %collective-permute-start.8 = (bf16[128,512]{1,0:T(8,128)(2,1)S(1)}, bf16[128,512]{1,0:T(8,128)(2,1)S(1)}, u32[]{:S(2)}, u32[]{:S(2)}) collective-permute-start(bf16[128,512]{1,0:T(8,128)(2,1)S(1)} %get-tuple-element.41), channel_id=1, source_target_pairs={{0,8},{4,12},{8,0},{12,4},{16,24},{20,28},{24,16},{28,20},{1,9},{5... | collective-permute-start | bytes 393224 | tf_op jit(solution)/shard_map/ppermute | solution.py:65
  3.9 33.3 %collective-permute-start.9 = (bf16[128,512]{1,0:T(8,128)(2,1)S(1)}, bf16[128,512]{1,0:T(8,128)(2,1)S(1)}, u32[]{:S(2)}, u32[]{:S(2)}) collective-permute-start(bf16[128,512]{1,0:T(8,128)(2,1)S(1)} %get-tuple-element.39), channel_id=1, source_target_pairs={{0,4},{4,0},{8,12},{12,8},{16,20},{20,16},{24,28},{28,24},{1,5},{5... | collective-permute-start | bytes 393224 | tf_op jit(solution)/shard_map/ppermute | solution.py:65
  5.6 17.4 %collective-permute-start = (bf16[128,256]{1,0:T(8,128)(2,1)S(1)}, bf16[128,256]{1,0:T(8,128)(2,1)S(1)}, u32[]{:S(2)}, u32[]{:S(2)}) collective-permute-start(bf16[128,256]{1,0:T(8,128)(2,1)S(1)} %get-tuple-element.32), channel_id=1, source_target_pairs={{0,28},{4,24},{8,20},{12,16},{16,12},{20,8},{24,4},{28,0},{1,29},{... | collective-permute-start | bytes 196616 | tf_op jit(solution)/shard_map/ppermute | solution.py:65
  6.8 14.4 %collective-permute-start.12 = (s32[1,512]{1,0:T(1,128)S(1)}, s32[1,512]{1,0:T(1,128)S(1)}, u32[]{:S(2)}, u32[]{:S(2)}) collective-permute-start(s32[1,512]{1,0:T(1,128)S(1)} %copy-done.18), channel_id=1, source_target_pairs={{0,4},{4,8},{8,12},{12,16},{16,20},{20,24},{24,28},{1,5},{5,9},{9,... | collective-permute-start | bytes 6152 | tf_op jit(solution)/shard_map/ppermute | solution.py:230
  12.6 3.5 %copy-start.2 = (bf16[1024,256]{1,0:T(8,128)(2,1)S(1)}, bf16[1024,256]{1,0:T(8,128)(2,1)}, u32[]{:S(2)}) copy-start(bf16[1024,256]{1,0:T(8,128)(2,1)} %param.13) | copy-start | bytes 1572868
  12.6 3.5 %copy-start.3 = (bf16[1024,256]{1,0:T(8,128)(2,1)S(1)}, bf16[1024,256]{1,0:T(8,128)(2,1)}, u32[]{:S(2)}) copy-start(bf16[1024,256]{1,0:T(8,128)(2,1)} %param.11) | copy-start | bytes 1572868
  16.0 3.7 %copy-start.15 = (f32[160]{0:T(256)}, f32[160]{0:T(256)S(1)}, u32[]{:S(2)}) copy-start(f32[160]{0:T(256)S(1)} %maximum_rsqrt_fusion) | copy-start | bytes 1924
  16.3 4.2 %copy-start.17 = (s32[8,4]{0,1:T(4,128)S(1)}, s32[8,4]{0,1:T(4,128)}, u32[]{:S(2)}) copy-start(s32[8,4]{0,1:T(4,128)} %param.15) | copy-start | bytes 388
  21.2 3.8 %collective-permute-start.1 = (bf16[128,256]{1,0:T(8,128)(2,1)S(1)}, bf16[128,256]{1,0:T(8,128)(2,1)S(1)}, u32[]{:S(2)}, u32[]{:S(2)}) collective-permute-start(bf16[128,256]{1,0:T(8,128)(2,1)S(1)} %get-tuple-element.31), channel_id=1, source_target_pairs={{0,24},{4,28},{8,16},{12,20},{16,8},{20,12},{24,0},{28,4},{1,25},{... | collective-permute-start | bytes 196616 | tf_op jit(solution)/shard_map/ppermute | solution.py:65
  23.0 6.4 %collective-permute-start.2 = (bf16[128,256]{1,0:T(8,128)(2,1)S(1)}, bf16[128,256]{1,0:T(8,128)(2,1)S(1)}, u32[]{:S(2)}, u32[]{:S(2)}) collective-permute-start(bf16[128,256]{1,0:T(8,128)(2,1)S(1)} %get-tuple-element.30), channel_id=1, source_target_pairs={{0,20},{4,16},{8,28},{12,24},{16,4},{20,0},{24,12},{28,8},{1,21},{... | collective-permute-start | bytes 196616 | tf_op jit(solution)/shard_map/ppermute | solution.py:65
  24.9 6.8 %collective-permute-start.3 = (bf16[128,256]{1,0:T(8,128)(2,1)S(1)}, bf16[128,256]{1,0:T(8,128)(2,1)S(1)}, u32[]{:S(2)}, u32[]{:S(2)}) collective-permute-start(bf16[128,256]{1,0:T(8,128)(2,1)S(1)} %get-tuple-element.29), channel_id=1, source_target_pairs={{0,16},{4,20},{8,24},{12,28},{16,0},{20,4},{24,8},{28,12},{1,17},{... | collective-permute-start | bytes 196616 | tf_op jit(solution)/shard_map/ppermute | solution.py:65
  31.8 11.3 %copy-start.10 = (bf16[512,256]{1,0:T(8,128)(2,1)}, bf16[512,256]{1,0:T(8,128)(2,1)S(1)}, u32[]{:S(2)}) copy-start(bf16[512,256]{1,0:T(8,128)(2,1)S(1)} %constant_dynamic-update-slice_fusion.refs_0_) | copy-start | bytes 786436
  31.8 5.5 %collective-permute-start.4 = (bf16[512,256]{1,0:T(8,128)(2,1)S(1)}, bf16[512,256]{1,0:T(8,128)(2,1)S(1)}, u32[]{:S(2)}, u32[]{:S(2)}) collective-permute-start(bf16[512,256]{1,0:T(8,128)(2,1)S(1)} %constant_dynamic-update-slice_fusion.refs_0_), channel_id=1, source_target_pairs={{0,2},{2,0},{1,3},{3,1},{4,6},{6,4},{5,7},{7,5},{8,10},{10,8},{9,1... | collective-permute-start | bytes 786440 | tf_op jit(solution)/shard_map/ppermute | solution.py:38
  33.0 8.9 %collective-permute-start.5 = (bf16[512,256]{1,0:T(8,128)(2,1)S(1)}, bf16[512,256]{1,0:T(8,128)(2,1)S(1)}, u32[]{:S(2)}, u32[]{:S(2)}) collective-permute-start(bf16[512,256]{1,0:T(8,128)(2,1)S(1)} %constant_dynamic-update-slice_fusion.refs_0_), channel_id=1, source_target_pairs={{0,1},{1,0},{2,3},{3,2},{4,5},{5,4},{6,7},{7,6},{8,9},{9,8},{10,11... | collective-permute-start | bytes 786440 | tf_op jit(solution)/shard_map/ppermute | solution.py:38
  37.2 5.9 %copy-start.1 = (bf16[384,512]{1,0:T(8,128)(2,1)}, bf16[384,512]{1,0:T(8,128)(2,1)S(1)}, u32[]{:S(2)}) copy-start(bf16[384,512]{1,0:T(8,128)(2,1)S(1)} %constant_dynamic-update-slice_fusion.4.refs_4_) | copy-start | bytes 1179652
  37.2 4.7 %collective-permute-start.10 = (bf16[384,512]{1,0:T(8,128)(2,1)S(1)}, bf16[384,512]{1,0:T(8,128)(2,1)S(1)}, u32[]{:S(2)}, u32[]{:S(2)}) collective-permute-start(bf16[384,512]{1,0:T(8,128)(2,1)S(1)} %constant_dynamic-update-slice_fusion.4.refs_4_), channel_id=1, source_target_pairs={{0,1},{1,0},{2,3},{3,2},{4,5},{5,4},{6,7},{7,6},{8,9},{9,8},{10,11... | collective-permute-start | bytes 1179656 | tf_op jit(solution)/shard_map/ppermute | solution.py:38
  37.3 5.8 %copy-start.12 = (bf16[512,256]{1,0:T(8,128)(2,1)}, bf16[512,256]{1,0:T(8,128)(2,1)S(1)}, u32[]{:S(2)}) copy-start(bf16[512,256]{1,0:T(8,128)(2,1)S(1)} %collective-permute-done.4.refs_1_) | copy-start | bytes 786436
  37.3 5.8 %collective-permute-start.6 = (bf16[512,256]{1,0:T(8,128)(2,1)S(1)}, bf16[512,256]{1,0:T(8,128)(2,1)S(1)}, u32[]{:S(2)}, u32[]{:S(2)}) collective-permute-start(bf16[512,256]{1,0:T(8,128)(2,1)S(1)} %collective-permute-done.4.refs_1_), channel_id=1, source_target_pairs={{0,1},{1,0},{2,3},{3,2},{4,5},{5,4},{6,7},{7,6},{8,9},{9,8},{10,11... | collective-permute-start | bytes 786440 | tf_op jit(solution)/shard_map/ppermute | solution.py:38
  41.9 1.2 %copy-start.13 = (bf16[512,256]{1,0:T(8,128)(2,1)}, bf16[512,256]{1,0:T(8,128)(2,1)S(1)}, u32[]{:S(2)}) copy-start(bf16[512,256]{1,0:T(8,128)(2,1)S(1)} %collective-permute-done.5.refs_2_) | copy-start | bytes 786436
  53.8 22.4 %collective-permute-start.11 = (bf16[1024,256]{1,0:T(8,128)(2,1)}, bf16[1024,256]{1,0:T(8,128)(2,1)S(1)}, u32[]{:S(2)}, u32[]{:S(2)}) collective-permute-start(bf16[1024,256]{1,0:T(8,128)(2,1)} %get-tuple-element.15), channel_id=1, source_target_pairs={{0,4},{4,8},{8,12},{12,16},{16,20},{20,24},{24,28},{1,5},{5,9},{9,... | collective-permute-start | bytes 1572872 | tf_op jit(solution)/shard_map/ppermute | solution.py:314
  57.4 18.7 %all-to-all-start = ((bf16[8,64,256]{2,1,0:T(8,128)(2,1)}), bf16[8,64,256]{2,1,0:T(8,128)(2,1)S(1)}, u32[]{:S(2)}, u32[]{:S(2)}) async-start(bf16[8,64,256]{2,1,0:T(8,128)(2,1)} %broadcast_in_dim.89), calls=%async_computation | async-start | bytes 524288 | tf_op jit(solution)/shard_map/all_to_all | solution.py:315
  76.2 1.3 %copy-start = (bf16[8,64,256]{2,1,0:T(8,128)(2,1)}, bf16[8,64,256]{2,1,0:T(8,128)(2,1)S(1)}, u32[]{:S(2)}) copy-start(bf16[8,64,256]{2,1,0:T(8,128)(2,1)S(1)} %all-to-all-done) | copy-start | bytes 786436
  76.2 1.3 %copy-start.4 = (bf16[1024,256]{1,0:T(8,128)(2,1)}, bf16[1024,256]{1,0:T(8,128)(2,1)S(1)}, u32[]{:S(2)}) copy-start(bf16[1024,256]{1,0:T(8,128)(2,1)S(1)} %collective-permute-done.11.comp_ref) | copy-start | bytes 1572868
  89.7 12.1 %collective-permute-start.13 = (bf16[1024,256]{1,0:T(8,128)(2,1)}, bf16[1024,256]{1,0:T(8,128)(2,1)S(1)}, u32[]{:S(2)}, u32[]{:S(2)}) collective-permute-start(bf16[1024,256]{1,0:T(8,128)(2,1)} %attend.1.a_ref), channel_id=1, source_target_pairs={{0,2},{2,0},{1,3},{3,1},{4,6},{6,4},{5,7},{7,5},{8,10},{10,8},{9,1... | collective-permute-start | bytes 1572872 | tf_op jit(solution)/shard_map/ppermute | solution.py:38
  90.8 14.2 %collective-permute-start.14 = (bf16[1024,256]{1,0:T(8,128)(2,1)}, bf16[1024,256]{1,0:T(8,128)(2,1)S(1)}, u32[]{:S(2)}, u32[]{:S(2)}) collective-permute-start(bf16[1024,256]{1,0:T(8,128)(2,1)} %attend.1.a_ref), channel_id=1, source_target_pairs={{0,1},{1,0},{2,3},{3,2},{4,5},{5,4},{6,7},{7,6},{8,9},{9,8},{10,11... | collective-permute-start | bytes 1572872 | tf_op jit(solution)/shard_map/ppermute | solution.py:38
  101.8 4.0 %copy-start.7 = (bf16[1024,256]{1,0:T(8,128)(2,1)}, bf16[1024,256]{1,0:T(8,128)(2,1)S(1)}, u32[]{:S(2)}) copy-start(bf16[1024,256]{1,0:T(8,128)(2,1)S(1)} %collective-permute-done.13.b_ref) | copy-start | bytes 1572868
  101.8 4.0 %collective-permute-start.15 = (bf16[1024,256]{1,0:T(8,128)(2,1)S(1)}, bf16[1024,256]{1,0:T(8,128)(2,1)S(1)}, u32[]{:S(2)}, u32[]{:S(2)}) collective-permute-start(bf16[1024,256]{1,0:T(8,128)(2,1)S(1)} %collective-permute-done.13.b_ref), channel_id=1, source_target_pairs={{0,1},{1,0},{2,3},{3,2},{4,5},{5,4},{6,7},{7,6},{8,9},{9,8},{10,11... | collective-permute-start | bytes 1572872 | tf_op jit(solution)/shard_map/ppermute | solution.py:38
  (4 other events, 3.4 us)

commit v2 on v1

v2 whole, which is shorter than its diff:
```python
import functools

import jax
import jax.numpy as jnp
from jax import lax
from jax.experimental import pallas as pl
from jax.experimental.pallas import tpu as pltpu
from jax.sharding import PartitionSpec as P

FBLK = 128
FINE_K = 4
POOL1 = 8
POOL2 = 64
POOL3 = 512
SUMM_ROWS = 32
BF = jnp.bfloat16
F32 = jnp.float32
I32 = jnp.int32
HIDE = -1e30
VMEM_LIMIT = 24 * 1024 * 1024

X_PAIRS = [(0, 2), (2, 0), (1, 3), (3, 1)]
CORE_PAIRS = [(0, 1), (1, 0), (2, 3), (3, 2)]


def nn(a, b):
    return lax.dot_general(a, b, (((1,), (0,)), ((), ())), preferred_element_type=F32)


def nt(a, b):
    return lax.dot_general(a, b, (((1,), (1,)), ((), ())), preferred_element_type=F32)


def iota(shape, axis):
    return lax.broadcasted_iota(I32, shape, axis)


def ones_where(condition):
    return jnp.where(condition, 1.0, 0.0).astype(BF)


def vmem_specs(count):
    return [pl.BlockSpec(memory_space=pltpu.VMEM)] * count


def smem_specs(count):
    return [pl.BlockSpec(memory_space=pltpu.SMEM)] * count


def over_head(block, pairs):
    return lax.ppermute(block, "head", pairs)


def to_next(block):
    return lax.ppermute(block, "seq", [(i, i + 1) for i in range(lax.axis_size("seq") - 1)])


def exchange_tokens(tokens, head):
    tok_rows, width = tokens.shape
    slabs = lax.axis_size("seq")
    rows = tok_rows // slabs
    quarter = width // 4
    slab = lax.axis_index("seq")
    split = tokens.reshape(slabs, rows, width)

    def columns(other):
        return lax.dynamic_slice_in_dim(split, (head ^ other) * quarter, quarter, axis=2)

    mine = columns(0)
    if slabs != 8:
        first = lax.all_to_all(mine, "seq", split_axis=0, concat_axis=0, tiled=True).reshape(
            tok_rows, quarter
        )
        third = over_head(first, X_PAIRS)
        second = over_head(first, CORE_PAIRS)
        fourth = over_head(third, CORE_PAIRS)
        pieces = [(first, 0, (0,)), (third, 0, (2,)), (second, 0, (1,)), (fourth, 0, (3,))]
        return pieces, 0, first
    both = jnp.concatenate([mine, columns(2)], axis=2)

    def to_peer(source, distance):
        block = lax.dynamic_index_in_dim(source, slab ^ distance, axis=0, keepdims=False)
        return lax.ppermute(block, "seq", [(i, i ^ distance) for i in range(slabs)])

    far = jnp.concatenate([to_peer(mine, d) for d in (7, 6, 5, 4)], axis=0)
    near = jnp.concatenate([to_peer(both, d) for d in (3, 2, 1)], axis=0)
    far_x = over_head(far, X_PAIRS)
    near_core = over_head(near, CORE_PAIRS)
    far_core = over_head(far, CORE_PAIRS)
    far_last = over_head(far_x, CORE_PAIRS)
    own = lax.dynamic_index_in_dim(split, slab, axis=0, keepdims=False)
    pieces = [(far, 0, (0,)), (far_x, 0, (2,)), (far_core, 0, (1,)), (far_last, 0, (3,))]
    pieces += [(near, 4 * rows, (0, 2)), (near_core, 4 * rows, (1, 3)), (own, 7 * rows, None)]
    return pieces, (slab ^ 7) * rows, far


def prepare_kernel(
    place_ref, order_ref, mask_ref, before_ref, wq_ref, wv_ref,
    p_ref, pt_ref, sel_ref, fcol_ref, frow_ref, e_ref, et_ref, bias_ref, selk_ref, selv_ref, wt_ref,
):
    slab, flip, slabs = place_ref[0], place_ref[1], place_ref[2]
    tok_rows = order_ref.shape[1]
    packed = e_ref.shape[1]
    mids, fars = tok_rows // POOL2, tok_rows // POOL3
    group = wq_ref.shape[1]
    lanes = 128

    def column(row):
        return jnp.transpose(jnp.broadcast_to(row.astype(F32), (lanes, row.shape[1]))).astype(I32)

    def ranks(ids):
        hidden = column(ids)
        parts = []
        for at in range(0, tok_rows, lanes):
            time = iota((1, lanes), 1) + at
            count = jnp.sum(jnp.where(hidden < time, 1.0, 0.0), axis=0, keepdims=True)
            here = jnp.sum(jnp.where(hidden == time, 1.0, 0.0), axis=0, keepdims=True)
            parts.append(jnp.where(here == 0.0, time - count.astype(I32), -1))
        return jnp.concatenate(parts, axis=1)

    place = order_ref[...] ^ flip
    place_column = column(place)
    for at in range(0, tok_rows, lanes):
        p_ref[:, at : at + lanes] = ones_where(place_column == iota((tok_rows, lanes), 1) + at)
        pt_ref[at : at + lanes] = ones_where(iota((lanes, tok_rows), 0) + at == place)
    rank = ranks(mask_ref[...])
    rank_before = jnp.where(slab > 0, ranks(before_ref[...]), -1)
    time = jnp.where(rank >= 0, iota((1, tok_rows), 1), -1) + 1
    line = iota((16, tok_rows), 0)
    stack = jnp.where(
        line == 0,
        time >> 5,
        jnp.where(
            line == 1,
            time & 31,
            jnp.where(line == 2, (rank + 1) >> 5, jnp.where(line == 3, (rank + 1) & 31, 0)),
        ),
    )
    moved = nn(stack.astype(F32).astype(BF), p_ref[...]).astype(I32)
    time_here = (moved[0:1] << 5) + moved[1:2] - 1
    rank_here = (moved[2:3] << 5) + moved[3:4] - 1
    for at in range(0, packed, lanes):
        sel_ref[at : at + lanes] = ones_where(iota((lanes, tok_rows), 0) + at == rank_here)
    line = iota((SUMM_ROWS, tok_rows), 0)
    sel_ref[packed : packed + SUMM_ROWS] = ones_where(
        ((time_here >> 6) == line) | (((time_here >> 9) + mids == line) & (time_here >= 0))
    )
    lead = packed + SUMM_ROWS
    near = sel_ref.shape[0] - lead
    sel_ref[lead:] = ones_where((time_here >> 3) == iota((near, tok_rows), 0))
    pools = sel_ref[packed:]
    fcol_ref[...] = 1.0 / jnp.sqrt(jnp.maximum(nn(pools, jnp.ones((tok_rows, lanes), BF)), 1.0))
    frow_ref[...] = 1.0 / jnp.sqrt(jnp.maximum(nt(jnp.ones((16, tok_rows), BF), pools), 1.0))
    rank_column = column(rank_before)
    for at in range(0, packed, lanes):
        e_ref[:, at : at + lanes] = ones_where(rank_column == iota((tok_rows, lanes), 1) + at)
        et_ref[at : at + lanes] = ones_where(iota((lanes, tok_rows), 0) + at == rank_before)
    bias_ref[:tok_rows] = jnp.where(rank_column >= 0, 0.0, HIDE)
    bias_ref[tok_rows:] = jnp.where(column(rank) >= 0, 0.0, HIDE)
    shape = selk_ref.shape
    line = iota(shape, 0)
    step = 2 * SUMM_ROWS
    turn = line // mids
    far = line - 3 * mids
    shard = slab - 1 + turn
    source = jnp.where(
        line < 3 * mids, shard * step + line - turn * mids, far // fars * step + mids + far % fars
    )
    source = jnp.where((line >= 3 * mids) | ((shard >= 0) & (shard < slabs)), source, -step)
    selk_ref[...] = ones_where(source == iota(shape, 1))
    selv_ref[...] = ones_where(source + SUMM_ROWS == iota(shape, 1))
    wt_ref[:group] = jnp.transpose(wq_ref[...])
    wt_ref[group:] = jnp.transpose(wv_ref[...])


def project_kernel(places, *refs):
    count = len(places)
    place_ref, piece_refs, refs = refs[0], refs[1 : count + 1], refs[count + 1 :]
    wt_ref, wk_ref, sel_ref, fcol_ref, frow_ref, comp_ref, summ_ref, k_ref, qv_ref, x_ref = refs
    quarter = x_ref.shape[1] // 4
    head = place_ref[3]
    for piece, (row, distances) in zip(piece_refs, places):
        height = piece.shape[0]
        if distances is None:
            x_ref[row : row + height] = piece[...]
            continue
        for part, distance in enumerate(distances):
            start = pl.multiple_of((head ^ distance) * quarter, quarter)
            x_ref[row : row + height, pl.ds(start, quarter)] = piece[
                :, part * quarter : (part + 1) * quarter
            ]
    group = wk_ref.shape[1]
    packed = comp_ref.shape[0] // 2
    lead = packed + SUMM_ROWS
    x = x_ref[...]
    keys = nn(x, wk_ref[...]).astype(BF)
    k_ref[...] = keys
    vt = nt(wt_ref[group:], x).astype(BF)
    qv_ref[group:] = vt
    sel = sel_ref[:lead]
    kl = nn(sel, keys)
    vl = nt(vt, sel)
    comp_ref[:packed] = kl[:packed].astype(BF)
    vc = vl[:, :packed].astype(BF)
    for part in range(packed // group):
        comp_ref[packed + part * group : packed + (part + 1) * group] = vc[
            :, part * group : (part + 1) * group
        ]
    factor = fcol_ref[:SUMM_ROWS, :1]
    summ_k = (kl[packed:] * factor).astype(BF)
    tail = jnp.concatenate(
        [vl[:, packed:], jnp.zeros((group, 128 - SUMM_ROWS), F32)], axis=1
    )
    summ_v = (jnp.transpose(tail)[:SUMM_ROWS] * factor).astype(BF)
    step = 2 * SUMM_ROWS
    for shard in range(summ_ref.shape[0]):
        summ_ref[shard, :SUMM_ROWS] = summ_k
        summ_ref[shard, SUMM_ROWS:] = summ_v
    qv_ref[:group] = nt(wt_ref[:group], x).astype(BF)


def order_kernel(
    p_ref, pt_ref, sel_ref, fcol_ref, frow_ref, k0_ref, qv_ref, qt_ref, vt_ref, k_ref, nk_ref, nvt_ref
):
    group = k_ref.shape[1]
    near = nk_ref.shape[0]
    k0 = k0_ref[...]
    k_ref[...] = nn(p_ref[...], k0).astype(BF)
    qv = qv_ref[...]
    timed = nn(qv, pt_ref[...])
    qt_ref[...] = (timed[:group] * 0.125).astype(BF)
    vt_ref[...] = timed[group:].astype(BF)
    pool = sel_ref[sel_ref.shape[0] - near :]
    nk_ref[...] = (nn(pool, k0) * fcol_ref[SUMM_ROWS:, :1]).astype(BF)
    nvt_ref[...] = (nt(qv[group:], pool) * frow_ref[:1, SUMM_ROWS:]).astype(BF)


def spread_heads(q4_ref, qt_ref, at, heads):
    width = q4_ref.shape[0] // heads
    for h in range(heads):
        rows = slice(h * width, (h + 1) * width)
        q4_ref[rows, h * FBLK : (h + 1) * FBLK] = qt_ref[rows, at : at + FBLK]


def own_kernel(
    mix_ref, qt_ref, k_ref, vt_ref, bias_ref, nk_ref, nvt_ref, acc_ref, near_ref, top_ref, den_ref, q4_ref, p_ref
):
    tok_rows, group = k_ref.shape
    heads = mix_ref.shape[1]
    width = group // heads
    q4_ref[...] = jnp.zeros_like(q4_ref)
    same = iota((FBLK, FBLK), 0) == iota((FBLK, FBLK), 1)
    nk = nk_ref[...]
    nvt = nvt_ref[...]
    near = nk.shape[0]
    for g in range(tok_rows // FBLK):
        at = g * FBLK
        slot = g % 2
        spread_heads(q4_ref.at[slot], qt_ref, at, heads)
        q4 = q4_ref[slot]
        bias = jnp.where(same, 0.0, bias_ref[tok_rows + at : tok_rows + at + FBLK])
        own_scores = nn(k_ref[at : at + FBLK], q4)
        near_scores = nn(nk, q4)
        scales = []
        for h in range(heads):
            lanes = slice(h * FBLK, (h + 1) * FBLK)
            part = own_scores[:, lanes] + bias
            top = jnp.max(part, axis=0, keepdims=True)
            weight = jnp.exp(part - top)
            top_ref[g : g + 1, lanes] = top
            den_ref[g : g + 1, lanes] = jnp.sum(weight, axis=0, keepdims=True)
            p_ref[slot, :FBLK, lanes] = weight.astype(BF)
            part = near_scores[:, lanes]
            weight = jnp.exp(part - jnp.max(part, axis=0, keepdims=True))
            scales.append(mix_ref[1, h] / jnp.sum(weight, axis=0, keepdims=True))
            p_ref[slot, FBLK:, lanes] = weight.astype(BF)
        own_out = nn(vt_ref[:, at : at + FBLK], p_ref[slot, :FBLK])
        near_out = nn(nvt, p_ref[slot, FBLK:])
        for h in range(heads):
            rows, lanes = slice(h * width, (h + 1) * width), slice(h * FBLK, (h + 1) * FBLK)
            acc_ref[rows, at : at + FBLK] = own_out[rows, lanes]
            near_ref[rows, at : at + FBLK] = near_out[rows, lanes] * scales[h]


def rest_kernel(
    first, blocks, lists_ref, mix_ref, qt_ref, k_ref, vt_ref, comp_ref, e_ref, et_ref, bias_ref, summ_ref,
    selk_ref, selv_ref, acc_ref, near_ref, top_ref, den_ref, out_ref, kw_ref, vw_ref, kc_ref, vc_ref, q4_ref, p_ref,
):
    tok_rows, group = k_ref.shape
    heads = mix_ref.shape[1]
    width = group // heads
    others = FINE_K - 1
    fine = others * FBLK
    mid = 3 * (tok_rows // POOL2)
    far_at = fine + mid
    total = kc_ref.shape[1]
    packed = e_ref.shape[1]
    kw_ref[:tok_rows] = nn(e_ref[...], comp_ref[:packed]).astype(BF)
    kw_ref[tok_rows:] = k_ref[...]
    prev = None
    for part in range(packed // group):
        term = nn(
            comp_ref[packed + part * group : packed + (part + 1) * group],
            et_ref[part * group : (part + 1) * group],
        )
        prev = term if prev is None else prev + term
    vw_ref[:, :tok_rows] = prev.astype(BF)
    vw_ref[:, tok_rows:] = vt_ref[...]
    summ = summ_ref[...]
    coarse_k = nn(selk_ref[...], summ).astype(BF)
    coarse_v = jnp.transpose(nn(selv_ref[...], summ)).astype(BF)
    for slot in range(2):
        kc_ref[slot, fine:] = coarse_k
        vc_ref[slot, :, fine:] = coarse_v
    q4_ref[...] = jnp.zeros_like(q4_ref)
    for index in range(blocks):
        g = first + index
        at = g * FBLK
        slot = index % 2
        biases = []
        for entry in range(others):
            start = pl.multiple_of(lists_ref[g, entry + 1] * FBLK, FBLK)
            kc_ref[slot, entry * FBLK : (entry + 1) * FBLK] = kw_ref[pl.ds(start, FBLK)]
            vc_ref[slot, :, entry * FBLK : (entry + 1) * FBLK] = vw_ref[:, pl.ds(start, FBLK)]
            biases.append(bias_ref[pl.ds(start, FBLK)])
        spread_heads(q4_ref.at[slot], qt_ref, at, heads)
        scores = nn(kc_ref[slot], q4_ref[slot])
        scales, keeps = [], []
        for h in range(heads):
            lanes = slice(h * FBLK, (h + 1) * FBLK)
            parts = [scores[e * FBLK : (e + 1) * FBLK, lanes] + biases[e] for e in range(others)]
            old_top = top_ref[g : g + 1, lanes]
            top = functools.reduce(
                jnp.maximum, [jnp.max(part, axis=0, keepdims=True) for part in parts] + [old_top]
            )
            keep = jnp.exp(old_top - top)
            den = den_ref[g : g + 1, lanes] * keep
            for e, part in enumerate(parts):
                weight = jnp.exp(part - top)
                den = den + jnp.sum(weight, axis=0, keepdims=True)
                p_ref[slot, e * FBLK : (e + 1) * FBLK, lanes] = weight.astype(BF)
            scale = mix_ref[0, h] / den
            scales.append(scale)
            keeps.append(keep * scale)
            for level, (low, high) in enumerate(((fine, far_at), (far_at, total))):
                part = scores[low:high, lanes]
                weight = jnp.exp(part - jnp.max(part, axis=0, keepdims=True))
                share = mix_ref[level + 2, h] / jnp.sum(weight, axis=0, keepdims=True)
                p_ref[slot, low:high, lanes] = (weight * share).astype(BF)
        fine_out = nn(vc_ref[slot, :, :fine], p_ref[slot, :fine])
        coarse_out = nn(vc_ref[slot, :, fine:], p_ref[slot, fine:])
        rows = []
        for h in range(heads):
            pick = (slice(h * width, (h + 1) * width), slice(h * FBLK, (h + 1) * FBLK))
            mine = (pick[0], slice(at, at + FBLK))
            rows.append(
                fine_out[pick] * scales[h]
                + acc_ref[mine] * keeps[h]
                + (coarse_out[pick] + near_ref[mine])
            )
        out_ref[index * FBLK : (index + 1) * FBLK] = jnp.transpose(
            jnp.concatenate(rows, axis=0)
        ).astype(BF)


def output_kernel(place_ref, w_ref, *refs):
    out_ref = refs[-1]
    group = w_ref.shape[1]
    head = place_ref[3]
    total = None
    for distance, part in zip((0, 2, 1, 3), refs[:4]):
        start = pl.multiple_of((head ^ distance) * group, group)
        term = nn(part[...], w_ref[pl.ds(start, group)])
        total = term if total is None else total + term
    out_ref[...] = total.astype(BF)


def local(tokens, w_query, w_key, w_value, w_out, level_mix, fine_blocks, order, mask_ids):
    tok_rows, width = tokens.shape
    slabs = lax.axis_size("seq")
    slab, head = lax.axis_index("seq"), lax.axis_index("head")
    group = w_query.shape[1]
    heads = level_mix.shape[1]
    packed = tok_rows - mask_ids.shape[1]
    near, mids, fars = tok_rows // POOL1, tok_rows // POOL2, tok_rows // POOL3
    coarse = 3 * mids + fars * slabs
    step = 2 * SUMM_ROWS
    chosen = packed + SUMM_ROWS + near

    before_mask = to_next(mask_ids)
    pieces, flip, early = exchange_tokens(tokens, head)
    place = jnp.stack([slab, flip, slabs, head]).astype(I32)
    order, mask_ids, before_mask, w_q, w_v, _ = lax.optimization_barrier(
        (order, mask_ids, before_mask, w_query, w_value, early)
    )

    shape = jax.ShapeDtypeStruct
    params = pltpu.CompilerParams(vmem_limit_bytes=VMEM_LIMIT)
    permute, permute_t, select, f_col, f_row, expand, expand_t, bias, select_k, select_v, w_t = pl.pallas_call(
        prepare_kernel,
        out_shape=(
            shape((tok_rows, tok_rows), BF),
            shape((tok_rows, tok_rows), BF),
            shape((chosen, tok_rows), BF),
            shape((SUMM_ROWS + near, 128), F32),
            shape((16, SUMM_ROWS + near), F32),
            shape((tok_rows, packed), BF),
            shape((packed, tok_rows), BF),
            shape((2 * tok_rows, FBLK), F32),
            shape((coarse, step * slabs), BF),
            shape((coarse, step * slabs), BF),
            shape((2 * group, width), BF),
        ),
        in_specs=smem_specs(1) + vmem_specs(5),
        out_specs=vmem_specs(11),
        compiler_params=params,
        name="prepare",
    )(place, order, mask_ids, before_mask, w_q, w_v)

    places = tuple((row, distances) for _, row, distances in pieces)
    comp, summ, k0, qv0 = pl.pallas_call(
        functools.partial(project_kernel, places),
        out_shape=(
            shape((2 * packed, group), BF),
            shape((slabs, step, group), BF),
            shape((tok_rows, group), BF),
            shape((2 * group, tok_rows), BF),
        ),
        in_specs=smem_specs(1) + vmem_specs(len(pieces) + 5),
        out_specs=vmem_specs(4),
        scratch_shapes=[pltpu.VMEM((tok_rows, width), BF)],
        compiler_params=params,
        name="project",
    )(place, *[piece for piece, _, _ in pieces], w_t, w_key, select, f_col, f_row)
    comp_before = to_next(comp)
    summ_all = lax.all_to_all(summ, "seq", split_axis=0, concat_axis=0, tiled=True).reshape(
        slabs * step, group
    )

    q_t, v_t, keys, near_k, near_vt = pl.pallas_call(
        order_kernel,
        out_shape=(
            shape((group, tok_rows), BF),
            shape((group, tok_rows), BF),
            shape((tok_rows, group), BF),
            shape((near, group), BF),
            shape((group, near), BF),
        ),
        in_specs=vmem_specs(7),
        out_specs=vmem_specs(5),
        compiler_params=params,
        name="order",
    )(permute, permute_t, select, f_col, f_row, k0, qv0)

    blocks = tok_rows // FBLK
    acc, near_out, top, den = pl.pallas_call(
        own_kernel,
        out_shape=(
            shape((group, tok_rows), F32),
            shape((group, tok_rows), F32),
            shape((blocks, heads * FBLK), F32),
            shape((blocks, heads * FBLK), F32),
        ),
        in_specs=smem_specs(1) + vmem_specs(6),
        out_specs=vmem_specs(4),
        scratch_shapes=[
            pltpu.VMEM((2, group, heads * FBLK), BF),
            pltpu.VMEM((2, FBLK + near, heads * FBLK), BF),
        ],
        compiler_params=params,
        name="own",
    )(level_mix, q_t, keys, v_t, bias, near_k, near_vt)

    total = (FINE_K - 1) * FBLK + coarse
    halves = 2
    part_blocks = blocks // halves
    part_rows = tok_rows // halves
    out = None
    for half in range(halves):
        attended = pl.pallas_call(
            functools.partial(rest_kernel, half * part_blocks, part_blocks),
            out_shape=shape((part_rows, group), BF),
            in_specs=smem_specs(2) + vmem_specs(14),
            out_specs=pl.BlockSpec(memory_space=pltpu.VMEM),
            scratch_shapes=[
                pltpu.VMEM((2 * tok_rows, group), BF),
                pltpu.VMEM((group, 2 * tok_rows), BF),
                pltpu.VMEM((2, total, group), BF),
                pltpu.VMEM((2, group, total), BF),
                pltpu.VMEM((2, group, heads * FBLK), BF),
                pltpu.VMEM((2, total, heads * FBLK), BF),
            ],
            compiler_params=params,
            name="rest",
        )(
            fine_blocks, level_mix, q_t, keys, v_t, comp_before, expand, expand_t, bias, summ_all,
            select_k, select_v, acc, near_out, top, den,
        )
        third = over_head(attended, X_PAIRS)
        second = over_head(attended, CORE_PAIRS)
        fourth = over_head(third, CORE_PAIRS)
        steps = 2
        rows = part_rows // steps
        tile = pl.BlockSpec((rows, group), lambda i: (i, 0))
        previous = [] if out is None else [out]
        out = pl.pallas_call(
            output_kernel,
            grid=(steps,),
            out_shape=shape((tok_rows, group), BF),
            in_specs=smem_specs(1)
            + [pl.BlockSpec((width, group), lambda i: (0, 0))]
            + [tile] * 4
            + [pl.BlockSpec(memory_space=pl.ANY)] * len(previous),
            out_specs=pl.BlockSpec((rows, group), lambda i, base=half * steps: (i + base, 0)),
            input_output_aliases={6: 0} if previous else {},
            compiler_params=params,
            name="output",
        )(place, w_out, attended, third, second, fourth, *previous)
    return out


def solution(mesh):
    placed = (
        P("seq", None),
        P(None, "head"),
        P(None, "head"),
        P(None, "head"),
        P(None, "head"),
        P(None, "head"),
        P("seq", None),
        P("seq", None),
        P("seq", None),
    )
    return jax.shard_map(
        local, mesh=mesh, in_specs=placed, out_specs=P("seq", "head"), check_vma=False
    )
```

time: 112 us -> 106 us (0.946)
  the two profiles are of different devices: /device:TPU:17 before, /device:TPU:0 now
where the time goes in v2:
time: 106 us; the launch traced here: 105 us
  local copies, waits for them, and re-layouts  34.2 us (32%)
  starting transfers between devices  29.5 us (28%)
  Pallas kernels  27.7 us (26%)
  waiting for transfers between devices  13.5 us (13%)
    unnamed x88, local copies, waits for them, and re-layouts  30.2 us
    ppermute x7, starting transfers between devices, to_peer(): return lax.ppermute(block, 'seq', [(i, i ^ distance) for i in range(slabs)])  12.6 us
    ppermute x10, waiting for transfers between devices, over_head(): return lax.ppermute(block, 'head', pairs)  10 us
    pallas_call x2, Pallas kernels, local(): pl.pallas_call(functools.partial(rest_kernel, half * part_blocks, part_bl...  9.26 us
    ppermute x2, starting transfers between devices, to_next(): lax.ppermute(block, 'seq', [(i, i + 1) for i in range(lax.axis_size('seq'...  8.09 us
    pallas_call x1, Pallas kernels, local(): pl.pallas_call(functools.partial(project_kernel, places), out_shape=(shap...  4.63 us
    ppermute x10, starting transfers between devices, over_head(): return lax.ppermute(block, 'head', pairs)  4.53 us
    all_to_all x1, starting transfers between devices, local(): lax.all_to_all(summ, 'seq', split_axis=0, concat_axis=0, tiled=True)  4.23 us
  transfers between devices with their start and end apart: 20, of which 8 were waited for; matrix products, arithmetic and copies ran while one was open for 5% of the time, Pallas kernels for 16%

profile of v2, /device:TPU:0, one launch (start us, length us, event | category | flops | bytes accessed | tf_op | source)
XLA Modules:
  0.0 105.3 jit_solution(16437949516854963819)
XLA Ops:
  0.0 1.2 %dynamic-slice_bitcast_fusion.1 = (bf16[128,256]{1,0:T(8,128)(2,1)S(1)}, bf16[128,256]{1,0:T(8,128)(2,1)S(1)}, bf16[128,256]{1,0:T(8,128)(2,1)S(1)}, bf16[128,256]{1,0:T(8,128)(2,1)S(1)}) fusion(bf16[8,128,1024]{2,1,0:T(8,128)(2,1)} %bitcast.21, s32[]{:T(128)S(6)} %select_n.52, s32[]{:T(128)S(6)} %select_n.46, s32[]{:T(128)S(6)} %select_n.50, ...), kind=kLoop, calls=%fused_computation.13 | loop fusion | bytes 524308 | tf_op jit(solution)/shard_map/jit(dynamic_index_in_dim)/squeeze | solution.py:82
  1.2 6.1 %collective-permute-start.1 = (bf16[128,256]{1,0:T(8,128)(2,1)S(1)}, bf16[128,256]{1,0:T(8,128)(2,1)S(1)}, u32[]{:S(2)}, u32[]{:S(2)}) collective-permute-start(bf16[128,256]{1,0:T(8,128)(2,1)S(1)} %get-tuple-element.68), channel_id=1, source_target_pairs={{0,28},{4,24},{8,20},{12,16},{16,12},{20,8},{24,4},{28,0},{1,29},{... | collective-permute-start | bytes 196616 | tf_op jit(solution)/shard_map/ppermute | solution.py:83
  8.2 2.0 %collective-permute-start.4 = (bf16[128,256]{1,0:T(8,128)(2,1)S(1)}, bf16[128,256]{1,0:T(8,128)(2,1)S(1)}, u32[]{:S(2)}, u32[]{:S(2)}) collective-permute-start(bf16[128,256]{1,0:T(8,128)(2,1)S(1)} %get-tuple-element.65), channel_id=1, source_target_pairs={{0,16},{4,20},{8,24},{12,28},{16,0},{20,4},{24,8},{28,12},{1,17},{... | collective-permute-start | bytes 196616 | tf_op jit(solution)/shard_map/ppermute | solution.py:83
  10.3 1.3 %constant_dynamic-slice_fusion.1 = (bf16[8,128,256]{2,1,0:T(8,128)(2,1)S(1)}, bf16[8,128,256]{2,1,0:T(8,128)(2,1)S(1)}) fusion(bf16[8,128,1024]{2,1,0:T(8,128)(2,1)} %bitcast.22, s32[]{:T(128)S(6)} %select_n.45, s32[]{:T(128)S(6)} %select_n.53), kind=kLoop, calls=%fused_computation.25 | loop fusion | bytes 2097160 | tf_op jit(solution)/shard_map/dynamic_slice | solution.py:67
  11.6 2.4 %collective-permute-start.8 = (bf16[128,512]{1,0:T(8,128)(2,1)S(1)}, bf16[128,512]{1,0:T(8,128)(2,1)S(1)}, u32[]{:S(2)}, u32[]{:S(2)}) collective-permute-start(bf16[128,512]{1,0:T(8,128)(2,1)S(1)} %get-tuple-element.70), channel_id=1, source_target_pairs={{0,12},{4,8},{8,4},{12,0},{16,28},{20,24},{24,20},{28,16},{1,13},{... | collective-permute-start | bytes 393224 | tf_op jit(solution)/shard_map/ppermute | solution.py:83
  17.5 1.1 %collective-permute-done.4 = bf16[128,256]{1,0:T(8,128)(2,1)S(1)} collective-permute-done((bf16[128,256]{1,0:T(8,128)(2,1)S(1)}, bf16[128,256]{1,0:T(8,128)(2,1)S(1)}, u32[]{:S(2)}, u32[]{:S(2)}) %collective-permute-start.4) | collective-permute-done | bytes 65568 | tf_op jit(solution)/shard_map/ppermute | solution.py:83
  19.1 1.3 %collective-permute-start.5 = (bf16[512,256]{1,0:T(8,128)(2,1)}, bf16[512,256]{1,0:T(8,128)(2,1)}, u32[]{:S(2)}, u32[]{:S(2)}) collective-permute-start(bf16[512,256]{1,0:T(8,128)(2,1)} %constant_dynamic-update-slice_fusion.refs_1_), channel_id=1, source_target_pairs={{0,2},{2,0},{1,3},{3,1},{4,6},{6,4},{5,7},{7,5},{8,10},{10,8},{9,1... | collective-permute-start | bytes 786440 | tf_op jit(solution)/shard_map/ppermute | solution.py:51
  20.8 1.5 %collective-permute-done.9 = bf16[128,512]{1,0:T(8,128)(2,1)S(1)} collective-permute-done((bf16[128,512]{1,0:T(8,128)(2,1)S(1)}, bf16[128,512]{1,0:T(8,128)(2,1)S(1)}, u32[]{:S(2)}, u32[]{:S(2)}) %collective-permute-start.9) | collective-permute-done | bytes 131104 | tf_op jit(solution)/shard_map/ppermute | solution.py:83
  22.8 4.1 %collective-permute-done.5.refs_2_ = bf16[512,256]{1,0:T(8,128)(2,1)} collective-permute-done((bf16[512,256]{1,0:T(8,128)(2,1)}, bf16[512,256]{1,0:T(8,128)(2,1)}, u32[]{:S(2)}, u32[]{:S(2)}) %collective-permute-start.5) | collective-permute-done | bytes 262176 | tf_op jit(solution)/shard_map/ppermute | solution.py:51
  27.0 3.1 %collective-permute-start = (s32[1,512]{1,0:T(1,128)S(1)}, s32[1,512]{1,0:T(1,128)S(1)}, u32[]{:S(2)}, u32[]{:S(2)}) collective-permute-start(s32[1,512]{1,0:T(1,128)S(1)} %copy-done.36), channel_id=1, source_target_pairs={{0,4},{4,8},{8,12},{12,16},{16,20},{20,24},{24,28},{1,5},{5,9},{9,... | collective-permute-start | bytes 6152 | tf_op jit(solution)/shard_map/ppermute | solution.py:55
  31.9 1.0 copy-done.20
  35.0 4.1 %prepare.1 = (bf16[1024,1024]{1,0:T(8,128)(2,1)S(1)}, bf16[1024,1024]{1,0:T(8,128)(2,1)S(1)}, bf16[672,1024]{1,0:T(8,128)(2,1)S(1)}, f32[160,128]{1,0:T(8,128)S(...) custom-call(s32[4]{0:T(128)S(1)} %pad_add_fusion.place_ref.refs_0_, ...), custom_call_target="tpu_custom_call" | custom-call | tf_op jit(solution)/shard_map/prepare/pallas_call | solution.py:399
  41.2 1.3 %copy-done.10 = bf16[1024,1024]{1,0:T(8,128)(2,1)} copy-done((bf16[1024,1024]{1,0:T(8,128)(2,1)}, bf16[1024,1024]{1,0:T(8,128)(2,1)S(1)}, u32[]{:S(2)}) %copy-start.10) | copy-done | bytes 2097176
  42.5 1.3 %copy-done.12 = bf16[1024,1024]{1,0:T(8,128)(2,1)} copy-done((bf16[1024,1024]{1,0:T(8,128)(2,1)}, bf16[1024,1024]{1,0:T(8,128)(2,1)S(1)}, u32[]{:S(2)}) %copy-start.12) | copy-done | bytes 2097176
  43.9 1.1 %copy-done.21 = bf16[1024,256]{1,0:T(8,128)(2,1)S(1)} copy-done((bf16[1024,256]{1,0:T(8,128)(2,1)S(1)}, bf16[1024,256]{1,0:T(8,128)(2,1)}, u32[]{:S(2)}) %copy-start.21) | copy-done | bytes 524312
  44.9 4.6 %project.1 = (bf16[1024,256]{1,0:T(8,128)(2,1)}, bf16[8,64,256]{2,1,0:T(8,128)(2,1)}, bf16[1024,256]{1,0:T(8,128)(2,1)S(1)}, bf16[512,1024]{1,0:T(8,128)(2,1)S(1)}) custom-call(s32[4]{0:T(128)S(1)} %pad_add_fusion.place_ref.refs_0_, bf16[512,256]{1,0:T(8,128)(2,1)} %constant_dynamic-update-slice_fusion.refs_1_, ...), custom_call_target="tpu_custom_call" | custom-call | tf_op jit(solution)/shard_map/project/pallas_call | solution.py:421
  51.4 5.0 %collective-permute-start.12 = (bf16[1024,256]{1,0:T(8,128)(2,1)}, bf16[1024,256]{1,0:T(8,128)(2,1)}, u32[]{:S(2)}, u32[]{:S(2)}) collective-permute-start(bf16[1024,256]{1,0:T(8,128)(2,1)} %get-tuple-element.50), channel_id=1, source_target_pairs={{0,4},{4,8},{8,12},{12,16},{16,20},{20,24},{24,28},{1,5},{5,9},{9,... | collective-permute-start | bytes 1572872 | tf_op jit(solution)/shard_map/ppermute | solution.py:55
  56.5 4.2 %all-to-all-start = ((bf16[8,64,256]{2,1,0:T(8,128)(2,1)}), bf16[8,64,256]{2,1,0:T(8,128)(2,1)}, u32[]{:S(2)}, u32[]{:S(2)}) async-start(bf16[8,64,256]{2,1,0:T(8,128)(2,1)} %get-tuple-element.54), calls=%async_computation | async-start | bytes 524288 | tf_op jit(solution)/shard_map/all_to_all | solution.py:436
  61.4 1.6 %copy-done.11 = bf16[1024,1024]{1,0:T(8,128)(2,1)S(1)} copy-done((bf16[1024,1024]{1,0:T(8,128)(2,1)S(1)}, bf16[1024,1024]{1,0:T(8,128)(2,1)}, u32[]{:S(2)}) %copy-start.11) | copy-done | bytes 2097176
  63.0 1.6 %copy-done.13 = bf16[1024,1024]{1,0:T(8,128)(2,1)S(1)} copy-done((bf16[1024,1024]{1,0:T(8,128)(2,1)S(1)}, bf16[1024,1024]{1,0:T(8,128)(2,1)}, u32[]{:S(2)}) %copy-start.13) | copy-done | bytes 2097176
  64.6 1.2 %copy-done.16 = bf16[512,1024]{1,0:T(8,128)(2,1)S(1)} copy-done((bf16[512,1024]{1,0:T(8,128)(2,1)S(1)}, bf16[512,1024]{1,0:T(8,128)(2,1)}, u32[]{:S(2)}) %copy-start.16) | copy-done | bytes 1048600
  67.5 2.0 %order.1 = (bf16[256,1024]{1,0:T(8,128)(2,1)S(1)}, bf16[256,1024]{1,0:T(8,128)(2,1)S(1)}, bf16[1024,256]{1,0:T(8,128)(2,1)S(1)}, bf16[128,256]{1,0:T(8,128)(2,1)S(1)}, bf16[256,128]{1,0:T(8,128)(2,1)S(1)}) custom-call(bf16[1024,1024]{1,0:T(8,128)(2,1)S(1)} %copy-done.11, bf16[1024,1024]{1,0:T(8,128)(2,1)S(1)} %copy-done.13, ...), custom_call_target="tpu_custom_call" | custom-call | tf_op jit(solution)/shard_map/order/pallas_call | solution.py:440
  69.6 3.9 %own.1 = (f32[256,1024]{1,0:T(8,128)S(1)}, f32[256,1024]{1,0:T(8,128)S(1)}, f32[8,512]{1,0:T(8,128)S(1)}, f32[8,512]{1,0:T(8,128)S(1)}) custom-call(f32[4,4]{1,0:T(4,128)S(1)} %copy-done.31, bf16[256,1024]{1,0:T(8,128)(2,1)S(1)} %get-tuple-element.47.qt_ref, bf16[1024,256]{1,0:T(8,128)(2,1)S(1)} %get-tuple-element.48.k_ref, ...), custom_call_target="tpu_custom_call" | custom-call | tf_op jit(solution)/shard_map/own/pallas_call | solution.py:456
  78.0 1.2 %copy-done.5 = bf16[512,1024]{1,0:T(8,128)(2,1)S(1)} copy-done((bf16[512,1024]{1,0:T(8,128)(2,1)S(1)}, bf16[512,1024]{1,0:T(8,128)(2,1)}, u32[]{:S(2)}) %copy-start.5) | copy-done | bytes 1048600
  79.2 1.2 %copy-done.7 = f32[256,1024]{1,0:T(8,128)S(1)} copy-done((f32[256,1024]{1,0:T(8,128)S(1)}, f32[256,1024]{1,0:T(8,128)}, u32[]{:S(2)}) %copy-start.7) | copy-done | bytes 1048600
  80.5 1.2 %copy-done.9 = f32[256,1024]{1,0:T(8,128)S(1)} copy-done((f32[256,1024]{1,0:T(8,128)S(1)}, f32[256,1024]{1,0:T(8,128)}, u32[]{:S(2)}) %copy-start.9) | copy-done | bytes 1048600
  83.8 4.6 %rest.3.refs_0_ = bf16[512,256]{1,0:T(8,128)(2,1)S(1)} custom-call(s32[8,4]{1,0:T(8,128)S(1)} %copy-done.30, f32[4,4]{1,0:T(4,128)S(1)} %copy-done.32, bf16[256,1024]{1,0:T(8,128)(2,1)S(1)} %get-tuple-element.47.qt_ref, bf16[1024,256]{1,0:T(8,128)(2,1)S(1)} %copy-done.1, bf16[256,1024]{1,0:T(8,128)(2,1)S(1)} %get-tuple-element.49.vt_ref, ...), custom_call_target="tpu_custom_call" | custom-call | tf_op jit(solution)/shard_map/rest/pallas_call | solution.py:480
  88.4 1.5 %collective-permute-start.16 = (bf16[512,256]{1,0:T(8,128)(2,1)S(1)}, bf16[512,256]{1,0:T(8,128)(2,1)S(1)}, u32[]{:S(2)}, u32[]{:S(2)}) collective-permute-start(bf16[512,256]{1,0:T(8,128)(2,1)S(1)} %rest.3.refs_0_), channel_id=1, source_target_pairs={{0,2},{2,0},{1,3},{3,1},{4,6},{6,4},{5,7},{7,5},{8,10},{10,8},{9,1... | collective-permute-start | bytes 786440 | tf_op jit(solution)/shard_map/ppermute | solution.py:51
  89.9 4.6 %rest.2.refs_0_ = bf16[512,256]{1,0:T(8,128)(2,1)S(1)} custom-call(s32[8,4]{1,0:T(8,128)S(1)} %copy-done.30, f32[4,4]{1,0:T(4,128)S(1)} %copy-done.32, bf16[256,1024]{1,0:T(8,128)(2,1)S(1)} %get-tuple-element.47.qt_ref, bf16[1024,256]{1,0:T(8,128)(2,1)S(1)} %copy-done.1, bf16[256,1024]{1,0:T(8,128)(2,1)S(1)} %get-tuple-element.49.vt_ref, ...), custom_call_target="tpu_custom_call" | custom-call | tf_op jit(solution)/shard_map/rest/pallas_call | solution.py:480
  96.3 5.3 %collective-permute-done.13.refs_1_ = bf16[512,256]{1,0:T(8,128)(2,1)S(1)} collective-permute-done((bf16[512,256]{1,0:T(8,128)(2,1)S(1)}, bf16[512,256]{1,0:T(8,128)(2,1)S(1)}, u32[]{:S(2)}, u32[]{:S(2)}) %collective-permute-start.13) | collective-permute-done | bytes 262176 | tf_op jit(solution)/shard_map/ppermute | solution.py:51
  101.6 1.9 %output.2.refs_4_ = bf16[1024,256]{1,0:T(8,128)(2,1)} custom-call(s32[4]{0:T(128)S(1)} %copy-done.34, bf16[1024,256]{1,0:T(8,128)(2,1)S(1)} %copy-done.14, bf16[512,256]{1,0:T(8,128)(2,1)S(1)} %rest.3.refs_0_, bf16[512,256]{1,0:T(8,128)(2,1)S(1)} %collective-permute-done.16.refs_1_, bf16[512,256]{1,0:T(8,128)(2,1)S(1)} %collective-permute-done.17.refs_2_, ...), custom_call_target="tpu_custom_call" | custom-call | tf_op jit(solution)/shard_map/output/pallas_call | solution.py:506
  103.5 1.9 %output.3 = bf16[1024,256]{1,0:T(8,128)(2,1)} custom-call(s32[4]{0:T(128)S(1)} %copy-done.34, bf16[1024,256]{1,0:T(8,128)(2,1)S(1)} %copy-done.14, bf16[512,256]{1,0:T(8,128)(2,1)S(1)} %rest.2.refs_0_, bf16[512,256]{1,0:T(8,128)(2,1)S(1)} %collective-permute-done.13.refs_1_, ...), custom_call_target="tpu_custom_call", output_to_operand_aliasing={{}: (6, {})} | custom-call | tf_op jit(solution)/shard_map/output/pallas_call | solution.py:506
  (111 shorter events, 24.5 us)
Async XLA Ops:
  1.2 12.8 %collective-permute-start.1 = (bf16[128,256]{1,0:T(8,128)(2,1)S(1)}, bf16[128,256]{1,0:T(8,128)(2,1)S(1)}, u32[]{:S(2)}, u32[]{:S(2)}) collective-permute-start(bf16[128,256]{1,0:T(8,128)(2,1)S(1)} %get-tuple-element.68), channel_id=1, source_target_pairs={{0,28},{4,24},{8,20},{12,16},{16,12},{20,8},{24,4},{28,0},{1,29},{... | collective-permute-start | bytes 196616 | tf_op jit(solution)/shard_map/ppermute | solution.py:83
  7.3 8.2 %collective-permute-start.2 = (bf16[128,256]{1,0:T(8,128)(2,1)S(1)}, bf16[128,256]{1,0:T(8,128)(2,1)S(1)}, u32[]{:S(2)}, u32[]{:S(2)}) collective-permute-start(bf16[128,256]{1,0:T(8,128)(2,1)S(1)} %get-tuple-element.67), channel_id=1, source_target_pairs={{0,24},{4,28},{8,16},{12,20},{16,8},{20,12},{24,0},{28,4},{1,25},{... | collective-permute-start | bytes 196616 | tf_op jit(solution)/shard_map/ppermute | solution.py:83
  7.5 9.4 %collective-permute-start.3 = (bf16[128,256]{1,0:T(8,128)(2,1)S(1)}, bf16[128,256]{1,0:T(8,128)(2,1)S(1)}, u32[]{:S(2)}, u32[]{:S(2)}) collective-permute-start(bf16[128,256]{1,0:T(8,128)(2,1)S(1)} %get-tuple-element.66), channel_id=1, source_target_pairs={{0,20},{4,16},{8,28},{12,24},{16,4},{20,0},{24,12},{28,8},{1,21},{... | collective-permute-start | bytes 196616 | tf_op jit(solution)/shard_map/ppermute | solution.py:83
  8.2 10.3 %collective-permute-start.4 = (bf16[128,256]{1,0:T(8,128)(2,1)S(1)}, bf16[128,256]{1,0:T(8,128)(2,1)S(1)}, u32[]{:S(2)}, u32[]{:S(2)}) collective-permute-start(bf16[128,256]{1,0:T(8,128)(2,1)S(1)} %get-tuple-element.65), channel_id=1, source_target_pairs={{0,16},{4,20},{8,24},{12,28},{16,0},{20,4},{24,8},{28,12},{1,17},{... | collective-permute-start | bytes 196616 | tf_op jit(solution)/shard_map/ppermute | solution.py:83
  10.3 16.7 %copy-start.36 = (s32[1,512]{1,0:T(1,128)S(1)}, s32[1,512]{1,0:T(1,128)}, u32[]{:S(2)}) copy-start(s32[1,512]{1,0:T(1,128)} %mask_ref) | copy-start | bytes 6148
  11.6 20.4 %copy-start.19 = (bf16[1024,256]{1,0:T(8,128)(2,1)S(1)}, bf16[1024,256]{1,0:T(8,128)(2,1)}, u32[]{:S(2)}) copy-start(bf16[1024,256]{1,0:T(8,128)(2,1)} %wq_ref) | copy-start | bytes 1572868
  11.6 9.1 %collective-permute-start.8 = (bf16[128,512]{1,0:T(8,128)(2,1)S(1)}, bf16[128,512]{1,0:T(8,128)(2,1)S(1)}, u32[]{:S(2)}, u32[]{:S(2)}) collective-permute-start(bf16[128,512]{1,0:T(8,128)(2,1)S(1)} %get-tuple-element.70), channel_id=1, source_target_pairs={{0,12},{4,8},{8,4},{12,0},{16,28},{20,24},{24,20},{28,16},{1,13},{... | collective-permute-start | bytes 393224 | tf_op jit(solution)/shard_map/ppermute | solution.py:83
  14.0 8.2 %collective-permute-start.9 = (bf16[128,512]{1,0:T(8,128)(2,1)S(1)}, bf16[128,512]{1,0:T(8,128)(2,1)S(1)}, u32[]{:S(2)}, u32[]{:S(2)}) collective-permute-start(bf16[128,512]{1,0:T(8,128)(2,1)S(1)} %get-tuple-element.71), channel_id=1, source_target_pairs={{0,8},{4,12},{8,0},{12,4},{16,24},{20,28},{24,16},{28,20},{1,9},{5... | collective-permute-start | bytes 393224 | tf_op jit(solution)/shard_map/ppermute | solution.py:83
  15.4 6.8 %collective-permute-start.10 = (bf16[128,512]{1,0:T(8,128)(2,1)S(1)}, bf16[128,512]{1,0:T(8,128)(2,1)S(1)}, u32[]{:S(2)}, u32[]{:S(2)}) collective-permute-start(bf16[128,512]{1,0:T(8,128)(2,1)S(1)} %get-tuple-element.69), channel_id=1, source_target_pairs={{0,4},{4,0},{8,12},{12,8},{16,20},{20,16},{24,28},{28,24},{1,5},{5... | collective-permute-start | bytes 393224 | tf_op jit(solution)/shard_map/ppermute | solution.py:83
  19.1 7.8 %collective-permute-start.5 = (bf16[512,256]{1,0:T(8,128)(2,1)}, bf16[512,256]{1,0:T(8,128)(2,1)}, u32[]{:S(2)}, u32[]{:S(2)}) collective-permute-start(bf16[512,256]{1,0:T(8,128)(2,1)} %constant_dynamic-update-slice_fusion.refs_1_), channel_id=1, source_target_pairs={{0,2},{2,0},{1,3},{3,1},{4,6},{6,4},{5,7},{7,5},{8,10},{10,8},{9,1... | collective-permute-start | bytes 786440 | tf_op jit(solution)/shard_map/ppermute | solution.py:51
  22.3 21.6 %collective-permute-start.11 = (bf16[384,512]{1,0:T(8,128)(2,1)S(1)}, bf16[384,512]{1,0:T(8,128)(2,1)}, u32[]{:S(2)}, u32[]{:S(2)}) collective-permute-start(bf16[384,512]{1,0:T(8,128)(2,1)S(1)} %constant_dynamic-update-slice_fusion.4.refs_5_), channel_id=1, source_target_pairs={{0,1},{1,0},{2,3},{3,2},{4,5},{5,4},{6,7},{7,6},{8,9},{9,8},{10,11... | collective-permute-start | bytes 1179656 | tf_op jit(solution)/shard_map/ppermute | solution.py:51
  22.3 21.5 %collective-permute-start.6 = (bf16[512,256]{1,0:T(8,128)(2,1)}, bf16[512,256]{1,0:T(8,128)(2,1)}, u32[]{:S(2)}, u32[]{:S(2)}) collective-permute-start(bf16[512,256]{1,0:T(8,128)(2,1)} %constant_dynamic-update-slice_fusion.refs_1_), channel_id=1, source_target_pairs={{0,1},{1,0},{2,3},{3,2},{4,5},{5,4},{6,7},{7,6},{8,9},{9,8},{10,11... | collective-permute-start | bytes 786440 | tf_op jit(solution)/shard_map/ppermute | solution.py:51
  27.0 16.9 %collective-permute-start.7 = (bf16[512,256]{1,0:T(8,128)(2,1)}, bf16[512,256]{1,0:T(8,128)(2,1)}, u32[]{:S(2)}, u32[]{:S(2)}) collective-permute-start(bf16[512,256]{1,0:T(8,128)(2,1)} %collective-permute-done.5.refs_2_), channel_id=1, source_target_pairs={{0,1},{1,0},{2,3},{3,2},{4,5},{5,4},{6,7},{7,6},{8,9},{9,8},{10,11... | collective-permute-start | bytes 786440 | tf_op jit(solution)/shard_map/ppermute | solution.py:51
  27.0 4.4 %collective-permute-start = (s32[1,512]{1,0:T(1,128)S(1)}, s32[1,512]{1,0:T(1,128)S(1)}, u32[]{:S(2)}, u32[]{:S(2)}) collective-permute-start(s32[1,512]{1,0:T(1,128)S(1)} %copy-done.36), channel_id=1, source_target_pairs={{0,4},{4,8},{8,12},{12,16},{16,20},{20,24},{24,28},{1,5},{5,9},{9,... | collective-permute-start | bytes 6152 | tf_op jit(solution)/shard_map/ppermute | solution.py:55
  31.1 18.5 %copy-start.33 = (s32[4]{0:T(128)}, s32[4]{0:T(128)S(1)}, u32[]{:S(2)}) copy-start(s32[4]{0:T(128)S(1)} %pad_add_fusion.place_ref.refs_0_) | copy-start | bytes 52
  43.8 5.8 %copy-start.22 = (bf16[64,512]{1,0:T(8,128)(2,1)}, bf16[64,512]{1,0:T(8,128)(2,1)S(1)}, u32[]{:S(2)}) copy-start(bf16[64,512]{1,0:T(8,128)(2,1)S(1)} %get-tuple-element.55.selk_ref) | copy-start | bytes 196612
  43.8 5.8 %copy-start.24 = (bf16[64,512]{1,0:T(8,128)(2,1)}, bf16[64,512]{1,0:T(8,128)(2,1)S(1)}, u32[]{:S(2)}) copy-start(bf16[64,512]{1,0:T(8,128)(2,1)S(1)} %get-tuple-element.56.selv_ref) | copy-start | bytes 196612
  43.8 5.8 %copy-start.26 = (f32[16,160]{1,0:T(8,128)}, f32[16,160]{1,0:T(8,128)S(1)}, u32[]{:S(2)}) copy-start(f32[16,160]{1,0:T(8,128)S(1)} %get-tuple-element.43.refs_12_.frow_ref) | copy-start | bytes 30724
  44.9 15.8 %copy-start.40 = (s32[8,4]{0,1:T(4,128)S(1)}, s32[8,4]{0,1:T(4,128)}, u32[]{:S(2)}) copy-start(s32[8,4]{0,1:T(4,128)} %param.15) | copy-start | bytes 388
  51.4 25.5 %collective-permute-start.12 = (bf16[1024,256]{1,0:T(8,128)(2,1)}, bf16[1024,256]{1,0:T(8,128)(2,1)}, u32[]{:S(2)}, u32[]{:S(2)}) collective-permute-start(bf16[1024,256]{1,0:T(8,128)(2,1)} %get-tuple-element.50), channel_id=1, source_target_pairs={{0,4},{4,8},{8,12},{12,16},{16,20},{20,24},{24,28},{1,5},{5,9},{9,... | collective-permute-start | bytes 1572872 | tf_op jit(solution)/shard_map/ppermute | solution.py:55
  56.5 20.5 %all-to-all-start = ((bf16[8,64,256]{2,1,0:T(8,128)(2,1)}), bf16[8,64,256]{2,1,0:T(8,128)(2,1)}, u32[]{:S(2)}, u32[]{:S(2)}) async-start(bf16[8,64,256]{2,1,0:T(8,128)(2,1)} %get-tuple-element.54), calls=%async_computation | async-start | bytes 524288 | tf_op jit(solution)/shard_map/all_to_all | solution.py:436
  69.6 7.4 %copy-start.3 = (bf16[1024,512]{1,0:T(8,128)(2,1)S(1)}, bf16[1024,512]{1,0:T(8,128)(2,1)}, u32[]{:S(2)}) copy-start(bf16[1024,512]{1,0:T(8,128)(2,1)} %copy-done.2) | copy-start | bytes 3145732
  69.6 7.4 %copy-start.23 = (bf16[64,512]{1,0:T(8,128)(2,1)S(1)}, bf16[64,512]{1,0:T(8,128)(2,1)}, u32[]{:S(2)}) copy-start(bf16[64,512]{1,0:T(8,128)(2,1)} %copy-done.22) | copy-start | bytes 196612
  69.6 7.4 %copy-start.25 = (bf16[64,512]{1,0:T(8,128)(2,1)S(1)}, bf16[64,512]{1,0:T(8,128)(2,1)}, u32[]{:S(2)}) copy-start(bf16[64,512]{1,0:T(8,128)(2,1)} %copy-done.24) | copy-start | bytes 196612
  88.4 13.2 %copy-start.14 = (bf16[1024,256]{1,0:T(8,128)(2,1)S(1)}, bf16[1024,256]{1,0:T(8,128)(2,1)}, u32[]{:S(2)}) copy-start(bf16[1024,256]{1,0:T(8,128)(2,1)} %w_ref.3) | copy-start | bytes 1572868
  88.4 13.2 %copy-start.34 = (s32[4]{0:T(128)S(1)}, s32[4]{0:T(128)}, u32[]{:S(2)}) copy-start(s32[4]{0:T(128)} %copy-done.33) | copy-start | bytes 52
  88.4 7.4 %collective-permute-start.16 = (bf16[512,256]{1,0:T(8,128)(2,1)S(1)}, bf16[512,256]{1,0:T(8,128)(2,1)S(1)}, u32[]{:S(2)}, u32[]{:S(2)}) collective-permute-start(bf16[512,256]{1,0:T(8,128)(2,1)S(1)} %rest.3.refs_0_), channel_id=1, source_target_pairs={{0,2},{2,0},{1,3},{3,1},{4,6},{6,4},{5,7},{7,5},{8,10},{10,8},{9,1... | collective-permute-start | bytes 786440 | tf_op jit(solution)/shard_map/ppermute | solution.py:51
  94.5 7.1 %collective-permute-start.13 = (bf16[512,256]{1,0:T(8,128)(2,1)S(1)}, bf16[512,256]{1,0:T(8,128)(2,1)S(1)}, u32[]{:S(2)}, u32[]{:S(2)}) collective-permute-start(bf16[512,256]{1,0:T(8,128)(2,1)S(1)} %rest.2.refs_0_), channel_id=1, source_target_pairs={{0,2},{2,0},{1,3},{3,1},{4,6},{6,4},{5,7},{7,5},{8,10},{10,8},{9,1... | collective-permute-start | bytes 786440 | tf_op jit(solution)/shard_map/ppermute | solution.py:51
  95.2 6.4 %collective-permute-start.17 = (bf16[512,256]{1,0:T(8,128)(2,1)S(1)}, bf16[512,256]{1,0:T(8,128)(2,1)S(1)}, u32[]{:S(2)}, u32[]{:S(2)}) collective-permute-start(bf16[512,256]{1,0:T(8,128)(2,1)S(1)} %rest.3.refs_0_), channel_id=1, source_target_pairs={{0,1},{1,0},{2,3},{3,2},{4,5},{5,4},{6,7},{7,6},{8,9},{9,8},{10,11... | collective-permute-start | bytes 786440 | tf_op jit(solution)/shard_map/ppermute | solution.py:51
  95.8 5.8 %collective-permute-start.18 = (bf16[512,256]{1,0:T(8,128)(2,1)S(1)}, bf16[512,256]{1,0:T(8,128)(2,1)S(1)}, u32[]{:S(2)}, u32[]{:S(2)}) collective-permute-start(bf16[512,256]{1,0:T(8,128)(2,1)S(1)} %collective-permute-done.16.refs_1_), channel_id=1, source_target_pairs={{0,1},{1,0},{2,3},{3,2},{4,5},{5,4},{6,7},{7,6},{8,9},{9,8},{10,11... | collective-permute-start | bytes 786440 | tf_op jit(solution)/shard_map/ppermute | solution.py:51
  95.8 7.7 %collective-permute-start.14 = (bf16[512,256]{1,0:T(8,128)(2,1)S(1)}, bf16[512,256]{1,0:T(8,128)(2,1)S(1)}, u32[]{:S(2)}, u32[]{:S(2)}) collective-permute-start(bf16[512,256]{1,0:T(8,128)(2,1)S(1)} %rest.2.refs_0_), channel_id=1, source_target_pairs={{0,1},{1,0},{2,3},{3,2},{4,5},{5,4},{6,7},{7,6},{8,9},{9,8},{10,11... | collective-permute-start | bytes 786440 | tf_op jit(solution)/shard_map/ppermute | solution.py:51
  101.6 1.9 %collective-permute-start.15 = (bf16[512,256]{1,0:T(8,128)(2,1)S(1)}, bf16[512,256]{1,0:T(8,128)(2,1)S(1)}, u32[]{:S(2)}, u32[]{:S(2)}) collective-permute-start(bf16[512,256]{1,0:T(8,128)(2,1)S(1)} %collective-permute-done.13.refs_1_), channel_id=1, source_target_pairs={{0,1},{1,0},{2,3},{3,2},{4,5},{5,4},{6,7},{7,6},{8,9},{9,8},{10,11... | collective-permute-start | bytes 786440 | tf_op jit(solution)/shard_map/ppermute | solution.py:51
  (29 other events, 29.7 us)

commit v3 on v2

v3 whole, which is shorter than its diff:
```python
import functools

import jax
import jax.numpy as jnp
from jax import lax
from jax.experimental import pallas as pl
from jax.experimental.pallas import tpu as pltpu
from jax.sharding import PartitionSpec as P

FBLK = 128
FINE_K = 4
POOL1 = 8
POOL2 = 64
POOL3 = 512
SUMM_ROWS = 32
BF = jnp.bfloat16
F32 = jnp.float32
I32 = jnp.int32
HIDE = -1e30
VMEM_LIMIT = 24 * 1024 * 1024

X_PAIRS = [(0, 2), (2, 0), (1, 3), (3, 1)]
CORE_PAIRS = [(0, 1), (1, 0), (2, 3), (3, 2)]


def nn(a, b):
    return lax.dot_general(a, b, (((1,), (0,)), ((), ())), preferred_element_type=F32)


def nt(a, b):
    return lax.dot_general(a, b, (((1,), (1,)), ((), ())), preferred_element_type=F32)


def iota(shape, axis):
    return lax.broadcasted_iota(I32, shape, axis)


def ones_where(condition):
    return jnp.where(condition, 1.0, 0.0).astype(BF)


def vmem_specs(count):
    return [pl.BlockSpec(memory_space=pltpu.VMEM)] * count


def smem_specs(count):
    return [pl.BlockSpec(memory_space=pltpu.SMEM)] * count


def over_head(block, pairs):
    return lax.ppermute(block, "head", pairs)


def to_next(block):
    return lax.ppermute(block, "seq", [(i, i + 1) for i in range(lax.axis_size("seq") - 1)])


def stack_kernel(counts, *refs):
    sources, targets = refs[: sum(counts)], refs[sum(counts) :]
    for count, target in zip(counts, targets):
        height = target.shape[0] // count
        for index in range(count):
            target[index * height : (index + 1) * height] = sources[index][...]
        sources = sources[count:]


def stacked(*lists):
    parts = [part for one in lists for part in one]
    return pl.pallas_call(
        functools.partial(stack_kernel, tuple(len(one) for one in lists)),
        out_shape=tuple(
            jax.ShapeDtypeStruct((len(one) * one[0].shape[0], one[0].shape[1]), one[0].dtype)
            for one in lists
        ),
        in_specs=vmem_specs(len(parts)),
        out_specs=vmem_specs(len(lists)),
        compiler_params=pltpu.CompilerParams(vmem_limit_bytes=VMEM_LIMIT),
        name="stack",
    )(*parts)


def by_distance(block, distance):
    return lax.ppermute(block, "seq", [(i, i ^ distance) for i in range(lax.axis_size("seq"))])


def exchange_tokens(tokens, head, prepare):
    tok_rows, width = tokens.shape
    slabs = lax.axis_size("seq")
    rows = tok_rows // slabs
    quarter = width // 4
    slab = lax.axis_index("seq")
    split = tokens.reshape(slabs, rows, width)

    def columns(other):
        return lax.dynamic_slice_in_dim(split, (head ^ other) * quarter, quarter, axis=2)

    mine = columns(0)
    if slabs != 8:
        first = lax.all_to_all(mine, "seq", split_axis=0, concat_axis=0, tiled=True).reshape(
            tok_rows, quarter
        )
        third = over_head(first, X_PAIRS)
        second = over_head(first, CORE_PAIRS)
        fourth = over_head(third, CORE_PAIRS)
        pieces = [(first, 0, (0,)), (third, 0, (2,)), (second, 0, (1,)), (fourth, 0, (3,))]
        return pieces, prepare(first)
    both = jnp.concatenate([mine, columns(2)], axis=2)

    def to_peer(source, distance):
        block = lax.dynamic_index_in_dim(source, slab ^ distance, axis=0, keepdims=False)
        return by_distance(block, distance)

    far, near = stacked(
        [to_peer(mine, d) for d in (7, 6, 5, 4)], [to_peer(both, d) for d in (3, 2, 1)]
    )
    far_x = over_head(far, X_PAIRS)
    near_core = over_head(near, CORE_PAIRS)
    far_core = over_head(far, CORE_PAIRS)
    prepared = prepare(far)
    far_x, prepared = lax.optimization_barrier((far_x, prepared))
    far_last = over_head(far_x, CORE_PAIRS)
    pieces = [(far, 0, (0,)), (far_x, 0, (2,)), (far_core, 0, (1,)), (far_last, 0, (3,))]
    pieces += [(near, 4 * rows, (0, 2)), (near_core, 4 * rows, (1, 3)), (tokens, 7 * rows, None)]
    return pieces, prepared


def column(row, lanes=128):
    return jnp.transpose(jnp.broadcast_to(row.astype(F32), (lanes, row.shape[1]))).astype(I32)


def ranks(ids, tok_rows, lanes=128):
    hidden = column(ids)
    parts = []
    for at in range(0, tok_rows, lanes):
        time = iota((1, lanes), 1) + at
        count = jnp.sum(jnp.where(hidden < time, 1.0, 0.0), axis=0, keepdims=True)
        here = jnp.sum(jnp.where(hidden == time, 1.0, 0.0), axis=0, keepdims=True)
        parts.append(jnp.where(here == 0.0, time - count.astype(I32), -1))
    return jnp.concatenate(parts, axis=1)


def prepare_kernel(
    order_ref, mask_ref, wq_ref, wv_ref, early_ref,
    p_ref, pt_ref, sel_ref, fcol_ref, frow_ref, bias_ref, wt_ref,
):
    slab, slabs = lax.axis_index("seq"), lax.axis_size("seq")
    tok_rows = order_ref.shape[1]
    packed = tok_rows - mask_ref.shape[1]
    flip = (slab ^ 7) * (tok_rows // slabs) if slabs == 8 else 0
    mids = tok_rows // POOL2
    group = wq_ref.shape[1]
    lanes = 128

    place = order_ref[...] ^ flip
    place_column = column(place)
    for at in range(0, tok_rows, lanes):
        p_ref[:, at : at + lanes] = ones_where(place_column == iota((tok_rows, lanes), 1) + at)
        pt_ref[at : at + lanes] = ones_where(iota((lanes, tok_rows), 0) + at == place)
    rank = ranks(mask_ref[...], tok_rows)
    time = jnp.where(rank >= 0, iota((1, tok_rows), 1), -1) + 1
    line = iota((16, tok_rows), 0)
    stack = jnp.where(
        line == 0,
        time >> 5,
        jnp.where(
            line == 1,
            time & 31,
            jnp.where(line == 2, (rank + 1) >> 5, jnp.where(line == 3, (rank + 1) & 31, 0)),
        ),
    )
    moved = nn(stack.astype(F32).astype(BF), p_ref[...]).astype(I32)
    time_here = (moved[0:1] << 5) + moved[1:2] - 1
    rank_here = (moved[2:3] << 5) + moved[3:4] - 1
    for at in range(0, packed, lanes):
        sel_ref[at : at + lanes] = ones_where(iota((lanes, tok_rows), 0) + at == rank_here)
    line = iota((SUMM_ROWS, tok_rows), 0)
    sel_ref[packed : packed + SUMM_ROWS] = ones_where(
        ((time_here >> 6) == line) | (((time_here >> 9) + mids == line) & (time_here >= 0))
    )
    lead = packed + SUMM_ROWS
    near = sel_ref.shape[0] - lead
    sel_ref[lead:] = ones_where((time_here >> 3) == iota((near, tok_rows), 0))
    pools = sel_ref[packed:]
    fcol_ref[...] = 1.0 / jnp.sqrt(jnp.maximum(nn(pools, jnp.ones((tok_rows, lanes), BF)), 1.0))
    frow_ref[...] = 1.0 / jnp.sqrt(jnp.maximum(nt(jnp.ones((16, tok_rows), BF), pools), 1.0))
    bias_ref[...] = jnp.where(column(rank) >= 0, 0.0, HIDE)
    wt_ref[:group] = jnp.transpose(wq_ref[...])
    wt_ref[group:] = jnp.transpose(wv_ref[...])


def project_kernel(places, *refs):
    count = len(places)
    piece_refs, refs = refs[:count], refs[count:]
    wt_ref, wk_ref, sel_ref, fcol_ref, comp_ref, summ_ref, k_ref, v_ref, x_ref, sem_ref = refs
    quarter = x_ref.shape[1] // 4
    head = lax.axis_index("head")
    loads = []
    for piece, (row, distances) in zip(piece_refs, places):
        height = piece.shape[0]
        if distances is None:
            rows = height // lax.axis_size("seq")
            start = pl.multiple_of(lax.axis_index("seq") * rows, rows)
            loads.append(
                pltpu.make_async_copy(
                    piece.at[pl.ds(start, rows)], x_ref.at[row : row + rows], sem_ref
                )
            )
            loads[-1].start()
    for piece, (row, distances) in zip(piece_refs, places):
        height = piece.shape[0]
        if distances is None:
            continue
        for part, distance in enumerate(distances):
            start = pl.multiple_of((head ^ distance) * quarter, quarter)
            x_ref[row : row + height, pl.ds(start, quarter)] = piece[
                :, part * quarter : (part + 1) * quarter
            ]
    group = wk_ref.shape[1]
    packed = comp_ref.shape[0] // 2
    lead = packed + SUMM_ROWS
    for load in loads:
        load.wait()
    x = x_ref[...]
    keys = nn(x, wk_ref[...]).astype(BF)
    k_ref[...] = keys
    vt = nt(wt_ref[group:], x).astype(BF)
    v_ref[...] = vt
    sel = sel_ref[:lead]
    kl = nn(sel, keys)
    vl = nt(vt, sel)
    comp_ref[:packed] = kl[:packed].astype(BF)
    vc = vl[:, :packed].astype(BF)
    for part in range(packed // group):
        comp_ref[packed + part * group : packed + (part + 1) * group] = vc[
            :, part * group : (part + 1) * group
        ]
    factor = fcol_ref[:SUMM_ROWS, :1]
    summ_k = (kl[packed:] * factor).astype(BF)
    tail = jnp.concatenate(
        [vl[:, packed:], jnp.zeros((group, 128 - SUMM_ROWS), F32)], axis=1
    )
    summ_v = (jnp.transpose(tail)[:SUMM_ROWS] * factor).astype(BF)
    summ_ref[:SUMM_ROWS] = summ_k
    summ_ref[SUMM_ROWS:] = summ_v


def spread_heads(q4_ref, qt_ref, at, heads):
    width = q4_ref.shape[0] // heads
    for h in range(heads):
        rows = slice(h * width, (h + 1) * width)
        q4_ref[rows, h * FBLK : (h + 1) * FBLK] = qt_ref[rows, at : at + FBLK]


def own_kernel(
    mix_ref, before_ref, p_in, pt_ref, sel_ref, fcol_ref, frow_ref, wt_ref, x_ref, k0_ref, v0_ref, seen_ref,
    qt_ref, vt_ref, k_ref, acc_ref, near_ref, top_ref, den_ref, e_ref, et_ref, bias_ref, q4_ref, p_ref,
):
    tok_rows, group = k_ref.shape
    heads = mix_ref.shape[1]
    width = group // heads
    near = tok_rows // POOL1
    q4_ref[...] = jnp.zeros_like(q4_ref)
    same = iota((FBLK, FBLK), 0) == iota((FBLK, FBLK), 1)
    k0, v0 = k0_ref[...], v0_ref[...]
    q0 = nt(wt_ref[:group], x_ref[...]).astype(BF)
    k_ref[...] = nn(p_in[...], k0).astype(BF)
    qt_ref[...] = (nn(q0, pt_ref[...]) * 0.125).astype(BF)
    vt_ref[...] = nn(v0, pt_ref[...]).astype(BF)
    pool = sel_ref[sel_ref.shape[0] - near :]
    nk = (nn(pool, k0) * fcol_ref[SUMM_ROWS:, :1]).astype(BF)
    nvt = (nt(v0, pool) * frow_ref[:1, SUMM_ROWS:]).astype(BF)
    for g in range(tok_rows // FBLK):
        at = g * FBLK
        slot = g % 2
        spread_heads(q4_ref.at[slot], qt_ref, at, heads)
        q4 = q4_ref[slot]
        bias = jnp.where(same, 0.0, seen_ref[at : at + FBLK])
        own_scores = nn(k_ref[at : at + FBLK], q4)
        near_scores = nn(nk, q4)
        scales = []
        for h in range(heads):
            lanes = slice(h * FBLK, (h + 1) * FBLK)
            part = own_scores[:, lanes] + bias
            top = jnp.max(part, axis=0, keepdims=True)
            weight = jnp.exp(part - top)
            top_ref[g : g + 1, lanes] = top
            den_ref[g : g + 1, lanes] = jnp.sum(weight, axis=0, keepdims=True)
            p_ref[slot, :FBLK, lanes] = weight.astype(BF)
            part = near_scores[:, lanes]
            weight = jnp.exp(part - jnp.max(part, axis=0, keepdims=True))
            scales.append(mix_ref[1, h] / jnp.sum(weight, axis=0, keepdims=True))
            p_ref[slot, FBLK:, lanes] = weight.astype(BF)
        own_out = nn(vt_ref[:, at : at + FBLK], p_ref[slot, :FBLK])
        near_out = nn(nvt, p_ref[slot, FBLK:])
        for h in range(heads):
            rows, lanes = slice(h * width, (h + 1) * width), slice(h * FBLK, (h + 1) * FBLK)
            acc_ref[rows, at : at + FBLK] = own_out[rows, lanes]
            near_ref[rows, at : at + FBLK] = near_out[rows, lanes] * scales[h]
    rank = jnp.where(lax.axis_index("seq") > 0, ranks(before_ref[...], tok_rows), -1)
    rank_column = column(rank)
    bias_ref[:tok_rows] = jnp.where(rank_column >= 0, 0.0, HIDE)
    bias_ref[tok_rows:] = seen_ref[...]
    for at in range(0, et_ref.shape[0], FBLK):
        e_ref[:, at : at + FBLK] = ones_where(rank_column == iota((tok_rows, FBLK), 1) + at)
        et_ref[at : at + FBLK] = ones_where(iota((FBLK, tok_rows), 0) + at == rank)


def window_kernel(k_ref, vt_ref, comp_ref, e_ref, et_ref, *refs):
    summ_refs, (kw_ref, vw_ref, ck_ref, cv_ref, all_ref) = refs[:-5], refs[-5:]
    tok_rows, group = k_ref.shape
    packed = e_ref.shape[1]
    kw_ref[:tok_rows] = nn(e_ref[...], comp_ref[:packed]).astype(BF)
    kw_ref[tok_rows:] = k_ref[...]
    prev = None
    for part in range(packed // group):
        term = nn(
            comp_ref[packed + part * group : packed + (part + 1) * group],
            et_ref[part * group : (part + 1) * group],
        )
        prev = term if prev is None else prev + term
    vw_ref[:, :tok_rows] = prev.astype(BF)
    vw_ref[:, tok_rows:] = vt_ref[...]
    at = 0
    for part in summ_refs:
        all_ref[at : at + part.shape[0]] = part[...]
        at += part.shape[0]
    slab, slabs = lax.axis_index("seq"), lax.axis_size("seq")
    mids, fars = tok_rows // POOL2, tok_rows // POOL3
    shape = (ck_ref.shape[0], all_ref.shape[0])
    line = iota(shape, 0)
    step = 2 * SUMM_ROWS
    turn = line // mids
    far = line - 3 * mids
    shard = slab - 1 + turn
    turned = slab if slabs == 8 else 0
    source = jnp.where(
        line < 3 * mids,
        (shard ^ turned) * step + line - turn * mids,
        ((far // fars) ^ turned) * step + mids + far % fars,
    )
    source = jnp.where((line >= 3 * mids) | ((shard >= 0) & (shard < slabs)), source, -step)
    gathered = all_ref[...]
    ck_ref[...] = nn(ones_where(source == iota(shape, 1)), gathered).astype(BF)
    values = nn(ones_where(source + SUMM_ROWS == iota(shape, 1)), gathered)
    cv_ref[...] = jnp.transpose(values).astype(BF)


def rest_kernel(
    first, blocks, lists_ref, mix_ref, qt_ref, kw_ref, vw_ref, ck_ref, cv_ref, bias_ref,
    acc_ref, near_ref, top_ref, den_ref, out_ref, kc_ref, vc_ref, q4_ref, p_ref,
):
    group, tok_rows = qt_ref.shape
    heads = mix_ref.shape[1]
    width = group // heads
    others = FINE_K - 1
    fine = others * FBLK
    mid = 3 * (tok_rows // POOL2)
    far_at = fine + mid
    total = kc_ref.shape[1]
    for slot in range(2):
        kc_ref[slot, fine:] = ck_ref[...]
        vc_ref[slot, :, fine:] = cv_ref[...]
    q4_ref[...] = jnp.zeros_like(q4_ref)
    for index in range(blocks):
        g = first + index
        at = g * FBLK
        slot = index % 2
        biases = []
        for entry in range(others):
            start = pl.multiple_of(lists_ref[entry + 1, g] * FBLK, FBLK)
            kc_ref[slot, entry * FBLK : (entry + 1) * FBLK] = kw_ref[pl.ds(start, FBLK)]
            vc_ref[slot, :, entry * FBLK : (entry + 1) * FBLK] = vw_ref[:, pl.ds(start, FBLK)]
            biases.append(bias_ref[pl.ds(start, FBLK)])
        spread_heads(q4_ref.at[slot], qt_ref, at, heads)
        scores = nn(kc_ref[slot], q4_ref[slot])
        scales, keeps = [], []
        for h in range(heads):
            lanes = slice(h * FBLK, (h + 1) * FBLK)
            parts = [scores[e * FBLK : (e + 1) * FBLK, lanes] + biases[e] for e in range(others)]
            old_top = top_ref[g : g + 1, lanes]
            top = functools.reduce(
                jnp.maximum, [jnp.max(part, axis=0, keepdims=True) for part in parts] + [old_top]
            )
            keep = jnp.exp(old_top - top)
            den = den_ref[g : g + 1, lanes] * keep
            for e, part in enumerate(parts):
                weight = jnp.exp(part - top)
                den = den + jnp.sum(weight, axis=0, keepdims=True)
                p_ref[slot, e * FBLK : (e + 1) * FBLK, lanes] = weight.astype(BF)
            scale = mix_ref[0, h] / den
            scales.append(scale)
            keeps.append(keep * scale)
            for level, (low, high) in enumerate(((fine, far_at), (far_at, total))):
                part = scores[low:high, lanes]
                weight = jnp.exp(part - jnp.max(part, axis=0, keepdims=True))
                share = mix_ref[level + 2, h] / jnp.sum(weight, axis=0, keepdims=True)
                p_ref[slot, low:high, lanes] = (weight * share).astype(BF)
        fine_out = nn(vc_ref[slot, :, :fine], p_ref[slot, :fine])
        coarse_out = nn(vc_ref[slot, :, fine:], p_ref[slot, fine:])
        rows = []
        for h in range(heads):
            pick = (slice(h * width, (h + 1) * width), slice(h * FBLK, (h + 1) * FBLK))
            mine = (pick[0], slice(at, at + FBLK))
            rows.append(
                fine_out[pick] * scales[h]
                + acc_ref[mine] * keeps[h]
                + (coarse_out[pick] + near_ref[mine])
            )
        out_ref[index * FBLK : (index + 1) * FBLK] = jnp.transpose(
            jnp.concatenate(rows, axis=0)
        ).astype(BF)


def output_kernel(w_ref, *refs):
    out_ref = refs[-1]
    group = w_ref.shape[1]
    head = lax.axis_index("head")
    total = None
    for distance, part in zip((0, 2, 1, 3), refs[:4]):
        start = pl.multiple_of((head ^ distance) * group, group)
        term = nn(part[...], w_ref[pl.ds(start, group)])
        total = term if total is None else total + term
    out_ref[...] = total.astype(BF)


def local(tokens, w_query, w_key, w_value, w_out, level_mix, fine_blocks, order, mask_ids):
    tok_rows, width = tokens.shape
    slabs = lax.axis_size("seq")
    slab, head = lax.axis_index("seq"), lax.axis_index("head")
    group = w_query.shape[1]
    heads = level_mix.shape[1]
    packed = tok_rows - mask_ids.shape[1]
    near, mids, fars = tok_rows // POOL1, tok_rows // POOL2, tok_rows // POOL3
    coarse = 3 * mids + fars * slabs
    step = 2 * SUMM_ROWS
    chosen = packed + SUMM_ROWS + near

    shape = jax.ShapeDtypeStruct
    params = pltpu.CompilerParams(vmem_limit_bytes=VMEM_LIMIT)
    before_mask = to_next(mask_ids)

    def prepare(early):
        return pl.pallas_call(
            prepare_kernel,
            out_shape=(
                shape((tok_rows, tok_rows), BF),
                shape((tok_rows, tok_rows), BF),
                shape((chosen, tok_rows), BF),
                shape((SUMM_ROWS + near, 128), F32),
                shape((16, SUMM_ROWS + near), F32),
                shape((tok_rows, FBLK), F32),
                shape((2 * group, width), BF),
            ),
            in_specs=vmem_specs(4) + [pl.BlockSpec(memory_space=pl.ANY)],
            out_specs=vmem_specs(7),
            compiler_params=params,
            name="prepare",
        )(order, mask_ids, w_query, w_value, early)

    pieces, prepared = exchange_tokens(tokens, head, prepare)
    permute, permute_t, select, f_col, f_row, seen, w_t = prepared
    places = tuple((row, distances) for _, row, distances in pieces)
    comp, summ, k0, v0, rows_here = pl.pallas_call(
        functools.partial(project_kernel, places),
        out_shape=(
            shape((2 * packed, group), BF),
            shape((step, group), BF),
            shape((tok_rows, group), BF),
            shape((group, tok_rows), BF),
            shape((tok_rows, width), BF),
        ),
        in_specs=[
            pl.BlockSpec(memory_space=pltpu.VMEM if distances else pl.ANY)
            for _, distances in places
        ]
        + vmem_specs(4),
        out_specs=vmem_specs(5),
        scratch_shapes=[pltpu.SemaphoreType.DMA],
        compiler_params=params,
        name="project",
    )(*[piece for piece, _, _ in pieces], w_t, w_key, select, f_col)
    comp_before = to_next(comp)
    if slabs == 8:
        summaries = [summ] + [by_distance(summ, d) for d in range(1, slabs)]
    else:
        copies = jnp.broadcast_to(summ[None], (slabs, step, group))
        copies = lax.all_to_all(copies, "seq", split_axis=0, concat_axis=0, tiled=True)
        summaries = [copies.reshape(slabs * step, group)]

    blocks = tok_rows // FBLK
    q_t, v_t, keys, acc, near_out, top, den, expand, expand_t, bias = pl.pallas_call(
        own_kernel,
        out_shape=(
            shape((group, tok_rows), BF),
            shape((group, tok_rows), BF),
            shape((tok_rows, group), BF),
            shape((group, tok_rows), F32),
            shape((group, tok_rows), F32),
            shape((blocks, heads * FBLK), F32),
            shape((blocks, heads * FBLK), F32),
            shape((tok_rows, packed), BF),
            shape((packed, tok_rows), BF),
            shape((2 * tok_rows, FBLK), F32),
        ),
        in_specs=smem_specs(1) + vmem_specs(11),
        out_specs=vmem_specs(10),
        scratch_shapes=[
            pltpu.VMEM((2, group, heads * FBLK), BF),
            pltpu.VMEM((2, FBLK + near, heads * FBLK), BF),
        ],
        compiler_params=params,
        name="own",
    )(level_mix, before_mask, permute, permute_t, select, f_col, f_row, w_t, rows_here, k0, v0, seen)

    window_k, window_v, coarse_k, coarse_v = pl.pallas_call(
        window_kernel,
        out_shape=(
            shape((2 * tok_rows, group), BF),
            shape((group, 2 * tok_rows), BF),
            shape((coarse, group), BF),
            shape((group, coarse), BF),
        ),
        in_specs=vmem_specs(5 + len(summaries)),
        out_specs=vmem_specs(4),
        scratch_shapes=[pltpu.VMEM((slabs * step, group), BF)],
        compiler_params=params,
        name="window",
    )(keys, v_t, comp_before, expand, expand_t, *summaries)

    total = (FINE_K - 1) * FBLK + coarse
    lists = fine_blocks.T
    halves = 2
    part_blocks = blocks // halves
    part_rows = tok_rows // halves
    out = None
    for half in range(halves):
        attended = pl.pallas_call(
            functools.partial(rest_kernel, half * part_blocks, part_blocks),
            out_shape=shape((part_rows, group), BF),
            in_specs=smem_specs(2) + vmem_specs(10),
            out_specs=pl.BlockSpec(memory_space=pltpu.VMEM),
            scratch_shapes=[
                pltpu.VMEM((2, total, group), BF),
                pltpu.VMEM((2, group, total), BF),
                pltpu.VMEM((2, group, heads * FBLK), BF),
                pltpu.VMEM((2, total, heads * FBLK), BF),
            ],
            compiler_params=params,
            name="rest",
        )(
            lists, level_mix, q_t, window_k, window_v, coarse_k, coarse_v, bias, acc, near_out, top, den
        )
        third = over_head(attended, X_PAIRS)
        second = over_head(attended, CORE_PAIRS)
        if out is not None:
            third, out = lax.optimization_barrier((third, out))
        fourth = over_head(third, CORE_PAIRS)
        steps = 2
        rows = part_rows // steps
        tile = pl.BlockSpec((rows, group), lambda i: (i, 0))
        previous = [] if out is None else [out]
        out = pl.pallas_call(
            output_kernel,
            grid=(steps,),
            out_shape=shape((tok_rows, group), BF),
            in_specs=[pl.BlockSpec((width, group), lambda i: (0, 0))]
            + [tile] * 4
            + [pl.BlockSpec(memory_space=pl.ANY)] * len(previous),
            out_specs=pl.BlockSpec((rows, group), lambda i, base=half * steps: (i + base, 0)),
            input_output_aliases={5: 0} if previous else {},
            compiler_params=params,
            name="output",
        )(w_out, attended, third, second, fourth, *previous)
    return out


def solution(mesh):
    placed = (
        P("seq", None),
        P(None, "head"),
        P(None, "head"),
        P(None, "head"),
        P(None, "head"),
        P(None, "head"),
        P("seq", None),
        P("seq", None),
        P("seq", None),
    )
    return jax.shard_map(
        local, mesh=mesh, in_specs=placed, out_specs=P("seq", "head"), check_vma=False
    )
```

time: 106 us -> 90 us (0.85)
  local copies, waits for them, and re-layouts: 34.2 us -> 3.56 us
  waiting for transfers between devices: 13.5 us -> 28.7 us
  Pallas kernels: 27.7 us -> 22.2 us
  starting transfers between devices: 29.5 us -> 33.9 us
    unnamed x88 -> x18, local copies, waits for them, and re-layouts: 30.2 us -> 0.04 us
    ppermute x7 -> x14, starting transfers between devices: 12.6 us -> 21.7 us  [by_distance(): lax.ppermute(block, 'seq', [(i, i ^ distance) for i in range(lax.axis_siz...]
    ppermute x10, waiting for transfers between devices: 10 us -> 16.3 us  [over_head(): return lax.ppermute(block, 'head', pairs)]
    ppermute x2, waiting for transfers between devices: 0.23 us -> 5.46 us  [to_next(): lax.ppermute(block, 'seq', [(i, i + 1) for i in range(lax.axis_size('seq'...]
    all_to_all x1 -> x0, starting transfers between devices: 4.23 us -> none  [local(): lax.all_to_all(summ, 'seq', split_axis=0, concat_axis=0, tiled=True)]
    ppermute x7 -> x14, waiting for transfers between devices: 3.22 us -> 6.98 us  [by_distance(): lax.ppermute(block, 'seq', [(i, i ^ distance) for i in range(lax.axis_siz...]
    pallas_call x2, Pallas kernels: 9.26 us -> 6.79 us  [local(): pl.pallas_call(functools.partial(rest_kernel, half * part_blocks, part_bl...]
    pallas_call x1, Pallas kernels: 4.63 us -> 2.32 us  [local(): pl.pallas_call(functools.partial(project_kernel, places), out_shape=(shap...]
  transfers between devices with their start and end apart: 20 -> 26, of which waited for: 8 -> 8; matrix products, arithmetic and copies ran while one was open for 5% -> 4% of each run, Pallas kernels for 16% -> 16%
where the time goes in v3:
time: 90 us; the launch traced here: 89.7 us
  starting transfers between devices  33.9 us (38%)
  waiting for transfers between devices  28.7 us (32%)
  Pallas kernels  22.2 us (25%)
  local copies, waits for them, and re-layouts  3.56 us (4%)
  other arithmetic  1.17 us (1%)
    ppermute x14, starting transfers between devices, by_distance(): lax.ppermute(block, 'seq', [(i, i ^ distance) for i in range(lax.axis_siz...  21.7 us
    ppermute x10, waiting for transfers between devices, over_head(): return lax.ppermute(block, 'head', pairs)  16.3 us
    pallas_call x1, Pallas kernels, local(): pl.pallas_call(own_kernel, out_shape=(shape((group, tok_rows), BF), shape...  7.03 us
    ppermute x2, starting transfers between devices, to_next(): lax.ppermute(block, 'seq', [(i, i + 1) for i in range(lax.axis_size('seq'...  7 us
    ppermute x14, waiting for transfers between devices, by_distance(): lax.ppermute(block, 'seq', [(i, i ^ distance) for i in range(lax.axis_siz...  6.98 us
    pallas_call x2, Pallas kernels, local(): pl.pallas_call(functools.partial(rest_kernel, half * part_blocks, part_bl...  6.79 us
    ppermute x2, waiting for transfers between devices, to_next(): lax.ppermute(block, 'seq', [(i, i + 1) for i in range(lax.axis_size('seq'...  5.46 us
    ppermute x10, starting transfers between devices, over_head(): return lax.ppermute(block, 'head', pairs)  5.21 us
  transfers between devices with their start and end apart: 26, of which 8 were waited for; matrix products, arithmetic and copies ran while one was open for 4% of the time, Pallas kernels for 16%

profile of v3, /device:TPU:0, one launch (start us, length us, event | category | flops | bytes accessed | tf_op | source)
XLA Modules:
  0.0 89.7 jit_solution(15393758998711209479)
XLA Ops:
  0.0 1.2 %dynamic-slice_bitcast_fusion = (bf16[128,256]{1,0:T(8,128)(2,1)S(1)}, bf16[128,256]{1,0:T(8,128)(2,1)S(1)}, bf16[128,256]{1,0:T(8,128)(2,1)S(1)}, bf16[128,256]{1,0:T(8,128)(2,1)S(1)}) fusion(bf16[8,128,1024]{2,1,0:T(8,128)(2,1)} %bitcast.16, s32[]{:T(128)S(6)} %select_n.48, s32[]{:T(128)S(6)} %select_n.42, s32[]{:T(128)S(6)} %select_n.46, ...), kind=kLoop, calls=%fused_computation.12 | loop fusion | bytes 524308 | tf_op jit(solution)/shard_map/jit(dynamic_index_in_dim)/squeeze | solution.py:110
  1.2 4.1 %collective-permute-start.4 = (bf16[128,256]{1,0:T(8,128)(2,1)S(1)}, bf16[128,256]{1,0:T(8,128)(2,1)S(1)}, u32[]{:S(2)}, u32[]{:S(2)}) collective-permute-start(bf16[128,256]{1,0:T(8,128)(2,1)S(1)} %get-tuple-element.83), channel_id=1, source_target_pairs={{0,16},{4,20},{8,24},{12,28},{16,0},{20,4},{24,8},{28,12},{1,17},{... | collective-permute-start | bytes 196616 | tf_op jit(solution)/shard_map/ppermute | solution.py:83
  5.3 1.3 %collective-permute-start.3 = (bf16[128,256]{1,0:T(8,128)(2,1)S(1)}, bf16[128,256]{1,0:T(8,128)(2,1)S(1)}, u32[]{:S(2)}, u32[]{:S(2)}) collective-permute-start(bf16[128,256]{1,0:T(8,128)(2,1)S(1)} %get-tuple-element.84), channel_id=1, source_target_pairs={{0,20},{4,16},{8,28},{12,24},{16,4},{20,0},{24,12},{28,8},{1,21},{... | collective-permute-start | bytes 196616 | tf_op jit(solution)/shard_map/ppermute | solution.py:83
  6.6 2.3 %constant_dynamic-slice_fusion.1 = (bf16[8,128,256]{2,1,0:T(8,128)(2,1)}, bf16[8,128,256]{2,1,0:T(8,128)(2,1)}) fusion(bf16[8,128,1024]{2,1,0:T(8,128)(2,1)} %bitcast.17, s32[]{:T(128)S(6)} %select_n.41, s32[]{:T(128)S(6)} %select_n.49), kind=kLoop, calls=%fused_computation.17 | loop fusion | bytes 2097160 | tf_op jit(solution)/shard_map/dynamic_slice | solution.py:95
  8.9 1.2 %fusion.5 = (bf16[128,512]{1,0:T(8,128)(2,1)S(1)}, bf16[128,512]{1,0:T(8,128)(2,1)S(1)}, bf16[128,512]{1,0:T(8,128)(2,1)S(1)}) fusion(s32[]{:T(128)S(6)} %select_n.52, bf16[8,128,256]{2,1,0:T(8,128)(2,1)} %get-tuple-element.82, bf16[8,128,256]{2,1,0:T(8,128)(2,1)} %get-tuple-element.81, s32[]{:T(128)S(6)} %select_n.50, s32[]{:T(128)S(6)} %select_n.51), kind=kLoop, calls=%fused_computation.11 | loop fusion | flops 786432 | bytes 1441804 | tf_op jit(solution)/shard_map/jit(dynamic_index_in_dim)/squeeze | solution.py:110
  10.4 2.8 %collective-permute-start.5 = (bf16[128,512]{1,0:T(8,128)(2,1)S(1)}, bf16[128,512]{1,0:T(8,128)(2,1)S(1)}, u32[]{:S(2)}, u32[]{:S(2)}) collective-permute-start(bf16[128,512]{1,0:T(8,128)(2,1)S(1)} %get-tuple-element.88), channel_id=1, source_target_pairs={{0,12},{4,8},{8,4},{12,0},{16,28},{20,24},{24,20},{28,16},{1,13},{... | collective-permute-start | bytes 393224 | tf_op jit(solution)/shard_map/ppermute | solution.py:83
  13.7 3.6 %collective-permute-start.2 = (bf16[128,256]{1,0:T(8,128)(2,1)S(1)}, bf16[128,256]{1,0:T(8,128)(2,1)S(1)}, u32[]{:S(2)}, u32[]{:S(2)}) collective-permute-start(bf16[128,256]{1,0:T(8,128)(2,1)S(1)} %get-tuple-element.85), channel_id=1, source_target_pairs={{0,24},{4,28},{8,16},{12,20},{16,8},{20,12},{24,0},{28,4},{1,25},{... | collective-permute-start | bytes 196616 | tf_op jit(solution)/shard_map/ppermute | solution.py:83
  17.3 5.7 %collective-permute-done.2.refs_1_ = bf16[128,256]{1,0:T(8,128)(2,1)S(1)} collective-permute-done((bf16[128,256]{1,0:T(8,128)(2,1)S(1)}, bf16[128,256]{1,0:T(8,128)(2,1)S(1)}, u32[]{:S(2)}, u32[]{:S(2)}) %collective-permute-start.2) | collective-permute-done | bytes 65568 | tf_op jit(solution)/shard_map/ppermute | solution.py:83
  23.0 1.2 %collective-permute-done.1.refs_0_ = bf16[128,256]{1,0:T(8,128)(2,1)S(1)} collective-permute-done((bf16[128,256]{1,0:T(8,128)(2,1)S(1)}, bf16[128,256]{1,0:T(8,128)(2,1)S(1)}, u32[]{:S(2)}, u32[]{:S(2)}) %collective-permute-start.1) | collective-permute-done | bytes 65568 | tf_op jit(solution)/shard_map/ppermute | solution.py:83
  24.3 1.6 %collective-permute-start.8 = (bf16[512,256]{1,0:T(8,128)(2,1)S(1)}, bf16[512,256]{1,0:T(8,128)(2,1)S(1)}, u32[]{:S(2)}, u32[]{:S(2)}) collective-permute-start(bf16[512,256]{1,0:T(8,128)(2,1)S(1)} %get-tuple-element.43.early_ref.refs_0_), channel_id=1, source_target_pairs={{0,2},{2,0},{1,3},{3,1},{4,6},{6,4},{5,7},{7,5},{8,10},{10,8},{9,1... | collective-permute-start | bytes 786440 | tf_op jit(solution)/shard_map/ppermute | solution.py:51
  26.4 2.5 %prepare.1 = (bf16[1024,1024]{1,0:T(8,128)(2,1)S(1)}, bf16[1024,1024]{1,0:T(8,128)(2,1)S(1)}, bf16[672,1024]{1,0:T(8,128)(2,1)S(1)}, f32[160,128]{1,0:T(8,128)S(...) custom-call(s32[1,1024]{1,0:T(1,128)S(1)} %copy-done.7, ...), custom_call_target="tpu_custom_call" | custom-call | tf_op jit(solution)/shard_map/prepare/pallas_call | solution.py:443
  28.9 1.8 %collective-permute-done.8.refs_1_ = bf16[512,256]{1,0:T(8,128)(2,1)S(1)} collective-permute-done((bf16[512,256]{1,0:T(8,128)(2,1)S(1)}, bf16[512,256]{1,0:T(8,128)(2,1)S(1)}, u32[]{:S(2)}, u32[]{:S(2)}) %collective-permute-start.8) | collective-permute-done | bytes 262176 | tf_op jit(solution)/shard_map/ppermute | solution.py:51
  30.8 1.5 %collective-permute-done.10.refs_3_ = bf16[512,256]{1,0:T(8,128)(2,1)S(1)} collective-permute-done((bf16[512,256]{1,0:T(8,128)(2,1)S(1)}, bf16[512,256]{1,0:T(8,128)(2,1)S(1)}, u32[]{:S(2)}, u32[]{:S(2)}) %collective-permute-start.10) | collective-permute-done | bytes 262176 | tf_op jit(solution)/shard_map/ppermute | solution.py:51
  32.3 2.3 %project.1 = (bf16[1024,256]{1,0:T(8,128)(2,1)S(1)}, bf16[64,256]{1,0:T(8,128)(2,1)S(1)}, bf16[1024,256]{1,0:T(8,128)(2,1)S(1)}, bf16[256,1024]{1,0:T(8,128)(2,1)S(1)}, bf16[1024,1024]{1,0:T(8,128)(2,1)S(1)}) custom-call(bf16[512,256]{1,0:T(8,128)(2,1)S(1)} %get-tuple-element.43.early_ref.refs_0_, bf16[512,256]{1,0:T(8,128)(2,1)S(1)} %collective-permute-done.8.refs_1_, ...), custom_call_target="tpu_custom_call" | custom-call | tf_op jit(solution)/shard_map/project/pallas_call | solution.py:463
  34.6 2.9 %collective-permute-start.12 = (bf16[1024,256]{1,0:T(8,128)(2,1)S(1)}, bf16[1024,256]{1,0:T(8,128)(2,1)S(1)}, u32[]{:S(2)}, u32[]{:S(2)}) collective-permute-start(bf16[1024,256]{1,0:T(8,128)(2,1)S(1)} %get-tuple-element.66), channel_id=1, source_target_pairs={{0,4},{4,8},{8,12},{12,16},{16,20},{20,24},{24,28},{1,5},{5,9},{9,... | collective-permute-start | bytes 1572872 | tf_op jit(solution)/shard_map/ppermute | solution.py:55
  37.8 3.0 %collective-permute-start.18 = (bf16[64,256]{1,0:T(8,128)(2,1)S(1)}, bf16[64,256]{1,0:T(8,128)(2,1)S(1)}, u32[]{:S(2)}, u32[]{:S(2)}) collective-permute-start(bf16[64,256]{1,0:T(8,128)(2,1)S(1)} %get-tuple-element.69.refs_0_), channel_id=1, source_target_pairs={{0,24},{4,28},{8,16},{12,20},{16,8},{20,12},{24,0},{28,4},{1,25},{... | collective-permute-start | bytes 98312 | tf_op jit(solution)/shard_map/ppermute | solution.py:83
  40.8 4.1 %collective-permute-start = (s32[1,512]{1,0:T(1,128)S(1)}, s32[1,512]{1,0:T(1,128)S(1)}, u32[]{:S(2)}, u32[]{:S(2)}) collective-permute-start(s32[1,512]{1,0:T(1,128)S(1)} %copy-done.8), channel_id=1, source_target_pairs={{0,4},{4,8},{8,12},{12,16},{16,20},{20,24},{24,28},{1,5},{5,9},{9,... | collective-permute-start | bytes 6152 | tf_op jit(solution)/shard_map/ppermute | solution.py:55
  44.9 5.5 %collective-permute-done.before_ref = s32[1,512]{1,0:T(1,128)S(1)} collective-permute-done((s32[1,512]{1,0:T(1,128)S(1)}, s32[1,512]{1,0:T(1,128)S(1)}, u32[]{:S(2)}, u32[]{:S(2)}) %collective-permute-start) | collective-permute-done | bytes 2080 | tf_op jit(solution)/shard_map/ppermute | solution.py:55
  50.4 1.8 %collective-permute-start.16 = (bf16[64,256]{1,0:T(8,128)(2,1)S(1)}, bf16[64,256]{1,0:T(8,128)(2,1)S(1)}, u32[]{:S(2)}, u32[]{:S(2)}) collective-permute-start(bf16[64,256]{1,0:T(8,128)(2,1)S(1)} %get-tuple-element.69.refs_0_), channel_id=1, source_target_pairs={{0,16},{4,20},{8,24},{12,28},{16,0},{20,4},{24,8},{28,12},{1,17},{... | collective-permute-start | bytes 98312 | tf_op jit(solution)/shard_map/ppermute | solution.py:83
  52.2 2.2 %collective-permute-start.15 = (bf16[64,256]{1,0:T(8,128)(2,1)S(1)}, bf16[64,256]{1,0:T(8,128)(2,1)S(1)}, u32[]{:S(2)}, u32[]{:S(2)}) collective-permute-start(bf16[64,256]{1,0:T(8,128)(2,1)S(1)} %get-tuple-element.69.refs_0_), channel_id=1, source_target_pairs={{0,12},{4,8},{8,4},{12,0},{16,28},{20,24},{24,20},{28,16},{1,13},{... | collective-permute-start | bytes 98312 | tf_op jit(solution)/shard_map/ppermute | solution.py:83
  54.8 1.5 %collective-permute-start.13 = (bf16[64,256]{1,0:T(8,128)(2,1)S(1)}, bf16[64,256]{1,0:T(8,128)(2,1)S(1)}, u32[]{:S(2)}, u32[]{:S(2)}) collective-permute-start(bf16[64,256]{1,0:T(8,128)(2,1)S(1)} %get-tuple-element.69.refs_0_), channel_id=1, source_target_pairs={{0,4},{4,0},{8,12},{12,8},{16,20},{20,16},{24,28},{28,24},{1,5},{5... | collective-permute-start | bytes 98312 | tf_op jit(solution)/shard_map/ppermute | solution.py:83
  56.2 7.0 %own.1 = (bf16[256,1024]{1,0:T(8,128)(2,1)S(1)}, bf16[256,1024]{1,0:T(8,128)(2,1)S(1)}, bf16[1024,256]{1,0:T(8,128)(2,1)S(1)}, f32[256,1024]{1,0:T(8,128)S(1)}, ...) custom-call(f32[4,4]{1,0:T(4,128)S(1)} %copy-done.5, ...), custom_call_target="tpu_custom_call" | custom-call | tf_op jit(solution)/shard_map/own/pallas_call | solution.py:491
  63.3 0.9 %window.1 = (bf16[2048,256]{1,0:T(8,128)(2,1)S(1)}, bf16[256,2048]{1,0:T(8,128)(2,1)S(1)}, bf16[64,256]{1,0:T(8,128)(2,1)S(1)}, bf16[256,64]{1,0:T(8,128)(2,1)S(1)}) custom-call(bf16[1024,256]{1,0:T(8,128)(2,1)S(1)} %get-tuple-element.64.k_ref, bf16[256,1024]{1,0:T(8,128)(2,1)S(1)} %get-tuple-element.65.vt_ref, ...), custom_call_target="tpu_custom_call" | custom-call | tf_op jit(solution)/shard_map/window/pallas_call | solution.py:515
  64.3 3.4 %rest.3.refs_0_ = bf16[512,256]{1,0:T(8,128)(2,1)S(1)} custom-call(s32[4,8]{1,0:T(4,128)S(1)} %bitcast.18, f32[4,4]{1,0:T(4,128)S(1)} %copy-done.5, bf16[256,1024]{1,0:T(8,128)(2,1)S(1)} %get-tuple-element.63.qt_ref, bf16[2048,256]{1,0:T(8,128)(2,1)S(1)} %get-tuple-element.70.kw_ref, bf16[256,2048]{1,0:T(8,128)(2,1)S(1)} %get-tuple-element.71.vw_ref, ...), custom_call_target="tpu_custom_call" | custom-call | tf_op jit(solution)/shard_map/rest/pallas_call | solution.py:537
  67.7 1.5 %collective-permute-start.21 = (bf16[512,256]{1,0:T(8,128)(2,1)S(1)}, bf16[512,256]{1,0:T(8,128)(2,1)S(1)}, u32[]{:S(2)}, u32[]{:S(2)}) collective-permute-start(bf16[512,256]{1,0:T(8,128)(2,1)S(1)} %rest.3.refs_0_), channel_id=1, source_target_pairs={{0,2},{2,0},{1,3},{3,1},{4,6},{6,4},{5,7},{7,5},{8,10},{10,8},{9,1... | collective-permute-start | bytes 786440 | tf_op jit(solution)/shard_map/ppermute | solution.py:51
  69.1 5.6 %collective-permute-done.21.refs_1_ = bf16[512,256]{1,0:T(8,128)(2,1)S(1)} collective-permute-done((bf16[512,256]{1,0:T(8,128)(2,1)S(1)}, bf16[512,256]{1,0:T(8,128)(2,1)S(1)}, u32[]{:S(2)}, u32[]{:S(2)}) %collective-permute-start.21) | collective-permute-done | bytes 262176 | tf_op jit(solution)/shard_map/ppermute | solution.py:51
  74.7 3.4 %rest.2.refs_0_ = bf16[512,256]{1,0:T(8,128)(2,1)S(1)} custom-call(s32[4,8]{1,0:T(4,128)S(1)} %bitcast.19, f32[4,4]{1,0:T(4,128)S(1)} %copy-done.5, bf16[256,1024]{1,0:T(8,128)(2,1)S(1)} %get-tuple-element.63.qt_ref, bf16[2048,256]{1,0:T(8,128)(2,1)S(1)} %get-tuple-element.70.kw_ref, bf16[256,2048]{1,0:T(8,128)(2,1)S(1)} %get-tuple-element.71.vw_ref, ...), custom_call_target="tpu_custom_call" | custom-call | tf_op jit(solution)/shard_map/rest/pallas_call | solution.py:537
  78.1 1.5 %collective-permute-start.20 = (bf16[512,256]{1,0:T(8,128)(2,1)S(1)}, bf16[512,256]{1,0:T(8,128)(2,1)S(1)}, u32[]{:S(2)}, u32[]{:S(2)}) collective-permute-start(bf16[512,256]{1,0:T(8,128)(2,1)S(1)} %rest.2.refs_0_), channel_id=1, source_target_pairs={{0,2},{2,0},{1,3},{3,1},{4,6},{6,4},{5,7},{7,5},{8,10},{10,8},{9,1... | collective-permute-start | bytes 786440 | tf_op jit(solution)/shard_map/ppermute | solution.py:51
  79.8 1.3 %output.2.refs_4_ = bf16[1024,256]{1,0:T(8,128)(2,1)} custom-call(bf16[1024,256]{1,0:T(8,128)(2,1)S(1)} %copy-done.1, bf16[512,256]{1,0:T(8,128)(2,1)S(1)} %rest.3.refs_0_, bf16[512,256]{1,0:T(8,128)(2,1)S(1)} %collective-permute-done.21.refs_1_, bf16[512,256]{1,0:T(8,128)(2,1)S(1)} %collective-permute-done.22.refs_2_, ...), custom_call_target="tpu_custom_call" | custom-call | tf_op jit(solution)/shard_map/output/pallas_call | solution.py:562
  81.2 5.8 %collective-permute-done.20.refs_1_ = bf16[512,256]{1,0:T(8,128)(2,1)S(1)} collective-permute-done((bf16[512,256]{1,0:T(8,128)(2,1)S(1)}, bf16[512,256]{1,0:T(8,128)(2,1)S(1)}, u32[]{:S(2)}, u32[]{:S(2)}) %collective-permute-start.20) | collective-permute-done | bytes 262176 | tf_op jit(solution)/shard_map/ppermute | solution.py:51
  86.9 1.5 %collective-permute-done.25.refs_3_ = bf16[512,256]{1,0:T(8,128)(2,1)S(1)} collective-permute-done((bf16[512,256]{1,0:T(8,128)(2,1)S(1)}, bf16[512,256]{1,0:T(8,128)(2,1)S(1)}, u32[]{:S(2)}, u32[]{:S(2)}) %collective-permute-start.25) | collective-permute-done | bytes 262176 | tf_op jit(solution)/shard_map/ppermute | solution.py:51
  88.5 1.3 %output.3 = bf16[1024,256]{1,0:T(8,128)(2,1)} custom-call(bf16[1024,256]{1,0:T(8,128)(2,1)S(1)} %copy-done.1, bf16[512,256]{1,0:T(8,128)(2,1)S(1)} %rest.2.refs_0_, bf16[512,256]{1,0:T(8,128)(2,1)S(1)} %collective-permute-done.20.refs_1_, bf16[512,256]{1,0:T(8,128)(2,1)S(1)} %collective-permute-done.24.refs_2_, ...), custom_call_target="tpu_custom_call", output_to_operand_aliasing={{}: (5, {})} | custom-call | tf_op jit(solution)/shard_map/output/pallas_call | solution.py:562
  (50 shorter events, 2.4 us)
Async XLA Ops:
  1.2 12.5 %collective-permute-start.4 = (bf16[128,256]{1,0:T(8,128)(2,1)S(1)}, bf16[128,256]{1,0:T(8,128)(2,1)S(1)}, u32[]{:S(2)}, u32[]{:S(2)}) collective-permute-start(bf16[128,256]{1,0:T(8,128)(2,1)S(1)} %get-tuple-element.83), channel_id=1, source_target_pairs={{0,16},{4,20},{8,24},{12,28},{16,0},{20,4},{24,8},{28,12},{1,17},{... | collective-permute-start | bytes 196616 | tf_op jit(solution)/shard_map/ppermute | solution.py:83
  5.3 12.0 %collective-permute-start.3 = (bf16[128,256]{1,0:T(8,128)(2,1)S(1)}, bf16[128,256]{1,0:T(8,128)(2,1)S(1)}, u32[]{:S(2)}, u32[]{:S(2)}) collective-permute-start(bf16[128,256]{1,0:T(8,128)(2,1)S(1)} %get-tuple-element.84), channel_id=1, source_target_pairs={{0,20},{4,16},{8,28},{12,24},{16,4},{20,0},{24,12},{28,8},{1,21},{... | collective-permute-start | bytes 196616 | tf_op jit(solution)/shard_map/ppermute | solution.py:83
  6.6 19.8 %copy-start.3 = (bf16[1024,256]{1,0:T(8,128)(2,1)S(1)}, bf16[1024,256]{1,0:T(8,128)(2,1)}, u32[]{:S(2)}) copy-start(bf16[1024,256]{1,0:T(8,128)(2,1)} %wv_ref.1) | copy-start | bytes 1572868
  6.6 19.8 %copy-start.7 = (s32[1,1024]{1,0:T(1,128)S(1)}, s32[1,1024]{1,0:T(1,128)}, u32[]{:S(2)}) copy-start(s32[1,1024]{1,0:T(1,128)} %order_ref.1) | copy-start | bytes 12292
  6.6 19.8 %copy-start.8 = (s32[1,512]{1,0:T(1,128)S(1)}, s32[1,512]{1,0:T(1,128)}, u32[]{:S(2)}) copy-start(s32[1,512]{1,0:T(1,128)} %mask_ref.1) | copy-start | bytes 6148
  8.9 23.4 %copy-start = (bf16[1024,1024]{1,0:T(8,128)(2,1)S(1)}, bf16[1024,1024]{1,0:T(8,128)(2,1)}, u32[]{:S(2)}) copy-start(bf16[1024,1024]{1,0:T(8,128)(2,1)} %refs_6_.1) | copy-start | bytes 6291460
  8.9 23.4 %copy-start.4 = (bf16[1024,256]{1,0:T(8,128)(2,1)S(1)}, bf16[1024,256]{1,0:T(8,128)(2,1)}, u32[]{:S(2)}) copy-start(bf16[1024,256]{1,0:T(8,128)(2,1)} %refs_8_.1) | copy-start | bytes 1572868
  10.1 14.1 %collective-permute-start.7 = (bf16[128,512]{1,0:T(8,128)(2,1)S(1)}, bf16[128,512]{1,0:T(8,128)(2,1)S(1)}, u32[]{:S(2)}, u32[]{:S(2)}) collective-permute-start(bf16[128,512]{1,0:T(8,128)(2,1)S(1)} %get-tuple-element.87), channel_id=1, source_target_pairs={{0,4},{4,0},{8,12},{12,8},{16,20},{20,16},{24,28},{28,24},{1,5},{5... | collective-permute-start | bytes 393224 | tf_op jit(solution)/shard_map/ppermute | solution.py:83
  10.4 13.8 %collective-permute-start.5 = (bf16[128,512]{1,0:T(8,128)(2,1)S(1)}, bf16[128,512]{1,0:T(8,128)(2,1)S(1)}, u32[]{:S(2)}, u32[]{:S(2)}) collective-permute-start(bf16[128,512]{1,0:T(8,128)(2,1)S(1)} %get-tuple-element.88), channel_id=1, source_target_pairs={{0,12},{4,8},{8,4},{12,0},{16,28},{20,24},{24,20},{28,16},{1,13},{... | collective-permute-start | bytes 393224 | tf_op jit(solution)/shard_map/ppermute | solution.py:83
  13.2 11.0 %collective-permute-start.6 = (bf16[128,512]{1,0:T(8,128)(2,1)S(1)}, bf16[128,512]{1,0:T(8,128)(2,1)S(1)}, u32[]{:S(2)}, u32[]{:S(2)}) collective-permute-start(bf16[128,512]{1,0:T(8,128)(2,1)S(1)} %get-tuple-element.89), channel_id=1, source_target_pairs={{0,8},{4,12},{8,0},{12,4},{16,24},{20,28},{24,16},{28,20},{1,9},{5... | collective-permute-start | bytes 393224 | tf_op jit(solution)/shard_map/ppermute | solution.py:83
  13.7 9.4 %collective-permute-start.2 = (bf16[128,256]{1,0:T(8,128)(2,1)S(1)}, bf16[128,256]{1,0:T(8,128)(2,1)S(1)}, u32[]{:S(2)}, u32[]{:S(2)}) collective-permute-start(bf16[128,256]{1,0:T(8,128)(2,1)S(1)} %get-tuple-element.85), channel_id=1, source_target_pairs={{0,24},{4,28},{8,16},{12,20},{16,8},{20,12},{24,0},{28,4},{1,25},{... | collective-permute-start | bytes 196616 | tf_op jit(solution)/shard_map/ppermute | solution.py:83
  17.3 7.0 %collective-permute-start.1 = (bf16[128,256]{1,0:T(8,128)(2,1)S(1)}, bf16[128,256]{1,0:T(8,128)(2,1)S(1)}, u32[]{:S(2)}, u32[]{:S(2)}) collective-permute-start(bf16[128,256]{1,0:T(8,128)(2,1)S(1)} %get-tuple-element.86), channel_id=1, source_target_pairs={{0,28},{4,24},{8,20},{12,16},{16,12},{20,8},{24,4},{28,0},{1,29},{... | collective-permute-start | bytes 196616 | tf_op jit(solution)/shard_map/ppermute | solution.py:83
  24.3 6.4 %collective-permute-start.8 = (bf16[512,256]{1,0:T(8,128)(2,1)S(1)}, bf16[512,256]{1,0:T(8,128)(2,1)S(1)}, u32[]{:S(2)}, u32[]{:S(2)}) collective-permute-start(bf16[512,256]{1,0:T(8,128)(2,1)S(1)} %get-tuple-element.43.early_ref.refs_0_), channel_id=1, source_target_pairs={{0,2},{2,0},{1,3},{3,1},{4,6},{6,4},{5,7},{7,5},{8,10},{10,8},{9,1... | collective-permute-start | bytes 786440 | tf_op jit(solution)/shard_map/ppermute | solution.py:51
  25.9 4.9 %collective-permute-start.11 = (bf16[384,512]{1,0:T(8,128)(2,1)S(1)}, bf16[384,512]{1,0:T(8,128)(2,1)S(1)}, u32[]{:S(2)}, u32[]{:S(2)}) collective-permute-start(bf16[384,512]{1,0:T(8,128)(2,1)S(1)} %get-tuple-element.58.refs_4_), channel_id=1, source_target_pairs={{0,1},{1,0},{2,3},{3,2},{4,5},{5,4},{6,7},{7,6},{8,9},{9,8},{10,11... | collective-permute-start | bytes 1179656 | tf_op jit(solution)/shard_map/ppermute | solution.py:51
  25.9 4.9 %collective-permute-start.9 = (bf16[512,256]{1,0:T(8,128)(2,1)S(1)}, bf16[512,256]{1,0:T(8,128)(2,1)S(1)}, u32[]{:S(2)}, u32[]{:S(2)}) collective-permute-start(bf16[512,256]{1,0:T(8,128)(2,1)S(1)} %get-tuple-element.43.early_ref.refs_0_), channel_id=1, source_target_pairs={{0,1},{1,0},{2,3},{3,2},{4,5},{5,4},{6,7},{7,6},{8,9},{9,8},{10,11... | collective-permute-start | bytes 786440 | tf_op jit(solution)/shard_map/ppermute | solution.py:51
  30.8 25.5 %copy-start.5 = (f32[4,4]{1,0:T(4,128)S(1)}, f32[4,4]{1,0:T(4,128)}, u32[]{:S(2)}) copy-start(f32[4,4]{1,0:T(4,128)} %mix_ref.5) | copy-start | bytes 196
  30.8 1.5 %collective-permute-start.10 = (bf16[512,256]{1,0:T(8,128)(2,1)S(1)}, bf16[512,256]{1,0:T(8,128)(2,1)S(1)}, u32[]{:S(2)}, u32[]{:S(2)}) collective-permute-start(bf16[512,256]{1,0:T(8,128)(2,1)S(1)} %collective-permute-done.8.refs_1_), channel_id=1, source_target_pairs={{0,1},{1,0},{2,3},{3,2},{4,5},{5,4},{6,7},{7,6},{8,9},{9,8},{10,11... | collective-permute-start | bytes 786440 | tf_op jit(solution)/shard_map/ppermute | solution.py:51
  34.6 28.7 %collective-permute-start.12 = (bf16[1024,256]{1,0:T(8,128)(2,1)S(1)}, bf16[1024,256]{1,0:T(8,128)(2,1)S(1)}, u32[]{:S(2)}, u32[]{:S(2)}) collective-permute-start(bf16[1024,256]{1,0:T(8,128)(2,1)S(1)} %get-tuple-element.66), channel_id=1, source_target_pairs={{0,4},{4,8},{8,12},{12,16},{16,20},{20,24},{24,28},{1,5},{5,9},{9,... | collective-permute-start | bytes 1572872 | tf_op jit(solution)/shard_map/ppermute | solution.py:55
  37.5 14.7 %collective-permute-start.19 = (bf16[64,256]{1,0:T(8,128)(2,1)S(1)}, bf16[64,256]{1,0:T(8,128)(2,1)S(1)}, u32[]{:S(2)}, u32[]{:S(2)}) collective-permute-start(bf16[64,256]{1,0:T(8,128)(2,1)S(1)} %get-tuple-element.69.refs_0_), channel_id=1, source_target_pairs={{0,28},{4,24},{8,20},{12,16},{16,12},{20,8},{24,4},{28,0},{1,29},{... | collective-permute-start | bytes 98312 | tf_op jit(solution)/shard_map/ppermute | solution.py:83
  37.8 16.5 %collective-permute-start.18 = (bf16[64,256]{1,0:T(8,128)(2,1)S(1)}, bf16[64,256]{1,0:T(8,128)(2,1)S(1)}, u32[]{:S(2)}, u32[]{:S(2)}) collective-permute-start(bf16[64,256]{1,0:T(8,128)(2,1)S(1)} %get-tuple-element.69.refs_0_), channel_id=1, source_target_pairs={{0,24},{4,28},{8,16},{12,20},{16,8},{20,12},{24,0},{28,4},{1,25},{... | collective-permute-start | bytes 98312 | tf_op jit(solution)/shard_map/ppermute | solution.py:83
  40.8 13.9 %collective-permute-start.17 = (bf16[64,256]{1,0:T(8,128)(2,1)S(1)}, bf16[64,256]{1,0:T(8,128)(2,1)S(1)}, u32[]{:S(2)}, u32[]{:S(2)}) collective-permute-start(bf16[64,256]{1,0:T(8,128)(2,1)S(1)} %get-tuple-element.69.refs_0_), channel_id=1, source_target_pairs={{0,20},{4,16},{8,28},{12,24},{16,4},{20,0},{24,12},{28,8},{1,21},{... | collective-permute-start | bytes 98312 | tf_op jit(solution)/shard_map/ppermute | solution.py:83
  40.8 9.6 %collective-permute-start = (s32[1,512]{1,0:T(1,128)S(1)}, s32[1,512]{1,0:T(1,128)S(1)}, u32[]{:S(2)}, u32[]{:S(2)}) collective-permute-start(s32[1,512]{1,0:T(1,128)S(1)} %copy-done.8), channel_id=1, source_target_pairs={{0,4},{4,8},{8,12},{12,16},{16,20},{20,24},{24,28},{1,5},{5,9},{9,... | collective-permute-start | bytes 6152 | tf_op jit(solution)/shard_map/ppermute | solution.py:55
  50.4 12.9 %collective-permute-start.16 = (bf16[64,256]{1,0:T(8,128)(2,1)S(1)}, bf16[64,256]{1,0:T(8,128)(2,1)S(1)}, u32[]{:S(2)}, u32[]{:S(2)}) collective-permute-start(bf16[64,256]{1,0:T(8,128)(2,1)S(1)} %get-tuple-element.69.refs_0_), channel_id=1, source_target_pairs={{0,16},{4,20},{8,24},{12,28},{16,0},{20,4},{24,8},{28,12},{1,17},{... | collective-permute-start | bytes 98312 | tf_op jit(solution)/shard_map/ppermute | solution.py:83
  52.2 11.1 %collective-permute-start.15 = (bf16[64,256]{1,0:T(8,128)(2,1)S(1)}, bf16[64,256]{1,0:T(8,128)(2,1)S(1)}, u32[]{:S(2)}, u32[]{:S(2)}) collective-permute-start(bf16[64,256]{1,0:T(8,128)(2,1)S(1)} %get-tuple-element.69.refs_0_), channel_id=1, source_target_pairs={{0,12},{4,8},{8,4},{12,0},{16,28},{20,24},{24,20},{28,16},{1,13},{... | collective-permute-start | bytes 98312 | tf_op jit(solution)/shard_map/ppermute | solution.py:83
  54.4 8.9 %collective-permute-start.14 = (bf16[64,256]{1,0:T(8,128)(2,1)S(1)}, bf16[64,256]{1,0:T(8,128)(2,1)S(1)}, u32[]{:S(2)}, u32[]{:S(2)}) collective-permute-start(bf16[64,256]{1,0:T(8,128)(2,1)S(1)} %get-tuple-element.69.refs_0_), channel_id=1, source_target_pairs={{0,8},{4,12},{8,0},{12,4},{16,24},{20,28},{24,16},{28,20},{1,9},{5... | collective-permute-start | bytes 98312 | tf_op jit(solution)/shard_map/ppermute | solution.py:83
  54.8 8.5 %collective-permute-start.13 = (bf16[64,256]{1,0:T(8,128)(2,1)S(1)}, bf16[64,256]{1,0:T(8,128)(2,1)S(1)}, u32[]{:S(2)}, u32[]{:S(2)}) collective-permute-start(bf16[64,256]{1,0:T(8,128)(2,1)S(1)} %get-tuple-element.69.refs_0_), channel_id=1, source_target_pairs={{0,4},{4,0},{8,12},{12,8},{16,20},{20,16},{24,28},{28,24},{1,5},{5... | collective-permute-start | bytes 98312 | tf_op jit(solution)/shard_map/ppermute | solution.py:83
  67.7 7.1 %collective-permute-start.21 = (bf16[512,256]{1,0:T(8,128)(2,1)S(1)}, bf16[512,256]{1,0:T(8,128)(2,1)S(1)}, u32[]{:S(2)}, u32[]{:S(2)}) collective-permute-start(bf16[512,256]{1,0:T(8,128)(2,1)S(1)} %rest.3.refs_0_), channel_id=1, source_target_pairs={{0,2},{2,0},{1,3},{3,1},{4,6},{6,4},{5,7},{7,5},{8,10},{10,8},{9,1... | collective-permute-start | bytes 786440 | tf_op jit(solution)/shard_map/ppermute | solution.py:51
  69.1 10.7 %collective-permute-start.22 = (bf16[512,256]{1,0:T(8,128)(2,1)S(1)}, bf16[512,256]{1,0:T(8,128)(2,1)S(1)}, u32[]{:S(2)}, u32[]{:S(2)}) collective-permute-start(bf16[512,256]{1,0:T(8,128)(2,1)S(1)} %rest.3.refs_0_), channel_id=1, source_target_pairs={{0,1},{1,0},{2,3},{3,2},{4,5},{5,4},{6,7},{7,6},{8,9},{9,8},{10,11... | collective-permute-start | bytes 786440 | tf_op jit(solution)/shard_map/ppermute | solution.py:51
  74.7 5.1 %collective-permute-start.23 = (bf16[512,256]{1,0:T(8,128)(2,1)S(1)}, bf16[512,256]{1,0:T(8,128)(2,1)S(1)}, u32[]{:S(2)}, u32[]{:S(2)}) collective-permute-start(bf16[512,256]{1,0:T(8,128)(2,1)S(1)} %collective-permute-done.21.refs_1_), channel_id=1, source_target_pairs={{0,1},{1,0},{2,3},{3,2},{4,5},{5,4},{6,7},{7,6},{8,9},{9,8},{10,11... | collective-permute-start | bytes 786440 | tf_op jit(solution)/shard_map/ppermute | solution.py:51
  78.1 8.8 %collective-permute-start.20 = (bf16[512,256]{1,0:T(8,128)(2,1)S(1)}, bf16[512,256]{1,0:T(8,128)(2,1)S(1)}, u32[]{:S(2)}, u32[]{:S(2)}) collective-permute-start(bf16[512,256]{1,0:T(8,128)(2,1)S(1)} %rest.2.refs_0_), channel_id=1, source_target_pairs={{0,2},{2,0},{1,3},{3,1},{4,6},{6,4},{5,7},{7,5},{8,10},{10,8},{9,1... | collective-permute-start | bytes 786440 | tf_op jit(solution)/shard_map/ppermute | solution.py:51
  79.6 7.3 %collective-permute-start.24 = (bf16[512,256]{1,0:T(8,128)(2,1)S(1)}, bf16[512,256]{1,0:T(8,128)(2,1)S(1)}, u32[]{:S(2)}, u32[]{:S(2)}) collective-permute-start(bf16[512,256]{1,0:T(8,128)(2,1)S(1)} %rest.2.refs_0_), channel_id=1, source_target_pairs={{0,1},{1,0},{2,3},{3,2},{4,5},{5,4},{6,7},{7,6},{8,9},{9,8},{10,11... | collective-permute-start | bytes 786440 | tf_op jit(solution)/shard_map/ppermute | solution.py:51
  86.9 1.5 %collective-permute-start.25 = (bf16[512,256]{1,0:T(8,128)(2,1)S(1)}, bf16[512,256]{1,0:T(8,128)(2,1)S(1)}, u32[]{:S(2)}, u32[]{:S(2)}) collective-permute-start(bf16[512,256]{1,0:T(8,128)(2,1)S(1)} %collective-permute-done.20.refs_1_), channel_id=1, source_target_pairs={{0,1},{1,0},{2,3},{3,2},{4,5},{5,4},{6,7},{7,6},{8,9},{9,8},{10,11... | collective-permute-start | bytes 786440 | tf_op jit(solution)/shard_map/ppermute | solution.py:51
  (3 other events, 33.0 us)

commit v4 on v3

--- a/solution.py
+++ b/solution.py
@@ -18,6 +18,7 @@
 I32 = jnp.int32
 HIDE = -1e30
 VMEM_LIMIT = 24 * 1024 * 1024
+PARTS = (2, 3, 3)
 
 X_PAIRS = [(0, 2), (2, 0), (1, 3), (3, 1)]
 CORE_PAIRS = [(0, 1), (1, 0), (2, 3), (3, 2)]
@@ -55,8 +56,35 @@
     return lax.ppermute(block, "seq", [(i, i + 1) for i in range(lax.axis_size("seq") - 1)])
 
 
+def send_kernel(distances, tokens_ref, *refs):
+    outs, own, sem_ref = refs[:-2], refs[-2], refs[-1]
+    slab, head = lax.axis_index("seq"), lax.axis_index("head")
+    rows = outs[0].shape[0]
+    quarter = tokens_ref.shape[1] // 4
+    copies = []
+    for distance, out in zip(distances, outs):
+        row = pl.multiple_of((slab ^ distance) * rows, rows)
+        for part in range(out.shape[1] // quarter):
+            start = pl.multiple_of((head ^ (2 * part)) * quarter, quarter)
+            copies.append(
+                pltpu.make_async_copy(
+                    tokens_ref.at[pl.ds(row, rows), pl.ds(start, quarter)],
+                    out.at[:, part * quarter : (part + 1) * quarter],
+                    sem_ref.at[len(copies)],
+                )
+            )
+    row = pl.multiple_of(slab * rows, rows)
+    copies.append(
+        pltpu.make_async_copy(tokens_ref.at[pl.ds(row, rows)], own, sem_ref.at[len(copies)])
+    )
+    for copy in copies:
+        copy.start()
+    for copy in copies:
+        copy.wait()
+
+
 def stack_kernel(counts, *refs):
-    sources, targets = refs[: sum(counts)], refs[sum(counts) :]
+    sources, targets = refs[: sum(counts)], refs[len(refs) - len(counts) :]
     for count, target in zip(counts, targets):
         height = target.shape[0] // count
         for index in range(count):
@@ -64,7 +92,7 @@
         sources = sources[count:]
 
 
-def stacked(*lists):
+def stacked(lists, after):
     parts = [part for one in lists for part in one]
     return pl.pallas_call(
         functools.partial(stack_kernel, tuple(len(one) for one in lists)),
@@ -72,30 +100,25 @@
             jax.ShapeDtypeStruct((len(one) * one[0].shape[0], one[0].shape[1]), one[0].dtype)
             for one in lists
         ),
-        in_specs=vmem_specs(len(parts)),
+        in_specs=vmem_specs(len(parts)) + [pl.BlockSpec(memory_space=pl.ANY)],
         out_specs=vmem_specs(len(lists)),
         compiler_params=pltpu.CompilerParams(vmem_limit_bytes=VMEM_LIMIT),
         name="stack",
-    )(*parts)
+    )(*parts, after)
 
 
 def by_distance(block, distance):
     return lax.ppermute(block, "seq", [(i, i ^ distance) for i in range(lax.axis_size("seq"))])
 
 
-def exchange_tokens(tokens, head, prepare):
+def exchange_tokens(tokens, before_mask, prepare):
     tok_rows, width = tokens.shape
     slabs = lax.axis_size("seq")
     rows = tok_rows // slabs
     quarter = width // 4
-    slab = lax.axis_index("seq")
-    split = tokens.reshape(slabs, rows, width)
-
-    def columns(other):
-        return lax.dynamic_slice_in_dim(split, (head ^ other) * quarter, quarter, axis=2)
-
-    mine = columns(0)
     if slabs != 8:
+        split = tokens.reshape(slabs, rows, width)
+        mine = lax.dynamic_slice_in_dim(split, lax.axis_index("head") * quarter, quarter, axis=2)
         first = lax.all_to_all(mine, "seq", split_axis=0, concat_axis=0, tiled=True).reshape(
             tok_rows, quarter
         )
@@ -104,15 +127,21 @@
         fourth = over_head(third, CORE_PAIRS)
         pieces = [(first, 0, (0,)), (third, 0, (2,)), (second, 0, (1,)), (fourth, 0, (3,))]
         return pieces, prepare(first)
-    both = jnp.concatenate([mine, columns(2)], axis=2)
-
-    def to_peer(source, distance):
-        block = lax.dynamic_index_in_dim(source, slab ^ distance, axis=0, keepdims=False)
-        return by_distance(block, distance)
-
-    far, near = stacked(
-        [to_peer(mine, d) for d in (7, 6, 5, 4)], [to_peer(both, d) for d in (3, 2, 1)]
-    )
+    distances = (7, 6, 5, 4, 3, 2, 1)
+    *blocks, own = pl.pallas_call(
+        functools.partial(send_kernel, distances),
+        out_shape=tuple(
+            jax.ShapeDtypeStruct((rows, columns), BF)
+            for columns in [quarter if d > 3 else 2 * quarter for d in distances] + [width]
+        ),
+        in_specs=[pl.BlockSpec(memory_space=pl.ANY)],
+        out_specs=[pl.BlockSpec(memory_space=pl.ANY)] * 8,
+        scratch_shapes=[pltpu.SemaphoreType.DMA((11,))],
+        compiler_params=pltpu.CompilerParams(vmem_limit_bytes=60 * 1024 * 1024),
+        name="send",
+    )(tokens)
+    arrived = [by_distance(block, d) for block, d in zip(blocks, distances)]
+    far, near = stacked((arrived[:4], arrived[4:]), before_mask)
     far_x = over_head(far, X_PAIRS)
     near_core = over_head(near, CORE_PAIRS)
     far_core = over_head(far, CORE_PAIRS)
@@ -120,7 +149,7 @@
     far_x, prepared = lax.optimization_barrier((far_x, prepared))
     far_last = over_head(far_x, CORE_PAIRS)
     pieces = [(far, 0, (0,)), (far_x, 0, (2,)), (far_core, 0, (1,)), (far_last, 0, (3,))]
-    pieces += [(near, 4 * rows, (0, 2)), (near_core, 4 * rows, (1, 3)), (tokens, 7 * rows, None)]
+    pieces += [(near, 4 * rows, (0, 2)), (near_core, 4 * rows, (1, 3)), (own, 7 * rows, None)]
     return pieces, prepared
 
 
@@ -140,8 +169,8 @@
 
 
 def prepare_kernel(
-    order_ref, mask_ref, wq_ref, wv_ref, early_ref,
-    p_ref, pt_ref, sel_ref, fcol_ref, frow_ref, bias_ref, wt_ref,
+    order_ref, mask_ref, before_ref, wq_ref, wv_ref, wk_in, early_ref,
+    p_ref, pt_ref, sel_ref, fcol_ref, frow_ref, e_ref, et_ref, bias_ref, wt_ref, wk_ref,
 ):
     slab, slabs = lax.axis_index("seq"), lax.axis_size("seq")
     tok_rows = order_ref.shape[1]
@@ -183,32 +212,28 @@
     pools = sel_ref[packed:]
     fcol_ref[...] = 1.0 / jnp.sqrt(jnp.maximum(nn(pools, jnp.ones((tok_rows, lanes), BF)), 1.0))
     frow_ref[...] = 1.0 / jnp.sqrt(jnp.maximum(nt(jnp.ones((16, tok_rows), BF), pools), 1.0))
-    bias_ref[...] = jnp.where(column(rank) >= 0, 0.0, HIDE)
+    rank_before = jnp.where(slab > 0, ranks(before_ref[...], tok_rows), -1)
+    rank_column = column(rank_before)
+    for at in range(0, packed, lanes):
+        e_ref[:, at : at + lanes] = ones_where(rank_column == iota((tok_rows, lanes), 1) + at)
+        et_ref[at : at + lanes] = ones_where(iota((lanes, tok_rows), 0) + at == rank_before)
+    bias_ref[:tok_rows] = jnp.where(rank_column >= 0, 0.0, HIDE)
+    bias_ref[tok_rows:] = jnp.where(column(rank) >= 0, 0.0, HIDE)
     wt_ref[:group] = jnp.transpose(wq_ref[...])
     wt_ref[group:] = jnp.transpose(wv_ref[...])
+    wk_ref[...] = wk_in[...]
 
 
 def project_kernel(places, *refs):
     count = len(places)
     piece_refs, refs = refs[:count], refs[count:]
-    wt_ref, wk_ref, sel_ref, fcol_ref, comp_ref, summ_ref, k_ref, v_ref, x_ref, sem_ref = refs
+    wt_ref, wk_ref, sel_ref, fcol_ref, comp_ref, summ_ref, k_ref, v_ref, x_ref = refs
     quarter = x_ref.shape[1] // 4
     head = lax.axis_index("head")
-    loads = []
     for piece, (row, distances) in zip(piece_refs, places):
         height = piece.shape[0]
         if distances is None:
-            rows = height // lax.axis_size("seq")
-            start = pl.multiple_of(lax.axis_index("seq") * rows, rows)
-            loads.append(
-                pltpu.make_async_copy(
-                    piece.at[pl.ds(start, rows)], x_ref.at[row : row + rows], sem_ref
-                )
-            )
-            loads[-1].start()
-    for piece, (row, distances) in zip(piece_refs, places):
-        height = piece.shape[0]
-        if distances is None:
+            x_ref[row : row + height] = piece[...]
             continue
         for part, distance in enumerate(distances):
             start = pl.multiple_of((head ^ distance) * quarter, quarter)
@@ -218,8 +243,6 @@
     group = wk_ref.shape[1]
     packed = comp_ref.shape[0] // 2
     lead = packed + SUMM_ROWS
-    for load in loads:
-        load.wait()
     x = x_ref[...]
     keys = nn(x, wk_ref[...]).astype(BF)
     k_ref[...] = keys
@@ -252,8 +275,8 @@
 
 
 def own_kernel(
-    mix_ref, before_ref, p_in, pt_ref, sel_ref, fcol_ref, frow_ref, wt_ref, x_ref, k0_ref, v0_ref, seen_ref,
-    qt_ref, vt_ref, k_ref, acc_ref, near_ref, top_ref, den_ref, e_ref, et_ref, bias_ref, q4_ref, p_ref,
+    mix_ref, p_in, pt_ref, sel_ref, fcol_ref, frow_ref, wt_ref, x_ref, k0_ref, v0_ref, bias_ref,
+    qt_ref, vt_ref, k_ref, acc_ref, near_ref, top_ref, den_ref, q4_ref, p_ref,
 ):
     tok_rows, group = k_ref.shape
     heads = mix_ref.shape[1]
@@ -274,7 +297,7 @@
         slot = g % 2
         spread_heads(q4_ref.at[slot], qt_ref, at, heads)
         q4 = q4_ref[slot]
-        bias = jnp.where(same, 0.0, seen_ref[at : at + FBLK])
+        bias = jnp.where(same, 0.0, bias_ref[tok_rows + at : tok_rows + at + FBLK])
         own_scores = nn(k_ref[at : at + FBLK], q4)
         near_scores = nn(nk, q4)
         scales = []
@@ -296,13 +319,6 @@
             rows, lanes = slice(h * width, (h + 1) * width), slice(h * FBLK, (h + 1) * FBLK)
             acc_ref[rows, at : at + FBLK] = own_out[rows, lanes]
             near_ref[rows, at : at + FBLK] = near_out[rows, lanes] * scales[h]
-    rank = jnp.where(lax.axis_index("seq") > 0, ranks(before_ref[...], tok_rows), -1)
-    rank_column = column(rank)
-    bias_ref[:tok_rows] = jnp.where(rank_column >= 0, 0.0, HIDE)
-    bias_ref[tok_rows:] = seen_ref[...]
-    for at in range(0, et_ref.shape[0], FBLK):
-        e_ref[:, at : at + FBLK] = ones_where(rank_column == iota((tok_rows, FBLK), 1) + at)
-        et_ref[at : at + FBLK] = ones_where(iota((FBLK, tok_rows), 0) + at == rank)
 
 
 def window_kernel(k_ref, vt_ref, comp_ref, e_ref, et_ref, *refs):
@@ -448,17 +464,20 @@
                 shape((chosen, tok_rows), BF),
                 shape((SUMM_ROWS + near, 128), F32),
                 shape((16, SUMM_ROWS + near), F32),
-                shape((tok_rows, FBLK), F32),
+                shape((tok_rows, packed), BF),
+                shape((packed, tok_rows), BF),
+                shape((2 * tok_rows, FBLK), F32),
                 shape((2 * group, width), BF),
+                shape((width, group), BF),
             ),
-            in_specs=vmem_specs(4) + [pl.BlockSpec(memory_space=pl.ANY)],
-            out_specs=vmem_specs(7),
+            in_specs=vmem_specs(6) + [pl.BlockSpec(memory_space=pl.ANY)],
+            out_specs=vmem_specs(10),
             compiler_params=params,
             name="prepare",
-        )(order, mask_ids, w_query, w_value, early)
-
-    pieces, prepared = exchange_tokens(tokens, head, prepare)
-    permute, permute_t, select, f_col, f_row, seen, w_t = prepared
+        )(order, mask_ids, before_mask, w_query, w_value, w_key, early)
+
+    pieces, prepared = exchange_tokens(tokens, before_mask, prepare)
+    permute, permute_t, select, f_col, f_row, expand, expand_t, bias, w_t, w_k = prepared
     places = tuple((row, distances) for _, row, distances in pieces)
     comp, summ, k0, v0, rows_here = pl.pallas_call(
         functools.partial(project_kernel, places),
@@ -469,16 +488,11 @@
             shape((group, tok_rows), BF),
             shape((tok_rows, width), BF),
         ),
-        in_specs=[
-            pl.BlockSpec(memory_space=pltpu.VMEM if distances else pl.ANY)
-            for _, distances in places
-        ]
-        + vmem_specs(4),
+        in_specs=vmem_specs(len(pieces) + 4),
         out_specs=vmem_specs(5),
-        scratch_shapes=[pltpu.SemaphoreType.DMA],
         compiler_params=params,
         name="project",
-    )(*[piece for piece, _, _ in pieces], w_t, w_key, select, f_col)
+    )(*[piece for piece, _, _ in pieces], w_t, w_k, select, f_col)
     comp_before = to_next(comp)
     if slabs == 8:
         summaries = [summ] + [by_distance(summ, d) for d in range(1, slabs)]
@@ -488,7 +502,7 @@
         summaries = [copies.reshape(slabs * step, group)]
 
     blocks = tok_rows // FBLK
-    q_t, v_t, keys, acc, near_out, top, den, expand, expand_t, bias = pl.pallas_call(
+    q_t, v_t, keys, acc, near_out, top, den = pl.pallas_call(
         own_kernel,
         out_shape=(
             shape((group, tok_rows), BF),
@@ -498,19 +512,16 @@
             shape((group, tok_rows), F32),
             shape((blocks, heads * FBLK), F32),
             shape((blocks, heads * FBLK), F32),
-            shape((tok_rows, packed), BF),
-            shape((packed, tok_rows), BF),
-            shape((2 * tok_rows, FBLK), F32),
         ),
-        in_specs=smem_specs(1) + vmem_specs(11),
-        out_specs=vmem_specs(10),
+        in_specs=smem_specs(1) + vmem_specs(10),
+        out_specs=vmem_specs(7),
         scratch_shapes=[
             pltpu.VMEM((2, group, heads * FBLK), BF),
             pltpu.VMEM((2, FBLK + near, heads * FBLK), BF),
         ],
         compiler_params=params,
         name="own",
-    )(level_mix, before_mask, permute, permute_t, select, f_col, f_row, w_t, rows_here, k0, v0, seen)
+    )(level_mix, permute, permute_t, select, f_col, f_row, w_t, rows_here, k0, v0, bias)
 
     window_k, window_v, coarse_k, coarse_v = pl.pallas_call(
         window_kernel,
@@ -529,14 +540,31 @@
 
     total = (FINE_K - 1) * FBLK + coarse
     lists = fine_blocks.T
-    halves = 2
-    part_blocks = blocks // halves
-    part_rows = tok_rows // halves
-    out = None
-    for half in range(halves):
+    parts = PARTS if sum(PARTS) == blocks else (blocks,)
+    waiting, out, first = None, None, 0
+
+    def finish(out, attended, third, second, base):
+        fourth = over_head(third, CORE_PAIRS)
+        rows = attended.shape[0]
+        previous = [] if out is None else [out]
+        tile = pl.BlockSpec((FBLK, group), lambda i: (i, 0))
+        return pl.pallas_call(
+            output_kernel,
+            grid=(rows // FBLK,),
+            out_shape=shape((tok_rows, group), BF),
+            in_specs=[pl.BlockSpec((width, group), lambda i: (0, 0))]
+            + [tile] * 4
+            + [pl.BlockSpec(memory_space=pl.ANY)] * len(previous),
+            out_specs=pl.BlockSpec((FBLK, group), lambda i, base=base: (i + base, 0)),
+            input_output_aliases={5: 0} if previous else {},
+            compiler_params=params,
+            name="output",
+        )(w_out, attended, third, second, fourth, *previous)
+
+    for count in parts:
         attended = pl.pallas_call(
-            functools.partial(rest_kernel, half * part_blocks, part_blocks),
-            out_shape=shape((part_rows, group), BF),
+            functools.partial(rest_kernel, first, count),
+            out_shape=shape((count * FBLK, group), BF),
             in_specs=smem_specs(2) + vmem_specs(10),
             out_specs=pl.BlockSpec(memory_space=pltpu.VMEM),
             scratch_shapes=[
@@ -552,26 +580,14 @@
         )
         third = over_head(attended, X_PAIRS)
         second = over_head(attended, CORE_PAIRS)
-        if out is not None:
+        if waiting is not None:
+            old, old_third, old_second, old_base = waiting
+            old_third, attended = lax.optimization_barrier((old_third, attended))
+            out = finish(out, old, old_third, old_second, old_base)
             third, out = lax.optimization_barrier((third, out))
-        fourth = over_head(third, CORE_PAIRS)
-        steps = 2
-        rows = part_rows // steps
-        tile = pl.BlockSpec((rows, group), lambda i: (i, 0))
-        previous = [] if out is None else [out]
-        out = pl.pallas_call(
-            output_kernel,
-            grid=(steps,),
-            out_shape=shape((tok_rows, group), BF),
-            in_specs=[pl.BlockSpec((width, group), lambda i: (0, 0))]
-            + [tile] * 4
-            + [pl.BlockSpec(memory_space=pl.ANY)] * len(previous),
-            out_specs=pl.BlockSpec((rows, group), lambda i, base=half * steps: (i + base, 0)),
-            input_output_aliases={5: 0} if previous else {},
-            compiler_params=params,
-            name="output",
-        )(w_out, attended, third, second, fourth, *previous)
-    return out
+        waiting = (attended, third, second, first)
+        first += count
+    return finish(out, *waiting)
 
 
 def solution(mesh):

time: 90 us -> 114 us (1.27)
  Pallas kernels: 22.2 us -> 54.2 us
  waiting for transfers between devices: 28.7 us -> 14.4 us
  starting transfers between devices: 33.9 us -> 43.9 us
  local copies, waits for them, and re-layouts: 3.56 us -> 0.04 us
  other arithmetic: 1.17 us -> 0 us
    pallas_call x4 -> x7, Pallas kernels: 9.41 us -> 41.2 us  [the longest x1 29 us: exchange_tokens(): pl.pallas_call(functools.partial(send_kernel, distances), out_shape=tuple...]
    ppermute x10 -> x13, waiting for transfers between devices: 16.3 us -> 8.03 us  [over_head(): return lax.ppermute(block, 'head', pairs)]
    ppermute x14, starting transfers between devices: 21.7 us -> 28.8 us  [by_distance(): lax.ppermute(block, 'seq', [(i, i ^ distance) for i in range(lax.axis_siz...]
    ppermute x2, waiting for transfers between devices: 5.46 us -> 0.01 us  [to_next(): lax.ppermute(block, 'seq', [(i, i + 1) for i in range(lax.axis_size('seq'...]
    dynamic_slice x1 -> x0, local copies, waits for them, and re-layouts: 2.35 us -> none  [columns(): lax.dynamic_slice_in_dim(split, (head ^ other) * quarter, quarter, axis=2)]
    ppermute x10 -> x13, starting transfers between devices: 5.21 us -> 7.14 us  [over_head(): return lax.ppermute(block, 'head', pairs)]
    squeeze x1 -> x0, local copies, waits for them, and re-layouts: 1.18 us -> none  [to_peer(): lax.dynamic_index_in_dim(source, slab ^ distance, axis=0, keepdims=False)]
    squeeze x1 -> x0, other arithmetic: 1.17 us -> none  [to_peer(): lax.dynamic_index_in_dim(source, slab ^ distance, axis=0, keepdims=False)]
  transfers between devices with their start and end apart: 26 -> 29, of which waited for: 8 -> 8; matrix products, arithmetic and copies ran while one was open for 4% -> 0% of each run, Pallas kernels for 16% -> 16%
where the time goes in v4:
time: 114 us; the launch traced here: 113 us
  Pallas kernels  54.2 us (48%)
  starting transfers between devices  43.9 us (39%)
  waiting for transfers between devices  14.4 us (13%)
    pallas_call x1, Pallas kernels, exchange_tokens(): pl.pallas_call(functools.partial(send_kernel, distances), out_shape=tuple...  29 us
    ppermute x14, starting transfers between devices, by_distance(): lax.ppermute(block, 'seq', [(i, i ^ distance) for i in range(lax.axis_siz...  28.8 us
    ppermute x13, waiting for transfers between devices, over_head(): return lax.ppermute(block, 'head', pairs)  8.03 us
    ppermute x2, starting transfers between devices, to_next(): lax.ppermute(block, 'seq', [(i, i + 1) for i in range(lax.axis_size('seq'...  7.96 us
    pallas_call x3, Pallas kernels, local(): pl.pallas_call(functools.partial(rest_kernel, first, count), out_shape=sh...  7.56 us
    ppermute x13, starting transfers between devices, over_head(): return lax.ppermute(block, 'head', pairs)  7.14 us
    ppermute x14, waiting for transfers between devices, by_distance(): lax.ppermute(block, 'seq', [(i, i ^ distance) for i in range(lax.axis_siz...  6.35 us
    pallas_call x1, Pallas kernels, local(): pl.pallas_call(own_kernel, out_shape=(shape((group, tok_rows), BF), shape...  6.21 us
  transfers between devices with their start and end apart: 29, of which 8 were waited for; matrix products, arithmetic and copies ran while one was open for 0% of the time, Pallas kernels for 16%

profile of v4, /device:TPU:0, one launch (start us, length us, event | category | flops | bytes accessed | tf_op | source)
XLA Modules:
  0.0 112.7 jit_solution(9112232882143195973)
XLA Ops:
  0.0 5.0 %collective-permute-start.7 = (s32[1,512]{1,0:T(1,128)}, s32[1,512]{1,0:T(1,128)S(1)}, u32[]{:S(2)}, u32[]{:S(2)}) collective-permute-start(s32[1,512]{1,0:T(1,128)} %mask_ref.1), channel_id=1, source_target_pairs={{0,4},{4,8},{8,12},{12,16},{16,20},{20,24},{24,28},{1,5},{5,9},{9,... | collective-permute-start | bytes 6152 | tf_op jit(solution)/shard_map/ppermute | solution.py:56
  5.0 29.0 %send.1 = (bf16[128,256]{1,0:T(8,128)(2,1)}, bf16[128,256]{1,0:T(8,128)(2,1)}, bf16[128,256]{1,0:T(8,128)(2,1)}, bf16[128,256]{1,0:T(8,128)(2,1)}, bf16[128,512]...) custom-call(bf16[1024,1024]{1,0:T(8,128)(2,1)} %tokens_ref.1), custom_call_target="tpu_custom_call" | custom-call | tf_op jit(solution)/shard_map/send/pallas_call | solution.py:131
  34.1 2.5 %collective-permute-start = (bf16[128,256]{1,0:T(8,128)(2,1)}, bf16[128,256]{1,0:T(8,128)(2,1)S(1)}, u32[]{:S(2)}, u32[]{:S(2)}) collective-permute-start(bf16[128,256]{1,0:T(8,128)(2,1)} %get-tuple-element.60), channel_id=1, source_target_pairs={{0,28},{4,24},{8,20},{12,16},{16,12},{20,8},{24,4},{28,0},{1,29},{... | collective-permute-start | bytes 196616 | tf_op jit(solution)/shard_map/ppermute | solution.py:111
  36.6 2.4 %collective-permute-start.1 = (bf16[128,256]{1,0:T(8,128)(2,1)}, bf16[128,256]{1,0:T(8,128)(2,1)S(1)}, u32[]{:S(2)}, u32[]{:S(2)}) collective-permute-start(bf16[128,256]{1,0:T(8,128)(2,1)} %get-tuple-element.61), channel_id=1, source_target_pairs={{0,24},{4,28},{8,16},{12,20},{16,8},{20,12},{24,0},{28,4},{1,25},{... | collective-permute-start | bytes 196616 | tf_op jit(solution)/shard_map/ppermute | solution.py:111
  38.9 2.0 %collective-permute-start.5 = (bf16[128,512]{1,0:T(8,128)(2,1)}, bf16[128,512]{1,0:T(8,128)(2,1)S(1)}, u32[]{:S(2)}, u32[]{:S(2)}) collective-permute-start(bf16[128,512]{1,0:T(8,128)(2,1)} %get-tuple-element.65), channel_id=1, source_target_pairs={{0,8},{4,12},{8,0},{12,4},{16,24},{20,28},{24,16},{28,20},{1,9},{5... | collective-permute-start | bytes 393224 | tf_op jit(solution)/shard_map/ppermute | solution.py:111
  40.9 1.5 %collective-permute-start.6 = (bf16[128,512]{1,0:T(8,128)(2,1)}, bf16[128,512]{1,0:T(8,128)(2,1)S(1)}, u32[]{:S(2)}, u32[]{:S(2)}) collective-permute-start(bf16[128,512]{1,0:T(8,128)(2,1)} %get-tuple-element.66), channel_id=1, source_target_pairs={{0,4},{4,0},{8,12},{12,8},{16,20},{20,16},{24,28},{28,24},{1,5},{5... | collective-permute-start | bytes 393224 | tf_op jit(solution)/shard_map/ppermute | solution.py:111
  42.4 3.3 %collective-permute-start.2 = (bf16[128,256]{1,0:T(8,128)(2,1)}, bf16[128,256]{1,0:T(8,128)(2,1)S(1)}, u32[]{:S(2)}, u32[]{:S(2)}) collective-permute-start(bf16[128,256]{1,0:T(8,128)(2,1)} %get-tuple-element.62), channel_id=1, source_target_pairs={{0,20},{4,16},{8,28},{12,24},{16,4},{20,0},{24,12},{28,8},{1,21},{... | collective-permute-start | bytes 196616 | tf_op jit(solution)/shard_map/ppermute | solution.py:111
  46.0 3.3 %collective-permute-done.2.refs_2_ = bf16[128,256]{1,0:T(8,128)(2,1)S(1)} collective-permute-done((bf16[128,256]{1,0:T(8,128)(2,1)}, bf16[128,256]{1,0:T(8,128)(2,1)S(1)}, u32[]{:S(2)}, u32[]{:S(2)}) %collective-permute-start.2) | collective-permute-done | bytes 65568 | tf_op jit(solution)/shard_map/ppermute | solution.py:111
  49.4 3.0 %collective-permute-done.3.refs_3_ = bf16[128,256]{1,0:T(8,128)(2,1)S(1)} collective-permute-done((bf16[128,256]{1,0:T(8,128)(2,1)}, bf16[128,256]{1,0:T(8,128)(2,1)S(1)}, u32[]{:S(2)}, u32[]{:S(2)}) %collective-permute-start.3) | collective-permute-done | bytes 65568 | tf_op jit(solution)/shard_map/ppermute | solution.py:111
  52.4 1.6 %collective-permute-start.8 = (bf16[512,256]{1,0:T(8,128)(2,1)S(1)}, bf16[512,256]{1,0:T(8,128)(2,1)S(1)}, u32[]{:S(2)}, u32[]{:S(2)}) collective-permute-start(bf16[512,256]{1,0:T(8,128)(2,1)S(1)} %get-tuple-element.67.early_ref.refs_0_), channel_id=1, source_target_pairs={{0,2},{2,0},{1,3},{3,1},{4,6},{6,4},{5,7},{7,5},{8,10},{10,8},{9,1... | collective-permute-start | bytes 786440 | tf_op jit(solution)/shard_map/ppermute | solution.py:52
  54.5 3.5 %prepare.1 = (bf16[1024,1024]{1,0:T(8,128)(2,1)S(1)}, bf16[1024,1024]{1,0:T(8,128)(2,1)S(1)}, bf16[672,1024]{1,0:T(8,128)(2,1)S(1)}, f32[160,128]{1,0:T(8,128)S(...) custom-call(s32[1,1024]{1,0:T(1,128)S(1)} %copy-done.7, ...), custom_call_target="tpu_custom_call" | custom-call | tf_op jit(solution)/shard_map/prepare/pallas_call | solution.py:459
  58.0 0.8 collective-permute-done.8.refs_1_
  58.9 1.5 %collective-permute-done.10.refs_3_ = bf16[512,256]{1,0:T(8,128)(2,1)S(1)} collective-permute-done((bf16[512,256]{1,0:T(8,128)(2,1)S(1)}, bf16[512,256]{1,0:T(8,128)(2,1)S(1)}, u32[]{:S(2)}, u32[]{:S(2)}) %collective-permute-start.10) | collective-permute-done | bytes 262176 | tf_op jit(solution)/shard_map/ppermute | solution.py:52
  60.4 2.3 %project.1 = (bf16[1024,256]{1,0:T(8,128)(2,1)S(1)}, bf16[64,256]{1,0:T(8,128)(2,1)S(1)}, bf16[1024,256]{1,0:T(8,128)(2,1)S(1)}, bf16[256,1024]{1,0:T(8,128)(2,1)S(1)}, bf16[1024,1024]{1,0:T(8,128)(2,1)S(1)}) custom-call(bf16[512,256]{1,0:T(8,128)(2,1)S(1)} %get-tuple-element.67.early_ref.refs_0_, bf16[512,256]{1,0:T(8,128)(2,1)S(1)} %collective-permute-done.8.refs_1_, ...), custom_call_target="tpu_custom_call" | custom-call | tf_op jit(solution)/shard_map/project/pallas_call | solution.py:482
  62.7 2.9 %collective-permute-start.12 = (bf16[1024,256]{1,0:T(8,128)(2,1)S(1)}, bf16[1024,256]{1,0:T(8,128)(2,1)S(1)}, u32[]{:S(2)}, u32[]{:S(2)}) collective-permute-start(bf16[1024,256]{1,0:T(8,128)(2,1)S(1)} %get-tuple-element.95), channel_id=1, source_target_pairs={{0,4},{4,8},{8,12},{12,16},{16,20},{20,24},{24,28},{1,5},{5,9},{9,... | collective-permute-start | bytes 1572872 | tf_op jit(solution)/shard_map/ppermute | solution.py:56
  65.6 1.3 %collective-permute-start.19 = (bf16[64,256]{1,0:T(8,128)(2,1)S(1)}, bf16[64,256]{1,0:T(8,128)(2,1)S(1)}, u32[]{:S(2)}, u32[]{:S(2)}) collective-permute-start(bf16[64,256]{1,0:T(8,128)(2,1)S(1)} %get-tuple-element.98.refs_0_), channel_id=1, source_target_pairs={{0,28},{4,24},{8,20},{12,16},{16,12},{20,8},{24,4},{28,0},{1,29},{... | collective-permute-start | bytes 98312 | tf_op jit(solution)/shard_map/ppermute | solution.py:111
  67.0 3.2 %collective-permute-start.18 = (bf16[64,256]{1,0:T(8,128)(2,1)S(1)}, bf16[64,256]{1,0:T(8,128)(2,1)S(1)}, u32[]{:S(2)}, u32[]{:S(2)}) collective-permute-start(bf16[64,256]{1,0:T(8,128)(2,1)S(1)} %get-tuple-element.98.refs_0_), channel_id=1, source_target_pairs={{0,24},{4,28},{8,16},{12,20},{16,8},{20,12},{24,0},{28,4},{1,25},{... | collective-permute-start | bytes 98312 | tf_op jit(solution)/shard_map/ppermute | solution.py:111
  70.2 3.2 %collective-permute-start.16 = (bf16[64,256]{1,0:T(8,128)(2,1)S(1)}, bf16[64,256]{1,0:T(8,128)(2,1)S(1)}, u32[]{:S(2)}, u32[]{:S(2)}) collective-permute-start(bf16[64,256]{1,0:T(8,128)(2,1)S(1)} %get-tuple-element.98.refs_0_), channel_id=1, source_target_pairs={{0,16},{4,20},{8,24},{12,28},{16,0},{20,4},{24,8},{28,12},{1,17},{... | collective-permute-start | bytes 98312 | tf_op jit(solution)/shard_map/ppermute | solution.py:111
  73.3 5.9 %collective-permute-start.15 = (bf16[64,256]{1,0:T(8,128)(2,1)S(1)}, bf16[64,256]{1,0:T(8,128)(2,1)S(1)}, u32[]{:S(2)}, u32[]{:S(2)}) collective-permute-start(bf16[64,256]{1,0:T(8,128)(2,1)S(1)} %get-tuple-element.98.refs_0_), channel_id=1, source_target_pairs={{0,12},{4,8},{8,4},{12,0},{16,28},{20,24},{24,20},{28,16},{1,13},{... | collective-permute-start | bytes 98312 | tf_op jit(solution)/shard_map/ppermute | solution.py:111
  79.2 3.2 %collective-permute-start.14 = (bf16[64,256]{1,0:T(8,128)(2,1)S(1)}, bf16[64,256]{1,0:T(8,128)(2,1)S(1)}, u32[]{:S(2)}, u32[]{:S(2)}) collective-permute-start(bf16[64,256]{1,0:T(8,128)(2,1)S(1)} %get-tuple-element.98.refs_0_), channel_id=1, source_target_pairs={{0,8},{4,12},{8,0},{12,4},{16,24},{20,28},{24,16},{28,20},{1,9},{5... | collective-permute-start | bytes 98312 | tf_op jit(solution)/shard_map/ppermute | solution.py:111
  82.4 6.2 %own.1 = (bf16[256,1024]{1,0:T(8,128)(2,1)S(1)}, bf16[256,1024]{1,0:T(8,128)(2,1)S(1)}, bf16[1024,256]{1,0:T(8,128)(2,1)S(1)}, f32[256,1024]{1,0:T(8,128)S(1)}, ...) custom-call(f32[4,4]{1,0:T(4,128)S(1)} %copy-done.5, ...), custom_call_target="tpu_custom_call" | custom-call | tf_op jit(solution)/shard_map/own/pallas_call | solution.py:505
  88.7 0.9 window.1
  89.7 2.1 %rest.4.refs_0_ = bf16[256,256]{1,0:T(8,128)(2,1)S(1)} custom-call(s32[4,8]{1,0:T(4,128)S(1)} %bitcast.1, f32[4,4]{1,0:T(4,128)S(1)} %copy-done.5, bf16[256,1024]{1,0:T(8,128)(2,1)S(1)} %get-tuple-element.92.qt_ref, bf16[2048,256]{1,0:T(8,128)(2,1)S(1)} %get-tuple-element.99.kw_ref, bf16[256,2048]{1,0:T(8,128)(2,1)S(1)} %get-tuple-element.100.vw_ref, ...), custom_call_target="tpu_custom_call" | custom-call | tf_op jit(solution)/shard_map/rest/pallas_call | solution.py:565
  91.8 1.6 %collective-permute-start.21 = (bf16[256,256]{1,0:T(8,128)(2,1)S(1)}, bf16[256,256]{1,0:T(8,128)(2,1)S(1)}, u32[]{:S(2)}, u32[]{:S(2)}) collective-permute-start(bf16[256,256]{1,0:T(8,128)(2,1)S(1)} %rest.4.refs_0_), channel_id=1, source_target_pairs={{0,2},{2,0},{1,3},{3,1},{4,6},{6,4},{5,7},{7,5},{8,10},{10,8},{9,1... | collective-permute-start | bytes 393224 | tf_op jit(solution)/shard_map/ppermute | solution.py:52
  93.3 2.7 %rest.3.refs_0_ = bf16[384,256]{1,0:T(8,128)(2,1)S(1)} custom-call(s32[4,8]{1,0:T(4,128)S(1)} %bitcast.2, f32[4,4]{1,0:T(4,128)S(1)} %copy-done.5, bf16[256,1024]{1,0:T(8,128)(2,1)S(1)} %get-tuple-element.92.qt_ref, bf16[2048,256]{1,0:T(8,128)(2,1)S(1)} %get-tuple-element.99.kw_ref, bf16[256,2048]{1,0:T(8,128)(2,1)S(1)} %get-tuple-element.100.vw_ref, ...), custom_call_target="tpu_custom_call" | custom-call | tf_op jit(solution)/shard_map/rest/pallas_call | solution.py:565
  97.2 2.7 %rest.5.refs_0_ = bf16[384,256]{1,0:T(8,128)(2,1)S(1)} custom-call(s32[4,8]{1,0:T(4,128)S(1)} %bitcast.3, f32[4,4]{1,0:T(4,128)S(1)} %copy-done.5, bf16[256,1024]{1,0:T(8,128)(2,1)S(1)} %get-tuple-element.92.qt_ref, bf16[2048,256]{1,0:T(8,128)(2,1)S(1)} %get-tuple-element.99.kw_ref, bf16[256,2048]{1,0:T(8,128)(2,1)S(1)} %get-tuple-element.100.vw_ref, ...), custom_call_target="tpu_custom_call" | custom-call | tf_op jit(solution)/shard_map/rest/pallas_call | solution.py:565
  100.3 1.2 %output.3.refs_4_ = bf16[1024,256]{1,0:T(8,128)(2,1)} custom-call(bf16[1024,256]{1,0:T(8,128)(2,1)S(1)} %copy-done, bf16[256,256]{1,0:T(8,128)(2,1)S(1)} %rest.4.refs_0_, bf16[256,256]{1,0:T(8,128)(2,1)S(1)} %collective-permute-done.21.refs_1_, bf16[256,256]{1,0:T(8,128)(2,1)S(1)} %collective-permute-done.22.refs_2_, ...), custom_call_target="tpu_custom_call" | custom-call | tf_op jit(solution)/shard_map/output/pallas_call | solution.py:551
  101.8 2.1 %collective-permute-start.24 = (bf16[384,256]{1,0:T(8,128)(2,1)S(1)}, bf16[384,256]{1,0:T(8,128)(2,1)S(1)}, u32[]{:S(2)}, u32[]{:S(2)}) collective-permute-start(bf16[384,256]{1,0:T(8,128)(2,1)S(1)} %rest.5.refs_0_), channel_id=1, source_target_pairs={{0,2},{2,0},{1,3},{3,1},{4,6},{6,4},{5,7},{7,5},{8,10},{10,8},{9,1... | collective-permute-start | bytes 589832 | tf_op jit(solution)/shard_map/ppermute | solution.py:52
  104.2 1.8 %output.4.refs_4_ = bf16[1024,256]{1,0:T(8,128)(2,1)} custom-call(bf16[1024,256]{1,0:T(8,128)(2,1)S(1)} %copy-done, bf16[384,256]{1,0:T(8,128)(2,1)S(1)} %rest.3.refs_0_, bf16[384,256]{1,0:T(8,128)(2,1)S(1)} %collective-permute-done.20.refs_1_, bf16[384,256]{1,0:T(8,128)(2,1)S(1)} %collective-permute-done.25.refs_2_, ...), custom_call_target="tpu_custom_call", output_to_operand_aliasing={{}: (5, {})} | custom-call | tf_op jit(solution)/shard_map/output/pallas_call | solution.py:551
  105.9 3.6 %collective-permute-done.24.refs_1_ = bf16[384,256]{1,0:T(8,128)(2,1)S(1)} collective-permute-done((bf16[384,256]{1,0:T(8,128)(2,1)S(1)}, bf16[384,256]{1,0:T(8,128)(2,1)S(1)}, u32[]{:S(2)}, u32[]{:S(2)}) %collective-permute-start.24) | collective-permute-done | bytes 196640 | tf_op jit(solution)/shard_map/ppermute | solution.py:52
  109.5 1.4 %collective-permute-done.28.refs_3_ = bf16[384,256]{1,0:T(8,128)(2,1)S(1)} collective-permute-done((bf16[384,256]{1,0:T(8,128)(2,1)S(1)}, bf16[384,256]{1,0:T(8,128)(2,1)S(1)}, u32[]{:S(2)}, u32[]{:S(2)}) %collective-permute-start.28) | collective-permute-done | bytes 196640 | tf_op jit(solution)/shard_map/ppermute | solution.py:52
  110.9 1.8 %output.5 = bf16[1024,256]{1,0:T(8,128)(2,1)} custom-call(bf16[1024,256]{1,0:T(8,128)(2,1)S(1)} %copy-done, bf16[384,256]{1,0:T(8,128)(2,1)S(1)} %rest.5.refs_0_, bf16[384,256]{1,0:T(8,128)(2,1)S(1)} %collective-permute-done.24.refs_1_, bf16[384,256]{1,0:T(8,128)(2,1)S(1)} %collective-permute-done.27.refs_2_, ...), custom_call_target="tpu_custom_call", output_to_operand_aliasing={{}: (5, {})} | custom-call | tf_op jit(solution)/shard_map/output/pallas_call | solution.py:551
  (56 shorter events, 3.0 us)
Async XLA Ops:
  0.0 54.5 %copy-start.2 = (bf16[1024,256]{1,0:T(8,128)(2,1)S(1)}, bf16[1024,256]{1,0:T(8,128)(2,1)}, u32[]{:S(2)}) copy-start(bf16[1024,256]{1,0:T(8,128)(2,1)} %wv_ref.1) | copy-start | bytes 1572868
  0.0 54.5 %copy-start.3 = (bf16[1024,256]{1,0:T(8,128)(2,1)S(1)}, bf16[1024,256]{1,0:T(8,128)(2,1)}, u32[]{:S(2)}) copy-start(bf16[1024,256]{1,0:T(8,128)(2,1)} %wk_in.1) | copy-start | bytes 1572868
  0.0 54.5 %copy-start.1 = (bf16[1024,256]{1,0:T(8,128)(2,1)S(1)}, bf16[1024,256]{1,0:T(8,128)(2,1)}, u32[]{:S(2)}) copy-start(bf16[1024,256]{1,0:T(8,128)(2,1)} %wq_ref.1) | copy-start | bytes 1572868
  0.0 40.9 %collective-permute-start.7 = (s32[1,512]{1,0:T(1,128)}, s32[1,512]{1,0:T(1,128)S(1)}, u32[]{:S(2)}, u32[]{:S(2)}) collective-permute-start(s32[1,512]{1,0:T(1,128)} %mask_ref.1), channel_id=1, source_target_pairs={{0,4},{4,8},{8,12},{12,16},{16,20},{20,24},{24,28},{1,5},{5,9},{9,... | collective-permute-start | bytes 6152 | tf_op jit(solution)/shard_map/ppermute | solution.py:56
  34.1 8.3 %collective-permute-start = (bf16[128,256]{1,0:T(8,128)(2,1)}, bf16[128,256]{1,0:T(8,128)(2,1)S(1)}, u32[]{:S(2)}, u32[]{:S(2)}) collective-permute-start(bf16[128,256]{1,0:T(8,128)(2,1)} %get-tuple-element.60), channel_id=1, source_target_pairs={{0,28},{4,24},{8,20},{12,16},{16,12},{20,8},{24,4},{28,0},{1,29},{... | collective-permute-start | bytes 196616 | tf_op jit(solution)/shard_map/ppermute | solution.py:111
  36.6 9.1 %collective-permute-start.1 = (bf16[128,256]{1,0:T(8,128)(2,1)}, bf16[128,256]{1,0:T(8,128)(2,1)S(1)}, u32[]{:S(2)}, u32[]{:S(2)}) collective-permute-start(bf16[128,256]{1,0:T(8,128)(2,1)} %get-tuple-element.61), channel_id=1, source_target_pairs={{0,24},{4,28},{8,16},{12,20},{16,8},{20,12},{24,0},{28,4},{1,25},{... | collective-permute-start | bytes 196616 | tf_op jit(solution)/shard_map/ppermute | solution.py:111
  38.9 13.4 %collective-permute-start.4 = (bf16[128,512]{1,0:T(8,128)(2,1)}, bf16[128,512]{1,0:T(8,128)(2,1)S(1)}, u32[]{:S(2)}, u32[]{:S(2)}) collective-permute-start(bf16[128,512]{1,0:T(8,128)(2,1)} %get-tuple-element.64), channel_id=1, source_target_pairs={{0,12},{4,8},{8,4},{12,0},{16,28},{20,24},{24,20},{28,16},{1,13},{... | collective-permute-start | bytes 393224 | tf_op jit(solution)/shard_map/ppermute | solution.py:111
  38.9 13.4 %collective-permute-start.5 = (bf16[128,512]{1,0:T(8,128)(2,1)}, bf16[128,512]{1,0:T(8,128)(2,1)S(1)}, u32[]{:S(2)}, u32[]{:S(2)}) collective-permute-start(bf16[128,512]{1,0:T(8,128)(2,1)} %get-tuple-element.65), channel_id=1, source_target_pairs={{0,8},{4,12},{8,0},{12,4},{16,24},{20,28},{24,16},{28,20},{1,9},{5... | collective-permute-start | bytes 393224 | tf_op jit(solution)/shard_map/ppermute | solution.py:111
  40.9 11.5 %collective-permute-start.6 = (bf16[128,512]{1,0:T(8,128)(2,1)}, bf16[128,512]{1,0:T(8,128)(2,1)S(1)}, u32[]{:S(2)}, u32[]{:S(2)}) collective-permute-start(bf16[128,512]{1,0:T(8,128)(2,1)} %get-tuple-element.66), channel_id=1, source_target_pairs={{0,4},{4,0},{8,12},{12,8},{16,20},{20,16},{24,28},{28,24},{1,5},{5... | collective-permute-start | bytes 393224 | tf_op jit(solution)/shard_map/ppermute | solution.py:111
  42.4 7.0 %collective-permute-start.2 = (bf16[128,256]{1,0:T(8,128)(2,1)}, bf16[128,256]{1,0:T(8,128)(2,1)S(1)}, u32[]{:S(2)}, u32[]{:S(2)}) collective-permute-start(bf16[128,256]{1,0:T(8,128)(2,1)} %get-tuple-element.62), channel_id=1, source_target_pairs={{0,20},{4,16},{8,28},{12,24},{16,4},{20,0},{24,12},{28,8},{1,21},{... | collective-permute-start | bytes 196616 | tf_op jit(solution)/shard_map/ppermute | solution.py:111
  45.7 6.7 %collective-permute-start.3 = (bf16[128,256]{1,0:T(8,128)(2,1)}, bf16[128,256]{1,0:T(8,128)(2,1)S(1)}, u32[]{:S(2)}, u32[]{:S(2)}) collective-permute-start(bf16[128,256]{1,0:T(8,128)(2,1)} %get-tuple-element.63), channel_id=1, source_target_pairs={{0,16},{4,20},{8,24},{12,28},{16,0},{20,4},{24,8},{28,12},{1,17},{... | collective-permute-start | bytes 196616 | tf_op jit(solution)/shard_map/ppermute | solution.py:111
  52.4 6.4 %collective-permute-start.8 = (bf16[512,256]{1,0:T(8,128)(2,1)S(1)}, bf16[512,256]{1,0:T(8,128)(2,1)S(1)}, u32[]{:S(2)}, u32[]{:S(2)}) collective-permute-start(bf16[512,256]{1,0:T(8,128)(2,1)S(1)} %get-tuple-element.67.early_ref.refs_0_), channel_id=1, source_target_pairs={{0,2},{2,0},{1,3},{3,1},{4,6},{6,4},{5,7},{7,5},{8,10},{10,8},{9,1... | collective-permute-start | bytes 786440 | tf_op jit(solution)/shard_map/ppermute | solution.py:52
  54.0 4.9 %collective-permute-start.11 = (bf16[384,512]{1,0:T(8,128)(2,1)S(1)}, bf16[384,512]{1,0:T(8,128)(2,1)S(1)}, u32[]{:S(2)}, u32[]{:S(2)}) collective-permute-start(bf16[384,512]{1,0:T(8,128)(2,1)S(1)} %get-tuple-element.85.refs_4_), channel_id=1, source_target_pairs={{0,1},{1,0},{2,3},{3,2},{4,5},{5,4},{6,7},{7,6},{8,9},{9,8},{10,11... | collective-permute-start | bytes 1179656 | tf_op jit(solution)/shard_map/ppermute | solution.py:52
  54.0 4.9 %collective-permute-start.9 = (bf16[512,256]{1,0:T(8,128)(2,1)S(1)}, bf16[512,256]{1,0:T(8,128)(2,1)S(1)}, u32[]{:S(2)}, u32[]{:S(2)}) collective-permute-start(bf16[512,256]{1,0:T(8,128)(2,1)S(1)} %get-tuple-element.67.early_ref.refs_0_), channel_id=1, source_target_pairs={{0,1},{1,0},{2,3},{3,2},{4,5},{5,4},{6,7},{7,6},{8,9},{9,8},{10,11... | collective-permute-start | bytes 786440 | tf_op jit(solution)/shard_map/ppermute | solution.py:52
  58.9 1.5 %collective-permute-start.10 = (bf16[512,256]{1,0:T(8,128)(2,1)S(1)}, bf16[512,256]{1,0:T(8,128)(2,1)S(1)}, u32[]{:S(2)}, u32[]{:S(2)}) collective-permute-start(bf16[512,256]{1,0:T(8,128)(2,1)S(1)} %collective-permute-done.8.refs_1_), channel_id=1, source_target_pairs={{0,1},{1,0},{2,3},{3,2},{4,5},{5,4},{6,7},{7,6},{8,9},{9,8},{10,11... | collective-permute-start | bytes 786440 | tf_op jit(solution)/shard_map/ppermute | solution.py:52
  62.7 26.1 %collective-permute-start.12 = (bf16[1024,256]{1,0:T(8,128)(2,1)S(1)}, bf16[1024,256]{1,0:T(8,128)(2,1)S(1)}, u32[]{:S(2)}, u32[]{:S(2)}) collective-permute-start(bf16[1024,256]{1,0:T(8,128)(2,1)S(1)} %get-tuple-element.95), channel_id=1, source_target_pairs={{0,4},{4,8},{8,12},{12,16},{16,20},{20,24},{24,28},{1,5},{5,9},{9,... | collective-permute-start | bytes 1572872 | tf_op jit(solution)/shard_map/ppermute | solution.py:56
  65.6 7.7 %collective-permute-start.19 = (bf16[64,256]{1,0:T(8,128)(2,1)S(1)}, bf16[64,256]{1,0:T(8,128)(2,1)S(1)}, u32[]{:S(2)}, u32[]{:S(2)}) collective-permute-start(bf16[64,256]{1,0:T(8,128)(2,1)S(1)} %get-tuple-element.98.refs_0_), channel_id=1, source_target_pairs={{0,28},{4,24},{8,20},{12,16},{16,12},{20,8},{24,4},{28,0},{1,29},{... | collective-permute-start | bytes 98312 | tf_op jit(solution)/shard_map/ppermute | solution.py:111
  67.0 12.3 %collective-permute-start.18 = (bf16[64,256]{1,0:T(8,128)(2,1)S(1)}, bf16[64,256]{1,0:T(8,128)(2,1)S(1)}, u32[]{:S(2)}, u32[]{:S(2)}) collective-permute-start(bf16[64,256]{1,0:T(8,128)(2,1)S(1)} %get-tuple-element.98.refs_0_), channel_id=1, source_target_pairs={{0,24},{4,28},{8,16},{12,20},{16,8},{20,12},{24,0},{28,4},{1,25},{... | collective-permute-start | bytes 98312 | tf_op jit(solution)/shard_map/ppermute | solution.py:111
  70.2 12.3 %collective-permute-start.17 = (bf16[64,256]{1,0:T(8,128)(2,1)S(1)}, bf16[64,256]{1,0:T(8,128)(2,1)S(1)}, u32[]{:S(2)}, u32[]{:S(2)}) collective-permute-start(bf16[64,256]{1,0:T(8,128)(2,1)S(1)} %get-tuple-element.98.refs_0_), channel_id=1, source_target_pairs={{0,20},{4,16},{8,28},{12,24},{16,4},{20,0},{24,12},{28,8},{1,21},{... | collective-permute-start | bytes 98312 | tf_op jit(solution)/shard_map/ppermute | solution.py:111
  70.2 18.5 %collective-permute-start.16 = (bf16[64,256]{1,0:T(8,128)(2,1)S(1)}, bf16[64,256]{1,0:T(8,128)(2,1)S(1)}, u32[]{:S(2)}, u32[]{:S(2)}) collective-permute-start(bf16[64,256]{1,0:T(8,128)(2,1)S(1)} %get-tuple-element.98.refs_0_), channel_id=1, source_target_pairs={{0,16},{4,20},{8,24},{12,28},{16,0},{20,4},{24,8},{28,12},{1,17},{... | collective-permute-start | bytes 98312 | tf_op jit(solution)/shard_map/ppermute | solution.py:111
  73.3 15.4 %collective-permute-start.15 = (bf16[64,256]{1,0:T(8,128)(2,1)S(1)}, bf16[64,256]{1,0:T(8,128)(2,1)S(1)}, u32[]{:S(2)}, u32[]{:S(2)}) collective-permute-start(bf16[64,256]{1,0:T(8,128)(2,1)S(1)} %get-tuple-element.98.refs_0_), channel_id=1, source_target_pairs={{0,12},{4,8},{8,4},{12,0},{16,28},{20,24},{24,20},{28,16},{1,13},{... | collective-permute-start | bytes 98312 | tf_op jit(solution)/shard_map/ppermute | solution.py:111
  79.2 9.5 %collective-permute-start.14 = (bf16[64,256]{1,0:T(8,128)(2,1)S(1)}, bf16[64,256]{1,0:T(8,128)(2,1)S(1)}, u32[]{:S(2)}, u32[]{:S(2)}) collective-permute-start(bf16[64,256]{1,0:T(8,128)(2,1)S(1)} %get-tuple-element.98.refs_0_), channel_id=1, source_target_pairs={{0,8},{4,12},{8,0},{12,4},{16,24},{20,28},{24,16},{28,20},{1,9},{5... | collective-permute-start | bytes 98312 | tf_op jit(solution)/shard_map/ppermute | solution.py:111
  82.4 6.3 %collective-permute-start.13 = (bf16[64,256]{1,0:T(8,128)(2,1)S(1)}, bf16[64,256]{1,0:T(8,128)(2,1)S(1)}, u32[]{:S(2)}, u32[]{:S(2)}) collective-permute-start(bf16[64,256]{1,0:T(8,128)(2,1)S(1)} %get-tuple-element.98.refs_0_), channel_id=1, source_target_pairs={{0,4},{4,0},{8,12},{12,8},{16,20},{20,16},{24,28},{28,24},{1,5},{5... | collective-permute-start | bytes 98312 | tf_op jit(solution)/shard_map/ppermute | solution.py:111
  91.8 5.2 %collective-permute-start.21 = (bf16[256,256]{1,0:T(8,128)(2,1)S(1)}, bf16[256,256]{1,0:T(8,128)(2,1)S(1)}, u32[]{:S(2)}, u32[]{:S(2)}) collective-permute-start(bf16[256,256]{1,0:T(8,128)(2,1)S(1)} %rest.4.refs_0_), channel_id=1, source_target_pairs={{0,2},{2,0},{1,3},{3,1},{4,6},{6,4},{5,7},{7,5},{8,10},{10,8},{9,1... | collective-permute-start | bytes 393224 | tf_op jit(solution)/shard_map/ppermute | solution.py:52
  96.1 5.7 %collective-permute-start.20 = (bf16[384,256]{1,0:T(8,128)(2,1)S(1)}, bf16[384,256]{1,0:T(8,128)(2,1)S(1)}, u32[]{:S(2)}, u32[]{:S(2)}) collective-permute-start(bf16[384,256]{1,0:T(8,128)(2,1)S(1)} %rest.3.refs_0_), channel_id=1, source_target_pairs={{0,2},{2,0},{1,3},{3,1},{4,6},{6,4},{5,7},{7,5},{8,10},{10,8},{9,1... | collective-permute-start | bytes 589832 | tf_op jit(solution)/shard_map/ppermute | solution.py:52
  96.7 3.6 %collective-permute-start.22 = (bf16[256,256]{1,0:T(8,128)(2,1)S(1)}, bf16[256,256]{1,0:T(8,128)(2,1)S(1)}, u32[]{:S(2)}, u32[]{:S(2)}) collective-permute-start(bf16[256,256]{1,0:T(8,128)(2,1)S(1)} %rest.4.refs_0_), channel_id=1, source_target_pairs={{0,1},{1,0},{2,3},{3,2},{4,5},{5,4},{6,7},{7,6},{8,9},{9,8},{10,11... | collective-permute-start | bytes 393224 | tf_op jit(solution)/shard_map/ppermute | solution.py:52
  96.9 3.3 %collective-permute-start.23 = (bf16[256,256]{1,0:T(8,128)(2,1)S(1)}, bf16[256,256]{1,0:T(8,128)(2,1)S(1)}, u32[]{:S(2)}, u32[]{:S(2)}) collective-permute-start(bf16[256,256]{1,0:T(8,128)(2,1)S(1)} %collective-permute-done.21.refs_1_), channel_id=1, source_target_pairs={{0,1},{1,0},{2,3},{3,2},{4,5},{5,4},{6,7},{7,6},{8,9},{9,8},{10,11... | collective-permute-start | bytes 393224 | tf_op jit(solution)/shard_map/ppermute | solution.py:52
  99.9 4.2 %collective-permute-start.25 = (bf16[384,256]{1,0:T(8,128)(2,1)S(1)}, bf16[384,256]{1,0:T(8,128)(2,1)S(1)}, u32[]{:S(2)}, u32[]{:S(2)}) collective-permute-start(bf16[384,256]{1,0:T(8,128)(2,1)S(1)} %rest.3.refs_0_), channel_id=1, source_target_pairs={{0,1},{1,0},{2,3},{3,2},{4,5},{5,4},{6,7},{7,6},{8,9},{9,8},{10,11... | collective-permute-start | bytes 589832 | tf_op jit(solution)/shard_map/ppermute | solution.py:52
  101.8 2.3 %collective-permute-start.26 = (bf16[384,256]{1,0:T(8,128)(2,1)S(1)}, bf16[384,256]{1,0:T(8,128)(2,1)S(1)}, u32[]{:S(2)}, u32[]{:S(2)}) collective-permute-start(bf16[384,256]{1,0:T(8,128)(2,1)S(1)} %collective-permute-done.20.refs_1_), channel_id=1, source_target_pairs={{0,1},{1,0},{2,3},{3,2},{4,5},{5,4},{6,7},{7,6},{8,9},{9,8},{10,11... | collective-permute-start | bytes 589832 | tf_op jit(solution)/shard_map/ppermute | solution.py:52
  101.8 7.7 %collective-permute-start.24 = (bf16[384,256]{1,0:T(8,128)(2,1)S(1)}, bf16[384,256]{1,0:T(8,128)(2,1)S(1)}, u32[]{:S(2)}, u32[]{:S(2)}) collective-permute-start(bf16[384,256]{1,0:T(8,128)(2,1)S(1)} %rest.5.refs_0_), channel_id=1, source_target_pairs={{0,2},{2,0},{1,3},{3,1},{4,6},{6,4},{5,7},{7,5},{8,10},{10,8},{9,1... | collective-permute-start | bytes 589832 | tf_op jit(solution)/shard_map/ppermute | solution.py:52
  104.0 5.5 %collective-permute-start.27 = (bf16[384,256]{1,0:T(8,128)(2,1)S(1)}, bf16[384,256]{1,0:T(8,128)(2,1)S(1)}, u32[]{:S(2)}, u32[]{:S(2)}) collective-permute-start(bf16[384,256]{1,0:T(8,128)(2,1)S(1)} %rest.5.refs_0_), channel_id=1, source_target_pairs={{0,1},{1,0},{2,3},{3,2},{4,5},{5,4},{6,7},{7,6},{8,9},{9,8},{10,11... | collective-permute-start | bytes 589832 | tf_op jit(solution)/shard_map/ppermute | solution.py:52
  109.5 1.4 %collective-permute-start.28 = (bf16[384,256]{1,0:T(8,128)(2,1)S(1)}, bf16[384,256]{1,0:T(8,128)(2,1)S(1)}, u32[]{:S(2)}, u32[]{:S(2)}) collective-permute-start(bf16[384,256]{1,0:T(8,128)(2,1)S(1)} %collective-permute-done.24.refs_1_), channel_id=1, source_target_pairs={{0,1},{1,0},{2,3},{3,2},{4,5},{5,4},{6,7},{7,6},{8,9},{9,8},{10,11... | collective-permute-start | bytes 589832 | tf_op jit(solution)/shard_map/ppermute | solution.py:52
  (6 other events, 162.6 us)

commit v5 on v4

--- a/solution.py
+++ b/solution.py
@@ -57,30 +57,18 @@
 
 
 def send_kernel(distances, tokens_ref, *refs):
-    outs, own, sem_ref = refs[:-2], refs[-2], refs[-1]
+    outs, own = refs[:-1], refs[-1]
     slab, head = lax.axis_index("seq"), lax.axis_index("head")
-    rows = outs[0].shape[0]
+    rows = own.shape[0]
     quarter = tokens_ref.shape[1] // 4
-    copies = []
     for distance, out in zip(distances, outs):
         row = pl.multiple_of((slab ^ distance) * rows, rows)
         for part in range(out.shape[1] // quarter):
             start = pl.multiple_of((head ^ (2 * part)) * quarter, quarter)
-            copies.append(
-                pltpu.make_async_copy(
-                    tokens_ref.at[pl.ds(row, rows), pl.ds(start, quarter)],
-                    out.at[:, part * quarter : (part + 1) * quarter],
-                    sem_ref.at[len(copies)],
-                )
-            )
-    row = pl.multiple_of(slab * rows, rows)
-    copies.append(
-        pltpu.make_async_copy(tokens_ref.at[pl.ds(row, rows)], own, sem_ref.at[len(copies)])
-    )
-    for copy in copies:
-        copy.start()
-    for copy in copies:
-        copy.wait()
+            out[:, part * quarter : (part + 1) * quarter] = tokens_ref[
+                pl.ds(row, rows), pl.ds(start, quarter)
+            ]
+    own[...] = tokens_ref[pl.ds(pl.multiple_of(slab * rows, rows), rows)]
 
 
 def stack_kernel(counts, *refs):
@@ -134,10 +122,9 @@
             jax.ShapeDtypeStruct((rows, columns), BF)
             for columns in [quarter if d > 3 else 2 * quarter for d in distances] + [width]
         ),
-        in_specs=[pl.BlockSpec(memory_space=pl.ANY)],
-        out_specs=[pl.BlockSpec(memory_space=pl.ANY)] * 8,
-        scratch_shapes=[pltpu.SemaphoreType.DMA((11,))],
-        compiler_params=pltpu.CompilerParams(vmem_limit_bytes=60 * 1024 * 1024),
+        in_specs=vmem_specs(1),
+        out_specs=vmem_specs(8),
+        compiler_params=pltpu.CompilerParams(vmem_limit_bytes=VMEM_LIMIT),
         name="send",
     )(tokens)
     arrived = [by_distance(block, d) for block, d in zip(blocks, distances)]

time: 114 us -> 86.8 us (0.76)
  the two profiles are of different devices: /device:TPU:0 before, /device:TPU:27 now
where the time goes in v5:
time: 86.8 us; the launch traced here: 86.6 us
  starting transfers between devices  40 us (46%)
  Pallas kernels  25.3 us (29%)
  waiting for transfers between devices  19.3 us (22%)
  local copies, waits for them, and re-layouts  1.62 us (2%)
    ppermute x14, starting transfers between devices, by_distance(): lax.ppermute(block, 'seq', [(i, i ^ distance) for i in range(lax.axis_siz...  18.2 us
    ppermute x13, starting transfers between devices, over_head(): return lax.ppermute(block, 'head', pairs)  14.9 us
    ppermute x14, waiting for transfers between devices, by_distance(): lax.ppermute(block, 'seq', [(i, i ^ distance) for i in range(lax.axis_siz...  12.7 us
    pallas_call x3, Pallas kernels, local(): pl.pallas_call(functools.partial(rest_kernel, first, count), out_shape=sh...  7.58 us
    ppermute x2, starting transfers between devices, to_next(): lax.ppermute(block, 'seq', [(i, i + 1) for i in range(lax.axis_size('seq'...  6.95 us
    ppermute x13, waiting for transfers between devices, over_head(): return lax.ppermute(block, 'head', pairs)  6.66 us
    pallas_call x1, Pallas kernels, local(): pl.pallas_call(own_kernel, out_shape=(shape((group, tok_rows), BF), shape...  6.2 us
    pallas_call x3, Pallas kernels, finish(): pl.pallas_call(output_kernel, grid=(rows // FBLK,), out_shape=shape((tok_...  4.66 us
  transfers between devices with their start and end apart: 29, of which 9 were waited for; matrix products, arithmetic and copies ran while one was open for 0% of the time, Pallas kernels for 21%

profile of v5, /device:TPU:27, one launch (start us, length us, event | category | flops | bytes accessed | tf_op | source)
XLA Modules:
  0.0 86.6 jit_solution(14377667047201789259)
XLA Ops:
  0.0 3.1 %collective-permute-start.7 = (s32[1,512]{1,0:T(1,128)}, s32[1,512]{1,0:T(1,128)S(1)}, u32[]{:S(2)}, u32[]{:S(2)}) collective-permute-start(s32[1,512]{1,0:T(1,128)} %mask_ref.1), channel_id=1, source_target_pairs={{0,4},{4,8},{8,12},{12,16},{16,20},{20,24},{24,28},{1,5},{5,9},{9,... | collective-permute-start | bytes 6152 | tf_op jit(solution)/shard_map/ppermute | solution.py:56
  3.2 1.6 %copy-done.1 = bf16[1024,1024]{1,0:T(8,128)(2,1)S(1)} copy-done((bf16[1024,1024]{1,0:T(8,128)(2,1)S(1)}, bf16[1024,1024]{1,0:T(8,128)(2,1)}, u32[]{:S(2)}) %copy-start.1) | copy-done | bytes 2097176
  4.9 1.0 %collective-permute-start = (bf16[128,256]{1,0:T(8,128)(2,1)S(1)}, bf16[128,256]{1,0:T(8,128)(2,1)S(1)}, u32[]{:S(2)}, u32[]{:S(2)}) collective-permute-start(bf16[128,256]{1,0:T(8,128)(2,1)S(1)} %get-tuple-element.60), channel_id=1, source_target_pairs={{0,28},{4,24},{8,20},{12,16},{16,12},{20,8},{24,4},{28,0},{1,29},{... | collective-permute-start | bytes 196616 | tf_op jit(solution)/shard_map/ppermute | solution.py:99
  5.8 1.5 %collective-permute-start.1 = (bf16[128,256]{1,0:T(8,128)(2,1)S(1)}, bf16[128,256]{1,0:T(8,128)(2,1)S(1)}, u32[]{:S(2)}, u32[]{:S(2)}) collective-permute-start(bf16[128,256]{1,0:T(8,128)(2,1)S(1)} %get-tuple-element.61), channel_id=1, source_target_pairs={{0,24},{4,28},{8,16},{12,20},{16,8},{20,12},{24,0},{28,4},{1,25},{... | collective-permute-start | bytes 196616 | tf_op jit(solution)/shard_map/ppermute | solution.py:99
  7.5 3.1 %collective-permute-start.5 = (bf16[128,512]{1,0:T(8,128)(2,1)S(1)}, bf16[128,512]{1,0:T(8,128)(2,1)S(1)}, u32[]{:S(2)}, u32[]{:S(2)}) collective-permute-start(bf16[128,512]{1,0:T(8,128)(2,1)S(1)} %get-tuple-element.65), channel_id=1, source_target_pairs={{0,8},{4,12},{8,0},{12,4},{16,24},{20,28},{24,16},{28,20},{1,9},{5... | collective-permute-start | bytes 393224 | tf_op jit(solution)/shard_map/ppermute | solution.py:99
  10.9 3.2 %collective-permute-start.3 = (bf16[128,256]{1,0:T(8,128)(2,1)S(1)}, bf16[128,256]{1,0:T(8,128)(2,1)S(1)}, u32[]{:S(2)}, u32[]{:S(2)}) collective-permute-start(bf16[128,256]{1,0:T(8,128)(2,1)S(1)} %get-tuple-element.63), channel_id=1, source_target_pairs={{0,16},{4,20},{8,24},{12,28},{16,0},{20,4},{24,8},{28,12},{1,17},{... | collective-permute-start | bytes 196616 | tf_op jit(solution)/shard_map/ppermute | solution.py:99
  14.1 2.2 %collective-permute-done.2.refs_2_ = bf16[128,256]{1,0:T(8,128)(2,1)S(1)} collective-permute-done((bf16[128,256]{1,0:T(8,128)(2,1)S(1)}, bf16[128,256]{1,0:T(8,128)(2,1)S(1)}, u32[]{:S(2)}, u32[]{:S(2)}) %collective-permute-start.2) | collective-permute-done | bytes 65568 | tf_op jit(solution)/shard_map/ppermute | solution.py:99
  16.4 1.4 %collective-permute-done.3.refs_3_ = bf16[128,256]{1,0:T(8,128)(2,1)S(1)} collective-permute-done((bf16[128,256]{1,0:T(8,128)(2,1)S(1)}, bf16[128,256]{1,0:T(8,128)(2,1)S(1)}, u32[]{:S(2)}, u32[]{:S(2)}) %collective-permute-start.3) | collective-permute-done | bytes 65568 | tf_op jit(solution)/shard_map/ppermute | solution.py:99
  18.6 3.8 %collective-permute-start.11 = (bf16[384,512]{1,0:T(8,128)(2,1)S(1)}, bf16[384,512]{1,0:T(8,128)(2,1)S(1)}, u32[]{:S(2)}, u32[]{:S(2)}) collective-permute-start(bf16[384,512]{1,0:T(8,128)(2,1)S(1)} %get-tuple-element.85.refs_4_), channel_id=1, source_target_pairs={{0,1},{1,0},{2,3},{3,2},{4,5},{5,4},{6,7},{7,6},{8,9},{9,8},{10,11... | collective-permute-start | bytes 1179656 | tf_op jit(solution)/shard_map/ppermute | solution.py:52
  22.4 3.5 %prepare.1 = (bf16[1024,1024]{1,0:T(8,128)(2,1)S(1)}, bf16[1024,1024]{1,0:T(8,128)(2,1)S(1)}, bf16[672,1024]{1,0:T(8,128)(2,1)S(1)}, f32[160,128]{1,0:T(8,128)S(...) custom-call(s32[1,1024]{1,0:T(1,128)S(1)} %copy-done.7, ...), custom_call_target="tpu_custom_call" | custom-call | tf_op jit(solution)/shard_map/prepare/pallas_call | solution.py:446
  26.0 2.3 %collective-permute-start.10 = (bf16[512,256]{1,0:T(8,128)(2,1)S(1)}, bf16[512,256]{1,0:T(8,128)(2,1)S(1)}, u32[]{:S(2)}, u32[]{:S(2)}) collective-permute-start(bf16[512,256]{1,0:T(8,128)(2,1)S(1)} %collective-permute-done.8.refs_1_), channel_id=1, source_target_pairs={{0,1},{1,0},{2,3},{3,2},{4,5},{5,4},{6,7},{7,6},{8,9},{9,8},{10,11... | collective-permute-start | bytes 786440 | tf_op jit(solution)/shard_map/ppermute | solution.py:52
  28.2 1.2 %collective-permute-done.10.refs_3_ = bf16[512,256]{1,0:T(8,128)(2,1)S(1)} collective-permute-done((bf16[512,256]{1,0:T(8,128)(2,1)S(1)}, bf16[512,256]{1,0:T(8,128)(2,1)S(1)}, u32[]{:S(2)}, u32[]{:S(2)}) %collective-permute-start.10) | collective-permute-done | bytes 262176 | tf_op jit(solution)/shard_map/ppermute | solution.py:52
  29.4 2.3 %project.1 = (bf16[1024,256]{1,0:T(8,128)(2,1)S(1)}, bf16[64,256]{1,0:T(8,128)(2,1)S(1)}, bf16[1024,256]{1,0:T(8,128)(2,1)S(1)}, bf16[256,1024]{1,0:T(8,128)(2,1)S(1)}, bf16[1024,1024]{1,0:T(8,128)(2,1)S(1)}) custom-call(bf16[512,256]{1,0:T(8,128)(2,1)S(1)} %get-tuple-element.67.early_ref.refs_0_, bf16[512,256]{1,0:T(8,128)(2,1)S(1)} %collective-permute-done.8.refs_1_, ...), custom_call_target="tpu_custom_call" | custom-call | tf_op jit(solution)/shard_map/project/pallas_call | solution.py:469
  31.7 3.8 %collective-permute-start.12 = (bf16[1024,256]{1,0:T(8,128)(2,1)S(1)}, bf16[1024,256]{1,0:T(8,128)(2,1)S(1)}, u32[]{:S(2)}, u32[]{:S(2)}) collective-permute-start(bf16[1024,256]{1,0:T(8,128)(2,1)S(1)} %get-tuple-element.95), channel_id=1, source_target_pairs={{0,4},{4,8},{8,12},{12,16},{16,20},{20,24},{24,28},{1,5},{5,9},{9,... | collective-permute-start | bytes 1572872 | tf_op jit(solution)/shard_map/ppermute | solution.py:56
  35.5 1.7 %collective-permute-start.19 = (bf16[64,256]{1,0:T(8,128)(2,1)S(1)}, bf16[64,256]{1,0:T(8,128)(2,1)S(1)}, u32[]{:S(2)}, u32[]{:S(2)}) collective-permute-start(bf16[64,256]{1,0:T(8,128)(2,1)S(1)} %get-tuple-element.98.refs_0_), channel_id=1, source_target_pairs={{0,28},{4,24},{8,20},{12,16},{16,12},{20,8},{24,4},{28,0},{1,29},{... | collective-permute-start | bytes 98312 | tf_op jit(solution)/shard_map/ppermute | solution.py:99
  37.9 4.2 %collective-permute-start.16 = (bf16[64,256]{1,0:T(8,128)(2,1)S(1)}, bf16[64,256]{1,0:T(8,128)(2,1)S(1)}, u32[]{:S(2)}, u32[]{:S(2)}) collective-permute-start(bf16[64,256]{1,0:T(8,128)(2,1)S(1)} %get-tuple-element.98.refs_0_), channel_id=1, source_target_pairs={{0,16},{4,20},{8,24},{12,28},{16,0},{20,4},{24,8},{28,12},{1,17},{... | collective-permute-start | bytes 98312 | tf_op jit(solution)/shard_map/ppermute | solution.py:99
  42.1 8.3 %collective-permute-done.19.refs_7_ = bf16[64,256]{1,0:T(8,128)(2,1)S(1)} collective-permute-done((bf16[64,256]{1,0:T(8,128)(2,1)S(1)}, bf16[64,256]{1,0:T(8,128)(2,1)S(1)}, u32[]{:S(2)}, u32[]{:S(2)}) %collective-permute-start.19) | collective-permute-done | bytes 32800 | tf_op jit(solution)/shard_map/ppermute | solution.py:99
  50.4 2.6 %collective-permute-start.13 = (bf16[64,256]{1,0:T(8,128)(2,1)S(1)}, bf16[64,256]{1,0:T(8,128)(2,1)S(1)}, u32[]{:S(2)}, u32[]{:S(2)}) collective-permute-start(bf16[64,256]{1,0:T(8,128)(2,1)S(1)} %get-tuple-element.98.refs_0_), channel_id=1, source_target_pairs={{0,4},{4,0},{8,12},{12,8},{16,20},{20,16},{24,28},{28,24},{1,5},{5... | collective-permute-start | bytes 98312 | tf_op jit(solution)/shard_map/ppermute | solution.py:99
  53.0 6.2 %own.1 = (bf16[256,1024]{1,0:T(8,128)(2,1)S(1)}, bf16[256,1024]{1,0:T(8,128)(2,1)S(1)}, bf16[1024,256]{1,0:T(8,128)(2,1)S(1)}, f32[256,1024]{1,0:T(8,128)S(1)}, ...) custom-call(f32[4,4]{1,0:T(4,128)S(1)} %copy-done.5, ...), custom_call_target="tpu_custom_call" | custom-call | tf_op jit(solution)/shard_map/own/pallas_call | solution.py:492
  59.3 0.9 %window.1 = (bf16[2048,256]{1,0:T(8,128)(2,1)S(1)}, bf16[256,2048]{1,0:T(8,128)(2,1)S(1)}, bf16[64,256]{1,0:T(8,128)(2,1)S(1)}, bf16[256,64]{1,0:T(8,128)(2,1)S(1)}) custom-call(bf16[1024,256]{1,0:T(8,128)(2,1)S(1)} %get-tuple-element.93.k_ref, bf16[256,1024]{1,0:T(8,128)(2,1)S(1)} %get-tuple-element.94.vt_ref, ...), custom_call_target="tpu_custom_call" | custom-call | tf_op jit(solution)/shard_map/window/pallas_call | solution.py:513
  60.2 2.1 %rest.4.refs_0_ = bf16[256,256]{1,0:T(8,128)(2,1)S(1)} custom-call(s32[4,8]{1,0:T(4,128)S(1)} %bitcast.1, f32[4,4]{1,0:T(4,128)S(1)} %copy-done.5, bf16[256,1024]{1,0:T(8,128)(2,1)S(1)} %get-tuple-element.92.qt_ref, bf16[2048,256]{1,0:T(8,128)(2,1)S(1)} %get-tuple-element.99.kw_ref, bf16[256,2048]{1,0:T(8,128)(2,1)S(1)} %get-tuple-element.100.vw_ref, ...), custom_call_target="tpu_custom_call" | custom-call | tf_op jit(solution)/shard_map/rest/pallas_call | solution.py:552
  62.7 2.7 %rest.3.refs_0_ = bf16[384,256]{1,0:T(8,128)(2,1)S(1)} custom-call(s32[4,8]{1,0:T(4,128)S(1)} %bitcast.2, f32[4,4]{1,0:T(4,128)S(1)} %copy-done.5, bf16[256,1024]{1,0:T(8,128)(2,1)S(1)} %get-tuple-element.92.qt_ref, bf16[2048,256]{1,0:T(8,128)(2,1)S(1)} %get-tuple-element.99.kw_ref, bf16[256,2048]{1,0:T(8,128)(2,1)S(1)} %get-tuple-element.100.vw_ref, ...), custom_call_target="tpu_custom_call" | custom-call | tf_op jit(solution)/shard_map/rest/pallas_call | solution.py:552
  65.4 1.3 %collective-permute-start.20 = (bf16[384,256]{1,0:T(8,128)(2,1)S(1)}, bf16[384,256]{1,0:T(8,128)(2,1)S(1)}, u32[]{:S(2)}, u32[]{:S(2)}) collective-permute-start(bf16[384,256]{1,0:T(8,128)(2,1)S(1)} %rest.3.refs_0_), channel_id=1, source_target_pairs={{0,2},{2,0},{1,3},{3,1},{4,6},{6,4},{5,7},{7,5},{8,10},{10,8},{9,1... | collective-permute-start | bytes 589832 | tf_op jit(solution)/shard_map/ppermute | solution.py:52
  66.7 3.8 %collective-permute-start.22 = (bf16[256,256]{1,0:T(8,128)(2,1)S(1)}, bf16[256,256]{1,0:T(8,128)(2,1)S(1)}, u32[]{:S(2)}, u32[]{:S(2)}) collective-permute-start(bf16[256,256]{1,0:T(8,128)(2,1)S(1)} %rest.4.refs_0_), channel_id=1, source_target_pairs={{0,1},{1,0},{2,3},{3,2},{4,5},{5,4},{6,7},{7,6},{8,9},{9,8},{10,11... | collective-permute-start | bytes 393224 | tf_op jit(solution)/shard_map/ppermute | solution.py:52
  70.5 1.5 %collective-permute-start.23 = (bf16[256,256]{1,0:T(8,128)(2,1)S(1)}, bf16[256,256]{1,0:T(8,128)(2,1)S(1)}, u32[]{:S(2)}, u32[]{:S(2)}) collective-permute-start(bf16[256,256]{1,0:T(8,128)(2,1)S(1)} %collective-permute-done.21.refs_1_), channel_id=1, source_target_pairs={{0,1},{1,0},{2,3},{3,2},{4,5},{5,4},{6,7},{7,6},{8,9},{9,8},{10,11... | collective-permute-start | bytes 393224 | tf_op jit(solution)/shard_map/ppermute | solution.py:52
  71.9 2.7 %rest.5.refs_0_ = bf16[384,256]{1,0:T(8,128)(2,1)S(1)} custom-call(s32[4,8]{1,0:T(4,128)S(1)} %bitcast.3, f32[4,4]{1,0:T(4,128)S(1)} %copy-done.5, bf16[256,1024]{1,0:T(8,128)(2,1)S(1)} %get-tuple-element.92.qt_ref, bf16[2048,256]{1,0:T(8,128)(2,1)S(1)} %get-tuple-element.99.kw_ref, bf16[256,2048]{1,0:T(8,128)(2,1)S(1)} %get-tuple-element.100.vw_ref, ...), custom_call_target="tpu_custom_call" | custom-call | tf_op jit(solution)/shard_map/rest/pallas_call | solution.py:552
  74.8 1.2 %output.3.refs_4_ = bf16[1024,256]{1,0:T(8,128)(2,1)} custom-call(bf16[1024,256]{1,0:T(8,128)(2,1)S(1)} %copy-done, bf16[256,256]{1,0:T(8,128)(2,1)S(1)} %rest.4.refs_0_, bf16[256,256]{1,0:T(8,128)(2,1)S(1)} %collective-permute-done.21.refs_1_, bf16[256,256]{1,0:T(8,128)(2,1)S(1)} %collective-permute-done.22.refs_2_, ...), custom_call_target="tpu_custom_call" | custom-call | tf_op jit(solution)/shard_map/output/pallas_call | solution.py:538
  77.5 1.7 %output.4.refs_4_ = bf16[1024,256]{1,0:T(8,128)(2,1)} custom-call(bf16[1024,256]{1,0:T(8,128)(2,1)S(1)} %copy-done, bf16[384,256]{1,0:T(8,128)(2,1)S(1)} %rest.3.refs_0_, bf16[384,256]{1,0:T(8,128)(2,1)S(1)} %collective-permute-done.20.refs_1_, bf16[384,256]{1,0:T(8,128)(2,1)S(1)} %collective-permute-done.25.refs_2_, ...), custom_call_target="tpu_custom_call", output_to_operand_aliasing={{}: (5, {})} | custom-call | tf_op jit(solution)/shard_map/output/pallas_call | solution.py:538
  79.3 3.7 %collective-permute-done.24.refs_1_ = bf16[384,256]{1,0:T(8,128)(2,1)S(1)} collective-permute-done((bf16[384,256]{1,0:T(8,128)(2,1)S(1)}, bf16[384,256]{1,0:T(8,128)(2,1)S(1)}, u32[]{:S(2)}, u32[]{:S(2)}) %collective-permute-start.24) | collective-permute-done | bytes 196640 | tf_op jit(solution)/shard_map/ppermute | solution.py:52
  82.9 0.8 collective-permute-start.28
  83.8 1.1 %collective-permute-done.28.refs_3_ = bf16[384,256]{1,0:T(8,128)(2,1)S(1)} collective-permute-done((bf16[384,256]{1,0:T(8,128)(2,1)S(1)}, bf16[384,256]{1,0:T(8,128)(2,1)S(1)}, u32[]{:S(2)}, u32[]{:S(2)}) %collective-permute-start.28) | collective-permute-done | bytes 196640 | tf_op jit(solution)/shard_map/ppermute | solution.py:52
  84.8 1.7 %output.5 = bf16[1024,256]{1,0:T(8,128)(2,1)} custom-call(bf16[1024,256]{1,0:T(8,128)(2,1)S(1)} %copy-done, bf16[384,256]{1,0:T(8,128)(2,1)S(1)} %rest.5.refs_0_, bf16[384,256]{1,0:T(8,128)(2,1)S(1)} %collective-permute-done.24.refs_1_, bf16[384,256]{1,0:T(8,128)(2,1)S(1)} %collective-permute-done.27.refs_2_, ...), custom_call_target="tpu_custom_call", output_to_operand_aliasing={{}: (5, {})} | custom-call | tf_op jit(solution)/shard_map/output/pallas_call | solution.py:538
  (56 shorter events, 4.2 us)
Async XLA Ops:
  0.0 10.6 %collective-permute-start.7 = (s32[1,512]{1,0:T(1,128)}, s32[1,512]{1,0:T(1,128)S(1)}, u32[]{:S(2)}, u32[]{:S(2)}) collective-permute-start(s32[1,512]{1,0:T(1,128)} %mask_ref.1), channel_id=1, source_target_pairs={{0,4},{4,8},{8,12},{12,16},{16,20},{20,24},{24,28},{1,5},{5,9},{9,... | collective-permute-start | bytes 6152 | tf_op jit(solution)/shard_map/ppermute | solution.py:56
  4.7 17.7 %copy-start.7 = (s32[1,1024]{1,0:T(1,128)S(1)}, s32[1,1024]{1,0:T(1,128)}, u32[]{:S(2)}) copy-start(s32[1,1024]{1,0:T(1,128)} %order_ref.1) | copy-start | bytes 12292
  4.7 17.7 %copy-start.8 = (s32[1,512]{1,0:T(1,128)S(1)}, s32[1,512]{1,0:T(1,128)}, u32[]{:S(2)}) copy-start(s32[1,512]{1,0:T(1,128)} %mask_ref.1) | copy-start | bytes 6148
  4.9 6.0 %collective-permute-start = (bf16[128,256]{1,0:T(8,128)(2,1)S(1)}, bf16[128,256]{1,0:T(8,128)(2,1)S(1)}, u32[]{:S(2)}, u32[]{:S(2)}) collective-permute-start(bf16[128,256]{1,0:T(8,128)(2,1)S(1)} %get-tuple-element.60), channel_id=1, source_target_pairs={{0,28},{4,24},{8,20},{12,16},{16,12},{20,8},{24,4},{28,0},{1,29},{... | collective-permute-start | bytes 196616 | tf_op jit(solution)/shard_map/ppermute | solution.py:99
  5.8 5.0 %collective-permute-start.1 = (bf16[128,256]{1,0:T(8,128)(2,1)S(1)}, bf16[128,256]{1,0:T(8,128)(2,1)S(1)}, u32[]{:S(2)}, u32[]{:S(2)}) collective-permute-start(bf16[128,256]{1,0:T(8,128)(2,1)S(1)} %get-tuple-element.61), channel_id=1, source_target_pairs={{0,24},{4,28},{8,16},{12,20},{16,8},{20,12},{24,0},{28,4},{1,25},{... | collective-permute-start | bytes 196616 | tf_op jit(solution)/shard_map/ppermute | solution.py:99
  7.3 10.5 %collective-permute-start.4 = (bf16[128,512]{1,0:T(8,128)(2,1)S(1)}, bf16[128,512]{1,0:T(8,128)(2,1)S(1)}, u32[]{:S(2)}, u32[]{:S(2)}) collective-permute-start(bf16[128,512]{1,0:T(8,128)(2,1)S(1)} %get-tuple-element.64), channel_id=1, source_target_pairs={{0,12},{4,8},{8,4},{12,0},{16,28},{20,24},{24,20},{28,16},{1,13},{... | collective-permute-start | bytes 393224 | tf_op jit(solution)/shard_map/ppermute | solution.py:99
  7.5 10.7 %collective-permute-start.5 = (bf16[128,512]{1,0:T(8,128)(2,1)S(1)}, bf16[128,512]{1,0:T(8,128)(2,1)S(1)}, u32[]{:S(2)}, u32[]{:S(2)}) collective-permute-start(bf16[128,512]{1,0:T(8,128)(2,1)S(1)} %get-tuple-element.65), channel_id=1, source_target_pairs={{0,8},{4,12},{8,0},{12,4},{16,24},{20,28},{24,16},{28,20},{1,9},{5... | collective-permute-start | bytes 393224 | tf_op jit(solution)/shard_map/ppermute | solution.py:99
  10.6 7.6 %collective-permute-start.6 = (bf16[128,512]{1,0:T(8,128)(2,1)S(1)}, bf16[128,512]{1,0:T(8,128)(2,1)S(1)}, u32[]{:S(2)}, u32[]{:S(2)}) collective-permute-start(bf16[128,512]{1,0:T(8,128)(2,1)S(1)} %get-tuple-element.66), channel_id=1, source_target_pairs={{0,4},{4,0},{8,12},{12,8},{16,20},{20,16},{24,28},{28,24},{1,5},{5... | collective-permute-start | bytes 393224 | tf_op jit(solution)/shard_map/ppermute | solution.py:99
  10.9 5.5 %collective-permute-start.2 = (bf16[128,256]{1,0:T(8,128)(2,1)S(1)}, bf16[128,256]{1,0:T(8,128)(2,1)S(1)}, u32[]{:S(2)}, u32[]{:S(2)}) collective-permute-start(bf16[128,256]{1,0:T(8,128)(2,1)S(1)} %get-tuple-element.62), channel_id=1, source_target_pairs={{0,20},{4,16},{8,28},{12,24},{16,4},{20,0},{24,12},{28,8},{1,21},{... | collective-permute-start | bytes 196616 | tf_op jit(solution)/shard_map/ppermute | solution.py:99
  10.9 6.9 %collective-permute-start.3 = (bf16[128,256]{1,0:T(8,128)(2,1)S(1)}, bf16[128,256]{1,0:T(8,128)(2,1)S(1)}, u32[]{:S(2)}, u32[]{:S(2)}) collective-permute-start(bf16[128,256]{1,0:T(8,128)(2,1)S(1)} %get-tuple-element.63), channel_id=1, source_target_pairs={{0,16},{4,20},{8,24},{12,28},{16,0},{20,4},{24,8},{28,12},{1,17},{... | collective-permute-start | bytes 196616 | tf_op jit(solution)/shard_map/ppermute | solution.py:99
  18.3 7.7 %collective-permute-start.8 = (bf16[512,256]{1,0:T(8,128)(2,1)S(1)}, bf16[512,256]{1,0:T(8,128)(2,1)S(1)}, u32[]{:S(2)}, u32[]{:S(2)}) collective-permute-start(bf16[512,256]{1,0:T(8,128)(2,1)S(1)} %get-tuple-element.67.early_ref.refs_0_), channel_id=1, source_target_pairs={{0,2},{2,0},{1,3},{3,1},{4,6},{6,4},{5,7},{7,5},{8,10},{10,8},{9,1... | collective-permute-start | bytes 786440 | tf_op jit(solution)/shard_map/ppermute | solution.py:52
  18.6 9.6 %collective-permute-start.11 = (bf16[384,512]{1,0:T(8,128)(2,1)S(1)}, bf16[384,512]{1,0:T(8,128)(2,1)S(1)}, u32[]{:S(2)}, u32[]{:S(2)}) collective-permute-start(bf16[384,512]{1,0:T(8,128)(2,1)S(1)} %get-tuple-element.85.refs_4_), channel_id=1, source_target_pairs={{0,1},{1,0},{2,3},{3,2},{4,5},{5,4},{6,7},{7,6},{8,9},{9,8},{10,11... | collective-permute-start | bytes 1179656 | tf_op jit(solution)/shard_map/ppermute | solution.py:52
  22.4 5.8 %collective-permute-start.9 = (bf16[512,256]{1,0:T(8,128)(2,1)S(1)}, bf16[512,256]{1,0:T(8,128)(2,1)S(1)}, u32[]{:S(2)}, u32[]{:S(2)}) collective-permute-start(bf16[512,256]{1,0:T(8,128)(2,1)S(1)} %get-tuple-element.67.early_ref.refs_0_), channel_id=1, source_target_pairs={{0,1},{1,0},{2,3},{3,2},{4,5},{5,4},{6,7},{7,6},{8,9},{9,8},{10,11... | collective-permute-start | bytes 786440 | tf_op jit(solution)/shard_map/ppermute | solution.py:52
  26.0 3.4 %collective-permute-start.10 = (bf16[512,256]{1,0:T(8,128)(2,1)S(1)}, bf16[512,256]{1,0:T(8,128)(2,1)S(1)}, u32[]{:S(2)}, u32[]{:S(2)}) collective-permute-start(bf16[512,256]{1,0:T(8,128)(2,1)S(1)} %collective-permute-done.8.refs_1_), channel_id=1, source_target_pairs={{0,1},{1,0},{2,3},{3,2},{4,5},{5,4},{6,7},{7,6},{8,9},{9,8},{10,11... | collective-permute-start | bytes 786440 | tf_op jit(solution)/shard_map/ppermute | solution.py:52
  29.4 23.6 %copy-start.5 = (f32[4,4]{1,0:T(4,128)S(1)}, f32[4,4]{1,0:T(4,128)}, u32[]{:S(2)}) copy-start(f32[4,4]{1,0:T(4,128)} %mix_ref.7) | copy-start | bytes 196
  31.7 27.6 %collective-permute-start.12 = (bf16[1024,256]{1,0:T(8,128)(2,1)S(1)}, bf16[1024,256]{1,0:T(8,128)(2,1)S(1)}, u32[]{:S(2)}, u32[]{:S(2)}) collective-permute-start(bf16[1024,256]{1,0:T(8,128)(2,1)S(1)} %get-tuple-element.95), channel_id=1, source_target_pairs={{0,4},{4,8},{8,12},{12,16},{16,20},{20,24},{24,28},{1,5},{5,9},{9,... | collective-permute-start | bytes 1572872 | tf_op jit(solution)/shard_map/ppermute | solution.py:56
  35.5 14.9 %collective-permute-start.19 = (bf16[64,256]{1,0:T(8,128)(2,1)S(1)}, bf16[64,256]{1,0:T(8,128)(2,1)S(1)}, u32[]{:S(2)}, u32[]{:S(2)}) collective-permute-start(bf16[64,256]{1,0:T(8,128)(2,1)S(1)} %get-tuple-element.98.refs_0_), channel_id=1, source_target_pairs={{0,28},{4,24},{8,20},{12,16},{16,12},{20,8},{24,4},{28,0},{1,29},{... | collective-permute-start | bytes 98312 | tf_op jit(solution)/shard_map/ppermute | solution.py:99
  37.2 13.2 %collective-permute-start.18 = (bf16[64,256]{1,0:T(8,128)(2,1)S(1)}, bf16[64,256]{1,0:T(8,128)(2,1)S(1)}, u32[]{:S(2)}, u32[]{:S(2)}) collective-permute-start(bf16[64,256]{1,0:T(8,128)(2,1)S(1)} %get-tuple-element.98.refs_0_), channel_id=1, source_target_pairs={{0,24},{4,28},{8,16},{12,20},{16,8},{20,12},{24,0},{28,4},{1,25},{... | collective-permute-start | bytes 98312 | tf_op jit(solution)/shard_map/ppermute | solution.py:99
  37.9 12.4 %collective-permute-start.17 = (bf16[64,256]{1,0:T(8,128)(2,1)S(1)}, bf16[64,256]{1,0:T(8,128)(2,1)S(1)}, u32[]{:S(2)}, u32[]{:S(2)}) collective-permute-start(bf16[64,256]{1,0:T(8,128)(2,1)S(1)} %get-tuple-element.98.refs_0_), channel_id=1, source_target_pairs={{0,20},{4,16},{8,28},{12,24},{16,4},{20,0},{24,12},{28,8},{1,21},{... | collective-permute-start | bytes 98312 | tf_op jit(solution)/shard_map/ppermute | solution.py:99
  37.9 21.3 %collective-permute-start.16 = (bf16[64,256]{1,0:T(8,128)(2,1)S(1)}, bf16[64,256]{1,0:T(8,128)(2,1)S(1)}, u32[]{:S(2)}, u32[]{:S(2)}) collective-permute-start(bf16[64,256]{1,0:T(8,128)(2,1)S(1)} %get-tuple-element.98.refs_0_), channel_id=1, source_target_pairs={{0,16},{4,20},{8,24},{12,28},{16,0},{20,4},{24,8},{28,12},{1,17},{... | collective-permute-start | bytes 98312 | tf_op jit(solution)/shard_map/ppermute | solution.py:99
  50.3 8.9 %collective-permute-start.15 = (bf16[64,256]{1,0:T(8,128)(2,1)S(1)}, bf16[64,256]{1,0:T(8,128)(2,1)S(1)}, u32[]{:S(2)}, u32[]{:S(2)}) collective-permute-start(bf16[64,256]{1,0:T(8,128)(2,1)S(1)} %get-tuple-element.98.refs_0_), channel_id=1, source_target_pairs={{0,12},{4,8},{8,4},{12,0},{16,28},{20,24},{24,20},{28,16},{1,13},{... | collective-permute-start | bytes 98312 | tf_op jit(solution)/shard_map/ppermute | solution.py:99
  50.3 8.9 %collective-permute-start.14 = (bf16[64,256]{1,0:T(8,128)(2,1)S(1)}, bf16[64,256]{1,0:T(8,128)(2,1)S(1)}, u32[]{:S(2)}, u32[]{:S(2)}) collective-permute-start(bf16[64,256]{1,0:T(8,128)(2,1)S(1)} %get-tuple-element.98.refs_0_), channel_id=1, source_target_pairs={{0,8},{4,12},{8,0},{12,4},{16,24},{20,28},{24,16},{28,20},{1,9},{5... | collective-permute-start | bytes 98312 | tf_op jit(solution)/shard_map/ppermute | solution.py:99
  50.4 8.9 %collective-permute-start.13 = (bf16[64,256]{1,0:T(8,128)(2,1)S(1)}, bf16[64,256]{1,0:T(8,128)(2,1)S(1)}, u32[]{:S(2)}, u32[]{:S(2)}) collective-permute-start(bf16[64,256]{1,0:T(8,128)(2,1)S(1)} %get-tuple-element.98.refs_0_), channel_id=1, source_target_pairs={{0,4},{4,0},{8,12},{12,8},{16,20},{20,16},{24,28},{28,24},{1,5},{5... | collective-permute-start | bytes 98312 | tf_op jit(solution)/shard_map/ppermute | solution.py:99
  62.3 8.2 %collective-permute-start.21 = (bf16[256,256]{1,0:T(8,128)(2,1)S(1)}, bf16[256,256]{1,0:T(8,128)(2,1)S(1)}, u32[]{:S(2)}, u32[]{:S(2)}) collective-permute-start(bf16[256,256]{1,0:T(8,128)(2,1)S(1)} %rest.4.refs_0_), channel_id=1, source_target_pairs={{0,2},{2,0},{1,3},{3,1},{4,6},{6,4},{5,7},{7,5},{8,10},{10,8},{9,1... | collective-permute-start | bytes 393224 | tf_op jit(solution)/shard_map/ppermute | solution.py:52
  65.4 10.5 %collective-permute-start.20 = (bf16[384,256]{1,0:T(8,128)(2,1)S(1)}, bf16[384,256]{1,0:T(8,128)(2,1)S(1)}, u32[]{:S(2)}, u32[]{:S(2)}) collective-permute-start(bf16[384,256]{1,0:T(8,128)(2,1)S(1)} %rest.3.refs_0_), channel_id=1, source_target_pairs={{0,2},{2,0},{1,3},{3,1},{4,6},{6,4},{5,7},{7,5},{8,10},{10,8},{9,1... | collective-permute-start | bytes 589832 | tf_op jit(solution)/shard_map/ppermute | solution.py:52
  66.7 8.1 %collective-permute-start.22 = (bf16[256,256]{1,0:T(8,128)(2,1)S(1)}, bf16[256,256]{1,0:T(8,128)(2,1)S(1)}, u32[]{:S(2)}, u32[]{:S(2)}) collective-permute-start(bf16[256,256]{1,0:T(8,128)(2,1)S(1)} %rest.4.refs_0_), channel_id=1, source_target_pairs={{0,1},{1,0},{2,3},{3,2},{4,5},{5,4},{6,7},{7,6},{8,9},{9,8},{10,11... | collective-permute-start | bytes 393224 | tf_op jit(solution)/shard_map/ppermute | solution.py:52
  70.5 4.3 %collective-permute-start.23 = (bf16[256,256]{1,0:T(8,128)(2,1)S(1)}, bf16[256,256]{1,0:T(8,128)(2,1)S(1)}, u32[]{:S(2)}, u32[]{:S(2)}) collective-permute-start(bf16[256,256]{1,0:T(8,128)(2,1)S(1)} %collective-permute-done.21.refs_1_), channel_id=1, source_target_pairs={{0,1},{1,0},{2,3},{3,2},{4,5},{5,4},{6,7},{7,6},{8,9},{9,8},{10,11... | collective-permute-start | bytes 393224 | tf_op jit(solution)/shard_map/ppermute | solution.py:52
  74.7 2.1 %collective-permute-start.25 = (bf16[384,256]{1,0:T(8,128)(2,1)S(1)}, bf16[384,256]{1,0:T(8,128)(2,1)S(1)}, u32[]{:S(2)}, u32[]{:S(2)}) collective-permute-start(bf16[384,256]{1,0:T(8,128)(2,1)S(1)} %rest.3.refs_0_), channel_id=1, source_target_pairs={{0,1},{1,0},{2,3},{3,2},{4,5},{5,4},{6,7},{7,6},{8,9},{9,8},{10,11... | collective-permute-start | bytes 589832 | tf_op jit(solution)/shard_map/ppermute | solution.py:52
  76.0 1.6 %collective-permute-start.26 = (bf16[384,256]{1,0:T(8,128)(2,1)S(1)}, bf16[384,256]{1,0:T(8,128)(2,1)S(1)}, u32[]{:S(2)}, u32[]{:S(2)}) collective-permute-start(bf16[384,256]{1,0:T(8,128)(2,1)S(1)} %collective-permute-done.20.refs_1_), channel_id=1, source_target_pairs={{0,1},{1,0},{2,3},{3,2},{4,5},{5,4},{6,7},{7,6},{8,9},{9,8},{10,11... | collective-permute-start | bytes 589832 | tf_op jit(solution)/shard_map/ppermute | solution.py:52
  76.4 6.5 %collective-permute-start.24 = (bf16[384,256]{1,0:T(8,128)(2,1)S(1)}, bf16[384,256]{1,0:T(8,128)(2,1)S(1)}, u32[]{:S(2)}, u32[]{:S(2)}) collective-permute-start(bf16[384,256]{1,0:T(8,128)(2,1)S(1)} %rest.5.refs_0_), channel_id=1, source_target_pairs={{0,2},{2,0},{1,3},{3,1},{4,6},{6,4},{5,7},{7,5},{8,10},{10,8},{9,1... | collective-permute-start | bytes 589832 | tf_op jit(solution)/shard_map/ppermute | solution.py:52
  76.5 7.3 %collective-permute-start.27 = (bf16[384,256]{1,0:T(8,128)(2,1)S(1)}, bf16[384,256]{1,0:T(8,128)(2,1)S(1)}, u32[]{:S(2)}, u32[]{:S(2)}) collective-permute-start(bf16[384,256]{1,0:T(8,128)(2,1)S(1)} %rest.5.refs_0_), channel_id=1, source_target_pairs={{0,1},{1,0},{2,3},{3,2},{4,5},{5,4},{6,7},{7,6},{8,9},{9,8},{10,11... | collective-permute-start | bytes 589832 | tf_op jit(solution)/shard_map/ppermute | solution.py:52
  82.9 1.9 %collective-permute-start.28 = (bf16[384,256]{1,0:T(8,128)(2,1)S(1)}, bf16[384,256]{1,0:T(8,128)(2,1)S(1)}, u32[]{:S(2)}, u32[]{:S(2)}) collective-permute-start(bf16[384,256]{1,0:T(8,128)(2,1)S(1)} %collective-permute-done.24.refs_1_), channel_id=1, source_target_pairs={{0,1},{1,0},{2,3},{3,2},{4,5},{5,4},{6,7},{7,6},{8,9},{9,8},{10,11... | collective-permute-start | bytes 589832 | tf_op jit(solution)/shard_map/ppermute | solution.py:52
  (6 other events, 65.0 us)

commit v6 on v5

--- a/solution.py
+++ b/solution.py
@@ -13,6 +13,7 @@
 POOL2 = 64
 POOL3 = 512
 SUMM_ROWS = 32
+CODE_ROWS = 16
 BF = jnp.bfloat16
 F32 = jnp.float32
 I32 = jnp.int32
@@ -56,50 +57,51 @@
     return lax.ppermute(block, "seq", [(i, i + 1) for i in range(lax.axis_size("seq") - 1)])
 
 
-def send_kernel(distances, tokens_ref, *refs):
+def send_kernel(distances, tokens_ref, mask_ref, *refs):
     outs, own = refs[:-1], refs[-1]
     slab, head = lax.axis_index("seq"), lax.axis_index("head")
     rows = own.shape[0]
     quarter = tokens_ref.shape[1] // 4
+    ids = mask_ref[...]
+    line = iota((CODE_ROWS, ids.shape[1]), 0)
+    code = jnp.where(line == 0, ids >> 5, jnp.where(line == 1, ids & 31, 0)).astype(F32).astype(BF)
     for distance, out in zip(distances, outs):
         row = pl.multiple_of((slab ^ distance) * rows, rows)
-        for part in range(out.shape[1] // quarter):
+        parts = out.shape[1] // quarter
+        for part in range(parts):
             start = pl.multiple_of((head ^ (2 * part)) * quarter, quarter)
-            out[:, part * quarter : (part + 1) * quarter] = tokens_ref[
+            out[:rows, part * quarter : (part + 1) * quarter] = tokens_ref[
                 pl.ds(row, rows), pl.ds(start, quarter)
             ]
+        for part in range(code.shape[1] // out.shape[1]):
+            at = rows + part * CODE_ROWS
+            out[at : at + CODE_ROWS] = code[:, part * out.shape[1] : (part + 1) * out.shape[1]]
     own[...] = tokens_ref[pl.ds(pl.multiple_of(slab * rows, rows), rows)]
 
 
-def stack_kernel(counts, *refs):
-    sources, targets = refs[: sum(counts)], refs[len(refs) - len(counts) :]
-    for count, target in zip(counts, targets):
-        height = target.shape[0] // count
-        for index in range(count):
-            target[index * height : (index + 1) * height] = sources[index][...]
-        sources = sources[count:]
-
-
-def stacked(lists, after):
-    parts = [part for one in lists for part in one]
+def stack_kernel(count, *refs):
+    target = refs[-1]
+    height = target.shape[0] // count
+    for index in range(count):
+        target[index * height : (index + 1) * height] = refs[index][:height]
+
+
+def stacked(parts, rows, after=()):
     return pl.pallas_call(
-        functools.partial(stack_kernel, tuple(len(one) for one in lists)),
-        out_shape=tuple(
-            jax.ShapeDtypeStruct((len(one) * one[0].shape[0], one[0].shape[1]), one[0].dtype)
-            for one in lists
-        ),
-        in_specs=vmem_specs(len(parts)) + [pl.BlockSpec(memory_space=pl.ANY)],
-        out_specs=vmem_specs(len(lists)),
+        functools.partial(stack_kernel, len(parts)),
+        out_shape=jax.ShapeDtypeStruct((len(parts) * rows, parts[0].shape[1]), parts[0].dtype),
+        in_specs=vmem_specs(len(parts)) + [pl.BlockSpec(memory_space=pl.ANY)] * len(after),
+        out_specs=pl.BlockSpec(memory_space=pltpu.VMEM),
         compiler_params=pltpu.CompilerParams(vmem_limit_bytes=VMEM_LIMIT),
         name="stack",
-    )(*parts, after)
+    )(*parts, *after)
 
 
 def by_distance(block, distance):
     return lax.ppermute(block, "seq", [(i, i ^ distance) for i in range(lax.axis_size("seq"))])
 
 
-def exchange_tokens(tokens, before_mask, prepare):
+def exchange_tokens(tokens, mask_ids, prepare):
     tok_rows, width = tokens.shape
     slabs = lax.axis_size("seq")
     rows = tok_rows // slabs
@@ -114,21 +116,24 @@
         second = over_head(first, CORE_PAIRS)
         fourth = over_head(third, CORE_PAIRS)
         pieces = [(first, 0, (0,)), (third, 0, (2,)), (second, 0, (1,)), (fourth, 0, (3,))]
-        return pieces, prepare(first)
+        return pieces, prepare(first), [to_next(mask_ids)]
     distances = (7, 6, 5, 4, 3, 2, 1)
+    near_rows, far_rows = rows + CODE_ROWS, rows + 2 * CODE_ROWS
     *blocks, own = pl.pallas_call(
         functools.partial(send_kernel, distances),
         out_shape=tuple(
-            jax.ShapeDtypeStruct((rows, columns), BF)
-            for columns in [quarter if d > 3 else 2 * quarter for d in distances] + [width]
-        ),
-        in_specs=vmem_specs(1),
+            jax.ShapeDtypeStruct((far_rows, quarter) if d > 3 else (near_rows, 2 * quarter), BF)
+            for d in distances
+        )
+        + (jax.ShapeDtypeStruct((rows, width), BF),),
+        in_specs=vmem_specs(2),
         out_specs=vmem_specs(8),
         compiler_params=pltpu.CompilerParams(vmem_limit_bytes=VMEM_LIMIT),
         name="send",
-    )(tokens)
+    )(tokens, mask_ids)
     arrived = [by_distance(block, d) for block, d in zip(blocks, distances)]
-    far, near = stacked((arrived[:4], arrived[4:]), before_mask)
+    far = stacked(arrived[:4], rows, (arrived[5],))
+    near = stacked(arrived[4:], rows)
     far_x = over_head(far, X_PAIRS)
     near_core = over_head(near, CORE_PAIRS)
     far_core = over_head(far, CORE_PAIRS)
@@ -137,7 +142,7 @@
     far_last = over_head(far_x, CORE_PAIRS)
     pieces = [(far, 0, (0,)), (far_x, 0, (2,)), (far_core, 0, (1,)), (far_last, 0, (3,))]
     pieces += [(near, 4 * rows, (0, 2)), (near_core, 4 * rows, (1, 3)), (own, 7 * rows, None)]
-    return pieces, prepared
+    return pieces, prepared, [arrived[6], arrived[4], arrived[0]]
 
 
 def column(row, lanes=128):
@@ -156,8 +161,8 @@
 
 
 def prepare_kernel(
-    order_ref, mask_ref, before_ref, wq_ref, wv_ref, wk_in, early_ref,
-    p_ref, pt_ref, sel_ref, fcol_ref, frow_ref, e_ref, et_ref, bias_ref, wt_ref, wk_ref,
+    order_ref, mask_ref, wq_ref, wv_ref, wk_in, early_ref,
+    p_ref, pt_ref, sel_ref, fcol_ref, frow_ref, bias_ref, wt_ref, wk_ref,
 ):
     slab, slabs = lax.axis_index("seq"), lax.axis_size("seq")
     tok_rows = order_ref.shape[1]
@@ -199,13 +204,7 @@
     pools = sel_ref[packed:]
     fcol_ref[...] = 1.0 / jnp.sqrt(jnp.maximum(nn(pools, jnp.ones((tok_rows, lanes), BF)), 1.0))
     frow_ref[...] = 1.0 / jnp.sqrt(jnp.maximum(nt(jnp.ones((16, tok_rows), BF), pools), 1.0))
-    rank_before = jnp.where(slab > 0, ranks(before_ref[...], tok_rows), -1)
-    rank_column = column(rank_before)
-    for at in range(0, packed, lanes):
-        e_ref[:, at : at + lanes] = ones_where(rank_column == iota((tok_rows, lanes), 1) + at)
-        et_ref[at : at + lanes] = ones_where(iota((lanes, tok_rows), 0) + at == rank_before)
-    bias_ref[:tok_rows] = jnp.where(rank_column >= 0, 0.0, HIDE)
-    bias_ref[tok_rows:] = jnp.where(column(rank) >= 0, 0.0, HIDE)
+    bias_ref[...] = jnp.where(column(rank) >= 0, 0.0, HIDE)
     wt_ref[:group] = jnp.transpose(wq_ref[...])
     wt_ref[group:] = jnp.transpose(wv_ref[...])
     wk_ref[...] = wk_in[...]
@@ -261,30 +260,65 @@
         q4_ref[rows, h * FBLK : (h + 1) * FBLK] = qt_ref[rows, at : at + FBLK]
 
 
+def order_kernel(
+    p_ref, pt_ref, sel_ref, fcol_ref, frow_ref, wt_ref, x_ref, k0_ref, v0_ref,
+    qt_ref, vt_ref, k_ref, nk_ref, nvt_ref,
+):
+    group = k_ref.shape[1]
+    near = nk_ref.shape[0]
+    k0, v0 = k0_ref[...], v0_ref[...]
+    q0 = nt(wt_ref[:group], x_ref[...]).astype(BF)
+    k_ref[...] = nn(p_ref[...], k0).astype(BF)
+    qt_ref[...] = (nn(q0, pt_ref[...]) * 0.125).astype(BF)
+    vt_ref[...] = nn(v0, pt_ref[...]).astype(BF)
+    pool = sel_ref[sel_ref.shape[0] - near :]
+    nk_ref[...] = (nn(pool, k0) * fcol_ref[SUMM_ROWS:, :1]).astype(BF)
+    nvt_ref[...] = (nt(v0, pool) * frow_ref[:1, SUMM_ROWS:]).astype(BF)
+
+
+def mask_before(refs, rows):
+    if len(refs) == 1:
+        return refs[0][...]
+    slab = lax.axis_index("seq")
+    digits = []
+    for block in refs:
+        width = block.shape[1]
+        parts = [
+            block[rows + at : rows + at + CODE_ROWS].astype(F32)
+            for at in range(0, block.shape[0] - rows, CODE_ROWS)
+        ]
+        digits.append(jnp.concatenate(parts, axis=1) if len(parts) > 1 else parts[0])
+    distance = slab ^ (slab - 1)
+    code = jnp.where(distance == 1, digits[0], jnp.where(distance == 3, digits[1], digits[2]))
+    code = code.astype(I32)
+    return (code[0:1] << 5) + code[1:2]
+
+
 def own_kernel(
-    mix_ref, p_in, pt_ref, sel_ref, fcol_ref, frow_ref, wt_ref, x_ref, k0_ref, v0_ref, bias_ref,
-    qt_ref, vt_ref, k_ref, acc_ref, near_ref, top_ref, den_ref, q4_ref, p_ref,
+    rows, codes, mix_ref, qt_ref, k_ref, vt_ref, nk_ref, nvt_ref, seen_ref, *refs,
 ):
+    code_refs = refs[:codes]
+    acc_ref, near_ref, top_ref, den_ref, e_ref, et_ref, bias_ref, q4_ref, p_ref = refs[codes:]
     tok_rows, group = k_ref.shape
     heads = mix_ref.shape[1]
     width = group // heads
-    near = tok_rows // POOL1
     q4_ref[...] = jnp.zeros_like(q4_ref)
     same = iota((FBLK, FBLK), 0) == iota((FBLK, FBLK), 1)
-    k0, v0 = k0_ref[...], v0_ref[...]
-    q0 = nt(wt_ref[:group], x_ref[...]).astype(BF)
-    k_ref[...] = nn(p_in[...], k0).astype(BF)
-    qt_ref[...] = (nn(q0, pt_ref[...]) * 0.125).astype(BF)
-    vt_ref[...] = nn(v0, pt_ref[...]).astype(BF)
-    pool = sel_ref[sel_ref.shape[0] - near :]
-    nk = (nn(pool, k0) * fcol_ref[SUMM_ROWS:, :1]).astype(BF)
-    nvt = (nt(v0, pool) * frow_ref[:1, SUMM_ROWS:]).astype(BF)
+    nk, nvt = nk_ref[...], nvt_ref[...]
+    rank = ranks(mask_before(code_refs, rows), tok_rows)
+    rank = jnp.where(lax.axis_index("seq") > 0, rank, -1)
+    rank_column = column(rank)
+    bias_ref[:tok_rows] = jnp.where(rank_column >= 0, 0.0, HIDE)
+    bias_ref[tok_rows:] = seen_ref[...]
+    for at in range(0, et_ref.shape[0], FBLK):
+        e_ref[:, at : at + FBLK] = ones_where(rank_column == iota((tok_rows, FBLK), 1) + at)
+        et_ref[at : at + FBLK] = ones_where(iota((FBLK, tok_rows), 0) + at == rank)
     for g in range(tok_rows // FBLK):
         at = g * FBLK
         slot = g % 2
         spread_heads(q4_ref.at[slot], qt_ref, at, heads)
         q4 = q4_ref[slot]
-        bias = jnp.where(same, 0.0, bias_ref[tok_rows + at : tok_rows + at + FBLK])
+        bias = jnp.where(same, 0.0, seen_ref[at : at + FBLK])
         own_scores = nn(k_ref[at : at + FBLK], q4)
         near_scores = nn(nk, q4)
         scales = []
@@ -440,7 +474,6 @@
 
     shape = jax.ShapeDtypeStruct
     params = pltpu.CompilerParams(vmem_limit_bytes=VMEM_LIMIT)
-    before_mask = to_next(mask_ids)
 
     def prepare(early):
         return pl.pallas_call(
@@ -451,20 +484,18 @@
                 shape((chosen, tok_rows), BF),
                 shape((SUMM_ROWS + near, 128), F32),
                 shape((16, SUMM_ROWS + near), F32),
-                shape((tok_rows, packed), BF),
-                shape((packed, tok_rows), BF),
-                shape((2 * tok_rows, FBLK), F32),
+                shape((tok_rows, FBLK), F32),
                 shape((2 * group, width), BF),
                 shape((width, group), BF),
             ),
-            in_specs=vmem_specs(6) + [pl.BlockSpec(memory_space=pl.ANY)],
-            out_specs=vmem_specs(10),
+            in_specs=vmem_specs(5) + [pl.BlockSpec(memory_space=pl.ANY)],
+            out_specs=vmem_specs(8),
             compiler_params=params,
             name="prepare",
-        )(order, mask_ids, before_mask, w_query, w_value, w_key, early)
-
-    pieces, prepared = exchange_tokens(tokens, before_mask, prepare)
-    permute, permute_t, select, f_col, f_row, expand, expand_t, bias, w_t, w_k = prepared
+        )(order, mask_ids, w_query, w_value, w_key, early)
+
+    pieces, prepared, before = exchange_tokens(tokens, mask_ids, prepare)
+    permute, permute_t, select, f_col, f_row, seen, w_t, w_k = prepared
     places = tuple((row, distances) for _, row, distances in pieces)
     comp, summ, k0, v0, rows_here = pl.pallas_call(
         functools.partial(project_kernel, places),
@@ -480,27 +511,45 @@
         compiler_params=params,
         name="project",
     )(*[piece for piece, _, _ in pieces], w_t, w_k, select, f_col)
+    if slabs == 8:
+        other = by_distance(summ, 1)
     comp_before = to_next(comp)
+
+    q_t, v_t, keys, near_k, near_vt = pl.pallas_call(
+        order_kernel,
+        out_shape=(
+            shape((group, tok_rows), BF),
+            shape((group, tok_rows), BF),
+            shape((tok_rows, group), BF),
+            shape((near, group), BF),
+            shape((group, near), BF),
+        ),
+        in_specs=vmem_specs(9),
+        out_specs=vmem_specs(5),
+        compiler_params=params,
+        name="order",
+    )(permute, permute_t, select, f_col, f_row, w_t, rows_here, k0, v0)
     if slabs == 8:
-        summaries = [summ] + [by_distance(summ, d) for d in range(1, slabs)]
+        pair = stacked((summ, other), step, (near_k,))
+        summaries = [pair] + [by_distance(pair, d) for d in (2, 4, 6)]
     else:
         copies = jnp.broadcast_to(summ[None], (slabs, step, group))
         copies = lax.all_to_all(copies, "seq", split_axis=0, concat_axis=0, tiled=True)
         summaries = [copies.reshape(slabs * step, group)]
 
     blocks = tok_rows // FBLK
-    q_t, v_t, keys, acc, near_out, top, den = pl.pallas_call(
-        own_kernel,
+    acc, near_out, top, den, expand, expand_t, bias = pl.pallas_call(
+        functools.partial(own_kernel, tok_rows // slabs, len(before)),
         out_shape=(
-            shape((group, tok_rows), BF),
-            shape((group, tok_rows), BF),
-            shape((tok_rows, group), BF),
             shape((group, tok_rows), F32),
             shape((group, tok_rows), F32),
             shape((blocks, heads * FBLK), F32),
             shape((blocks, heads * FBLK), F32),
+            shape((tok_rows, packed), BF),
+            shape((packed, tok_rows), BF),
+            shape((2 * tok_rows, FBLK), F32),
         ),
-        in_specs=smem_specs(1) + vmem_specs(10),
+        in_specs=smem_specs(1) + vmem_specs(6 + len(before)),
         out_specs=vmem_specs(7),
         scratch_shapes=[
             pltpu.VMEM((2, group, heads * FBLK), BF),
@@ -508,7 +557,7 @@
         ],
         compiler_params=params,
         name="own",
-    )(level_mix, permute, permute_t, select, f_col, f_row, w_t, rows_here, k0, v0, bias)
+    )(level_mix, q_t, keys, v_t, near_k, near_vt, seen, *before)
 
     window_k, window_v, coarse_k, coarse_v = pl.pallas_call(
         window_kernel,
@@ -571,7 +620,6 @@
             old, old_third, old_second, old_base = waiting
             old_third, attended = lax.optimization_barrier((old_third, attended))
             out = finish(out, old, old_third, old_second, old_base)
-            third, out = lax.optimization_barrier((third, out))
         waiting = (attended, third, second, first)
         first += count
     return finish(out, *waiting)

time: 86.8 us -> 83.4 us (0.961)
  the two profiles are of different devices: /device:TPU:27 before, /device:TPU:0 now
where the time goes in v6:
time: 83.4 us; the launch traced here: 83.2 us
  starting transfers between devices  31.4 us (38%)
  Pallas kernels  25.7 us (31%)
  waiting for transfers between devices  23.6 us (28%)
  local copies, waits for them, and re-layouts  2.31 us (3%)
    ppermute x11, starting transfers between devices, by_distance(): lax.ppermute(block, 'seq', [(i, i ^ distance) for i in range(lax.axis_siz...  20.9 us
    ppermute x11, waiting for transfers between devices, by_distance(): lax.ppermute(block, 'seq', [(i, i ^ distance) for i in range(lax.axis_siz...  14.6 us
    ppermute x13, waiting for transfers between devices, over_head(): return lax.ppermute(block, 'head', pairs)  8.95 us
    pallas_call x3, Pallas kernels, local(): pl.pallas_call(functools.partial(rest_kernel, first, count), out_shape=sh...  7.6 us
    ppermute x13, starting transfers between devices, over_head(): return lax.ppermute(block, 'head', pairs)  6.92 us
    pallas_call x1, Pallas kernels, local(): pl.pallas_call(functools.partial(own_kernel, tok_rows // slabs, len(befor...  4.9 us
    pallas_call x3, Pallas kernels, finish(): pl.pallas_call(output_kernel, grid=(rows // FBLK,), out_shape=shape((tok_...  4.68 us
    ppermute x1, starting transfers between devices, to_next(): lax.ppermute(block, 'seq', [(i, i + 1) for i in range(lax.axis_size('seq'...  3.62 us
  transfers between devices with their start and end apart: 25, of which 10 were waited for; matrix products, arithmetic and copies ran while one was open for 0% of the time, Pallas kernels for 22%

profile of v6, /device:TPU:0, one launch (start us, length us, event | category | flops | bytes accessed | tf_op | source)
XLA Modules:
  0.0 83.2 jit_solution(18205420287916860903)
XLA Ops:
  0.0 1.6 %copy-done.1 = bf16[1024,1024]{1,0:T(8,128)(2,1)S(1)} copy-done((bf16[1024,1024]{1,0:T(8,128)(2,1)S(1)}, bf16[1024,1024]{1,0:T(8,128)(2,1)}, u32[]{:S(2)}) %copy-start.1) | copy-done | bytes 2097176
  1.6 0.7 copy-done.7
  2.4 3.1 %collective-permute-start.4 = (bf16[144,512]{1,0:T(8,128)(2,1)S(1)}, bf16[144,512]{1,0:T(8,128)(2,1)S(1)}, u32[]{:S(2)}, u32[]{:S(2)}) collective-permute-start(bf16[144,512]{1,0:T(8,128)(2,1)S(1)} %get-tuple-element.59), channel_id=1, source_target_pairs={{0,8},{4,12},{8,0},{12,4},{16,24},{20,28},{24,16},{28,20},{1,9},{5... | collective-permute-start | bytes 442376 | tf_op jit(solution)/shard_map/ppermute | solution.py:101
  5.5 3.4 %collective-permute-start = (bf16[160,256]{1,0:T(8,128)(2,1)S(1)}, bf16[160,256]{1,0:T(8,128)(2,1)S(1)}, u32[]{:S(2)}, u32[]{:S(2)}) collective-permute-start(bf16[160,256]{1,0:T(8,128)(2,1)S(1)} %get-tuple-element.55), channel_id=1, source_target_pairs={{0,28},{4,24},{8,20},{12,16},{16,12},{20,8},{24,4},{28,0},{1,29},{... | collective-permute-start | bytes 245768 | tf_op jit(solution)/shard_map/ppermute | solution.py:101
  8.9 1.3 %collective-permute-start.1 = (bf16[160,256]{1,0:T(8,128)(2,1)S(1)}, bf16[160,256]{1,0:T(8,128)(2,1)S(1)}, u32[]{:S(2)}, u32[]{:S(2)}) collective-permute-start(bf16[160,256]{1,0:T(8,128)(2,1)S(1)} %get-tuple-element.56), channel_id=1, source_target_pairs={{0,24},{4,28},{8,16},{12,20},{16,8},{20,12},{24,0},{28,4},{1,25},{... | collective-permute-start | bytes 245768 | tf_op jit(solution)/shard_map/ppermute | solution.py:101
  10.3 0.7 collective-permute-start.2
  11.0 2.1 %collective-permute-start.3 = (bf16[160,256]{1,0:T(8,128)(2,1)S(1)}, bf16[160,256]{1,0:T(8,128)(2,1)S(1)}, u32[]{:S(2)}, u32[]{:S(2)}) collective-permute-start(bf16[160,256]{1,0:T(8,128)(2,1)S(1)} %get-tuple-element.58), channel_id=1, source_target_pairs={{0,16},{4,20},{8,24},{12,28},{16,0},{20,4},{24,8},{28,12},{1,17},{... | collective-permute-start | bytes 245768 | tf_op jit(solution)/shard_map/ppermute | solution.py:101
  13.2 2.4 %collective-permute-done.refs_0_.refs_2_ = bf16[160,256]{1,0:T(8,128)(2,1)S(1)} collective-permute-done((bf16[160,256]{1,0:T(8,128)(2,1)S(1)}, bf16[160,256]{1,0:T(8,128)(2,1)S(1)}, u32[]{:S(2)}, u32[]{:S(2)}) %collective-permute-start) | collective-permute-done | bytes 81952 | tf_op jit(solution)/shard_map/ppermute | solution.py:101
  15.5 3.2 %collective-permute-start.8 = (bf16[144,512]{1,0:T(8,128)(2,1)S(1)}, bf16[144,512]{1,0:T(8,128)(2,1)S(1)}, u32[]{:S(2)}, u32[]{:S(2)}) collective-permute-start(bf16[144,512]{1,0:T(8,128)(2,1)S(1)} %get-tuple-element.75), channel_id=1, source_target_pairs={{0,12},{4,8},{8,4},{12,0},{16,28},{20,24},{24,20},{28,16},{1,13},{... | collective-permute-start | bytes 442376 | tf_op jit(solution)/shard_map/ppermute | solution.py:101
  18.7 1.7 %collective-permute-start.9 = (bf16[144,512]{1,0:T(8,128)(2,1)S(1)}, bf16[144,512]{1,0:T(8,128)(2,1)S(1)}, u32[]{:S(2)}, u32[]{:S(2)}) collective-permute-start(bf16[144,512]{1,0:T(8,128)(2,1)S(1)} %get-tuple-element.76), channel_id=1, source_target_pairs={{0,4},{4,0},{8,12},{12,8},{16,20},{20,16},{24,28},{28,24},{1,5},{5... | collective-permute-start | bytes 442376 | tf_op jit(solution)/shard_map/ppermute | solution.py:101
  20.4 2.3 %collective-permute-done.2.refs_2_ = bf16[160,256]{1,0:T(8,128)(2,1)S(1)} collective-permute-done((bf16[160,256]{1,0:T(8,128)(2,1)S(1)}, bf16[160,256]{1,0:T(8,128)(2,1)S(1)}, u32[]{:S(2)}, u32[]{:S(2)}) %collective-permute-start.2) | collective-permute-done | bytes 81952 | tf_op jit(solution)/shard_map/ppermute | solution.py:101
  23.2 1.6 %collective-permute-start.5 = (bf16[512,256]{1,0:T(8,128)(2,1)S(1)}, bf16[512,256]{1,0:T(8,128)(2,1)S(1)}, u32[]{:S(2)}, u32[]{:S(2)}) collective-permute-start(bf16[512,256]{1,0:T(8,128)(2,1)S(1)} %stack.3.early_ref.refs_0_), channel_id=1, source_target_pairs={{0,2},{2,0},{1,3},{3,1},{4,6},{6,4},{5,7},{7,5},{8,10},{10,8},{9,1... | collective-permute-start | bytes 786440 | tf_op jit(solution)/shard_map/ppermute | solution.py:53
  25.7 2.5 %prepare.1 = (bf16[1024,1024]{1,0:T(8,128)(2,1)S(1)}, bf16[1024,1024]{1,0:T(8,128)(2,1)S(1)}, bf16[672,1024]{1,0:T(8,128)(2,1)S(1)}, f32[160,128]{1,0:T(8,128)S(...) custom-call(s32[1,1024]{1,0:T(1,128)S(1)} %copy-done.9, ...), custom_call_target="tpu_custom_call" | custom-call | tf_op jit(solution)/shard_map/prepare/pallas_call | solution.py:479
  28.3 2.4 %collective-permute-done.5.refs_1_ = bf16[512,256]{1,0:T(8,128)(2,1)S(1)} collective-permute-done((bf16[512,256]{1,0:T(8,128)(2,1)S(1)}, bf16[512,256]{1,0:T(8,128)(2,1)S(1)}, u32[]{:S(2)}, u32[]{:S(2)}) %collective-permute-start.5) | collective-permute-done | bytes 262176 | tf_op jit(solution)/shard_map/ppermute | solution.py:53
  30.7 1.5 %collective-permute-done.7.refs_3_ = bf16[512,256]{1,0:T(8,128)(2,1)S(1)} collective-permute-done((bf16[512,256]{1,0:T(8,128)(2,1)S(1)}, bf16[512,256]{1,0:T(8,128)(2,1)S(1)}, u32[]{:S(2)}, u32[]{:S(2)}) %collective-permute-start.7) | collective-permute-done | bytes 262176 | tf_op jit(solution)/shard_map/ppermute | solution.py:53
  32.2 2.3 %project.1 = (bf16[1024,256]{1,0:T(8,128)(2,1)S(1)}, bf16[64,256]{1,0:T(8,128)(2,1)S(1)}, bf16[1024,256]{1,0:T(8,128)(2,1)S(1)}, bf16[256,1024]{1,0:T(8,128)(2,1)S(1)}, bf16[1024,1024]{1,0:T(8,128)(2,1)S(1)}) custom-call(bf16[512,256]{1,0:T(8,128)(2,1)S(1)} %stack.3.early_ref.refs_0_, bf16[512,256]{1,0:T(8,128)(2,1)S(1)} %collective-permute-done.5.refs_1_, ...), custom_call_target="tpu_custom_call" | custom-call | tf_op jit(solution)/shard_map/project/pallas_call | solution.py:500
  34.5 3.6 %collective-permute-start.11 = (bf16[1024,256]{1,0:T(8,128)(2,1)S(1)}, bf16[1024,256]{1,0:T(8,128)(2,1)S(1)}, u32[]{:S(2)}, u32[]{:S(2)}) collective-permute-start(bf16[1024,256]{1,0:T(8,128)(2,1)S(1)} %get-tuple-element.85), channel_id=1, source_target_pairs={{0,4},{4,8},{8,12},{12,16},{16,20},{20,24},{24,28},{1,5},{5,9},{9,... | collective-permute-start | bytes 1572872 | tf_op jit(solution)/shard_map/ppermute | solution.py:57
  38.2 2.7 %order.1 = (bf16[256,1024]{1,0:T(8,128)(2,1)S(1)}, bf16[256,1024]{1,0:T(8,128)(2,1)S(1)}, bf16[1024,256]{1,0:T(8,128)(2,1)S(1)}, bf16[128,256]{1,0:T(8,128)(2,1)S(1)}, bf16[256,128]{1,0:T(8,128)(2,1)S(1)}) custom-call(bf16[1024,1024]{1,0:T(8,128)(2,1)S(1)} %get-tuple-element.68.p_ref, bf16[1024,1024]{1,0:T(8,128)(2,1)S(1)} %get-tuple-element.69.pt_ref, ...), custom_call_target="tpu_custom_call" | custom-call | tf_op jit(solution)/shard_map/order/pallas_call | solution.py:518
  40.9 9.2 %collective-permute-done.12.refs_1_ = bf16[64,256]{1,0:T(8,128)(2,1)S(1)} collective-permute-done((bf16[64,256]{1,0:T(8,128)(2,1)S(1)}, bf16[64,256]{1,0:T(8,128)(2,1)S(1)}, u32[]{:S(2)}, u32[]{:S(2)}) %collective-permute-start.12) | collective-permute-done | bytes 32800 | tf_op jit(solution)/shard_map/ppermute | solution.py:101
  50.1 4.5 %collective-permute-start.15 = (bf16[128,256]{1,0:T(8,128)(2,1)S(1)}, bf16[128,256]{1,0:T(8,128)(2,1)S(1)}, u32[]{:S(2)}, u32[]{:S(2)}) collective-permute-start(bf16[128,256]{1,0:T(8,128)(2,1)S(1)} %stack.5.refs_0_), channel_id=1, source_target_pairs={{0,24},{4,28},{8,16},{12,20},{16,8},{20,12},{24,0},{28,4},{1,25},{... | collective-permute-start | bytes 196616 | tf_op jit(solution)/shard_map/ppermute | solution.py:101
  55.2 4.9 %own.1 = (f32[256,1024]{1,0:T(8,128)S(1)}, f32[256,1024]{1,0:T(8,128)S(1)}, f32[8,512]{1,0:T(8,128)S(1)}, f32[8,512]{1,0:T(8,128)S(1)}, bf16[1024,512]{1,0:T(8,1...) custom-call(f32[4,4]{1,0:T(4,128)S(1)} %copy-done.5, ...), custom_call_target="tpu_custom_call" | custom-call | tf_op jit(solution)/shard_map/own/pallas_call | solution.py:541
  60.1 1.0 %window.1 = (bf16[2048,256]{1,0:T(8,128)(2,1)S(1)}, bf16[256,2048]{1,0:T(8,128)(2,1)S(1)}, bf16[64,256]{1,0:T(8,128)(2,1)S(1)}, bf16[256,64]{1,0:T(8,128)(2,1)S(1)}) custom-call(bf16[1024,256]{1,0:T(8,128)(2,1)S(1)} %get-tuple-element.83.k_ref, bf16[256,1024]{1,0:T(8,128)(2,1)S(1)} %get-tuple-element.84.vt_ref, ...), custom_call_target="tpu_custom_call" | custom-call | tf_op jit(solution)/shard_map/window/pallas_call | solution.py:562
  61.1 2.8 %rest.3.refs_0_ = bf16[384,256]{1,0:T(8,128)(2,1)S(1)} custom-call(s32[4,8]{1,0:T(4,128)S(1)} %bitcast.1, f32[4,4]{1,0:T(4,128)S(1)} %copy-done.5, bf16[256,1024]{1,0:T(8,128)(2,1)S(1)} %get-tuple-element.82.qt_ref, bf16[2048,256]{1,0:T(8,128)(2,1)S(1)} %get-tuple-element.92.kw_ref, bf16[256,2048]{1,0:T(8,128)(2,1)S(1)} %get-tuple-element.93.vw_ref, ...), custom_call_target="tpu_custom_call" | custom-call | tf_op jit(solution)/shard_map/rest/pallas_call | solution.py:601
  63.8 1.5 %collective-permute-start.16 = (bf16[384,256]{1,0:T(8,128)(2,1)S(1)}, bf16[384,256]{1,0:T(8,128)(2,1)S(1)}, u32[]{:S(2)}, u32[]{:S(2)}) collective-permute-start(bf16[384,256]{1,0:T(8,128)(2,1)S(1)} %rest.3.refs_0_), channel_id=1, source_target_pairs={{0,2},{2,0},{1,3},{3,1},{4,6},{6,4},{5,7},{7,5},{8,10},{10,8},{9,1... | collective-permute-start | bytes 589832 | tf_op jit(solution)/shard_map/ppermute | solution.py:53
  65.4 2.7 %rest.4.refs_0_ = bf16[384,256]{1,0:T(8,128)(2,1)S(1)} custom-call(s32[4,8]{1,0:T(4,128)S(1)} %bitcast.2, f32[4,4]{1,0:T(4,128)S(1)} %copy-done.5, bf16[256,1024]{1,0:T(8,128)(2,1)S(1)} %get-tuple-element.82.qt_ref, bf16[2048,256]{1,0:T(8,128)(2,1)S(1)} %get-tuple-element.92.kw_ref, bf16[256,2048]{1,0:T(8,128)(2,1)S(1)} %get-tuple-element.93.vw_ref, ...), custom_call_target="tpu_custom_call" | custom-call | tf_op jit(solution)/shard_map/rest/pallas_call | solution.py:601
  68.8 2.1 %rest.5.refs_0_ = bf16[256,256]{1,0:T(8,128)(2,1)S(1)} custom-call(s32[4,8]{1,0:T(4,128)S(1)} %bitcast.3, f32[4,4]{1,0:T(4,128)S(1)} %copy-done.5, bf16[256,1024]{1,0:T(8,128)(2,1)S(1)} %get-tuple-element.82.qt_ref, bf16[2048,256]{1,0:T(8,128)(2,1)S(1)} %get-tuple-element.92.kw_ref, bf16[256,2048]{1,0:T(8,128)(2,1)S(1)} %get-tuple-element.93.vw_ref, ...), custom_call_target="tpu_custom_call" | custom-call | tf_op jit(solution)/shard_map/rest/pallas_call | solution.py:601
  70.9 1.5 %collective-permute-start.20 = (bf16[256,256]{1,0:T(8,128)(2,1)S(1)}, bf16[256,256]{1,0:T(8,128)(2,1)S(1)}, u32[]{:S(2)}, u32[]{:S(2)}) collective-permute-start(bf16[256,256]{1,0:T(8,128)(2,1)S(1)} %rest.5.refs_0_), channel_id=1, source_target_pairs={{0,2},{2,0},{1,3},{3,1},{4,6},{6,4},{5,7},{7,5},{8,10},{10,8},{9,1... | collective-permute-start | bytes 393224 | tf_op jit(solution)/shard_map/ppermute | solution.py:53
  72.9 3.7 %collective-permute-done.20.refs_1_ = bf16[256,256]{1,0:T(8,128)(2,1)S(1)} collective-permute-done((bf16[256,256]{1,0:T(8,128)(2,1)S(1)}, bf16[256,256]{1,0:T(8,128)(2,1)S(1)}, u32[]{:S(2)}, u32[]{:S(2)}) %collective-permute-start.20) | collective-permute-done | bytes 131104 | tf_op jit(solution)/shard_map/ppermute | solution.py:53
  77.2 1.3 %collective-permute-done.24.refs_3_ = bf16[256,256]{1,0:T(8,128)(2,1)S(1)} collective-permute-done((bf16[256,256]{1,0:T(8,128)(2,1)S(1)}, bf16[256,256]{1,0:T(8,128)(2,1)S(1)}, u32[]{:S(2)}, u32[]{:S(2)}) %collective-permute-start.24) | collective-permute-done | bytes 131104 | tf_op jit(solution)/shard_map/ppermute | solution.py:53
  78.5 1.1 %output.3.refs_4_ = bf16[1024,256]{1,0:T(8,128)(2,1)} custom-call(bf16[1024,256]{1,0:T(8,128)(2,1)S(1)} %copy-done, bf16[256,256]{1,0:T(8,128)(2,1)S(1)} %rest.5.refs_0_, bf16[256,256]{1,0:T(8,128)(2,1)S(1)} %collective-permute-done.20.refs_1_, bf16[256,256]{1,0:T(8,128)(2,1)S(1)} %collective-permute-done.23.refs_2_, ...), custom_call_target="tpu_custom_call" | custom-call | tf_op jit(solution)/shard_map/output/pallas_call | solution.py:587
  79.7 1.8 %output.4.refs_4_ = bf16[1024,256]{1,0:T(8,128)(2,1)} custom-call(bf16[1024,256]{1,0:T(8,128)(2,1)S(1)} %copy-done, bf16[384,256]{1,0:T(8,128)(2,1)S(1)} %rest.3.refs_0_, bf16[384,256]{1,0:T(8,128)(2,1)S(1)} %collective-permute-done.16.refs_1_, bf16[384,256]{1,0:T(8,128)(2,1)S(1)} %collective-permute-done.21.refs_2_, ...), custom_call_target="tpu_custom_call", output_to_operand_aliasing={{}: (5, {})} | custom-call | tf_op jit(solution)/shard_map/output/pallas_call | solution.py:587
  81.4 1.8 %output.5 = bf16[1024,256]{1,0:T(8,128)(2,1)} custom-call(bf16[1024,256]{1,0:T(8,128)(2,1)S(1)} %copy-done, bf16[384,256]{1,0:T(8,128)(2,1)S(1)} %rest.4.refs_0_, bf16[384,256]{1,0:T(8,128)(2,1)S(1)} %collective-permute-done.17.refs_1_, bf16[384,256]{1,0:T(8,128)(2,1)S(1)} %collective-permute-done.18.refs_2_, ...), custom_call_target="tpu_custom_call", output_to_operand_aliasing={{}: (5, {})} | custom-call | tf_op jit(solution)/shard_map/output/pallas_call | solution.py:587
  (53 shorter events, 4.1 us)
Async XLA Ops:
  2.3 23.4 %copy-start.2 = (bf16[1024,256]{1,0:T(8,128)(2,1)S(1)}, bf16[1024,256]{1,0:T(8,128)(2,1)}, u32[]{:S(2)}) copy-start(bf16[1024,256]{1,0:T(8,128)(2,1)} %wq_ref.1) | copy-start | bytes 1572868
  2.3 23.4 %copy-start.3 = (bf16[1024,256]{1,0:T(8,128)(2,1)S(1)}, bf16[1024,256]{1,0:T(8,128)(2,1)}, u32[]{:S(2)}) copy-start(bf16[1024,256]{1,0:T(8,128)(2,1)} %wv_ref.1) | copy-start | bytes 1572868
  2.3 23.4 %copy-start.4 = (bf16[1024,256]{1,0:T(8,128)(2,1)S(1)}, bf16[1024,256]{1,0:T(8,128)(2,1)}, u32[]{:S(2)}) copy-start(bf16[1024,256]{1,0:T(8,128)(2,1)} %wk_in.1) | copy-start | bytes 1572868
  2.3 23.4 %copy-start.8 = (s32[1,512]{1,0:T(1,128)S(1)}, s32[1,512]{1,0:T(1,128)}, u32[]{:S(2)}) copy-start(s32[1,512]{1,0:T(1,128)} %mask_ref.3) | copy-start | bytes 6148
  2.3 23.4 %copy-start.9 = (s32[1,1024]{1,0:T(1,128)S(1)}, s32[1,1024]{1,0:T(1,128)}, u32[]{:S(2)}) copy-start(s32[1,1024]{1,0:T(1,128)} %order_ref.1) | copy-start | bytes 12292
  2.4 20.8 %collective-permute-start.4 = (bf16[144,512]{1,0:T(8,128)(2,1)S(1)}, bf16[144,512]{1,0:T(8,128)(2,1)S(1)}, u32[]{:S(2)}, u32[]{:S(2)}) collective-permute-start(bf16[144,512]{1,0:T(8,128)(2,1)S(1)} %get-tuple-element.59), channel_id=1, source_target_pairs={{0,8},{4,12},{8,0},{12,4},{16,24},{20,28},{24,16},{28,20},{1,9},{5... | collective-permute-start | bytes 442376 | tf_op jit(solution)/shard_map/ppermute | solution.py:101
  5.5 10.0 %collective-permute-start = (bf16[160,256]{1,0:T(8,128)(2,1)S(1)}, bf16[160,256]{1,0:T(8,128)(2,1)S(1)}, u32[]{:S(2)}, u32[]{:S(2)}) collective-permute-start(bf16[160,256]{1,0:T(8,128)(2,1)S(1)} %get-tuple-element.55), channel_id=1, source_target_pairs={{0,28},{4,24},{8,20},{12,16},{16,12},{20,8},{24,4},{28,0},{1,29},{... | collective-permute-start | bytes 245768 | tf_op jit(solution)/shard_map/ppermute | solution.py:101
  8.9 9.8 %collective-permute-start.1 = (bf16[160,256]{1,0:T(8,128)(2,1)S(1)}, bf16[160,256]{1,0:T(8,128)(2,1)S(1)}, u32[]{:S(2)}, u32[]{:S(2)}) collective-permute-start(bf16[160,256]{1,0:T(8,128)(2,1)S(1)} %get-tuple-element.56), channel_id=1, source_target_pairs={{0,24},{4,28},{8,16},{12,20},{16,8},{20,12},{24,0},{28,4},{1,25},{... | collective-permute-start | bytes 245768 | tf_op jit(solution)/shard_map/ppermute | solution.py:101
  10.3 12.4 %collective-permute-start.2 = (bf16[160,256]{1,0:T(8,128)(2,1)S(1)}, bf16[160,256]{1,0:T(8,128)(2,1)S(1)}, u32[]{:S(2)}, u32[]{:S(2)}) collective-permute-start(bf16[160,256]{1,0:T(8,128)(2,1)S(1)} %get-tuple-element.57), channel_id=1, source_target_pairs={{0,20},{4,16},{8,28},{12,24},{16,4},{20,0},{24,12},{28,8},{1,21},{... | collective-permute-start | bytes 245768 | tf_op jit(solution)/shard_map/ppermute | solution.py:101
  11.0 12.2 %collective-permute-start.3 = (bf16[160,256]{1,0:T(8,128)(2,1)S(1)}, bf16[160,256]{1,0:T(8,128)(2,1)S(1)}, u32[]{:S(2)}, u32[]{:S(2)}) collective-permute-start(bf16[160,256]{1,0:T(8,128)(2,1)S(1)} %get-tuple-element.58), channel_id=1, source_target_pairs={{0,16},{4,20},{8,24},{12,28},{16,0},{20,4},{24,8},{28,12},{1,17},{... | collective-permute-start | bytes 245768 | tf_op jit(solution)/shard_map/ppermute | solution.py:101
  15.5 9.5 %collective-permute-start.8 = (bf16[144,512]{1,0:T(8,128)(2,1)S(1)}, bf16[144,512]{1,0:T(8,128)(2,1)S(1)}, u32[]{:S(2)}, u32[]{:S(2)}) collective-permute-start(bf16[144,512]{1,0:T(8,128)(2,1)S(1)} %get-tuple-element.75), channel_id=1, source_target_pairs={{0,12},{4,8},{8,4},{12,0},{16,28},{20,24},{24,20},{28,16},{1,13},{... | collective-permute-start | bytes 442376 | tf_op jit(solution)/shard_map/ppermute | solution.py:101
  18.7 6.4 %collective-permute-start.9 = (bf16[144,512]{1,0:T(8,128)(2,1)S(1)}, bf16[144,512]{1,0:T(8,128)(2,1)S(1)}, u32[]{:S(2)}, u32[]{:S(2)}) collective-permute-start(bf16[144,512]{1,0:T(8,128)(2,1)S(1)} %get-tuple-element.76), channel_id=1, source_target_pairs={{0,4},{4,0},{8,12},{12,8},{16,20},{20,16},{24,28},{28,24},{1,5},{5... | collective-permute-start | bytes 442376 | tf_op jit(solution)/shard_map/ppermute | solution.py:101
  23.2 7.5 %collective-permute-start.5 = (bf16[512,256]{1,0:T(8,128)(2,1)S(1)}, bf16[512,256]{1,0:T(8,128)(2,1)S(1)}, u32[]{:S(2)}, u32[]{:S(2)}) collective-permute-start(bf16[512,256]{1,0:T(8,128)(2,1)S(1)} %stack.3.early_ref.refs_0_), channel_id=1, source_target_pairs={{0,2},{2,0},{1,3},{3,1},{4,6},{6,4},{5,7},{7,5},{8,10},{10,8},{9,1... | collective-permute-start | bytes 786440 | tf_op jit(solution)/shard_map/ppermute | solution.py:53
  25.1 5.5 %collective-permute-start.10 = (bf16[384,512]{1,0:T(8,128)(2,1)S(1)}, bf16[384,512]{1,0:T(8,128)(2,1)S(1)}, u32[]{:S(2)}, u32[]{:S(2)}) collective-permute-start(bf16[384,512]{1,0:T(8,128)(2,1)S(1)} %stack.4.refs_4_), channel_id=1, source_target_pairs={{0,1},{1,0},{2,3},{3,2},{4,5},{5,4},{6,7},{7,6},{8,9},{9,8},{10,11... | collective-permute-start | bytes 1179656 | tf_op jit(solution)/shard_map/ppermute | solution.py:53
  25.2 5.5 %collective-permute-start.6 = (bf16[512,256]{1,0:T(8,128)(2,1)S(1)}, bf16[512,256]{1,0:T(8,128)(2,1)S(1)}, u32[]{:S(2)}, u32[]{:S(2)}) collective-permute-start(bf16[512,256]{1,0:T(8,128)(2,1)S(1)} %stack.3.early_ref.refs_0_), channel_id=1, source_target_pairs={{0,1},{1,0},{2,3},{3,2},{4,5},{5,4},{6,7},{7,6},{8,9},{9,8},{10,11... | collective-permute-start | bytes 786440 | tf_op jit(solution)/shard_map/ppermute | solution.py:53
  30.7 1.5 %collective-permute-start.7 = (bf16[512,256]{1,0:T(8,128)(2,1)S(1)}, bf16[512,256]{1,0:T(8,128)(2,1)S(1)}, u32[]{:S(2)}, u32[]{:S(2)}) collective-permute-start(bf16[512,256]{1,0:T(8,128)(2,1)S(1)} %collective-permute-done.5.refs_1_), channel_id=1, source_target_pairs={{0,1},{1,0},{2,3},{3,2},{4,5},{5,4},{6,7},{7,6},{8,9},{9,8},{10,11... | collective-permute-start | bytes 786440 | tf_op jit(solution)/shard_map/ppermute | solution.py:53
  34.5 25.6 %collective-permute-start.11 = (bf16[1024,256]{1,0:T(8,128)(2,1)S(1)}, bf16[1024,256]{1,0:T(8,128)(2,1)S(1)}, u32[]{:S(2)}, u32[]{:S(2)}) collective-permute-start(bf16[1024,256]{1,0:T(8,128)(2,1)S(1)} %get-tuple-element.85), channel_id=1, source_target_pairs={{0,4},{4,8},{8,12},{12,16},{16,20},{20,24},{24,28},{1,5},{5,9},{9,... | collective-permute-start | bytes 1572872 | tf_op jit(solution)/shard_map/ppermute | solution.py:57
  38.1 12.0 %collective-permute-start.12 = (bf16[64,256]{1,0:T(8,128)(2,1)S(1)}, bf16[64,256]{1,0:T(8,128)(2,1)S(1)}, u32[]{:S(2)}, u32[]{:S(2)}) collective-permute-start(bf16[64,256]{1,0:T(8,128)(2,1)S(1)} %get-tuple-element.91.refs_0_), channel_id=1, source_target_pairs={{0,4},{4,0},{8,12},{12,8},{16,20},{20,16},{24,28},{28,24},{1,5},{5... | collective-permute-start | bytes 98312 | tf_op jit(solution)/shard_map/ppermute | solution.py:101
  38.2 16.9 %copy-start.5 = (f32[4,4]{1,0:T(4,128)S(1)}, f32[4,4]{1,0:T(4,128)}, u32[]{:S(2)}) copy-start(f32[4,4]{1,0:T(4,128)} %mix_ref.7) | copy-start | bytes 196
  50.1 10.0 %collective-permute-start.15 = (bf16[128,256]{1,0:T(8,128)(2,1)S(1)}, bf16[128,256]{1,0:T(8,128)(2,1)S(1)}, u32[]{:S(2)}, u32[]{:S(2)}) collective-permute-start(bf16[128,256]{1,0:T(8,128)(2,1)S(1)} %stack.5.refs_0_), channel_id=1, source_target_pairs={{0,24},{4,28},{8,16},{12,20},{16,8},{20,12},{24,0},{28,4},{1,25},{... | collective-permute-start | bytes 196616 | tf_op jit(solution)/shard_map/ppermute | solution.py:101
  54.5 5.6 %collective-permute-start.14 = (bf16[128,256]{1,0:T(8,128)(2,1)S(1)}, bf16[128,256]{1,0:T(8,128)(2,1)S(1)}, u32[]{:S(2)}, u32[]{:S(2)}) collective-permute-start(bf16[128,256]{1,0:T(8,128)(2,1)S(1)} %stack.5.refs_0_), channel_id=1, source_target_pairs={{0,16},{4,20},{8,24},{12,28},{16,0},{20,4},{24,8},{28,12},{1,17},{... | collective-permute-start | bytes 196616 | tf_op jit(solution)/shard_map/ppermute | solution.py:101
  54.5 5.6 %collective-permute-start.13 = (bf16[128,256]{1,0:T(8,128)(2,1)S(1)}, bf16[128,256]{1,0:T(8,128)(2,1)S(1)}, u32[]{:S(2)}, u32[]{:S(2)}) collective-permute-start(bf16[128,256]{1,0:T(8,128)(2,1)S(1)} %stack.5.refs_0_), channel_id=1, source_target_pairs={{0,8},{4,12},{8,0},{12,4},{16,24},{20,28},{24,16},{28,20},{1,9},{5... | collective-permute-start | bytes 196616 | tf_op jit(solution)/shard_map/ppermute | solution.py:101
  63.8 9.1 %collective-permute-start.16 = (bf16[384,256]{1,0:T(8,128)(2,1)S(1)}, bf16[384,256]{1,0:T(8,128)(2,1)S(1)}, u32[]{:S(2)}, u32[]{:S(2)}) collective-permute-start(bf16[384,256]{1,0:T(8,128)(2,1)S(1)} %rest.3.refs_0_), channel_id=1, source_target_pairs={{0,2},{2,0},{1,3},{3,1},{4,6},{6,4},{5,7},{7,5},{8,10},{10,8},{9,1... | collective-permute-start | bytes 589832 | tf_op jit(solution)/shard_map/ppermute | solution.py:53
  68.1 10.4 %copy-start = (bf16[1024,256]{1,0:T(8,128)(2,1)S(1)}, bf16[1024,256]{1,0:T(8,128)(2,1)}, u32[]{:S(2)}) copy-start(bf16[1024,256]{1,0:T(8,128)(2,1)} %w_ref.5) | copy-start | bytes 1572868
  68.2 8.5 %collective-permute-start.17 = (bf16[384,256]{1,0:T(8,128)(2,1)S(1)}, bf16[384,256]{1,0:T(8,128)(2,1)S(1)}, u32[]{:S(2)}, u32[]{:S(2)}) collective-permute-start(bf16[384,256]{1,0:T(8,128)(2,1)S(1)} %rest.4.refs_0_), channel_id=1, source_target_pairs={{0,2},{2,0},{1,3},{3,1},{4,6},{6,4},{5,7},{7,5},{8,10},{10,8},{9,1... | collective-permute-start | bytes 589832 | tf_op jit(solution)/shard_map/ppermute | solution.py:53
  70.9 5.7 %collective-permute-start.20 = (bf16[256,256]{1,0:T(8,128)(2,1)S(1)}, bf16[256,256]{1,0:T(8,128)(2,1)S(1)}, u32[]{:S(2)}, u32[]{:S(2)}) collective-permute-start(bf16[256,256]{1,0:T(8,128)(2,1)S(1)} %rest.5.refs_0_), channel_id=1, source_target_pairs={{0,2},{2,0},{1,3},{3,1},{4,6},{6,4},{5,7},{7,5},{8,10},{10,8},{9,1... | collective-permute-start | bytes 393224 | tf_op jit(solution)/shard_map/ppermute | solution.py:53
  72.4 4.7 %collective-permute-start.23 = (bf16[256,256]{1,0:T(8,128)(2,1)S(1)}, bf16[256,256]{1,0:T(8,128)(2,1)S(1)}, u32[]{:S(2)}, u32[]{:S(2)}) collective-permute-start(bf16[256,256]{1,0:T(8,128)(2,1)S(1)} %rest.5.refs_0_), channel_id=1, source_target_pairs={{0,1},{1,0},{2,3},{3,2},{4,5},{5,4},{6,7},{7,6},{8,9},{9,8},{10,11... | collective-permute-start | bytes 393224 | tf_op jit(solution)/shard_map/ppermute | solution.py:53
  72.4 7.2 %collective-permute-start.21 = (bf16[384,256]{1,0:T(8,128)(2,1)S(1)}, bf16[384,256]{1,0:T(8,128)(2,1)S(1)}, u32[]{:S(2)}, u32[]{:S(2)}) collective-permute-start(bf16[384,256]{1,0:T(8,128)(2,1)S(1)} %rest.3.refs_0_), channel_id=1, source_target_pairs={{0,1},{1,0},{2,3},{3,2},{4,5},{5,4},{6,7},{7,6},{8,9},{9,8},{10,11... | collective-permute-start | bytes 589832 | tf_op jit(solution)/shard_map/ppermute | solution.py:53
  72.9 6.7 %collective-permute-start.22 = (bf16[384,256]{1,0:T(8,128)(2,1)S(1)}, bf16[384,256]{1,0:T(8,128)(2,1)S(1)}, u32[]{:S(2)}, u32[]{:S(2)}) collective-permute-start(bf16[384,256]{1,0:T(8,128)(2,1)S(1)} %collective-permute-done.16.refs_1_), channel_id=1, source_target_pairs={{0,1},{1,0},{2,3},{3,2},{4,5},{5,4},{6,7},{7,6},{8,9},{9,8},{10,11... | collective-permute-start | bytes 589832 | tf_op jit(solution)/shard_map/ppermute | solution.py:53
  76.6 4.8 %collective-permute-start.18 = (bf16[384,256]{1,0:T(8,128)(2,1)S(1)}, bf16[384,256]{1,0:T(8,128)(2,1)S(1)}, u32[]{:S(2)}, u32[]{:S(2)}) collective-permute-start(bf16[384,256]{1,0:T(8,128)(2,1)S(1)} %rest.4.refs_0_), channel_id=1, source_target_pairs={{0,1},{1,0},{2,3},{3,2},{4,5},{5,4},{6,7},{7,6},{8,9},{9,8},{10,11... | collective-permute-start | bytes 589832 | tf_op jit(solution)/shard_map/ppermute | solution.py:53
  76.6 4.8 %collective-permute-start.19 = (bf16[384,256]{1,0:T(8,128)(2,1)S(1)}, bf16[384,256]{1,0:T(8,128)(2,1)S(1)}, u32[]{:S(2)}, u32[]{:S(2)}) collective-permute-start(bf16[384,256]{1,0:T(8,128)(2,1)S(1)} %collective-permute-done.17.refs_1_), channel_id=1, source_target_pairs={{0,1},{1,0},{2,3},{3,2},{4,5},{5,4},{6,7},{7,6},{8,9},{9,8},{10,11... | collective-permute-start | bytes 589832 | tf_op jit(solution)/shard_map/ppermute | solution.py:53
  77.1 1.4 %collective-permute-start.24 = (bf16[256,256]{1,0:T(8,128)(2,1)S(1)}, bf16[256,256]{1,0:T(8,128)(2,1)S(1)}, u32[]{:S(2)}, u32[]{:S(2)}) collective-permute-start(bf16[256,256]{1,0:T(8,128)(2,1)S(1)} %collective-permute-done.20.refs_1_), channel_id=1, source_target_pairs={{0,1},{1,0},{2,3},{3,2},{4,5},{5,4},{6,7},{7,6},{8,9},{9,8},{10,11... | collective-permute-start | bytes 393224 | tf_op jit(solution)/shard_map/ppermute | solution.py:53
  (3 other events, 3.3 us)

commit v7 on v6

--- a/solution.py
+++ b/solution.py
@@ -19,7 +19,8 @@
 I32 = jnp.int32
 HIDE = -1e30
 VMEM_LIMIT = 24 * 1024 * 1024
-PARTS = (2, 3, 3)
+COST = pl.CostEstimate(flops=1, bytes_accessed=1, transcendentals=0)
+PARTS = (4, 4)
 
 X_PAIRS = [(0, 2), (2, 0), (1, 3), (3, 1)]
 CORE_PAIRS = [(0, 1), (1, 0), (2, 3), (3, 2)]
@@ -93,8 +94,23 @@
         in_specs=vmem_specs(len(parts)) + [pl.BlockSpec(memory_space=pl.ANY)] * len(after),
         out_specs=pl.BlockSpec(memory_space=pltpu.VMEM),
         compiler_params=pltpu.CompilerParams(vmem_limit_bytes=VMEM_LIMIT),
+        cost_estimate=COST,
         name="stack",
     )(*parts, *after)
+
+
+def packed_rows(select, packed, parts):
+    quarter = min(part.shape[1] for part in parts)
+    return pl.pallas_call(
+        pack_kernel,
+        out_shape=jax.ShapeDtypeStruct((packed, quarter), BF),
+        in_specs=vmem_specs(1 + len(parts)),
+        out_specs=pl.BlockSpec(memory_space=pltpu.VMEM),
+        scratch_shapes=[pltpu.VMEM((sum(part.shape[0] for part in parts), quarter), BF)],
+        compiler_params=pltpu.CompilerParams(vmem_limit_bytes=VMEM_LIMIT),
+        cost_estimate=COST,
+        name="pack",
+    )(select, *parts)
 
 
 def by_distance(block, distance):
@@ -106,6 +122,7 @@
     slabs = lax.axis_size("seq")
     rows = tok_rows // slabs
     quarter = width // 4
+    packed = tok_rows - mask_ids.shape[1]
     if slabs != 8:
         split = tokens.reshape(slabs, rows, width)
         mine = lax.dynamic_slice_in_dim(split, lax.axis_index("head") * quarter, quarter, axis=2)
@@ -116,7 +133,9 @@
         second = over_head(first, CORE_PAIRS)
         fourth = over_head(third, CORE_PAIRS)
         pieces = [(first, 0, (0,)), (third, 0, (2,)), (second, 0, (1,)), (fourth, 0, (3,))]
-        return pieces, prepare(first), [to_next(mask_ids)]
+        prepared = prepare(first)
+        halo = to_next(packed_rows(prepared[2], packed, (first,)))
+        return pieces, prepared, [to_next(mask_ids)], halo
     distances = (7, 6, 5, 4, 3, 2, 1)
     near_rows, far_rows = rows + CODE_ROWS, rows + 2 * CODE_ROWS
     *blocks, own = pl.pallas_call(
@@ -129,20 +148,23 @@
         in_specs=vmem_specs(2),
         out_specs=vmem_specs(8),
         compiler_params=pltpu.CompilerParams(vmem_limit_bytes=VMEM_LIMIT),
+        cost_estimate=COST,
         name="send",
     )(tokens, mask_ids)
     arrived = [by_distance(block, d) for block, d in zip(blocks, distances)]
-    far = stacked(arrived[:4], rows, (arrived[5],))
+    prepared = prepare(arrived[0])
+    far = stacked(arrived[:4], rows, (arrived[6], prepared[2]))
     near = stacked(arrived[4:], rows)
     far_x = over_head(far, X_PAIRS)
+    halo = packed_rows(prepared[2], packed, (far, near, own))
     near_core = over_head(near, CORE_PAIRS)
     far_core = over_head(far, CORE_PAIRS)
-    prepared = prepare(far)
-    far_x, prepared = lax.optimization_barrier((far_x, prepared))
+    far_x, _ = lax.optimization_barrier((far_x, halo))
+    halo = to_next(halo)
     far_last = over_head(far_x, CORE_PAIRS)
     pieces = [(far, 0, (0,)), (far_x, 0, (2,)), (far_core, 0, (1,)), (far_last, 0, (3,))]
     pieces += [(near, 4 * rows, (0, 2)), (near_core, 4 * rows, (1, 3)), (own, 7 * rows, None)]
-    return pieces, prepared, [arrived[6], arrived[4], arrived[0]]
+    return pieces, prepared, [arrived[6], arrived[4], arrived[0]], halo
 
 
 def column(row, lanes=128):
@@ -210,10 +232,25 @@
     wk_ref[...] = wk_in[...]
 
 
+def pack_kernel(sel_ref, *refs):
+    parts, (out_ref, rows_ref) = refs[:-2], refs[-2:]
+    quarter = out_ref.shape[1]
+    at = 0
+    for part in parts:
+        height, width = part.shape
+        if width == 4 * quarter:
+            start = pl.multiple_of(lax.axis_index("head") * quarter, quarter)
+            rows_ref[at : at + height] = part[:, pl.ds(start, quarter)]
+        else:
+            rows_ref[at : at + height] = part[:, :quarter]
+        at += height
+    out_ref[...] = nn(sel_ref[: out_ref.shape[0]], rows_ref[...]).astype(BF)
+
+
 def project_kernel(places, *refs):
     count = len(places)
     piece_refs, refs = refs[:count], refs[count:]
-    wt_ref, wk_ref, sel_ref, fcol_ref, comp_ref, summ_ref, k_ref, v_ref, x_ref = refs
+    wt_ref, wk_ref, sel_ref, fcol_ref, summ_ref, k_ref, v_ref, x_ref = refs
     quarter = x_ref.shape[1] // 4
     head = lax.axis_index("head")
     for piece, (row, distances) in zip(piece_refs, places):
@@ -227,26 +264,20 @@
                 :, part * quarter : (part + 1) * quarter
             ]
     group = wk_ref.shape[1]
-    packed = comp_ref.shape[0] // 2
-    lead = packed + SUMM_ROWS
+    near = x_ref.shape[0] // POOL1
+    lead = sel_ref.shape[0] - near
     x = x_ref[...]
     keys = nn(x, wk_ref[...]).astype(BF)
     k_ref[...] = keys
     vt = nt(wt_ref[group:], x).astype(BF)
     v_ref[...] = vt
-    sel = sel_ref[:lead]
+    sel = sel_ref[lead - SUMM_ROWS : lead]
     kl = nn(sel, keys)
     vl = nt(vt, sel)
-    comp_ref[:packed] = kl[:packed].astype(BF)
-    vc = vl[:, :packed].astype(BF)
-    for part in range(packed // group):
-        comp_ref[packed + part * group : packed + (part + 1) * group] = vc[
-            :, part * group : (part + 1) * group
-        ]
     factor = fcol_ref[:SUMM_ROWS, :1]
-    summ_k = (kl[packed:] * factor).astype(BF)
+    summ_k = (kl * factor).astype(BF)
     tail = jnp.concatenate(
-        [vl[:, packed:], jnp.zeros((group, 128 - SUMM_ROWS), F32)], axis=1
+        [vl, jnp.zeros((group, 128 - SUMM_ROWS), F32)], axis=1
     )
     summ_v = (jnp.transpose(tail)[:SUMM_ROWS] * factor).astype(BF)
     summ_ref[:SUMM_ROWS] = summ_k
@@ -342,20 +373,19 @@
             near_ref[rows, at : at + FBLK] = near_out[rows, lanes] * scales[h]
 
 
-def window_kernel(k_ref, vt_ref, comp_ref, e_ref, et_ref, *refs):
-    summ_refs, (kw_ref, vw_ref, ck_ref, cv_ref, all_ref) = refs[:-5], refs[-5:]
+def window_kernel(k_ref, vt_ref, wt_ref, wk_ref, e_ref, et_ref, *refs):
+    halo_refs, refs = refs[:4], refs[4:]
+    summ_refs, (kw_ref, vw_ref, ck_ref, cv_ref, all_ref, x_ref) = refs[:-6], refs[-6:]
     tok_rows, group = k_ref.shape
-    packed = e_ref.shape[1]
-    kw_ref[:tok_rows] = nn(e_ref[...], comp_ref[:packed]).astype(BF)
+    quarter = x_ref.shape[1] // 4
+    head = lax.axis_index("head")
+    for distance, part in zip((0, 2, 1, 3), halo_refs):
+        start = pl.multiple_of((head ^ distance) * quarter, quarter)
+        x_ref[:, pl.ds(start, quarter)] = part[...]
+    x = x_ref[...]
+    kw_ref[:tok_rows] = nn(e_ref[...], nn(x, wk_ref[...]).astype(BF)).astype(BF)
     kw_ref[tok_rows:] = k_ref[...]
-    prev = None
-    for part in range(packed // group):
-        term = nn(
-            comp_ref[packed + part * group : packed + (part + 1) * group],
-            et_ref[part * group : (part + 1) * group],
-        )
-        prev = term if prev is None else prev + term
-    vw_ref[:, :tok_rows] = prev.astype(BF)
+    vw_ref[:, :tok_rows] = nn(nt(wt_ref[group:], x).astype(BF), et_ref[...]).astype(BF)
     vw_ref[:, tok_rows:] = vt_ref[...]
     at = 0
     for part in summ_refs:
@@ -491,29 +521,32 @@
             in_specs=vmem_specs(5) + [pl.BlockSpec(memory_space=pl.ANY)],
             out_specs=vmem_specs(8),
             compiler_params=params,
+            cost_estimate=COST,
             name="prepare",
         )(order, mask_ids, w_query, w_value, w_key, early)
 
-    pieces, prepared, before = exchange_tokens(tokens, mask_ids, prepare)
+    pieces, prepared, before, halo = exchange_tokens(tokens, mask_ids, prepare)
     permute, permute_t, select, f_col, f_row, seen, w_t, w_k = prepared
     places = tuple((row, distances) for _, row, distances in pieces)
-    comp, summ, k0, v0, rows_here = pl.pallas_call(
+    summ, k0, v0, rows_here = pl.pallas_call(
         functools.partial(project_kernel, places),
         out_shape=(
-            shape((2 * packed, group), BF),
             shape((step, group), BF),
             shape((tok_rows, group), BF),
             shape((group, tok_rows), BF),
             shape((tok_rows, width), BF),
         ),
         in_specs=vmem_specs(len(pieces) + 4),
-        out_specs=vmem_specs(5),
+        out_specs=vmem_specs(4),
         compiler_params=params,
+        cost_estimate=COST,
         name="project",
     )(*[piece for piece, _, _ in pieces], w_t, w_k, select, f_col)
     if slabs == 8:
         other = by_distance(summ, 1)
-    comp_before = to_next(comp)
+    halo, summ = lax.optimization_barrier((halo, summ))
+    halo_x = over_head(halo, X_PAIRS)
+    halo_core = over_head(halo, CORE_PAIRS)
 
     q_t, v_t, keys, near_k, near_vt = pl.pallas_call(
         order_kernel,
@@ -527,6 +560,7 @@
         in_specs=vmem_specs(9),
         out_specs=vmem_specs(5),
         compiler_params=params,
+        cost_estimate=COST,
         name="order",
     )(permute, permute_t, select, f_col, f_row, w_t, rows_here, k0, v0)
     if slabs == 8:
@@ -556,9 +590,12 @@
             pltpu.VMEM((2, FBLK + near, heads * FBLK), BF),
         ],
         compiler_params=params,
+        cost_estimate=COST,
         name="own",
     )(level_mix, q_t, keys, v_t, near_k, near_vt, seen, *before)
 
+    halo_x, _ = lax.optimization_barrier((halo_x, top))
+    halo_last = over_head(halo_x, CORE_PAIRS)
     window_k, window_v, coarse_k, coarse_v = pl.pallas_call(
         window_kernel,
         out_shape=(
@@ -567,12 +604,13 @@
             shape((coarse, group), BF),
             shape((group, coarse), BF),
         ),
-        in_specs=vmem_specs(5 + len(summaries)),
+        in_specs=vmem_specs(10 + len(summaries)),
         out_specs=vmem_specs(4),
-        scratch_shapes=[pltpu.VMEM((slabs * step, group), BF)],
+        scratch_shapes=[pltpu.VMEM((slabs * step, group), BF), pltpu.VMEM((packed, width), BF)],
         compiler_params=params,
+        cost_estimate=COST,
         name="window",
-    )(keys, v_t, comp_before, expand, expand_t, *summaries)
+    )(keys, v_t, w_t, w_k, expand, expand_t, halo, halo_x, halo_core, halo_last, *summaries)
 
     total = (FINE_K - 1) * FBLK + coarse
     lists = fine_blocks.T
@@ -594,6 +632,7 @@
             out_specs=pl.BlockSpec((FBLK, group), lambda i, base=base: (i + base, 0)),
             input_output_aliases={5: 0} if previous else {},
             compiler_params=params,
+            cost_estimate=COST,
             name="output",
         )(w_out, attended, third, second, fourth, *previous)
 
@@ -610,6 +649,7 @@
                 pltpu.VMEM((2, total, heads * FBLK), BF),
             ],
             compiler_params=params,
+            cost_estimate=COST,
             name="rest",
         )(
             lists, level_mix, q_t, window_k, window_v, coarse_k, coarse_v, bias, acc, near_out, top, den
@@ -620,6 +660,7 @@
             old, old_third, old_second, old_base = waiting
             old_third, attended = lax.optimization_barrier((old_third, attended))
             out = finish(out, old, old_third, old_second, old_base)
+            third, out = lax.optimization_barrier((third, out))
         waiting = (attended, third, second, first)
         first += count
     return finish(out, *waiting)

time: 83.4 us -> 88.1 us (1.056)
  starting transfers between devices: 31.4 us -> 34.3 us
  waiting for transfers between devices: 23.6 us -> 25.5 us
    ppermute x11, waiting for transfers between devices: 14.6 us -> 8.71 us  [by_distance(): lax.ppermute(block, 'seq', [(i, i ^ distance) for i in range(lax.axis_siz...]
    ppermute x11, starting transfers between devices: 20.9 us -> 25.1 us  [by_distance(): lax.ppermute(block, 'seq', [(i, i ^ distance) for i in range(lax.axis_siz...]
    ppermute x1, waiting for transfers between devices: 0.01 us -> 4.08 us  [to_next(): lax.ppermute(block, 'seq', [(i, i + 1) for i in range(lax.axis_size('seq'...]
    ppermute x13, waiting for transfers between devices: 8.95 us -> 12.7 us  [over_head(): return lax.ppermute(block, 'head', pairs)]
    ppermute x13, starting transfers between devices: 6.92 us -> 5.64 us  [over_head(): return lax.ppermute(block, 'head', pairs)]
    pallas_call x1, Pallas kernels: 0.96 us -> 2.16 us  [local(): pl.pallas_call(window_kernel, out_shape=(shape((2 * tok_rows, group), BF)...]
    pallas_call x3 -> x2, Pallas kernels: 4.68 us -> 3.99 us  [finish(): pl.pallas_call(output_kernel, grid=(rows // FBLK,), out_shape=shape((tok_...]
    pallas_call x3 -> x2, Pallas kernels: 7.6 us -> 6.98 us  [local(): pl.pallas_call(functools.partial(rest_kernel, first, count), out_shape=sh...]
  transfers between devices with their start and end apart: 25 -> 25, of which waited for: 10 -> 11; matrix products, arithmetic and copies ran while one was open for 0% -> 0% of each run, Pallas kernels for 22% -> 20%
where the time goes in v7:
time: 88.1 us; the launch traced here: 87.9 us
  starting transfers between devices  34.3 us (39%)
  Pallas kernels  25.6 us (29%)
  waiting for transfers between devices  25.5 us (29%)
  local copies, waits for them, and re-layouts  2.3 us (3%)
    ppermute x11, starting transfers between devices, by_distance(): lax.ppermute(block, 'seq', [(i, i ^ distance) for i in range(lax.axis_siz...  25.1 us
    ppermute x13, waiting for transfers between devices, over_head(): return lax.ppermute(block, 'head', pairs)  12.7 us
    ppermute x11, waiting for transfers between devices, by_distance(): lax.ppermute(block, 'seq', [(i, i ^ distance) for i in range(lax.axis_siz...  8.71 us
    pallas_call x2, Pallas kernels, local(): pl.pallas_call(functools.partial(rest_kernel, first, count), out_shape=sh...  6.98 us
    ppermute x13, starting transfers between devices, over_head(): return lax.ppermute(block, 'head', pairs)  5.64 us
    pallas_call x1, Pallas kernels, local(): pl.pallas_call(functools.partial(own_kernel, tok_rows // slabs, len(befor...  4.86 us
    ppermute x1, waiting for transfers between devices, to_next(): lax.ppermute(block, 'seq', [(i, i + 1) for i in range(lax.axis_size('seq'...  4.08 us
    pallas_call x2, Pallas kernels, finish(): pl.pallas_call(output_kernel, grid=(rows // FBLK,), out_shape=shape((tok_...  3.99 us
  transfers between devices with their start and end apart: 25, of which 11 were waited for; matrix products, arithmetic and copies ran while one was open for 0% of the time, Pallas kernels for 20%

profile of v7, /device:TPU:0, one launch (start us, length us, event | category | flops | bytes accessed | tf_op | source)
XLA Modules:
  0.0 87.9 jit_solution(15187291527789569624)
XLA Ops:
  0.0 1.6 %copy-done = bf16[1024,1024]{1,0:T(8,128)(2,1)S(1)} copy-done((bf16[1024,1024]{1,0:T(8,128)(2,1)S(1)}, bf16[1024,1024]{1,0:T(8,128)(2,1)}, u32[]{:S(2)}) %copy-start) | copy-done | bytes 2097176
  1.6 0.7 copy-done.6
  2.4 3.0 %collective-permute-start.4 = (bf16[144,512]{1,0:T(8,128)(2,1)S(1)}, bf16[144,512]{1,0:T(8,128)(2,1)S(1)}, u32[]{:S(2)}, u32[]{:S(2)}) collective-permute-start(bf16[144,512]{1,0:T(8,128)(2,1)S(1)} %get-tuple-element.59), channel_id=1, source_target_pairs={{0,4},{4,0},{8,12},{12,8},{16,20},{20,16},{24,28},{28,24},{1,5},{5... | collective-permute-start | bytes 442376 | tf_op jit(solution)/shard_map/ppermute | solution.py:117
  5.4 3.5 %collective-permute-start = (bf16[160,256]{1,0:T(8,128)(2,1)S(1)}, bf16[160,256]{1,0:T(8,128)(2,1)S(1)}, u32[]{:S(2)}, u32[]{:S(2)}) collective-permute-start(bf16[160,256]{1,0:T(8,128)(2,1)S(1)} %get-tuple-element.49), channel_id=1, source_target_pairs={{0,28},{4,24},{8,20},{12,16},{16,12},{20,8},{24,4},{28,0},{1,29},{... | collective-permute-start | bytes 245768 | tf_op jit(solution)/shard_map/ppermute | solution.py:117
  9.0 1.9 %collective-permute-start.2 = (bf16[160,256]{1,0:T(8,128)(2,1)S(1)}, bf16[160,256]{1,0:T(8,128)(2,1)S(1)}, u32[]{:S(2)}, u32[]{:S(2)}) collective-permute-start(bf16[160,256]{1,0:T(8,128)(2,1)S(1)} %get-tuple-element.57), channel_id=1, source_target_pairs={{0,20},{4,16},{8,28},{12,24},{16,4},{20,0},{24,12},{28,8},{1,21},{... | collective-permute-start | bytes 245768 | tf_op jit(solution)/shard_map/ppermute | solution.py:117
  10.9 2.1 %collective-permute-start.3 = (bf16[160,256]{1,0:T(8,128)(2,1)S(1)}, bf16[160,256]{1,0:T(8,128)(2,1)S(1)}, u32[]{:S(2)}, u32[]{:S(2)}) collective-permute-start(bf16[160,256]{1,0:T(8,128)(2,1)S(1)} %get-tuple-element.58), channel_id=1, source_target_pairs={{0,16},{4,20},{8,24},{12,28},{16,0},{20,4},{24,8},{28,12},{1,17},{... | collective-permute-start | bytes 245768 | tf_op jit(solution)/shard_map/ppermute | solution.py:117
  13.1 5.7 %collective-permute-start.6 = (bf16[144,512]{1,0:T(8,128)(2,1)S(1)}, bf16[144,512]{1,0:T(8,128)(2,1)S(1)}, u32[]{:S(2)}, u32[]{:S(2)}) collective-permute-start(bf16[144,512]{1,0:T(8,128)(2,1)S(1)} %get-tuple-element.60), channel_id=1, source_target_pairs={{0,12},{4,8},{8,4},{12,0},{16,28},{20,24},{24,20},{28,16},{1,13},{... | collective-permute-start | bytes 442376 | tf_op jit(solution)/shard_map/ppermute | solution.py:117
  18.8 1.7 %collective-permute-start.7 = (bf16[144,512]{1,0:T(8,128)(2,1)S(1)}, bf16[144,512]{1,0:T(8,128)(2,1)S(1)}, u32[]{:S(2)}, u32[]{:S(2)}) collective-permute-start(bf16[144,512]{1,0:T(8,128)(2,1)S(1)} %get-tuple-element.61), channel_id=1, source_target_pairs={{0,8},{4,12},{8,0},{12,4},{16,24},{20,28},{24,16},{28,20},{1,9},{5... | collective-permute-start | bytes 442376 | tf_op jit(solution)/shard_map/ppermute | solution.py:117
  20.6 2.5 %prepare.1 = (bf16[1024,1024]{1,0:T(8,128)(2,1)S(1)}, bf16[1024,1024]{1,0:T(8,128)(2,1)S(1)}, bf16[672,1024]{1,0:T(8,128)(2,1)S(1)}, f32[160,128]{1,0:T(8,128)S(...) custom-call(s32[1,1024]{1,0:T(1,128)S(1)} %copy-done.8, ...), custom_call_target="tpu_custom_call" | custom-call | flops 1 | bytes 1 | tf_op jit(solution)/shard_map/prepare/pallas_call | solution.py:509
  23.1 1.6 %collective-permute-start.5 = (bf16[512,256]{1,0:T(8,128)(2,1)S(1)}, bf16[512,256]{1,0:T(8,128)(2,1)S(1)}, u32[]{:S(2)}, u32[]{:S(2)}) collective-permute-start(bf16[512,256]{1,0:T(8,128)(2,1)S(1)} %stack.3.refs_0_), channel_id=1, source_target_pairs={{0,2},{2,0},{1,3},{3,1},{4,6},{6,4},{5,7},{7,5},{8,10},{10,8},{9,1... | collective-permute-start | bytes 786440 | tf_op jit(solution)/shard_map/ppermute | solution.py:54
  24.7 1.2 %collective-permute-done.6.refs_0_.refs_1_ = bf16[144,512]{1,0:T(8,128)(2,1)S(1)} collective-permute-done((bf16[144,512]{1,0:T(8,128)(2,1)S(1)}, bf16[144,512]{1,0:T(8,128)(2,1)S(1)}, u32[]{:S(2)}, u32[]{:S(2)}) %collective-permute-start.6) | collective-permute-done | bytes 147488 | tf_op jit(solution)/shard_map/ppermute | solution.py:117
  27.5 2.7 %collective-permute-done.5.refs_1_ = bf16[512,256]{1,0:T(8,128)(2,1)S(1)} collective-permute-done((bf16[512,256]{1,0:T(8,128)(2,1)S(1)}, bf16[512,256]{1,0:T(8,128)(2,1)S(1)}, u32[]{:S(2)}, u32[]{:S(2)}) %collective-permute-start.5) | collective-permute-done | bytes 262176 | tf_op jit(solution)/shard_map/ppermute | solution.py:54
  30.2 3.6 %collective-permute-start.11 = (bf16[512,256]{1,0:T(8,128)(2,1)S(1)}, bf16[512,256]{1,0:T(8,128)(2,1)S(1)}, u32[]{:S(2)}, u32[]{:S(2)}) collective-permute-start(bf16[512,256]{1,0:T(8,128)(2,1)S(1)} %pack.1), channel_id=1, source_target_pairs={{0,4},{4,8},{8,12},{12,16},{16,20},{20,24},{24,28},{1,5},{5,9},{9,... | collective-permute-start | bytes 786440 | tf_op jit(solution)/shard_map/ppermute | solution.py:58
  33.8 1.9 %project.1 = (bf16[64,256]{1,0:T(8,128)(2,1)S(1)}, bf16[1024,256]{1,0:T(8,128)(2,1)S(1)}, bf16[256,1024]{1,0:T(8,128)(2,1)S(1)}, bf16[1024,1024]{1,0:T(8,128)(2,1)S(1)}) custom-call(bf16[512,256]{1,0:T(8,128)(2,1)S(1)} %stack.3.refs_0_, bf16[512,256]{1,0:T(8,128)(2,1)S(1)} %collective-permute-done.5.refs_1_, ...), custom_call_target="tpu_custom_call" | custom-call | flops 1 | bytes 1 | tf_op jit(solution)/shard_map/project/pallas_call | solution.py:531
  35.7 4.1 %collective-permute-done.11.refs_0_ = bf16[512,256]{1,0:T(8,128)(2,1)S(1)} collective-permute-done((bf16[512,256]{1,0:T(8,128)(2,1)S(1)}, bf16[512,256]{1,0:T(8,128)(2,1)S(1)}, u32[]{:S(2)}, u32[]{:S(2)}) %collective-permute-start.11) | collective-permute-done | bytes 262176 | tf_op jit(solution)/shard_map/ppermute | solution.py:58
  39.8 1.5 %collective-permute-start.12 = (bf16[512,256]{1,0:T(8,128)(2,1)S(1)}, bf16[512,256]{1,0:T(8,128)(2,1)S(1)}, u32[]{:S(2)}, u32[]{:S(2)}) collective-permute-start(bf16[512,256]{1,0:T(8,128)(2,1)S(1)} %collective-permute-done.11.refs_0_), channel_id=1, source_target_pairs={{0,2},{2,0},{1,3},{3,1},{4,6},{6,4},{5,7},{7,5},{8,10},{10,8},{9,1... | collective-permute-start | bytes 786440 | tf_op jit(solution)/shard_map/ppermute | solution.py:54
  41.3 2.6 %order.1 = (bf16[256,1024]{1,0:T(8,128)(2,1)S(1)}, bf16[256,1024]{1,0:T(8,128)(2,1)S(1)}, bf16[1024,256]{1,0:T(8,128)(2,1)S(1)}, bf16[128,256]{1,0:T(8,128)(2,1)S(1)}, bf16[256,128]{1,0:T(8,128)(2,1)S(1)}) custom-call(bf16[1024,1024]{1,0:T(8,128)(2,1)S(1)} %get-tuple-element.50.p_ref, bf16[1024,1024]{1,0:T(8,128)(2,1)S(1)} %get-tuple-element.51.pt_ref, ...), custom_call_target="tpu_custom_call" | custom-call | flops 1 | bytes 1 | tf_op jit(solution)/shard_map/order/pallas_call | solution.py:551
  43.9 4.9 %own.1 = (f32[256,1024]{1,0:T(8,128)S(1)}, f32[256,1024]{1,0:T(8,128)S(1)}, f32[8,512]{1,0:T(8,128)S(1)}, f32[8,512]{1,0:T(8,128)S(1)}, bf16[1024,512]{1,0:T(8,1...) custom-call(f32[4,4]{1,0:T(4,128)S(1)} %copy-done.5, ...), custom_call_target="tpu_custom_call" | custom-call | flops 1 | bytes 1 | tf_op jit(solution)/shard_map/own/pallas_call | solution.py:575
  49.4 2.5 %collective-permute-start.15 = (bf16[64,256]{1,0:T(8,128)(2,1)S(1)}, bf16[64,256]{1,0:T(8,128)(2,1)S(1)}, u32[]{:S(2)}, u32[]{:S(2)}) collective-permute-start(bf16[64,256]{1,0:T(8,128)(2,1)S(1)} %get-tuple-element.80.refs_0_), channel_id=1, source_target_pairs={{0,4},{4,0},{8,12},{12,8},{16,20},{20,16},{24,28},{28,24},{1,5},{5... | collective-permute-start | bytes 98312 | tf_op jit(solution)/shard_map/ppermute | solution.py:117
  51.9 1.9 %collective-permute-done.15.refs_1_ = bf16[64,256]{1,0:T(8,128)(2,1)S(1)} collective-permute-done((bf16[64,256]{1,0:T(8,128)(2,1)S(1)}, bf16[64,256]{1,0:T(8,128)(2,1)S(1)}, u32[]{:S(2)}, u32[]{:S(2)}) %collective-permute-start.15) | collective-permute-done | bytes 32800 | tf_op jit(solution)/shard_map/ppermute | solution.py:117
  53.8 3.8 %collective-permute-start.18 = (bf16[128,256]{1,0:T(8,128)(2,1)S(1)}, bf16[128,256]{1,0:T(8,128)(2,1)S(1)}, u32[]{:S(2)}, u32[]{:S(2)}) collective-permute-start(bf16[128,256]{1,0:T(8,128)(2,1)S(1)} %stack.5.refs_4_), channel_id=1, source_target_pairs={{0,24},{4,28},{8,16},{12,20},{16,8},{20,12},{24,0},{28,4},{1,25},{... | collective-permute-start | bytes 196616 | tf_op jit(solution)/shard_map/ppermute | solution.py:117
  58.2 2.1 %collective-permute-done.18.refs_7_ = bf16[128,256]{1,0:T(8,128)(2,1)S(1)} collective-permute-done((bf16[128,256]{1,0:T(8,128)(2,1)S(1)}, bf16[128,256]{1,0:T(8,128)(2,1)S(1)}, u32[]{:S(2)}, u32[]{:S(2)}) %collective-permute-start.18) | collective-permute-done | bytes 65568 | tf_op jit(solution)/shard_map/ppermute | solution.py:117
  60.4 2.9 %collective-permute-done.17.refs_6_ = bf16[128,256]{1,0:T(8,128)(2,1)S(1)} collective-permute-done((bf16[128,256]{1,0:T(8,128)(2,1)S(1)}, bf16[128,256]{1,0:T(8,128)(2,1)S(1)}, u32[]{:S(2)}, u32[]{:S(2)}) %collective-permute-start.17) | collective-permute-done | bytes 65568 | tf_op jit(solution)/shard_map/ppermute | solution.py:117
  63.3 2.2 %window.1 = (bf16[2048,256]{1,0:T(8,128)(2,1)S(1)}, bf16[256,2048]{1,0:T(8,128)(2,1)S(1)}, bf16[64,256]{1,0:T(8,128)(2,1)S(1)}, bf16[256,64]{1,0:T(8,128)(2,1)S(1)}) custom-call(bf16[1024,256]{1,0:T(8,128)(2,1)S(1)} %get-tuple-element.69.k_ref, bf16[256,1024]{1,0:T(8,128)(2,1)S(1)} %get-tuple-element.70.vt_ref, ...), custom_call_target="tpu_custom_call" | custom-call | flops 1 | bytes 1 | tf_op jit(solution)/shard_map/window/pallas_call | solution.py:599
  65.4 3.6 %rest.2.refs_0_ = bf16[512,256]{1,0:T(8,128)(2,1)S(1)} custom-call(s32[4,8]{1,0:T(4,128)S(1)} %bitcast.1, f32[4,4]{1,0:T(4,128)S(1)} %copy-done.5, bf16[256,1024]{1,0:T(8,128)(2,1)S(1)} %get-tuple-element.68.qt_ref, bf16[2048,256]{1,0:T(8,128)(2,1)S(1)} %get-tuple-element.81.kw_ref, bf16[256,2048]{1,0:T(8,128)(2,1)S(1)} %get-tuple-element.82.vw_ref, ...), custom_call_target="tpu_custom_call" | custom-call | flops 1 | bytes 1 | tf_op jit(solution)/shard_map/rest/pallas_call | solution.py:640
  69.7 3.4 %rest.3.refs_0_ = bf16[512,256]{1,0:T(8,128)(2,1)S(1)} custom-call(s32[4,8]{1,0:T(4,128)S(1)} %bitcast.2, f32[4,4]{1,0:T(4,128)S(1)} %copy-done.5, bf16[256,1024]{1,0:T(8,128)(2,1)S(1)} %get-tuple-element.68.qt_ref, bf16[2048,256]{1,0:T(8,128)(2,1)S(1)} %get-tuple-element.81.kw_ref, bf16[256,2048]{1,0:T(8,128)(2,1)S(1)} %get-tuple-element.82.vw_ref, ...), custom_call_target="tpu_custom_call" | custom-call | flops 1 | bytes 1 | tf_op jit(solution)/shard_map/rest/pallas_call | solution.py:640
  73.1 2.6 %collective-permute-done.19.refs_1_ = bf16[512,256]{1,0:T(8,128)(2,1)S(1)} collective-permute-done((bf16[512,256]{1,0:T(8,128)(2,1)S(1)}, bf16[512,256]{1,0:T(8,128)(2,1)S(1)}, u32[]{:S(2)}, u32[]{:S(2)}) %collective-permute-start.19) | collective-permute-done | bytes 262176 | tf_op jit(solution)/shard_map/ppermute | solution.py:54
  76.4 0.8 collective-permute-done.22.refs_3_
  77.2 2.0 %output.2.refs_4_ = bf16[1024,256]{1,0:T(8,128)(2,1)} custom-call(bf16[1024,256]{1,0:T(8,128)(2,1)S(1)} %copy-done.1, bf16[512,256]{1,0:T(8,128)(2,1)S(1)} %rest.2.refs_0_, bf16[512,256]{1,0:T(8,128)(2,1)S(1)} %collective-permute-done.19.refs_1_, bf16[512,256]{1,0:T(8,128)(2,1)S(1)} %collective-permute-done.21.refs_2_, ...), custom_call_target="tpu_custom_call" | custom-call | flops 1 | bytes 1 | tf_op jit(solution)/shard_map/output/pallas_call | solution.py:625
  79.2 5.2 %collective-permute-done.20.refs_1_ = bf16[512,256]{1,0:T(8,128)(2,1)S(1)} collective-permute-done((bf16[512,256]{1,0:T(8,128)(2,1)S(1)}, bf16[512,256]{1,0:T(8,128)(2,1)S(1)}, u32[]{:S(2)}, u32[]{:S(2)}) %collective-permute-start.20) | collective-permute-done | bytes 262176 | tf_op jit(solution)/shard_map/ppermute | solution.py:54
  84.4 1.5 %collective-permute-done.24.refs_3_ = bf16[512,256]{1,0:T(8,128)(2,1)S(1)} collective-permute-done((bf16[512,256]{1,0:T(8,128)(2,1)S(1)}, bf16[512,256]{1,0:T(8,128)(2,1)S(1)}, u32[]{:S(2)}, u32[]{:S(2)}) %collective-permute-start.24) | collective-permute-done | bytes 262176 | tf_op jit(solution)/shard_map/ppermute | solution.py:54
  85.9 2.0 %output.3 = bf16[1024,256]{1,0:T(8,128)(2,1)} custom-call(bf16[1024,256]{1,0:T(8,128)(2,1)S(1)} %copy-done.1, bf16[512,256]{1,0:T(8,128)(2,1)S(1)} %rest.3.refs_0_, bf16[512,256]{1,0:T(8,128)(2,1)S(1)} %collective-permute-done.20.refs_1_, bf16[512,256]{1,0:T(8,128)(2,1)S(1)} %collective-permute-done.23.refs_2_, ...), custom_call_target="tpu_custom_call", output_to_operand_aliasing={{}: (5, {})} | custom-call | flops 1 | bytes 1 | tf_op jit(solution)/shard_map/output/pallas_call | solution.py:625
  (50 shorter events, 4.6 us)
Async XLA Ops:
  2.3 18.3 %copy-start.2 = (bf16[1024,256]{1,0:T(8,128)(2,1)S(1)}, bf16[1024,256]{1,0:T(8,128)(2,1)}, u32[]{:S(2)}) copy-start(bf16[1024,256]{1,0:T(8,128)(2,1)} %wq_ref.1) | copy-start | bytes 1572868
  2.3 18.3 %copy-start.3 = (bf16[1024,256]{1,0:T(8,128)(2,1)S(1)}, bf16[1024,256]{1,0:T(8,128)(2,1)}, u32[]{:S(2)}) copy-start(bf16[1024,256]{1,0:T(8,128)(2,1)} %wv_ref.1) | copy-start | bytes 1572868
  2.3 18.3 %copy-start.4 = (bf16[1024,256]{1,0:T(8,128)(2,1)S(1)}, bf16[1024,256]{1,0:T(8,128)(2,1)}, u32[]{:S(2)}) copy-start(bf16[1024,256]{1,0:T(8,128)(2,1)} %wk_in.1) | copy-start | bytes 1572868
  2.3 18.3 %copy-start.8 = (s32[1,1024]{1,0:T(1,128)S(1)}, s32[1,1024]{1,0:T(1,128)}, u32[]{:S(2)}) copy-start(s32[1,1024]{1,0:T(1,128)} %order_ref.1) | copy-start | bytes 12292
  2.4 20.7 %collective-permute-start.4 = (bf16[144,512]{1,0:T(8,128)(2,1)S(1)}, bf16[144,512]{1,0:T(8,128)(2,1)S(1)}, u32[]{:S(2)}, u32[]{:S(2)}) collective-permute-start(bf16[144,512]{1,0:T(8,128)(2,1)S(1)} %get-tuple-element.59), channel_id=1, source_target_pairs={{0,4},{4,0},{8,12},{12,8},{16,20},{20,16},{24,28},{28,24},{1,5},{5... | collective-permute-start | bytes 442376 | tf_op jit(solution)/shard_map/ppermute | solution.py:117
  5.4 7.7 %collective-permute-start = (bf16[160,256]{1,0:T(8,128)(2,1)S(1)}, bf16[160,256]{1,0:T(8,128)(2,1)S(1)}, u32[]{:S(2)}, u32[]{:S(2)}) collective-permute-start(bf16[160,256]{1,0:T(8,128)(2,1)S(1)} %get-tuple-element.49), channel_id=1, source_target_pairs={{0,28},{4,24},{8,20},{12,16},{16,12},{20,8},{24,4},{28,0},{1,29},{... | collective-permute-start | bytes 245768 | tf_op jit(solution)/shard_map/ppermute | solution.py:117
  9.0 9.8 %collective-permute-start.1 = (bf16[160,256]{1,0:T(8,128)(2,1)S(1)}, bf16[160,256]{1,0:T(8,128)(2,1)S(1)}, u32[]{:S(2)}, u32[]{:S(2)}) collective-permute-start(bf16[160,256]{1,0:T(8,128)(2,1)S(1)} %get-tuple-element.56), channel_id=1, source_target_pairs={{0,24},{4,28},{8,16},{12,20},{16,8},{20,12},{24,0},{28,4},{1,25},{... | collective-permute-start | bytes 245768 | tf_op jit(solution)/shard_map/ppermute | solution.py:117
  9.0 14.0 %collective-permute-start.2 = (bf16[160,256]{1,0:T(8,128)(2,1)S(1)}, bf16[160,256]{1,0:T(8,128)(2,1)S(1)}, u32[]{:S(2)}, u32[]{:S(2)}) collective-permute-start(bf16[160,256]{1,0:T(8,128)(2,1)S(1)} %get-tuple-element.57), channel_id=1, source_target_pairs={{0,20},{4,16},{8,28},{12,24},{16,4},{20,0},{24,12},{28,8},{1,21},{... | collective-permute-start | bytes 245768 | tf_op jit(solution)/shard_map/ppermute | solution.py:117
  10.9 12.1 %collective-permute-start.3 = (bf16[160,256]{1,0:T(8,128)(2,1)S(1)}, bf16[160,256]{1,0:T(8,128)(2,1)S(1)}, u32[]{:S(2)}, u32[]{:S(2)}) collective-permute-start(bf16[160,256]{1,0:T(8,128)(2,1)S(1)} %get-tuple-element.58), channel_id=1, source_target_pairs={{0,16},{4,20},{8,24},{12,28},{16,0},{20,4},{24,8},{28,12},{1,17},{... | collective-permute-start | bytes 245768 | tf_op jit(solution)/shard_map/ppermute | solution.py:117
  13.1 12.8 %collective-permute-start.6 = (bf16[144,512]{1,0:T(8,128)(2,1)S(1)}, bf16[144,512]{1,0:T(8,128)(2,1)S(1)}, u32[]{:S(2)}, u32[]{:S(2)}) collective-permute-start(bf16[144,512]{1,0:T(8,128)(2,1)S(1)} %get-tuple-element.60), channel_id=1, source_target_pairs={{0,12},{4,8},{8,4},{12,0},{16,28},{20,24},{24,20},{28,16},{1,13},{... | collective-permute-start | bytes 442376 | tf_op jit(solution)/shard_map/ppermute | solution.py:117
  18.8 7.7 %collective-permute-start.7 = (bf16[144,512]{1,0:T(8,128)(2,1)S(1)}, bf16[144,512]{1,0:T(8,128)(2,1)S(1)}, u32[]{:S(2)}, u32[]{:S(2)}) collective-permute-start(bf16[144,512]{1,0:T(8,128)(2,1)S(1)} %get-tuple-element.61), channel_id=1, source_target_pairs={{0,8},{4,12},{8,0},{12,4},{16,24},{20,28},{24,16},{28,20},{1,9},{5... | collective-permute-start | bytes 442376 | tf_op jit(solution)/shard_map/ppermute | solution.py:117
  23.1 7.1 %collective-permute-start.5 = (bf16[512,256]{1,0:T(8,128)(2,1)S(1)}, bf16[512,256]{1,0:T(8,128)(2,1)S(1)}, u32[]{:S(2)}, u32[]{:S(2)}) collective-permute-start(bf16[512,256]{1,0:T(8,128)(2,1)S(1)} %stack.3.refs_0_), channel_id=1, source_target_pairs={{0,2},{2,0},{1,3},{3,1},{4,6},{6,4},{5,7},{7,5},{8,10},{10,8},{9,1... | collective-permute-start | bytes 786440 | tf_op jit(solution)/shard_map/ppermute | solution.py:54
  26.5 7.3 %collective-permute-start.10 = (bf16[384,512]{1,0:T(8,128)(2,1)S(1)}, bf16[384,512]{1,0:T(8,128)(2,1)S(1)}, u32[]{:S(2)}, u32[]{:S(2)}) collective-permute-start(bf16[384,512]{1,0:T(8,128)(2,1)S(1)} %stack.4.refs_1_.refs_4_), channel_id=1, source_target_pairs={{0,1},{1,0},{2,3},{3,2},{4,5},{5,4},{6,7},{7,6},{8,9},{9,8},{10,11... | collective-permute-start | bytes 1179656 | tf_op jit(solution)/shard_map/ppermute | solution.py:54
  26.6 7.2 %collective-permute-start.8 = (bf16[512,256]{1,0:T(8,128)(2,1)S(1)}, bf16[512,256]{1,0:T(8,128)(2,1)S(1)}, u32[]{:S(2)}, u32[]{:S(2)}) collective-permute-start(bf16[512,256]{1,0:T(8,128)(2,1)S(1)} %stack.3.refs_0_), channel_id=1, source_target_pairs={{0,1},{1,0},{2,3},{3,2},{4,5},{5,4},{6,7},{7,6},{8,9},{9,8},{10,11... | collective-permute-start | bytes 786440 | tf_op jit(solution)/shard_map/ppermute | solution.py:54
  30.2 3.6 %collective-permute-start.9 = (bf16[512,256]{1,0:T(8,128)(2,1)S(1)}, bf16[512,256]{1,0:T(8,128)(2,1)S(1)}, u32[]{:S(2)}, u32[]{:S(2)}) collective-permute-start(bf16[512,256]{1,0:T(8,128)(2,1)S(1)} %collective-permute-done.5.refs_1_), channel_id=1, source_target_pairs={{0,1},{1,0},{2,3},{3,2},{4,5},{5,4},{6,7},{7,6},{8,9},{9,8},{10,11... | collective-permute-start | bytes 786440 | tf_op jit(solution)/shard_map/ppermute | solution.py:54
  30.2 9.6 %collective-permute-start.11 = (bf16[512,256]{1,0:T(8,128)(2,1)S(1)}, bf16[512,256]{1,0:T(8,128)(2,1)S(1)}, u32[]{:S(2)}, u32[]{:S(2)}) collective-permute-start(bf16[512,256]{1,0:T(8,128)(2,1)S(1)} %pack.1), channel_id=1, source_target_pairs={{0,4},{4,8},{8,12},{12,16},{16,20},{20,24},{24,28},{1,5},{5,9},{9,... | collective-permute-start | bytes 786440 | tf_op jit(solution)/shard_map/ppermute | solution.py:58
  39.8 9.0 %collective-permute-start.12 = (bf16[512,256]{1,0:T(8,128)(2,1)S(1)}, bf16[512,256]{1,0:T(8,128)(2,1)S(1)}, u32[]{:S(2)}, u32[]{:S(2)}) collective-permute-start(bf16[512,256]{1,0:T(8,128)(2,1)S(1)} %collective-permute-done.11.refs_0_), channel_id=1, source_target_pairs={{0,2},{2,0},{1,3},{3,1},{4,6},{6,4},{5,7},{7,5},{8,10},{10,8},{9,1... | collective-permute-start | bytes 786440 | tf_op jit(solution)/shard_map/ppermute | solution.py:54
  41.3 22.0 %collective-permute-start.13 = (bf16[512,256]{1,0:T(8,128)(2,1)S(1)}, bf16[512,256]{1,0:T(8,128)(2,1)S(1)}, u32[]{:S(2)}, u32[]{:S(2)}) collective-permute-start(bf16[512,256]{1,0:T(8,128)(2,1)S(1)} %collective-permute-done.11.refs_0_), channel_id=1, source_target_pairs={{0,1},{1,0},{2,3},{3,2},{4,5},{5,4},{6,7},{7,6},{8,9},{9,8},{10,11... | collective-permute-start | bytes 786440 | tf_op jit(solution)/shard_map/ppermute | solution.py:54
  41.3 2.6 %copy-start.5 = (f32[4,4]{1,0:T(4,128)S(1)}, f32[4,4]{1,0:T(4,128)}, u32[]{:S(2)}) copy-start(f32[4,4]{1,0:T(4,128)} %mix_ref.5) | copy-start | bytes 196
  48.8 14.4 %collective-permute-start.14 = (bf16[512,256]{1,0:T(8,128)(2,1)S(1)}, bf16[512,256]{1,0:T(8,128)(2,1)S(1)}, u32[]{:S(2)}, u32[]{:S(2)}) collective-permute-start(bf16[512,256]{1,0:T(8,128)(2,1)S(1)} %collective-permute-done.12.refs_1_), channel_id=1, source_target_pairs={{0,1},{1,0},{2,3},{3,2},{4,5},{5,4},{6,7},{7,6},{8,9},{9,8},{10,11... | collective-permute-start | bytes 786440 | tf_op jit(solution)/shard_map/ppermute | solution.py:54
  49.4 4.4 %collective-permute-start.15 = (bf16[64,256]{1,0:T(8,128)(2,1)S(1)}, bf16[64,256]{1,0:T(8,128)(2,1)S(1)}, u32[]{:S(2)}, u32[]{:S(2)}) collective-permute-start(bf16[64,256]{1,0:T(8,128)(2,1)S(1)} %get-tuple-element.80.refs_0_), channel_id=1, source_target_pairs={{0,4},{4,0},{8,12},{12,8},{16,20},{20,16},{24,28},{28,24},{1,5},{5... | collective-permute-start | bytes 98312 | tf_op jit(solution)/shard_map/ppermute | solution.py:117
  53.8 6.6 %collective-permute-start.18 = (bf16[128,256]{1,0:T(8,128)(2,1)S(1)}, bf16[128,256]{1,0:T(8,128)(2,1)S(1)}, u32[]{:S(2)}, u32[]{:S(2)}) collective-permute-start(bf16[128,256]{1,0:T(8,128)(2,1)S(1)} %stack.5.refs_4_), channel_id=1, source_target_pairs={{0,24},{4,28},{8,16},{12,20},{16,8},{20,12},{24,0},{28,4},{1,25},{... | collective-permute-start | bytes 196616 | tf_op jit(solution)/shard_map/ppermute | solution.py:117
  57.6 5.6 %collective-permute-start.17 = (bf16[128,256]{1,0:T(8,128)(2,1)S(1)}, bf16[128,256]{1,0:T(8,128)(2,1)S(1)}, u32[]{:S(2)}, u32[]{:S(2)}) collective-permute-start(bf16[128,256]{1,0:T(8,128)(2,1)S(1)} %stack.5.refs_4_), channel_id=1, source_target_pairs={{0,16},{4,20},{8,24},{12,28},{16,0},{20,4},{24,8},{28,12},{1,17},{... | collective-permute-start | bytes 196616 | tf_op jit(solution)/shard_map/ppermute | solution.py:117
  57.6 5.6 %collective-permute-start.16 = (bf16[128,256]{1,0:T(8,128)(2,1)S(1)}, bf16[128,256]{1,0:T(8,128)(2,1)S(1)}, u32[]{:S(2)}, u32[]{:S(2)}) collective-permute-start(bf16[128,256]{1,0:T(8,128)(2,1)S(1)} %stack.5.refs_4_), channel_id=1, source_target_pairs={{0,8},{4,12},{8,0},{12,4},{16,24},{20,28},{24,16},{28,20},{1,9},{5... | collective-permute-start | bytes 196616 | tf_op jit(solution)/shard_map/ppermute | solution.py:117
  63.3 2.2 %copy-start.7 = (s32[8,4]{0,1:T(4,128)S(1)}, s32[8,4]{0,1:T(4,128)}, u32[]{:S(2)}) copy-start(s32[8,4]{0,1:T(4,128)} %param.15) | copy-start | bytes 388
  69.0 8.2 %copy-start.1 = (bf16[1024,256]{1,0:T(8,128)(2,1)S(1)}, bf16[1024,256]{1,0:T(8,128)(2,1)}, u32[]{:S(2)}) copy-start(bf16[1024,256]{1,0:T(8,128)(2,1)} %w_ref.3) | copy-start | bytes 1572868
  69.1 6.6 %collective-permute-start.19 = (bf16[512,256]{1,0:T(8,128)(2,1)S(1)}, bf16[512,256]{1,0:T(8,128)(2,1)S(1)}, u32[]{:S(2)}, u32[]{:S(2)}) collective-permute-start(bf16[512,256]{1,0:T(8,128)(2,1)S(1)} %rest.2.refs_0_), channel_id=1, source_target_pairs={{0,2},{2,0},{1,3},{3,1},{4,6},{6,4},{5,7},{7,5},{8,10},{10,8},{9,1... | collective-permute-start | bytes 786440 | tf_op jit(solution)/shard_map/ppermute | solution.py:54
  73.0 3.4 %collective-permute-start.21 = (bf16[512,256]{1,0:T(8,128)(2,1)S(1)}, bf16[512,256]{1,0:T(8,128)(2,1)S(1)}, u32[]{:S(2)}, u32[]{:S(2)}) collective-permute-start(bf16[512,256]{1,0:T(8,128)(2,1)S(1)} %rest.2.refs_0_), channel_id=1, source_target_pairs={{0,1},{1,0},{2,3},{3,2},{4,5},{5,4},{6,7},{7,6},{8,9},{9,8},{10,11... | collective-permute-start | bytes 786440 | tf_op jit(solution)/shard_map/ppermute | solution.py:54
  75.7 1.5 %collective-permute-start.22 = (bf16[512,256]{1,0:T(8,128)(2,1)S(1)}, bf16[512,256]{1,0:T(8,128)(2,1)S(1)}, u32[]{:S(2)}, u32[]{:S(2)}) collective-permute-start(bf16[512,256]{1,0:T(8,128)(2,1)S(1)} %collective-permute-done.19.refs_1_), channel_id=1, source_target_pairs={{0,1},{1,0},{2,3},{3,2},{4,5},{5,4},{6,7},{7,6},{8,9},{9,8},{10,11... | collective-permute-start | bytes 786440 | tf_op jit(solution)/shard_map/ppermute | solution.py:54
  75.7 8.7 %collective-permute-start.20 = (bf16[512,256]{1,0:T(8,128)(2,1)S(1)}, bf16[512,256]{1,0:T(8,128)(2,1)S(1)}, u32[]{:S(2)}, u32[]{:S(2)}) collective-permute-start(bf16[512,256]{1,0:T(8,128)(2,1)S(1)} %rest.3.refs_0_), channel_id=1, source_target_pairs={{0,2},{2,0},{1,3},{3,1},{4,6},{6,4},{5,7},{7,5},{8,10},{10,8},{9,1... | collective-permute-start | bytes 786440 | tf_op jit(solution)/shard_map/ppermute | solution.py:54
  76.2 8.2 %collective-permute-start.23 = (bf16[512,256]{1,0:T(8,128)(2,1)S(1)}, bf16[512,256]{1,0:T(8,128)(2,1)S(1)}, u32[]{:S(2)}, u32[]{:S(2)}) collective-permute-start(bf16[512,256]{1,0:T(8,128)(2,1)S(1)} %rest.3.refs_0_), channel_id=1, source_target_pairs={{0,1},{1,0},{2,3},{3,2},{4,5},{5,4},{6,7},{7,6},{8,9},{9,8},{10,11... | collective-permute-start | bytes 786440 | tf_op jit(solution)/shard_map/ppermute | solution.py:54
  84.4 1.5 %collective-permute-start.24 = (bf16[512,256]{1,0:T(8,128)(2,1)S(1)}, bf16[512,256]{1,0:T(8,128)(2,1)S(1)}, u32[]{:S(2)}, u32[]{:S(2)}) collective-permute-start(bf16[512,256]{1,0:T(8,128)(2,1)S(1)} %collective-permute-done.20.refs_1_), channel_id=1, source_target_pairs={{0,1},{1,0},{2,3},{3,2},{4,5},{5,4},{6,7},{7,6},{8,9},{9,8},{10,11... | collective-permute-start | bytes 786440 | tf_op jit(solution)/shard_map/ppermute | solution.py:54
  (2 other events, 2.3 us)

commit v8 on v6

--- a/solution.py
+++ b/solution.py
@@ -19,7 +19,8 @@
 I32 = jnp.int32
 HIDE = -1e30
 VMEM_LIMIT = 24 * 1024 * 1024
-PARTS = (2, 3, 3)
+COST = pl.CostEstimate(flops=1, bytes_accessed=1, transcendentals=0)
+PARTS = (4, 4)
 
 X_PAIRS = [(0, 2), (2, 0), (1, 3), (3, 1)]
 CORE_PAIRS = [(0, 1), (1, 0), (2, 3), (3, 2)]
@@ -57,42 +58,40 @@
     return lax.ppermute(block, "seq", [(i, i + 1) for i in range(lax.axis_size("seq") - 1)])
 
 
-def send_kernel(distances, tokens_ref, mask_ref, *refs):
+def send_kernel(tokens_ref, mask_ref, *refs):
     outs, own = refs[:-1], refs[-1]
     slab, head = lax.axis_index("seq"), lax.axis_index("head")
-    rows = own.shape[0]
-    quarter = tokens_ref.shape[1] // 4
+    core = head & 1
+    rows, width = own.shape
+    half = width // 2
     ids = mask_ref[...]
     line = iota((CODE_ROWS, ids.shape[1]), 0)
     code = jnp.where(line == 0, ids >> 5, jnp.where(line == 1, ids & 31, 0)).astype(F32).astype(BF)
-    for distance, out in zip(distances, outs):
+    sides = (head >> 1, head >> 1, None, core)
+    for distance, side, out in zip((7 - core, 5 - core, 3 - core, 1), sides, outs):
         row = pl.multiple_of((slab ^ distance) * rows, rows)
-        parts = out.shape[1] // quarter
-        for part in range(parts):
-            start = pl.multiple_of((head ^ (2 * part)) * quarter, quarter)
-            out[:rows, part * quarter : (part + 1) * quarter] = tokens_ref[
-                pl.ds(row, rows), pl.ds(start, quarter)
-            ]
-        for part in range(code.shape[1] // out.shape[1]):
-            at = rows + part * CODE_ROWS
-            out[at : at + CODE_ROWS] = code[:, part * out.shape[1] : (part + 1) * out.shape[1]]
+        start = 0 if side is None else pl.multiple_of(side * half, half)
+        out[:rows] = tokens_ref[pl.ds(row, rows), pl.ds(start, out.shape[1])]
+        out[rows:, : code.shape[1]] = code
     own[...] = tokens_ref[pl.ds(pl.multiple_of(slab * rows, rows), rows)]
 
 
-def stack_kernel(count, *refs):
+def stack_kernel(places, *refs):
     target = refs[-1]
-    height = target.shape[0] // count
-    for index in range(count):
-        target[index * height : (index + 1) * height] = refs[index][:height]
-
-
-def stacked(parts, rows, after=()):
+    at = 0
+    for source, row, height, column in places:
+        target[at : at + height] = refs[source][row : row + height, column : column + target.shape[1]]
+        at += height
+
+
+def stacked(parts, places, width, after=()):
     return pl.pallas_call(
-        functools.partial(stack_kernel, len(parts)),
-        out_shape=jax.ShapeDtypeStruct((len(parts) * rows, parts[0].shape[1]), parts[0].dtype),
+        functools.partial(stack_kernel, places),
+        out_shape=jax.ShapeDtypeStruct((sum(place[2] for place in places), width), BF),
         in_specs=vmem_specs(len(parts)) + [pl.BlockSpec(memory_space=pl.ANY)] * len(after),
         out_specs=pl.BlockSpec(memory_space=pltpu.VMEM),
         compiler_params=pltpu.CompilerParams(vmem_limit_bytes=VMEM_LIMIT),
+        cost_estimate=COST,
         name="stack",
     )(*parts, *after)
 
@@ -101,12 +100,22 @@
     return lax.ppermute(block, "seq", [(i, i ^ distance) for i in range(lax.axis_size("seq"))])
 
 
-def exchange_tokens(tokens, mask_ids, prepare):
+def by_core(block, distances):
+    heads = lax.axis_size("head")
+    pairs = [
+        (slab * heads + head, (slab ^ distances[head & 1]) * heads + head)
+        for slab in range(lax.axis_size("seq"))
+        for head in range(heads)
+    ]
+    return lax.ppermute(block, ("seq", "head"), pairs)
+
+
+def exchange_tokens(tokens, mask_ids, prepare, expand):
     tok_rows, width = tokens.shape
     slabs = lax.axis_size("seq")
     rows = tok_rows // slabs
-    quarter = width // 4
     if slabs != 8:
+        quarter = width // 4
         split = tokens.reshape(slabs, rows, width)
         mine = lax.dynamic_slice_in_dim(split, lax.axis_index("head") * quarter, quarter, axis=2)
         first = lax.all_to_all(mine, "seq", split_axis=0, concat_axis=0, tiled=True).reshape(
@@ -115,34 +124,47 @@
         third = over_head(first, X_PAIRS)
         second = over_head(first, CORE_PAIRS)
         fourth = over_head(third, CORE_PAIRS)
-        pieces = [(first, 0, (0,)), (third, 0, (2,)), (second, 0, (1,)), (fourth, 0, (3,))]
-        return pieces, prepare(first), [to_next(mask_ids)]
-    distances = (7, 6, 5, 4, 3, 2, 1)
-    near_rows, far_rows = rows + CODE_ROWS, rows + 2 * CODE_ROWS
+        prepared = prepare(first)
+        return [first, third, second, fourth], prepared, expand(prepared, [to_next(mask_ids)])
+    half = width // 2
+    tall = rows + CODE_ROWS
     *blocks, own = pl.pallas_call(
-        functools.partial(send_kernel, distances),
-        out_shape=tuple(
-            jax.ShapeDtypeStruct((far_rows, quarter) if d > 3 else (near_rows, 2 * quarter), BF)
-            for d in distances
-        )
-        + (jax.ShapeDtypeStruct((rows, width), BF),),
+        send_kernel,
+        out_shape=(
+            jax.ShapeDtypeStruct((tall, half), BF),
+            jax.ShapeDtypeStruct((tall, half), BF),
+            jax.ShapeDtypeStruct((tall, width), BF),
+            jax.ShapeDtypeStruct((tall, half), BF),
+            jax.ShapeDtypeStruct((rows, width), BF),
+        ),
         in_specs=vmem_specs(2),
-        out_specs=vmem_specs(8),
-        compiler_params=pltpu.CompilerParams(vmem_limit_bytes=VMEM_LIMIT),
+        out_specs=vmem_specs(5),
+        compiler_params=pltpu.CompilerParams(vmem_limit_bytes=60 * 1024 * 1024),
+        cost_estimate=COST,
         name="send",
     )(tokens, mask_ids)
-    arrived = [by_distance(block, d) for block, d in zip(blocks, distances)]
-    far = stacked(arrived[:4], rows, (arrived[5],))
-    near = stacked(arrived[4:], rows)
+    routes = ((7, 6), (5, 4), (3, 2), (1, 1))
+    one, two, three, four = [by_core(block, route) for block, route in zip(blocks, routes)]
+    far = stacked((one, two), ((0, 0, rows, 0), (1, 0, rows, 0), (0, rows, CODE_ROWS, 0)), half, (four,))
+    near = stacked(
+        (three, four),
+        (
+            (0, 0, rows, 0),
+            (0, 0, rows, half),
+            (1, 0, rows, 0),
+            (0, rows, CODE_ROWS, 0),
+            (1, rows, CODE_ROWS, 0),
+        ),
+        half,
+    )
     far_x = over_head(far, X_PAIRS)
     near_core = over_head(near, CORE_PAIRS)
     far_core = over_head(far, CORE_PAIRS)
     prepared = prepare(far)
-    far_x, prepared = lax.optimization_barrier((far_x, prepared))
+    expanded = expand(prepared, [far, far_core, near, near_core])
+    far_x, _, _ = lax.optimization_barrier((far_x, prepared, expanded))
     far_last = over_head(far_x, CORE_PAIRS)
-    pieces = [(far, 0, (0,)), (far_x, 0, (2,)), (far_core, 0, (1,)), (far_last, 0, (3,))]
-    pieces += [(near, 4 * rows, (0, 2)), (near_core, 4 * rows, (1, 3)), (own, 7 * rows, None)]
-    return pieces, prepared, [arrived[6], arrived[4], arrived[0]]
+    return [far, far_x, far_core, far_last, near, near_core, own], prepared, expanded
 
 
 def column(row, lanes=128):
@@ -210,22 +232,68 @@
     wk_ref[...] = wk_in[...]
 
 
-def project_kernel(places, *refs):
-    count = len(places)
+def mask_before(refs, rows):
+    if len(refs) == 1:
+        return refs[0][...]
+    far, far_core, near, near_core = refs
+    core = lax.axis_index("head") & 1
+
+    def digits(ref, row):
+        return ref[row : row + CODE_ROWS].astype(F32)
+
+    by_one = digits(near, 3 * rows + CODE_ROWS)
+    by_three = jnp.where(core == 0, digits(near, 3 * rows), digits(near_core, 3 * rows))
+    by_seven = jnp.where(core == 0, digits(far, 2 * rows), digits(far_core, 2 * rows))
+    slab = lax.axis_index("seq")
+    distance = slab ^ (slab - 1)
+    code = jnp.where(distance == 1, by_one, jnp.where(distance == 3, by_three, by_seven)).astype(I32)
+    return (code[0:1] << 5) + code[1:2]
+
+
+def expand_kernel(rows, seen_ref, *refs):
+    code_refs, (e_ref, et_ref, bias_ref) = refs[:-3], refs[-3:]
+    tok_rows = seen_ref.shape[0]
+    rank = ranks(mask_before(code_refs, rows), tok_rows)
+    rank = jnp.where(lax.axis_index("seq") > 0, rank, -1)
+    rank_column = column(rank)
+    bias_ref[:tok_rows] = jnp.where(rank_column >= 0, 0.0, HIDE)
+    bias_ref[tok_rows:] = seen_ref[...]
+    for at in range(0, et_ref.shape[0], FBLK):
+        e_ref[:, at : at + FBLK] = ones_where(rank_column == iota((tok_rows, FBLK), 1) + at)
+        et_ref[at : at + FBLK] = ones_where(iota((FBLK, tok_rows), 0) + at == rank)
+
+
+def assemble(piece_refs, x_ref):
+    head = lax.axis_index("head")
+    tok_rows, width = x_ref.shape
+    if len(piece_refs) == 4:
+        quarter = width // 4
+        for distance, piece in zip((0, 2, 1, 3), piece_refs):
+            start = pl.multiple_of((head ^ distance) * quarter, quarter)
+            x_ref[:, pl.ds(start, quarter)] = piece[...]
+        return
+    far, far_x, far_core, far_last, near, near_core, own = piece_refs
+    rows, half = own.shape[0], width // 2
+    core, side = head & 1, head >> 1
+    for holder, pieces in ((core, (far, far_x)), (1 - core, (far_core, far_last))):
+        for part in range(2):
+            row = pl.multiple_of((2 * part + holder) * rows, rows)
+            for turn, piece in enumerate(pieces):
+                start = pl.multiple_of((side ^ turn) * half, half)
+                x_ref[pl.ds(row, rows), pl.ds(start, half)] = piece[part * rows : (part + 1) * rows]
+    for holder, piece in ((core, near), (1 - core, near_core)):
+        row = pl.multiple_of((4 + holder) * rows, rows)
+        x_ref[pl.ds(row, rows), :half] = piece[:rows]
+        x_ref[pl.ds(row, rows), half:] = piece[rows : 2 * rows]
+        start = pl.multiple_of(holder * half, half)
+        x_ref[6 * rows : 7 * rows, pl.ds(start, half)] = piece[2 * rows : 3 * rows]
+    x_ref[7 * rows :] = own[...]
+
+
+def project_kernel(count, *refs):
     piece_refs, refs = refs[:count], refs[count:]
     wt_ref, wk_ref, sel_ref, fcol_ref, comp_ref, summ_ref, k_ref, v_ref, x_ref = refs
-    quarter = x_ref.shape[1] // 4
-    head = lax.axis_index("head")
-    for piece, (row, distances) in zip(piece_refs, places):
-        height = piece.shape[0]
-        if distances is None:
-            x_ref[row : row + height] = piece[...]
-            continue
-        for part, distance in enumerate(distances):
-            start = pl.multiple_of((head ^ distance) * quarter, quarter)
-            x_ref[row : row + height, pl.ds(start, quarter)] = piece[
-                :, part * quarter : (part + 1) * quarter
-            ]
+    assemble(piece_refs, x_ref)
     group = wk_ref.shape[1]
     packed = comp_ref.shape[0] // 2
     lead = packed + SUMM_ROWS
@@ -276,43 +344,16 @@
     nvt_ref[...] = (nt(v0, pool) * frow_ref[:1, SUMM_ROWS:]).astype(BF)
 
 
-def mask_before(refs, rows):
-    if len(refs) == 1:
-        return refs[0][...]
-    slab = lax.axis_index("seq")
-    digits = []
-    for block in refs:
-        width = block.shape[1]
-        parts = [
-            block[rows + at : rows + at + CODE_ROWS].astype(F32)
-            for at in range(0, block.shape[0] - rows, CODE_ROWS)
-        ]
-        digits.append(jnp.concatenate(parts, axis=1) if len(parts) > 1 else parts[0])
-    distance = slab ^ (slab - 1)
-    code = jnp.where(distance == 1, digits[0], jnp.where(distance == 3, digits[1], digits[2]))
-    code = code.astype(I32)
-    return (code[0:1] << 5) + code[1:2]
-
-
 def own_kernel(
-    rows, codes, mix_ref, qt_ref, k_ref, vt_ref, nk_ref, nvt_ref, seen_ref, *refs,
+    mix_ref, qt_ref, k_ref, vt_ref, nk_ref, nvt_ref, seen_ref, column_ref,
+    acc_ref, near_ref, top_ref, den_ref, q4_ref, p_ref,
 ):
-    code_refs = refs[:codes]
-    acc_ref, near_ref, top_ref, den_ref, e_ref, et_ref, bias_ref, q4_ref, p_ref = refs[codes:]
     tok_rows, group = k_ref.shape
     heads = mix_ref.shape[1]
     width = group // heads
     q4_ref[...] = jnp.zeros_like(q4_ref)
     same = iota((FBLK, FBLK), 0) == iota((FBLK, FBLK), 1)
     nk, nvt = nk_ref[...], nvt_ref[...]
-    rank = ranks(mask_before(code_refs, rows), tok_rows)
-    rank = jnp.where(lax.axis_index("seq") > 0, rank, -1)
-    rank_column = column(rank)
-    bias_ref[:tok_rows] = jnp.where(rank_column >= 0, 0.0, HIDE)
-    bias_ref[tok_rows:] = seen_ref[...]
-    for at in range(0, et_ref.shape[0], FBLK):
-        e_ref[:, at : at + FBLK] = ones_where(rank_column == iota((tok_rows, FBLK), 1) + at)
-        et_ref[at : at + FBLK] = ones_where(iota((FBLK, tok_rows), 0) + at == rank)
     for g in range(tok_rows // FBLK):
         at = g * FBLK
         slot = g % 2
@@ -370,11 +411,9 @@
     far = line - 3 * mids
     shard = slab - 1 + turn
     turned = slab if slabs == 8 else 0
-    source = jnp.where(
-        line < 3 * mids,
-        (shard ^ turned) * step + line - turn * mids,
-        ((far // fars) ^ turned) * step + mids + far % fars,
-    )
+    distance = jnp.where(line < 3 * mids, shard, far // fars) ^ turned
+    slot = (distance >> 1) + (distance & 1) * (slabs // 2) if slabs == 8 else distance
+    source = slot * step + jnp.where(line < 3 * mids, line - turn * mids, mids + far % fars)
     source = jnp.where((line >= 3 * mids) | ((shard >= 0) & (shard < slabs)), source, -step)
     gathered = all_ref[...]
     ck_ref[...] = nn(ones_where(source == iota(shape, 1)), gathered).astype(BF)
@@ -491,14 +530,30 @@
             in_specs=vmem_specs(5) + [pl.BlockSpec(memory_space=pl.ANY)],
             out_specs=vmem_specs(8),
             compiler_params=params,
+            cost_estimate=COST,
             name="prepare",
         )(order, mask_ids, w_query, w_value, w_key, early)
 
-    pieces, prepared, before = exchange_tokens(tokens, mask_ids, prepare)
+    def expand(prepared, sources):
+        return pl.pallas_call(
+            functools.partial(expand_kernel, tok_rows // slabs),
+            out_shape=(
+                shape((tok_rows, packed), BF),
+                shape((packed, tok_rows), BF),
+                shape((2 * tok_rows, FBLK), F32),
+            ),
+            in_specs=vmem_specs(1 + len(sources)),
+            out_specs=vmem_specs(3),
+            compiler_params=params,
+            cost_estimate=COST,
+            name="expand",
+        )(prepared[5], *sources)
+
+    pieces, prepared, expanded = exchange_tokens(tokens, mask_ids, prepare, expand)
     permute, permute_t, select, f_col, f_row, seen, w_t, w_k = prepared
-    places = tuple((row, distances) for _, row, distances in pieces)
+    spread, spread_t, bias = expanded
     comp, summ, k0, v0, rows_here = pl.pallas_call(
-        functools.partial(project_kernel, places),
+        functools.partial(project_kernel, len(pieces)),
         out_shape=(
             shape((2 * packed, group), BF),
             shape((step, group), BF),
@@ -509,10 +564,11 @@
         in_specs=vmem_specs(len(pieces) + 4),
         out_specs=vmem_specs(5),
         compiler_params=params,
+        cost_estimate=COST,
         name="project",
-    )(*[piece for piece, _, _ in pieces], w_t, w_k, select, f_col)
+    )(*pieces, w_t, w_k, select, f_col)
     if slabs == 8:
-        other = by_distance(summ, 1)
+        lined = [summ] + [by_distance(summ, d) for d in (2, 4, 6)]
     comp_before = to_next(comp)
 
     q_t, v_t, keys, near_k, near_vt = pl.pallas_call(
@@ -527,37 +583,37 @@
         in_specs=vmem_specs(9),
         out_specs=vmem_specs(5),
         compiler_params=params,
+        cost_estimate=COST,
         name="order",
     )(permute, permute_t, select, f_col, f_row, w_t, rows_here, k0, v0)
     if slabs == 8:
-        pair = stacked((summ, other), step, (near_k,))
-        summaries = [pair] + [by_distance(pair, d) for d in (2, 4, 6)]
+        places = tuple((index, 0, step, 0) for index in range(4))
+        column = stacked(lined, places, group, (near_k,))
+        summaries = [column, by_distance(column, 1)]
     else:
         copies = jnp.broadcast_to(summ[None], (slabs, step, group))
         copies = lax.all_to_all(copies, "seq", split_axis=0, concat_axis=0, tiled=True)
         summaries = [copies.reshape(slabs * step, group)]
 
     blocks = tok_rows // FBLK
-    acc, near_out, top, den, expand, expand_t, bias = pl.pallas_call(
-        functools.partial(own_kernel, tok_rows // slabs, len(before)),
+    acc, near_out, top, den = pl.pallas_call(
+        own_kernel,
         out_shape=(
             shape((group, tok_rows), F32),
             shape((group, tok_rows), F32),
             shape((blocks, heads * FBLK), F32),
             shape((blocks, heads * FBLK), F32),
-            shape((tok_rows, packed), BF),
-            shape((packed, tok_rows), BF),
-            shape((2 * tok_rows, FBLK), F32),
         ),
-        in_specs=smem_specs(1) + vmem_specs(6 + len(before)),
-        out_specs=vmem_specs(7),
+        in_specs=smem_specs(1) + vmem_specs(6) + [pl.BlockSpec(memory_space=pl.ANY)],
+        out_specs=vmem_specs(4),
         scratch_shapes=[
             pltpu.VMEM((2, group, heads * FBLK), BF),
             pltpu.VMEM((2, FBLK + near, heads * FBLK), BF),
         ],
         compiler_params=params,
+        cost_estimate=COST,
         name="own",
-    )(level_mix, q_t, keys, v_t, near_k, near_vt, seen, *before)
+    )(level_mix, q_t, keys, v_t, near_k, near_vt, seen, summaries[0])
 
     window_k, window_v, coarse_k, coarse_v = pl.pallas_call(
         window_kernel,
@@ -571,8 +627,9 @@
         out_specs=vmem_specs(4),
         scratch_shapes=[pltpu.VMEM((slabs * step, group), BF)],
         compiler_params=params,
+        cost_estimate=COST,
         name="window",
-    )(keys, v_t, comp_before, expand, expand_t, *summaries)
+    )(keys, v_t, comp_before, spread, spread_t, *summaries)
 
     total = (FINE_K - 1) * FBLK + coarse
     lists = fine_blocks.T
@@ -594,6 +651,7 @@
             out_specs=pl.BlockSpec((FBLK, group), lambda i, base=base: (i + base, 0)),
             input_output_aliases={5: 0} if previous else {},
             compiler_params=params,
+            cost_estimate=COST,
             name="output",
         )(w_out, attended, third, second, fourth, *previous)
 
@@ -610,6 +668,7 @@
                 pltpu.VMEM((2, total, heads * FBLK), BF),
             ],
             compiler_params=params,
+            cost_estimate=COST,
             name="rest",
         )(
             lists, level_mix, q_t, window_k, window_v, coarse_k, coarse_v, bias, acc, near_out, top, den
@@ -620,6 +679,7 @@
             old, old_third, old_second, old_base = waiting
             old_third, attended = lax.optimization_barrier((old_third, attended))
             out = finish(out, old, old_third, old_second, old_base)
+            third, out = lax.optimization_barrier((third, out))
         waiting = (attended, third, second, first)
         first += count
     return finish(out, *waiting)

time: 83.4 us -> 81.2 us (0.974)
  starting transfers between devices: 31.4 us -> 26.7 us
  waiting for transfers between devices: 23.6 us -> 27.2 us
  local copies, waits for them, and re-layouts: 2.31 us -> 0.04 us
  Pallas kernels: 25.7 us -> 26.8 us
    ppermute x11 -> x4, waiting for transfers between devices: 14.6 us -> 0.38 us  [by_distance(): lax.ppermute(block, 'seq', [(i, i ^ distance) for i in range(lax.axis_siz...]
    ppermute x0 -> x4, waiting for transfers between devices: none -> 12.6 us  [by_core(): return lax.ppermute(block, ('seq', 'head'), pairs)]
    ppermute x11 -> x4, starting transfers between devices: 20.9 us -> 10.7 us  [by_distance(): lax.ppermute(block, 'seq', [(i, i ^ distance) for i in range(lax.axis_siz...]
    ppermute x0 -> x4, starting transfers between devices: none -> 8.05 us  [by_core(): return lax.ppermute(block, ('seq', 'head'), pairs)]
    ppermute x13 -> x10, waiting for transfers between devices: 8.95 us -> 14.2 us  [over_head(): return lax.ppermute(block, 'head', pairs)]
    pallas_call x6 -> x7, Pallas kernels: 7.32 us -> 10 us  [the longest x1 3.94 us: local(): pl.pallas_call(own_kernel, out_shape=(shape((group, tok_rows), F32), shap...]
    unnamed x20 -> x18, local copies, waits for them, and re-layouts: 2.31 us -> 0.04 us
    ppermute x13 -> x10, starting transfers between devices: 6.92 us -> 5.06 us  [over_head(): return lax.ppermute(block, 'head', pairs)]
  transfers between devices with their start and end apart: 25 -> 19, of which waited for: 10 -> 10; matrix products, arithmetic and copies ran while one was open for 0% -> 0% of each run, Pallas kernels for 22% -> 19%
where the time goes in v8:
time: 81.2 us; the launch traced here: 81 us
  waiting for transfers between devices  27.2 us (33%)
  Pallas kernels  26.8 us (33%)
  starting transfers between devices  26.7 us (33%)
    ppermute x10, waiting for transfers between devices, over_head(): return lax.ppermute(block, 'head', pairs)  14.2 us
    ppermute x4, waiting for transfers between devices, by_core(): return lax.ppermute(block, ('seq', 'head'), pairs)  12.6 us
    ppermute x4, starting transfers between devices, by_distance(): lax.ppermute(block, 'seq', [(i, i ^ distance) for i in range(lax.axis_siz...  10.7 us
    ppermute x4, starting transfers between devices, by_core(): return lax.ppermute(block, ('seq', 'head'), pairs)  8.05 us
    pallas_call x2, Pallas kernels, local(): pl.pallas_call(functools.partial(rest_kernel, first, count), out_shape=sh...  6.76 us
    ppermute x10, starting transfers between devices, over_head(): return lax.ppermute(block, 'head', pairs)  5.06 us
    pallas_call x2, Pallas kernels, finish(): pl.pallas_call(output_kernel, grid=(rows // FBLK,), out_shape=shape((tok_...  4.01 us
    pallas_call x1, Pallas kernels, local(): pl.pallas_call(own_kernel, out_shape=(shape((group, tok_rows), F32), shap...  3.94 us
  transfers between devices with their start and end apart: 19, of which 10 were waited for; matrix products, arithmetic and copies ran while one was open for 0% of the time, Pallas kernels for 19%

profile of v8, /device:TPU:0, one launch (start us, length us, event | category | flops | bytes accessed | tf_op | source)
XLA Modules:
  0.0 81.0 jit_solution(15455275477915620957)
XLA Ops:
  0.0 2.7 %send.1 = (bf16[144,512]{1,0:T(8,128)(2,1)}, bf16[144,512]{1,0:T(8,128)(2,1)}, bf16[144,1024]{1,0:T(8,128)(2,1)}, bf16[144,512]{1,0:T(8,128)(2,1)}, bf16[128,1024]{1,0:T(8,128)(2,1)}) custom-call(bf16[1024,1024]{1,0:T(8,128)(2,1)} %tokens_ref.1, s32[1,512]{1,0:T(1,128)} %mask_ref.3), custom_call_target="tpu_custom_call" | custom-call | flops 1 | bytes 1 | tf_op jit(solution)/shard_map/send/pallas_call | solution.py:131
  2.7 4.0 %collective-permute-start.5 = (bf16[144,1024]{1,0:T(8,128)(2,1)}, bf16[144,1024]{1,0:T(8,128)(2,1)S(1)}, u32[]{:S(2)}, u32[]{:S(2)}) collective-permute-start(bf16[144,1024]{1,0:T(8,128)(2,1)} %get-tuple-element.55), channel_id=1, source_target_pairs={{0,12},{1,9},{2,14},{3,11},{4,8},{5,13},{6,10},{7,15},{8,4},{9,1},... | collective-permute-start | bytes 884744 | tf_op jit(solution)/shard_map/ppermute | solution.py:110
  6.7 0.5 collective-permute-start.2
  7.2 3.4 %collective-permute-start = (bf16[144,512]{1,0:T(8,128)(2,1)}, bf16[144,512]{1,0:T(8,128)(2,1)S(1)}, u32[]{:S(2)}, u32[]{:S(2)}) collective-permute-start(bf16[144,512]{1,0:T(8,128)(2,1)} %get-tuple-element.44), channel_id=1, source_target_pairs={{0,28},{1,25},{2,30},{3,27},{4,24},{5,29},{6,26},{7,31},{8,20},{9,... | collective-permute-start | bytes 442376 | tf_op jit(solution)/shard_map/ppermute | solution.py:110
  10.8 2.8 %collective-permute-done.2.refs_2_.refs_1_ = bf16[144,512]{1,0:T(8,128)(2,1)S(1)} collective-permute-done((bf16[144,512]{1,0:T(8,128)(2,1)}, bf16[144,512]{1,0:T(8,128)(2,1)S(1)}, u32[]{:S(2)}, u32[]{:S(2)}) %collective-permute-start.2) | collective-permute-done | bytes 147488 | tf_op jit(solution)/shard_map/ppermute | solution.py:110
  13.6 4.8 %collective-permute-done.5.refs_0_ = bf16[144,1024]{1,0:T(8,128)(2,1)S(1)} collective-permute-done((bf16[144,1024]{1,0:T(8,128)(2,1)}, bf16[144,1024]{1,0:T(8,128)(2,1)S(1)}, u32[]{:S(2)}, u32[]{:S(2)}) %collective-permute-start.5) | collective-permute-done | bytes 294944 | tf_op jit(solution)/shard_map/ppermute | solution.py:110
  18.5 2.0 %collective-permute-done.refs_0_ = bf16[144,512]{1,0:T(8,128)(2,1)S(1)} collective-permute-done((bf16[144,512]{1,0:T(8,128)(2,1)}, bf16[144,512]{1,0:T(8,128)(2,1)S(1)}, u32[]{:S(2)}, u32[]{:S(2)}) %collective-permute-start) | collective-permute-done | bytes 147488 | tf_op jit(solution)/shard_map/ppermute | solution.py:110
  20.5 3.1 %collective-permute-done.1.refs_1_ = bf16[144,512]{1,0:T(8,128)(2,1)S(1)} collective-permute-done((bf16[144,512]{1,0:T(8,128)(2,1)}, bf16[144,512]{1,0:T(8,128)(2,1)S(1)}, u32[]{:S(2)}, u32[]{:S(2)}) %collective-permute-start.1) | collective-permute-done | bytes 147488 | tf_op jit(solution)/shard_map/ppermute | solution.py:110
  23.6 1.6 %collective-permute-start.3 = (bf16[272,512]{1,0:T(8,128)(2,1)S(1)}, bf16[272,512]{1,0:T(8,128)(2,1)S(1)}, u32[]{:S(2)}, u32[]{:S(2)}) collective-permute-start(bf16[272,512]{1,0:T(8,128)(2,1)S(1)} %stack.3.early_ref.refs_0_), channel_id=1, source_target_pairs={{0,2},{2,0},{1,3},{3,1},{4,6},{6,4},{5,7},{7,5},{8,10},{10,8},{9,1... | collective-permute-start | bytes 835592 | tf_op jit(solution)/shard_map/ppermute | solution.py:54
  25.2 2.5 %prepare.1 = (bf16[1024,1024]{1,0:T(8,128)(2,1)S(1)}, bf16[1024,1024]{1,0:T(8,128)(2,1)S(1)}, bf16[672,1024]{1,0:T(8,128)(2,1)S(1)}, f32[160,128]{1,0:T(8,128)S(...) custom-call(s32[1,1024]{1,0:T(1,128)S(1)} %copy-done.8, ...), custom_call_target="tpu_custom_call" | custom-call | flops 1 | bytes 1 | tf_op jit(solution)/shard_map/prepare/pallas_call | solution.py:518
  27.7 1.2 %expand.1 = (bf16[1024,512]{1,0:T(8,128)(2,1)S(1)}, bf16[512,1024]{1,0:T(8,128)(2,1)S(1)}, f32[2048,128]{1,0:T(8,128)S(1)}) custom-call(f32[1024,128]{1,0:T(8,128)S(1)} %get-tuple-element.53.seen_ref, bf16[272,512]{1,0:T(8,128)(2,1)S(1)} %stack.3.early_ref.refs_0_, bf16[272,512]{1,0:T(8,128)(2,1)S(1)} %collective-permute-done.4.refs_1_.refs_2_, ...), custom_call_target="tpu_custom_call" | custom-call | flops 1 | bytes 1 | tf_op jit(solution)/shard_map/expand/pallas_call | solution.py:538
  29.0 3.7 %collective-permute-done.3.refs_1_ = bf16[272,512]{1,0:T(8,128)(2,1)S(1)} collective-permute-done((bf16[272,512]{1,0:T(8,128)(2,1)S(1)}, bf16[272,512]{1,0:T(8,128)(2,1)S(1)}, u32[]{:S(2)}, u32[]{:S(2)}) %collective-permute-start.3) | collective-permute-done | bytes 278560 | tf_op jit(solution)/shard_map/ppermute | solution.py:54
  32.7 1.6 %collective-permute-done.7.refs_3_ = bf16[272,512]{1,0:T(8,128)(2,1)S(1)} collective-permute-done((bf16[272,512]{1,0:T(8,128)(2,1)S(1)}, bf16[272,512]{1,0:T(8,128)(2,1)S(1)}, u32[]{:S(2)}, u32[]{:S(2)}) %collective-permute-start.7) | collective-permute-done | bytes 278560 | tf_op jit(solution)/shard_map/ppermute | solution.py:54
  34.3 2.1 %project.1 = (bf16[1024,256]{1,0:T(8,128)(2,1)S(1)}, bf16[64,256]{1,0:T(8,128)(2,1)S(1)}, bf16[1024,256]{1,0:T(8,128)(2,1)S(1)}, bf16[256,1024]{1,0:T(8,128)(2,1)S(1)}, bf16[1024,1024]{1,0:T(8,128)(2,1)S(1)}) custom-call(bf16[272,512]{1,0:T(8,128)(2,1)S(1)} %stack.3.early_ref.refs_0_, bf16[272,512]{1,0:T(8,128)(2,1)S(1)} %collective-permute-done.3.refs_1_, ...), custom_call_target="tpu_custom_call" | custom-call | flops 1 | bytes 1 | tf_op jit(solution)/shard_map/project/pallas_call | solution.py:555
  36.4 2.9 %collective-permute-start.8 = (bf16[1024,256]{1,0:T(8,128)(2,1)S(1)}, bf16[1024,256]{1,0:T(8,128)(2,1)S(1)}, u32[]{:S(2)}, u32[]{:S(2)}) collective-permute-start(bf16[1024,256]{1,0:T(8,128)(2,1)S(1)} %get-tuple-element.67), channel_id=1, source_target_pairs={{0,4},{4,8},{8,12},{12,16},{16,20},{20,24},{24,28},{1,5},{5,9},{9,... | collective-permute-start | bytes 1572872 | tf_op jit(solution)/shard_map/ppermute | solution.py:58
  39.3 2.7 %collective-permute-start.11 = (bf16[64,256]{1,0:T(8,128)(2,1)S(1)}, bf16[64,256]{1,0:T(8,128)(2,1)S(1)}, u32[]{:S(2)}, u32[]{:S(2)}) collective-permute-start(bf16[64,256]{1,0:T(8,128)(2,1)S(1)} %get-tuple-element.68.refs_0_), channel_id=1, source_target_pairs={{0,24},{4,28},{8,16},{12,20},{16,8},{20,12},{24,0},{28,4},{1,25},{... | collective-permute-start | bytes 98312 | tf_op jit(solution)/shard_map/ppermute | solution.py:100
  42.0 1.8 %collective-permute-start.9 = (bf16[64,256]{1,0:T(8,128)(2,1)S(1)}, bf16[64,256]{1,0:T(8,128)(2,1)S(1)}, u32[]{:S(2)}, u32[]{:S(2)}) collective-permute-start(bf16[64,256]{1,0:T(8,128)(2,1)S(1)} %get-tuple-element.68.refs_0_), channel_id=1, source_target_pairs={{0,8},{4,12},{8,0},{12,4},{16,24},{20,28},{24,16},{28,20},{1,9},{5... | collective-permute-start | bytes 98312 | tf_op jit(solution)/shard_map/ppermute | solution.py:100
  43.8 2.6 %order.1 = (bf16[256,1024]{1,0:T(8,128)(2,1)S(1)}, bf16[256,1024]{1,0:T(8,128)(2,1)S(1)}, bf16[1024,256]{1,0:T(8,128)(2,1)S(1)}, bf16[128,256]{1,0:T(8,128)(2,1)S(1)}, bf16[256,128]{1,0:T(8,128)(2,1)S(1)}) custom-call(bf16[1024,1024]{1,0:T(8,128)(2,1)S(1)} %get-tuple-element.47.p_ref, bf16[1024,1024]{1,0:T(8,128)(2,1)S(1)} %get-tuple-element.48.pt_ref, ...), custom_call_target="tpu_custom_call" | custom-call | flops 1 | bytes 1 | tf_op jit(solution)/shard_map/order/pallas_call | solution.py:574
  46.4 0.4 collective-permute-done.10.refs_2_
  46.8 6.2 %collective-permute-start.12 = (bf16[256,256]{1,0:T(8,128)(2,1)S(1)}, bf16[256,256]{1,0:T(8,128)(2,1)S(1)}, u32[]{:S(2)}, u32[]{:S(2)}) collective-permute-start(bf16[256,256]{1,0:T(8,128)(2,1)S(1)} %stack.5.refs_0_.column_ref), channel_id=1, source_target_pairs={{0,4},{4,0},{8,12},{12,8},{16,20},{20,16},{24,28},{28,24},{1,5},{5... | collective-permute-start | bytes 393224 | tf_op jit(solution)/shard_map/ppermute | solution.py:100
  53.0 3.9 %own.1 = (f32[256,1024]{1,0:T(8,128)S(1)}, f32[256,1024]{1,0:T(8,128)S(1)}, f32[8,512]{1,0:T(8,128)S(1)}, f32[8,512]{1,0:T(8,128)S(1)}) custom-call(f32[4,4]{1,0:T(4,128)S(1)} %copy-done.5, bf16[256,1024]{1,0:T(8,128)(2,1)S(1)} %get-tuple-element.64.qt_ref, bf16[1024,256]{1,0:T(8,128)(2,1)S(1)} %get-tuple-element.65.k_ref, ...), custom_call_target="tpu_custom_call" | custom-call | flops 1 | bytes 1 | tf_op jit(solution)/shard_map/own/pallas_call | solution.py:599
  57.0 0.9 %window.1 = (bf16[2048,256]{1,0:T(8,128)(2,1)S(1)}, bf16[256,2048]{1,0:T(8,128)(2,1)S(1)}, bf16[64,256]{1,0:T(8,128)(2,1)S(1)}, bf16[256,64]{1,0:T(8,128)(2,1)S(1)}) custom-call(bf16[1024,256]{1,0:T(8,128)(2,1)S(1)} %get-tuple-element.65.k_ref, bf16[256,1024]{1,0:T(8,128)(2,1)S(1)} %get-tuple-element.66.vt_ref, ...), custom_call_target="tpu_custom_call" | custom-call | flops 1 | bytes 1 | tf_op jit(solution)/shard_map/window/pallas_call | solution.py:618
  58.0 3.4 %rest.2.refs_0_ = bf16[512,256]{1,0:T(8,128)(2,1)S(1)} custom-call(s32[4,8]{1,0:T(4,128)S(1)} %bitcast.1, f32[4,4]{1,0:T(4,128)S(1)} %copy-done.5, bf16[256,1024]{1,0:T(8,128)(2,1)S(1)} %get-tuple-element.64.qt_ref, bf16[2048,256]{1,0:T(8,128)(2,1)S(1)} %get-tuple-element.70.kw_ref, bf16[256,2048]{1,0:T(8,128)(2,1)S(1)} %get-tuple-element.71.vw_ref, ...), custom_call_target="tpu_custom_call" | custom-call | flops 1 | bytes 1 | tf_op jit(solution)/shard_map/rest/pallas_call | solution.py:659
  61.4 1.6 %collective-permute-start.13 = (bf16[512,256]{1,0:T(8,128)(2,1)S(1)}, bf16[512,256]{1,0:T(8,128)(2,1)S(1)}, u32[]{:S(2)}, u32[]{:S(2)}) collective-permute-start(bf16[512,256]{1,0:T(8,128)(2,1)S(1)} %rest.2.refs_0_), channel_id=1, source_target_pairs={{0,2},{2,0},{1,3},{3,1},{4,6},{6,4},{5,7},{7,5},{8,10},{10,8},{9,1... | collective-permute-start | bytes 786440 | tf_op jit(solution)/shard_map/ppermute | solution.py:54
  62.9 3.4 %rest.3.refs_0_ = bf16[512,256]{1,0:T(8,128)(2,1)S(1)} custom-call(s32[4,8]{1,0:T(4,128)S(1)} %bitcast.2, f32[4,4]{1,0:T(4,128)S(1)} %copy-done.5, bf16[256,1024]{1,0:T(8,128)(2,1)S(1)} %get-tuple-element.64.qt_ref, bf16[2048,256]{1,0:T(8,128)(2,1)S(1)} %get-tuple-element.70.kw_ref, bf16[256,2048]{1,0:T(8,128)(2,1)S(1)} %get-tuple-element.71.vw_ref, ...), custom_call_target="tpu_custom_call" | custom-call | flops 1 | bytes 1 | tf_op jit(solution)/shard_map/rest/pallas_call | solution.py:659
  66.4 2.4 %collective-permute-done.13.refs_1_ = bf16[512,256]{1,0:T(8,128)(2,1)S(1)} collective-permute-done((bf16[512,256]{1,0:T(8,128)(2,1)S(1)}, bf16[512,256]{1,0:T(8,128)(2,1)S(1)}, u32[]{:S(2)}, u32[]{:S(2)}) %collective-permute-start.13) | collective-permute-done | bytes 262176 | tf_op jit(solution)/shard_map/ppermute | solution.py:54
  68.8 1.5 %collective-permute-start.14 = (bf16[512,256]{1,0:T(8,128)(2,1)S(1)}, bf16[512,256]{1,0:T(8,128)(2,1)S(1)}, u32[]{:S(2)}, u32[]{:S(2)}) collective-permute-start(bf16[512,256]{1,0:T(8,128)(2,1)S(1)} %rest.3.refs_0_), channel_id=1, source_target_pairs={{0,2},{2,0},{1,3},{3,1},{4,6},{6,4},{5,7},{7,5},{8,10},{10,8},{9,1... | collective-permute-start | bytes 786440 | tf_op jit(solution)/shard_map/ppermute | solution.py:54
  70.3 0.2 collective-permute-start.17
  70.5 2.0 %output.2.refs_4_ = bf16[1024,256]{1,0:T(8,128)(2,1)} custom-call(bf16[1024,256]{1,0:T(8,128)(2,1)S(1)} %copy-done, bf16[512,256]{1,0:T(8,128)(2,1)S(1)} %rest.2.refs_0_, bf16[512,256]{1,0:T(8,128)(2,1)S(1)} %collective-permute-done.13.refs_1_, bf16[512,256]{1,0:T(8,128)(2,1)S(1)} %collective-permute-done.15.refs_2_, ...), custom_call_target="tpu_custom_call" | custom-call | flops 1 | bytes 1 | tf_op jit(solution)/shard_map/output/pallas_call | solution.py:644
  72.5 5.0 %collective-permute-done.14.refs_1_ = bf16[512,256]{1,0:T(8,128)(2,1)S(1)} collective-permute-done((bf16[512,256]{1,0:T(8,128)(2,1)S(1)}, bf16[512,256]{1,0:T(8,128)(2,1)S(1)}, u32[]{:S(2)}, u32[]{:S(2)}) %collective-permute-start.14) | collective-permute-done | bytes 262176 | tf_op jit(solution)/shard_map/ppermute | solution.py:54
  77.5 1.5 %collective-permute-done.18.refs_3_ = bf16[512,256]{1,0:T(8,128)(2,1)S(1)} collective-permute-done((bf16[512,256]{1,0:T(8,128)(2,1)S(1)}, bf16[512,256]{1,0:T(8,128)(2,1)S(1)}, u32[]{:S(2)}, u32[]{:S(2)}) %collective-permute-start.18) | collective-permute-done | bytes 262176 | tf_op jit(solution)/shard_map/ppermute | solution.py:54
  79.0 2.0 %output.3 = bf16[1024,256]{1,0:T(8,128)(2,1)} custom-call(bf16[1024,256]{1,0:T(8,128)(2,1)S(1)} %copy-done, bf16[512,256]{1,0:T(8,128)(2,1)S(1)} %rest.3.refs_0_, bf16[512,256]{1,0:T(8,128)(2,1)S(1)} %collective-permute-done.14.refs_1_, bf16[512,256]{1,0:T(8,128)(2,1)S(1)} %collective-permute-done.17.refs_2_, ...), custom_call_target="tpu_custom_call", output_to_operand_aliasing={{}: (5, {})} | custom-call | flops 1 | bytes 1 | tf_op jit(solution)/shard_map/output/pallas_call | solution.py:644
  (38 shorter events, 0.5 us)
Async XLA Ops:
  0.0 25.2 %copy-start.7 = (s32[1,512]{1,0:T(1,128)S(1)}, s32[1,512]{1,0:T(1,128)}, u32[]{:S(2)}) copy-start(s32[1,512]{1,0:T(1,128)} %mask_ref.3) | copy-start | bytes 6148
  0.0 25.2 %copy-start.8 = (s32[1,1024]{1,0:T(1,128)S(1)}, s32[1,1024]{1,0:T(1,128)}, u32[]{:S(2)}) copy-start(s32[1,1024]{1,0:T(1,128)} %order_ref.1) | copy-start | bytes 12292
  0.0 25.2 %copy-start.2 = (bf16[1024,256]{1,0:T(8,128)(2,1)S(1)}, bf16[1024,256]{1,0:T(8,128)(2,1)}, u32[]{:S(2)}) copy-start(bf16[1024,256]{1,0:T(8,128)(2,1)} %wv_ref.1) | copy-start | bytes 1572868
  0.0 25.2 %copy-start.3 = (bf16[1024,256]{1,0:T(8,128)(2,1)S(1)}, bf16[1024,256]{1,0:T(8,128)(2,1)}, u32[]{:S(2)}) copy-start(bf16[1024,256]{1,0:T(8,128)(2,1)} %wk_in.1) | copy-start | bytes 1572868
  0.0 25.2 %copy-start.1 = (bf16[1024,256]{1,0:T(8,128)(2,1)S(1)}, bf16[1024,256]{1,0:T(8,128)(2,1)}, u32[]{:S(2)}) copy-start(bf16[1024,256]{1,0:T(8,128)(2,1)} %wq_ref.1) | copy-start | bytes 1572868
  2.7 15.7 %collective-permute-start.5 = (bf16[144,1024]{1,0:T(8,128)(2,1)}, bf16[144,1024]{1,0:T(8,128)(2,1)S(1)}, u32[]{:S(2)}, u32[]{:S(2)}) collective-permute-start(bf16[144,1024]{1,0:T(8,128)(2,1)} %get-tuple-element.55), channel_id=1, source_target_pairs={{0,12},{1,9},{2,14},{3,11},{4,8},{5,13},{6,10},{7,15},{8,4},{9,1},... | collective-permute-start | bytes 884744 | tf_op jit(solution)/shard_map/ppermute | solution.py:110
  6.7 6.9 %collective-permute-start.2 = (bf16[144,512]{1,0:T(8,128)(2,1)}, bf16[144,512]{1,0:T(8,128)(2,1)S(1)}, u32[]{:S(2)}, u32[]{:S(2)}) collective-permute-start(bf16[144,512]{1,0:T(8,128)(2,1)} %get-tuple-element.46), channel_id=1, source_target_pairs={{0,4},{1,5},{2,6},{3,7},{4,0},{5,1},{6,2},{7,3},{8,12},{9,13},{10,... | collective-permute-start | bytes 442376 | tf_op jit(solution)/shard_map/ppermute | solution.py:110
  7.2 13.2 %collective-permute-start = (bf16[144,512]{1,0:T(8,128)(2,1)}, bf16[144,512]{1,0:T(8,128)(2,1)S(1)}, u32[]{:S(2)}, u32[]{:S(2)}) collective-permute-start(bf16[144,512]{1,0:T(8,128)(2,1)} %get-tuple-element.44), channel_id=1, source_target_pairs={{0,28},{1,25},{2,30},{3,27},{4,24},{5,29},{6,26},{7,31},{8,20},{9,... | collective-permute-start | bytes 442376 | tf_op jit(solution)/shard_map/ppermute | solution.py:110
  10.7 12.9 %collective-permute-start.1 = (bf16[144,512]{1,0:T(8,128)(2,1)}, bf16[144,512]{1,0:T(8,128)(2,1)S(1)}, u32[]{:S(2)}, u32[]{:S(2)}) collective-permute-start(bf16[144,512]{1,0:T(8,128)(2,1)} %get-tuple-element.45), channel_id=1, source_target_pairs={{0,20},{1,17},{2,22},{3,19},{4,16},{5,21},{6,18},{7,23},{8,28},{9,... | collective-permute-start | bytes 442376 | tf_op jit(solution)/shard_map/ppermute | solution.py:110
  18.4 15.9 %copy-start.4 = (bf16[128,1024]{1,0:T(8,128)(2,1)S(1)}, bf16[128,1024]{1,0:T(8,128)(2,1)}, u32[]{:S(2)}) copy-start(bf16[128,1024]{1,0:T(8,128)(2,1)} %get-tuple-element.60.refs_6_) | copy-start | bytes 786436
  18.4 9.3 %collective-permute-start.6 = (bf16[416,512]{1,0:T(8,128)(2,1)S(1)}, bf16[416,512]{1,0:T(8,128)(2,1)S(1)}, u32[]{:S(2)}, u32[]{:S(2)}) collective-permute-start(bf16[416,512]{1,0:T(8,128)(2,1)S(1)} %stack.4.refs_2_.refs_4_), channel_id=1, source_target_pairs={{0,1},{1,0},{2,3},{3,2},{4,5},{5,4},{6,7},{7,6},{8,9},{9,8},{10,11... | collective-permute-start | bytes 1277960 | tf_op jit(solution)/shard_map/ppermute | solution.py:54
  23.6 4.2 %collective-permute-start.4 = (bf16[272,512]{1,0:T(8,128)(2,1)S(1)}, bf16[272,512]{1,0:T(8,128)(2,1)S(1)}, u32[]{:S(2)}, u32[]{:S(2)}) collective-permute-start(bf16[272,512]{1,0:T(8,128)(2,1)S(1)} %stack.3.early_ref.refs_0_), channel_id=1, source_target_pairs={{0,1},{1,0},{2,3},{3,2},{4,5},{5,4},{6,7},{7,6},{8,9},{9,8},{10,11... | collective-permute-start | bytes 835592 | tf_op jit(solution)/shard_map/ppermute | solution.py:54
  23.6 9.1 %collective-permute-start.3 = (bf16[272,512]{1,0:T(8,128)(2,1)S(1)}, bf16[272,512]{1,0:T(8,128)(2,1)S(1)}, u32[]{:S(2)}, u32[]{:S(2)}) collective-permute-start(bf16[272,512]{1,0:T(8,128)(2,1)S(1)} %stack.3.early_ref.refs_0_), channel_id=1, source_target_pairs={{0,2},{2,0},{1,3},{3,1},{4,6},{6,4},{5,7},{7,5},{8,10},{10,8},{9,1... | collective-permute-start | bytes 835592 | tf_op jit(solution)/shard_map/ppermute | solution.py:54
  32.7 1.6 %collective-permute-start.7 = (bf16[272,512]{1,0:T(8,128)(2,1)S(1)}, bf16[272,512]{1,0:T(8,128)(2,1)S(1)}, u32[]{:S(2)}, u32[]{:S(2)}) collective-permute-start(bf16[272,512]{1,0:T(8,128)(2,1)S(1)} %collective-permute-done.3.refs_1_), channel_id=1, source_target_pairs={{0,1},{1,0},{2,3},{3,2},{4,5},{5,4},{6,7},{7,6},{8,9},{9,8},{10,11... | collective-permute-start | bytes 835592 | tf_op jit(solution)/shard_map/ppermute | solution.py:54
  36.4 20.7 %collective-permute-start.8 = (bf16[1024,256]{1,0:T(8,128)(2,1)S(1)}, bf16[1024,256]{1,0:T(8,128)(2,1)S(1)}, u32[]{:S(2)}, u32[]{:S(2)}) collective-permute-start(bf16[1024,256]{1,0:T(8,128)(2,1)S(1)} %get-tuple-element.67), channel_id=1, source_target_pairs={{0,4},{4,8},{8,12},{12,16},{16,20},{20,24},{24,28},{1,5},{5,9},{9,... | collective-permute-start | bytes 1572872 | tf_op jit(solution)/shard_map/ppermute | solution.py:58
  39.3 7.1 %collective-permute-start.11 = (bf16[64,256]{1,0:T(8,128)(2,1)S(1)}, bf16[64,256]{1,0:T(8,128)(2,1)S(1)}, u32[]{:S(2)}, u32[]{:S(2)}) collective-permute-start(bf16[64,256]{1,0:T(8,128)(2,1)S(1)} %get-tuple-element.68.refs_0_), channel_id=1, source_target_pairs={{0,24},{4,28},{8,16},{12,20},{16,8},{20,12},{24,0},{28,4},{1,25},{... | collective-permute-start | bytes 98312 | tf_op jit(solution)/shard_map/ppermute | solution.py:100
  42.0 4.8 %collective-permute-start.10 = (bf16[64,256]{1,0:T(8,128)(2,1)S(1)}, bf16[64,256]{1,0:T(8,128)(2,1)S(1)}, u32[]{:S(2)}, u32[]{:S(2)}) collective-permute-start(bf16[64,256]{1,0:T(8,128)(2,1)S(1)} %get-tuple-element.68.refs_0_), channel_id=1, source_target_pairs={{0,16},{4,20},{8,24},{12,28},{16,0},{20,4},{24,8},{28,12},{1,17},{... | collective-permute-start | bytes 98312 | tf_op jit(solution)/shard_map/ppermute | solution.py:100
  42.0 4.8 %collective-permute-start.9 = (bf16[64,256]{1,0:T(8,128)(2,1)S(1)}, bf16[64,256]{1,0:T(8,128)(2,1)S(1)}, u32[]{:S(2)}, u32[]{:S(2)}) collective-permute-start(bf16[64,256]{1,0:T(8,128)(2,1)S(1)} %get-tuple-element.68.refs_0_), channel_id=1, source_target_pairs={{0,8},{4,12},{8,0},{12,4},{16,24},{20,28},{24,16},{28,20},{1,9},{5... | collective-permute-start | bytes 98312 | tf_op jit(solution)/shard_map/ppermute | solution.py:100
  43.8 9.3 %copy-start.5 = (f32[4,4]{1,0:T(4,128)S(1)}, f32[4,4]{1,0:T(4,128)}, u32[]{:S(2)}) copy-start(f32[4,4]{1,0:T(4,128)} %mix_ref.5) | copy-start | bytes 196
  46.8 10.2 %collective-permute-start.12 = (bf16[256,256]{1,0:T(8,128)(2,1)S(1)}, bf16[256,256]{1,0:T(8,128)(2,1)S(1)}, u32[]{:S(2)}, u32[]{:S(2)}) collective-permute-start(bf16[256,256]{1,0:T(8,128)(2,1)S(1)} %stack.5.refs_0_.column_ref), channel_id=1, source_target_pairs={{0,4},{4,0},{8,12},{12,8},{16,20},{20,16},{24,28},{28,24},{1,5},{5... | collective-permute-start | bytes 393224 | tf_op jit(solution)/shard_map/ppermute | solution.py:100
  57.0 1.0 %copy-start.6 = (s32[8,4]{0,1:T(4,128)S(1)}, s32[8,4]{0,1:T(4,128)}, u32[]{:S(2)}) copy-start(s32[8,4]{0,1:T(4,128)} %param.15) | copy-start | bytes 388
  61.3 9.1 %copy-start = (bf16[1024,256]{1,0:T(8,128)(2,1)S(1)}, bf16[1024,256]{1,0:T(8,128)(2,1)}, u32[]{:S(2)}) copy-start(bf16[1024,256]{1,0:T(8,128)(2,1)} %w_ref.3) | copy-start | bytes 1572868
  61.4 7.4 %collective-permute-start.13 = (bf16[512,256]{1,0:T(8,128)(2,1)S(1)}, bf16[512,256]{1,0:T(8,128)(2,1)S(1)}, u32[]{:S(2)}, u32[]{:S(2)}) collective-permute-start(bf16[512,256]{1,0:T(8,128)(2,1)S(1)} %rest.2.refs_0_), channel_id=1, source_target_pairs={{0,2},{2,0},{1,3},{3,1},{4,6},{6,4},{5,7},{7,5},{8,10},{10,8},{9,1... | collective-permute-start | bytes 786440 | tf_op jit(solution)/shard_map/ppermute | solution.py:54
  66.3 4.2 %collective-permute-start.15 = (bf16[512,256]{1,0:T(8,128)(2,1)S(1)}, bf16[512,256]{1,0:T(8,128)(2,1)S(1)}, u32[]{:S(2)}, u32[]{:S(2)}) collective-permute-start(bf16[512,256]{1,0:T(8,128)(2,1)S(1)} %rest.2.refs_0_), channel_id=1, source_target_pairs={{0,1},{1,0},{2,3},{3,2},{4,5},{5,4},{6,7},{7,6},{8,9},{9,8},{10,11... | collective-permute-start | bytes 786440 | tf_op jit(solution)/shard_map/ppermute | solution.py:54
  68.8 1.7 %collective-permute-start.16 = (bf16[512,256]{1,0:T(8,128)(2,1)S(1)}, bf16[512,256]{1,0:T(8,128)(2,1)S(1)}, u32[]{:S(2)}, u32[]{:S(2)}) collective-permute-start(bf16[512,256]{1,0:T(8,128)(2,1)S(1)} %collective-permute-done.13.refs_1_), channel_id=1, source_target_pairs={{0,1},{1,0},{2,3},{3,2},{4,5},{5,4},{6,7},{7,6},{8,9},{9,8},{10,11... | collective-permute-start | bytes 786440 | tf_op jit(solution)/shard_map/ppermute | solution.py:54
  68.8 8.7 %collective-permute-start.14 = (bf16[512,256]{1,0:T(8,128)(2,1)S(1)}, bf16[512,256]{1,0:T(8,128)(2,1)S(1)}, u32[]{:S(2)}, u32[]{:S(2)}) collective-permute-start(bf16[512,256]{1,0:T(8,128)(2,1)S(1)} %rest.3.refs_0_), channel_id=1, source_target_pairs={{0,2},{2,0},{1,3},{3,1},{4,6},{6,4},{5,7},{7,5},{8,10},{10,8},{9,1... | collective-permute-start | bytes 786440 | tf_op jit(solution)/shard_map/ppermute | solution.py:54
  70.3 7.2 %collective-permute-start.17 = (bf16[512,256]{1,0:T(8,128)(2,1)S(1)}, bf16[512,256]{1,0:T(8,128)(2,1)S(1)}, u32[]{:S(2)}, u32[]{:S(2)}) collective-permute-start(bf16[512,256]{1,0:T(8,128)(2,1)S(1)} %rest.3.refs_0_), channel_id=1, source_target_pairs={{0,1},{1,0},{2,3},{3,2},{4,5},{5,4},{6,7},{7,6},{8,9},{9,8},{10,11... | collective-permute-start | bytes 786440 | tf_op jit(solution)/shard_map/ppermute | solution.py:54
  77.5 1.5 %collective-permute-start.18 = (bf16[512,256]{1,0:T(8,128)(2,1)S(1)}, bf16[512,256]{1,0:T(8,128)(2,1)S(1)}, u32[]{:S(2)}, u32[]{:S(2)}) collective-permute-start(bf16[512,256]{1,0:T(8,128)(2,1)S(1)} %collective-permute-done.14.refs_1_), channel_id=1, source_target_pairs={{0,1},{1,0},{2,3},{3,2},{4,5},{5,4},{6,7},{7,6},{8,9},{9,8},{10,11... | collective-permute-start | bytes 786440 | tf_op jit(solution)/shard_map/ppermute | solution.py:54

commit v9 on v8

--- a/solution.py
+++ b/solution.py
@@ -67,12 +67,13 @@
     ids = mask_ref[...]
     line = iota((CODE_ROWS, ids.shape[1]), 0)
     code = jnp.where(line == 0, ids >> 5, jnp.where(line == 1, ids & 31, 0)).astype(F32).astype(BF)
-    sides = (head >> 1, head >> 1, None, core)
-    for distance, side, out in zip((7 - core, 5 - core, 3 - core, 1), sides, outs):
+    sides = (head >> 1, head >> 1, core, core, core)
+    for distance, side, out in zip((7 - core, 5 - core, 3, 2, 1), sides, outs):
         row = pl.multiple_of((slab ^ distance) * rows, rows)
-        start = 0 if side is None else pl.multiple_of(side * half, half)
-        out[:rows] = tokens_ref[pl.ds(row, rows), pl.ds(start, out.shape[1])]
-        out[rows:, : code.shape[1]] = code
+        start = pl.multiple_of(side * half, half)
+        out[:rows] = tokens_ref[pl.ds(row, rows), pl.ds(start, half)]
+        if out.shape[0] > rows:
+            out[rows:] = code
     own[...] = tokens_ref[pl.ds(pl.multiple_of(slab * rows, rows), rows)]
 
 
@@ -132,39 +133,42 @@
         send_kernel,
         out_shape=(
             jax.ShapeDtypeStruct((tall, half), BF),
+            jax.ShapeDtypeStruct((rows, half), BF),
             jax.ShapeDtypeStruct((tall, half), BF),
-            jax.ShapeDtypeStruct((tall, width), BF),
+            jax.ShapeDtypeStruct((rows, half), BF),
             jax.ShapeDtypeStruct((tall, half), BF),
             jax.ShapeDtypeStruct((rows, width), BF),
         ),
         in_specs=vmem_specs(2),
-        out_specs=vmem_specs(5),
+        out_specs=vmem_specs(6),
         compiler_params=pltpu.CompilerParams(vmem_limit_bytes=60 * 1024 * 1024),
         cost_estimate=COST,
         name="send",
     )(tokens, mask_ids)
-    routes = ((7, 6), (5, 4), (3, 2), (1, 1))
-    one, two, three, four = [by_core(block, route) for block, route in zip(blocks, routes)]
-    far = stacked((one, two), ((0, 0, rows, 0), (1, 0, rows, 0), (0, rows, CODE_ROWS, 0)), half, (four,))
+    routes = ((7, 6), (5, 4), (3, 3), (2, 2), (1, 1))
+    one, two, three, four, five = [by_core(block, route) for block, route in zip(blocks, routes)]
+    prepared = prepare(own)
+    one, _ = lax.optimization_barrier((one, prepared))
+    far = [one, two]
+    far_core = [over_head(part, CORE_PAIRS) for part in far]
+    far_x = [over_head(part, X_PAIRS) for part in far]
     near = stacked(
-        (three, four),
+        (three, four, five),
         (
             (0, 0, rows, 0),
-            (0, 0, rows, half),
             (1, 0, rows, 0),
+            (2, 0, rows, 0),
             (0, rows, CODE_ROWS, 0),
-            (1, rows, CODE_ROWS, 0),
+            (2, rows, CODE_ROWS, 0),
         ),
         half,
+        (one, two),
     )
-    far_x = over_head(far, X_PAIRS)
     near_core = over_head(near, CORE_PAIRS)
-    far_core = over_head(far, CORE_PAIRS)
-    prepared = prepare(far)
-    expanded = expand(prepared, [far, far_core, near, near_core])
-    far_x, _, _ = lax.optimization_barrier((far_x, prepared, expanded))
-    far_last = over_head(far_x, CORE_PAIRS)
-    return [far, far_x, far_core, far_last, near, near_core, own], prepared, expanded
+    expanded = expand(prepared, [one, far_core[0], near])
+    far_x[1], _ = lax.optimization_barrier((far_x[1], expanded))
+    far_last = [over_head(part, CORE_PAIRS) for part in far_x]
+    return far + far_x + far_core + far_last + [near, near_core, own], prepared, expanded
 
 
 def column(row, lanes=128):
@@ -235,15 +239,15 @@
 def mask_before(refs, rows):
     if len(refs) == 1:
         return refs[0][...]
-    far, far_core, near, near_core = refs
+    far, far_core, near = refs
     core = lax.axis_index("head") & 1
 
     def digits(ref, row):
         return ref[row : row + CODE_ROWS].astype(F32)
 
     by_one = digits(near, 3 * rows + CODE_ROWS)
-    by_three = jnp.where(core == 0, digits(near, 3 * rows), digits(near_core, 3 * rows))
-    by_seven = jnp.where(core == 0, digits(far, 2 * rows), digits(far_core, 2 * rows))
+    by_three = digits(near, 3 * rows)
+    by_seven = jnp.where(core == 0, digits(far, rows), digits(far_core, rows))
     slab = lax.axis_index("seq")
     distance = slab ^ (slab - 1)
     code = jnp.where(distance == 1, by_one, jnp.where(distance == 3, by_three, by_seven)).astype(I32)
@@ -272,21 +276,17 @@
             start = pl.multiple_of((head ^ distance) * quarter, quarter)
             x_ref[:, pl.ds(start, quarter)] = piece[...]
         return
-    far, far_x, far_core, far_last, near, near_core, own = piece_refs
+    far_refs, (near, near_core, own) = piece_refs[:8], piece_refs[8:]
     rows, half = own.shape[0], width // 2
     core, side = head & 1, head >> 1
-    for holder, pieces in ((core, (far, far_x)), (1 - core, (far_core, far_last))):
-        for part in range(2):
-            row = pl.multiple_of((2 * part + holder) * rows, rows)
-            for turn, piece in enumerate(pieces):
-                start = pl.multiple_of((side ^ turn) * half, half)
-                x_ref[pl.ds(row, rows), pl.ds(start, half)] = piece[part * rows : (part + 1) * rows]
-    for holder, piece in ((core, near), (1 - core, near_core)):
-        row = pl.multiple_of((4 + holder) * rows, rows)
-        x_ref[pl.ds(row, rows), :half] = piece[:rows]
-        x_ref[pl.ds(row, rows), half:] = piece[rows : 2 * rows]
-        start = pl.multiple_of(holder * half, half)
-        x_ref[6 * rows : 7 * rows, pl.ds(start, half)] = piece[2 * rows : 3 * rows]
+    for index, piece in enumerate(far_refs):
+        turn, crossed = (index // 2) % 2, index // 4
+        row = pl.multiple_of((2 * (index % 2) + (core ^ crossed)) * rows, rows)
+        start = pl.multiple_of((side ^ turn) * half, half)
+        x_ref[pl.ds(row, rows), pl.ds(start, half)] = piece[:rows]
+    for crossed, piece in enumerate((near, near_core)):
+        start = pl.multiple_of((core ^ crossed) * half, half)
+        x_ref[4 * rows : 7 * rows, pl.ds(start, half)] = piece[: 3 * rows]
     x_ref[7 * rows :] = own[...]
 
 
@@ -345,7 +345,7 @@
 
 
 def own_kernel(
-    mix_ref, qt_ref, k_ref, vt_ref, nk_ref, nvt_ref, seen_ref, column_ref,
+    mix_ref, qt_ref, k_ref, vt_ref, nk_ref, nvt_ref, seen_ref,
     acc_ref, near_ref, top_ref, den_ref, q4_ref, p_ref,
 ):
     tok_rows, group = k_ref.shape
@@ -586,15 +586,6 @@
         cost_estimate=COST,
         name="order",
     )(permute, permute_t, select, f_col, f_row, w_t, rows_here, k0, v0)
-    if slabs == 8:
-        places = tuple((index, 0, step, 0) for index in range(4))
-        column = stacked(lined, places, group, (near_k,))
-        summaries = [column, by_distance(column, 1)]
-    else:
-        copies = jnp.broadcast_to(summ[None], (slabs, step, group))
-        copies = lax.all_to_all(copies, "seq", split_axis=0, concat_axis=0, tiled=True)
-        summaries = [copies.reshape(slabs * step, group)]
-
     blocks = tok_rows // FBLK
     acc, near_out, top, den = pl.pallas_call(
         own_kernel,
@@ -604,7 +595,7 @@
             shape((blocks, heads * FBLK), F32),
             shape((blocks, heads * FBLK), F32),
         ),
-        in_specs=smem_specs(1) + vmem_specs(6) + [pl.BlockSpec(memory_space=pl.ANY)],
+        in_specs=smem_specs(1) + vmem_specs(6),
         out_specs=vmem_specs(4),
         scratch_shapes=[
             pltpu.VMEM((2, group, heads * FBLK), BF),
@@ -613,7 +604,16 @@
         compiler_params=params,
         cost_estimate=COST,
         name="own",
-    )(level_mix, q_t, keys, v_t, near_k, near_vt, seen, summaries[0])
+    )(level_mix, q_t, keys, v_t, near_k, near_vt, seen)
+
+    if slabs == 8:
+        places = tuple((index, 0, step, 0) for index in range(4))
+        column = stacked(lined, places, group, (top,))
+        summaries = [column, by_distance(column, 1)]
+    else:
+        copies = jnp.broadcast_to(summ[None], (slabs, step, group))
+        copies = lax.all_to_all(copies, "seq", split_axis=0, concat_axis=0, tiled=True)
+        summaries = [copies.reshape(slabs * step, group)]
 
     window_k, window_v, coarse_k, coarse_v = pl.pallas_call(
         window_kernel,

time: 81.2 us -> 78.6 us (0.968)
  waiting for transfers between devices: 27.2 us -> 23.2 us
  local copies, waits for them, and re-layouts: 0.04 us -> 0.98 us
    ppermute x4 -> x5, waiting for transfers between devices: 12.6 us -> 5.64 us  [by_core(): return lax.ppermute(block, ('seq', 'head'), pairs)]
    ppermute x4, waiting for transfers between devices: 0.38 us -> 2.99 us  [by_distance(): lax.ppermute(block, 'seq', [(i, i ^ distance) for i in range(lax.axis_siz...]
    ppermute x4, starting transfers between devices: 10.7 us -> 8.37 us  [by_distance(): lax.ppermute(block, 'seq', [(i, i ^ distance) for i in range(lax.axis_siz...]
    ppermute x4 -> x5, starting transfers between devices: 8.05 us -> 9.51 us  [by_core(): return lax.ppermute(block, ('seq', 'head'), pairs)]
    ppermute x10 -> x13, starting transfers between devices: 5.06 us -> 6.17 us  [over_head(): return lax.ppermute(block, 'head', pairs)]
    unnamed x18 -> x20, local copies, waits for them, and re-layouts: 0.04 us -> 0.98 us
    ppermute x10 -> x13, waiting for transfers between devices: 14.2 us -> 14.6 us  [over_head(): return lax.ppermute(block, 'head', pairs)]
  transfers between devices with their start and end apart: 19 -> 23, of which waited for: 10 -> 9; matrix products, arithmetic and copies ran while one was open for 0% -> 0% of each run, Pallas kernels for 19% -> 20%
where the time goes in v9:
time: 78.6 us; the launch traced here: 78.5 us
  starting transfers between devices  27.1 us (34%)
  Pallas kernels  27 us (34%)
  waiting for transfers between devices  23.2 us (30%)
  local copies, waits for them, and re-layouts  0.98 us (1%)
    ppermute x13, waiting for transfers between devices, over_head(): return lax.ppermute(block, 'head', pairs)  14.6 us
    ppermute x5, starting transfers between devices, by_core(): return lax.ppermute(block, ('seq', 'head'), pairs)  9.51 us
    ppermute x4, starting transfers between devices, by_distance(): lax.ppermute(block, 'seq', [(i, i ^ distance) for i in range(lax.axis_siz...  8.37 us
    pallas_call x2, Pallas kernels, local(): pl.pallas_call(functools.partial(rest_kernel, first, count), out_shape=sh...  6.76 us
    ppermute x13, starting transfers between devices, over_head(): return lax.ppermute(block, 'head', pairs)  6.17 us
    ppermute x5, waiting for transfers between devices, by_core(): return lax.ppermute(block, ('seq', 'head'), pairs)  5.64 us
    pallas_call x2, Pallas kernels, finish(): pl.pallas_call(output_kernel, grid=(rows // FBLK,), out_shape=shape((tok_...  4.05 us
    pallas_call x1, Pallas kernels, local(): pl.pallas_call(own_kernel, out_shape=(shape((group, tok_rows), F32), shap...  3.99 us
  transfers between devices with their start and end apart: 23, of which 9 were waited for; matrix products, arithmetic and copies ran while one was open for 0% of the time, Pallas kernels for 20%

profile of v9, /device:TPU:0, one launch (start us, length us, event | category | flops | bytes accessed | tf_op | source)
XLA Modules:
  0.0 78.5 jit_solution(17465577705823210284)
XLA Ops:
  0.0 2.7 %send.1 = (bf16[144,512]{1,0:T(8,128)(2,1)}, bf16[128,512]{1,0:T(8,128)(2,1)}, bf16[144,512]{1,0:T(8,128)(2,1)}, bf16[128,512]{1,0:T(8,128)(2,1)}, bf16[144,512]{1,0:T(8,128)(2,1)}, /*index=5*/bf16[128,1024]{1,0:T(8,128)(2,1)}) custom-call(bf16[1024,1024]{1,0:T(8,128)(2,1)} %tokens_ref.1, s32[1,512]{1,0:T(1,128)} %mask_ref.3), custom_call_target="tpu_custom_call" | custom-call | flops 1 | bytes 1 | tf_op jit(solution)/shard_map/send/pallas_call | solution.py:132
  2.7 6.0 %collective-permute-start = (bf16[144,512]{1,0:T(8,128)(2,1)}, bf16[144,512]{1,0:T(8,128)(2,1)S(1)}, u32[]{:S(2)}, u32[]{:S(2)}) collective-permute-start(bf16[144,512]{1,0:T(8,128)(2,1)} %get-tuple-element.53), channel_id=1, source_target_pairs={{0,28},{1,25},{2,30},{3,27},{4,24},{5,29},{6,26},{7,31},{8,20},{9,... | collective-permute-start | bytes 442376 | tf_op jit(solution)/shard_map/ppermute | solution.py:111
  8.8 1.0 %collective-permute-start.7 = (bf16[144,512]{1,0:T(8,128)(2,1)}, bf16[144,512]{1,0:T(8,128)(2,1)S(1)}, u32[]{:S(2)}, u32[]{:S(2)}) collective-permute-start(bf16[144,512]{1,0:T(8,128)(2,1)} %get-tuple-element.60), channel_id=1, source_target_pairs={{0,4},{1,5},{2,6},{3,7},{4,0},{5,1},{6,2},{7,3},{8,12},{9,13},{10,... | collective-permute-start | bytes 442376 | tf_op jit(solution)/shard_map/ppermute | solution.py:111
  9.8 1.0 %collective-permute-start.1 = (bf16[128,512]{1,0:T(8,128)(2,1)}, bf16[128,512]{1,0:T(8,128)(2,1)S(1)}, u32[]{:S(2)}, u32[]{:S(2)}) collective-permute-start(bf16[128,512]{1,0:T(8,128)(2,1)} %get-tuple-element.57), channel_id=1, source_target_pairs={{0,20},{1,17},{2,22},{3,19},{4,16},{5,21},{6,18},{7,23},{8,28},{9,... | collective-permute-start | bytes 393224 | tf_op jit(solution)/shard_map/ppermute | solution.py:111
  10.8 1.5 %collective-permute-start.6 = (bf16[128,512]{1,0:T(8,128)(2,1)}, bf16[128,512]{1,0:T(8,128)(2,1)S(1)}, u32[]{:S(2)}, u32[]{:S(2)}) collective-permute-start(bf16[128,512]{1,0:T(8,128)(2,1)} %get-tuple-element.59), channel_id=1, source_target_pairs={{0,8},{1,9},{2,10},{3,11},{4,12},{5,13},{6,14},{7,15},{8,0},{9,1},... | collective-permute-start | bytes 393224 | tf_op jit(solution)/shard_map/ppermute | solution.py:111
  12.3 0.9 %copy-done.1 = bf16[128,1024]{1,0:T(8,128)(2,1)S(1)} copy-done((bf16[128,1024]{1,0:T(8,128)(2,1)S(1)}, bf16[128,1024]{1,0:T(8,128)(2,1)}, u32[]{:S(2)}) %copy-start.1) | copy-done | bytes 262168
  13.2 2.5 %prepare.1 = (bf16[1024,1024]{1,0:T(8,128)(2,1)S(1)}, bf16[1024,1024]{1,0:T(8,128)(2,1)S(1)}, bf16[672,1024]{1,0:T(8,128)(2,1)S(1)}, f32[160,128]{1,0:T(8,128)S(...) custom-call(s32[1,1024]{1,0:T(1,128)S(1)} %copy-done.9, ...), custom_call_target="tpu_custom_call" | custom-call | flops 1 | bytes 1 | tf_op jit(solution)/shard_map/prepare/pallas_call | solution.py:518
  15.7 5.1 %collective-permute-done.1.refs_4_.refs_1_ = bf16[128,512]{1,0:T(8,128)(2,1)S(1)} collective-permute-done((bf16[128,512]{1,0:T(8,128)(2,1)}, bf16[128,512]{1,0:T(8,128)(2,1)S(1)}, u32[]{:S(2)}, u32[]{:S(2)}) %collective-permute-start.1) | collective-permute-done | bytes 131104 | tf_op jit(solution)/shard_map/ppermute | solution.py:111
  21.5 1.6 %collective-permute-start.2 = (bf16[144,512]{1,0:T(8,128)(2,1)S(1)}, bf16[144,512]{1,0:T(8,128)(2,1)S(1)}, u32[]{:S(2)}, u32[]{:S(2)}) collective-permute-start(bf16[144,512]{1,0:T(8,128)(2,1)S(1)} %collective-permute-done.refs_3_.refs_0_), channel_id=1, source_target_pairs={{0,2},{2,0},{1,3},{3,1},{4,6},{6,4},{5,7},{7,5},{8,10},{10,8},{9,1... | collective-permute-start | bytes 442376 | tf_op jit(solution)/shard_map/ppermute | solution.py:54
  23.7 4.5 %collective-permute-done.2.refs_2_ = bf16[144,512]{1,0:T(8,128)(2,1)S(1)} collective-permute-done((bf16[144,512]{1,0:T(8,128)(2,1)S(1)}, bf16[144,512]{1,0:T(8,128)(2,1)S(1)}, u32[]{:S(2)}, u32[]{:S(2)}) %collective-permute-start.2) | collective-permute-done | bytes 147488 | tf_op jit(solution)/shard_map/ppermute | solution.py:54
  28.7 1.2 %expand.1 = (bf16[1024,512]{1,0:T(8,128)(2,1)S(1)}, bf16[512,1024]{1,0:T(8,128)(2,1)S(1)}, f32[2048,128]{1,0:T(8,128)S(1)}) custom-call(f32[1024,128]{1,0:T(8,128)S(1)} %get-tuple-element.54.seen_ref, bf16[144,512]{1,0:T(8,128)(2,1)S(1)} %collective-permute-done.refs_3_.refs_0_, bf16[144,512]{1,0:T(8,128)(2,1)S(1)} %collective-permute-done.4.refs_1_.refs_4_, ...), custom_call_target="tpu_custom_call" | custom-call | flops 1 | bytes 1 | tf_op jit(solution)/shard_map/expand/pallas_call | solution.py:538
  29.9 0.6 collective-permute-done.3.refs_3_
  30.6 1.3 %collective-permute-done.10.refs_7_ = bf16[128,512]{1,0:T(8,128)(2,1)S(1)} collective-permute-done((bf16[128,512]{1,0:T(8,128)(2,1)S(1)}, bf16[128,512]{1,0:T(8,128)(2,1)S(1)}, u32[]{:S(2)}, u32[]{:S(2)}) %collective-permute-start.10) | collective-permute-done | bytes 131104 | tf_op jit(solution)/shard_map/ppermute | solution.py:54
  31.9 2.1 %project.1 = (bf16[1024,256]{1,0:T(8,128)(2,1)S(1)}, bf16[64,256]{1,0:T(8,128)(2,1)S(1)}, bf16[1024,256]{1,0:T(8,128)(2,1)S(1)}, bf16[256,1024]{1,0:T(8,128)(2,1)S(1)}, bf16[1024,1024]{1,0:T(8,128)(2,1)S(1)}) custom-call(bf16[144,512]{1,0:T(8,128)(2,1)S(1)} %collective-permute-done.refs_3_.refs_0_, ...), custom_call_target="tpu_custom_call" | custom-call | flops 1 | bytes 1 | tf_op jit(solution)/shard_map/project/pallas_call | solution.py:555
  34.0 3.0 %collective-permute-start.12 = (bf16[1024,256]{1,0:T(8,128)(2,1)S(1)}, bf16[1024,256]{1,0:T(8,128)(2,1)S(1)}, u32[]{:S(2)}, u32[]{:S(2)}) collective-permute-start(bf16[1024,256]{1,0:T(8,128)(2,1)S(1)} %get-tuple-element.71), channel_id=1, source_target_pairs={{0,4},{4,8},{8,12},{12,16},{16,20},{20,24},{24,28},{1,5},{5,9},{9,... | collective-permute-start | bytes 1572872 | tf_op jit(solution)/shard_map/ppermute | solution.py:58
  37.0 2.0 %collective-permute-start.15 = (bf16[64,256]{1,0:T(8,128)(2,1)S(1)}, bf16[64,256]{1,0:T(8,128)(2,1)S(1)}, u32[]{:S(2)}, u32[]{:S(2)}) collective-permute-start(bf16[64,256]{1,0:T(8,128)(2,1)S(1)} %get-tuple-element.72.refs_0_), channel_id=1, source_target_pairs={{0,24},{4,28},{8,16},{12,20},{16,8},{20,12},{24,0},{28,4},{1,25},{... | collective-permute-start | bytes 98312 | tf_op jit(solution)/shard_map/ppermute | solution.py:101
  39.0 1.2 %collective-permute-start.14 = (bf16[64,256]{1,0:T(8,128)(2,1)S(1)}, bf16[64,256]{1,0:T(8,128)(2,1)S(1)}, u32[]{:S(2)}, u32[]{:S(2)}) collective-permute-start(bf16[64,256]{1,0:T(8,128)(2,1)S(1)} %get-tuple-element.72.refs_0_), channel_id=1, source_target_pairs={{0,16},{4,20},{8,24},{12,28},{16,0},{20,4},{24,8},{28,12},{1,17},{... | collective-permute-start | bytes 98312 | tf_op jit(solution)/shard_map/ppermute | solution.py:101
  40.3 1.2 %collective-permute-start.13 = (bf16[64,256]{1,0:T(8,128)(2,1)S(1)}, bf16[64,256]{1,0:T(8,128)(2,1)S(1)}, u32[]{:S(2)}, u32[]{:S(2)}) collective-permute-start(bf16[64,256]{1,0:T(8,128)(2,1)S(1)} %get-tuple-element.72.refs_0_), channel_id=1, source_target_pairs={{0,8},{4,12},{8,0},{12,4},{16,24},{20,28},{24,16},{28,20},{1,9},{5... | collective-permute-start | bytes 98312 | tf_op jit(solution)/shard_map/ppermute | solution.py:101
  41.5 2.6 %order.1 = (bf16[256,1024]{1,0:T(8,128)(2,1)S(1)}, bf16[256,1024]{1,0:T(8,128)(2,1)S(1)}, bf16[1024,256]{1,0:T(8,128)(2,1)S(1)}, bf16[128,256]{1,0:T(8,128)(2,1)S(1)}, bf16[256,128]{1,0:T(8,128)(2,1)S(1)}) custom-call(bf16[1024,1024]{1,0:T(8,128)(2,1)S(1)} %get-tuple-element.47.p_ref, bf16[1024,1024]{1,0:T(8,128)(2,1)S(1)} %get-tuple-element.48.pt_ref, ...), custom_call_target="tpu_custom_call" | custom-call | flops 1 | bytes 1 | tf_op jit(solution)/shard_map/order/pallas_call | solution.py:574
  44.2 4.0 %own.1 = (f32[256,1024]{1,0:T(8,128)S(1)}, f32[256,1024]{1,0:T(8,128)S(1)}, f32[8,512]{1,0:T(8,128)S(1)}, f32[8,512]{1,0:T(8,128)S(1)}) custom-call(f32[4,4]{1,0:T(4,128)S(1)} %copy-done.6, bf16[256,1024]{1,0:T(8,128)(2,1)S(1)} %get-tuple-element.68.qt_ref, bf16[1024,256]{1,0:T(8,128)(2,1)S(1)} %get-tuple-element.69.k_ref, ...), custom_call_target="tpu_custom_call" | custom-call | flops 1 | bytes 1 | tf_op jit(solution)/shard_map/own/pallas_call | solution.py:590
  48.2 3.9 %collective-permute-start.16 = (bf16[256,256]{1,0:T(8,128)(2,1)S(1)}, bf16[256,256]{1,0:T(8,128)(2,1)S(1)}, u32[]{:S(2)}, u32[]{:S(2)}) collective-permute-start(bf16[256,256]{1,0:T(8,128)(2,1)S(1)} %stack.3.refs_0_), channel_id=1, source_target_pairs={{0,4},{4,0},{8,12},{12,8},{16,20},{20,16},{24,28},{28,24},{1,5},{5... | collective-permute-start | bytes 393224 | tf_op jit(solution)/shard_map/ppermute | solution.py:101
  52.1 3.0 %collective-permute-done.16.refs_1_ = bf16[256,256]{1,0:T(8,128)(2,1)S(1)} collective-permute-done((bf16[256,256]{1,0:T(8,128)(2,1)S(1)}, bf16[256,256]{1,0:T(8,128)(2,1)S(1)}, u32[]{:S(2)}, u32[]{:S(2)}) %collective-permute-start.16) | collective-permute-done | bytes 131104 | tf_op jit(solution)/shard_map/ppermute | solution.py:101
  55.1 1.0 %window.1 = (bf16[2048,256]{1,0:T(8,128)(2,1)S(1)}, bf16[256,2048]{1,0:T(8,128)(2,1)S(1)}, bf16[64,256]{1,0:T(8,128)(2,1)S(1)}, bf16[256,64]{1,0:T(8,128)(2,1)S(1)}) custom-call(bf16[1024,256]{1,0:T(8,128)(2,1)S(1)} %get-tuple-element.69.k_ref, bf16[256,1024]{1,0:T(8,128)(2,1)S(1)} %get-tuple-element.70.vt_ref, ...), custom_call_target="tpu_custom_call" | custom-call | flops 1 | bytes 1 | tf_op jit(solution)/shard_map/window/pallas_call | solution.py:618
  56.1 3.4 %rest.2.refs_0_ = bf16[512,256]{1,0:T(8,128)(2,1)S(1)} custom-call(s32[4,8]{1,0:T(4,128)S(1)} %bitcast.1, f32[4,4]{1,0:T(4,128)S(1)} %copy-done.6, bf16[256,1024]{1,0:T(8,128)(2,1)S(1)} %get-tuple-element.68.qt_ref, bf16[2048,256]{1,0:T(8,128)(2,1)S(1)} %get-tuple-element.76.kw_ref, bf16[256,2048]{1,0:T(8,128)(2,1)S(1)} %get-tuple-element.77.vw_ref, ...), custom_call_target="tpu_custom_call" | custom-call | flops 1 | bytes 1 | tf_op jit(solution)/shard_map/rest/pallas_call | solution.py:659
  59.5 1.5 %collective-permute-start.17 = (bf16[512,256]{1,0:T(8,128)(2,1)S(1)}, bf16[512,256]{1,0:T(8,128)(2,1)S(1)}, u32[]{:S(2)}, u32[]{:S(2)}) collective-permute-start(bf16[512,256]{1,0:T(8,128)(2,1)S(1)} %rest.2.refs_0_), channel_id=1, source_target_pairs={{0,2},{2,0},{1,3},{3,1},{4,6},{6,4},{5,7},{7,5},{8,10},{10,8},{9,1... | collective-permute-start | bytes 786440 | tf_op jit(solution)/shard_map/ppermute | solution.py:54
  61.0 3.4 %rest.3.refs_0_ = bf16[512,256]{1,0:T(8,128)(2,1)S(1)} custom-call(s32[4,8]{1,0:T(4,128)S(1)} %bitcast.2, f32[4,4]{1,0:T(4,128)S(1)} %copy-done.6, bf16[256,1024]{1,0:T(8,128)(2,1)S(1)} %get-tuple-element.68.qt_ref, bf16[2048,256]{1,0:T(8,128)(2,1)S(1)} %get-tuple-element.76.kw_ref, bf16[256,2048]{1,0:T(8,128)(2,1)S(1)} %get-tuple-element.77.vw_ref, ...), custom_call_target="tpu_custom_call" | custom-call | flops 1 | bytes 1 | tf_op jit(solution)/shard_map/rest/pallas_call | solution.py:659
  64.5 1.7 %collective-permute-done.17.refs_1_ = bf16[512,256]{1,0:T(8,128)(2,1)S(1)} collective-permute-done((bf16[512,256]{1,0:T(8,128)(2,1)S(1)}, bf16[512,256]{1,0:T(8,128)(2,1)S(1)}, u32[]{:S(2)}, u32[]{:S(2)}) %collective-permute-start.17) | collective-permute-done | bytes 262176 | tf_op jit(solution)/shard_map/ppermute | solution.py:54
  66.2 1.5 %collective-permute-start.18 = (bf16[512,256]{1,0:T(8,128)(2,1)S(1)}, bf16[512,256]{1,0:T(8,128)(2,1)S(1)}, u32[]{:S(2)}, u32[]{:S(2)}) collective-permute-start(bf16[512,256]{1,0:T(8,128)(2,1)S(1)} %rest.3.refs_0_), channel_id=1, source_target_pairs={{0,2},{2,0},{1,3},{3,1},{4,6},{6,4},{5,7},{7,5},{8,10},{10,8},{9,1... | collective-permute-start | bytes 786440 | tf_op jit(solution)/shard_map/ppermute | solution.py:54
  67.9 2.0 %output.2.refs_4_ = bf16[1024,256]{1,0:T(8,128)(2,1)} custom-call(bf16[1024,256]{1,0:T(8,128)(2,1)S(1)} %copy-done, bf16[512,256]{1,0:T(8,128)(2,1)S(1)} %rest.2.refs_0_, bf16[512,256]{1,0:T(8,128)(2,1)S(1)} %collective-permute-done.17.refs_1_, bf16[512,256]{1,0:T(8,128)(2,1)S(1)} %collective-permute-done.19.refs_2_, ...), custom_call_target="tpu_custom_call" | custom-call | flops 1 | bytes 1 | tf_op jit(solution)/shard_map/output/pallas_call | solution.py:644
  70.0 5.0 %collective-permute-done.18.refs_1_ = bf16[512,256]{1,0:T(8,128)(2,1)S(1)} collective-permute-done((bf16[512,256]{1,0:T(8,128)(2,1)S(1)}, bf16[512,256]{1,0:T(8,128)(2,1)S(1)}, u32[]{:S(2)}, u32[]{:S(2)}) %collective-permute-start.18) | collective-permute-done | bytes 262176 | tf_op jit(solution)/shard_map/ppermute | solution.py:54
  74.9 1.5 %collective-permute-done.22.refs_3_ = bf16[512,256]{1,0:T(8,128)(2,1)S(1)} collective-permute-done((bf16[512,256]{1,0:T(8,128)(2,1)S(1)}, bf16[512,256]{1,0:T(8,128)(2,1)S(1)}, u32[]{:S(2)}, u32[]{:S(2)}) %collective-permute-start.22) | collective-permute-done | bytes 262176 | tf_op jit(solution)/shard_map/ppermute | solution.py:54
  76.4 2.0 %output.3 = bf16[1024,256]{1,0:T(8,128)(2,1)} custom-call(bf16[1024,256]{1,0:T(8,128)(2,1)S(1)} %copy-done, bf16[512,256]{1,0:T(8,128)(2,1)S(1)} %rest.3.refs_0_, bf16[512,256]{1,0:T(8,128)(2,1)S(1)} %collective-permute-done.18.refs_1_, bf16[512,256]{1,0:T(8,128)(2,1)S(1)} %collective-permute-done.21.refs_2_, ...), custom_call_target="tpu_custom_call", output_to_operand_aliasing={{}: (5, {})} | custom-call | flops 1 | bytes 1 | tf_op jit(solution)/shard_map/output/pallas_call | solution.py:644
  (47 shorter events, 2.2 us)
Async XLA Ops:
  0.0 12.2 %copy-start.8 = (s32[1,512]{1,0:T(1,128)S(1)}, s32[1,512]{1,0:T(1,128)}, u32[]{:S(2)}) copy-start(s32[1,512]{1,0:T(1,128)} %mask_ref.3) | copy-start | bytes 6148
  0.0 12.2 %copy-start.9 = (s32[1,1024]{1,0:T(1,128)S(1)}, s32[1,1024]{1,0:T(1,128)}, u32[]{:S(2)}) copy-start(s32[1,1024]{1,0:T(1,128)} %order_ref.1) | copy-start | bytes 12292
  0.0 12.2 %copy-start.4 = (bf16[1024,256]{1,0:T(8,128)(2,1)S(1)}, bf16[1024,256]{1,0:T(8,128)(2,1)}, u32[]{:S(2)}) copy-start(bf16[1024,256]{1,0:T(8,128)(2,1)} %wv_ref.1) | copy-start | bytes 1572868
  0.0 12.2 %copy-start.5 = (bf16[1024,256]{1,0:T(8,128)(2,1)S(1)}, bf16[1024,256]{1,0:T(8,128)(2,1)}, u32[]{:S(2)}) copy-start(bf16[1024,256]{1,0:T(8,128)(2,1)} %wk_in.1) | copy-start | bytes 1572868
  0.0 12.3 %copy-start.3 = (bf16[1024,256]{1,0:T(8,128)(2,1)S(1)}, bf16[1024,256]{1,0:T(8,128)(2,1)}, u32[]{:S(2)}) copy-start(bf16[1024,256]{1,0:T(8,128)(2,1)} %wq_ref.1) | copy-start | bytes 1572868
  2.7 13.0 %collective-permute-start = (bf16[144,512]{1,0:T(8,128)(2,1)}, bf16[144,512]{1,0:T(8,128)(2,1)S(1)}, u32[]{:S(2)}, u32[]{:S(2)}) collective-permute-start(bf16[144,512]{1,0:T(8,128)(2,1)} %get-tuple-element.53), channel_id=1, source_target_pairs={{0,28},{1,25},{2,30},{3,27},{4,24},{5,29},{6,26},{7,31},{8,20},{9,... | collective-permute-start | bytes 442376 | tf_op jit(solution)/shard_map/ppermute | solution.py:111
  8.8 12.6 %collective-permute-start.5 = (bf16[144,512]{1,0:T(8,128)(2,1)}, bf16[144,512]{1,0:T(8,128)(2,1)S(1)}, u32[]{:S(2)}, u32[]{:S(2)}) collective-permute-start(bf16[144,512]{1,0:T(8,128)(2,1)} %get-tuple-element.58), channel_id=1, source_target_pairs={{0,12},{1,13},{2,14},{3,15},{4,8},{5,9},{6,10},{7,11},{8,4},{9,5},... | collective-permute-start | bytes 442376 | tf_op jit(solution)/shard_map/ppermute | solution.py:111
  8.8 12.6 %collective-permute-start.7 = (bf16[144,512]{1,0:T(8,128)(2,1)}, bf16[144,512]{1,0:T(8,128)(2,1)S(1)}, u32[]{:S(2)}, u32[]{:S(2)}) collective-permute-start(bf16[144,512]{1,0:T(8,128)(2,1)} %get-tuple-element.60), channel_id=1, source_target_pairs={{0,4},{1,5},{2,6},{3,7},{4,0},{5,1},{6,2},{7,3},{8,12},{9,13},{10,... | collective-permute-start | bytes 442376 | tf_op jit(solution)/shard_map/ppermute | solution.py:111
  9.8 11.1 %collective-permute-start.1 = (bf16[128,512]{1,0:T(8,128)(2,1)}, bf16[128,512]{1,0:T(8,128)(2,1)S(1)}, u32[]{:S(2)}, u32[]{:S(2)}) collective-permute-start(bf16[128,512]{1,0:T(8,128)(2,1)} %get-tuple-element.57), channel_id=1, source_target_pairs={{0,20},{1,17},{2,22},{3,19},{4,16},{5,21},{6,18},{7,23},{8,28},{9,... | collective-permute-start | bytes 393224 | tf_op jit(solution)/shard_map/ppermute | solution.py:111
  10.8 10.6 %collective-permute-start.6 = (bf16[128,512]{1,0:T(8,128)(2,1)}, bf16[128,512]{1,0:T(8,128)(2,1)S(1)}, u32[]{:S(2)}, u32[]{:S(2)}) collective-permute-start(bf16[128,512]{1,0:T(8,128)(2,1)} %get-tuple-element.59), channel_id=1, source_target_pairs={{0,8},{1,9},{2,10},{3,11},{4,12},{5,13},{6,14},{7,15},{8,0},{9,1},... | collective-permute-start | bytes 393224 | tf_op jit(solution)/shard_map/ppermute | solution.py:111
  13.2 18.7 %copy-start.2 = (bf16[128,1024]{1,0:T(8,128)(2,1)S(1)}, bf16[128,1024]{1,0:T(8,128)(2,1)}, u32[]{:S(2)}) copy-start(bf16[128,1024]{1,0:T(8,128)(2,1)} %get-tuple-element.46.early_ref.refs_10_) | copy-start | bytes 786436
  21.4 10.5 %collective-permute-start.11 = (bf16[416,512]{1,0:T(8,128)(2,1)S(1)}, bf16[416,512]{1,0:T(8,128)(2,1)S(1)}, u32[]{:S(2)}, u32[]{:S(2)}) collective-permute-start(bf16[416,512]{1,0:T(8,128)(2,1)S(1)} %stack.2.refs_2_.refs_8_), channel_id=1, source_target_pairs={{0,1},{1,0},{2,3},{3,2},{4,5},{5,4},{6,7},{7,6},{8,9},{9,8},{10,11... | collective-permute-start | bytes 1277960 | tf_op jit(solution)/shard_map/ppermute | solution.py:54
  21.5 6.7 %collective-permute-start.2 = (bf16[144,512]{1,0:T(8,128)(2,1)S(1)}, bf16[144,512]{1,0:T(8,128)(2,1)S(1)}, u32[]{:S(2)}, u32[]{:S(2)}) collective-permute-start(bf16[144,512]{1,0:T(8,128)(2,1)S(1)} %collective-permute-done.refs_3_.refs_0_), channel_id=1, source_target_pairs={{0,2},{2,0},{1,3},{3,1},{4,6},{6,4},{5,7},{7,5},{8,10},{10,8},{9,1... | collective-permute-start | bytes 442376 | tf_op jit(solution)/shard_map/ppermute | solution.py:54
  23.0 5.7 %collective-permute-start.4 = (bf16[144,512]{1,0:T(8,128)(2,1)S(1)}, bf16[144,512]{1,0:T(8,128)(2,1)S(1)}, u32[]{:S(2)}, u32[]{:S(2)}) collective-permute-start(bf16[144,512]{1,0:T(8,128)(2,1)S(1)} %collective-permute-done.refs_3_.refs_0_), channel_id=1, source_target_pairs={{0,1},{1,0},{2,3},{3,2},{4,5},{5,4},{6,7},{7,6},{8,9},{9,8},{10,11... | collective-permute-start | bytes 442376 | tf_op jit(solution)/shard_map/ppermute | solution.py:54
  23.2 7.3 %collective-permute-start.3 = (bf16[128,512]{1,0:T(8,128)(2,1)S(1)}, bf16[128,512]{1,0:T(8,128)(2,1)S(1)}, u32[]{:S(2)}, u32[]{:S(2)}) collective-permute-start(bf16[128,512]{1,0:T(8,128)(2,1)S(1)} %collective-permute-done.1.refs_4_.refs_1_), channel_id=1, source_target_pairs={{0,2},{2,0},{1,3},{3,1},{4,6},{6,4},{5,7},{7,5},{8,10},{10,8},{9,1... | collective-permute-start | bytes 393224 | tf_op jit(solution)/shard_map/ppermute | solution.py:54
  28.2 3.7 %collective-permute-start.9 = (bf16[144,512]{1,0:T(8,128)(2,1)S(1)}, bf16[144,512]{1,0:T(8,128)(2,1)S(1)}, u32[]{:S(2)}, u32[]{:S(2)}) collective-permute-start(bf16[144,512]{1,0:T(8,128)(2,1)S(1)} %collective-permute-done.2.refs_2_), channel_id=1, source_target_pairs={{0,1},{1,0},{2,3},{3,2},{4,5},{5,4},{6,7},{7,6},{8,9},{9,8},{10,11... | collective-permute-start | bytes 442376 | tf_op jit(solution)/shard_map/ppermute | solution.py:54
  28.2 2.4 %collective-permute-start.8 = (bf16[128,512]{1,0:T(8,128)(2,1)S(1)}, bf16[128,512]{1,0:T(8,128)(2,1)S(1)}, u32[]{:S(2)}, u32[]{:S(2)}) collective-permute-start(bf16[128,512]{1,0:T(8,128)(2,1)S(1)} %collective-permute-done.1.refs_4_.refs_1_), channel_id=1, source_target_pairs={{0,1},{1,0},{2,3},{3,2},{4,5},{5,4},{6,7},{7,6},{8,9},{9,8},{10,11... | collective-permute-start | bytes 393224 | tf_op jit(solution)/shard_map/ppermute | solution.py:54
  30.5 1.3 %collective-permute-start.10 = (bf16[128,512]{1,0:T(8,128)(2,1)S(1)}, bf16[128,512]{1,0:T(8,128)(2,1)S(1)}, u32[]{:S(2)}, u32[]{:S(2)}) collective-permute-start(bf16[128,512]{1,0:T(8,128)(2,1)S(1)} %collective-permute-done.3.refs_3_), channel_id=1, source_target_pairs={{0,1},{1,0},{2,3},{3,2},{4,5},{5,4},{6,7},{7,6},{8,9},{9,8},{10,11... | collective-permute-start | bytes 393224 | tf_op jit(solution)/shard_map/ppermute | solution.py:54
  34.0 21.1 %collective-permute-start.12 = (bf16[1024,256]{1,0:T(8,128)(2,1)S(1)}, bf16[1024,256]{1,0:T(8,128)(2,1)S(1)}, u32[]{:S(2)}, u32[]{:S(2)}) collective-permute-start(bf16[1024,256]{1,0:T(8,128)(2,1)S(1)} %get-tuple-element.71), channel_id=1, source_target_pairs={{0,4},{4,8},{8,12},{12,16},{16,20},{20,24},{24,28},{1,5},{5,9},{9,... | collective-permute-start | bytes 1572872 | tf_op jit(solution)/shard_map/ppermute | solution.py:58
  37.0 11.1 %collective-permute-start.15 = (bf16[64,256]{1,0:T(8,128)(2,1)S(1)}, bf16[64,256]{1,0:T(8,128)(2,1)S(1)}, u32[]{:S(2)}, u32[]{:S(2)}) collective-permute-start(bf16[64,256]{1,0:T(8,128)(2,1)S(1)} %get-tuple-element.72.refs_0_), channel_id=1, source_target_pairs={{0,24},{4,28},{8,16},{12,20},{16,8},{20,12},{24,0},{28,4},{1,25},{... | collective-permute-start | bytes 98312 | tf_op jit(solution)/shard_map/ppermute | solution.py:101
  39.0 9.1 %collective-permute-start.14 = (bf16[64,256]{1,0:T(8,128)(2,1)S(1)}, bf16[64,256]{1,0:T(8,128)(2,1)S(1)}, u32[]{:S(2)}, u32[]{:S(2)}) collective-permute-start(bf16[64,256]{1,0:T(8,128)(2,1)S(1)} %get-tuple-element.72.refs_0_), channel_id=1, source_target_pairs={{0,16},{4,20},{8,24},{12,28},{16,0},{20,4},{24,8},{28,12},{1,17},{... | collective-permute-start | bytes 98312 | tf_op jit(solution)/shard_map/ppermute | solution.py:101
  40.3 7.9 %collective-permute-start.13 = (bf16[64,256]{1,0:T(8,128)(2,1)S(1)}, bf16[64,256]{1,0:T(8,128)(2,1)S(1)}, u32[]{:S(2)}, u32[]{:S(2)}) collective-permute-start(bf16[64,256]{1,0:T(8,128)(2,1)S(1)} %get-tuple-element.72.refs_0_), channel_id=1, source_target_pairs={{0,8},{4,12},{8,0},{12,4},{16,24},{20,28},{24,16},{28,20},{1,9},{5... | collective-permute-start | bytes 98312 | tf_op jit(solution)/shard_map/ppermute | solution.py:101
  41.5 2.6 %copy-start.6 = (f32[4,4]{1,0:T(4,128)S(1)}, f32[4,4]{1,0:T(4,128)}, u32[]{:S(2)}) copy-start(f32[4,4]{1,0:T(4,128)} %mix_ref.5) | copy-start | bytes 196
  48.2 7.9 %copy-start.7 = (s32[8,4]{0,1:T(4,128)S(1)}, s32[8,4]{0,1:T(4,128)}, u32[]{:S(2)}) copy-start(s32[8,4]{0,1:T(4,128)} %param.15) | copy-start | bytes 388
  48.2 6.9 %collective-permute-start.16 = (bf16[256,256]{1,0:T(8,128)(2,1)S(1)}, bf16[256,256]{1,0:T(8,128)(2,1)S(1)}, u32[]{:S(2)}, u32[]{:S(2)}) collective-permute-start(bf16[256,256]{1,0:T(8,128)(2,1)S(1)} %stack.3.refs_0_), channel_id=1, source_target_pairs={{0,4},{4,0},{8,12},{12,8},{16,20},{20,16},{24,28},{28,24},{1,5},{5... | collective-permute-start | bytes 393224 | tf_op jit(solution)/shard_map/ppermute | solution.py:101
  59.5 8.4 %copy-start = (bf16[1024,256]{1,0:T(8,128)(2,1)S(1)}, bf16[1024,256]{1,0:T(8,128)(2,1)}, u32[]{:S(2)}) copy-start(bf16[1024,256]{1,0:T(8,128)(2,1)} %w_ref.3) | copy-start | bytes 1572868
  59.5 6.7 %collective-permute-start.17 = (bf16[512,256]{1,0:T(8,128)(2,1)S(1)}, bf16[512,256]{1,0:T(8,128)(2,1)S(1)}, u32[]{:S(2)}, u32[]{:S(2)}) collective-permute-start(bf16[512,256]{1,0:T(8,128)(2,1)S(1)} %rest.2.refs_0_), channel_id=1, source_target_pairs={{0,2},{2,0},{1,3},{3,1},{4,6},{6,4},{5,7},{7,5},{8,10},{10,8},{9,1... | collective-permute-start | bytes 786440 | tf_op jit(solution)/shard_map/ppermute | solution.py:54
  64.4 3.5 %collective-permute-start.19 = (bf16[512,256]{1,0:T(8,128)(2,1)S(1)}, bf16[512,256]{1,0:T(8,128)(2,1)S(1)}, u32[]{:S(2)}, u32[]{:S(2)}) collective-permute-start(bf16[512,256]{1,0:T(8,128)(2,1)S(1)} %rest.2.refs_0_), channel_id=1, source_target_pairs={{0,1},{1,0},{2,3},{3,2},{4,5},{5,4},{6,7},{7,6},{8,9},{9,8},{10,11... | collective-permute-start | bytes 786440 | tf_op jit(solution)/shard_map/ppermute | solution.py:54
  66.2 1.7 %collective-permute-start.20 = (bf16[512,256]{1,0:T(8,128)(2,1)S(1)}, bf16[512,256]{1,0:T(8,128)(2,1)S(1)}, u32[]{:S(2)}, u32[]{:S(2)}) collective-permute-start(bf16[512,256]{1,0:T(8,128)(2,1)S(1)} %collective-permute-done.17.refs_1_), channel_id=1, source_target_pairs={{0,1},{1,0},{2,3},{3,2},{4,5},{5,4},{6,7},{7,6},{8,9},{9,8},{10,11... | collective-permute-start | bytes 786440 | tf_op jit(solution)/shard_map/ppermute | solution.py:54
  66.2 8.7 %collective-permute-start.18 = (bf16[512,256]{1,0:T(8,128)(2,1)S(1)}, bf16[512,256]{1,0:T(8,128)(2,1)S(1)}, u32[]{:S(2)}, u32[]{:S(2)}) collective-permute-start(bf16[512,256]{1,0:T(8,128)(2,1)S(1)} %rest.3.refs_0_), channel_id=1, source_target_pairs={{0,2},{2,0},{1,3},{3,1},{4,6},{6,4},{5,7},{7,5},{8,10},{10,8},{9,1... | collective-permute-start | bytes 786440 | tf_op jit(solution)/shard_map/ppermute | solution.py:54
  67.7 7.2 %collective-permute-start.21 = (bf16[512,256]{1,0:T(8,128)(2,1)S(1)}, bf16[512,256]{1,0:T(8,128)(2,1)S(1)}, u32[]{:S(2)}, u32[]{:S(2)}) collective-permute-start(bf16[512,256]{1,0:T(8,128)(2,1)S(1)} %rest.3.refs_0_), channel_id=1, source_target_pairs={{0,1},{1,0},{2,3},{3,2},{4,5},{5,4},{6,7},{7,6},{8,9},{9,8},{10,11... | collective-permute-start | bytes 786440 | tf_op jit(solution)/shard_map/ppermute | solution.py:54
  74.9 1.5 %collective-permute-start.22 = (bf16[512,256]{1,0:T(8,128)(2,1)S(1)}, bf16[512,256]{1,0:T(8,128)(2,1)S(1)}, u32[]{:S(2)}, u32[]{:S(2)}) collective-permute-start(bf16[512,256]{1,0:T(8,128)(2,1)S(1)} %collective-permute-done.18.refs_1_), channel_id=1, source_target_pairs={{0,1},{1,0},{2,3},{3,2},{4,5},{5,4},{6,7},{7,6},{8,9},{9,8},{10,11... | collective-permute-start | bytes 786440 | tf_op jit(solution)/shard_map/ppermute | solution.py:54
  (1 other events, 1.0 us)

commit v10 on v9

--- a/solution.py
+++ b/solution.py
@@ -19,7 +19,9 @@
 I32 = jnp.int32
 HIDE = -1e30
 VMEM_LIMIT = 24 * 1024 * 1024
+LONG_BYTES = 20_000_000
 COST = pl.CostEstimate(flops=1, bytes_accessed=1, transcendentals=0)
+LONG = pl.CostEstimate(flops=1, bytes_accessed=LONG_BYTES, transcendentals=0)
 PARTS = (4, 4)
 
 X_PAIRS = [(0, 2), (2, 0), (1, 3), (3, 1)]
@@ -73,7 +75,7 @@
         start = pl.multiple_of(side * half, half)
         out[:rows] = tokens_ref[pl.ds(row, rows), pl.ds(start, half)]
         if out.shape[0] > rows:
-            out[rows:] = code
+            out[rows:] = code[: out.shape[0] - rows]
     own[...] = tokens_ref[pl.ds(pl.multiple_of(slab * rows, rows), rows)]
 
 
@@ -85,14 +87,14 @@
         at += height
 
 
-def stacked(parts, places, width, after=()):
+def stacked(parts, places, width, after=(), cost=COST):
     return pl.pallas_call(
         functools.partial(stack_kernel, places),
         out_shape=jax.ShapeDtypeStruct((sum(place[2] for place in places), width), BF),
         in_specs=vmem_specs(len(parts)) + [pl.BlockSpec(memory_space=pl.ANY)] * len(after),
         out_specs=pl.BlockSpec(memory_space=pltpu.VMEM),
         compiler_params=pltpu.CompilerParams(vmem_limit_bytes=VMEM_LIMIT),
-        cost_estimate=COST,
+        cost_estimate=cost,
         name="stack",
     )(*parts, *after)
 
@@ -133,7 +135,7 @@
         send_kernel,
         out_shape=(
             jax.ShapeDtypeStruct((tall, half), BF),
-            jax.ShapeDtypeStruct((rows, half), BF),
+            jax.ShapeDtypeStruct((tall, half), BF),
             jax.ShapeDtypeStruct((tall, half), BF),
             jax.ShapeDtypeStruct((rows, half), BF),
             jax.ShapeDtypeStruct((tall, half), BF),
@@ -149,26 +151,17 @@
     one, two, three, four, five = [by_core(block, route) for block, route in zip(blocks, routes)]
     prepared = prepare(own)
     one, _ = lax.optimization_barrier((one, prepared))
+    first_x = over_head(one, X_PAIRS)
+    two, first_x = lax.optimization_barrier((two, first_x))
     far = [one, two]
     far_core = [over_head(part, CORE_PAIRS) for part in far]
-    far_x = [over_head(part, X_PAIRS) for part in far]
-    near = stacked(
-        (three, four, five),
-        (
-            (0, 0, rows, 0),
-            (1, 0, rows, 0),
-            (2, 0, rows, 0),
-            (0, rows, CODE_ROWS, 0),
-            (2, rows, CODE_ROWS, 0),
-        ),
-        half,
-        (one, two),
-    )
-    near_core = over_head(near, CORE_PAIRS)
-    expanded = expand(prepared, [one, far_core[0], near])
+    far_x = [first_x, over_head(two, X_PAIRS)]
+    near = [three, four, five]
+    near_core = [over_head(part, CORE_PAIRS) for part in near]
+    expanded = expand(prepared, [one, far_core[0], three, five])
     far_x[1], _ = lax.optimization_barrier((far_x[1], expanded))
     far_last = [over_head(part, CORE_PAIRS) for part in far_x]
-    return far + far_x + far_core + far_last + [near, near_core, own], prepared, expanded
+    return far + far_x + far_core + far_last + near + near_core + [own], prepared, expanded
 
 
 def column(row, lanes=128):
@@ -239,18 +232,18 @@
 def mask_before(refs, rows):
     if len(refs) == 1:
         return refs[0][...]
-    far, far_core, near = refs
+    far, far_core, near_three, near_one = refs
     core = lax.axis_index("head") & 1
 
-    def digits(ref, row):
-        return ref[row : row + CODE_ROWS].astype(F32)
-
-    by_one = digits(near, 3 * rows + CODE_ROWS)
-    by_three = digits(near, 3 * rows)
-    by_seven = jnp.where(core == 0, digits(far, rows), digits(far_core, rows))
+    def digits(ref):
+        return ref[rows : rows + CODE_ROWS // 2].astype(F32)
+
+    three, one = digits(near_three), digits(near_one)
+    seven = jnp.where(core == 0, digits(far), digits(far_core))
     slab = lax.axis_index("seq")
     distance = slab ^ (slab - 1)
-    code = jnp.where(distance == 1, by_one, jnp.where(distance == 3, by_three, by_seven)).astype(I32)
+
+    code = jnp.where(distance == 1, one, jnp.where(distance == 3, three, seven)).astype(I32)
     return (code[0:1] << 5) + code[1:2]
 
 
@@ -276,7 +269,7 @@
             start = pl.multiple_of((head ^ distance) * quarter, quarter)
             x_ref[:, pl.ds(start, quarter)] = piece[...]
         return
-    far_refs, (near, near_core, own) = piece_refs[:8], piece_refs[8:]
+    far_refs, near_refs, own = piece_refs[:8], piece_refs[8:14], piece_refs[14]
     rows, half = own.shape[0], width // 2
     core, side = head & 1, head >> 1
     for index, piece in enumerate(far_refs):
@@ -284,9 +277,10 @@
         row = pl.multiple_of((2 * (index % 2) + (core ^ crossed)) * rows, rows)
         start = pl.multiple_of((side ^ turn) * half, half)
         x_ref[pl.ds(row, rows), pl.ds(start, half)] = piece[:rows]
-    for crossed, piece in enumerate((near, near_core)):
-        start = pl.multiple_of((core ^ crossed) * half, half)
-        x_ref[4 * rows : 7 * rows, pl.ds(start, half)] = piece[: 3 * rows]
+    for index, piece in enumerate(near_refs):
+        row = (4 + index % 3) * rows
+        start = pl.multiple_of((core ^ (index // 3)) * half, half)
+        x_ref[row : row + rows, pl.ds(start, half)] = piece[:rows]
     x_ref[7 * rows :] = own[...]
 
 
@@ -312,13 +306,16 @@
             :, part * group : (part + 1) * group
         ]
     factor = fcol_ref[:SUMM_ROWS, :1]
-    summ_k = (kl[packed:] * factor).astype(BF)
+    summ_k = kl[packed:] * factor
     tail = jnp.concatenate(
         [vl[:, packed:], jnp.zeros((group, 128 - SUMM_ROWS), F32)], axis=1
     )
-    summ_v = (jnp.transpose(tail)[:SUMM_ROWS] * factor).astype(BF)
-    summ_ref[:SUMM_ROWS] = summ_k
-    summ_ref[SUMM_ROWS:] = summ_v
+    summ_v = jnp.transpose(tail)[:SUMM_ROWS] * factor
+    mids = x_ref.shape[0] // POOL2
+    fars = x_ref.shape[0] // POOL3
+    summ_ref[:mids] = summ_k[:mids].astype(BF)
+    summ_ref[mids : 2 * mids] = summ_v[:mids].astype(BF)
+    summ_ref[2 * mids :] = (summ_k[mids:] + pltpu.roll(summ_v[mids:], fars, 0)).astype(BF)
 
 
 def spread_heads(q4_ref, qt_ref, at, heads):
@@ -406,18 +403,18 @@
     mids, fars = tok_rows // POOL2, tok_rows // POOL3
     shape = (ck_ref.shape[0], all_ref.shape[0])
     line = iota(shape, 0)
-    step = 2 * SUMM_ROWS
+    step = 3 * mids
     turn = line // mids
     far = line - 3 * mids
     shard = slab - 1 + turn
     turned = slab if slabs == 8 else 0
     distance = jnp.where(line < 3 * mids, shard, far // fars) ^ turned
     slot = (distance >> 1) + (distance & 1) * (slabs // 2) if slabs == 8 else distance
-    source = slot * step + jnp.where(line < 3 * mids, line - turn * mids, mids + far % fars)
-    source = jnp.where((line >= 3 * mids) | ((shard >= 0) & (shard < slabs)), source, -step)
+    source = slot * step + jnp.where(line < 3 * mids, line - turn * mids, 2 * mids + far % fars)
+    source = jnp.where((line >= 3 * mids) | ((shard >= 0) & (shard < slabs)), source, -2 * step)
     gathered = all_ref[...]
     ck_ref[...] = nn(ones_where(source == iota(shape, 1)), gathered).astype(BF)
-    values = nn(ones_where(source + SUMM_ROWS == iota(shape, 1)), gathered)
+    values = nn(ones_where(source + jnp.where(line < 3 * mids, mids, fars) == iota(shape, 1)), gathered)
     cv_ref[...] = jnp.transpose(values).astype(BF)
 
 
@@ -466,22 +463,18 @@
             scale = mix_ref[0, h] / den
             scales.append(scale)
             keeps.append(keep * scale)
+            relative = den / mix_ref[0, h]
             for level, (low, high) in enumerate(((fine, far_at), (far_at, total))):
                 part = scores[low:high, lanes]
                 weight = jnp.exp(part - jnp.max(part, axis=0, keepdims=True))
-                share = mix_ref[level + 2, h] / jnp.sum(weight, axis=0, keepdims=True)
+                share = mix_ref[level + 2, h] / jnp.sum(weight, axis=0, keepdims=True) * relative
                 p_ref[slot, low:high, lanes] = (weight * share).astype(BF)
-        fine_out = nn(vc_ref[slot, :, :fine], p_ref[slot, :fine])
-        coarse_out = nn(vc_ref[slot, :, fine:], p_ref[slot, fine:])
+        total_out = nn(vc_ref[slot], p_ref[slot])
         rows = []
         for h in range(heads):
             pick = (slice(h * width, (h + 1) * width), slice(h * FBLK, (h + 1) * FBLK))
             mine = (pick[0], slice(at, at + FBLK))
-            rows.append(
-                fine_out[pick] * scales[h]
-                + acc_ref[mine] * keeps[h]
-                + (coarse_out[pick] + near_ref[mine])
-            )
+            rows.append(total_out[pick] * scales[h] + acc_ref[mine] * keeps[h] + near_ref[mine])
         out_ref[index * FBLK : (index + 1) * FBLK] = jnp.transpose(
             jnp.concatenate(rows, axis=0)
         ).astype(BF)
@@ -508,7 +501,7 @@
     packed = tok_rows - mask_ids.shape[1]
     near, mids, fars = tok_rows // POOL1, tok_rows // POOL2, tok_rows // POOL3
     coarse = 3 * mids + fars * slabs
-    step = 2 * SUMM_ROWS
+    step = 3 * mids
     chosen = packed + SUMM_ROWS + near
 
     shape = jax.ShapeDtypeStruct
@@ -636,24 +629,25 @@
     parts = PARTS if sum(PARTS) == blocks else (blocks,)
     waiting, out, first = None, None, 0
 
-    def finish(out, attended, third, second, base):
+    def finish(out, attended, third, second, base, after=()):
         fourth = over_head(third, CORE_PAIRS)
         rows = attended.shape[0]
         previous = [] if out is None else [out]
-        tile = pl.BlockSpec((FBLK, group), lambda i: (i, 0))
+        height = min(2 * FBLK, rows)
+        tile = pl.BlockSpec((height, group), lambda i: (i, 0))
         return pl.pallas_call(
             output_kernel,
-            grid=(rows // FBLK,),
+            grid=(rows // height,),
             out_shape=shape((tok_rows, group), BF),
             in_specs=[pl.BlockSpec((width, group), lambda i: (0, 0))]
             + [tile] * 4
-            + [pl.BlockSpec(memory_space=pl.ANY)] * len(previous),
-            out_specs=pl.BlockSpec((FBLK, group), lambda i, base=base: (i + base, 0)),
+            + [pl.BlockSpec(memory_space=pl.ANY)] * (len(previous) + len(after)),
+            out_specs=pl.BlockSpec((height, group), lambda i, base=base * FBLK // height: (i + base, 0)),
             input_output_aliases={5: 0} if previous else {},
             compiler_params=params,
             cost_estimate=COST,
             name="output",
-        )(w_out, attended, third, second, fourth, *previous)
+        )(w_out, attended, third, second, fourth, *previous, *after)
 
     for count in parts:
         attended = pl.pallas_call(
@@ -678,8 +672,7 @@
         if waiting is not None:
             old, old_third, old_second, old_base = waiting
             old_third, attended = lax.optimization_barrier((old_third, attended))
-            out = finish(out, old, old_third, old_second, old_base)
-            third, out = lax.optimization_barrier((third, out))
+            out = finish(out, old, old_third, old_second, old_base, [third])
         waiting = (attended, third, second, first)
         first += count
     return finish(out, *waiting)

time: 78.6 us -> 75.1 us (0.955); the launches traced: 78.5 us -> 73.9 us
  waiting for transfers between devices: 23.2 us -> 17.2 us
  starting transfers between devices: 27.1 us -> 30.4 us
  Pallas kernels: 27 us -> 25.1 us
    ppermute x13 -> x15, waiting for transfers between devices: 14.6 us -> 7.95 us  [over_head(): return lax.ppermute(block, 'head', pairs)]
    ppermute x5, starting transfers between devices: 9.51 us -> 13.4 us  [by_core(): return lax.ppermute(block, ('seq', 'head'), pairs)]
    pallas_call x2, Pallas kernels: 4.05 us -> 2.6 us  [finish(): pl.pallas_call(output_kernel, grid=(rows // height,), out_shape=shape((to...]
    ppermute x5, waiting for transfers between devices: 5.64 us -> 6.7 us  [by_core(): return lax.ppermute(block, ('seq', 'head'), pairs)]
    ppermute x13 -> x15, starting transfers between devices: 6.17 us -> 5.98 us  [over_head(): return lax.ppermute(block, 'head', pairs)]
  transfers between devices with their start and end apart: 23 -> 25, of which waited for: 9 -> 10; matrix products, arithmetic and copies ran while one was open for 0% -> 0% of each run, Pallas kernels for 20% -> 20%
where the time goes in v10:
time: 75.1 us; the launch traced here: 73.9 us
  starting transfers between devices  30.4 us (40%)
  Pallas kernels  25.1 us (33%)
  waiting for transfers between devices  17.2 us (23%)
  local copies, waits for them, and re-layouts  0.98 us (1%)
    ppermute x5, starting transfers between devices, by_core(): return lax.ppermute(block, ('seq', 'head'), pairs)  13.4 us
    ppermute x15, waiting for transfers between devices, over_head(): return lax.ppermute(block, 'head', pairs)  7.95 us
    ppermute x4, starting transfers between devices, by_distance(): lax.ppermute(block, 'seq', [(i, i ^ distance) for i in range(lax.axis_siz...  7.81 us
    ppermute x5, waiting for transfers between devices, by_core(): return lax.ppermute(block, ('seq', 'head'), pairs)  6.7 us
    pallas_call x2, Pallas kernels, local(): pl.pallas_call(functools.partial(rest_kernel, first, count), out_shape=sh...  6.32 us
    ppermute x15, starting transfers between devices, over_head(): return lax.ppermute(block, 'head', pairs)  5.98 us
    pallas_call x1, Pallas kernels, local(): pl.pallas_call(own_kernel, out_shape=(shape((group, tok_rows), F32), shap...  3.98 us
    ppermute x1, starting transfers between devices, to_next(): lax.ppermute(block, 'seq', [(i, i + 1) for i in range(lax.axis_size('seq'...  3.22 us
  transfers between devices with their start and end apart: 25, of which 10 were waited for; matrix products, arithmetic and copies ran while one was open for 0% of the time, Pallas kernels for 20%

profile of v10, /device:TPU:0, one launch (start us, length us, event | category | flops | bytes accessed | tf_op | source)
XLA Modules:
  0.0 73.9 jit_solution(17729120050603041693)
XLA Ops:
  0.0 2.7 %send.1 = (bf16[144,512]{1,0:T(8,128)(2,1)}, bf16[144,512]{1,0:T(8,128)(2,1)}, bf16[144,512]{1,0:T(8,128)(2,1)}, bf16[128,512]{1,0:T(8,128)(2,1)}, bf16[144,512]{1,0:T(8,128)(2,1)}, /*index=5*/bf16[128,1024]{1,0:T(8,128)(2,1)}) custom-call(bf16[1024,1024]{1,0:T(8,128)(2,1)} %tokens_ref.1, s32[1,512]{1,0:T(1,128)} %mask_ref.3), custom_call_target="tpu_custom_call" | custom-call | flops 1 | bytes 1 | tf_op jit(solution)/shard_map/send/pallas_call | solution.py:134
  2.7 6.0 %collective-permute-start = (bf16[144,512]{1,0:T(8,128)(2,1)}, bf16[144,512]{1,0:T(8,128)(2,1)S(1)}, u32[]{:S(2)}, u32[]{:S(2)}) collective-permute-start(bf16[144,512]{1,0:T(8,128)(2,1)} %get-tuple-element.53), channel_id=1, source_target_pairs={{0,28},{1,25},{2,30},{3,27},{4,24},{5,29},{6,26},{7,31},{8,20},{9,... | collective-permute-start | bytes 442376 | tf_op jit(solution)/shard_map/ppermute | solution.py:113
  8.8 0.9 %copy-done.1 = bf16[128,1024]{1,0:T(8,128)(2,1)S(1)} copy-done((bf16[128,1024]{1,0:T(8,128)(2,1)S(1)}, bf16[128,1024]{1,0:T(8,128)(2,1)}, u32[]{:S(2)}) %copy-start.1) | copy-done | bytes 262168
  9.8 2.5 %prepare.1 = (bf16[1024,1024]{1,0:T(8,128)(2,1)S(1)}, bf16[1024,1024]{1,0:T(8,128)(2,1)S(1)}, bf16[672,1024]{1,0:T(8,128)(2,1)S(1)}, f32[160,128]{1,0:T(8,128)S(...) custom-call(s32[1,1024]{1,0:T(1,128)S(1)} %copy-done.8, ...), custom_call_target="tpu_custom_call" | custom-call | flops 1 | bytes 1 | tf_op jit(solution)/shard_map/prepare/pallas_call | solution.py:511
  12.2 1.5 %collective-permute-done.refs_0_ = bf16[144,512]{1,0:T(8,128)(2,1)S(1)} collective-permute-done((bf16[144,512]{1,0:T(8,128)(2,1)}, bf16[144,512]{1,0:T(8,128)(2,1)S(1)}, u32[]{:S(2)}, u32[]{:S(2)}) %collective-permute-start) | collective-permute-done | bytes 147488 | tf_op jit(solution)/shard_map/ppermute | solution.py:113
  13.7 1.6 %collective-permute-start.2 = (bf16[144,512]{1,0:T(8,128)(2,1)S(1)}, bf16[144,512]{1,0:T(8,128)(2,1)S(1)}, u32[]{:S(2)}, u32[]{:S(2)}) collective-permute-start(bf16[144,512]{1,0:T(8,128)(2,1)S(1)} %collective-permute-done.refs_0_), channel_id=1, source_target_pairs={{0,2},{2,0},{1,3},{3,1},{4,6},{6,4},{5,7},{7,5},{8,10},{10,8},{9,1... | collective-permute-start | bytes 442376 | tf_op jit(solution)/shard_map/ppermute | solution.py:56
  15.4 5.9 %collective-permute-start.10 = (bf16[128,512]{1,0:T(8,128)(2,1)}, bf16[128,512]{1,0:T(8,128)(2,1)S(1)}, u32[]{:S(2)}, u32[]{:S(2)}) collective-permute-start(bf16[128,512]{1,0:T(8,128)(2,1)} %get-tuple-element.66), channel_id=1, source_target_pairs={{0,8},{1,9},{2,10},{3,11},{4,12},{5,13},{6,14},{7,15},{8,0},{9,1},... | collective-permute-start | bytes 393224 | tf_op jit(solution)/shard_map/ppermute | solution.py:113
  21.3 1.5 %collective-permute-start.6 = (bf16[144,512]{1,0:T(8,128)(2,1)}, bf16[144,512]{1,0:T(8,128)(2,1)S(1)}, u32[]{:S(2)}, u32[]{:S(2)}) collective-permute-start(bf16[144,512]{1,0:T(8,128)(2,1)} %get-tuple-element.61), channel_id=1, source_target_pairs={{0,4},{1,5},{2,6},{3,7},{4,0},{5,1},{6,2},{7,3},{8,12},{9,13},{10,... | collective-permute-start | bytes 442376 | tf_op jit(solution)/shard_map/ppermute | solution.py:113
  22.8 0.6 collective-permute-start.3
  23.4 1.6 %collective-permute-done.10.refs_9_ = bf16[128,512]{1,0:T(8,128)(2,1)S(1)} collective-permute-done((bf16[128,512]{1,0:T(8,128)(2,1)}, bf16[128,512]{1,0:T(8,128)(2,1)S(1)}, u32[]{:S(2)}, u32[]{:S(2)}) %collective-permute-start.10) | collective-permute-done | bytes 131104 | tf_op jit(solution)/shard_map/ppermute | solution.py:113
  24.9 2.7 %collective-permute-done.5.refs_2_.refs_8_ = bf16[144,512]{1,0:T(8,128)(2,1)S(1)} collective-permute-done((bf16[144,512]{1,0:T(8,128)(2,1)}, bf16[144,512]{1,0:T(8,128)(2,1)S(1)}, u32[]{:S(2)}, u32[]{:S(2)}) %collective-permute-start.5) | collective-permute-done | bytes 147488 | tf_op jit(solution)/shard_map/ppermute | solution.py:113
  27.6 1.0 %collective-permute-done.6.refs_3_.refs_10_ = bf16[144,512]{1,0:T(8,128)(2,1)S(1)} collective-permute-done((bf16[144,512]{1,0:T(8,128)(2,1)}, bf16[144,512]{1,0:T(8,128)(2,1)S(1)}, u32[]{:S(2)}, u32[]{:S(2)}) %collective-permute-start.6) | collective-permute-done | bytes 147488 | tf_op jit(solution)/shard_map/ppermute | solution.py:113
  28.6 0.5 collective-permute-start.7
  29.1 1.2 %expand.1 = (bf16[1024,512]{1,0:T(8,128)(2,1)S(1)}, bf16[512,1024]{1,0:T(8,128)(2,1)S(1)}, f32[2048,128]{1,0:T(8,128)S(1)}) custom-call(f32[1024,128]{1,0:T(8,128)S(1)} %get-tuple-element.54.seen_ref, bf16[144,512]{1,0:T(8,128)(2,1)S(1)} %collective-permute-done.refs_0_, bf16[144,512]{1,0:T(8,128)(2,1)S(1)} %collective-permute-done.4.refs_1_.refs_4_, ...), custom_call_target="tpu_custom_call" | custom-call | flops 1 | bytes 1 | tf_op jit(solution)/shard_map/expand/pallas_call | solution.py:531
  30.9 0.9 %collective-permute-done.8.refs_6_ = bf16[144,512]{1,0:T(8,128)(2,1)S(1)} collective-permute-done((bf16[144,512]{1,0:T(8,128)(2,1)S(1)}, bf16[144,512]{1,0:T(8,128)(2,1)S(1)}, u32[]{:S(2)}, u32[]{:S(2)}) %collective-permute-start.8) | collective-permute-done | bytes 147488 | tf_op jit(solution)/shard_map/ppermute | solution.py:56
  32.0 2.1 %project.1 = (bf16[1024,256]{1,0:T(8,128)(2,1)S(1)}, bf16[48,256]{1,0:T(8,128)(2,1)S(1)}, bf16[1024,256]{1,0:T(8,128)(2,1)S(1)}, bf16[256,1024]{1,0:T(8,128)(2,1)S(1)}, bf16[1024,1024]{1,0:T(8,128)(2,1)S(1)}) custom-call(bf16[144,512]{1,0:T(8,128)(2,1)S(1)} %collective-permute-done.refs_0_, bf16[144,512]{1,0:T(8,128)(2,1)S(1)} %collective-permute-done.1.refs_1_, ...), custom_call_target="tpu_custom_call" | custom-call | flops 1 | bytes 1 | tf_op jit(solution)/shard_map/project/pallas_call | solution.py:548
  34.1 3.2 %collective-permute-start.14 = (bf16[1024,256]{1,0:T(8,128)(2,1)S(1)}, bf16[1024,256]{1,0:T(8,128)(2,1)S(1)}, u32[]{:S(2)}, u32[]{:S(2)}) collective-permute-start(bf16[1024,256]{1,0:T(8,128)(2,1)S(1)} %get-tuple-element.73), channel_id=1, source_target_pairs={{0,4},{4,8},{8,12},{12,16},{16,20},{20,24},{24,28},{1,5},{5,9},{9,... | collective-permute-start | bytes 1572872 | tf_op jit(solution)/shard_map/ppermute | solution.py:60
  37.3 2.6 %collective-permute-start.17 = (bf16[48,256]{1,0:T(8,128)(2,1)S(1)}, bf16[48,256]{1,0:T(8,128)(2,1)S(1)}, u32[]{:S(2)}, u32[]{:S(2)}) collective-permute-start(bf16[48,256]{1,0:T(8,128)(2,1)S(1)} %get-tuple-element.74.refs_0_), channel_id=1, source_target_pairs={{0,24},{4,28},{8,16},{12,20},{16,8},{20,12},{24,0},{28,4},{1,25},{... | collective-permute-start | bytes 73736 | tf_op jit(solution)/shard_map/ppermute | solution.py:103
  40.2 1.5 %collective-permute-start.15 = (bf16[48,256]{1,0:T(8,128)(2,1)S(1)}, bf16[48,256]{1,0:T(8,128)(2,1)S(1)}, u32[]{:S(2)}, u32[]{:S(2)}) collective-permute-start(bf16[48,256]{1,0:T(8,128)(2,1)S(1)} %get-tuple-element.74.refs_0_), channel_id=1, source_target_pairs={{0,8},{4,12},{8,0},{12,4},{16,24},{20,28},{24,16},{28,20},{1,9},{5... | collective-permute-start | bytes 73736 | tf_op jit(solution)/shard_map/ppermute | solution.py:103
  41.8 2.7 %order.1 = (bf16[256,1024]{1,0:T(8,128)(2,1)S(1)}, bf16[256,1024]{1,0:T(8,128)(2,1)S(1)}, bf16[1024,256]{1,0:T(8,128)(2,1)S(1)}, bf16[128,256]{1,0:T(8,128)(2,1)S(1)}, bf16[256,128]{1,0:T(8,128)(2,1)S(1)}) custom-call(bf16[1024,1024]{1,0:T(8,128)(2,1)S(1)} %get-tuple-element.47.p_ref, bf16[1024,1024]{1,0:T(8,128)(2,1)S(1)} %get-tuple-element.48.pt_ref, ...), custom_call_target="tpu_custom_call" | custom-call | flops 1 | bytes 1 | tf_op jit(solution)/shard_map/order/pallas_call | solution.py:567
  44.5 4.0 %own.1 = (f32[256,1024]{1,0:T(8,128)S(1)}, f32[256,1024]{1,0:T(8,128)S(1)}, f32[8,512]{1,0:T(8,128)S(1)}, f32[8,512]{1,0:T(8,128)S(1)}) custom-call(f32[4,4]{1,0:T(4,128)S(1)} %copy-done.5, bf16[256,1024]{1,0:T(8,128)(2,1)S(1)} %get-tuple-element.70.qt_ref, bf16[1024,256]{1,0:T(8,128)(2,1)S(1)} %get-tuple-element.71.k_ref, ...), custom_call_target="tpu_custom_call" | custom-call | flops 1 | bytes 1 | tf_op jit(solution)/shard_map/own/pallas_call | solution.py:583
  48.5 3.4 %collective-permute-start.18 = (bf16[192,256]{1,0:T(8,128)(2,1)S(1)}, bf16[192,256]{1,0:T(8,128)(2,1)S(1)}, u32[]{:S(2)}, u32[]{:S(2)}) collective-permute-start(bf16[192,256]{1,0:T(8,128)(2,1)S(1)} %stack.1.refs_0_), channel_id=1, source_target_pairs={{0,4},{4,0},{8,12},{12,8},{16,20},{20,16},{24,28},{28,24},{1,5},{5... | collective-permute-start | bytes 294920 | tf_op jit(solution)/shard_map/ppermute | solution.py:103
  51.9 2.6 %collective-permute-done.18.refs_1_ = bf16[192,256]{1,0:T(8,128)(2,1)S(1)} collective-permute-done((bf16[192,256]{1,0:T(8,128)(2,1)S(1)}, bf16[192,256]{1,0:T(8,128)(2,1)S(1)}, u32[]{:S(2)}, u32[]{:S(2)}) %collective-permute-start.18) | collective-permute-done | bytes 98336 | tf_op jit(solution)/shard_map/ppermute | solution.py:103
  54.5 0.9 %window.1 = (bf16[2048,256]{1,0:T(8,128)(2,1)S(1)}, bf16[256,2048]{1,0:T(8,128)(2,1)S(1)}, bf16[64,256]{1,0:T(8,128)(2,1)S(1)}, bf16[256,64]{1,0:T(8,128)(2,1)S(1)}) custom-call(bf16[1024,256]{1,0:T(8,128)(2,1)S(1)} %get-tuple-element.71.k_ref, bf16[256,1024]{1,0:T(8,128)(2,1)S(1)} %get-tuple-element.72.vt_ref, ...), custom_call_target="tpu_custom_call" | custom-call | flops 1 | bytes 1 | tf_op jit(solution)/shard_map/window/pallas_call | solution.py:611
  55.4 3.2 %rest.2.refs_0_ = bf16[512,256]{1,0:T(8,128)(2,1)S(1)} custom-call(s32[4,8]{1,0:T(4,128)S(1)} %bitcast.1, f32[4,4]{1,0:T(4,128)S(1)} %copy-done.5, bf16[256,1024]{1,0:T(8,128)(2,1)S(1)} %get-tuple-element.70.qt_ref, bf16[2048,256]{1,0:T(8,128)(2,1)S(1)} %get-tuple-element.78.kw_ref, bf16[256,2048]{1,0:T(8,128)(2,1)S(1)} %get-tuple-element.79.vw_ref, ...), custom_call_target="tpu_custom_call" | custom-call | flops 1 | bytes 1 | tf_op jit(solution)/shard_map/rest/pallas_call | solution.py:653
  58.6 0.6 collective-permute-start.19
  59.2 3.2 %rest.3.refs_0_ = bf16[512,256]{1,0:T(8,128)(2,1)S(1)} custom-call(s32[4,8]{1,0:T(4,128)S(1)} %bitcast.2, f32[4,4]{1,0:T(4,128)S(1)} %copy-done.5, bf16[256,1024]{1,0:T(8,128)(2,1)S(1)} %get-tuple-element.70.qt_ref, bf16[2048,256]{1,0:T(8,128)(2,1)S(1)} %get-tuple-element.78.kw_ref, bf16[256,2048]{1,0:T(8,128)(2,1)S(1)} %get-tuple-element.79.vw_ref, ...), custom_call_target="tpu_custom_call" | custom-call | flops 1 | bytes 1 | tf_op jit(solution)/shard_map/rest/pallas_call | solution.py:653
  62.4 1.6 %collective-permute-start.20 = (bf16[512,256]{1,0:T(8,128)(2,1)S(1)}, bf16[512,256]{1,0:T(8,128)(2,1)S(1)}, u32[]{:S(2)}, u32[]{:S(2)}) collective-permute-start(bf16[512,256]{1,0:T(8,128)(2,1)S(1)} %rest.3.refs_0_), channel_id=1, source_target_pairs={{0,2},{2,0},{1,3},{3,1},{4,6},{6,4},{5,7},{7,5},{8,10},{10,8},{9,1... | collective-permute-start | bytes 786440 | tf_op jit(solution)/shard_map/ppermute | solution.py:56
  63.9 3.7 %collective-permute-done.19.refs_1_ = bf16[512,256]{1,0:T(8,128)(2,1)S(1)} collective-permute-done((bf16[512,256]{1,0:T(8,128)(2,1)S(1)}, bf16[512,256]{1,0:T(8,128)(2,1)S(1)}, u32[]{:S(2)}, u32[]{:S(2)}) %collective-permute-start.19) | collective-permute-done | bytes 262176 | tf_op jit(solution)/shard_map/ppermute | solution.py:56
  68.1 3.0 %collective-permute-done.20.refs_4_.refs_1_ = bf16[512,256]{1,0:T(8,128)(2,1)S(1)} collective-permute-done((bf16[512,256]{1,0:T(8,128)(2,1)S(1)}, bf16[512,256]{1,0:T(8,128)(2,1)S(1)}, u32[]{:S(2)}, u32[]{:S(2)}) %collective-permute-start.20) | collective-permute-done | bytes 262176 | tf_op jit(solution)/shard_map/ppermute | solution.py:56
  71.1 1.3 %output.2.refs_4_ = bf16[1024,256]{1,0:T(8,128)(2,1)} custom-call(bf16[1024,256]{1,0:T(8,128)(2,1)S(1)} %copy-done, bf16[512,256]{1,0:T(8,128)(2,1)S(1)} %rest.2.refs_0_, bf16[512,256]{1,0:T(8,128)(2,1)S(1)} %collective-permute-done.19.refs_1_, bf16[512,256]{1,0:T(8,128)(2,1)S(1)} %collective-permute-done.23.refs_2_, ...), custom_call_target="tpu_custom_call" | custom-call | flops 1 | bytes 1 | tf_op jit(solution)/shard_map/output/pallas_call | solution.py:638
  72.7 1.3 %output.3 = bf16[1024,256]{1,0:T(8,128)(2,1)} custom-call(bf16[1024,256]{1,0:T(8,128)(2,1)S(1)} %copy-done, bf16[512,256]{1,0:T(8,128)(2,1)S(1)} %rest.3.refs_0_, bf16[512,256]{1,0:T(8,128)(2,1)S(1)} %collective-permute-done.20.refs_4_.refs_1_, bf16[512,256]{1,0:T(8,128)(2,1)S(1)} %collective-permute-done.21.refs_2_, ...), custom_call_target="tpu_custom_call", output_to_operand_aliasing={{}: (5, {})} | custom-call | flops 1 | bytes 1 | tf_op jit(solution)/shard_map/output/pallas_call | solution.py:638
  (48 shorter events, 1.8 us)
Async XLA Ops:
  0.0 8.8 %copy-start.7 = (s32[1,512]{1,0:T(1,128)S(1)}, s32[1,512]{1,0:T(1,128)}, u32[]{:S(2)}) copy-start(s32[1,512]{1,0:T(1,128)} %mask_ref.3) | copy-start | bytes 6148
  0.0 8.8 %copy-start.8 = (s32[1,1024]{1,0:T(1,128)S(1)}, s32[1,1024]{1,0:T(1,128)}, u32[]{:S(2)}) copy-start(s32[1,1024]{1,0:T(1,128)} %order_ref.1) | copy-start | bytes 12292
  0.0 8.8 %copy-start.3 = (bf16[1024,256]{1,0:T(8,128)(2,1)S(1)}, bf16[1024,256]{1,0:T(8,128)(2,1)}, u32[]{:S(2)}) copy-start(bf16[1024,256]{1,0:T(8,128)(2,1)} %wv_ref.1) | copy-start | bytes 1572868
  0.0 8.8 %copy-start.4 = (bf16[1024,256]{1,0:T(8,128)(2,1)S(1)}, bf16[1024,256]{1,0:T(8,128)(2,1)}, u32[]{:S(2)}) copy-start(bf16[1024,256]{1,0:T(8,128)(2,1)} %wk_in.1) | copy-start | bytes 1572868
  0.0 8.8 %copy-start.2 = (bf16[1024,256]{1,0:T(8,128)(2,1)S(1)}, bf16[1024,256]{1,0:T(8,128)(2,1)}, u32[]{:S(2)}) copy-start(bf16[1024,256]{1,0:T(8,128)(2,1)} %wq_ref.1) | copy-start | bytes 1572868
  2.7 11.0 %collective-permute-start = (bf16[144,512]{1,0:T(8,128)(2,1)}, bf16[144,512]{1,0:T(8,128)(2,1)S(1)}, u32[]{:S(2)}, u32[]{:S(2)}) collective-permute-start(bf16[144,512]{1,0:T(8,128)(2,1)} %get-tuple-element.53), channel_id=1, source_target_pairs={{0,28},{1,25},{2,30},{3,27},{4,24},{5,29},{6,26},{7,31},{8,20},{9,... | collective-permute-start | bytes 442376 | tf_op jit(solution)/shard_map/ppermute | solution.py:113
  8.8 14.0 %collective-permute-start.1 = (bf16[144,512]{1,0:T(8,128)(2,1)}, bf16[144,512]{1,0:T(8,128)(2,1)S(1)}, u32[]{:S(2)}, u32[]{:S(2)}) collective-permute-start(bf16[144,512]{1,0:T(8,128)(2,1)} %get-tuple-element.57), channel_id=1, source_target_pairs={{0,20},{1,17},{2,22},{3,19},{4,16},{5,21},{6,18},{7,23},{8,28},{9,... | collective-permute-start | bytes 442376 | tf_op jit(solution)/shard_map/ppermute | solution.py:113
  13.7 9.0 %collective-permute-start.2 = (bf16[144,512]{1,0:T(8,128)(2,1)S(1)}, bf16[144,512]{1,0:T(8,128)(2,1)S(1)}, u32[]{:S(2)}, u32[]{:S(2)}) collective-permute-start(bf16[144,512]{1,0:T(8,128)(2,1)S(1)} %collective-permute-done.refs_0_), channel_id=1, source_target_pairs={{0,2},{2,0},{1,3},{3,1},{4,6},{6,4},{5,7},{7,5},{8,10},{10,8},{9,1... | collective-permute-start | bytes 442376 | tf_op jit(solution)/shard_map/ppermute | solution.py:56
  15.4 9.6 %collective-permute-start.10 = (bf16[128,512]{1,0:T(8,128)(2,1)}, bf16[128,512]{1,0:T(8,128)(2,1)S(1)}, u32[]{:S(2)}, u32[]{:S(2)}) collective-permute-start(bf16[128,512]{1,0:T(8,128)(2,1)} %get-tuple-element.66), channel_id=1, source_target_pairs={{0,8},{1,9},{2,10},{3,11},{4,12},{5,13},{6,14},{7,15},{8,0},{9,1},... | collective-permute-start | bytes 393224 | tf_op jit(solution)/shard_map/ppermute | solution.py:113
  21.3 6.3 %collective-permute-start.5 = (bf16[144,512]{1,0:T(8,128)(2,1)}, bf16[144,512]{1,0:T(8,128)(2,1)S(1)}, u32[]{:S(2)}, u32[]{:S(2)}) collective-permute-start(bf16[144,512]{1,0:T(8,128)(2,1)} %get-tuple-element.60), channel_id=1, source_target_pairs={{0,12},{1,13},{2,14},{3,15},{4,8},{5,9},{6,10},{7,11},{8,4},{9,5},... | collective-permute-start | bytes 442376 | tf_op jit(solution)/shard_map/ppermute | solution.py:113
  21.3 7.3 %collective-permute-start.6 = (bf16[144,512]{1,0:T(8,128)(2,1)}, bf16[144,512]{1,0:T(8,128)(2,1)S(1)}, u32[]{:S(2)}, u32[]{:S(2)}) collective-permute-start(bf16[144,512]{1,0:T(8,128)(2,1)} %get-tuple-element.61), channel_id=1, source_target_pairs={{0,4},{1,5},{2,6},{3,7},{4,0},{5,1},{6,2},{7,3},{8,12},{9,13},{10,... | collective-permute-start | bytes 442376 | tf_op jit(solution)/shard_map/ppermute | solution.py:113
  22.8 5.8 %collective-permute-start.4 = (bf16[144,512]{1,0:T(8,128)(2,1)S(1)}, bf16[144,512]{1,0:T(8,128)(2,1)S(1)}, u32[]{:S(2)}, u32[]{:S(2)}) collective-permute-start(bf16[144,512]{1,0:T(8,128)(2,1)S(1)} %collective-permute-done.refs_0_), channel_id=1, source_target_pairs={{0,1},{1,0},{2,3},{3,2},{4,5},{5,4},{6,7},{7,6},{8,9},{9,8},{10,11... | collective-permute-start | bytes 442376 | tf_op jit(solution)/shard_map/ppermute | solution.py:56
  22.8 7.6 %collective-permute-start.3 = (bf16[144,512]{1,0:T(8,128)(2,1)S(1)}, bf16[144,512]{1,0:T(8,128)(2,1)S(1)}, u32[]{:S(2)}, u32[]{:S(2)}) collective-permute-start(bf16[144,512]{1,0:T(8,128)(2,1)S(1)} %collective-permute-done.1.refs_1_), channel_id=1, source_target_pairs={{0,2},{2,0},{1,3},{3,1},{4,6},{6,4},{5,7},{7,5},{8,10},{10,8},{9,1... | collective-permute-start | bytes 442376 | tf_op jit(solution)/shard_map/ppermute | solution.py:56
  24.9 5.5 %collective-permute-start.12 = (bf16[128,512]{1,0:T(8,128)(2,1)S(1)}, bf16[128,512]{1,0:T(8,128)(2,1)S(1)}, u32[]{:S(2)}, u32[]{:S(2)}) collective-permute-start(bf16[128,512]{1,0:T(8,128)(2,1)S(1)} %collective-permute-done.10.refs_9_), channel_id=1, source_target_pairs={{0,1},{1,0},{2,3},{3,2},{4,5},{5,4},{6,7},{7,6},{8,9},{9,8},{10,11... | collective-permute-start | bytes 393224 | tf_op jit(solution)/shard_map/ppermute | solution.py:56
  27.6 3.3 %collective-permute-start.11 = (bf16[144,512]{1,0:T(8,128)(2,1)S(1)}, bf16[144,512]{1,0:T(8,128)(2,1)S(1)}, u32[]{:S(2)}, u32[]{:S(2)}) collective-permute-start(bf16[144,512]{1,0:T(8,128)(2,1)S(1)} %collective-permute-done.5.refs_2_.refs_8_), channel_id=1, source_target_pairs={{0,1},{1,0},{2,3},{3,2},{4,5},{5,4},{6,7},{7,6},{8,9},{9,8},{10,11... | collective-permute-start | bytes 442376 | tf_op jit(solution)/shard_map/ppermute | solution.py:56
  28.6 2.3 %collective-permute-start.13 = (bf16[144,512]{1,0:T(8,128)(2,1)S(1)}, bf16[144,512]{1,0:T(8,128)(2,1)S(1)}, u32[]{:S(2)}, u32[]{:S(2)}) collective-permute-start(bf16[144,512]{1,0:T(8,128)(2,1)S(1)} %collective-permute-done.6.refs_3_.refs_10_), channel_id=1, source_target_pairs={{0,1},{1,0},{2,3},{3,2},{4,5},{5,4},{6,7},{7,6},{8,9},{9,8},{10,11... | collective-permute-start | bytes 442376 | tf_op jit(solution)/shard_map/ppermute | solution.py:56
  28.6 3.2 %collective-permute-start.7 = (bf16[144,512]{1,0:T(8,128)(2,1)S(1)}, bf16[144,512]{1,0:T(8,128)(2,1)S(1)}, u32[]{:S(2)}, u32[]{:S(2)}) collective-permute-start(bf16[144,512]{1,0:T(8,128)(2,1)S(1)} %collective-permute-done.1.refs_1_), channel_id=1, source_target_pairs={{0,1},{1,0},{2,3},{3,2},{4,5},{5,4},{6,7},{7,6},{8,9},{9,8},{10,11... | collective-permute-start | bytes 442376 | tf_op jit(solution)/shard_map/ppermute | solution.py:56
  30.3 1.4 %collective-permute-start.8 = (bf16[144,512]{1,0:T(8,128)(2,1)S(1)}, bf16[144,512]{1,0:T(8,128)(2,1)S(1)}, u32[]{:S(2)}, u32[]{:S(2)}) collective-permute-start(bf16[144,512]{1,0:T(8,128)(2,1)S(1)} %collective-permute-done.2.refs_2_), channel_id=1, source_target_pairs={{0,1},{1,0},{2,3},{3,2},{4,5},{5,4},{6,7},{7,6},{8,9},{9,8},{10,11... | collective-permute-start | bytes 442376 | tf_op jit(solution)/shard_map/ppermute | solution.py:56
  30.4 1.6 %collective-permute-start.9 = (bf16[144,512]{1,0:T(8,128)(2,1)S(1)}, bf16[144,512]{1,0:T(8,128)(2,1)S(1)}, u32[]{:S(2)}, u32[]{:S(2)}) collective-permute-start(bf16[144,512]{1,0:T(8,128)(2,1)S(1)} %collective-permute-done.3.refs_3_), channel_id=1, source_target_pairs={{0,1},{1,0},{2,3},{3,2},{4,5},{5,4},{6,7},{7,6},{8,9},{9,8},{10,11... | collective-permute-start | bytes 442376 | tf_op jit(solution)/shard_map/ppermute | solution.py:56
  34.1 20.4 %collective-permute-start.14 = (bf16[1024,256]{1,0:T(8,128)(2,1)S(1)}, bf16[1024,256]{1,0:T(8,128)(2,1)S(1)}, u32[]{:S(2)}, u32[]{:S(2)}) collective-permute-start(bf16[1024,256]{1,0:T(8,128)(2,1)S(1)} %get-tuple-element.73), channel_id=1, source_target_pairs={{0,4},{4,8},{8,12},{12,16},{16,20},{20,24},{24,28},{1,5},{5,9},{9,... | collective-permute-start | bytes 1572872 | tf_op jit(solution)/shard_map/ppermute | solution.py:60
  37.3 11.1 %collective-permute-start.17 = (bf16[48,256]{1,0:T(8,128)(2,1)S(1)}, bf16[48,256]{1,0:T(8,128)(2,1)S(1)}, u32[]{:S(2)}, u32[]{:S(2)}) collective-permute-start(bf16[48,256]{1,0:T(8,128)(2,1)S(1)} %get-tuple-element.74.refs_0_), channel_id=1, source_target_pairs={{0,24},{4,28},{8,16},{12,20},{16,8},{20,12},{24,0},{28,4},{1,25},{... | collective-permute-start | bytes 73736 | tf_op jit(solution)/shard_map/ppermute | solution.py:103
  40.0 8.5 %collective-permute-start.16 = (bf16[48,256]{1,0:T(8,128)(2,1)S(1)}, bf16[48,256]{1,0:T(8,128)(2,1)S(1)}, u32[]{:S(2)}, u32[]{:S(2)}) collective-permute-start(bf16[48,256]{1,0:T(8,128)(2,1)S(1)} %get-tuple-element.74.refs_0_), channel_id=1, source_target_pairs={{0,16},{4,20},{8,24},{12,28},{16,0},{20,4},{24,8},{28,12},{1,17},{... | collective-permute-start | bytes 73736 | tf_op jit(solution)/shard_map/ppermute | solution.py:103
  40.2 8.2 %collective-permute-start.15 = (bf16[48,256]{1,0:T(8,128)(2,1)S(1)}, bf16[48,256]{1,0:T(8,128)(2,1)S(1)}, u32[]{:S(2)}, u32[]{:S(2)}) collective-permute-start(bf16[48,256]{1,0:T(8,128)(2,1)S(1)} %get-tuple-element.74.refs_0_), channel_id=1, source_target_pairs={{0,8},{4,12},{8,0},{12,4},{16,24},{20,28},{24,16},{28,20},{1,9},{5... | collective-permute-start | bytes 73736 | tf_op jit(solution)/shard_map/ppermute | solution.py:103
  48.5 7.0 %copy-start.6 = (s32[8,4]{0,1:T(4,128)S(1)}, s32[8,4]{0,1:T(4,128)}, u32[]{:S(2)}) copy-start(s32[8,4]{0,1:T(4,128)} %param.15) | copy-start | bytes 388
  48.5 6.0 %collective-permute-start.18 = (bf16[192,256]{1,0:T(8,128)(2,1)S(1)}, bf16[192,256]{1,0:T(8,128)(2,1)S(1)}, u32[]{:S(2)}, u32[]{:S(2)}) collective-permute-start(bf16[192,256]{1,0:T(8,128)(2,1)S(1)} %stack.1.refs_0_), channel_id=1, source_target_pairs={{0,4},{4,0},{8,12},{12,8},{16,20},{20,16},{24,28},{28,24},{1,5},{5... | collective-permute-start | bytes 294920 | tf_op jit(solution)/shard_map/ppermute | solution.py:103
  58.6 12.5 %copy-start = (bf16[1024,256]{1,0:T(8,128)(2,1)S(1)}, bf16[1024,256]{1,0:T(8,128)(2,1)}, u32[]{:S(2)}) copy-start(bf16[1024,256]{1,0:T(8,128)(2,1)} %w_ref.3) | copy-start | bytes 1572868
  58.6 9.0 %collective-permute-start.19 = (bf16[512,256]{1,0:T(8,128)(2,1)S(1)}, bf16[512,256]{1,0:T(8,128)(2,1)S(1)}, u32[]{:S(2)}, u32[]{:S(2)}) collective-permute-start(bf16[512,256]{1,0:T(8,128)(2,1)S(1)} %rest.2.refs_0_), channel_id=1, source_target_pairs={{0,2},{2,0},{1,3},{3,1},{4,6},{6,4},{5,7},{7,5},{8,10},{10,8},{9,1... | collective-permute-start | bytes 786440 | tf_op jit(solution)/shard_map/ppermute | solution.py:56
  62.4 8.7 %collective-permute-start.20 = (bf16[512,256]{1,0:T(8,128)(2,1)S(1)}, bf16[512,256]{1,0:T(8,128)(2,1)S(1)}, u32[]{:S(2)}, u32[]{:S(2)}) collective-permute-start(bf16[512,256]{1,0:T(8,128)(2,1)S(1)} %rest.3.refs_0_), channel_id=1, source_target_pairs={{0,2},{2,0},{1,3},{3,1},{4,6},{6,4},{5,7},{7,5},{8,10},{10,8},{9,1... | collective-permute-start | bytes 786440 | tf_op jit(solution)/shard_map/ppermute | solution.py:56
  63.9 7.2 %collective-permute-start.23 = (bf16[512,256]{1,0:T(8,128)(2,1)S(1)}, bf16[512,256]{1,0:T(8,128)(2,1)S(1)}, u32[]{:S(2)}, u32[]{:S(2)}) collective-permute-start(bf16[512,256]{1,0:T(8,128)(2,1)S(1)} %rest.2.refs_0_), channel_id=1, source_target_pairs={{0,1},{1,0},{2,3},{3,2},{4,5},{5,4},{6,7},{7,6},{8,9},{9,8},{10,11... | collective-permute-start | bytes 786440 | tf_op jit(solution)/shard_map/ppermute | solution.py:56
  67.6 3.5 %collective-permute-start.24 = (bf16[512,256]{1,0:T(8,128)(2,1)S(1)}, bf16[512,256]{1,0:T(8,128)(2,1)S(1)}, u32[]{:S(2)}, u32[]{:S(2)}) collective-permute-start(bf16[512,256]{1,0:T(8,128)(2,1)S(1)} %collective-permute-done.19.refs_1_), channel_id=1, source_target_pairs={{0,1},{1,0},{2,3},{3,2},{4,5},{5,4},{6,7},{7,6},{8,9},{9,8},{10,11... | collective-permute-start | bytes 786440 | tf_op jit(solution)/shard_map/ppermute | solution.py:56
  67.6 4.8 %collective-permute-start.21 = (bf16[512,256]{1,0:T(8,128)(2,1)S(1)}, bf16[512,256]{1,0:T(8,128)(2,1)S(1)}, u32[]{:S(2)}, u32[]{:S(2)}) collective-permute-start(bf16[512,256]{1,0:T(8,128)(2,1)S(1)} %rest.3.refs_0_), channel_id=1, source_target_pairs={{0,1},{1,0},{2,3},{3,2},{4,5},{5,4},{6,7},{7,6},{8,9},{9,8},{10,11... | collective-permute-start | bytes 786440 | tf_op jit(solution)/shard_map/ppermute | solution.py:56
  71.1 1.5 %collective-permute-start.22 = (bf16[512,256]{1,0:T(8,128)(2,1)S(1)}, bf16[512,256]{1,0:T(8,128)(2,1)S(1)}, u32[]{:S(2)}, u32[]{:S(2)}) collective-permute-start(bf16[512,256]{1,0:T(8,128)(2,1)S(1)} %collective-permute-done.20.refs_4_.refs_1_), channel_id=1, source_target_pairs={{0,1},{1,0},{2,3},{3,2},{4,5},{5,4},{6,7},{7,6},{8,9},{9,8},{10,11... | collective-permute-start | bytes 786440 | tf_op jit(solution)/shard_map/ppermute | solution.py:56
  (2 other events, 3.6 us)

commit v11 on v10

--- a/solution.py
+++ b/solution.py
@@ -137,7 +137,7 @@
             jax.ShapeDtypeStruct((tall, half), BF),
             jax.ShapeDtypeStruct((tall, half), BF),
             jax.ShapeDtypeStruct((tall, half), BF),
-            jax.ShapeDtypeStruct((rows, half), BF),
+            jax.ShapeDtypeStruct((tall, half), BF),
             jax.ShapeDtypeStruct((tall, half), BF),
             jax.ShapeDtypeStruct((rows, width), BF),
         ),
@@ -151,8 +151,9 @@
     one, two, three, four, five = [by_core(block, route) for block, route in zip(blocks, routes)]
     prepared = prepare(own)
     one, _ = lax.optimization_barrier((one, prepared))
-    first_x = over_head(one, X_PAIRS)
+    first_x = over_head(stacked((one,), ((0, 0, rows, 0),), half, (three, four, five)), X_PAIRS)
     two, first_x = lax.optimization_barrier((two, first_x))
+    two = stacked((two,), ((0, 0, rows, 0),), half)
     far = [one, two]
     far_core = [over_head(part, CORE_PAIRS) for part in far]
     far_x = [first_x, over_head(two, X_PAIRS)]

time: 75.1 us -> 74.7 us (level); the launches traced: 73.9 us -> 74.4 us
  waiting for transfers between devices: 17.2 us -> 21.7 us
  starting transfers between devices: 30.4 us -> 26.5 us
    ppermute x15, waiting for transfers between devices: 7.95 us -> 12.7 us  [over_head(): return lax.ppermute(block, 'head', pairs)]
    ppermute x5, starting transfers between devices: 13.4 us -> 9.51 us  [by_core(): return lax.ppermute(block, ('seq', 'head'), pairs)]
    ppermute x15, starting transfers between devices: 5.98 us -> 7.32 us  [over_head(): return lax.ppermute(block, 'head', pairs)]
    ppermute x4, starting transfers between devices: 7.81 us -> 6.59 us  [by_distance(): lax.ppermute(block, 'seq', [(i, i ^ distance) for i in range(lax.axis_siz...]
where the time goes in v11:
time: 74.7 us; the launch traced here: 74.4 us
  starting transfers between devices  26.5 us (35%)
  Pallas kernels  25.1 us (34%)
  waiting for transfers between devices  21.7 us (29%)
  local copies, waits for them, and re-layouts  0.98 us (1%)
    ppermute x15, waiting for transfers between devices, over_head(): return lax.ppermute(block, 'head', pairs)  12.7 us
    ppermute x5, starting transfers between devices, by_core(): return lax.ppermute(block, ('seq', 'head'), pairs)  9.51 us
    ppermute x15, starting transfers between devices, over_head(): return lax.ppermute(block, 'head', pairs)  7.32 us
    ppermute x4, starting transfers between devices, by_distance(): lax.ppermute(block, 'seq', [(i, i ^ distance) for i in range(lax.axis_siz...  6.59 us
    pallas_call x2, Pallas kernels, local(): pl.pallas_call(functools.partial(rest_kernel, first, count), out_shape=sh...  6.33 us
    ppermute x5, waiting for transfers between devices, by_core(): return lax.ppermute(block, ('seq', 'head'), pairs)  6.33 us
    pallas_call x1, Pallas kernels, local(): pl.pallas_call(own_kernel, out_shape=(shape((group, tok_rows), F32), shap...  3.99 us
    ppermute x1, starting transfers between devices, to_next(): lax.ppermute(block, 'seq', [(i, i + 1) for i in range(lax.axis_size('seq'...  3.04 us
  transfers between devices with their start and end apart: 25, of which 10 were waited for; matrix products, arithmetic and copies ran while one was open for 0% of the time, Pallas kernels for 20%

profile of v11, /device:TPU:0, one launch (start us, length us, event | category | flops | bytes accessed | tf_op | source)
XLA Modules:
  0.0 74.4 jit_solution(7257274267535511831)
XLA Ops:
  0.0 2.7 %send.1 = (bf16[144,512]{1,0:T(8,128)(2,1)}, bf16[144,512]{1,0:T(8,128)(2,1)}, bf16[144,512]{1,0:T(8,128)(2,1)}, bf16[144,512]{1,0:T(8,128)(2,1)}, bf16[144,512]{1,0:T(8,128)(2,1)}, /*index=5*/bf16[128,1024]{1,0:T(8,128)(2,1)}) custom-call(bf16[1024,1024]{1,0:T(8,128)(2,1)} %tokens_ref.1, s32[1,512]{1,0:T(1,128)} %mask_ref.3), custom_call_target="tpu_custom_call" | custom-call | flops 1 | bytes 1 | tf_op jit(solution)/shard_map/send/pallas_call | solution.py:134
  2.7 6.0 %collective-permute-start = (bf16[144,512]{1,0:T(8,128)(2,1)}, bf16[144,512]{1,0:T(8,128)(2,1)S(1)}, u32[]{:S(2)}, u32[]{:S(2)}) collective-permute-start(bf16[144,512]{1,0:T(8,128)(2,1)} %get-tuple-element.53), channel_id=1, source_target_pairs={{0,28},{1,25},{2,30},{3,27},{4,24},{5,29},{6,26},{7,31},{8,20},{9,... | collective-permute-start | bytes 442376 | tf_op jit(solution)/shard_map/ppermute | solution.py:113
  8.8 2.0 %collective-permute-start.3 = (bf16[144,512]{1,0:T(8,128)(2,1)}, bf16[144,512]{1,0:T(8,128)(2,1)S(1)}, u32[]{:S(2)}, u32[]{:S(2)}) collective-permute-start(bf16[144,512]{1,0:T(8,128)(2,1)} %get-tuple-element.59), channel_id=1, source_target_pairs={{0,8},{1,9},{2,10},{3,11},{4,12},{5,13},{6,14},{7,15},{8,0},{9,1},... | collective-permute-start | bytes 442376 | tf_op jit(solution)/shard_map/ppermute | solution.py:113
  10.7 1.5 %collective-permute-start.4 = (bf16[144,512]{1,0:T(8,128)(2,1)}, bf16[144,512]{1,0:T(8,128)(2,1)S(1)}, u32[]{:S(2)}, u32[]{:S(2)}) collective-permute-start(bf16[144,512]{1,0:T(8,128)(2,1)} %get-tuple-element.60), channel_id=1, source_target_pairs={{0,4},{1,5},{2,6},{3,7},{4,0},{5,1},{6,2},{7,3},{8,12},{9,13},{10,... | collective-permute-start | bytes 442376 | tf_op jit(solution)/shard_map/ppermute | solution.py:113
  12.3 0.9 %copy-done.1 = bf16[128,1024]{1,0:T(8,128)(2,1)S(1)} copy-done((bf16[128,1024]{1,0:T(8,128)(2,1)S(1)}, bf16[128,1024]{1,0:T(8,128)(2,1)}, u32[]{:S(2)}) %copy-start.1) | copy-done | bytes 262168
  13.3 2.5 %prepare.1 = (bf16[1024,1024]{1,0:T(8,128)(2,1)S(1)}, bf16[1024,1024]{1,0:T(8,128)(2,1)S(1)}, bf16[672,1024]{1,0:T(8,128)(2,1)S(1)}, f32[160,128]{1,0:T(8,128)S(...) custom-call(s32[1,1024]{1,0:T(1,128)S(1)} %copy-done.9, ...), custom_call_target="tpu_custom_call" | custom-call | flops 1 | bytes 1 | tf_op jit(solution)/shard_map/prepare/pallas_call | solution.py:512
  15.7 3.9 %collective-permute-done.2.refs_1_.refs_2_.refs_8_ = bf16[144,512]{1,0:T(8,128)(2,1)S(1)} collective-permute-done((bf16[144,512]{1,0:T(8,128)(2,1)}, bf16[144,512]{1,0:T(8,128)(2,1)S(1)}, u32[]{:S(2)}, u32[]{:S(2)}) %collective-permute-start.2) | collective-permute-done | bytes 147488 | tf_op jit(solution)/shard_map/ppermute | solution.py:113
  19.6 2.4 %collective-permute-done.3.refs_2_.refs_9_ = bf16[144,512]{1,0:T(8,128)(2,1)S(1)} collective-permute-done((bf16[144,512]{1,0:T(8,128)(2,1)}, bf16[144,512]{1,0:T(8,128)(2,1)S(1)}, u32[]{:S(2)}, u32[]{:S(2)}) %collective-permute-start.3) | collective-permute-done | bytes 147488 | tf_op jit(solution)/shard_map/ppermute | solution.py:113
  22.1 1.6 %collective-permute-start.5 = (bf16[128,512]{1,0:T(8,128)(2,1)S(1)}, bf16[128,512]{1,0:T(8,128)(2,1)S(1)}, u32[]{:S(2)}, u32[]{:S(2)}) collective-permute-start(bf16[128,512]{1,0:T(8,128)(2,1)S(1)} %stack.3), channel_id=1, source_target_pairs={{0,2},{2,0},{1,3},{3,1},{4,6},{6,4},{5,7},{7,5},{8,10},{10,8},{9,1... | collective-permute-start | bytes 393224 | tf_op jit(solution)/shard_map/ppermute | solution.py:56
  24.2 3.0 %collective-permute-done.5.refs_2_ = bf16[128,512]{1,0:T(8,128)(2,1)S(1)} collective-permute-done((bf16[128,512]{1,0:T(8,128)(2,1)S(1)}, bf16[128,512]{1,0:T(8,128)(2,1)S(1)}, u32[]{:S(2)}, u32[]{:S(2)}) %collective-permute-start.5) | collective-permute-done | bytes 131104 | tf_op jit(solution)/shard_map/ppermute | solution.py:56
  27.1 1.6 %collective-permute-start.6 = (bf16[128,512]{1,0:T(8,128)(2,1)S(1)}, bf16[128,512]{1,0:T(8,128)(2,1)S(1)}, u32[]{:S(2)}, u32[]{:S(2)}) collective-permute-start(bf16[128,512]{1,0:T(8,128)(2,1)S(1)} %stack.4.refs_1_), channel_id=1, source_target_pairs={{0,2},{2,0},{1,3},{3,1},{4,6},{6,4},{5,7},{7,5},{8,10},{10,8},{9,1... | collective-permute-start | bytes 393224 | tf_op jit(solution)/shard_map/ppermute | solution.py:56
  29.2 1.2 %expand.1 = (bf16[1024,512]{1,0:T(8,128)(2,1)S(1)}, bf16[512,1024]{1,0:T(8,128)(2,1)S(1)}, f32[2048,128]{1,0:T(8,128)S(1)}) custom-call(f32[1024,128]{1,0:T(8,128)S(1)} %get-tuple-element.54.seen_ref, bf16[144,512]{1,0:T(8,128)(2,1)S(1)} %collective-permute-done.refs_0_, bf16[144,512]{1,0:T(8,128)(2,1)S(1)} %collective-permute-done.7.refs_1_.refs_4_, ...), custom_call_target="tpu_custom_call" | custom-call | flops 1 | bytes 1 | tf_op jit(solution)/shard_map/expand/pallas_call | solution.py:532
  30.4 1.7 %collective-permute-done.6.refs_3_ = bf16[128,512]{1,0:T(8,128)(2,1)S(1)} collective-permute-done((bf16[128,512]{1,0:T(8,128)(2,1)S(1)}, bf16[128,512]{1,0:T(8,128)(2,1)S(1)}, u32[]{:S(2)}, u32[]{:S(2)}) %collective-permute-start.6) | collective-permute-done | bytes 131104 | tf_op jit(solution)/shard_map/ppermute | solution.py:56
  32.2 0.5 collective-permute-start.10
  32.7 0.8 %collective-permute-done.9.refs_6_ = bf16[128,512]{1,0:T(8,128)(2,1)S(1)} collective-permute-done((bf16[128,512]{1,0:T(8,128)(2,1)S(1)}, bf16[128,512]{1,0:T(8,128)(2,1)S(1)}, u32[]{:S(2)}, u32[]{:S(2)}) %collective-permute-start.9) | collective-permute-done | bytes 131104 | tf_op jit(solution)/shard_map/ppermute | solution.py:56
  33.7 2.1 %project.1 = (bf16[1024,256]{1,0:T(8,128)(2,1)S(1)}, bf16[48,256]{1,0:T(8,128)(2,1)S(1)}, bf16[1024,256]{1,0:T(8,128)(2,1)S(1)}, bf16[256,1024]{1,0:T(8,128)(2,1)S(1)}, bf16[1024,1024]{1,0:T(8,128)(2,1)S(1)}) custom-call(bf16[144,512]{1,0:T(8,128)(2,1)S(1)} %collective-permute-done.refs_0_, bf16[128,512]{1,0:T(8,128)(2,1)S(1)} %stack.4.refs_1_, ...), custom_call_target="tpu_custom_call" | custom-call | flops 1 | bytes 1 | tf_op jit(solution)/shard_map/project/pallas_call | solution.py:549
  35.8 3.0 %collective-permute-start.14 = (bf16[1024,256]{1,0:T(8,128)(2,1)S(1)}, bf16[1024,256]{1,0:T(8,128)(2,1)S(1)}, u32[]{:S(2)}, u32[]{:S(2)}) collective-permute-start(bf16[1024,256]{1,0:T(8,128)(2,1)S(1)} %get-tuple-element.73), channel_id=1, source_target_pairs={{0,4},{4,8},{8,12},{12,16},{16,20},{20,24},{24,28},{1,5},{5,9},{9,... | collective-permute-start | bytes 1572872 | tf_op jit(solution)/shard_map/ppermute | solution.py:60
  38.9 1.9 %collective-permute-start.17 = (bf16[48,256]{1,0:T(8,128)(2,1)S(1)}, bf16[48,256]{1,0:T(8,128)(2,1)S(1)}, u32[]{:S(2)}, u32[]{:S(2)}) collective-permute-start(bf16[48,256]{1,0:T(8,128)(2,1)S(1)} %get-tuple-element.74.refs_0_), channel_id=1, source_target_pairs={{0,24},{4,28},{8,16},{12,20},{16,8},{20,12},{24,0},{28,4},{1,25},{... | collective-permute-start | bytes 73736 | tf_op jit(solution)/shard_map/ppermute | solution.py:103
  40.7 2.6 %collective-permute-start.15 = (bf16[48,256]{1,0:T(8,128)(2,1)S(1)}, bf16[48,256]{1,0:T(8,128)(2,1)S(1)}, u32[]{:S(2)}, u32[]{:S(2)}) collective-permute-start(bf16[48,256]{1,0:T(8,128)(2,1)S(1)} %get-tuple-element.74.refs_0_), channel_id=1, source_target_pairs={{0,8},{4,12},{8,0},{12,4},{16,24},{20,28},{24,16},{28,20},{1,9},{5... | collective-permute-start | bytes 73736 | tf_op jit(solution)/shard_map/ppermute | solution.py:103
  43.3 2.7 %order.1 = (bf16[256,1024]{1,0:T(8,128)(2,1)S(1)}, bf16[256,1024]{1,0:T(8,128)(2,1)S(1)}, bf16[1024,256]{1,0:T(8,128)(2,1)S(1)}, bf16[128,256]{1,0:T(8,128)(2,1)S(1)}, bf16[256,128]{1,0:T(8,128)(2,1)S(1)}) custom-call(bf16[1024,1024]{1,0:T(8,128)(2,1)S(1)} %get-tuple-element.47.p_ref, bf16[1024,1024]{1,0:T(8,128)(2,1)S(1)} %get-tuple-element.48.pt_ref, ...), custom_call_target="tpu_custom_call" | custom-call | flops 1 | bytes 1 | tf_op jit(solution)/shard_map/order/pallas_call | solution.py:568
  46.0 4.0 %own.1 = (f32[256,1024]{1,0:T(8,128)S(1)}, f32[256,1024]{1,0:T(8,128)S(1)}, f32[8,512]{1,0:T(8,128)S(1)}, f32[8,512]{1,0:T(8,128)S(1)}) custom-call(f32[4,4]{1,0:T(4,128)S(1)} %copy-done.6, bf16[256,1024]{1,0:T(8,128)(2,1)S(1)} %get-tuple-element.70.qt_ref, bf16[1024,256]{1,0:T(8,128)(2,1)S(1)} %get-tuple-element.71.k_ref, ...), custom_call_target="tpu_custom_call" | custom-call | flops 1 | bytes 1 | tf_op jit(solution)/shard_map/own/pallas_call | solution.py:584
  50.1 2.1 %collective-permute-start.18 = (bf16[192,256]{1,0:T(8,128)(2,1)S(1)}, bf16[192,256]{1,0:T(8,128)(2,1)S(1)}, u32[]{:S(2)}, u32[]{:S(2)}) collective-permute-start(bf16[192,256]{1,0:T(8,128)(2,1)S(1)} %stack.5.refs_0_), channel_id=1, source_target_pairs={{0,4},{4,0},{8,12},{12,8},{16,20},{20,16},{24,28},{28,24},{1,5},{5... | collective-permute-start | bytes 294920 | tf_op jit(solution)/shard_map/ppermute | solution.py:103
  52.2 2.6 %collective-permute-done.18.refs_1_ = bf16[192,256]{1,0:T(8,128)(2,1)S(1)} collective-permute-done((bf16[192,256]{1,0:T(8,128)(2,1)S(1)}, bf16[192,256]{1,0:T(8,128)(2,1)S(1)}, u32[]{:S(2)}, u32[]{:S(2)}) %collective-permute-start.18) | collective-permute-done | bytes 98336 | tf_op jit(solution)/shard_map/ppermute | solution.py:103
  54.8 0.9 %window.1 = (bf16[2048,256]{1,0:T(8,128)(2,1)S(1)}, bf16[256,2048]{1,0:T(8,128)(2,1)S(1)}, bf16[64,256]{1,0:T(8,128)(2,1)S(1)}, bf16[256,64]{1,0:T(8,128)(2,1)S(1)}) custom-call(bf16[1024,256]{1,0:T(8,128)(2,1)S(1)} %get-tuple-element.71.k_ref, bf16[256,1024]{1,0:T(8,128)(2,1)S(1)} %get-tuple-element.72.vt_ref, ...), custom_call_target="tpu_custom_call" | custom-call | flops 1 | bytes 1 | tf_op jit(solution)/shard_map/window/pallas_call | solution.py:612
  55.8 3.2 %rest.2.refs_0_ = bf16[512,256]{1,0:T(8,128)(2,1)S(1)} custom-call(s32[4,8]{1,0:T(4,128)S(1)} %bitcast.1, f32[4,4]{1,0:T(4,128)S(1)} %copy-done.6, bf16[256,1024]{1,0:T(8,128)(2,1)S(1)} %get-tuple-element.70.qt_ref, bf16[2048,256]{1,0:T(8,128)(2,1)S(1)} %get-tuple-element.78.kw_ref, bf16[256,2048]{1,0:T(8,128)(2,1)S(1)} %get-tuple-element.79.vw_ref, ...), custom_call_target="tpu_custom_call" | custom-call | flops 1 | bytes 1 | tf_op jit(solution)/shard_map/rest/pallas_call | solution.py:654
  58.9 1.5 %collective-permute-start.19 = (bf16[512,256]{1,0:T(8,128)(2,1)S(1)}, bf16[512,256]{1,0:T(8,128)(2,1)S(1)}, u32[]{:S(2)}, u32[]{:S(2)}) collective-permute-start(bf16[512,256]{1,0:T(8,128)(2,1)S(1)} %rest.2.refs_0_), channel_id=1, source_target_pairs={{0,2},{2,0},{1,3},{3,1},{4,6},{6,4},{5,7},{7,5},{8,10},{10,8},{9,1... | collective-permute-start | bytes 786440 | tf_op jit(solution)/shard_map/ppermute | solution.py:56
  60.5 3.2 %rest.3.refs_0_ = bf16[512,256]{1,0:T(8,128)(2,1)S(1)} custom-call(s32[4,8]{1,0:T(4,128)S(1)} %bitcast.2, f32[4,4]{1,0:T(4,128)S(1)} %copy-done.6, bf16[256,1024]{1,0:T(8,128)(2,1)S(1)} %get-tuple-element.70.qt_ref, bf16[2048,256]{1,0:T(8,128)(2,1)S(1)} %get-tuple-element.78.kw_ref, bf16[256,2048]{1,0:T(8,128)(2,1)S(1)} %get-tuple-element.79.vw_ref, ...), custom_call_target="tpu_custom_call" | custom-call | flops 1 | bytes 1 | tf_op jit(solution)/shard_map/rest/pallas_call | solution.py:654
  63.6 0.6 collective-permute-start.20
  64.3 2.9 %collective-permute-done.19.refs_1_ = bf16[512,256]{1,0:T(8,128)(2,1)S(1)} collective-permute-done((bf16[512,256]{1,0:T(8,128)(2,1)S(1)}, bf16[512,256]{1,0:T(8,128)(2,1)S(1)}, u32[]{:S(2)}, u32[]{:S(2)}) %collective-permute-start.19) | collective-permute-done | bytes 262176 | tf_op jit(solution)/shard_map/ppermute | solution.py:56
  67.7 3.9 %collective-permute-done.20.refs_4_.refs_1_ = bf16[512,256]{1,0:T(8,128)(2,1)S(1)} collective-permute-done((bf16[512,256]{1,0:T(8,128)(2,1)S(1)}, bf16[512,256]{1,0:T(8,128)(2,1)S(1)}, u32[]{:S(2)}, u32[]{:S(2)}) %collective-permute-start.20) | collective-permute-done | bytes 262176 | tf_op jit(solution)/shard_map/ppermute | solution.py:56
  71.6 1.3 %output.2.refs_4_ = bf16[1024,256]{1,0:T(8,128)(2,1)} custom-call(bf16[1024,256]{1,0:T(8,128)(2,1)S(1)} %copy-done, bf16[512,256]{1,0:T(8,128)(2,1)S(1)} %rest.2.refs_0_, bf16[512,256]{1,0:T(8,128)(2,1)S(1)} %collective-permute-done.19.refs_1_, bf16[512,256]{1,0:T(8,128)(2,1)S(1)} %collective-permute-done.23.refs_2_, ...), custom_call_target="tpu_custom_call" | custom-call | flops 1 | bytes 1 | tf_op jit(solution)/shard_map/output/pallas_call | solution.py:639
  73.1 1.3 %output.3 = bf16[1024,256]{1,0:T(8,128)(2,1)} custom-call(bf16[1024,256]{1,0:T(8,128)(2,1)S(1)} %copy-done, bf16[512,256]{1,0:T(8,128)(2,1)S(1)} %rest.3.refs_0_, bf16[512,256]{1,0:T(8,128)(2,1)S(1)} %collective-permute-done.20.refs_4_.refs_1_, bf16[512,256]{1,0:T(8,128)(2,1)S(1)} %collective-permute-done.21.refs_2_, ...), custom_call_target="tpu_custom_call", output_to_operand_aliasing={{}: (5, {})} | custom-call | flops 1 | bytes 1 | tf_op jit(solution)/shard_map/output/pallas_call | solution.py:639
  (52 shorter events, 2.0 us)
Async XLA Ops:
  0.0 12.3 %copy-start.8 = (s32[1,512]{1,0:T(1,128)S(1)}, s32[1,512]{1,0:T(1,128)}, u32[]{:S(2)}) copy-start(s32[1,512]{1,0:T(1,128)} %mask_ref.3) | copy-start | bytes 6148
  0.0 12.3 %copy-start.9 = (s32[1,1024]{1,0:T(1,128)S(1)}, s32[1,1024]{1,0:T(1,128)}, u32[]{:S(2)}) copy-start(s32[1,1024]{1,0:T(1,128)} %order_ref.1) | copy-start | bytes 12292
  0.0 12.3 %copy-start.4 = (bf16[1024,256]{1,0:T(8,128)(2,1)S(1)}, bf16[1024,256]{1,0:T(8,128)(2,1)}, u32[]{:S(2)}) copy-start(bf16[1024,256]{1,0:T(8,128)(2,1)} %wv_ref.1) | copy-start | bytes 1572868
  0.0 12.3 %copy-start.5 = (bf16[1024,256]{1,0:T(8,128)(2,1)S(1)}, bf16[1024,256]{1,0:T(8,128)(2,1)}, u32[]{:S(2)}) copy-start(bf16[1024,256]{1,0:T(8,128)(2,1)} %wk_in.1) | copy-start | bytes 1572868
  0.0 12.3 %copy-start.3 = (bf16[1024,256]{1,0:T(8,128)(2,1)S(1)}, bf16[1024,256]{1,0:T(8,128)(2,1)}, u32[]{:S(2)}) copy-start(bf16[1024,256]{1,0:T(8,128)(2,1)} %wq_ref.1) | copy-start | bytes 1572868
  2.7 13.0 %collective-permute-start = (bf16[144,512]{1,0:T(8,128)(2,1)}, bf16[144,512]{1,0:T(8,128)(2,1)S(1)}, u32[]{:S(2)}, u32[]{:S(2)}) collective-permute-start(bf16[144,512]{1,0:T(8,128)(2,1)} %get-tuple-element.53), channel_id=1, source_target_pairs={{0,28},{1,25},{2,30},{3,27},{4,24},{5,29},{6,26},{7,31},{8,20},{9,... | collective-permute-start | bytes 442376 | tf_op jit(solution)/shard_map/ppermute | solution.py:113
  8.8 10.9 %collective-permute-start.2 = (bf16[144,512]{1,0:T(8,128)(2,1)}, bf16[144,512]{1,0:T(8,128)(2,1)S(1)}, u32[]{:S(2)}, u32[]{:S(2)}) collective-permute-start(bf16[144,512]{1,0:T(8,128)(2,1)} %get-tuple-element.58), channel_id=1, source_target_pairs={{0,12},{1,13},{2,14},{3,15},{4,8},{5,9},{6,10},{7,11},{8,4},{9,5},... | collective-permute-start | bytes 442376 | tf_op jit(solution)/shard_map/ppermute | solution.py:113
  8.8 13.3 %collective-permute-start.3 = (bf16[144,512]{1,0:T(8,128)(2,1)}, bf16[144,512]{1,0:T(8,128)(2,1)S(1)}, u32[]{:S(2)}, u32[]{:S(2)}) collective-permute-start(bf16[144,512]{1,0:T(8,128)(2,1)} %get-tuple-element.59), channel_id=1, source_target_pairs={{0,8},{1,9},{2,10},{3,11},{4,12},{5,13},{6,14},{7,15},{8,0},{9,1},... | collective-permute-start | bytes 442376 | tf_op jit(solution)/shard_map/ppermute | solution.py:113
  10.7 11.3 %collective-permute-start.4 = (bf16[144,512]{1,0:T(8,128)(2,1)}, bf16[144,512]{1,0:T(8,128)(2,1)S(1)}, u32[]{:S(2)}, u32[]{:S(2)}) collective-permute-start(bf16[144,512]{1,0:T(8,128)(2,1)} %get-tuple-element.60), channel_id=1, source_target_pairs={{0,4},{1,5},{2,6},{3,7},{4,0},{5,1},{6,2},{7,3},{8,12},{9,13},{10,... | collective-permute-start | bytes 442376 | tf_op jit(solution)/shard_map/ppermute | solution.py:113
  12.3 11.9 %collective-permute-start.1 = (bf16[144,512]{1,0:T(8,128)(2,1)}, bf16[144,512]{1,0:T(8,128)(2,1)S(1)}, u32[]{:S(2)}, u32[]{:S(2)}) collective-permute-start(bf16[144,512]{1,0:T(8,128)(2,1)} %get-tuple-element.57), channel_id=1, source_target_pairs={{0,20},{1,17},{2,22},{3,19},{4,16},{5,21},{6,18},{7,23},{8,28},{9,... | collective-permute-start | bytes 442376 | tf_op jit(solution)/shard_map/ppermute | solution.py:113
  13.2 20.5 %copy-start.2 = (bf16[128,1024]{1,0:T(8,128)(2,1)S(1)}, bf16[128,1024]{1,0:T(8,128)(2,1)}, u32[]{:S(2)}) copy-start(bf16[128,1024]{1,0:T(8,128)(2,1)} %get-tuple-element.46.early_ref.refs_14_) | copy-start | bytes 786436
  22.1 5.0 %collective-permute-start.5 = (bf16[128,512]{1,0:T(8,128)(2,1)S(1)}, bf16[128,512]{1,0:T(8,128)(2,1)S(1)}, u32[]{:S(2)}, u32[]{:S(2)}) collective-permute-start(bf16[128,512]{1,0:T(8,128)(2,1)S(1)} %stack.3), channel_id=1, source_target_pairs={{0,2},{2,0},{1,3},{3,1},{4,6},{6,4},{5,7},{7,5},{8,10},{10,8},{9,1... | collective-permute-start | bytes 393224 | tf_op jit(solution)/shard_map/ppermute | solution.py:56
  23.6 5.6 %collective-permute-start.7 = (bf16[144,512]{1,0:T(8,128)(2,1)S(1)}, bf16[144,512]{1,0:T(8,128)(2,1)S(1)}, u32[]{:S(2)}, u32[]{:S(2)}) collective-permute-start(bf16[144,512]{1,0:T(8,128)(2,1)S(1)} %collective-permute-done.refs_0_), channel_id=1, source_target_pairs={{0,1},{1,0},{2,3},{3,2},{4,5},{5,4},{6,7},{7,6},{8,9},{9,8},{10,11... | collective-permute-start | bytes 442376 | tf_op jit(solution)/shard_map/ppermute | solution.py:56
  23.6 8.5 %collective-permute-start.11 = (bf16[144,512]{1,0:T(8,128)(2,1)S(1)}, bf16[144,512]{1,0:T(8,128)(2,1)S(1)}, u32[]{:S(2)}, u32[]{:S(2)}) collective-permute-start(bf16[144,512]{1,0:T(8,128)(2,1)S(1)} %collective-permute-done.2.refs_1_.refs_2_.refs_8_), channel_id=1, source_target_pairs={{0,1},{1,0},{2,3},{3,2},{4,5},{5,4},{6,7},{7,6},{8,9},{9,8},{10,11... | collective-permute-start | bytes 442376 | tf_op jit(solution)/shard_map/ppermute | solution.py:56
  27.1 5.0 %collective-permute-start.6 = (bf16[128,512]{1,0:T(8,128)(2,1)S(1)}, bf16[128,512]{1,0:T(8,128)(2,1)S(1)}, u32[]{:S(2)}, u32[]{:S(2)}) collective-permute-start(bf16[128,512]{1,0:T(8,128)(2,1)S(1)} %stack.4.refs_1_), channel_id=1, source_target_pairs={{0,2},{2,0},{1,3},{3,1},{4,6},{6,4},{5,7},{7,5},{8,10},{10,8},{9,1... | collective-permute-start | bytes 393224 | tf_op jit(solution)/shard_map/ppermute | solution.py:56
  28.7 4.0 %collective-permute-start.12 = (bf16[144,512]{1,0:T(8,128)(2,1)S(1)}, bf16[144,512]{1,0:T(8,128)(2,1)S(1)}, u32[]{:S(2)}, u32[]{:S(2)}) collective-permute-start(bf16[144,512]{1,0:T(8,128)(2,1)S(1)} %collective-permute-done.3.refs_2_.refs_9_), channel_id=1, source_target_pairs={{0,1},{1,0},{2,3},{3,2},{4,5},{5,4},{6,7},{7,6},{8,9},{9,8},{10,11... | collective-permute-start | bytes 442376 | tf_op jit(solution)/shard_map/ppermute | solution.py:56
  28.7 4.0 %collective-permute-start.13 = (bf16[144,512]{1,0:T(8,128)(2,1)S(1)}, bf16[144,512]{1,0:T(8,128)(2,1)S(1)}, u32[]{:S(2)}, u32[]{:S(2)}) collective-permute-start(bf16[144,512]{1,0:T(8,128)(2,1)S(1)} %collective-permute-done.4.refs_3_.refs_10_), channel_id=1, source_target_pairs={{0,1},{1,0},{2,3},{3,2},{4,5},{5,4},{6,7},{7,6},{8,9},{9,8},{10,11... | collective-permute-start | bytes 442376 | tf_op jit(solution)/shard_map/ppermute | solution.py:56
  29.2 3.5 %collective-permute-start.8 = (bf16[128,512]{1,0:T(8,128)(2,1)S(1)}, bf16[128,512]{1,0:T(8,128)(2,1)S(1)}, u32[]{:S(2)}, u32[]{:S(2)}) collective-permute-start(bf16[128,512]{1,0:T(8,128)(2,1)S(1)} %stack.4.refs_1_), channel_id=1, source_target_pairs={{0,1},{1,0},{2,3},{3,2},{4,5},{5,4},{6,7},{7,6},{8,9},{9,8},{10,11... | collective-permute-start | bytes 393224 | tf_op jit(solution)/shard_map/ppermute | solution.py:56
  32.2 1.3 %collective-permute-start.9 = (bf16[128,512]{1,0:T(8,128)(2,1)S(1)}, bf16[128,512]{1,0:T(8,128)(2,1)S(1)}, u32[]{:S(2)}, u32[]{:S(2)}) collective-permute-start(bf16[128,512]{1,0:T(8,128)(2,1)S(1)} %collective-permute-done.5.refs_2_), channel_id=1, source_target_pairs={{0,1},{1,0},{2,3},{3,2},{4,5},{5,4},{6,7},{7,6},{8,9},{9,8},{10,11... | collective-permute-start | bytes 393224 | tf_op jit(solution)/shard_map/ppermute | solution.py:56
  32.2 1.5 %collective-permute-start.10 = (bf16[128,512]{1,0:T(8,128)(2,1)S(1)}, bf16[128,512]{1,0:T(8,128)(2,1)S(1)}, u32[]{:S(2)}, u32[]{:S(2)}) collective-permute-start(bf16[128,512]{1,0:T(8,128)(2,1)S(1)} %collective-permute-done.6.refs_3_), channel_id=1, source_target_pairs={{0,1},{1,0},{2,3},{3,2},{4,5},{5,4},{6,7},{7,6},{8,9},{9,8},{10,11... | collective-permute-start | bytes 393224 | tf_op jit(solution)/shard_map/ppermute | solution.py:56
  35.8 19.0 %collective-permute-start.14 = (bf16[1024,256]{1,0:T(8,128)(2,1)S(1)}, bf16[1024,256]{1,0:T(8,128)(2,1)S(1)}, u32[]{:S(2)}, u32[]{:S(2)}) collective-permute-start(bf16[1024,256]{1,0:T(8,128)(2,1)S(1)} %get-tuple-element.73), channel_id=1, source_target_pairs={{0,4},{4,8},{8,12},{12,16},{16,20},{20,24},{24,28},{1,5},{5,9},{9,... | collective-permute-start | bytes 1572872 | tf_op jit(solution)/shard_map/ppermute | solution.py:60
  38.9 11.1 %collective-permute-start.17 = (bf16[48,256]{1,0:T(8,128)(2,1)S(1)}, bf16[48,256]{1,0:T(8,128)(2,1)S(1)}, u32[]{:S(2)}, u32[]{:S(2)}) collective-permute-start(bf16[48,256]{1,0:T(8,128)(2,1)S(1)} %get-tuple-element.74.refs_0_), channel_id=1, source_target_pairs={{0,24},{4,28},{8,16},{12,20},{16,8},{20,12},{24,0},{28,4},{1,25},{... | collective-permute-start | bytes 73736 | tf_op jit(solution)/shard_map/ppermute | solution.py:103
  40.7 9.3 %collective-permute-start.16 = (bf16[48,256]{1,0:T(8,128)(2,1)S(1)}, bf16[48,256]{1,0:T(8,128)(2,1)S(1)}, u32[]{:S(2)}, u32[]{:S(2)}) collective-permute-start(bf16[48,256]{1,0:T(8,128)(2,1)S(1)} %get-tuple-element.74.refs_0_), channel_id=1, source_target_pairs={{0,16},{4,20},{8,24},{12,28},{16,0},{20,4},{24,8},{28,12},{1,17},{... | collective-permute-start | bytes 73736 | tf_op jit(solution)/shard_map/ppermute | solution.py:103
  40.7 9.3 %collective-permute-start.15 = (bf16[48,256]{1,0:T(8,128)(2,1)S(1)}, bf16[48,256]{1,0:T(8,128)(2,1)S(1)}, u32[]{:S(2)}, u32[]{:S(2)}) collective-permute-start(bf16[48,256]{1,0:T(8,128)(2,1)S(1)} %get-tuple-element.74.refs_0_), channel_id=1, source_target_pairs={{0,8},{4,12},{8,0},{12,4},{16,24},{20,28},{24,16},{28,20},{1,9},{5... | collective-permute-start | bytes 73736 | tf_op jit(solution)/shard_map/ppermute | solution.py:103
  50.1 4.7 %collective-permute-start.18 = (bf16[192,256]{1,0:T(8,128)(2,1)S(1)}, bf16[192,256]{1,0:T(8,128)(2,1)S(1)}, u32[]{:S(2)}, u32[]{:S(2)}) collective-permute-start(bf16[192,256]{1,0:T(8,128)(2,1)S(1)} %stack.5.refs_0_), channel_id=1, source_target_pairs={{0,4},{4,0},{8,12},{12,8},{16,20},{20,16},{24,28},{28,24},{1,5},{5... | collective-permute-start | bytes 294920 | tf_op jit(solution)/shard_map/ppermute | solution.py:103
  58.9 12.7 %copy-start = (bf16[1024,256]{1,0:T(8,128)(2,1)S(1)}, bf16[1024,256]{1,0:T(8,128)(2,1)}, u32[]{:S(2)}) copy-start(bf16[1024,256]{1,0:T(8,128)(2,1)} %w_ref.3) | copy-start | bytes 1572868
  58.9 8.2 %collective-permute-start.19 = (bf16[512,256]{1,0:T(8,128)(2,1)S(1)}, bf16[512,256]{1,0:T(8,128)(2,1)S(1)}, u32[]{:S(2)}, u32[]{:S(2)}) collective-permute-start(bf16[512,256]{1,0:T(8,128)(2,1)S(1)} %rest.2.refs_0_), channel_id=1, source_target_pairs={{0,2},{2,0},{1,3},{3,1},{4,6},{6,4},{5,7},{7,5},{8,10},{10,8},{9,1... | collective-permute-start | bytes 786440 | tf_op jit(solution)/shard_map/ppermute | solution.py:56
  63.6 8.0 %collective-permute-start.20 = (bf16[512,256]{1,0:T(8,128)(2,1)S(1)}, bf16[512,256]{1,0:T(8,128)(2,1)S(1)}, u32[]{:S(2)}, u32[]{:S(2)}) collective-permute-start(bf16[512,256]{1,0:T(8,128)(2,1)S(1)} %rest.3.refs_0_), channel_id=1, source_target_pairs={{0,2},{2,0},{1,3},{3,1},{4,6},{6,4},{5,7},{7,5},{8,10},{10,8},{9,1... | collective-permute-start | bytes 786440 | tf_op jit(solution)/shard_map/ppermute | solution.py:56
  64.3 7.3 %collective-permute-start.23 = (bf16[512,256]{1,0:T(8,128)(2,1)S(1)}, bf16[512,256]{1,0:T(8,128)(2,1)S(1)}, u32[]{:S(2)}, u32[]{:S(2)}) collective-permute-start(bf16[512,256]{1,0:T(8,128)(2,1)S(1)} %rest.2.refs_0_), channel_id=1, source_target_pairs={{0,1},{1,0},{2,3},{3,2},{4,5},{5,4},{6,7},{7,6},{8,9},{9,8},{10,11... | collective-permute-start | bytes 786440 | tf_op jit(solution)/shard_map/ppermute | solution.py:56
  67.1 4.5 %collective-permute-start.24 = (bf16[512,256]{1,0:T(8,128)(2,1)S(1)}, bf16[512,256]{1,0:T(8,128)(2,1)S(1)}, u32[]{:S(2)}, u32[]{:S(2)}) collective-permute-start(bf16[512,256]{1,0:T(8,128)(2,1)S(1)} %collective-permute-done.19.refs_1_), channel_id=1, source_target_pairs={{0,1},{1,0},{2,3},{3,2},{4,5},{5,4},{6,7},{7,6},{8,9},{9,8},{10,11... | collective-permute-start | bytes 786440 | tf_op jit(solution)/shard_map/ppermute | solution.py:56
  67.1 5.8 %collective-permute-start.21 = (bf16[512,256]{1,0:T(8,128)(2,1)S(1)}, bf16[512,256]{1,0:T(8,128)(2,1)S(1)}, u32[]{:S(2)}, u32[]{:S(2)}) collective-permute-start(bf16[512,256]{1,0:T(8,128)(2,1)S(1)} %rest.3.refs_0_), channel_id=1, source_target_pairs={{0,1},{1,0},{2,3},{3,2},{4,5},{5,4},{6,7},{7,6},{8,9},{9,8},{10,11... | collective-permute-start | bytes 786440 | tf_op jit(solution)/shard_map/ppermute | solution.py:56
  71.6 1.5 %collective-permute-start.22 = (bf16[512,256]{1,0:T(8,128)(2,1)S(1)}, bf16[512,256]{1,0:T(8,128)(2,1)S(1)}, u32[]{:S(2)}, u32[]{:S(2)}) collective-permute-start(bf16[512,256]{1,0:T(8,128)(2,1)S(1)} %collective-permute-done.20.refs_4_.refs_1_), channel_id=1, source_target_pairs={{0,1},{1,0},{2,3},{3,2},{4,5},{5,4},{6,7},{7,6},{8,9},{9,8},{10,11... | collective-permute-start | bytes 786440 | tf_op jit(solution)/shard_map/ppermute | solution.py:56
  (3 other events, 9.4 us)

commit v12 on v11

--- a/solution.py
+++ b/solution.py
@@ -75,7 +75,7 @@
         start = pl.multiple_of(side * half, half)
         out[:rows] = tokens_ref[pl.ds(row, rows), pl.ds(start, half)]
         if out.shape[0] > rows:
-            out[rows:] = code[: out.shape[0] - rows]
+            out[rows : rows + CODE_ROWS] = code
     own[...] = tokens_ref[pl.ds(pl.multiple_of(slab * rows, rows), rows)]
 
 
@@ -127,7 +127,7 @@
         third = over_head(first, X_PAIRS)
         second = over_head(first, CORE_PAIRS)
         fourth = over_head(third, CORE_PAIRS)
-        prepared = prepare(first)
+        prepared = prepare()
         return [first, third, second, fourth], prepared, expand(prepared, [to_next(mask_ids)])
     half = width // 2
     tall = rows + CODE_ROWS
@@ -149,7 +149,7 @@
     )(tokens, mask_ids)
     routes = ((7, 6), (5, 4), (3, 3), (2, 2), (1, 1))
     one, two, three, four, five = [by_core(block, route) for block, route in zip(blocks, routes)]
-    prepared = prepare(own)
+    prepared = prepare()
     one, _ = lax.optimization_barrier((one, prepared))
     first_x = over_head(stacked((one,), ((0, 0, rows, 0),), half, (three, four, five)), X_PAIRS)
     two, first_x = lax.optimization_barrier((two, first_x))
@@ -181,7 +181,7 @@
 
 
 def prepare_kernel(
-    order_ref, mask_ref, wq_ref, wv_ref, wk_in, early_ref,
+    order_ref, mask_ref, wq_ref, wv_ref, wk_in,
     p_ref, pt_ref, sel_ref, fcol_ref, frow_ref, bias_ref, wt_ref, wk_ref,
 ):
     slab, slabs = lax.axis_index("seq"), lax.axis_size("seq")
@@ -508,7 +508,7 @@
     shape = jax.ShapeDtypeStruct
     params = pltpu.CompilerParams(vmem_limit_bytes=VMEM_LIMIT)
 
-    def prepare(early):
+    def prepare():
         return pl.pallas_call(
             prepare_kernel,
             out_shape=(
@@ -521,12 +521,12 @@
                 shape((2 * group, width), BF),
                 shape((width, group), BF),
             ),
-            in_specs=vmem_specs(5) + [pl.BlockSpec(memory_space=pl.ANY)],
+            in_specs=vmem_specs(5),
             out_specs=vmem_specs(8),
             compiler_params=params,
             cost_estimate=COST,
             name="prepare",
-        )(order, mask_ids, w_query, w_value, w_key, early)
+        )(order, mask_ids, w_query, w_value, w_key)
 
     def expand(prepared, sources):
         return pl.pallas_call(
@@ -563,6 +563,7 @@
     )(*pieces, w_t, w_k, select, f_col)
     if slabs == 8:
         lined = [summ] + [by_distance(summ, d) for d in (2, 4, 6)]
+        comp, *lined = lax.optimization_barrier((comp, *lined))
     comp_before = to_next(comp)
 
     q_t, v_t, keys, near_k, near_vt = pl.pallas_call(

time: 74.7 us -> 79.9 us (1.070)
  the two profiles are of different devices: /device:TPU:0 before, /device:TPU:9 now
where the time goes in v12:
time: 79.9 us; the launch traced here: 79.8 us
  starting transfers between devices  28.4 us (36%)
  waiting for transfers between devices  26 us (33%)
  Pallas kernels  25.1 us (31%)
    ppermute x15, starting transfers between devices, over_head(): return lax.ppermute(block, 'head', pairs)  15 us
    ppermute x4, waiting for transfers between devices, by_distance(): lax.ppermute(block, 'seq', [(i, i ^ distance) for i in range(lax.axis_siz...  10.5 us
    ppermute x5, waiting for transfers between devices, by_core(): return lax.ppermute(block, ('seq', 'head'), pairs)  7.94 us
    ppermute x15, waiting for transfers between devices, over_head(): return lax.ppermute(block, 'head', pairs)  7.53 us
    pallas_call x2, Pallas kernels, local(): pl.pallas_call(functools.partial(rest_kernel, first, count), out_shape=sh...  6.32 us
    ppermute x4, starting transfers between devices, by_distance(): lax.ppermute(block, 'seq', [(i, i ^ distance) for i in range(lax.axis_siz...  5.7 us
    ppermute x5, starting transfers between devices, by_core(): return lax.ppermute(block, ('seq', 'head'), pairs)  5.02 us
    pallas_call x1, Pallas kernels, local(): pl.pallas_call(own_kernel, out_shape=(shape((group, tok_rows), F32), shap...  3.99 us
  transfers between devices with their start and end apart: 25, of which 10 were waited for; matrix products, arithmetic and copies ran while one was open for 0% of the time, Pallas kernels for 19%

profile of v12, /device:TPU:9, one launch (start us, length us, event | category | flops | bytes accessed | tf_op | source)
XLA Modules:
  0.0 79.8 jit_solution(8402919845626277737)
XLA Ops:
  0.0 2.7 %send.1 = (bf16[144,512]{1,0:T(8,128)(2,1)}, bf16[144,512]{1,0:T(8,128)(2,1)}, bf16[144,512]{1,0:T(8,128)(2,1)}, bf16[144,512]{1,0:T(8,128)(2,1)}, bf16[144,512]{1,0:T(8,128)(2,1)}, /*index=5*/bf16[128,1024]{1,0:T(8,128)(2,1)}) custom-call(bf16[1024,1024]{1,0:T(8,128)(2,1)} %tokens_ref.1, s32[1,512]{1,0:T(1,128)} %mask_ref.3), custom_call_target="tpu_custom_call" | custom-call | flops 1 | bytes 1 | tf_op jit(solution)/shard_map/send/pallas_call | solution.py:134
  2.8 1.3 %collective-permute-start = (bf16[144,512]{1,0:T(8,128)(2,1)}, bf16[144,512]{1,0:T(8,128)(2,1)S(1)}, u32[]{:S(2)}, u32[]{:S(2)}) collective-permute-start(bf16[144,512]{1,0:T(8,128)(2,1)} %get-tuple-element.57), channel_id=1, source_target_pairs={{0,28},{1,25},{2,30},{3,27},{4,24},{5,29},{6,26},{7,31},{8,20},{9,... | collective-permute-start | bytes 442376 | tf_op jit(solution)/shard_map/ppermute | solution.py:113
  4.1 3.2 %collective-permute-start.2 = (bf16[144,512]{1,0:T(8,128)(2,1)}, bf16[144,512]{1,0:T(8,128)(2,1)S(1)}, u32[]{:S(2)}, u32[]{:S(2)}) collective-permute-start(bf16[144,512]{1,0:T(8,128)(2,1)} %get-tuple-element.62), channel_id=1, source_target_pairs={{0,12},{1,13},{2,14},{3,15},{4,8},{5,9},{6,10},{7,11},{8,4},{9,5},... | collective-permute-start | bytes 442376 | tf_op jit(solution)/shard_map/ppermute | solution.py:113
  7.8 2.5 %prepare.1 = (bf16[1024,1024]{1,0:T(8,128)(2,1)S(1)}, bf16[1024,1024]{1,0:T(8,128)(2,1)S(1)}, bf16[672,1024]{1,0:T(8,128)(2,1)S(1)}, f32[160,128]{1,0:T(8,128)S(...) custom-call(s32[1,1024]{1,0:T(1,128)S(1)} %copy-done.8, ...), custom_call_target="tpu_custom_call" | custom-call | flops 1 | bytes 1 | tf_op jit(solution)/shard_map/prepare/pallas_call | solution.py:512
  10.3 4.0 %collective-permute-done.2.refs_1_.refs_2_.refs_8_ = bf16[144,512]{1,0:T(8,128)(2,1)S(1)} collective-permute-done((bf16[144,512]{1,0:T(8,128)(2,1)}, bf16[144,512]{1,0:T(8,128)(2,1)S(1)}, u32[]{:S(2)}, u32[]{:S(2)}) %collective-permute-start.2) | collective-permute-done | bytes 147488 | tf_op jit(solution)/shard_map/ppermute | solution.py:113
  14.3 3.9 %collective-permute-done.3.refs_2_.refs_9_ = bf16[144,512]{1,0:T(8,128)(2,1)S(1)} collective-permute-done((bf16[144,512]{1,0:T(8,128)(2,1)}, bf16[144,512]{1,0:T(8,128)(2,1)S(1)}, u32[]{:S(2)}, u32[]{:S(2)}) %collective-permute-start.3) | collective-permute-done | bytes 147488 | tf_op jit(solution)/shard_map/ppermute | solution.py:113
  18.3 1.3 %collective-permute-start.5 = (bf16[128,512]{1,0:T(8,128)(2,1)S(1)}, bf16[128,512]{1,0:T(8,128)(2,1)S(1)}, u32[]{:S(2)}, u32[]{:S(2)}) collective-permute-start(bf16[128,512]{1,0:T(8,128)(2,1)S(1)} %stack.3), channel_id=1, source_target_pairs={{0,2},{2,0},{1,3},{3,1},{4,6},{6,4},{5,7},{7,5},{8,10},{10,8},{9,1... | collective-permute-start | bytes 393224 | tf_op jit(solution)/shard_map/ppermute | solution.py:56
  19.5 1.4 %collective-permute-start.7 = (bf16[144,512]{1,0:T(8,128)(2,1)S(1)}, bf16[144,512]{1,0:T(8,128)(2,1)S(1)}, u32[]{:S(2)}, u32[]{:S(2)}) collective-permute-start(bf16[144,512]{1,0:T(8,128)(2,1)S(1)} %collective-permute-done.refs_0_), channel_id=1, source_target_pairs={{0,1},{1,0},{2,3},{3,2},{4,5},{5,4},{6,7},{7,6},{8,9},{9,8},{10,11... | collective-permute-start | bytes 442376 | tf_op jit(solution)/shard_map/ppermute | solution.py:56
  21.0 1.2 %collective-permute-done.5.refs_2_ = bf16[128,512]{1,0:T(8,128)(2,1)S(1)} collective-permute-done((bf16[128,512]{1,0:T(8,128)(2,1)S(1)}, bf16[128,512]{1,0:T(8,128)(2,1)S(1)}, u32[]{:S(2)}, u32[]{:S(2)}) %collective-permute-start.5) | collective-permute-done | bytes 131104 | tf_op jit(solution)/shard_map/ppermute | solution.py:56
  22.2 1.3 %collective-permute-start.6 = (bf16[128,512]{1,0:T(8,128)(2,1)S(1)}, bf16[128,512]{1,0:T(8,128)(2,1)S(1)}, u32[]{:S(2)}, u32[]{:S(2)}) collective-permute-start(bf16[128,512]{1,0:T(8,128)(2,1)S(1)} %stack.4.refs_1_), channel_id=1, source_target_pairs={{0,2},{2,0},{1,3},{3,1},{4,6},{6,4},{5,7},{7,5},{8,10},{10,8},{9,1... | collective-permute-start | bytes 393224 | tf_op jit(solution)/shard_map/ppermute | solution.py:56
  23.4 2.6 %collective-permute-start.12 = (bf16[144,512]{1,0:T(8,128)(2,1)S(1)}, bf16[144,512]{1,0:T(8,128)(2,1)S(1)}, u32[]{:S(2)}, u32[]{:S(2)}) collective-permute-start(bf16[144,512]{1,0:T(8,128)(2,1)S(1)} %collective-permute-done.3.refs_2_.refs_9_), channel_id=1, source_target_pairs={{0,1},{1,0},{2,3},{3,2},{4,5},{5,4},{6,7},{7,6},{8,9},{9,8},{10,11... | collective-permute-start | bytes 442376 | tf_op jit(solution)/shard_map/ppermute | solution.py:56
  26.5 1.2 %expand.1 = (bf16[1024,512]{1,0:T(8,128)(2,1)S(1)}, bf16[512,1024]{1,0:T(8,128)(2,1)S(1)}, f32[2048,128]{1,0:T(8,128)S(1)}) custom-call(f32[1024,128]{1,0:T(8,128)S(1)} %get-tuple-element.58.seen_ref, bf16[144,512]{1,0:T(8,128)(2,1)S(1)} %collective-permute-done.refs_0_, bf16[144,512]{1,0:T(8,128)(2,1)S(1)} %collective-permute-done.7.refs_1_.refs_4_, ...), custom_call_target="tpu_custom_call" | custom-call | flops 1 | bytes 1 | tf_op jit(solution)/shard_map/expand/pallas_call | solution.py:532
  27.8 1.7 %collective-permute-start.9 = (bf16[128,512]{1,0:T(8,128)(2,1)S(1)}, bf16[128,512]{1,0:T(8,128)(2,1)S(1)}, u32[]{:S(2)}, u32[]{:S(2)}) collective-permute-start(bf16[128,512]{1,0:T(8,128)(2,1)S(1)} %collective-permute-done.5.refs_2_), channel_id=1, source_target_pairs={{0,1},{1,0},{2,3},{3,2},{4,5},{5,4},{6,7},{7,6},{8,9},{9,8},{10,11... | collective-permute-start | bytes 393224 | tf_op jit(solution)/shard_map/ppermute | solution.py:56
  30.8 2.1 %project.1 = (bf16[1024,256]{1,0:T(8,128)(2,1)S(1)}, bf16[48,256]{1,0:T(8,128)(2,1)S(1)}, bf16[1024,256]{1,0:T(8,128)(2,1)S(1)}, bf16[256,1024]{1,0:T(8,128)(2,1)S(1)}, bf16[1024,1024]{1,0:T(8,128)(2,1)S(1)}) custom-call(bf16[144,512]{1,0:T(8,128)(2,1)S(1)} %collective-permute-done.refs_0_, bf16[128,512]{1,0:T(8,128)(2,1)S(1)} %stack.4.refs_1_, ...), custom_call_target="tpu_custom_call" | custom-call | flops 1 | bytes 1 | tf_op jit(solution)/shard_map/project/pallas_call | solution.py:549
  33.9 3.3 %collective-permute-start.15 = (bf16[48,256]{1,0:T(8,128)(2,1)S(1)}, bf16[48,256]{1,0:T(8,128)(2,1)S(1)}, u32[]{:S(2)}, u32[]{:S(2)}) collective-permute-start(bf16[48,256]{1,0:T(8,128)(2,1)S(1)} %get-tuple-element.81.refs_0_), channel_id=1, source_target_pairs={{0,16},{4,20},{8,24},{12,28},{16,0},{20,4},{24,8},{28,12},{1,17},{... | collective-permute-start | bytes 73736 | tf_op jit(solution)/shard_map/ppermute | solution.py:103
  37.2 1.5 %collective-permute-done.15.refs_2_ = bf16[48,256]{1,0:T(8,128)(2,1)S(1)} collective-permute-done((bf16[48,256]{1,0:T(8,128)(2,1)S(1)}, bf16[48,256]{1,0:T(8,128)(2,1)S(1)}, u32[]{:S(2)}, u32[]{:S(2)}) %collective-permute-start.15) | collective-permute-done | bytes 24608 | tf_op jit(solution)/shard_map/ppermute | solution.py:103
  38.7 1.2 %collective-permute-done.14.refs_1_ = bf16[48,256]{1,0:T(8,128)(2,1)S(1)} collective-permute-done((bf16[48,256]{1,0:T(8,128)(2,1)S(1)}, bf16[48,256]{1,0:T(8,128)(2,1)S(1)}, u32[]{:S(2)}, u32[]{:S(2)}) %collective-permute-start.14) | collective-permute-done | bytes 24608 | tf_op jit(solution)/shard_map/ppermute | solution.py:103
  39.9 2.7 %collective-permute-start.17 = (bf16[1024,256]{1,0:T(8,128)(2,1)S(1)}, bf16[1024,256]{1,0:T(8,128)(2,1)S(1)}, u32[]{:S(2)}, u32[]{:S(2)}) collective-permute-start(bf16[1024,256]{1,0:T(8,128)(2,1)S(1)} %get-tuple-element.80), channel_id=1, source_target_pairs={{0,4},{4,8},{8,12},{12,16},{16,20},{20,24},{24,28},{1,5},{5,9},{9,... | collective-permute-start | bytes 1572872 | tf_op jit(solution)/shard_map/ppermute | solution.py:60
  42.6 2.7 %order.1 = (bf16[256,1024]{1,0:T(8,128)(2,1)S(1)}, bf16[256,1024]{1,0:T(8,128)(2,1)S(1)}, bf16[1024,256]{1,0:T(8,128)(2,1)S(1)}, bf16[128,256]{1,0:T(8,128)(2,1)S(1)}, bf16[256,128]{1,0:T(8,128)(2,1)S(1)}) custom-call(bf16[1024,1024]{1,0:T(8,128)(2,1)S(1)} %get-tuple-element.51.p_ref, bf16[1024,1024]{1,0:T(8,128)(2,1)S(1)} %get-tuple-element.52.pt_ref, ...), custom_call_target="tpu_custom_call" | custom-call | flops 1 | bytes 1 | tf_op jit(solution)/shard_map/order/pallas_call | solution.py:569
  45.3 4.0 %own.1 = (f32[256,1024]{1,0:T(8,128)S(1)}, f32[256,1024]{1,0:T(8,128)S(1)}, f32[8,512]{1,0:T(8,128)S(1)}, f32[8,512]{1,0:T(8,128)S(1)}) custom-call(f32[4,4]{1,0:T(4,128)S(1)} %copy-done.5, bf16[256,1024]{1,0:T(8,128)(2,1)S(1)} %get-tuple-element.75.qt_ref, bf16[1024,256]{1,0:T(8,128)(2,1)S(1)} %get-tuple-element.76.k_ref, ...), custom_call_target="tpu_custom_call" | custom-call | flops 1 | bytes 1 | tf_op jit(solution)/shard_map/own/pallas_call | solution.py:585
  49.3 1.5 %collective-permute-start.18 = (bf16[192,256]{1,0:T(8,128)(2,1)S(1)}, bf16[192,256]{1,0:T(8,128)(2,1)S(1)}, u32[]{:S(2)}, u32[]{:S(2)}) collective-permute-start(bf16[192,256]{1,0:T(8,128)(2,1)S(1)} %stack.5.refs_0_), channel_id=1, source_target_pairs={{0,4},{4,0},{8,12},{12,8},{16,20},{20,16},{24,28},{28,24},{1,5},{5... | collective-permute-start | bytes 294920 | tf_op jit(solution)/shard_map/ppermute | solution.py:103
  50.8 7.8 %collective-permute-done.18.refs_1_ = bf16[192,256]{1,0:T(8,128)(2,1)S(1)} collective-permute-done((bf16[192,256]{1,0:T(8,128)(2,1)S(1)}, bf16[192,256]{1,0:T(8,128)(2,1)S(1)}, u32[]{:S(2)}, u32[]{:S(2)}) %collective-permute-start.18) | collective-permute-done | bytes 98336 | tf_op jit(solution)/shard_map/ppermute | solution.py:103
  59.6 3.2 %rest.2.refs_0_ = bf16[512,256]{1,0:T(8,128)(2,1)S(1)} custom-call(s32[4,8]{1,0:T(4,128)S(1)} %bitcast.1, f32[4,4]{1,0:T(4,128)S(1)} %copy-done.5, bf16[256,1024]{1,0:T(8,128)(2,1)S(1)} %get-tuple-element.75.qt_ref, bf16[2048,256]{1,0:T(8,128)(2,1)S(1)} %get-tuple-element.88.kw_ref, bf16[256,2048]{1,0:T(8,128)(2,1)S(1)} %get-tuple-element.89.vw_ref, ...), custom_call_target="tpu_custom_call" | custom-call | flops 1 | bytes 1 | tf_op jit(solution)/shard_map/rest/pallas_call | solution.py:655
  62.7 1.3 %collective-permute-start.19 = (bf16[512,256]{1,0:T(8,128)(2,1)S(1)}, bf16[512,256]{1,0:T(8,128)(2,1)S(1)}, u32[]{:S(2)}, u32[]{:S(2)}) collective-permute-start(bf16[512,256]{1,0:T(8,128)(2,1)S(1)} %rest.2.refs_0_), channel_id=1, source_target_pairs={{0,2},{2,0},{1,3},{3,1},{4,6},{6,4},{5,7},{7,5},{8,10},{10,8},{9,1... | collective-permute-start | bytes 786440 | tf_op jit(solution)/shard_map/ppermute | solution.py:56
  64.0 3.2 %rest.3.refs_0_ = bf16[512,256]{1,0:T(8,128)(2,1)S(1)} custom-call(s32[4,8]{1,0:T(4,128)S(1)} %bitcast.2, f32[4,4]{1,0:T(4,128)S(1)} %copy-done.5, bf16[256,1024]{1,0:T(8,128)(2,1)S(1)} %get-tuple-element.75.qt_ref, bf16[2048,256]{1,0:T(8,128)(2,1)S(1)} %get-tuple-element.88.kw_ref, bf16[256,2048]{1,0:T(8,128)(2,1)S(1)} %get-tuple-element.89.vw_ref, ...), custom_call_target="tpu_custom_call" | custom-call | flops 1 | bytes 1 | tf_op jit(solution)/shard_map/rest/pallas_call | solution.py:655
  67.5 1.0 %collective-permute-start.23 = (bf16[512,256]{1,0:T(8,128)(2,1)S(1)}, bf16[512,256]{1,0:T(8,128)(2,1)S(1)}, u32[]{:S(2)}, u32[]{:S(2)}) collective-permute-start(bf16[512,256]{1,0:T(8,128)(2,1)S(1)} %rest.2.refs_0_), channel_id=1, source_target_pairs={{0,1},{1,0},{2,3},{3,2},{4,5},{5,4},{6,7},{7,6},{8,9},{9,8},{10,11... | collective-permute-start | bytes 786440 | tf_op jit(solution)/shard_map/ppermute | solution.py:56
  68.5 1.6 %collective-permute-done.19.refs_1_ = bf16[512,256]{1,0:T(8,128)(2,1)S(1)} collective-permute-done((bf16[512,256]{1,0:T(8,128)(2,1)S(1)}, bf16[512,256]{1,0:T(8,128)(2,1)S(1)}, u32[]{:S(2)}, u32[]{:S(2)}) %collective-permute-start.19) | collective-permute-done | bytes 262176 | tf_op jit(solution)/shard_map/ppermute | solution.py:56
  70.2 2.3 %collective-permute-start.24 = (bf16[512,256]{1,0:T(8,128)(2,1)S(1)}, bf16[512,256]{1,0:T(8,128)(2,1)S(1)}, u32[]{:S(2)}, u32[]{:S(2)}) collective-permute-start(bf16[512,256]{1,0:T(8,128)(2,1)S(1)} %collective-permute-done.19.refs_1_), channel_id=1, source_target_pairs={{0,1},{1,0},{2,3},{3,2},{4,5},{5,4},{6,7},{7,6},{8,9},{9,8},{10,11... | collective-permute-start | bytes 786440 | tf_op jit(solution)/shard_map/ppermute | solution.py:56
  72.5 3.3 %collective-permute-done.20.refs_4_.refs_1_ = bf16[512,256]{1,0:T(8,128)(2,1)S(1)} collective-permute-done((bf16[512,256]{1,0:T(8,128)(2,1)S(1)}, bf16[512,256]{1,0:T(8,128)(2,1)S(1)}, u32[]{:S(2)}, u32[]{:S(2)}) %collective-permute-start.20) | collective-permute-done | bytes 262176 | tf_op jit(solution)/shard_map/ppermute | solution.py:56
  75.8 1.3 %collective-permute-start.22 = (bf16[512,256]{1,0:T(8,128)(2,1)S(1)}, bf16[512,256]{1,0:T(8,128)(2,1)S(1)}, u32[]{:S(2)}, u32[]{:S(2)}) collective-permute-start(bf16[512,256]{1,0:T(8,128)(2,1)S(1)} %collective-permute-done.20.refs_4_.refs_1_), channel_id=1, source_target_pairs={{0,1},{1,0},{2,3},{3,2},{4,5},{5,4},{6,7},{7,6},{8,9},{9,8},{10,11... | collective-permute-start | bytes 786440 | tf_op jit(solution)/shard_map/ppermute | solution.py:56
  77.2 1.3 %output.2.refs_4_ = bf16[1024,256]{1,0:T(8,128)(2,1)} custom-call(bf16[1024,256]{1,0:T(8,128)(2,1)S(1)} %copy-done, bf16[512,256]{1,0:T(8,128)(2,1)S(1)} %rest.2.refs_0_, bf16[512,256]{1,0:T(8,128)(2,1)S(1)} %collective-permute-done.19.refs_1_, bf16[512,256]{1,0:T(8,128)(2,1)S(1)} %collective-permute-done.23.refs_2_, ...), custom_call_target="tpu_custom_call" | custom-call | flops 1 | bytes 1 | tf_op jit(solution)/shard_map/output/pallas_call | solution.py:640
  78.5 1.3 %output.3 = bf16[1024,256]{1,0:T(8,128)(2,1)} custom-call(bf16[1024,256]{1,0:T(8,128)(2,1)S(1)} %copy-done, bf16[512,256]{1,0:T(8,128)(2,1)S(1)} %rest.3.refs_0_, bf16[512,256]{1,0:T(8,128)(2,1)S(1)} %collective-permute-done.20.refs_4_.refs_1_, bf16[512,256]{1,0:T(8,128)(2,1)S(1)} %collective-permute-done.21.refs_2_, ...), custom_call_target="tpu_custom_call", output_to_operand_aliasing={{}: (5, {})} | custom-call | flops 1 | bytes 1 | tf_op jit(solution)/shard_map/output/pallas_call | solution.py:640
  (50 shorter events, 4.7 us)
Async XLA Ops:
  0.0 7.8 %copy-start.6 = (s32[1,512]{1,0:T(1,128)S(1)}, s32[1,512]{1,0:T(1,128)}, u32[]{:S(2)}) copy-start(s32[1,512]{1,0:T(1,128)} %mask_ref.3) | copy-start | bytes 6148
  0.0 7.8 %copy-start.8 = (s32[1,1024]{1,0:T(1,128)S(1)}, s32[1,1024]{1,0:T(1,128)}, u32[]{:S(2)}) copy-start(s32[1,1024]{1,0:T(1,128)} %order_ref.1) | copy-start | bytes 12292
  0.0 7.8 %copy-start.2 = (bf16[1024,256]{1,0:T(8,128)(2,1)S(1)}, bf16[1024,256]{1,0:T(8,128)(2,1)}, u32[]{:S(2)}) copy-start(bf16[1024,256]{1,0:T(8,128)(2,1)} %wv_ref.1) | copy-start | bytes 1572868
  0.0 7.8 %copy-start.3 = (bf16[1024,256]{1,0:T(8,128)(2,1)S(1)}, bf16[1024,256]{1,0:T(8,128)(2,1)}, u32[]{:S(2)}) copy-start(bf16[1024,256]{1,0:T(8,128)(2,1)} %wk_in.1) | copy-start | bytes 1572868
  2.8 28.1 %copy-start.4 = (bf16[128,1024]{1,0:T(8,128)(2,1)S(1)}, bf16[128,1024]{1,0:T(8,128)(2,1)}, u32[]{:S(2)}) copy-start(bf16[128,1024]{1,0:T(8,128)(2,1)} %get-tuple-element.71.refs_14_) | copy-start | bytes 786436
  2.8 7.5 %collective-permute-start = (bf16[144,512]{1,0:T(8,128)(2,1)}, bf16[144,512]{1,0:T(8,128)(2,1)S(1)}, u32[]{:S(2)}, u32[]{:S(2)}) collective-permute-start(bf16[144,512]{1,0:T(8,128)(2,1)} %get-tuple-element.57), channel_id=1, source_target_pairs={{0,28},{1,25},{2,30},{3,27},{4,24},{5,29},{6,26},{7,31},{8,20},{9,... | collective-permute-start | bytes 442376 | tf_op jit(solution)/shard_map/ppermute | solution.py:113
  4.1 10.3 %collective-permute-start.2 = (bf16[144,512]{1,0:T(8,128)(2,1)}, bf16[144,512]{1,0:T(8,128)(2,1)S(1)}, u32[]{:S(2)}, u32[]{:S(2)}) collective-permute-start(bf16[144,512]{1,0:T(8,128)(2,1)} %get-tuple-element.62), channel_id=1, source_target_pairs={{0,12},{1,13},{2,14},{3,15},{4,8},{5,9},{6,10},{7,11},{8,4},{9,5},... | collective-permute-start | bytes 442376 | tf_op jit(solution)/shard_map/ppermute | solution.py:113
  7.2 11.0 %collective-permute-start.3 = (bf16[144,512]{1,0:T(8,128)(2,1)}, bf16[144,512]{1,0:T(8,128)(2,1)S(1)}, u32[]{:S(2)}, u32[]{:S(2)}) collective-permute-start(bf16[144,512]{1,0:T(8,128)(2,1)} %get-tuple-element.63), channel_id=1, source_target_pairs={{0,8},{1,9},{2,10},{3,11},{4,12},{5,13},{6,14},{7,15},{8,0},{9,1},... | collective-permute-start | bytes 442376 | tf_op jit(solution)/shard_map/ppermute | solution.py:113
  7.2 11.0 %collective-permute-start.4 = (bf16[144,512]{1,0:T(8,128)(2,1)}, bf16[144,512]{1,0:T(8,128)(2,1)S(1)}, u32[]{:S(2)}, u32[]{:S(2)}) collective-permute-start(bf16[144,512]{1,0:T(8,128)(2,1)} %get-tuple-element.64), channel_id=1, source_target_pairs={{0,4},{1,5},{2,6},{3,7},{4,0},{5,1},{6,2},{7,3},{8,12},{9,13},{10,... | collective-permute-start | bytes 442376 | tf_op jit(solution)/shard_map/ppermute | solution.py:113
  7.5 13.5 %collective-permute-start.1 = (bf16[144,512]{1,0:T(8,128)(2,1)}, bf16[144,512]{1,0:T(8,128)(2,1)S(1)}, u32[]{:S(2)}, u32[]{:S(2)}) collective-permute-start(bf16[144,512]{1,0:T(8,128)(2,1)} %get-tuple-element.61), channel_id=1, source_target_pairs={{0,20},{1,17},{2,22},{3,19},{4,16},{5,21},{6,18},{7,23},{8,28},{9,... | collective-permute-start | bytes 442376 | tf_op jit(solution)/shard_map/ppermute | solution.py:113
  18.3 3.9 %collective-permute-start.5 = (bf16[128,512]{1,0:T(8,128)(2,1)S(1)}, bf16[128,512]{1,0:T(8,128)(2,1)S(1)}, u32[]{:S(2)}, u32[]{:S(2)}) collective-permute-start(bf16[128,512]{1,0:T(8,128)(2,1)S(1)} %stack.3), channel_id=1, source_target_pairs={{0,2},{2,0},{1,3},{3,1},{4,6},{6,4},{5,7},{7,5},{8,10},{10,8},{9,1... | collective-permute-start | bytes 393224 | tf_op jit(solution)/shard_map/ppermute | solution.py:56
  19.5 6.5 %collective-permute-start.7 = (bf16[144,512]{1,0:T(8,128)(2,1)S(1)}, bf16[144,512]{1,0:T(8,128)(2,1)S(1)}, u32[]{:S(2)}, u32[]{:S(2)}) collective-permute-start(bf16[144,512]{1,0:T(8,128)(2,1)S(1)} %collective-permute-done.refs_0_), channel_id=1, source_target_pairs={{0,1},{1,0},{2,3},{3,2},{4,5},{5,4},{6,7},{7,6},{8,9},{9,8},{10,11... | collective-permute-start | bytes 442376 | tf_op jit(solution)/shard_map/ppermute | solution.py:56
  20.9 8.5 %collective-permute-start.11 = (bf16[144,512]{1,0:T(8,128)(2,1)S(1)}, bf16[144,512]{1,0:T(8,128)(2,1)S(1)}, u32[]{:S(2)}, u32[]{:S(2)}) collective-permute-start(bf16[144,512]{1,0:T(8,128)(2,1)S(1)} %collective-permute-done.2.refs_1_.refs_2_.refs_8_), channel_id=1, source_target_pairs={{0,1},{1,0},{2,3},{3,2},{4,5},{5,4},{6,7},{7,6},{8,9},{9,8},{10,11... | collective-permute-start | bytes 442376 | tf_op jit(solution)/shard_map/ppermute | solution.py:56
  22.2 5.6 %collective-permute-start.6 = (bf16[128,512]{1,0:T(8,128)(2,1)S(1)}, bf16[128,512]{1,0:T(8,128)(2,1)S(1)}, u32[]{:S(2)}, u32[]{:S(2)}) collective-permute-start(bf16[128,512]{1,0:T(8,128)(2,1)S(1)} %stack.4.refs_1_), channel_id=1, source_target_pairs={{0,2},{2,0},{1,3},{3,1},{4,6},{6,4},{5,7},{7,5},{8,10},{10,8},{9,1... | collective-permute-start | bytes 393224 | tf_op jit(solution)/shard_map/ppermute | solution.py:56
  23.4 6.0 %collective-permute-start.12 = (bf16[144,512]{1,0:T(8,128)(2,1)S(1)}, bf16[144,512]{1,0:T(8,128)(2,1)S(1)}, u32[]{:S(2)}, u32[]{:S(2)}) collective-permute-start(bf16[144,512]{1,0:T(8,128)(2,1)S(1)} %collective-permute-done.3.refs_2_.refs_9_), channel_id=1, source_target_pairs={{0,1},{1,0},{2,3},{3,2},{4,5},{5,4},{6,7},{7,6},{8,9},{9,8},{10,11... | collective-permute-start | bytes 442376 | tf_op jit(solution)/shard_map/ppermute | solution.py:56
  26.0 3.5 %collective-permute-start.13 = (bf16[144,512]{1,0:T(8,128)(2,1)S(1)}, bf16[144,512]{1,0:T(8,128)(2,1)S(1)}, u32[]{:S(2)}, u32[]{:S(2)}) collective-permute-start(bf16[144,512]{1,0:T(8,128)(2,1)S(1)} %collective-permute-done.4.refs_3_.refs_10_), channel_id=1, source_target_pairs={{0,1},{1,0},{2,3},{3,2},{4,5},{5,4},{6,7},{7,6},{8,9},{9,8},{10,11... | collective-permute-start | bytes 442376 | tf_op jit(solution)/shard_map/ppermute | solution.py:56
  26.0 3.5 %collective-permute-start.8 = (bf16[128,512]{1,0:T(8,128)(2,1)S(1)}, bf16[128,512]{1,0:T(8,128)(2,1)S(1)}, u32[]{:S(2)}, u32[]{:S(2)}) collective-permute-start(bf16[128,512]{1,0:T(8,128)(2,1)S(1)} %stack.4.refs_1_), channel_id=1, source_target_pairs={{0,1},{1,0},{2,3},{3,2},{4,5},{5,4},{6,7},{7,6},{8,9},{9,8},{10,11... | collective-permute-start | bytes 393224 | tf_op jit(solution)/shard_map/ppermute | solution.py:56
  27.8 2.7 %collective-permute-start.9 = (bf16[128,512]{1,0:T(8,128)(2,1)S(1)}, bf16[128,512]{1,0:T(8,128)(2,1)S(1)}, u32[]{:S(2)}, u32[]{:S(2)}) collective-permute-start(bf16[128,512]{1,0:T(8,128)(2,1)S(1)} %collective-permute-done.5.refs_2_), channel_id=1, source_target_pairs={{0,1},{1,0},{2,3},{3,2},{4,5},{5,4},{6,7},{7,6},{8,9},{9,8},{10,11... | collective-permute-start | bytes 393224 | tf_op jit(solution)/shard_map/ppermute | solution.py:56
  29.5 1.3 %collective-permute-start.10 = (bf16[128,512]{1,0:T(8,128)(2,1)S(1)}, bf16[128,512]{1,0:T(8,128)(2,1)S(1)}, u32[]{:S(2)}, u32[]{:S(2)}) collective-permute-start(bf16[128,512]{1,0:T(8,128)(2,1)S(1)} %collective-permute-done.6.refs_3_), channel_id=1, source_target_pairs={{0,1},{1,0},{2,3},{3,2},{4,5},{5,4},{6,7},{7,6},{8,9},{9,8},{10,11... | collective-permute-start | bytes 393224 | tf_op jit(solution)/shard_map/ppermute | solution.py:56
  33.0 4.2 %collective-permute-start.16 = (bf16[48,256]{1,0:T(8,128)(2,1)S(1)}, bf16[48,256]{1,0:T(8,128)(2,1)S(1)}, u32[]{:S(2)}, u32[]{:S(2)}) collective-permute-start(bf16[48,256]{1,0:T(8,128)(2,1)S(1)} %get-tuple-element.81.refs_0_), channel_id=1, source_target_pairs={{0,24},{4,28},{8,16},{12,20},{16,8},{20,12},{24,0},{28,4},{1,25},{... | collective-permute-start | bytes 73736 | tf_op jit(solution)/shard_map/ppermute | solution.py:103
  33.9 4.8 %collective-permute-start.15 = (bf16[48,256]{1,0:T(8,128)(2,1)S(1)}, bf16[48,256]{1,0:T(8,128)(2,1)S(1)}, u32[]{:S(2)}, u32[]{:S(2)}) collective-permute-start(bf16[48,256]{1,0:T(8,128)(2,1)S(1)} %get-tuple-element.81.refs_0_), channel_id=1, source_target_pairs={{0,16},{4,20},{8,24},{12,28},{16,0},{20,4},{24,8},{28,12},{1,17},{... | collective-permute-start | bytes 73736 | tf_op jit(solution)/shard_map/ppermute | solution.py:103
  37.2 2.7 %collective-permute-start.14 = (bf16[48,256]{1,0:T(8,128)(2,1)S(1)}, bf16[48,256]{1,0:T(8,128)(2,1)S(1)}, u32[]{:S(2)}, u32[]{:S(2)}) collective-permute-start(bf16[48,256]{1,0:T(8,128)(2,1)S(1)} %get-tuple-element.81.refs_0_), channel_id=1, source_target_pairs={{0,8},{4,12},{8,0},{12,4},{16,24},{20,28},{24,16},{28,20},{1,9},{5... | collective-permute-start | bytes 73736 | tf_op jit(solution)/shard_map/ppermute | solution.py:103
  39.9 18.7 %collective-permute-start.17 = (bf16[1024,256]{1,0:T(8,128)(2,1)S(1)}, bf16[1024,256]{1,0:T(8,128)(2,1)S(1)}, u32[]{:S(2)}, u32[]{:S(2)}) collective-permute-start(bf16[1024,256]{1,0:T(8,128)(2,1)S(1)} %get-tuple-element.80), channel_id=1, source_target_pairs={{0,4},{4,8},{8,12},{12,16},{16,20},{20,24},{24,28},{1,5},{5,9},{9,... | collective-permute-start | bytes 1572872 | tf_op jit(solution)/shard_map/ppermute | solution.py:60
  49.3 10.3 %copy-start.7 = (s32[8,4]{0,1:T(4,128)S(1)}, s32[8,4]{0,1:T(4,128)}, u32[]{:S(2)}) copy-start(s32[8,4]{0,1:T(4,128)} %param.15) | copy-start | bytes 388
  49.3 9.3 %collective-permute-start.18 = (bf16[192,256]{1,0:T(8,128)(2,1)S(1)}, bf16[192,256]{1,0:T(8,128)(2,1)S(1)}, u32[]{:S(2)}, u32[]{:S(2)}) collective-permute-start(bf16[192,256]{1,0:T(8,128)(2,1)S(1)} %stack.5.refs_0_), channel_id=1, source_target_pairs={{0,4},{4,0},{8,12},{12,8},{16,20},{20,16},{24,28},{28,24},{1,5},{5... | collective-permute-start | bytes 294920 | tf_op jit(solution)/shard_map/ppermute | solution.py:103
  62.7 14.4 %copy-start = (bf16[1024,256]{1,0:T(8,128)(2,1)S(1)}, bf16[1024,256]{1,0:T(8,128)(2,1)}, u32[]{:S(2)}) copy-start(bf16[1024,256]{1,0:T(8,128)(2,1)} %w_ref.3) | copy-start | bytes 1572868
  62.7 7.5 %collective-permute-start.19 = (bf16[512,256]{1,0:T(8,128)(2,1)S(1)}, bf16[512,256]{1,0:T(8,128)(2,1)S(1)}, u32[]{:S(2)}, u32[]{:S(2)}) collective-permute-start(bf16[512,256]{1,0:T(8,128)(2,1)S(1)} %rest.2.refs_0_), channel_id=1, source_target_pairs={{0,2},{2,0},{1,3},{3,1},{4,6},{6,4},{5,7},{7,5},{8,10},{10,8},{9,1... | collective-permute-start | bytes 786440 | tf_op jit(solution)/shard_map/ppermute | solution.py:56
  67.2 8.6 %collective-permute-start.20 = (bf16[512,256]{1,0:T(8,128)(2,1)S(1)}, bf16[512,256]{1,0:T(8,128)(2,1)S(1)}, u32[]{:S(2)}, u32[]{:S(2)}) collective-permute-start(bf16[512,256]{1,0:T(8,128)(2,1)S(1)} %rest.3.refs_0_), channel_id=1, source_target_pairs={{0,2},{2,0},{1,3},{3,1},{4,6},{6,4},{5,7},{7,5},{8,10},{10,8},{9,1... | collective-permute-start | bytes 786440 | tf_op jit(solution)/shard_map/ppermute | solution.py:56
  67.5 9.6 %collective-permute-start.23 = (bf16[512,256]{1,0:T(8,128)(2,1)S(1)}, bf16[512,256]{1,0:T(8,128)(2,1)S(1)}, u32[]{:S(2)}, u32[]{:S(2)}) collective-permute-start(bf16[512,256]{1,0:T(8,128)(2,1)S(1)} %rest.2.refs_0_), channel_id=1, source_target_pairs={{0,1},{1,0},{2,3},{3,2},{4,5},{5,4},{6,7},{7,6},{8,9},{9,8},{10,11... | collective-permute-start | bytes 786440 | tf_op jit(solution)/shard_map/ppermute | solution.py:56
  70.2 7.0 %collective-permute-start.24 = (bf16[512,256]{1,0:T(8,128)(2,1)S(1)}, bf16[512,256]{1,0:T(8,128)(2,1)S(1)}, u32[]{:S(2)}, u32[]{:S(2)}) collective-permute-start(bf16[512,256]{1,0:T(8,128)(2,1)S(1)} %collective-permute-done.19.refs_1_), channel_id=1, source_target_pairs={{0,1},{1,0},{2,3},{3,2},{4,5},{5,4},{6,7},{7,6},{8,9},{9,8},{10,11... | collective-permute-start | bytes 786440 | tf_op jit(solution)/shard_map/ppermute | solution.py:56
  72.5 6.0 %collective-permute-start.21 = (bf16[512,256]{1,0:T(8,128)(2,1)S(1)}, bf16[512,256]{1,0:T(8,128)(2,1)S(1)}, u32[]{:S(2)}, u32[]{:S(2)}) collective-permute-start(bf16[512,256]{1,0:T(8,128)(2,1)S(1)} %rest.3.refs_0_), channel_id=1, source_target_pairs={{0,1},{1,0},{2,3},{3,2},{4,5},{5,4},{6,7},{7,6},{8,9},{9,8},{10,11... | collective-permute-start | bytes 786440 | tf_op jit(solution)/shard_map/ppermute | solution.py:56
  75.8 2.7 %collective-permute-start.22 = (bf16[512,256]{1,0:T(8,128)(2,1)S(1)}, bf16[512,256]{1,0:T(8,128)(2,1)S(1)}, u32[]{:S(2)}, u32[]{:S(2)}) collective-permute-start(bf16[512,256]{1,0:T(8,128)(2,1)S(1)} %collective-permute-done.20.refs_4_.refs_1_), channel_id=1, source_target_pairs={{0,1},{1,0},{2,3},{3,2},{4,5},{5,4},{6,7},{7,6},{8,9},{9,8},{10,11... | collective-permute-start | bytes 786440 | tf_op jit(solution)/shard_map/ppermute | solution.py:56
  (2 other events, 10.5 us)

commit v13 on v12

--- a/solution.py
+++ b/solution.py
@@ -99,6 +99,19 @@
     )(*parts, *after)
 
 
+def packed_rows(select, packed, quarter, parts):
+    return pl.pallas_call(
+        pack_kernel,
+        out_shape=jax.ShapeDtypeStruct((packed, quarter), BF),
+        in_specs=vmem_specs(1 + len(parts)),
+        out_specs=pl.BlockSpec(memory_space=pltpu.VMEM),
+        scratch_shapes=[pltpu.VMEM((select.shape[1], quarter), BF)],
+        compiler_params=pltpu.CompilerParams(vmem_limit_bytes=VMEM_LIMIT),
+        cost_estimate=COST,
+        name="pack",
+    )(select, *parts)
+
+
 def by_distance(block, distance):
     return lax.ppermute(block, "seq", [(i, i ^ distance) for i in range(lax.axis_size("seq"))])
 
@@ -128,7 +141,9 @@
         second = over_head(first, CORE_PAIRS)
         fourth = over_head(third, CORE_PAIRS)
         prepared = prepare()
-        return [first, third, second, fourth], prepared, expand(prepared, [to_next(mask_ids)])
+        halo = to_next(packed_rows(prepared[2], tok_rows - mask_ids.shape[1], quarter, [first]))
+        expanded = expand(prepared, [to_next(mask_ids)])
+        return [first, third, second, fourth], prepared, expanded, halo
     half = width // 2
     tall = rows + CODE_ROWS
     *blocks, own = pl.pallas_call(
@@ -160,9 +175,13 @@
     near = [three, four, five]
     near_core = [over_head(part, CORE_PAIRS) for part in near]
     expanded = expand(prepared, [one, far_core[0], three, five])
-    far_x[1], _ = lax.optimization_barrier((far_x[1], expanded))
+    halo = packed_rows(
+        prepared[2], tok_rows - mask_ids.shape[1], half // 2, far + far_core + near + near_core + [own]
+    )
+    far_x[1], _, _ = lax.optimization_barrier((far_x[1], expanded, halo))
+    halo = to_next(halo)
     far_last = [over_head(part, CORE_PAIRS) for part in far_x]
-    return far + far_x + far_core + far_last + near + near_core + [own], prepared, expanded
+    return far + far_x + far_core + far_last + near + near_core + [own], prepared, expanded, halo
 
 
 def column(row, lanes=128):
@@ -285,31 +304,47 @@
     x_ref[7 * rows :] = own[...]
 
 
+def pack_kernel(sel_ref, *refs):
+    parts, (out_ref, rows_ref) = refs[:-2], refs[-2:]
+    packed, quarter = out_ref.shape
+    head = lax.axis_index("head")
+    if len(parts) == 1:
+        rows_ref[...] = parts[0][...]
+    else:
+        core, side = head & 1, head >> 1
+        far_refs, near_refs, own = parts[:4], parts[4:10], parts[10]
+        rows = own.shape[0]
+        here = pl.ds(pl.multiple_of(core * quarter, quarter), quarter)
+        for index, piece in enumerate(far_refs):
+            row = pl.multiple_of((2 * (index % 2) + (core ^ (index // 2))) * rows, rows)
+            rows_ref[pl.ds(row, rows)] = piece[:rows, here]
+        for index in range(3):
+            rows_ref[(4 + index) * rows : (5 + index) * rows] = jnp.where(
+                core == side, near_refs[index][:rows, here], near_refs[3 + index][:rows, here]
+            )
+        rows_ref[7 * rows :] = own[:, pl.ds(pl.multiple_of(head * quarter, quarter), quarter)]
+    out_ref[...] = nn(sel_ref[:packed], rows_ref[...]).astype(BF)
+
+
 def project_kernel(count, *refs):
     piece_refs, refs = refs[:count], refs[count:]
-    wt_ref, wk_ref, sel_ref, fcol_ref, comp_ref, summ_ref, k_ref, v_ref, x_ref = refs
+    wt_ref, wk_ref, sel_ref, fcol_ref, summ_ref, k_ref, v_ref, x_ref = refs
     assemble(piece_refs, x_ref)
     group = wk_ref.shape[1]
-    packed = comp_ref.shape[0] // 2
-    lead = packed + SUMM_ROWS
+    near = x_ref.shape[0] // POOL1
+    lead = sel_ref.shape[0] - near
     x = x_ref[...]
     keys = nn(x, wk_ref[...]).astype(BF)
     k_ref[...] = keys
     vt = nt(wt_ref[group:], x).astype(BF)
     v_ref[...] = vt
-    sel = sel_ref[:lead]
+    sel = sel_ref[lead - SUMM_ROWS : lead]
     kl = nn(sel, keys)
     vl = nt(vt, sel)
-    comp_ref[:packed] = kl[:packed].astype(BF)
-    vc = vl[:, :packed].astype(BF)
-    for part in range(packed // group):
-        comp_ref[packed + part * group : packed + (part + 1) * group] = vc[
-            :, part * group : (part + 1) * group
-        ]
     factor = fcol_ref[:SUMM_ROWS, :1]
-    summ_k = kl[packed:] * factor
+    summ_k = kl * factor
     tail = jnp.concatenate(
-        [vl[:, packed:], jnp.zeros((group, 128 - SUMM_ROWS), F32)], axis=1
+        [vl, jnp.zeros((group, 128 - SUMM_ROWS), F32)], axis=1
     )
     summ_v = jnp.transpose(tail)[:SUMM_ROWS] * factor
     mids = x_ref.shape[0] // POOL2
@@ -381,20 +416,19 @@
             near_ref[rows, at : at + FBLK] = near_out[rows, lanes] * scales[h]
 
 
-def window_kernel(k_ref, vt_ref, comp_ref, e_ref, et_ref, *refs):
-    summ_refs, (kw_ref, vw_ref, ck_ref, cv_ref, all_ref) = refs[:-5], refs[-5:]
+def window_kernel(k_ref, vt_ref, wt_ref, wk_ref, e_ref, et_ref, *refs):
+    halo_refs, refs = refs[:4], refs[4:]
+    summ_refs, (kw_ref, vw_ref, ck_ref, cv_ref, all_ref, x_ref) = refs[:-6], refs[-6:]
     tok_rows, group = k_ref.shape
-    packed = e_ref.shape[1]
-    kw_ref[:tok_rows] = nn(e_ref[...], comp_ref[:packed]).astype(BF)
+    quarter = x_ref.shape[1] // 4
+    head = lax.axis_index("head")
+    for distance, part in zip((0, 2, 1, 3), halo_refs):
+        start = pl.multiple_of((head ^ distance) * quarter, quarter)
+        x_ref[:, pl.ds(start, quarter)] = part[...]
+    x = x_ref[...]
+    kw_ref[:tok_rows] = nn(e_ref[...], nn(x, wk_ref[...]).astype(BF)).astype(BF)
     kw_ref[tok_rows:] = k_ref[...]
-    prev = None
-    for part in range(packed // group):
-        term = nn(
-            comp_ref[packed + part * group : packed + (part + 1) * group],
-            et_ref[part * group : (part + 1) * group],
-        )
-        prev = term if prev is None else prev + term
-    vw_ref[:, :tok_rows] = prev.astype(BF)
+    vw_ref[:, :tok_rows] = nn(nt(wt_ref[group:], x).astype(BF), et_ref[...]).astype(BF)
     vw_ref[:, tok_rows:] = vt_ref[...]
     at = 0
     for part in summ_refs:
@@ -543,28 +577,27 @@
             name="expand",
         )(prepared[5], *sources)
 
-    pieces, prepared, expanded = exchange_tokens(tokens, mask_ids, prepare, expand)
+    pieces, prepared, expanded, halo = exchange_tokens(tokens, mask_ids, prepare, expand)
     permute, permute_t, select, f_col, f_row, seen, w_t, w_k = prepared
     spread, spread_t, bias = expanded
-    comp, summ, k0, v0, rows_here = pl.pallas_call(
+    summ, k0, v0, rows_here = pl.pallas_call(
         functools.partial(project_kernel, len(pieces)),
         out_shape=(
-            shape((2 * packed, group), BF),
             shape((step, group), BF),
             shape((tok_rows, group), BF),
             shape((group, tok_rows), BF),
             shape((tok_rows, width), BF),
         ),
         in_specs=vmem_specs(len(pieces) + 4),
-        out_specs=vmem_specs(5),
+        out_specs=vmem_specs(4),
         compiler_params=params,
         cost_estimate=COST,
         name="project",
     )(*pieces, w_t, w_k, select, f_col)
     if slabs == 8:
         lined = [summ] + [by_distance(summ, d) for d in (2, 4, 6)]
-        comp, *lined = lax.optimization_barrier((comp, *lined))
-    comp_before = to_next(comp)
+    else:
+        lined = [summ]
 
     q_t, v_t, keys, near_k, near_vt = pl.pallas_call(
         order_kernel,
@@ -581,6 +614,19 @@
         cost_estimate=COST,
         name="order",
     )(permute, permute_t, select, f_col, f_row, w_t, rows_here, k0, v0)
+    halo, near_k, *lined = lax.optimization_barrier((halo, near_k, *lined))
+    halo_x = over_head(halo, X_PAIRS)
+    halo_core = over_head(halo, CORE_PAIRS)
+    if slabs == 8:
+        places = tuple((index, 0, step, 0) for index in range(4))
+        column = stacked(lined, places, group)
+        column, q_t = lax.optimization_barrier((column, q_t))
+        summaries = [column, by_distance(column, 1)]
+    else:
+        copies = jnp.broadcast_to(summ[None], (slabs, step, group))
+        copies = lax.all_to_all(copies, "seq", split_axis=0, concat_axis=0, tiled=True)
+        summaries = [copies.reshape(slabs * step, group)]
+
     blocks = tok_rows // FBLK
     acc, near_out, top, den = pl.pallas_call(
         own_kernel,
@@ -601,15 +647,8 @@
         name="own",
     )(level_mix, q_t, keys, v_t, near_k, near_vt, seen)
 
-    if slabs == 8:
-        places = tuple((index, 0, step, 0) for index in range(4))
-        column = stacked(lined, places, group, (top,))
-        summaries = [column, by_distance(column, 1)]
-    else:
-        copies = jnp.broadcast_to(summ[None], (slabs, step, group))
-        copies = lax.all_to_all(copies, "seq", split_axis=0, concat_axis=0, tiled=True)
-        summaries = [copies.reshape(slabs * step, group)]
-
+    halo_x, _, *summaries = lax.optimization_barrier((halo_x, top, *summaries))
+    halo_last = over_head(halo_x, CORE_PAIRS)
     window_k, window_v, coarse_k, coarse_v = pl.pallas_call(
         window_kernel,
         out_shape=(
@@ -618,13 +657,13 @@
             shape((coarse, group), BF),
             shape((group, coarse), BF),
         ),
-        in_specs=vmem_specs(5 + len(summaries)),
+        in_specs=vmem_specs(10 + len(summaries)),
         out_specs=vmem_specs(4),
-        scratch_shapes=[pltpu.VMEM((slabs * step, group), BF)],
+        scratch_shapes=[pltpu.VMEM((slabs * step, group), BF), pltpu.VMEM((packed, width), BF)],
         compiler_params=params,
         cost_estimate=COST,
         name="window",
-    )(keys, v_t, comp_before, spread, spread_t, *summaries)
+    )(keys, v_t, w_t, w_k, spread, spread_t, halo, halo_x, halo_core, halo_last, *summaries)
 
     total = (FINE_K - 1) * FBLK + coarse
     lists = fine_blocks.T

time: 79.9 us -> 76 us (0.951)
  the two profiles are of different devices: /device:TPU:9 before, /device:TPU:0 now
where the time goes in v13:
time: 76 us; the launch traced here: 75.8 us
  Pallas kernels  26.6 us (35%)
  starting transfers between devices  26.3 us (35%)
  waiting for transfers between devices  22.7 us (30%)
    ppermute x18, waiting for transfers between devices, over_head(): return lax.ppermute(block, 'head', pairs)  15.2 us
    ppermute x5, starting transfers between devices, by_core(): return lax.ppermute(block, ('seq', 'head'), pairs)  9.51 us
    ppermute x18, starting transfers between devices, over_head(): return lax.ppermute(block, 'head', pairs)  8.8 us
    ppermute x5, waiting for transfers between devices, by_core(): return lax.ppermute(block, ('seq', 'head'), pairs)  7.28 us
    pallas_call x2, Pallas kernels, local(): pl.pallas_call(functools.partial(rest_kernel, first, count), out_shape=sh...  6.53 us
    ppermute x4, starting transfers between devices, by_distance(): lax.ppermute(block, 'seq', [(i, i ^ distance) for i in range(lax.axis_siz...  4.96 us
    pallas_call x1, Pallas kernels, local(): pl.pallas_call(own_kernel, out_shape=(shape((group, tok_rows), F32), shap...  3.94 us
    ppermute x1, starting transfers between devices, to_next(): lax.ppermute(block, 'seq', [(i, i + 1) for i in range(lax.axis_size('seq'...  2.99 us
  transfers between devices with their start and end apart: 28, of which 10 were waited for; matrix products, arithmetic and copies ran while one was open for 0% of the time, Pallas kernels for 23%

profile of v13, /device:TPU:0, one launch (start us, length us, event | category | flops | bytes accessed | tf_op | source)
XLA Modules:
  0.0 75.8 jit_solution(7633718899300673572)
XLA Ops:
  0.0 2.7 %send.1 = (bf16[144,512]{1,0:T(8,128)(2,1)}, bf16[144,512]{1,0:T(8,128)(2,1)}, bf16[144,512]{1,0:T(8,128)(2,1)}, bf16[144,512]{1,0:T(8,128)(2,1)}, bf16[144,512]{1,0:T(8,128)(2,1)}, /*index=5*/bf16[128,1024]{1,0:T(8,128)(2,1)}) custom-call(bf16[1024,1024]{1,0:T(8,128)(2,1)} %tokens_ref.1, s32[1,512]{1,0:T(1,128)} %mask_ref.3), custom_call_target="tpu_custom_call" | custom-call | flops 1 | bytes 1 | tf_op jit(solution)/shard_map/send/pallas_call | solution.py:149
  2.7 6.0 %collective-permute-start = (bf16[144,512]{1,0:T(8,128)(2,1)}, bf16[144,512]{1,0:T(8,128)(2,1)S(1)}, u32[]{:S(2)}, u32[]{:S(2)}) collective-permute-start(bf16[144,512]{1,0:T(8,128)(2,1)} %get-tuple-element.57), channel_id=1, source_target_pairs={{0,28},{1,25},{2,30},{3,27},{4,24},{5,29},{6,26},{7,31},{8,20},{9,... | collective-permute-start | bytes 442376 | tf_op jit(solution)/shard_map/ppermute | solution.py:126
  8.8 2.0 %collective-permute-start.3 = (bf16[144,512]{1,0:T(8,128)(2,1)}, bf16[144,512]{1,0:T(8,128)(2,1)S(1)}, u32[]{:S(2)}, u32[]{:S(2)}) collective-permute-start(bf16[144,512]{1,0:T(8,128)(2,1)} %get-tuple-element.68), channel_id=1, source_target_pairs={{0,8},{1,9},{2,10},{3,11},{4,12},{5,13},{6,14},{7,15},{8,0},{9,1},... | collective-permute-start | bytes 442376 | tf_op jit(solution)/shard_map/ppermute | solution.py:126
  10.7 1.5 %collective-permute-start.4 = (bf16[144,512]{1,0:T(8,128)(2,1)}, bf16[144,512]{1,0:T(8,128)(2,1)S(1)}, u32[]{:S(2)}, u32[]{:S(2)}) collective-permute-start(bf16[144,512]{1,0:T(8,128)(2,1)} %get-tuple-element.69), channel_id=1, source_target_pairs={{0,4},{1,5},{2,6},{3,7},{4,0},{5,1},{6,2},{7,3},{8,12},{9,13},{10,... | collective-permute-start | bytes 442376 | tf_op jit(solution)/shard_map/ppermute | solution.py:126
  12.3 2.5 %prepare.1 = (bf16[1024,1024]{1,0:T(8,128)(2,1)S(1)}, bf16[1024,1024]{1,0:T(8,128)(2,1)S(1)}, bf16[672,1024]{1,0:T(8,128)(2,1)S(1)}, f32[160,128]{1,0:T(8,128)S(...) custom-call(s32[1,1024]{1,0:T(1,128)S(1)} %copy-done.8, ...), custom_call_target="tpu_custom_call" | custom-call | flops 1 | bytes 1 | tf_op jit(solution)/shard_map/prepare/pallas_call | solution.py:546
  14.8 4.8 %collective-permute-done.2.refs_1_.refs_4_.refs_2_.refs_8_ = bf16[144,512]{1,0:T(8,128)(2,1)S(1)} collective-permute-done((bf16[144,512]{1,0:T(8,128)(2,1)}, bf16[144,512]{1,0:T(8,128)(2,1)S(1)}, u32[]{:S(2)}, u32[]{:S(2)}) %collective-permute-start.2) | collective-permute-done | bytes 147488 | tf_op jit(solution)/shard_map/ppermute | solution.py:126
  19.6 2.4 %collective-permute-done.3.refs_2_.refs_5_.refs_9_ = bf16[144,512]{1,0:T(8,128)(2,1)S(1)} collective-permute-done((bf16[144,512]{1,0:T(8,128)(2,1)}, bf16[144,512]{1,0:T(8,128)(2,1)S(1)}, u32[]{:S(2)}, u32[]{:S(2)}) %collective-permute-start.3) | collective-permute-done | bytes 147488 | tf_op jit(solution)/shard_map/ppermute | solution.py:126
  22.1 1.6 %collective-permute-start.5 = (bf16[128,512]{1,0:T(8,128)(2,1)S(1)}, bf16[128,512]{1,0:T(8,128)(2,1)S(1)}, u32[]{:S(2)}, u32[]{:S(2)}) collective-permute-start(bf16[128,512]{1,0:T(8,128)(2,1)S(1)} %stack.3), channel_id=1, source_target_pairs={{0,2},{2,0},{1,3},{3,1},{4,6},{6,4},{5,7},{7,5},{8,10},{10,8},{9,1... | collective-permute-start | bytes 393224 | tf_op jit(solution)/shard_map/ppermute | solution.py:56
  24.2 0.5 collective-permute-start.6
  24.7 2.5 %collective-permute-done.5.refs_2_ = bf16[128,512]{1,0:T(8,128)(2,1)S(1)} collective-permute-done((bf16[128,512]{1,0:T(8,128)(2,1)S(1)}, bf16[128,512]{1,0:T(8,128)(2,1)S(1)}, u32[]{:S(2)}, u32[]{:S(2)}) %collective-permute-start.5) | collective-permute-done | bytes 131104 | tf_op jit(solution)/shard_map/ppermute | solution.py:56
  27.2 1.6 %collective-permute-start.12 = (bf16[128,512]{1,0:T(8,128)(2,1)S(1)}, bf16[128,512]{1,0:T(8,128)(2,1)S(1)}, u32[]{:S(2)}, u32[]{:S(2)}) collective-permute-start(bf16[128,512]{1,0:T(8,128)(2,1)S(1)} %stack.4.refs_1_), channel_id=1, source_target_pairs={{0,2},{2,0},{1,3},{3,1},{4,6},{6,4},{5,7},{7,5},{8,10},{10,8},{9,1... | collective-permute-start | bytes 393224 | tf_op jit(solution)/shard_map/ppermute | solution.py:56
  29.3 3.0 %collective-permute-start.11 = (bf16[512,256]{1,0:T(8,128)(2,1)S(1)}, bf16[512,256]{1,0:T(8,128)(2,1)S(1)}, u32[]{:S(2)}, u32[]{:S(2)}) collective-permute-start(bf16[512,256]{1,0:T(8,128)(2,1)S(1)} %pack.1), channel_id=1, source_target_pairs={{0,4},{4,8},{8,12},{12,16},{16,20},{20,24},{24,28},{1,5},{5,9},{9,... | collective-permute-start | bytes 786440 | tf_op jit(solution)/shard_map/ppermute | solution.py:60
  32.4 1.2 %expand.1 = (bf16[1024,512]{1,0:T(8,128)(2,1)S(1)}, bf16[512,1024]{1,0:T(8,128)(2,1)S(1)}, f32[2048,128]{1,0:T(8,128)S(1)}) custom-call(f32[1024,128]{1,0:T(8,128)S(1)} %get-tuple-element.62.seen_ref, bf16[144,512]{1,0:T(8,128)(2,1)S(1)} %collective-permute-done.refs_0_, bf16[144,512]{1,0:T(8,128)(2,1)S(1)} %collective-permute-done.6.refs_2_.refs_1_.refs_4_, ...), custom_call_target="tpu_custom_call" | custom-call | flops 1 | bytes 1 | tf_op jit(solution)/shard_map/expand/pallas_call | solution.py:566
  33.6 0.6 collective-permute-start.14
  34.2 1.0 %collective-permute-done.14.refs_7_ = bf16[128,512]{1,0:T(8,128)(2,1)S(1)} collective-permute-done((bf16[128,512]{1,0:T(8,128)(2,1)S(1)}, bf16[128,512]{1,0:T(8,128)(2,1)S(1)}, u32[]{:S(2)}, u32[]{:S(2)}) %collective-permute-start.14) | collective-permute-done | bytes 131104 | tf_op jit(solution)/shard_map/ppermute | solution.py:56
  35.2 1.8 %project.1 = (bf16[48,256]{1,0:T(8,128)(2,1)S(1)}, bf16[1024,256]{1,0:T(8,128)(2,1)S(1)}, bf16[256,1024]{1,0:T(8,128)(2,1)S(1)}, bf16[1024,1024]{1,0:T(8,128)(2,1)S(1)}) custom-call(bf16[144,512]{1,0:T(8,128)(2,1)S(1)} %collective-permute-done.refs_0_, bf16[128,512]{1,0:T(8,128)(2,1)S(1)} %stack.4.refs_1_, ...), custom_call_target="tpu_custom_call" | custom-call | flops 1 | bytes 1 | tf_op jit(solution)/shard_map/project/pallas_call | solution.py:583
  37.0 1.7 %collective-permute-start.17 = (bf16[48,256]{1,0:T(8,128)(2,1)S(1)}, bf16[48,256]{1,0:T(8,128)(2,1)S(1)}, u32[]{:S(2)}, u32[]{:S(2)}) collective-permute-start(bf16[48,256]{1,0:T(8,128)(2,1)S(1)} %get-tuple-element.82.refs_0_), channel_id=1, source_target_pairs={{0,24},{4,28},{8,16},{12,20},{16,8},{20,12},{24,0},{28,4},{1,25},{... | collective-permute-start | bytes 73736 | tf_op jit(solution)/shard_map/ppermute | solution.py:116
  38.7 2.7 %collective-permute-start.15 = (bf16[48,256]{1,0:T(8,128)(2,1)S(1)}, bf16[48,256]{1,0:T(8,128)(2,1)S(1)}, u32[]{:S(2)}, u32[]{:S(2)}) collective-permute-start(bf16[48,256]{1,0:T(8,128)(2,1)S(1)} %get-tuple-element.82.refs_0_), channel_id=1, source_target_pairs={{0,8},{4,12},{8,0},{12,4},{16,24},{20,28},{24,16},{28,20},{1,9},{5... | collective-permute-start | bytes 73736 | tf_op jit(solution)/shard_map/ppermute | solution.py:116
  41.4 2.6 %order.1 = (bf16[256,1024]{1,0:T(8,128)(2,1)S(1)}, bf16[256,1024]{1,0:T(8,128)(2,1)S(1)}, bf16[1024,256]{1,0:T(8,128)(2,1)S(1)}, bf16[128,256]{1,0:T(8,128)(2,1)S(1)}, bf16[256,128]{1,0:T(8,128)(2,1)S(1)}) custom-call(bf16[1024,1024]{1,0:T(8,128)(2,1)S(1)} %get-tuple-element.58.p_ref, bf16[1024,1024]{1,0:T(8,128)(2,1)S(1)} %get-tuple-element.59.pt_ref, ...), custom_call_target="tpu_custom_call" | custom-call | flops 1 | bytes 1 | tf_op jit(solution)/shard_map/order/pallas_call | solution.py:602
  44.1 1.3 %collective-permute-start.18 = (bf16[512,256]{1,0:T(8,128)(2,1)S(1)}, bf16[512,256]{1,0:T(8,128)(2,1)S(1)}, u32[]{:S(2)}, u32[]{:S(2)}) collective-permute-start(bf16[512,256]{1,0:T(8,128)(2,1)S(1)} %collective-permute-done.11.refs_0_), channel_id=1, source_target_pairs={{0,2},{2,0},{1,3},{3,1},{4,6},{6,4},{5,7},{7,5},{8,10},{10,8},{9,1... | collective-permute-start | bytes 786440 | tf_op jit(solution)/shard_map/ppermute | solution.py:56
  45.9 3.9 %own.1 = (f32[256,1024]{1,0:T(8,128)S(1)}, f32[256,1024]{1,0:T(8,128)S(1)}, f32[8,512]{1,0:T(8,128)S(1)}, f32[8,512]{1,0:T(8,128)S(1)}) custom-call(f32[4,4]{1,0:T(4,128)S(1)} %copy-done.5, bf16[256,1024]{1,0:T(8,128)(2,1)S(1)} %get-tuple-element.87.qt_ref, bf16[1024,256]{1,0:T(8,128)(2,1)S(1)} %get-tuple-element.88.k_ref, ...), custom_call_target="tpu_custom_call" | custom-call | flops 1 | bytes 1 | tf_op jit(solution)/shard_map/own/pallas_call | solution.py:631
  50.1 1.8 %collective-permute-done.18.refs_1_ = bf16[512,256]{1,0:T(8,128)(2,1)S(1)} collective-permute-done((bf16[512,256]{1,0:T(8,128)(2,1)S(1)}, bf16[512,256]{1,0:T(8,128)(2,1)S(1)}, u32[]{:S(2)}, u32[]{:S(2)}) %collective-permute-start.18) | collective-permute-done | bytes 262176 | tf_op jit(solution)/shard_map/ppermute | solution.py:56
  51.9 1.5 %collective-permute-done.21.refs_3_ = bf16[512,256]{1,0:T(8,128)(2,1)S(1)} collective-permute-done((bf16[512,256]{1,0:T(8,128)(2,1)S(1)}, bf16[512,256]{1,0:T(8,128)(2,1)S(1)}, u32[]{:S(2)}, u32[]{:S(2)}) %collective-permute-start.21) | collective-permute-done | bytes 262176 | tf_op jit(solution)/shard_map/ppermute | solution.py:56
  53.4 2.1 %window.1 = (bf16[2048,256]{1,0:T(8,128)(2,1)S(1)}, bf16[256,2048]{1,0:T(8,128)(2,1)S(1)}, bf16[64,256]{1,0:T(8,128)(2,1)S(1)}, bf16[256,64]{1,0:T(8,128)(2,1)S(1)}) custom-call(bf16[1024,256]{1,0:T(8,128)(2,1)S(1)} %get-tuple-element.88.k_ref, bf16[256,1024]{1,0:T(8,128)(2,1)S(1)} %get-tuple-element.89.vt_ref, ...), custom_call_target="tpu_custom_call" | custom-call | flops 1 | bytes 1 | tf_op jit(solution)/shard_map/window/pallas_call | solution.py:652
  55.6 3.4 %rest.2.refs_0_ = bf16[512,256]{1,0:T(8,128)(2,1)S(1)} custom-call(s32[4,8]{1,0:T(4,128)S(1)} %bitcast.1, f32[4,4]{1,0:T(4,128)S(1)} %copy-done.5, bf16[256,1024]{1,0:T(8,128)(2,1)S(1)} %get-tuple-element.87.qt_ref, bf16[2048,256]{1,0:T(8,128)(2,1)S(1)} %get-tuple-element.98.kw_ref, bf16[256,2048]{1,0:T(8,128)(2,1)S(1)} %get-tuple-element.99.vw_ref, ...), custom_call_target="tpu_custom_call" | custom-call | flops 1 | bytes 1 | tf_op jit(solution)/shard_map/rest/pallas_call | solution.py:694
  59.0 1.3 %collective-permute-start.22 = (bf16[512,256]{1,0:T(8,128)(2,1)S(1)}, bf16[512,256]{1,0:T(8,128)(2,1)S(1)}, u32[]{:S(2)}, u32[]{:S(2)}) collective-permute-start(bf16[512,256]{1,0:T(8,128)(2,1)S(1)} %rest.2.refs_0_), channel_id=1, source_target_pairs={{0,2},{2,0},{1,3},{3,1},{4,6},{6,4},{5,7},{7,5},{8,10},{10,8},{9,1... | collective-permute-start | bytes 786440 | tf_op jit(solution)/shard_map/ppermute | solution.py:56
  60.3 3.1 %rest.3.refs_0_ = bf16[512,256]{1,0:T(8,128)(2,1)S(1)} custom-call(s32[4,8]{1,0:T(4,128)S(1)} %bitcast.2, f32[4,4]{1,0:T(4,128)S(1)} %copy-done.5, bf16[256,1024]{1,0:T(8,128)(2,1)S(1)} %get-tuple-element.87.qt_ref, bf16[2048,256]{1,0:T(8,128)(2,1)S(1)} %get-tuple-element.98.kw_ref, bf16[256,2048]{1,0:T(8,128)(2,1)S(1)} %get-tuple-element.99.vw_ref, ...), custom_call_target="tpu_custom_call" | custom-call | flops 1 | bytes 1 | tf_op jit(solution)/shard_map/rest/pallas_call | solution.py:694
  63.4 0.9 %collective-permute-start.23 = (bf16[512,256]{1,0:T(8,128)(2,1)S(1)}, bf16[512,256]{1,0:T(8,128)(2,1)S(1)}, u32[]{:S(2)}, u32[]{:S(2)}) collective-permute-start(bf16[512,256]{1,0:T(8,128)(2,1)S(1)} %rest.3.refs_0_), channel_id=1, source_target_pairs={{0,2},{2,0},{1,3},{3,1},{4,6},{6,4},{5,7},{7,5},{8,10},{10,8},{9,1... | collective-permute-start | bytes 786440 | tf_op jit(solution)/shard_map/ppermute | solution.py:56
  64.3 3.9 %collective-permute-done.22.refs_1_ = bf16[512,256]{1,0:T(8,128)(2,1)S(1)} collective-permute-done((bf16[512,256]{1,0:T(8,128)(2,1)S(1)}, bf16[512,256]{1,0:T(8,128)(2,1)S(1)}, u32[]{:S(2)}, u32[]{:S(2)}) %collective-permute-start.22) | collective-permute-done | bytes 262176 | tf_op jit(solution)/shard_map/ppermute | solution.py:56
  68.7 4.3 %collective-permute-done.23.refs_4_.refs_1_ = bf16[512,256]{1,0:T(8,128)(2,1)S(1)} collective-permute-done((bf16[512,256]{1,0:T(8,128)(2,1)S(1)}, bf16[512,256]{1,0:T(8,128)(2,1)S(1)}, u32[]{:S(2)}, u32[]{:S(2)}) %collective-permute-start.23) | collective-permute-done | bytes 262176 | tf_op jit(solution)/shard_map/ppermute | solution.py:56
  73.0 1.3 %output.2.refs_4_ = bf16[1024,256]{1,0:T(8,128)(2,1)} custom-call(bf16[1024,256]{1,0:T(8,128)(2,1)S(1)} %copy-done, bf16[512,256]{1,0:T(8,128)(2,1)S(1)} %rest.2.refs_0_, bf16[512,256]{1,0:T(8,128)(2,1)S(1)} %collective-permute-done.22.refs_1_, bf16[512,256]{1,0:T(8,128)(2,1)S(1)} %collective-permute-done.26.refs_2_, ...), custom_call_target="tpu_custom_call" | custom-call | flops 1 | bytes 1 | tf_op jit(solution)/shard_map/output/pallas_call | solution.py:679
  74.5 1.3 %output.3 = bf16[1024,256]{1,0:T(8,128)(2,1)} custom-call(bf16[1024,256]{1,0:T(8,128)(2,1)S(1)} %copy-done, bf16[512,256]{1,0:T(8,128)(2,1)S(1)} %rest.3.refs_0_, bf16[512,256]{1,0:T(8,128)(2,1)S(1)} %collective-permute-done.23.refs_4_.refs_1_, bf16[512,256]{1,0:T(8,128)(2,1)S(1)} %collective-permute-done.24.refs_2_, ...), custom_call_target="tpu_custom_call", output_to_operand_aliasing={{}: (5, {})} | custom-call | flops 1 | bytes 1 | tf_op jit(solution)/shard_map/output/pallas_call | solution.py:679
  (57 shorter events, 2.7 us)
Async XLA Ops:
  0.0 12.3 %copy-start.4 = (bf16[1024,256]{1,0:T(8,128)(2,1)S(1)}, bf16[1024,256]{1,0:T(8,128)(2,1)}, u32[]{:S(2)}) copy-start(bf16[1024,256]{1,0:T(8,128)(2,1)} %wk_in.1) | copy-start | bytes 1572868
  0.0 12.3 %copy-start.2 = (bf16[1024,256]{1,0:T(8,128)(2,1)S(1)}, bf16[1024,256]{1,0:T(8,128)(2,1)}, u32[]{:S(2)}) copy-start(bf16[1024,256]{1,0:T(8,128)(2,1)} %wq_ref.1) | copy-start | bytes 1572868
  2.7 26.1 %copy-start.1 = (bf16[128,1024]{1,0:T(8,128)(2,1)S(1)}, bf16[128,1024]{1,0:T(8,128)(2,1)}, u32[]{:S(2)}) copy-start(bf16[128,1024]{1,0:T(8,128)(2,1)} %get-tuple-element.71.refs_10_.refs_14_) | copy-start | bytes 786436
  2.7 12.0 %collective-permute-start = (bf16[144,512]{1,0:T(8,128)(2,1)}, bf16[144,512]{1,0:T(8,128)(2,1)S(1)}, u32[]{:S(2)}, u32[]{:S(2)}) collective-permute-start(bf16[144,512]{1,0:T(8,128)(2,1)} %get-tuple-element.57), channel_id=1, source_target_pairs={{0,28},{1,25},{2,30},{3,27},{4,24},{5,29},{6,26},{7,31},{8,20},{9,... | collective-permute-start | bytes 442376 | tf_op jit(solution)/shard_map/ppermute | solution.py:126
  8.8 10.9 %collective-permute-start.2 = (bf16[144,512]{1,0:T(8,128)(2,1)}, bf16[144,512]{1,0:T(8,128)(2,1)S(1)}, u32[]{:S(2)}, u32[]{:S(2)}) collective-permute-start(bf16[144,512]{1,0:T(8,128)(2,1)} %get-tuple-element.67), channel_id=1, source_target_pairs={{0,12},{1,13},{2,14},{3,15},{4,8},{5,9},{6,10},{7,11},{8,4},{9,5},... | collective-permute-start | bytes 442376 | tf_op jit(solution)/shard_map/ppermute | solution.py:126
  8.8 13.3 %collective-permute-start.3 = (bf16[144,512]{1,0:T(8,128)(2,1)}, bf16[144,512]{1,0:T(8,128)(2,1)S(1)}, u32[]{:S(2)}, u32[]{:S(2)}) collective-permute-start(bf16[144,512]{1,0:T(8,128)(2,1)} %get-tuple-element.68), channel_id=1, source_target_pairs={{0,8},{1,9},{2,10},{3,11},{4,12},{5,13},{6,14},{7,15},{8,0},{9,1},... | collective-permute-start | bytes 442376 | tf_op jit(solution)/shard_map/ppermute | solution.py:126
  10.7 11.3 %collective-permute-start.4 = (bf16[144,512]{1,0:T(8,128)(2,1)}, bf16[144,512]{1,0:T(8,128)(2,1)S(1)}, u32[]{:S(2)}, u32[]{:S(2)}) collective-permute-start(bf16[144,512]{1,0:T(8,128)(2,1)} %get-tuple-element.69), channel_id=1, source_target_pairs={{0,4},{1,5},{2,6},{3,7},{4,0},{5,1},{6,2},{7,3},{8,12},{9,13},{10,... | collective-permute-start | bytes 442376 | tf_op jit(solution)/shard_map/ppermute | solution.py:126
  12.3 11.9 %collective-permute-start.1 = (bf16[144,512]{1,0:T(8,128)(2,1)}, bf16[144,512]{1,0:T(8,128)(2,1)S(1)}, u32[]{:S(2)}, u32[]{:S(2)}) collective-permute-start(bf16[144,512]{1,0:T(8,128)(2,1)} %get-tuple-element.66), channel_id=1, source_target_pairs={{0,20},{1,17},{2,22},{3,19},{4,16},{5,21},{6,18},{7,23},{8,28},{9,... | collective-permute-start | bytes 442376 | tf_op jit(solution)/shard_map/ppermute | solution.py:126
  22.1 5.0 %collective-permute-start.5 = (bf16[128,512]{1,0:T(8,128)(2,1)S(1)}, bf16[128,512]{1,0:T(8,128)(2,1)S(1)}, u32[]{:S(2)}, u32[]{:S(2)}) collective-permute-start(bf16[128,512]{1,0:T(8,128)(2,1)S(1)} %stack.3), channel_id=1, source_target_pairs={{0,2},{2,0},{1,3},{3,1},{4,6},{6,4},{5,7},{7,5},{8,10},{10,8},{9,1... | collective-permute-start | bytes 393224 | tf_op jit(solution)/shard_map/ppermute | solution.py:56
  23.6 3.6 %collective-permute-start.8 = (bf16[144,512]{1,0:T(8,128)(2,1)S(1)}, bf16[144,512]{1,0:T(8,128)(2,1)S(1)}, u32[]{:S(2)}, u32[]{:S(2)}) collective-permute-start(bf16[144,512]{1,0:T(8,128)(2,1)S(1)} %collective-permute-done.2.refs_1_.refs_4_.refs_2_.refs_8_), channel_id=1, source_target_pairs={{0,1},{1,0},{2,3},{3,2},{4,5},{5,4},{6,7},{7,6},{8,9},{9,8},{10,11... | collective-permute-start | bytes 442376 | tf_op jit(solution)/shard_map/ppermute | solution.py:56
  23.6 5.1 %collective-permute-start.9 = (bf16[144,512]{1,0:T(8,128)(2,1)S(1)}, bf16[144,512]{1,0:T(8,128)(2,1)S(1)}, u32[]{:S(2)}, u32[]{:S(2)}) collective-permute-start(bf16[144,512]{1,0:T(8,128)(2,1)S(1)} %collective-permute-done.3.refs_2_.refs_5_.refs_9_), channel_id=1, source_target_pairs={{0,1},{1,0},{2,3},{3,2},{4,5},{5,4},{6,7},{7,6},{8,9},{9,8},{10,11... | collective-permute-start | bytes 442376 | tf_op jit(solution)/shard_map/ppermute | solution.py:56
  24.2 4.6 %collective-permute-start.10 = (bf16[144,512]{1,0:T(8,128)(2,1)S(1)}, bf16[144,512]{1,0:T(8,128)(2,1)S(1)}, u32[]{:S(2)}, u32[]{:S(2)}) collective-permute-start(bf16[144,512]{1,0:T(8,128)(2,1)S(1)} %collective-permute-done.4.refs_3_.refs_6_.refs_10_), channel_id=1, source_target_pairs={{0,1},{1,0},{2,3},{3,2},{4,5},{5,4},{6,7},{7,6},{8,9},{9,8},{10,11... | collective-permute-start | bytes 442376 | tf_op jit(solution)/shard_map/ppermute | solution.py:56
  24.2 4.6 %collective-permute-start.6 = (bf16[144,512]{1,0:T(8,128)(2,1)S(1)}, bf16[144,512]{1,0:T(8,128)(2,1)S(1)}, u32[]{:S(2)}, u32[]{:S(2)}) collective-permute-start(bf16[144,512]{1,0:T(8,128)(2,1)S(1)} %collective-permute-done.refs_0_), channel_id=1, source_target_pairs={{0,1},{1,0},{2,3},{3,2},{4,5},{5,4},{6,7},{7,6},{8,9},{9,8},{10,11... | collective-permute-start | bytes 442376 | tf_op jit(solution)/shard_map/ppermute | solution.py:56
  27.1 1.7 %collective-permute-start.7 = (bf16[128,512]{1,0:T(8,128)(2,1)S(1)}, bf16[128,512]{1,0:T(8,128)(2,1)S(1)}, u32[]{:S(2)}, u32[]{:S(2)}) collective-permute-start(bf16[128,512]{1,0:T(8,128)(2,1)S(1)} %stack.4.refs_1_), channel_id=1, source_target_pairs={{0,1},{1,0},{2,3},{3,2},{4,5},{5,4},{6,7},{7,6},{8,9},{9,8},{10,11... | collective-permute-start | bytes 393224 | tf_op jit(solution)/shard_map/ppermute | solution.py:56
  27.2 6.4 %collective-permute-start.12 = (bf16[128,512]{1,0:T(8,128)(2,1)S(1)}, bf16[128,512]{1,0:T(8,128)(2,1)S(1)}, u32[]{:S(2)}, u32[]{:S(2)}) collective-permute-start(bf16[128,512]{1,0:T(8,128)(2,1)S(1)} %stack.4.refs_1_), channel_id=1, source_target_pairs={{0,2},{2,0},{1,3},{3,1},{4,6},{6,4},{5,7},{7,5},{8,10},{10,8},{9,1... | collective-permute-start | bytes 393224 | tf_op jit(solution)/shard_map/ppermute | solution.py:56
  29.3 14.8 %collective-permute-start.11 = (bf16[512,256]{1,0:T(8,128)(2,1)S(1)}, bf16[512,256]{1,0:T(8,128)(2,1)S(1)}, u32[]{:S(2)}, u32[]{:S(2)}) collective-permute-start(bf16[512,256]{1,0:T(8,128)(2,1)S(1)} %pack.1), channel_id=1, source_target_pairs={{0,4},{4,8},{8,12},{12,16},{16,20},{20,24},{24,28},{1,5},{5,9},{9,... | collective-permute-start | bytes 786440 | tf_op jit(solution)/shard_map/ppermute | solution.py:60
  32.3 1.9 %collective-permute-start.13 = (bf16[128,512]{1,0:T(8,128)(2,1)S(1)}, bf16[128,512]{1,0:T(8,128)(2,1)S(1)}, u32[]{:S(2)}, u32[]{:S(2)}) collective-permute-start(bf16[128,512]{1,0:T(8,128)(2,1)S(1)} %collective-permute-done.5.refs_2_), channel_id=1, source_target_pairs={{0,1},{1,0},{2,3},{3,2},{4,5},{5,4},{6,7},{7,6},{8,9},{9,8},{10,11... | collective-permute-start | bytes 393224 | tf_op jit(solution)/shard_map/ppermute | solution.py:56
  33.6 1.5 %collective-permute-start.14 = (bf16[128,512]{1,0:T(8,128)(2,1)S(1)}, bf16[128,512]{1,0:T(8,128)(2,1)S(1)}, u32[]{:S(2)}, u32[]{:S(2)}) collective-permute-start(bf16[128,512]{1,0:T(8,128)(2,1)S(1)} %collective-permute-done.12.refs_3_), channel_id=1, source_target_pairs={{0,1},{1,0},{2,3},{3,2},{4,5},{5,4},{6,7},{7,6},{8,9},{9,8},{10,11... | collective-permute-start | bytes 393224 | tf_op jit(solution)/shard_map/ppermute | solution.py:56
  37.0 7.1 %collective-permute-start.17 = (bf16[48,256]{1,0:T(8,128)(2,1)S(1)}, bf16[48,256]{1,0:T(8,128)(2,1)S(1)}, u32[]{:S(2)}, u32[]{:S(2)}) collective-permute-start(bf16[48,256]{1,0:T(8,128)(2,1)S(1)} %get-tuple-element.82.refs_0_), channel_id=1, source_target_pairs={{0,24},{4,28},{8,16},{12,20},{16,8},{20,12},{24,0},{28,4},{1,25},{... | collective-permute-start | bytes 73736 | tf_op jit(solution)/shard_map/ppermute | solution.py:116
  38.7 5.4 %collective-permute-start.16 = (bf16[48,256]{1,0:T(8,128)(2,1)S(1)}, bf16[48,256]{1,0:T(8,128)(2,1)S(1)}, u32[]{:S(2)}, u32[]{:S(2)}) collective-permute-start(bf16[48,256]{1,0:T(8,128)(2,1)S(1)} %get-tuple-element.82.refs_0_), channel_id=1, source_target_pairs={{0,16},{4,20},{8,24},{12,28},{16,0},{20,4},{24,8},{28,12},{1,17},{... | collective-permute-start | bytes 73736 | tf_op jit(solution)/shard_map/ppermute | solution.py:116
  38.7 5.4 %collective-permute-start.15 = (bf16[48,256]{1,0:T(8,128)(2,1)S(1)}, bf16[48,256]{1,0:T(8,128)(2,1)S(1)}, u32[]{:S(2)}, u32[]{:S(2)}) collective-permute-start(bf16[48,256]{1,0:T(8,128)(2,1)S(1)} %get-tuple-element.82.refs_0_), channel_id=1, source_target_pairs={{0,8},{4,12},{8,0},{12,4},{16,24},{20,28},{24,16},{28,20},{1,9},{5... | collective-permute-start | bytes 73736 | tf_op jit(solution)/shard_map/ppermute | solution.py:116
  44.1 7.8 %collective-permute-start.18 = (bf16[512,256]{1,0:T(8,128)(2,1)S(1)}, bf16[512,256]{1,0:T(8,128)(2,1)S(1)}, u32[]{:S(2)}, u32[]{:S(2)}) collective-permute-start(bf16[512,256]{1,0:T(8,128)(2,1)S(1)} %collective-permute-done.11.refs_0_), channel_id=1, source_target_pairs={{0,2},{2,0},{1,3},{3,1},{4,6},{6,4},{5,7},{7,5},{8,10},{10,8},{9,1... | collective-permute-start | bytes 786440 | tf_op jit(solution)/shard_map/ppermute | solution.py:56
  45.4 4.7 %collective-permute-start.19 = (bf16[192,256]{1,0:T(8,128)(2,1)S(1)}, bf16[192,256]{1,0:T(8,128)(2,1)S(1)}, u32[]{:S(2)}, u32[]{:S(2)}) collective-permute-start(bf16[192,256]{1,0:T(8,128)(2,1)S(1)} %stack.5.refs_4_), channel_id=1, source_target_pairs={{0,4},{4,0},{8,12},{12,8},{16,20},{20,16},{24,28},{28,24},{1,5},{5... | collective-permute-start | bytes 294920 | tf_op jit(solution)/shard_map/ppermute | solution.py:116
  45.9 6.0 %collective-permute-start.20 = (bf16[512,256]{1,0:T(8,128)(2,1)S(1)}, bf16[512,256]{1,0:T(8,128)(2,1)S(1)}, u32[]{:S(2)}, u32[]{:S(2)}) collective-permute-start(bf16[512,256]{1,0:T(8,128)(2,1)S(1)} %collective-permute-done.11.refs_0_), channel_id=1, source_target_pairs={{0,1},{1,0},{2,3},{3,2},{4,5},{5,4},{6,7},{7,6},{8,9},{9,8},{10,11... | collective-permute-start | bytes 786440 | tf_op jit(solution)/shard_map/ppermute | solution.py:56
  51.9 1.5 %collective-permute-start.21 = (bf16[512,256]{1,0:T(8,128)(2,1)S(1)}, bf16[512,256]{1,0:T(8,128)(2,1)S(1)}, u32[]{:S(2)}, u32[]{:S(2)}) collective-permute-start(bf16[512,256]{1,0:T(8,128)(2,1)S(1)} %collective-permute-done.18.refs_1_), channel_id=1, source_target_pairs={{0,1},{1,0},{2,3},{3,2},{4,5},{5,4},{6,7},{7,6},{8,9},{9,8},{10,11... | collective-permute-start | bytes 786440 | tf_op jit(solution)/shard_map/ppermute | solution.py:56
  59.0 14.0 %copy-start = (bf16[1024,256]{1,0:T(8,128)(2,1)S(1)}, bf16[1024,256]{1,0:T(8,128)(2,1)}, u32[]{:S(2)}) copy-start(bf16[1024,256]{1,0:T(8,128)(2,1)} %w_ref.3) | copy-start | bytes 1572868
  59.0 9.2 %collective-permute-start.22 = (bf16[512,256]{1,0:T(8,128)(2,1)S(1)}, bf16[512,256]{1,0:T(8,128)(2,1)S(1)}, u32[]{:S(2)}, u32[]{:S(2)}) collective-permute-start(bf16[512,256]{1,0:T(8,128)(2,1)S(1)} %rest.2.refs_0_), channel_id=1, source_target_pairs={{0,2},{2,0},{1,3},{3,1},{4,6},{6,4},{5,7},{7,5},{8,10},{10,8},{9,1... | collective-permute-start | bytes 786440 | tf_op jit(solution)/shard_map/ppermute | solution.py:56
  63.4 9.6 %collective-permute-start.23 = (bf16[512,256]{1,0:T(8,128)(2,1)S(1)}, bf16[512,256]{1,0:T(8,128)(2,1)S(1)}, u32[]{:S(2)}, u32[]{:S(2)}) collective-permute-start(bf16[512,256]{1,0:T(8,128)(2,1)S(1)} %rest.3.refs_0_), channel_id=1, source_target_pairs={{0,2},{2,0},{1,3},{3,1},{4,6},{6,4},{5,7},{7,5},{8,10},{10,8},{9,1... | collective-permute-start | bytes 786440 | tf_op jit(solution)/shard_map/ppermute | solution.py:56
  64.3 8.7 %collective-permute-start.26 = (bf16[512,256]{1,0:T(8,128)(2,1)S(1)}, bf16[512,256]{1,0:T(8,128)(2,1)S(1)}, u32[]{:S(2)}, u32[]{:S(2)}) collective-permute-start(bf16[512,256]{1,0:T(8,128)(2,1)S(1)} %rest.2.refs_0_), channel_id=1, source_target_pairs={{0,1},{1,0},{2,3},{3,2},{4,5},{5,4},{6,7},{7,6},{8,9},{9,8},{10,11... | collective-permute-start | bytes 786440 | tf_op jit(solution)/shard_map/ppermute | solution.py:56
  68.2 4.8 %collective-permute-start.27 = (bf16[512,256]{1,0:T(8,128)(2,1)S(1)}, bf16[512,256]{1,0:T(8,128)(2,1)S(1)}, u32[]{:S(2)}, u32[]{:S(2)}) collective-permute-start(bf16[512,256]{1,0:T(8,128)(2,1)S(1)} %collective-permute-done.22.refs_1_), channel_id=1, source_target_pairs={{0,1},{1,0},{2,3},{3,2},{4,5},{5,4},{6,7},{7,6},{8,9},{9,8},{10,11... | collective-permute-start | bytes 786440 | tf_op jit(solution)/shard_map/ppermute | solution.py:56
  68.2 6.1 %collective-permute-start.24 = (bf16[512,256]{1,0:T(8,128)(2,1)S(1)}, bf16[512,256]{1,0:T(8,128)(2,1)S(1)}, u32[]{:S(2)}, u32[]{:S(2)}) collective-permute-start(bf16[512,256]{1,0:T(8,128)(2,1)S(1)} %rest.3.refs_0_), channel_id=1, source_target_pairs={{0,1},{1,0},{2,3},{3,2},{4,5},{5,4},{6,7},{7,6},{8,9},{9,8},{10,11... | collective-permute-start | bytes 786440 | tf_op jit(solution)/shard_map/ppermute | solution.py:56
  73.0 1.5 %collective-permute-start.25 = (bf16[512,256]{1,0:T(8,128)(2,1)S(1)}, bf16[512,256]{1,0:T(8,128)(2,1)S(1)}, u32[]{:S(2)}, u32[]{:S(2)}) collective-permute-start(bf16[512,256]{1,0:T(8,128)(2,1)S(1)} %collective-permute-done.23.refs_4_.refs_1_), channel_id=1, source_target_pairs={{0,1},{1,0},{2,3},{3,2},{4,5},{5,4},{6,7},{7,6},{8,9},{9,8},{10,11... | collective-permute-start | bytes 786440 | tf_op jit(solution)/shard_map/ppermute | solution.py:56
  (5 other events, 45.0 us)

commit v14 on v13

--- a/solution.py
+++ b/solution.py
@@ -61,22 +61,31 @@
 
 
 def send_kernel(tokens_ref, mask_ref, *refs):
-    outs, own = refs[:-1], refs[-1]
+    outs, own, sem_ref = refs[:-2], refs[-2], refs[-1]
     slab, head = lax.axis_index("seq"), lax.axis_index("head")
     core = head & 1
     rows, width = own.shape
     half = width // 2
+    sides = (head >> 1, head >> 1, core, core, core)
+    loads = []
+    for distance, side, out in zip((7 - core, 5 - core, 3, 2, 1), sides, outs):
+        row = pl.multiple_of((slab ^ distance) * rows, rows)
+        start = pl.multiple_of(side * half, half)
+        loads.append((tokens_ref.at[pl.ds(row, rows), pl.ds(start, half)], out.at[:rows]))
+    loads.append((tokens_ref.at[pl.ds(pl.multiple_of(slab * rows, rows), rows)], own))
+    copies = [
+        pltpu.make_async_copy(source, target, sem_ref.at[index])
+        for index, (source, target) in enumerate(loads)
+    ]
+    for copy in copies:
+        copy.start()
     ids = mask_ref[...]
     line = iota((CODE_ROWS, ids.shape[1]), 0)
     code = jnp.where(line == 0, ids >> 5, jnp.where(line == 1, ids & 31, 0)).astype(F32).astype(BF)
-    sides = (head >> 1, head >> 1, core, core, core)
-    for distance, side, out in zip((7 - core, 5 - core, 3, 2, 1), sides, outs):
-        row = pl.multiple_of((slab ^ distance) * rows, rows)
-        start = pl.multiple_of(side * half, half)
-        out[:rows] = tokens_ref[pl.ds(row, rows), pl.ds(start, half)]
-        if out.shape[0] > rows:
-            out[rows : rows + CODE_ROWS] = code
-    own[...] = tokens_ref[pl.ds(pl.multiple_of(slab * rows, rows), rows)]
+    for out in outs:
+        out[rows:] = code
+    for copy in copies:
+        copy.wait()
 
 
 def stack_kernel(places, *refs):
@@ -126,7 +135,7 @@
     return lax.ppermute(block, ("seq", "head"), pairs)
 
 
-def exchange_tokens(tokens, mask_ids, prepare, expand):
+def exchange_tokens(tokens, mask_ids, prepare):
     tok_rows, width = tokens.shape
     slabs = lax.axis_size("seq")
     rows = tok_rows // slabs
@@ -142,8 +151,7 @@
         fourth = over_head(third, CORE_PAIRS)
         prepared = prepare()
         halo = to_next(packed_rows(prepared[2], tok_rows - mask_ids.shape[1], quarter, [first]))
-        expanded = expand(prepared, [to_next(mask_ids)])
-        return [first, third, second, fourth], prepared, expanded, halo
+        return [first, third, second, fourth], prepared, [to_next(mask_ids)], halo
     half = width // 2
     tall = rows + CODE_ROWS
     *blocks, own = pl.pallas_call(
@@ -156,8 +164,9 @@
             jax.ShapeDtypeStruct((tall, half), BF),
             jax.ShapeDtypeStruct((rows, width), BF),
         ),
-        in_specs=vmem_specs(2),
+        in_specs=[pl.BlockSpec(memory_space=pl.ANY)] + vmem_specs(1),
         out_specs=vmem_specs(6),
+        scratch_shapes=[pltpu.SemaphoreType.DMA((6,))],
         compiler_params=pltpu.CompilerParams(vmem_limit_bytes=60 * 1024 * 1024),
         cost_estimate=COST,
         name="send",
@@ -174,14 +183,13 @@
     far_x = [first_x, over_head(two, X_PAIRS)]
     near = [three, four, five]
     near_core = [over_head(part, CORE_PAIRS) for part in near]
-    expanded = expand(prepared, [one, far_core[0], three, five])
     halo = packed_rows(
         prepared[2], tok_rows - mask_ids.shape[1], half // 2, far + far_core + near + near_core + [own]
     )
-    far_x[1], _, _ = lax.optimization_barrier((far_x[1], expanded, halo))
+    far_x[1], _ = lax.optimization_barrier((far_x[1], halo))
     halo = to_next(halo)
     far_last = [over_head(part, CORE_PAIRS) for part in far_x]
-    return far + far_x + far_core + far_last + near + near_core + [own], prepared, expanded, halo
+    return far + far_x + far_core + far_last + near + near_core + [own], prepared, [one, far_core[0], three, five], halo
 
 
 def column(row, lanes=128):
@@ -562,7 +570,7 @@
             name="prepare",
         )(order, mask_ids, w_query, w_value, w_key)
 
-    def expand(prepared, sources):
+    def expand(seen, sources):
         return pl.pallas_call(
             functools.partial(expand_kernel, tok_rows // slabs),
             out_shape=(
@@ -575,11 +583,10 @@
             compiler_params=params,
             cost_estimate=COST,
             name="expand",
-        )(prepared[5], *sources)
-
-    pieces, prepared, expanded, halo = exchange_tokens(tokens, mask_ids, prepare, expand)
+        )(seen, *sources)
+
+    pieces, prepared, before, halo = exchange_tokens(tokens, mask_ids, prepare)
     permute, permute_t, select, f_col, f_row, seen, w_t, w_k = prepared
-    spread, spread_t, bias = expanded
     summ, k0, v0, rows_here = pl.pallas_call(
         functools.partial(project_kernel, len(pieces)),
         out_shape=(
@@ -649,6 +656,8 @@
 
     halo_x, _, *summaries = lax.optimization_barrier((halo_x, top, *summaries))
     halo_last = over_head(halo_x, CORE_PAIRS)
+    seen, _ = lax.optimization_barrier((seen, top))
+    spread, spread_t, bias = expand(seen, before)
     window_k, window_v, coarse_k, coarse_v = pl.pallas_call(
         window_kernel,
         out_shape=(

time: 76 us -> 75.6 us (level)
  waiting for transfers between devices: 22.7 us -> 21.7 us
  transfers between devices with their start and end apart: 28 -> 28, of which waited for: 10 -> 11; matrix products, arithmetic and copies ran while one was open for 0% -> 0% of each run, Pallas kernels for 23% -> 23%
where the time goes in v14:
time: 75.6 us; the launch traced here: 75.5 us
  Pallas kernels  26.9 us (36%)
  starting transfers between devices  26.5 us (35%)
  waiting for transfers between devices  21.7 us (29%)
    ppermute x18, waiting for transfers between devices, over_head(): return lax.ppermute(block, 'head', pairs)  14.4 us
    ppermute x5, starting transfers between devices, by_core(): return lax.ppermute(block, ('seq', 'head'), pairs)  9.58 us
    ppermute x18, starting transfers between devices, over_head(): return lax.ppermute(block, 'head', pairs)  8.52 us
    ppermute x5, waiting for transfers between devices, by_core(): return lax.ppermute(block, ('seq', 'head'), pairs)  7.28 us
    pallas_call x2, Pallas kernels, local(): pl.pallas_call(functools.partial(rest_kernel, first, count), out_shape=sh...  6.54 us
    ppermute x4, starting transfers between devices, by_distance(): lax.ppermute(block, 'seq', [(i, i ^ distance) for i in range(lax.axis_siz...  5.4 us
    pallas_call x1, Pallas kernels, local(): pl.pallas_call(own_kernel, out_shape=(shape((group, tok_rows), F32), shap...  3.94 us
    pallas_call x1, Pallas kernels, exchange_tokens(): pl.pallas_call(send_kernel, out_shape=(jax.ShapeDtypeStruct((tall, half),...  3.06 us
  transfers between devices with their start and end apart: 28, of which 11 were waited for; matrix products, arithmetic and copies ran while one was open for 0% of the time, Pallas kernels for 23%

profile of v14, /device:TPU:0, one launch (start us, length us, event | category | flops | bytes accessed | tf_op | source)
XLA Modules:
  0.0 75.5 jit_solution(17154096539696943395)
XLA Ops:
  0.0 3.1 %send.1 = (bf16[144,512]{1,0:T(8,128)(2,1)}, bf16[144,512]{1,0:T(8,128)(2,1)}, bf16[144,512]{1,0:T(8,128)(2,1)}, bf16[144,512]{1,0:T(8,128)(2,1)}, bf16[144,512]{1,0:T(8,128)(2,1)}, /*index=5*/bf16[128,1024]{1,0:T(8,128)(2,1)}) custom-call(bf16[1024,1024]{1,0:T(8,128)(2,1)} %tokens_ref.1, s32[1,512]{1,0:T(1,128)} %mask_ref.3), custom_call_target="tpu_custom_call" | custom-call | flops 1 | bytes 1 | tf_op jit(solution)/shard_map/send/pallas_call | solution.py:157
  3.1 6.1 %collective-permute-start = (bf16[144,512]{1,0:T(8,128)(2,1)}, bf16[144,512]{1,0:T(8,128)(2,1)S(1)}, u32[]{:S(2)}, u32[]{:S(2)}) collective-permute-start(bf16[144,512]{1,0:T(8,128)(2,1)} %get-tuple-element.58), channel_id=1, source_target_pairs={{0,28},{1,25},{2,30},{3,27},{4,24},{5,29},{6,26},{7,31},{8,20},{9,... | collective-permute-start | bytes 442376 | tf_op jit(solution)/shard_map/ppermute | solution.py:135
  9.2 2.0 %collective-permute-start.3 = (bf16[144,512]{1,0:T(8,128)(2,1)}, bf16[144,512]{1,0:T(8,128)(2,1)S(1)}, u32[]{:S(2)}, u32[]{:S(2)}) collective-permute-start(bf16[144,512]{1,0:T(8,128)(2,1)} %get-tuple-element.69), channel_id=1, source_target_pairs={{0,8},{1,9},{2,10},{3,11},{4,12},{5,13},{6,14},{7,15},{8,0},{9,1},... | collective-permute-start | bytes 442376 | tf_op jit(solution)/shard_map/ppermute | solution.py:135
  11.1 1.5 %collective-permute-start.4 = (bf16[144,512]{1,0:T(8,128)(2,1)}, bf16[144,512]{1,0:T(8,128)(2,1)S(1)}, u32[]{:S(2)}, u32[]{:S(2)}) collective-permute-start(bf16[144,512]{1,0:T(8,128)(2,1)} %get-tuple-element.70), channel_id=1, source_target_pairs={{0,4},{1,5},{2,6},{3,7},{4,0},{5,1},{6,2},{7,3},{8,12},{9,13},{10,... | collective-permute-start | bytes 442376 | tf_op jit(solution)/shard_map/ppermute | solution.py:135
  12.7 2.5 %prepare.1 = (bf16[1024,1024]{1,0:T(8,128)(2,1)S(1)}, bf16[1024,1024]{1,0:T(8,128)(2,1)S(1)}, bf16[672,1024]{1,0:T(8,128)(2,1)S(1)}, f32[160,128]{1,0:T(8,128)S(...) custom-call(s32[1,1024]{1,0:T(1,128)S(1)} %copy-done.8, ...), custom_call_target="tpu_custom_call" | custom-call | flops 1 | bytes 1 | tf_op jit(solution)/shard_map/prepare/pallas_call | solution.py:554
  15.2 4.8 %collective-permute-done.2.refs_1_.refs_4_.refs_8_.refs_2_ = bf16[144,512]{1,0:T(8,128)(2,1)S(1)} collective-permute-done((bf16[144,512]{1,0:T(8,128)(2,1)}, bf16[144,512]{1,0:T(8,128)(2,1)S(1)}, u32[]{:S(2)}, u32[]{:S(2)}) %collective-permute-start.2) | collective-permute-done | bytes 147488 | tf_op jit(solution)/shard_map/ppermute | solution.py:135
  20.0 2.4 %collective-permute-done.3.refs_2_.refs_5_.refs_9_ = bf16[144,512]{1,0:T(8,128)(2,1)S(1)} collective-permute-done((bf16[144,512]{1,0:T(8,128)(2,1)}, bf16[144,512]{1,0:T(8,128)(2,1)S(1)}, u32[]{:S(2)}, u32[]{:S(2)}) %collective-permute-start.3) | collective-permute-done | bytes 147488 | tf_op jit(solution)/shard_map/ppermute | solution.py:135
  22.5 1.6 %collective-permute-start.5 = (bf16[128,512]{1,0:T(8,128)(2,1)S(1)}, bf16[128,512]{1,0:T(8,128)(2,1)S(1)}, u32[]{:S(2)}, u32[]{:S(2)}) collective-permute-start(bf16[128,512]{1,0:T(8,128)(2,1)S(1)} %stack.3), channel_id=1, source_target_pairs={{0,2},{2,0},{1,3},{3,1},{4,6},{6,4},{5,7},{7,5},{8,10},{10,8},{9,1... | collective-permute-start | bytes 393224 | tf_op jit(solution)/shard_map/ppermute | solution.py:56
  25.1 2.5 %collective-permute-done.5.refs_2_ = bf16[128,512]{1,0:T(8,128)(2,1)S(1)} collective-permute-done((bf16[128,512]{1,0:T(8,128)(2,1)S(1)}, bf16[128,512]{1,0:T(8,128)(2,1)S(1)}, u32[]{:S(2)}, u32[]{:S(2)}) %collective-permute-start.5) | collective-permute-done | bytes 131104 | tf_op jit(solution)/shard_map/ppermute | solution.py:56
  27.6 1.6 %collective-permute-start.12 = (bf16[128,512]{1,0:T(8,128)(2,1)S(1)}, bf16[128,512]{1,0:T(8,128)(2,1)S(1)}, u32[]{:S(2)}, u32[]{:S(2)}) collective-permute-start(bf16[128,512]{1,0:T(8,128)(2,1)S(1)} %stack.4.refs_1_), channel_id=1, source_target_pairs={{0,2},{2,0},{1,3},{3,1},{4,6},{6,4},{5,7},{7,5},{8,10},{10,8},{9,1... | collective-permute-start | bytes 393224 | tf_op jit(solution)/shard_map/ppermute | solution.py:56
  29.7 3.0 %collective-permute-start.11 = (bf16[512,256]{1,0:T(8,128)(2,1)S(1)}, bf16[512,256]{1,0:T(8,128)(2,1)S(1)}, u32[]{:S(2)}, u32[]{:S(2)}) collective-permute-start(bf16[512,256]{1,0:T(8,128)(2,1)S(1)} %pack.1), channel_id=1, source_target_pairs={{0,4},{4,8},{8,12},{12,16},{16,20},{20,24},{24,28},{1,5},{5,9},{9,... | collective-permute-start | bytes 786440 | tf_op jit(solution)/shard_map/ppermute | solution.py:60
  32.8 0.7 collective-permute-done.12.refs_3_
  33.5 0.6 collective-permute-done.13.refs_6_
  34.1 0.8 collective-permute-done.14.refs_7_
  34.9 1.8 %project.1 = (bf16[48,256]{1,0:T(8,128)(2,1)S(1)}, bf16[1024,256]{1,0:T(8,128)(2,1)S(1)}, bf16[256,1024]{1,0:T(8,128)(2,1)S(1)}, bf16[1024,1024]{1,0:T(8,128)(2,1)S(1)}) custom-call(bf16[144,512]{1,0:T(8,128)(2,1)S(1)} %collective-permute-done.refs_0_, bf16[128,512]{1,0:T(8,128)(2,1)S(1)} %stack.4.refs_1_, ...), custom_call_target="tpu_custom_call" | custom-call | flops 1 | bytes 1 | tf_op jit(solution)/shard_map/project/pallas_call | solution.py:590
  36.7 2.1 %collective-permute-start.17 = (bf16[48,256]{1,0:T(8,128)(2,1)S(1)}, bf16[48,256]{1,0:T(8,128)(2,1)S(1)}, u32[]{:S(2)}, u32[]{:S(2)}) collective-permute-start(bf16[48,256]{1,0:T(8,128)(2,1)S(1)} %get-tuple-element.80.refs_0_), channel_id=1, source_target_pairs={{0,24},{4,28},{8,16},{12,20},{16,8},{20,12},{24,0},{28,4},{1,25},{... | collective-permute-start | bytes 73736 | tf_op jit(solution)/shard_map/ppermute | solution.py:125
  38.8 2.3 %collective-permute-start.15 = (bf16[48,256]{1,0:T(8,128)(2,1)S(1)}, bf16[48,256]{1,0:T(8,128)(2,1)S(1)}, u32[]{:S(2)}, u32[]{:S(2)}) collective-permute-start(bf16[48,256]{1,0:T(8,128)(2,1)S(1)} %get-tuple-element.80.refs_0_), channel_id=1, source_target_pairs={{0,8},{4,12},{8,0},{12,4},{16,24},{20,28},{24,16},{28,20},{1,9},{5... | collective-permute-start | bytes 73736 | tf_op jit(solution)/shard_map/ppermute | solution.py:125
  41.1 2.7 %order.1 = (bf16[256,1024]{1,0:T(8,128)(2,1)S(1)}, bf16[256,1024]{1,0:T(8,128)(2,1)S(1)}, bf16[1024,256]{1,0:T(8,128)(2,1)S(1)}, bf16[128,256]{1,0:T(8,128)(2,1)S(1)}, bf16[256,128]{1,0:T(8,128)(2,1)S(1)}) custom-call(bf16[1024,1024]{1,0:T(8,128)(2,1)S(1)} %get-tuple-element.59.p_ref, bf16[1024,1024]{1,0:T(8,128)(2,1)S(1)} %get-tuple-element.60.pt_ref, ...), custom_call_target="tpu_custom_call" | custom-call | flops 1 | bytes 1 | tf_op jit(solution)/shard_map/order/pallas_call | solution.py:609
  43.8 1.6 %collective-permute-start.18 = (bf16[512,256]{1,0:T(8,128)(2,1)S(1)}, bf16[512,256]{1,0:T(8,128)(2,1)S(1)}, u32[]{:S(2)}, u32[]{:S(2)}) collective-permute-start(bf16[512,256]{1,0:T(8,128)(2,1)S(1)} %collective-permute-done.11.refs_0_), channel_id=1, source_target_pairs={{0,2},{2,0},{1,3},{3,1},{4,6},{6,4},{5,7},{7,5},{8,10},{10,8},{9,1... | collective-permute-start | bytes 786440 | tf_op jit(solution)/shard_map/ppermute | solution.py:56
  45.4 1.0 %collective-permute-start.19 = (bf16[192,256]{1,0:T(8,128)(2,1)S(1)}, bf16[192,256]{1,0:T(8,128)(2,1)S(1)}, u32[]{:S(2)}, u32[]{:S(2)}) collective-permute-start(bf16[192,256]{1,0:T(8,128)(2,1)S(1)} %stack.5.refs_4_), channel_id=1, source_target_pairs={{0,4},{4,0},{8,12},{12,8},{16,20},{20,16},{24,28},{28,24},{1,5},{5... | collective-permute-start | bytes 294920 | tf_op jit(solution)/shard_map/ppermute | solution.py:125
  46.4 3.9 %own.1 = (f32[256,1024]{1,0:T(8,128)S(1)}, f32[256,1024]{1,0:T(8,128)S(1)}, f32[8,512]{1,0:T(8,128)S(1)}, f32[8,512]{1,0:T(8,128)S(1)}) custom-call(f32[4,4]{1,0:T(4,128)S(1)} %copy-done.5, bf16[256,1024]{1,0:T(8,128)(2,1)S(1)} %get-tuple-element.85.qt_ref, bf16[1024,256]{1,0:T(8,128)(2,1)S(1)} %get-tuple-element.86.k_ref, ...), custom_call_target="tpu_custom_call" | custom-call | flops 1 | bytes 1 | tf_op jit(solution)/shard_map/own/pallas_call | solution.py:638
  50.3 1.1 %collective-permute-done.18.refs_1_ = bf16[512,256]{1,0:T(8,128)(2,1)S(1)} collective-permute-done((bf16[512,256]{1,0:T(8,128)(2,1)S(1)}, bf16[512,256]{1,0:T(8,128)(2,1)S(1)}, u32[]{:S(2)}, u32[]{:S(2)}) %collective-permute-start.18) | collective-permute-done | bytes 262176 | tf_op jit(solution)/shard_map/ppermute | solution.py:56
  51.4 1.2 %expand.1 = (bf16[1024,512]{1,0:T(8,128)(2,1)S(1)}, bf16[512,1024]{1,0:T(8,128)(2,1)S(1)}, f32[2048,128]{1,0:T(8,128)S(1)}) custom-call(f32[1024,128]{1,0:T(8,128)S(1)} %get-tuple-element.91.seen_ref, bf16[144,512]{1,0:T(8,128)(2,1)S(1)} %collective-permute-done.refs_0_, bf16[144,512]{1,0:T(8,128)(2,1)S(1)} %collective-permute-done.6.refs_2_.refs_4_.refs_1_, ...), custom_call_target="tpu_custom_call" | custom-call | flops 1 | bytes 1 | tf_op jit(solution)/shard_map/expand/pallas_call | solution.py:574
  52.9 2.1 %window.1 = (bf16[2048,256]{1,0:T(8,128)(2,1)S(1)}, bf16[256,2048]{1,0:T(8,128)(2,1)S(1)}, bf16[64,256]{1,0:T(8,128)(2,1)S(1)}, bf16[256,64]{1,0:T(8,128)(2,1)S(1)}) custom-call(bf16[1024,256]{1,0:T(8,128)(2,1)S(1)} %get-tuple-element.86.k_ref, bf16[256,1024]{1,0:T(8,128)(2,1)S(1)} %get-tuple-element.87.vt_ref, ...), custom_call_target="tpu_custom_call" | custom-call | flops 1 | bytes 1 | tf_op jit(solution)/shard_map/window/pallas_call | solution.py:661
  55.1 3.4 %rest.2.refs_0_ = bf16[512,256]{1,0:T(8,128)(2,1)S(1)} custom-call(s32[4,8]{1,0:T(4,128)S(1)} %bitcast.1, f32[4,4]{1,0:T(4,128)S(1)} %copy-done.5, bf16[256,1024]{1,0:T(8,128)(2,1)S(1)} %get-tuple-element.85.qt_ref, bf16[2048,256]{1,0:T(8,128)(2,1)S(1)} %get-tuple-element.99.kw_ref, bf16[256,2048]{1,0:T(8,128)(2,1)S(1)} %get-tuple-element.100.vw_ref, ...), custom_call_target="tpu_custom_call" | custom-call | flops 1 | bytes 1 | tf_op jit(solution)/shard_map/rest/pallas_call | solution.py:703
  58.5 1.6 %collective-permute-start.22 = (bf16[512,256]{1,0:T(8,128)(2,1)S(1)}, bf16[512,256]{1,0:T(8,128)(2,1)S(1)}, u32[]{:S(2)}, u32[]{:S(2)}) collective-permute-start(bf16[512,256]{1,0:T(8,128)(2,1)S(1)} %rest.2.refs_0_), channel_id=1, source_target_pairs={{0,2},{2,0},{1,3},{3,1},{4,6},{6,4},{5,7},{7,5},{8,10},{10,8},{9,1... | collective-permute-start | bytes 786440 | tf_op jit(solution)/shard_map/ppermute | solution.py:56
  60.1 3.2 %rest.3.refs_0_ = bf16[512,256]{1,0:T(8,128)(2,1)S(1)} custom-call(s32[4,8]{1,0:T(4,128)S(1)} %bitcast.2, f32[4,4]{1,0:T(4,128)S(1)} %copy-done.5, bf16[256,1024]{1,0:T(8,128)(2,1)S(1)} %get-tuple-element.85.qt_ref, bf16[2048,256]{1,0:T(8,128)(2,1)S(1)} %get-tuple-element.99.kw_ref, bf16[256,2048]{1,0:T(8,128)(2,1)S(1)} %get-tuple-element.100.vw_ref, ...), custom_call_target="tpu_custom_call" | custom-call | flops 1 | bytes 1 | tf_op jit(solution)/shard_map/rest/pallas_call | solution.py:703
  63.2 0.6 collective-permute-start.23
  63.8 3.9 %collective-permute-done.22.refs_1_ = bf16[512,256]{1,0:T(8,128)(2,1)S(1)} collective-permute-done((bf16[512,256]{1,0:T(8,128)(2,1)S(1)}, bf16[512,256]{1,0:T(8,128)(2,1)S(1)}, u32[]{:S(2)}, u32[]{:S(2)}) %collective-permute-start.22) | collective-permute-done | bytes 262176 | tf_op jit(solution)/shard_map/ppermute | solution.py:56
  68.2 4.4 %collective-permute-done.23.refs_4_.refs_1_ = bf16[512,256]{1,0:T(8,128)(2,1)S(1)} collective-permute-done((bf16[512,256]{1,0:T(8,128)(2,1)S(1)}, bf16[512,256]{1,0:T(8,128)(2,1)S(1)}, u32[]{:S(2)}, u32[]{:S(2)}) %collective-permute-start.23) | collective-permute-done | bytes 262176 | tf_op jit(solution)/shard_map/ppermute | solution.py:56
  72.7 1.3 %output.2.refs_4_ = bf16[1024,256]{1,0:T(8,128)(2,1)} custom-call(bf16[1024,256]{1,0:T(8,128)(2,1)S(1)} %copy-done, bf16[512,256]{1,0:T(8,128)(2,1)S(1)} %rest.2.refs_0_, bf16[512,256]{1,0:T(8,128)(2,1)S(1)} %collective-permute-done.22.refs_1_, bf16[512,256]{1,0:T(8,128)(2,1)S(1)} %collective-permute-done.26.refs_2_, ...), custom_call_target="tpu_custom_call" | custom-call | flops 1 | bytes 1 | tf_op jit(solution)/shard_map/output/pallas_call | solution.py:688
  74.2 1.3 %output.3 = bf16[1024,256]{1,0:T(8,128)(2,1)} custom-call(bf16[1024,256]{1,0:T(8,128)(2,1)S(1)} %copy-done, bf16[512,256]{1,0:T(8,128)(2,1)S(1)} %rest.3.refs_0_, bf16[512,256]{1,0:T(8,128)(2,1)S(1)} %collective-permute-done.23.refs_4_.refs_1_, bf16[512,256]{1,0:T(8,128)(2,1)S(1)} %collective-permute-done.24.refs_2_, ...), custom_call_target="tpu_custom_call", output_to_operand_aliasing={{}: (5, {})} | custom-call | flops 1 | bytes 1 | tf_op jit(solution)/shard_map/output/pallas_call | solution.py:688
  (57 shorter events, 2.8 us)
Async XLA Ops:
  0.0 12.7 %copy-start.4 = (bf16[1024,256]{1,0:T(8,128)(2,1)S(1)}, bf16[1024,256]{1,0:T(8,128)(2,1)}, u32[]{:S(2)}) copy-start(bf16[1024,256]{1,0:T(8,128)(2,1)} %wk_in.1) | copy-start | bytes 1572868
  0.0 12.7 %copy-start.2 = (bf16[1024,256]{1,0:T(8,128)(2,1)S(1)}, bf16[1024,256]{1,0:T(8,128)(2,1)}, u32[]{:S(2)}) copy-start(bf16[1024,256]{1,0:T(8,128)(2,1)} %wq_ref.1) | copy-start | bytes 1572868
  3.1 26.1 %copy-start.1 = (bf16[128,1024]{1,0:T(8,128)(2,1)S(1)}, bf16[128,1024]{1,0:T(8,128)(2,1)}, u32[]{:S(2)}) copy-start(bf16[128,1024]{1,0:T(8,128)(2,1)} %get-tuple-element.72.refs_10_.refs_14_) | copy-start | bytes 786436
  3.1 12.1 %collective-permute-start = (bf16[144,512]{1,0:T(8,128)(2,1)}, bf16[144,512]{1,0:T(8,128)(2,1)S(1)}, u32[]{:S(2)}, u32[]{:S(2)}) collective-permute-start(bf16[144,512]{1,0:T(8,128)(2,1)} %get-tuple-element.58), channel_id=1, source_target_pairs={{0,28},{1,25},{2,30},{3,27},{4,24},{5,29},{6,26},{7,31},{8,20},{9,... | collective-permute-start | bytes 442376 | tf_op jit(solution)/shard_map/ppermute | solution.py:135
  9.2 10.9 %collective-permute-start.2 = (bf16[144,512]{1,0:T(8,128)(2,1)}, bf16[144,512]{1,0:T(8,128)(2,1)S(1)}, u32[]{:S(2)}, u32[]{:S(2)}) collective-permute-start(bf16[144,512]{1,0:T(8,128)(2,1)} %get-tuple-element.68), channel_id=1, source_target_pairs={{0,12},{1,13},{2,14},{3,15},{4,8},{5,9},{6,10},{7,11},{8,4},{9,5},... | collective-permute-start | bytes 442376 | tf_op jit(solution)/shard_map/ppermute | solution.py:135
  9.2 13.3 %collective-permute-start.3 = (bf16[144,512]{1,0:T(8,128)(2,1)}, bf16[144,512]{1,0:T(8,128)(2,1)S(1)}, u32[]{:S(2)}, u32[]{:S(2)}) collective-permute-start(bf16[144,512]{1,0:T(8,128)(2,1)} %get-tuple-element.69), channel_id=1, source_target_pairs={{0,8},{1,9},{2,10},{3,11},{4,12},{5,13},{6,14},{7,15},{8,0},{9,1},... | collective-permute-start | bytes 442376 | tf_op jit(solution)/shard_map/ppermute | solution.py:135
  11.1 11.3 %collective-permute-start.4 = (bf16[144,512]{1,0:T(8,128)(2,1)}, bf16[144,512]{1,0:T(8,128)(2,1)S(1)}, u32[]{:S(2)}, u32[]{:S(2)}) collective-permute-start(bf16[144,512]{1,0:T(8,128)(2,1)} %get-tuple-element.70), channel_id=1, source_target_pairs={{0,4},{1,5},{2,6},{3,7},{4,0},{5,1},{6,2},{7,3},{8,12},{9,13},{10,... | collective-permute-start | bytes 442376 | tf_op jit(solution)/shard_map/ppermute | solution.py:135
  12.7 11.9 %collective-permute-start.1 = (bf16[144,512]{1,0:T(8,128)(2,1)}, bf16[144,512]{1,0:T(8,128)(2,1)S(1)}, u32[]{:S(2)}, u32[]{:S(2)}) collective-permute-start(bf16[144,512]{1,0:T(8,128)(2,1)} %get-tuple-element.67), channel_id=1, source_target_pairs={{0,20},{1,17},{2,22},{3,19},{4,16},{5,21},{6,18},{7,23},{8,28},{9,... | collective-permute-start | bytes 442376 | tf_op jit(solution)/shard_map/ppermute | solution.py:135
  22.5 5.0 %collective-permute-start.5 = (bf16[128,512]{1,0:T(8,128)(2,1)S(1)}, bf16[128,512]{1,0:T(8,128)(2,1)S(1)}, u32[]{:S(2)}, u32[]{:S(2)}) collective-permute-start(bf16[128,512]{1,0:T(8,128)(2,1)S(1)} %stack.3), channel_id=1, source_target_pairs={{0,2},{2,0},{1,3},{3,1},{4,6},{6,4},{5,7},{7,5},{8,10},{10,8},{9,1... | collective-permute-start | bytes 393224 | tf_op jit(solution)/shard_map/ppermute | solution.py:56
  24.1 3.6 %collective-permute-start.8 = (bf16[144,512]{1,0:T(8,128)(2,1)S(1)}, bf16[144,512]{1,0:T(8,128)(2,1)S(1)}, u32[]{:S(2)}, u32[]{:S(2)}) collective-permute-start(bf16[144,512]{1,0:T(8,128)(2,1)S(1)} %collective-permute-done.2.refs_1_.refs_4_.refs_8_.refs_2_), channel_id=1, source_target_pairs={{0,1},{1,0},{2,3},{3,2},{4,5},{5,4},{6,7},{7,6},{8,9},{9,8},{10,11... | collective-permute-start | bytes 442376 | tf_op jit(solution)/shard_map/ppermute | solution.py:56
  24.1 5.1 %collective-permute-start.9 = (bf16[144,512]{1,0:T(8,128)(2,1)S(1)}, bf16[144,512]{1,0:T(8,128)(2,1)S(1)}, u32[]{:S(2)}, u32[]{:S(2)}) collective-permute-start(bf16[144,512]{1,0:T(8,128)(2,1)S(1)} %collective-permute-done.3.refs_2_.refs_5_.refs_9_), channel_id=1, source_target_pairs={{0,1},{1,0},{2,3},{3,2},{4,5},{5,4},{6,7},{7,6},{8,9},{9,8},{10,11... | collective-permute-start | bytes 442376 | tf_op jit(solution)/shard_map/ppermute | solution.py:56
  24.6 4.6 %collective-permute-start.10 = (bf16[144,512]{1,0:T(8,128)(2,1)S(1)}, bf16[144,512]{1,0:T(8,128)(2,1)S(1)}, u32[]{:S(2)}, u32[]{:S(2)}) collective-permute-start(bf16[144,512]{1,0:T(8,128)(2,1)S(1)} %collective-permute-done.4.refs_3_.refs_6_.refs_10_), channel_id=1, source_target_pairs={{0,1},{1,0},{2,3},{3,2},{4,5},{5,4},{6,7},{7,6},{8,9},{9,8},{10,11... | collective-permute-start | bytes 442376 | tf_op jit(solution)/shard_map/ppermute | solution.py:56
  24.6 4.6 %collective-permute-start.6 = (bf16[144,512]{1,0:T(8,128)(2,1)S(1)}, bf16[144,512]{1,0:T(8,128)(2,1)S(1)}, u32[]{:S(2)}, u32[]{:S(2)}) collective-permute-start(bf16[144,512]{1,0:T(8,128)(2,1)S(1)} %collective-permute-done.refs_0_), channel_id=1, source_target_pairs={{0,1},{1,0},{2,3},{3,2},{4,5},{5,4},{6,7},{7,6},{8,9},{9,8},{10,11... | collective-permute-start | bytes 442376 | tf_op jit(solution)/shard_map/ppermute | solution.py:56
  27.5 1.7 %collective-permute-start.7 = (bf16[128,512]{1,0:T(8,128)(2,1)S(1)}, bf16[128,512]{1,0:T(8,128)(2,1)S(1)}, u32[]{:S(2)}, u32[]{:S(2)}) collective-permute-start(bf16[128,512]{1,0:T(8,128)(2,1)S(1)} %stack.4.refs_1_), channel_id=1, source_target_pairs={{0,1},{1,0},{2,3},{3,2},{4,5},{5,4},{6,7},{7,6},{8,9},{9,8},{10,11... | collective-permute-start | bytes 393224 | tf_op jit(solution)/shard_map/ppermute | solution.py:56
  27.6 5.9 %collective-permute-start.12 = (bf16[128,512]{1,0:T(8,128)(2,1)S(1)}, bf16[128,512]{1,0:T(8,128)(2,1)S(1)}, u32[]{:S(2)}, u32[]{:S(2)}) collective-permute-start(bf16[128,512]{1,0:T(8,128)(2,1)S(1)} %stack.4.refs_1_), channel_id=1, source_target_pairs={{0,2},{2,0},{1,3},{3,1},{4,6},{6,4},{5,7},{7,5},{8,10},{10,8},{9,1... | collective-permute-start | bytes 393224 | tf_op jit(solution)/shard_map/ppermute | solution.py:56
  29.7 14.1 %collective-permute-start.11 = (bf16[512,256]{1,0:T(8,128)(2,1)S(1)}, bf16[512,256]{1,0:T(8,128)(2,1)S(1)}, u32[]{:S(2)}, u32[]{:S(2)}) collective-permute-start(bf16[512,256]{1,0:T(8,128)(2,1)S(1)} %pack.1), channel_id=1, source_target_pairs={{0,4},{4,8},{8,12},{12,16},{16,20},{20,24},{24,28},{1,5},{5,9},{9,... | collective-permute-start | bytes 786440 | tf_op jit(solution)/shard_map/ppermute | solution.py:60
  32.7 1.4 %collective-permute-start.13 = (bf16[128,512]{1,0:T(8,128)(2,1)S(1)}, bf16[128,512]{1,0:T(8,128)(2,1)S(1)}, u32[]{:S(2)}, u32[]{:S(2)}) collective-permute-start(bf16[128,512]{1,0:T(8,128)(2,1)S(1)} %collective-permute-done.5.refs_2_), channel_id=1, source_target_pairs={{0,1},{1,0},{2,3},{3,2},{4,5},{5,4},{6,7},{7,6},{8,9},{9,8},{10,11... | collective-permute-start | bytes 393224 | tf_op jit(solution)/shard_map/ppermute | solution.py:56
  33.5 1.3 %collective-permute-start.14 = (bf16[128,512]{1,0:T(8,128)(2,1)S(1)}, bf16[128,512]{1,0:T(8,128)(2,1)S(1)}, u32[]{:S(2)}, u32[]{:S(2)}) collective-permute-start(bf16[128,512]{1,0:T(8,128)(2,1)S(1)} %collective-permute-done.12.refs_3_), channel_id=1, source_target_pairs={{0,1},{1,0},{2,3},{3,2},{4,5},{5,4},{6,7},{7,6},{8,9},{9,8},{10,11... | collective-permute-start | bytes 393224 | tf_op jit(solution)/shard_map/ppermute | solution.py:56
  36.7 7.1 %collective-permute-start.17 = (bf16[48,256]{1,0:T(8,128)(2,1)S(1)}, bf16[48,256]{1,0:T(8,128)(2,1)S(1)}, u32[]{:S(2)}, u32[]{:S(2)}) collective-permute-start(bf16[48,256]{1,0:T(8,128)(2,1)S(1)} %get-tuple-element.80.refs_0_), channel_id=1, source_target_pairs={{0,24},{4,28},{8,16},{12,20},{16,8},{20,12},{24,0},{28,4},{1,25},{... | collective-permute-start | bytes 73736 | tf_op jit(solution)/shard_map/ppermute | solution.py:125
  38.8 5.0 %collective-permute-start.16 = (bf16[48,256]{1,0:T(8,128)(2,1)S(1)}, bf16[48,256]{1,0:T(8,128)(2,1)S(1)}, u32[]{:S(2)}, u32[]{:S(2)}) collective-permute-start(bf16[48,256]{1,0:T(8,128)(2,1)S(1)} %get-tuple-element.80.refs_0_), channel_id=1, source_target_pairs={{0,16},{4,20},{8,24},{12,28},{16,0},{20,4},{24,8},{28,12},{1,17},{... | collective-permute-start | bytes 73736 | tf_op jit(solution)/shard_map/ppermute | solution.py:125
  38.8 5.0 %collective-permute-start.15 = (bf16[48,256]{1,0:T(8,128)(2,1)S(1)}, bf16[48,256]{1,0:T(8,128)(2,1)S(1)}, u32[]{:S(2)}, u32[]{:S(2)}) collective-permute-start(bf16[48,256]{1,0:T(8,128)(2,1)S(1)} %get-tuple-element.80.refs_0_), channel_id=1, source_target_pairs={{0,8},{4,12},{8,0},{12,4},{16,24},{20,28},{24,16},{28,20},{1,9},{5... | collective-permute-start | bytes 73736 | tf_op jit(solution)/shard_map/ppermute | solution.py:125
  43.8 7.6 %collective-permute-start.18 = (bf16[512,256]{1,0:T(8,128)(2,1)S(1)}, bf16[512,256]{1,0:T(8,128)(2,1)S(1)}, u32[]{:S(2)}, u32[]{:S(2)}) collective-permute-start(bf16[512,256]{1,0:T(8,128)(2,1)S(1)} %collective-permute-done.11.refs_0_), channel_id=1, source_target_pairs={{0,2},{2,0},{1,3},{3,1},{4,6},{6,4},{5,7},{7,5},{8,10},{10,8},{9,1... | collective-permute-start | bytes 786440 | tf_op jit(solution)/shard_map/ppermute | solution.py:56
  45.4 4.9 %collective-permute-start.19 = (bf16[192,256]{1,0:T(8,128)(2,1)S(1)}, bf16[192,256]{1,0:T(8,128)(2,1)S(1)}, u32[]{:S(2)}, u32[]{:S(2)}) collective-permute-start(bf16[192,256]{1,0:T(8,128)(2,1)S(1)} %stack.5.refs_4_), channel_id=1, source_target_pairs={{0,4},{4,0},{8,12},{12,8},{16,20},{20,16},{24,28},{28,24},{1,5},{5... | collective-permute-start | bytes 294920 | tf_op jit(solution)/shard_map/ppermute | solution.py:125
  46.3 6.3 %collective-permute-start.20 = (bf16[512,256]{1,0:T(8,128)(2,1)S(1)}, bf16[512,256]{1,0:T(8,128)(2,1)S(1)}, u32[]{:S(2)}, u32[]{:S(2)}) collective-permute-start(bf16[512,256]{1,0:T(8,128)(2,1)S(1)} %collective-permute-done.11.refs_0_), channel_id=1, source_target_pairs={{0,1},{1,0},{2,3},{3,2},{4,5},{5,4},{6,7},{7,6},{8,9},{9,8},{10,11... | collective-permute-start | bytes 786440 | tf_op jit(solution)/shard_map/ppermute | solution.py:56
  51.4 1.5 %collective-permute-start.21 = (bf16[512,256]{1,0:T(8,128)(2,1)S(1)}, bf16[512,256]{1,0:T(8,128)(2,1)S(1)}, u32[]{:S(2)}, u32[]{:S(2)}) collective-permute-start(bf16[512,256]{1,0:T(8,128)(2,1)S(1)} %collective-permute-done.18.refs_1_), channel_id=1, source_target_pairs={{0,1},{1,0},{2,3},{3,2},{4,5},{5,4},{6,7},{7,6},{8,9},{9,8},{10,11... | collective-permute-start | bytes 786440 | tf_op jit(solution)/shard_map/ppermute | solution.py:56
  58.5 14.2 %copy-start = (bf16[1024,256]{1,0:T(8,128)(2,1)S(1)}, bf16[1024,256]{1,0:T(8,128)(2,1)}, u32[]{:S(2)}) copy-start(bf16[1024,256]{1,0:T(8,128)(2,1)} %w_ref.3) | copy-start | bytes 1572868
  58.5 9.2 %collective-permute-start.22 = (bf16[512,256]{1,0:T(8,128)(2,1)S(1)}, bf16[512,256]{1,0:T(8,128)(2,1)S(1)}, u32[]{:S(2)}, u32[]{:S(2)}) collective-permute-start(bf16[512,256]{1,0:T(8,128)(2,1)S(1)} %rest.2.refs_0_), channel_id=1, source_target_pairs={{0,2},{2,0},{1,3},{3,1},{4,6},{6,4},{5,7},{7,5},{8,10},{10,8},{9,1... | collective-permute-start | bytes 786440 | tf_op jit(solution)/shard_map/ppermute | solution.py:56
  63.2 9.4 %collective-permute-start.23 = (bf16[512,256]{1,0:T(8,128)(2,1)S(1)}, bf16[512,256]{1,0:T(8,128)(2,1)S(1)}, u32[]{:S(2)}, u32[]{:S(2)}) collective-permute-start(bf16[512,256]{1,0:T(8,128)(2,1)S(1)} %rest.3.refs_0_), channel_id=1, source_target_pairs={{0,2},{2,0},{1,3},{3,1},{4,6},{6,4},{5,7},{7,5},{8,10},{10,8},{9,1... | collective-permute-start | bytes 786440 | tf_op jit(solution)/shard_map/ppermute | solution.py:56
  63.8 8.8 %collective-permute-start.26 = (bf16[512,256]{1,0:T(8,128)(2,1)S(1)}, bf16[512,256]{1,0:T(8,128)(2,1)S(1)}, u32[]{:S(2)}, u32[]{:S(2)}) collective-permute-start(bf16[512,256]{1,0:T(8,128)(2,1)S(1)} %rest.2.refs_0_), channel_id=1, source_target_pairs={{0,1},{1,0},{2,3},{3,2},{4,5},{5,4},{6,7},{7,6},{8,9},{9,8},{10,11... | collective-permute-start | bytes 786440 | tf_op jit(solution)/shard_map/ppermute | solution.py:56
  67.7 4.9 %collective-permute-start.27 = (bf16[512,256]{1,0:T(8,128)(2,1)S(1)}, bf16[512,256]{1,0:T(8,128)(2,1)S(1)}, u32[]{:S(2)}, u32[]{:S(2)}) collective-permute-start(bf16[512,256]{1,0:T(8,128)(2,1)S(1)} %collective-permute-done.22.refs_1_), channel_id=1, source_target_pairs={{0,1},{1,0},{2,3},{3,2},{4,5},{5,4},{6,7},{7,6},{8,9},{9,8},{10,11... | collective-permute-start | bytes 786440 | tf_op jit(solution)/shard_map/ppermute | solution.py:56
  67.7 6.3 %collective-permute-start.24 = (bf16[512,256]{1,0:T(8,128)(2,1)S(1)}, bf16[512,256]{1,0:T(8,128)(2,1)S(1)}, u32[]{:S(2)}, u32[]{:S(2)}) collective-permute-start(bf16[512,256]{1,0:T(8,128)(2,1)S(1)} %rest.3.refs_0_), channel_id=1, source_target_pairs={{0,1},{1,0},{2,3},{3,2},{4,5},{5,4},{6,7},{7,6},{8,9},{9,8},{10,11... | collective-permute-start | bytes 786440 | tf_op jit(solution)/shard_map/ppermute | solution.py:56
  72.6 1.5 %collective-permute-start.25 = (bf16[512,256]{1,0:T(8,128)(2,1)S(1)}, bf16[512,256]{1,0:T(8,128)(2,1)S(1)}, u32[]{:S(2)}, u32[]{:S(2)}) collective-permute-start(bf16[512,256]{1,0:T(8,128)(2,1)S(1)} %collective-permute-done.23.refs_4_.refs_1_), channel_id=1, source_target_pairs={{0,1},{1,0},{2,3},{3,2},{4,5},{5,4},{6,7},{7,6},{8,9},{9,8},{10,11... | collective-permute-start | bytes 786440 | tf_op jit(solution)/shard_map/ppermute | solution.py:56
  (5 other events, 45.4 us)

commit v15 on v12

--- a/solution.py
+++ b/solution.py
@@ -22,7 +22,7 @@
 LONG_BYTES = 20_000_000
 COST = pl.CostEstimate(flops=1, bytes_accessed=1, transcendentals=0)
 LONG = pl.CostEstimate(flops=1, bytes_accessed=LONG_BYTES, transcendentals=0)
-PARTS = (4, 4)
+PARTS = (2, 2, 4)
 
 X_PAIRS = [(0, 2), (2, 0), (1, 3), (3, 1)]
 CORE_PAIRS = [(0, 1), (1, 0), (2, 3), (3, 2)]
@@ -563,7 +563,6 @@
     )(*pieces, w_t, w_k, select, f_col)
     if slabs == 8:
         lined = [summ] + [by_distance(summ, d) for d in (2, 4, 6)]
-        comp, *lined = lax.optimization_barrier((comp, *lined))
     comp_before = to_next(comp)
 
     q_t, v_t, keys, near_k, near_vt = pl.pallas_call(

time: 79.9 us -> 76.6 us (0.959)
  the two profiles are of different devices: /device:TPU:9 before, /device:TPU:0 now
where the time goes in v15:
time: 76.6 us; the launch traced here: 76.5 us
  starting transfers between devices  28.5 us (37%)
  Pallas kernels  26.4 us (34%)
  waiting for transfers between devices  21.3 us (28%)
    ppermute x18, waiting for transfers between devices, over_head(): return lax.ppermute(block, 'head', pairs)  11.4 us
    ppermute x5, starting transfers between devices, by_core(): return lax.ppermute(block, ('seq', 'head'), pairs)  9.51 us
    ppermute x18, starting transfers between devices, over_head(): return lax.ppermute(block, 'head', pairs)  9.32 us
    ppermute x5, waiting for transfers between devices, by_core(): return lax.ppermute(block, ('seq', 'head'), pairs)  7.28 us
    pallas_call x3, Pallas kernels, local(): pl.pallas_call(functools.partial(rest_kernel, first, count), out_shape=sh...  7.09 us
    ppermute x4, starting transfers between devices, by_distance(): lax.ppermute(block, 'seq', [(i, i ^ distance) for i in range(lax.axis_siz...  6.65 us
    pallas_call x1, Pallas kernels, local(): pl.pallas_call(own_kernel, out_shape=(shape((group, tok_rows), F32), shap...  3.94 us
    pallas_call x3, Pallas kernels, finish(): pl.pallas_call(output_kernel, grid=(rows // height,), out_shape=shape((to...  3.23 us
  transfers between devices with their start and end apart: 28, of which 11 were waited for; matrix products, arithmetic and copies ran while one was open for 0% of the time, Pallas kernels for 21%

profile of v15, /device:TPU:0, one launch (start us, length us, event | category | flops | bytes accessed | tf_op | source)
XLA Modules:
  0.0 76.5 jit_solution(15588795877888258748)
XLA Ops:
  0.0 2.7 %send.1 = (bf16[144,512]{1,0:T(8,128)(2,1)}, bf16[144,512]{1,0:T(8,128)(2,1)}, bf16[144,512]{1,0:T(8,128)(2,1)}, bf16[144,512]{1,0:T(8,128)(2,1)}, bf16[144,512]{1,0:T(8,128)(2,1)}, /*index=5*/bf16[128,1024]{1,0:T(8,128)(2,1)}) custom-call(bf16[1024,1024]{1,0:T(8,128)(2,1)} %tokens_ref.1, s32[1,512]{1,0:T(1,128)} %mask_ref.3), custom_call_target="tpu_custom_call" | custom-call | flops 1 | bytes 1 | tf_op jit(solution)/shard_map/send/pallas_call | solution.py:134
  2.7 6.0 %collective-permute-start = (bf16[144,512]{1,0:T(8,128)(2,1)}, bf16[144,512]{1,0:T(8,128)(2,1)S(1)}, u32[]{:S(2)}, u32[]{:S(2)}) collective-permute-start(bf16[144,512]{1,0:T(8,128)(2,1)} %get-tuple-element.54), channel_id=1, source_target_pairs={{0,28},{1,25},{2,30},{3,27},{4,24},{5,29},{6,26},{7,31},{8,20},{9,... | collective-permute-start | bytes 442376 | tf_op jit(solution)/shard_map/ppermute | solution.py:113
  8.8 2.0 %collective-permute-start.3 = (bf16[144,512]{1,0:T(8,128)(2,1)}, bf16[144,512]{1,0:T(8,128)(2,1)S(1)}, u32[]{:S(2)}, u32[]{:S(2)}) collective-permute-start(bf16[144,512]{1,0:T(8,128)(2,1)} %get-tuple-element.60), channel_id=1, source_target_pairs={{0,8},{1,9},{2,10},{3,11},{4,12},{5,13},{6,14},{7,15},{8,0},{9,1},... | collective-permute-start | bytes 442376 | tf_op jit(solution)/shard_map/ppermute | solution.py:113
  10.7 1.5 %collective-permute-start.4 = (bf16[144,512]{1,0:T(8,128)(2,1)}, bf16[144,512]{1,0:T(8,128)(2,1)S(1)}, u32[]{:S(2)}, u32[]{:S(2)}) collective-permute-start(bf16[144,512]{1,0:T(8,128)(2,1)} %get-tuple-element.61), channel_id=1, source_target_pairs={{0,4},{1,5},{2,6},{3,7},{4,0},{5,1},{6,2},{7,3},{8,12},{9,13},{10,... | collective-permute-start | bytes 442376 | tf_op jit(solution)/shard_map/ppermute | solution.py:113
  12.3 2.5 %prepare.1 = (bf16[1024,1024]{1,0:T(8,128)(2,1)S(1)}, bf16[1024,1024]{1,0:T(8,128)(2,1)S(1)}, bf16[672,1024]{1,0:T(8,128)(2,1)S(1)}, f32[160,128]{1,0:T(8,128)S(...) custom-call(s32[1,1024]{1,0:T(1,128)S(1)} %copy-done.8, ...), custom_call_target="tpu_custom_call" | custom-call | flops 1 | bytes 1 | tf_op jit(solution)/shard_map/prepare/pallas_call | solution.py:512
  14.8 4.8 %collective-permute-done.2.refs_1_.refs_2_.refs_8_ = bf16[144,512]{1,0:T(8,128)(2,1)S(1)} collective-permute-done((bf16[144,512]{1,0:T(8,128)(2,1)}, bf16[144,512]{1,0:T(8,128)(2,1)S(1)}, u32[]{:S(2)}, u32[]{:S(2)}) %collective-permute-start.2) | collective-permute-done | bytes 147488 | tf_op jit(solution)/shard_map/ppermute | solution.py:113
  19.6 2.4 %collective-permute-done.3.refs_2_.refs_9_ = bf16[144,512]{1,0:T(8,128)(2,1)S(1)} collective-permute-done((bf16[144,512]{1,0:T(8,128)(2,1)}, bf16[144,512]{1,0:T(8,128)(2,1)S(1)}, u32[]{:S(2)}, u32[]{:S(2)}) %collective-permute-start.3) | collective-permute-done | bytes 147488 | tf_op jit(solution)/shard_map/ppermute | solution.py:113
  22.1 1.6 %collective-permute-start.5 = (bf16[128,512]{1,0:T(8,128)(2,1)S(1)}, bf16[128,512]{1,0:T(8,128)(2,1)S(1)}, u32[]{:S(2)}, u32[]{:S(2)}) collective-permute-start(bf16[128,512]{1,0:T(8,128)(2,1)S(1)} %stack.3), channel_id=1, source_target_pairs={{0,2},{2,0},{1,3},{3,1},{4,6},{6,4},{5,7},{7,5},{8,10},{10,8},{9,1... | collective-permute-start | bytes 393224 | tf_op jit(solution)/shard_map/ppermute | solution.py:56
  24.2 3.0 %collective-permute-done.5.refs_2_ = bf16[128,512]{1,0:T(8,128)(2,1)S(1)} collective-permute-done((bf16[128,512]{1,0:T(8,128)(2,1)S(1)}, bf16[128,512]{1,0:T(8,128)(2,1)S(1)}, u32[]{:S(2)}, u32[]{:S(2)}) %collective-permute-start.5) | collective-permute-done | bytes 131104 | tf_op jit(solution)/shard_map/ppermute | solution.py:56
  27.1 1.6 %collective-permute-start.6 = (bf16[128,512]{1,0:T(8,128)(2,1)S(1)}, bf16[128,512]{1,0:T(8,128)(2,1)S(1)}, u32[]{:S(2)}, u32[]{:S(2)}) collective-permute-start(bf16[128,512]{1,0:T(8,128)(2,1)S(1)} %stack.4.refs_1_), channel_id=1, source_target_pairs={{0,2},{2,0},{1,3},{3,1},{4,6},{6,4},{5,7},{7,5},{8,10},{10,8},{9,1... | collective-permute-start | bytes 393224 | tf_op jit(solution)/shard_map/ppermute | solution.py:56
  29.2 1.2 %expand.1 = (bf16[1024,512]{1,0:T(8,128)(2,1)S(1)}, bf16[512,1024]{1,0:T(8,128)(2,1)S(1)}, f32[2048,128]{1,0:T(8,128)S(1)}) custom-call(f32[1024,128]{1,0:T(8,128)S(1)} %get-tuple-element.55.seen_ref, bf16[144,512]{1,0:T(8,128)(2,1)S(1)} %collective-permute-done.refs_0_, bf16[144,512]{1,0:T(8,128)(2,1)S(1)} %collective-permute-done.7.refs_1_.refs_4_, ...), custom_call_target="tpu_custom_call" | custom-call | flops 1 | bytes 1 | tf_op jit(solution)/shard_map/expand/pallas_call | solution.py:532
  30.4 1.7 %collective-permute-done.6.refs_3_ = bf16[128,512]{1,0:T(8,128)(2,1)S(1)} collective-permute-done((bf16[128,512]{1,0:T(8,128)(2,1)S(1)}, bf16[128,512]{1,0:T(8,128)(2,1)S(1)}, u32[]{:S(2)}, u32[]{:S(2)}) %collective-permute-start.6) | collective-permute-done | bytes 131104 | tf_op jit(solution)/shard_map/ppermute | solution.py:56
  33.7 2.1 %project.1 = (bf16[1024,256]{1,0:T(8,128)(2,1)S(1)}, bf16[48,256]{1,0:T(8,128)(2,1)S(1)}, bf16[1024,256]{1,0:T(8,128)(2,1)S(1)}, bf16[256,1024]{1,0:T(8,128)(2,1)S(1)}, bf16[1024,1024]{1,0:T(8,128)(2,1)S(1)}) custom-call(bf16[144,512]{1,0:T(8,128)(2,1)S(1)} %collective-permute-done.refs_0_, bf16[128,512]{1,0:T(8,128)(2,1)S(1)} %stack.4.refs_1_, ...), custom_call_target="tpu_custom_call" | custom-call | flops 1 | bytes 1 | tf_op jit(solution)/shard_map/project/pallas_call | solution.py:549
  35.8 3.0 %collective-permute-start.14 = (bf16[1024,256]{1,0:T(8,128)(2,1)S(1)}, bf16[1024,256]{1,0:T(8,128)(2,1)S(1)}, u32[]{:S(2)}, u32[]{:S(2)}) collective-permute-start(bf16[1024,256]{1,0:T(8,128)(2,1)S(1)} %get-tuple-element.75), channel_id=1, source_target_pairs={{0,4},{4,8},{8,12},{12,16},{16,20},{20,24},{24,28},{1,5},{5,9},{9,... | collective-permute-start | bytes 1572872 | tf_op jit(solution)/shard_map/ppermute | solution.py:60
  38.9 1.9 %collective-permute-start.17 = (bf16[48,256]{1,0:T(8,128)(2,1)S(1)}, bf16[48,256]{1,0:T(8,128)(2,1)S(1)}, u32[]{:S(2)}, u32[]{:S(2)}) collective-permute-start(bf16[48,256]{1,0:T(8,128)(2,1)S(1)} %get-tuple-element.76.refs_0_), channel_id=1, source_target_pairs={{0,24},{4,28},{8,16},{12,20},{16,8},{20,12},{24,0},{28,4},{1,25},{... | collective-permute-start | bytes 73736 | tf_op jit(solution)/shard_map/ppermute | solution.py:103
  40.8 2.5 %collective-permute-start.15 = (bf16[48,256]{1,0:T(8,128)(2,1)S(1)}, bf16[48,256]{1,0:T(8,128)(2,1)S(1)}, u32[]{:S(2)}, u32[]{:S(2)}) collective-permute-start(bf16[48,256]{1,0:T(8,128)(2,1)S(1)} %get-tuple-element.76.refs_0_), channel_id=1, source_target_pairs={{0,8},{4,12},{8,0},{12,4},{16,24},{20,28},{24,16},{28,20},{1,9},{5... | collective-permute-start | bytes 73736 | tf_op jit(solution)/shard_map/ppermute | solution.py:103
  43.3 2.7 %order.1 = (bf16[256,1024]{1,0:T(8,128)(2,1)S(1)}, bf16[256,1024]{1,0:T(8,128)(2,1)S(1)}, bf16[1024,256]{1,0:T(8,128)(2,1)S(1)}, bf16[128,256]{1,0:T(8,128)(2,1)S(1)}, bf16[256,128]{1,0:T(8,128)(2,1)S(1)}) custom-call(bf16[1024,1024]{1,0:T(8,128)(2,1)S(1)} %get-tuple-element.48.p_ref, bf16[1024,1024]{1,0:T(8,128)(2,1)S(1)} %get-tuple-element.49.pt_ref, ...), custom_call_target="tpu_custom_call" | custom-call | flops 1 | bytes 1 | tf_op jit(solution)/shard_map/order/pallas_call | solution.py:568
  46.0 3.9 %own.1 = (f32[256,1024]{1,0:T(8,128)S(1)}, f32[256,1024]{1,0:T(8,128)S(1)}, f32[8,512]{1,0:T(8,128)S(1)}, f32[8,512]{1,0:T(8,128)S(1)}) custom-call(f32[4,4]{1,0:T(4,128)S(1)} %copy-done.5, bf16[256,1024]{1,0:T(8,128)(2,1)S(1)} %get-tuple-element.72.qt_ref, bf16[1024,256]{1,0:T(8,128)(2,1)S(1)} %get-tuple-element.73.k_ref, ...), custom_call_target="tpu_custom_call" | custom-call | flops 1 | bytes 1 | tf_op jit(solution)/shard_map/own/pallas_call | solution.py:584
  50.0 2.2 %collective-permute-start.18 = (bf16[192,256]{1,0:T(8,128)(2,1)S(1)}, bf16[192,256]{1,0:T(8,128)(2,1)S(1)}, u32[]{:S(2)}, u32[]{:S(2)}) collective-permute-start(bf16[192,256]{1,0:T(8,128)(2,1)S(1)} %stack.5.refs_0_), channel_id=1, source_target_pairs={{0,4},{4,0},{8,12},{12,8},{16,20},{20,16},{24,28},{28,24},{1,5},{5... | collective-permute-start | bytes 294920 | tf_op jit(solution)/shard_map/ppermute | solution.py:103
  52.2 2.6 %collective-permute-done.18.refs_1_ = bf16[192,256]{1,0:T(8,128)(2,1)S(1)} collective-permute-done((bf16[192,256]{1,0:T(8,128)(2,1)S(1)}, bf16[192,256]{1,0:T(8,128)(2,1)S(1)}, u32[]{:S(2)}, u32[]{:S(2)}) %collective-permute-start.18) | collective-permute-done | bytes 98336 | tf_op jit(solution)/shard_map/ppermute | solution.py:103
  54.8 0.9 %window.1 = (bf16[2048,256]{1,0:T(8,128)(2,1)S(1)}, bf16[256,2048]{1,0:T(8,128)(2,1)S(1)}, bf16[64,256]{1,0:T(8,128)(2,1)S(1)}, bf16[256,64]{1,0:T(8,128)(2,1)S(1)}) custom-call(bf16[1024,256]{1,0:T(8,128)(2,1)S(1)} %get-tuple-element.73.k_ref, bf16[256,1024]{1,0:T(8,128)(2,1)S(1)} %get-tuple-element.74.vt_ref, ...), custom_call_target="tpu_custom_call" | custom-call | flops 1 | bytes 1 | tf_op jit(solution)/shard_map/window/pallas_call | solution.py:612
  55.7 3.2 %rest.4.refs_0_ = bf16[512,256]{1,0:T(8,128)(2,1)S(1)} custom-call(s32[4,8]{1,0:T(4,128)S(1)} %bitcast.1, f32[4,4]{1,0:T(4,128)S(1)} %copy-done.5, bf16[256,1024]{1,0:T(8,128)(2,1)S(1)} %get-tuple-element.72.qt_ref, bf16[2048,256]{1,0:T(8,128)(2,1)S(1)} %get-tuple-element.80.kw_ref, bf16[256,2048]{1,0:T(8,128)(2,1)S(1)} %get-tuple-element.81.vw_ref, ...), custom_call_target="tpu_custom_call" | custom-call | flops 1 | bytes 1 | tf_op jit(solution)/shard_map/rest/pallas_call | solution.py:654
  58.9 1.5 %collective-permute-start.20 = (bf16[512,256]{1,0:T(8,128)(2,1)S(1)}, bf16[512,256]{1,0:T(8,128)(2,1)S(1)}, u32[]{:S(2)}, u32[]{:S(2)}) collective-permute-start(bf16[512,256]{1,0:T(8,128)(2,1)S(1)} %rest.4.refs_0_), channel_id=1, source_target_pairs={{0,2},{2,0},{1,3},{3,1},{4,6},{6,4},{5,7},{7,5},{8,10},{10,8},{9,1... | collective-permute-start | bytes 786440 | tf_op jit(solution)/shard_map/ppermute | solution.py:56
  60.4 2.0 %rest.5.refs_0_ = bf16[256,256]{1,0:T(8,128)(2,1)S(1)} custom-call(s32[4,8]{1,0:T(4,128)S(1)} %bitcast.2, f32[4,4]{1,0:T(4,128)S(1)} %copy-done.5, bf16[256,1024]{1,0:T(8,128)(2,1)S(1)} %get-tuple-element.72.qt_ref, bf16[2048,256]{1,0:T(8,128)(2,1)S(1)} %get-tuple-element.80.kw_ref, bf16[256,2048]{1,0:T(8,128)(2,1)S(1)} %get-tuple-element.81.vw_ref, ...), custom_call_target="tpu_custom_call" | custom-call | flops 1 | bytes 1 | tf_op jit(solution)/shard_map/rest/pallas_call | solution.py:654
  63.1 2.0 %rest.3.refs_0_ = bf16[256,256]{1,0:T(8,128)(2,1)S(1)} custom-call(s32[4,8]{1,0:T(4,128)S(1)} %bitcast.3, f32[4,4]{1,0:T(4,128)S(1)} %copy-done.5, bf16[256,1024]{1,0:T(8,128)(2,1)S(1)} %get-tuple-element.72.qt_ref, bf16[2048,256]{1,0:T(8,128)(2,1)S(1)} %get-tuple-element.80.kw_ref, bf16[256,2048]{1,0:T(8,128)(2,1)S(1)} %get-tuple-element.81.vw_ref, ...), custom_call_target="tpu_custom_call" | custom-call | flops 1 | bytes 1 | tf_op jit(solution)/shard_map/rest/pallas_call | solution.py:654
  65.0 1.5 %collective-permute-start.19 = (bf16[256,256]{1,0:T(8,128)(2,1)S(1)}, bf16[256,256]{1,0:T(8,128)(2,1)S(1)}, u32[]{:S(2)}, u32[]{:S(2)}) collective-permute-start(bf16[256,256]{1,0:T(8,128)(2,1)S(1)} %rest.3.refs_0_), channel_id=1, source_target_pairs={{0,2},{2,0},{1,3},{3,1},{4,6},{6,4},{5,7},{7,5},{8,10},{10,8},{9,1... | collective-permute-start | bytes 393224 | tf_op jit(solution)/shard_map/ppermute | solution.py:56
  67.0 1.2 %collective-permute-done.20.refs_5_.refs_1_ = bf16[512,256]{1,0:T(8,128)(2,1)S(1)} collective-permute-done((bf16[512,256]{1,0:T(8,128)(2,1)S(1)}, bf16[512,256]{1,0:T(8,128)(2,1)S(1)}, u32[]{:S(2)}, u32[]{:S(2)}) %collective-permute-start.20) | collective-permute-done | bytes 262176 | tf_op jit(solution)/shard_map/ppermute | solution.py:56
  68.2 2.3 %collective-permute-done.23.refs_1_ = bf16[256,256]{1,0:T(8,128)(2,1)S(1)} collective-permute-done((bf16[256,256]{1,0:T(8,128)(2,1)S(1)}, bf16[256,256]{1,0:T(8,128)(2,1)S(1)}, u32[]{:S(2)}, u32[]{:S(2)}) %collective-permute-start.23) | collective-permute-done | bytes 131104 | tf_op jit(solution)/shard_map/ppermute | solution.py:56
  70.5 1.4 %collective-permute-done.19.refs_4_.refs_1_ = bf16[256,256]{1,0:T(8,128)(2,1)S(1)} collective-permute-done((bf16[256,256]{1,0:T(8,128)(2,1)S(1)}, bf16[256,256]{1,0:T(8,128)(2,1)S(1)}, u32[]{:S(2)}, u32[]{:S(2)}) %collective-permute-start.19) | collective-permute-done | bytes 131104 | tf_op jit(solution)/shard_map/ppermute | solution.py:56
  73.2 1.0 %output.3.refs_4_ = bf16[1024,256]{1,0:T(8,128)(2,1)} custom-call(bf16[1024,256]{1,0:T(8,128)(2,1)S(1)} %copy-done, bf16[256,256]{1,0:T(8,128)(2,1)S(1)} %rest.5.refs_0_, bf16[256,256]{1,0:T(8,128)(2,1)S(1)} %collective-permute-done.23.refs_1_, bf16[256,256]{1,0:T(8,128)(2,1)S(1)} %collective-permute-done.26.refs_2_, ...), custom_call_target="tpu_custom_call" | custom-call | flops 1 | bytes 1 | tf_op jit(solution)/shard_map/output/pallas_call | solution.py:639
  74.2 1.0 %output.4.refs_4_ = bf16[1024,256]{1,0:T(8,128)(2,1)} custom-call(bf16[1024,256]{1,0:T(8,128)(2,1)S(1)} %copy-done, bf16[256,256]{1,0:T(8,128)(2,1)S(1)} %rest.3.refs_0_, bf16[256,256]{1,0:T(8,128)(2,1)S(1)} %collective-permute-done.19.refs_4_.refs_1_, bf16[256,256]{1,0:T(8,128)(2,1)S(1)} %collective-permute-done.24.refs_2_, ...), custom_call_target="tpu_custom_call", output_to_operand_aliasing={{}: (5, {})} | custom-call | flops 1 | bytes 1 | tf_op jit(solution)/shard_map/output/pallas_call | solution.py:639
  75.2 1.3 %output.5 = bf16[1024,256]{1,0:T(8,128)(2,1)} custom-call(bf16[1024,256]{1,0:T(8,128)(2,1)S(1)} %copy-done, bf16[512,256]{1,0:T(8,128)(2,1)S(1)} %rest.4.refs_0_, bf16[512,256]{1,0:T(8,128)(2,1)S(1)} %collective-permute-done.20.refs_5_.refs_1_, bf16[512,256]{1,0:T(8,128)(2,1)S(1)} %collective-permute-done.21.refs_2_, ...), custom_call_target="tpu_custom_call", output_to_operand_aliasing={{}: (5, {})} | custom-call | flops 1 | bytes 1 | tf_op jit(solution)/shard_map/output/pallas_call | solution.py:639
  (58 shorter events, 5.2 us)
Async XLA Ops:
  0.0 12.3 %copy-start.2 = (bf16[1024,256]{1,0:T(8,128)(2,1)S(1)}, bf16[1024,256]{1,0:T(8,128)(2,1)}, u32[]{:S(2)}) copy-start(bf16[1024,256]{1,0:T(8,128)(2,1)} %wv_ref.1) | copy-start | bytes 1572868
  0.0 12.3 %copy-start.3 = (bf16[1024,256]{1,0:T(8,128)(2,1)S(1)}, bf16[1024,256]{1,0:T(8,128)(2,1)}, u32[]{:S(2)}) copy-start(bf16[1024,256]{1,0:T(8,128)(2,1)} %wk_in.1) | copy-start | bytes 1572868
  0.0 12.3 %copy-start.1 = (bf16[1024,256]{1,0:T(8,128)(2,1)S(1)}, bf16[1024,256]{1,0:T(8,128)(2,1)}, u32[]{:S(2)}) copy-start(bf16[1024,256]{1,0:T(8,128)(2,1)} %wq_ref.1) | copy-start | bytes 1572868
  2.7 31.0 %copy-start.4 = (bf16[128,1024]{1,0:T(8,128)(2,1)S(1)}, bf16[128,1024]{1,0:T(8,128)(2,1)}, u32[]{:S(2)}) copy-start(bf16[128,1024]{1,0:T(8,128)(2,1)} %get-tuple-element.68.refs_14_) | copy-start | bytes 786436
  2.7 12.0 %collective-permute-start = (bf16[144,512]{1,0:T(8,128)(2,1)}, bf16[144,512]{1,0:T(8,128)(2,1)S(1)}, u32[]{:S(2)}, u32[]{:S(2)}) collective-permute-start(bf16[144,512]{1,0:T(8,128)(2,1)} %get-tuple-element.54), channel_id=1, source_target_pairs={{0,28},{1,25},{2,30},{3,27},{4,24},{5,29},{6,26},{7,31},{8,20},{9,... | collective-permute-start | bytes 442376 | tf_op jit(solution)/shard_map/ppermute | solution.py:113
  8.8 10.9 %collective-permute-start.2 = (bf16[144,512]{1,0:T(8,128)(2,1)}, bf16[144,512]{1,0:T(8,128)(2,1)S(1)}, u32[]{:S(2)}, u32[]{:S(2)}) collective-permute-start(bf16[144,512]{1,0:T(8,128)(2,1)} %get-tuple-element.59), channel_id=1, source_target_pairs={{0,12},{1,13},{2,14},{3,15},{4,8},{5,9},{6,10},{7,11},{8,4},{9,5},... | collective-permute-start | bytes 442376 | tf_op jit(solution)/shard_map/ppermute | solution.py:113
  8.8 13.3 %collective-permute-start.3 = (bf16[144,512]{1,0:T(8,128)(2,1)}, bf16[144,512]{1,0:T(8,128)(2,1)S(1)}, u32[]{:S(2)}, u32[]{:S(2)}) collective-permute-start(bf16[144,512]{1,0:T(8,128)(2,1)} %get-tuple-element.60), channel_id=1, source_target_pairs={{0,8},{1,9},{2,10},{3,11},{4,12},{5,13},{6,14},{7,15},{8,0},{9,1},... | collective-permute-start | bytes 442376 | tf_op jit(solution)/shard_map/ppermute | solution.py:113
  10.7 11.3 %collective-permute-start.4 = (bf16[144,512]{1,0:T(8,128)(2,1)}, bf16[144,512]{1,0:T(8,128)(2,1)S(1)}, u32[]{:S(2)}, u32[]{:S(2)}) collective-permute-start(bf16[144,512]{1,0:T(8,128)(2,1)} %get-tuple-element.61), channel_id=1, source_target_pairs={{0,4},{1,5},{2,6},{3,7},{4,0},{5,1},{6,2},{7,3},{8,12},{9,13},{10,... | collective-permute-start | bytes 442376 | tf_op jit(solution)/shard_map/ppermute | solution.py:113
  12.3 11.9 %collective-permute-start.1 = (bf16[144,512]{1,0:T(8,128)(2,1)}, bf16[144,512]{1,0:T(8,128)(2,1)S(1)}, u32[]{:S(2)}, u32[]{:S(2)}) collective-permute-start(bf16[144,512]{1,0:T(8,128)(2,1)} %get-tuple-element.58), channel_id=1, source_target_pairs={{0,20},{1,17},{2,22},{3,19},{4,16},{5,21},{6,18},{7,23},{8,28},{9,... | collective-permute-start | bytes 442376 | tf_op jit(solution)/shard_map/ppermute | solution.py:113
  22.1 5.0 %collective-permute-start.5 = (bf16[128,512]{1,0:T(8,128)(2,1)S(1)}, bf16[128,512]{1,0:T(8,128)(2,1)S(1)}, u32[]{:S(2)}, u32[]{:S(2)}) collective-permute-start(bf16[128,512]{1,0:T(8,128)(2,1)S(1)} %stack.3), channel_id=1, source_target_pairs={{0,2},{2,0},{1,3},{3,1},{4,6},{6,4},{5,7},{7,5},{8,10},{10,8},{9,1... | collective-permute-start | bytes 393224 | tf_op jit(solution)/shard_map/ppermute | solution.py:56
  23.6 5.6 %collective-permute-start.7 = (bf16[144,512]{1,0:T(8,128)(2,1)S(1)}, bf16[144,512]{1,0:T(8,128)(2,1)S(1)}, u32[]{:S(2)}, u32[]{:S(2)}) collective-permute-start(bf16[144,512]{1,0:T(8,128)(2,1)S(1)} %collective-permute-done.refs_0_), channel_id=1, source_target_pairs={{0,1},{1,0},{2,3},{3,2},{4,5},{5,4},{6,7},{7,6},{8,9},{9,8},{10,11... | collective-permute-start | bytes 442376 | tf_op jit(solution)/shard_map/ppermute | solution.py:56
  23.6 8.5 %collective-permute-start.11 = (bf16[144,512]{1,0:T(8,128)(2,1)S(1)}, bf16[144,512]{1,0:T(8,128)(2,1)S(1)}, u32[]{:S(2)}, u32[]{:S(2)}) collective-permute-start(bf16[144,512]{1,0:T(8,128)(2,1)S(1)} %collective-permute-done.2.refs_1_.refs_2_.refs_8_), channel_id=1, source_target_pairs={{0,1},{1,0},{2,3},{3,2},{4,5},{5,4},{6,7},{7,6},{8,9},{9,8},{10,11... | collective-permute-start | bytes 442376 | tf_op jit(solution)/shard_map/ppermute | solution.py:56
  27.1 5.0 %collective-permute-start.6 = (bf16[128,512]{1,0:T(8,128)(2,1)S(1)}, bf16[128,512]{1,0:T(8,128)(2,1)S(1)}, u32[]{:S(2)}, u32[]{:S(2)}) collective-permute-start(bf16[128,512]{1,0:T(8,128)(2,1)S(1)} %stack.4.refs_1_), channel_id=1, source_target_pairs={{0,2},{2,0},{1,3},{3,1},{4,6},{6,4},{5,7},{7,5},{8,10},{10,8},{9,1... | collective-permute-start | bytes 393224 | tf_op jit(solution)/shard_map/ppermute | solution.py:56
  28.7 4.0 %collective-permute-start.12 = (bf16[144,512]{1,0:T(8,128)(2,1)S(1)}, bf16[144,512]{1,0:T(8,128)(2,1)S(1)}, u32[]{:S(2)}, u32[]{:S(2)}) collective-permute-start(bf16[144,512]{1,0:T(8,128)(2,1)S(1)} %collective-permute-done.3.refs_2_.refs_9_), channel_id=1, source_target_pairs={{0,1},{1,0},{2,3},{3,2},{4,5},{5,4},{6,7},{7,6},{8,9},{9,8},{10,11... | collective-permute-start | bytes 442376 | tf_op jit(solution)/shard_map/ppermute | solution.py:56
  28.7 4.0 %collective-permute-start.13 = (bf16[144,512]{1,0:T(8,128)(2,1)S(1)}, bf16[144,512]{1,0:T(8,128)(2,1)S(1)}, u32[]{:S(2)}, u32[]{:S(2)}) collective-permute-start(bf16[144,512]{1,0:T(8,128)(2,1)S(1)} %collective-permute-done.4.refs_3_.refs_10_), channel_id=1, source_target_pairs={{0,1},{1,0},{2,3},{3,2},{4,5},{5,4},{6,7},{7,6},{8,9},{9,8},{10,11... | collective-permute-start | bytes 442376 | tf_op jit(solution)/shard_map/ppermute | solution.py:56
  29.2 3.5 %collective-permute-start.8 = (bf16[128,512]{1,0:T(8,128)(2,1)S(1)}, bf16[128,512]{1,0:T(8,128)(2,1)S(1)}, u32[]{:S(2)}, u32[]{:S(2)}) collective-permute-start(bf16[128,512]{1,0:T(8,128)(2,1)S(1)} %stack.4.refs_1_), channel_id=1, source_target_pairs={{0,1},{1,0},{2,3},{3,2},{4,5},{5,4},{6,7},{7,6},{8,9},{9,8},{10,11... | collective-permute-start | bytes 393224 | tf_op jit(solution)/shard_map/ppermute | solution.py:56
  32.2 1.3 %collective-permute-start.9 = (bf16[128,512]{1,0:T(8,128)(2,1)S(1)}, bf16[128,512]{1,0:T(8,128)(2,1)S(1)}, u32[]{:S(2)}, u32[]{:S(2)}) collective-permute-start(bf16[128,512]{1,0:T(8,128)(2,1)S(1)} %collective-permute-done.5.refs_2_), channel_id=1, source_target_pairs={{0,1},{1,0},{2,3},{3,2},{4,5},{5,4},{6,7},{7,6},{8,9},{9,8},{10,11... | collective-permute-start | bytes 393224 | tf_op jit(solution)/shard_map/ppermute | solution.py:56
  32.2 1.5 %collective-permute-start.10 = (bf16[128,512]{1,0:T(8,128)(2,1)S(1)}, bf16[128,512]{1,0:T(8,128)(2,1)S(1)}, u32[]{:S(2)}, u32[]{:S(2)}) collective-permute-start(bf16[128,512]{1,0:T(8,128)(2,1)S(1)} %collective-permute-done.6.refs_3_), channel_id=1, source_target_pairs={{0,1},{1,0},{2,3},{3,2},{4,5},{5,4},{6,7},{7,6},{8,9},{9,8},{10,11... | collective-permute-start | bytes 393224 | tf_op jit(solution)/shard_map/ppermute | solution.py:56
  35.8 19.0 %collective-permute-start.14 = (bf16[1024,256]{1,0:T(8,128)(2,1)S(1)}, bf16[1024,256]{1,0:T(8,128)(2,1)S(1)}, u32[]{:S(2)}, u32[]{:S(2)}) collective-permute-start(bf16[1024,256]{1,0:T(8,128)(2,1)S(1)} %get-tuple-element.75), channel_id=1, source_target_pairs={{0,4},{4,8},{8,12},{12,16},{16,20},{20,24},{24,28},{1,5},{5,9},{9,... | collective-permute-start | bytes 1572872 | tf_op jit(solution)/shard_map/ppermute | solution.py:60
  38.9 11.1 %collective-permute-start.17 = (bf16[48,256]{1,0:T(8,128)(2,1)S(1)}, bf16[48,256]{1,0:T(8,128)(2,1)S(1)}, u32[]{:S(2)}, u32[]{:S(2)}) collective-permute-start(bf16[48,256]{1,0:T(8,128)(2,1)S(1)} %get-tuple-element.76.refs_0_), channel_id=1, source_target_pairs={{0,24},{4,28},{8,16},{12,20},{16,8},{20,12},{24,0},{28,4},{1,25},{... | collective-permute-start | bytes 73736 | tf_op jit(solution)/shard_map/ppermute | solution.py:103
  40.8 9.2 %collective-permute-start.16 = (bf16[48,256]{1,0:T(8,128)(2,1)S(1)}, bf16[48,256]{1,0:T(8,128)(2,1)S(1)}, u32[]{:S(2)}, u32[]{:S(2)}) collective-permute-start(bf16[48,256]{1,0:T(8,128)(2,1)S(1)} %get-tuple-element.76.refs_0_), channel_id=1, source_target_pairs={{0,16},{4,20},{8,24},{12,28},{16,0},{20,4},{24,8},{28,12},{1,17},{... | collective-permute-start | bytes 73736 | tf_op jit(solution)/shard_map/ppermute | solution.py:103
  40.8 9.2 %collective-permute-start.15 = (bf16[48,256]{1,0:T(8,128)(2,1)S(1)}, bf16[48,256]{1,0:T(8,128)(2,1)S(1)}, u32[]{:S(2)}, u32[]{:S(2)}) collective-permute-start(bf16[48,256]{1,0:T(8,128)(2,1)S(1)} %get-tuple-element.76.refs_0_), channel_id=1, source_target_pairs={{0,8},{4,12},{8,0},{12,4},{16,24},{20,28},{24,16},{28,20},{1,9},{5... | collective-permute-start | bytes 73736 | tf_op jit(solution)/shard_map/ppermute | solution.py:103
  50.0 4.8 %collective-permute-start.18 = (bf16[192,256]{1,0:T(8,128)(2,1)S(1)}, bf16[192,256]{1,0:T(8,128)(2,1)S(1)}, u32[]{:S(2)}, u32[]{:S(2)}) collective-permute-start(bf16[192,256]{1,0:T(8,128)(2,1)S(1)} %stack.5.refs_0_), channel_id=1, source_target_pairs={{0,4},{4,0},{8,12},{12,8},{16,20},{20,16},{24,28},{28,24},{1,5},{5... | collective-permute-start | bytes 294920 | tf_op jit(solution)/shard_map/ppermute | solution.py:103
  58.9 9.3 %collective-permute-start.20 = (bf16[512,256]{1,0:T(8,128)(2,1)S(1)}, bf16[512,256]{1,0:T(8,128)(2,1)S(1)}, u32[]{:S(2)}, u32[]{:S(2)}) collective-permute-start(bf16[512,256]{1,0:T(8,128)(2,1)S(1)} %rest.4.refs_0_), channel_id=1, source_target_pairs={{0,2},{2,0},{1,3},{3,1},{4,6},{6,4},{5,7},{7,5},{8,10},{10,8},{9,1... | collective-permute-start | bytes 786440 | tf_op jit(solution)/shard_map/ppermute | solution.py:56
  62.4 8.1 %collective-permute-start.23 = (bf16[256,256]{1,0:T(8,128)(2,1)S(1)}, bf16[256,256]{1,0:T(8,128)(2,1)S(1)}, u32[]{:S(2)}, u32[]{:S(2)}) collective-permute-start(bf16[256,256]{1,0:T(8,128)(2,1)S(1)} %rest.5.refs_0_), channel_id=1, source_target_pairs={{0,2},{2,0},{1,3},{3,1},{4,6},{6,4},{5,7},{7,5},{8,10},{10,8},{9,1... | collective-permute-start | bytes 393224 | tf_op jit(solution)/shard_map/ppermute | solution.py:56
  65.0 6.9 %collective-permute-start.19 = (bf16[256,256]{1,0:T(8,128)(2,1)S(1)}, bf16[256,256]{1,0:T(8,128)(2,1)S(1)}, u32[]{:S(2)}, u32[]{:S(2)}) collective-permute-start(bf16[256,256]{1,0:T(8,128)(2,1)S(1)} %rest.3.refs_0_), channel_id=1, source_target_pairs={{0,2},{2,0},{1,3},{3,1},{4,6},{6,4},{5,7},{7,5},{8,10},{10,8},{9,1... | collective-permute-start | bytes 393224 | tf_op jit(solution)/shard_map/ppermute | solution.py:56
  66.5 5.4 %collective-permute-start.26 = (bf16[256,256]{1,0:T(8,128)(2,1)S(1)}, bf16[256,256]{1,0:T(8,128)(2,1)S(1)}, u32[]{:S(2)}, u32[]{:S(2)}) collective-permute-start(bf16[256,256]{1,0:T(8,128)(2,1)S(1)} %rest.5.refs_0_), channel_id=1, source_target_pairs={{0,1},{1,0},{2,3},{3,2},{4,5},{5,4},{6,7},{7,6},{8,9},{9,8},{10,11... | collective-permute-start | bytes 393224 | tf_op jit(solution)/shard_map/ppermute | solution.py:56
  66.5 8.7 %collective-permute-start.21 = (bf16[512,256]{1,0:T(8,128)(2,1)S(1)}, bf16[512,256]{1,0:T(8,128)(2,1)S(1)}, u32[]{:S(2)}, u32[]{:S(2)}) collective-permute-start(bf16[512,256]{1,0:T(8,128)(2,1)S(1)} %rest.4.refs_0_), channel_id=1, source_target_pairs={{0,1},{1,0},{2,3},{3,2},{4,5},{5,4},{6,7},{7,6},{8,9},{9,8},{10,11... | collective-permute-start | bytes 786440 | tf_op jit(solution)/shard_map/ppermute | solution.py:56
  68.2 7.0 %collective-permute-start.22 = (bf16[512,256]{1,0:T(8,128)(2,1)S(1)}, bf16[512,256]{1,0:T(8,128)(2,1)S(1)}, u32[]{:S(2)}, u32[]{:S(2)}) collective-permute-start(bf16[512,256]{1,0:T(8,128)(2,1)S(1)} %collective-permute-done.20.refs_5_.refs_1_), channel_id=1, source_target_pairs={{0,1},{1,0},{2,3},{3,2},{4,5},{5,4},{6,7},{7,6},{8,9},{9,8},{10,11... | collective-permute-start | bytes 786440 | tf_op jit(solution)/shard_map/ppermute | solution.py:56
  70.5 3.7 %collective-permute-start.24 = (bf16[256,256]{1,0:T(8,128)(2,1)S(1)}, bf16[256,256]{1,0:T(8,128)(2,1)S(1)}, u32[]{:S(2)}, u32[]{:S(2)}) collective-permute-start(bf16[256,256]{1,0:T(8,128)(2,1)S(1)} %rest.3.refs_0_), channel_id=1, source_target_pairs={{0,1},{1,0},{2,3},{3,2},{4,5},{5,4},{6,7},{7,6},{8,9},{9,8},{10,11... | collective-permute-start | bytes 393224 | tf_op jit(solution)/shard_map/ppermute | solution.py:56
  71.9 1.3 %collective-permute-start.27 = (bf16[256,256]{1,0:T(8,128)(2,1)S(1)}, bf16[256,256]{1,0:T(8,128)(2,1)S(1)}, u32[]{:S(2)}, u32[]{:S(2)}) collective-permute-start(bf16[256,256]{1,0:T(8,128)(2,1)S(1)} %collective-permute-done.23.refs_1_), channel_id=1, source_target_pairs={{0,1},{1,0},{2,3},{3,2},{4,5},{5,4},{6,7},{7,6},{8,9},{9,8},{10,11... | collective-permute-start | bytes 393224 | tf_op jit(solution)/shard_map/ppermute | solution.py:56
  71.9 2.3 %collective-permute-start.25 = (bf16[256,256]{1,0:T(8,128)(2,1)S(1)}, bf16[256,256]{1,0:T(8,128)(2,1)S(1)}, u32[]{:S(2)}, u32[]{:S(2)}) collective-permute-start(bf16[256,256]{1,0:T(8,128)(2,1)S(1)} %collective-permute-done.19.refs_4_.refs_1_), channel_id=1, source_target_pairs={{0,1},{1,0},{2,3},{3,2},{4,5},{5,4},{6,7},{7,6},{8,9},{9,8},{10,11... | collective-permute-start | bytes 393224 | tf_op jit(solution)/shard_map/ppermute | solution.py:56
  (5 other events, 43.9 us)

commit v16 on v13

--- a/solution.py
+++ b/solution.py
@@ -594,6 +594,9 @@
         cost_estimate=COST,
         name="project",
     )(*pieces, w_t, w_k, select, f_col)
+    halo, summ = lax.optimization_barrier((halo, summ))
+    halo_x = over_head(halo, X_PAIRS)
+    halo_core = over_head(halo, CORE_PAIRS)
     if slabs == 8:
         lined = [summ] + [by_distance(summ, d) for d in (2, 4, 6)]
     else:
@@ -614,9 +617,8 @@
         cost_estimate=COST,
         name="order",
     )(permute, permute_t, select, f_col, f_row, w_t, rows_here, k0, v0)
-    halo, near_k, *lined = lax.optimization_barrier((halo, near_k, *lined))
-    halo_x = over_head(halo, X_PAIRS)
-    halo_core = over_head(halo, CORE_PAIRS)
+    near_k, halo_x, *lined = lax.optimization_barrier((near_k, halo_x, *lined))
+    halo_last = over_head(halo_x, CORE_PAIRS)
     if slabs == 8:
         places = tuple((index, 0, step, 0) for index in range(4))
         column = stacked(lined, places, group)
@@ -647,8 +649,6 @@
         name="own",
     )(level_mix, q_t, keys, v_t, near_k, near_vt, seen)
 
-    halo_x, _, *summaries = lax.optimization_barrier((halo_x, top, *summaries))
-    halo_last = over_head(halo_x, CORE_PAIRS)
     window_k, window_v, coarse_k, coarse_v = pl.pallas_call(
         window_kernel,
         out_shape=(

time: 76 us -> 75.9 us (level)
  waiting for transfers between devices: 22.7 us -> 21.5 us
  starting transfers between devices: 26.3 us -> 27.3 us
    ppermute x18, waiting for transfers between devices: 15.2 us -> 11.4 us  [over_head(): return lax.ppermute(block, 'head', pairs)]
    ppermute x4, waiting for transfers between devices: 0.23 us -> 1.75 us  [by_distance(): lax.ppermute(block, 'seq', [(i, i ^ distance) for i in range(lax.axis_siz...]
    ppermute x4, starting transfers between devices: 4.96 us -> 6.05 us  [by_distance(): lax.ppermute(block, 'seq', [(i, i ^ distance) for i in range(lax.axis_siz...]
    ppermute x1, waiting for transfers between devices: 0.01 us -> 1.02 us  [to_next(): lax.ppermute(block, 'seq', [(i, i + 1) for i in range(lax.axis_size('seq'...]
where the time goes in v16:
time: 75.9 us; the launch traced here: 75.7 us
  starting transfers between devices  27.3 us (36%)
  Pallas kernels  26.6 us (35%)
  waiting for transfers between devices  21.5 us (28%)
    ppermute x18, waiting for transfers between devices, over_head(): return lax.ppermute(block, 'head', pairs)  11.4 us
    ppermute x5, starting transfers between devices, by_core(): return lax.ppermute(block, ('seq', 'head'), pairs)  9.51 us
    ppermute x18, starting transfers between devices, over_head(): return lax.ppermute(block, 'head', pairs)  8.79 us
    ppermute x5, waiting for transfers between devices, by_core(): return lax.ppermute(block, ('seq', 'head'), pairs)  7.28 us
    pallas_call x2, Pallas kernels, local(): pl.pallas_call(functools.partial(rest_kernel, first, count), out_shape=sh...  6.52 us
    ppermute x4, starting transfers between devices, by_distance(): lax.ppermute(block, 'seq', [(i, i ^ distance) for i in range(lax.axis_siz...  6.05 us
    pallas_call x1, Pallas kernels, local(): pl.pallas_call(own_kernel, out_shape=(shape((group, tok_rows), F32), shap...  3.94 us
    ppermute x1, starting transfers between devices, to_next(): lax.ppermute(block, 'seq', [(i, i + 1) for i in range(lax.axis_size('seq'...  2.99 us
  transfers between devices with their start and end apart: 28, of which 10 were waited for; matrix products, arithmetic and copies ran while one was open for 0% of the time, Pallas kernels for 23%

profile of v16, /device:TPU:0, one launch (start us, length us, event | category | flops | bytes accessed | tf_op | source)
XLA Modules:
  0.0 75.7 jit_solution(14773186792436064516)
XLA Ops:
  0.0 2.7 %send.1 = (bf16[144,512]{1,0:T(8,128)(2,1)}, bf16[144,512]{1,0:T(8,128)(2,1)}, bf16[144,512]{1,0:T(8,128)(2,1)}, bf16[144,512]{1,0:T(8,128)(2,1)}, bf16[144,512]{1,0:T(8,128)(2,1)}, /*index=5*/bf16[128,1024]{1,0:T(8,128)(2,1)}) custom-call(bf16[1024,1024]{1,0:T(8,128)(2,1)} %tokens_ref.1, s32[1,512]{1,0:T(1,128)} %mask_ref.3), custom_call_target="tpu_custom_call" | custom-call | flops 1 | bytes 1 | tf_op jit(solution)/shard_map/send/pallas_call | solution.py:149
  2.7 6.0 %collective-permute-start = (bf16[144,512]{1,0:T(8,128)(2,1)}, bf16[144,512]{1,0:T(8,128)(2,1)S(1)}, u32[]{:S(2)}, u32[]{:S(2)}) collective-permute-start(bf16[144,512]{1,0:T(8,128)(2,1)} %get-tuple-element.61), channel_id=1, source_target_pairs={{0,28},{1,25},{2,30},{3,27},{4,24},{5,29},{6,26},{7,31},{8,20},{9,... | collective-permute-start | bytes 442376 | tf_op jit(solution)/shard_map/ppermute | solution.py:126
  8.8 2.0 %collective-permute-start.3 = (bf16[144,512]{1,0:T(8,128)(2,1)}, bf16[144,512]{1,0:T(8,128)(2,1)S(1)}, u32[]{:S(2)}, u32[]{:S(2)}) collective-permute-start(bf16[144,512]{1,0:T(8,128)(2,1)} %get-tuple-element.67), channel_id=1, source_target_pairs={{0,8},{1,9},{2,10},{3,11},{4,12},{5,13},{6,14},{7,15},{8,0},{9,1},... | collective-permute-start | bytes 442376 | tf_op jit(solution)/shard_map/ppermute | solution.py:126
  10.7 1.5 %collective-permute-start.4 = (bf16[144,512]{1,0:T(8,128)(2,1)}, bf16[144,512]{1,0:T(8,128)(2,1)S(1)}, u32[]{:S(2)}, u32[]{:S(2)}) collective-permute-start(bf16[144,512]{1,0:T(8,128)(2,1)} %get-tuple-element.68), channel_id=1, source_target_pairs={{0,4},{1,5},{2,6},{3,7},{4,0},{5,1},{6,2},{7,3},{8,12},{9,13},{10,... | collective-permute-start | bytes 442376 | tf_op jit(solution)/shard_map/ppermute | solution.py:126
  12.3 2.5 %prepare.1 = (bf16[1024,1024]{1,0:T(8,128)(2,1)S(1)}, bf16[1024,1024]{1,0:T(8,128)(2,1)S(1)}, bf16[672,1024]{1,0:T(8,128)(2,1)S(1)}, f32[160,128]{1,0:T(8,128)S(...) custom-call(s32[1,1024]{1,0:T(1,128)S(1)} %copy-done.8, ...), custom_call_target="tpu_custom_call" | custom-call | flops 1 | bytes 1 | tf_op jit(solution)/shard_map/prepare/pallas_call | solution.py:546
  14.8 4.8 %collective-permute-done.2.refs_1_.refs_2_.refs_4_.refs_8_ = bf16[144,512]{1,0:T(8,128)(2,1)S(1)} collective-permute-done((bf16[144,512]{1,0:T(8,128)(2,1)}, bf16[144,512]{1,0:T(8,128)(2,1)S(1)}, u32[]{:S(2)}, u32[]{:S(2)}) %collective-permute-start.2) | collective-permute-done | bytes 147488 | tf_op jit(solution)/shard_map/ppermute | solution.py:126
  19.6 2.4 %collective-permute-done.3.refs_2_.refs_5_.refs_9_ = bf16[144,512]{1,0:T(8,128)(2,1)S(1)} collective-permute-done((bf16[144,512]{1,0:T(8,128)(2,1)}, bf16[144,512]{1,0:T(8,128)(2,1)S(1)}, u32[]{:S(2)}, u32[]{:S(2)}) %collective-permute-start.3) | collective-permute-done | bytes 147488 | tf_op jit(solution)/shard_map/ppermute | solution.py:126
  22.1 1.6 %collective-permute-start.5 = (bf16[128,512]{1,0:T(8,128)(2,1)S(1)}, bf16[128,512]{1,0:T(8,128)(2,1)S(1)}, u32[]{:S(2)}, u32[]{:S(2)}) collective-permute-start(bf16[128,512]{1,0:T(8,128)(2,1)S(1)} %stack.3), channel_id=1, source_target_pairs={{0,2},{2,0},{1,3},{3,1},{4,6},{6,4},{5,7},{7,5},{8,10},{10,8},{9,1... | collective-permute-start | bytes 393224 | tf_op jit(solution)/shard_map/ppermute | solution.py:56
  24.7 2.5 %collective-permute-done.5.refs_2_ = bf16[128,512]{1,0:T(8,128)(2,1)S(1)} collective-permute-done((bf16[128,512]{1,0:T(8,128)(2,1)S(1)}, bf16[128,512]{1,0:T(8,128)(2,1)S(1)}, u32[]{:S(2)}, u32[]{:S(2)}) %collective-permute-start.5) | collective-permute-done | bytes 131104 | tf_op jit(solution)/shard_map/ppermute | solution.py:56
  27.2 1.6 %collective-permute-start.6 = (bf16[128,512]{1,0:T(8,128)(2,1)S(1)}, bf16[128,512]{1,0:T(8,128)(2,1)S(1)}, u32[]{:S(2)}, u32[]{:S(2)}) collective-permute-start(bf16[128,512]{1,0:T(8,128)(2,1)S(1)} %stack.4.refs_1_), channel_id=1, source_target_pairs={{0,2},{2,0},{1,3},{3,1},{4,6},{6,4},{5,7},{7,5},{8,10},{10,8},{9,1... | collective-permute-start | bytes 393224 | tf_op jit(solution)/shard_map/ppermute | solution.py:56
  29.3 3.0 %collective-permute-start.14 = (bf16[512,256]{1,0:T(8,128)(2,1)S(1)}, bf16[512,256]{1,0:T(8,128)(2,1)S(1)}, u32[]{:S(2)}, u32[]{:S(2)}) collective-permute-start(bf16[512,256]{1,0:T(8,128)(2,1)S(1)} %pack.1), channel_id=1, source_target_pairs={{0,4},{4,8},{8,12},{12,16},{16,20},{20,24},{24,28},{1,5},{5,9},{9,... | collective-permute-start | bytes 786440 | tf_op jit(solution)/shard_map/ppermute | solution.py:60
  32.4 1.2 %expand.1 = (bf16[1024,512]{1,0:T(8,128)(2,1)S(1)}, bf16[512,1024]{1,0:T(8,128)(2,1)S(1)}, f32[2048,128]{1,0:T(8,128)S(1)}) custom-call(f32[1024,128]{1,0:T(8,128)S(1)} %get-tuple-element.62.seen_ref, bf16[144,512]{1,0:T(8,128)(2,1)S(1)} %collective-permute-done.refs_0_, bf16[144,512]{1,0:T(8,128)(2,1)S(1)} %collective-permute-done.7.refs_1_.refs_2_.refs_4_, ...), custom_call_target="tpu_custom_call" | custom-call | flops 1 | bytes 1 | tf_op jit(solution)/shard_map/expand/pallas_call | solution.py:566
  33.6 0.6 collective-permute-start.13
  34.2 1.0 %collective-permute-done.13.refs_7_ = bf16[128,512]{1,0:T(8,128)(2,1)S(1)} collective-permute-done((bf16[128,512]{1,0:T(8,128)(2,1)S(1)}, bf16[128,512]{1,0:T(8,128)(2,1)S(1)}, u32[]{:S(2)}, u32[]{:S(2)}) %collective-permute-start.13) | collective-permute-done | bytes 131104 | tf_op jit(solution)/shard_map/ppermute | solution.py:56
  35.2 1.8 %project.1 = (bf16[48,256]{1,0:T(8,128)(2,1)S(1)}, bf16[1024,256]{1,0:T(8,128)(2,1)S(1)}, bf16[256,1024]{1,0:T(8,128)(2,1)S(1)}, bf16[1024,1024]{1,0:T(8,128)(2,1)S(1)}) custom-call(bf16[144,512]{1,0:T(8,128)(2,1)S(1)} %collective-permute-done.refs_0_, bf16[128,512]{1,0:T(8,128)(2,1)S(1)} %stack.4.refs_1_, ...), custom_call_target="tpu_custom_call" | custom-call | flops 1 | bytes 1 | tf_op jit(solution)/shard_map/project/pallas_call | solution.py:583
  37.0 1.0 %collective-permute-done.14.refs_0_ = bf16[512,256]{1,0:T(8,128)(2,1)S(1)} collective-permute-done((bf16[512,256]{1,0:T(8,128)(2,1)S(1)}, bf16[512,256]{1,0:T(8,128)(2,1)S(1)}, u32[]{:S(2)}, u32[]{:S(2)}) %collective-permute-start.14) | collective-permute-done | bytes 262176 | tf_op jit(solution)/shard_map/ppermute | solution.py:60
  38.0 1.2 %collective-permute-start.15 = (bf16[512,256]{1,0:T(8,128)(2,1)S(1)}, bf16[512,256]{1,0:T(8,128)(2,1)S(1)}, u32[]{:S(2)}, u32[]{:S(2)}) collective-permute-start(bf16[512,256]{1,0:T(8,128)(2,1)S(1)} %collective-permute-done.14.refs_0_), channel_id=1, source_target_pairs={{0,2},{2,0},{1,3},{3,1},{4,6},{6,4},{5,7},{7,5},{8,10},{10,8},{9,1... | collective-permute-start | bytes 786440 | tf_op jit(solution)/shard_map/ppermute | solution.py:56
  39.2 4.5 %collective-permute-start.18 = (bf16[48,256]{1,0:T(8,128)(2,1)S(1)}, bf16[48,256]{1,0:T(8,128)(2,1)S(1)}, u32[]{:S(2)}, u32[]{:S(2)}) collective-permute-start(bf16[48,256]{1,0:T(8,128)(2,1)S(1)} %get-tuple-element.83.refs_0_), channel_id=1, source_target_pairs={{0,24},{4,28},{8,16},{12,20},{16,8},{20,12},{24,0},{28,4},{1,25},{... | collective-permute-start | bytes 73736 | tf_op jit(solution)/shard_map/ppermute | solution.py:116
  43.7 0.6 collective-permute-start.16
  44.3 2.6 %order.1 = (bf16[256,1024]{1,0:T(8,128)(2,1)S(1)}, bf16[256,1024]{1,0:T(8,128)(2,1)S(1)}, bf16[1024,256]{1,0:T(8,128)(2,1)S(1)}, bf16[128,256]{1,0:T(8,128)(2,1)S(1)}, bf16[256,128]{1,0:T(8,128)(2,1)S(1)}) custom-call(bf16[1024,1024]{1,0:T(8,128)(2,1)S(1)} %get-tuple-element.55.p_ref, bf16[1024,1024]{1,0:T(8,128)(2,1)S(1)} %get-tuple-element.56.pt_ref, ...), custom_call_target="tpu_custom_call" | custom-call | flops 1 | bytes 1 | tf_op jit(solution)/shard_map/order/pallas_call | solution.py:605
  47.0 1.4 %collective-permute-done.17.refs_2_ = bf16[48,256]{1,0:T(8,128)(2,1)S(1)} collective-permute-done((bf16[48,256]{1,0:T(8,128)(2,1)S(1)}, bf16[48,256]{1,0:T(8,128)(2,1)S(1)}, u32[]{:S(2)}, u32[]{:S(2)}) %collective-permute-start.17) | collective-permute-done | bytes 24608 | tf_op jit(solution)/shard_map/ppermute | solution.py:116
  48.5 1.0 %collective-permute-start.21 = (bf16[192,256]{1,0:T(8,128)(2,1)S(1)}, bf16[192,256]{1,0:T(8,128)(2,1)S(1)}, u32[]{:S(2)}, u32[]{:S(2)}) collective-permute-start(bf16[192,256]{1,0:T(8,128)(2,1)S(1)} %stack.5.refs_4_), channel_id=1, source_target_pairs={{0,4},{4,0},{8,12},{12,8},{16,20},{20,16},{24,28},{28,24},{1,5},{5... | collective-permute-start | bytes 294920 | tf_op jit(solution)/shard_map/ppermute | solution.py:116
  49.5 3.9 %own.1 = (f32[256,1024]{1,0:T(8,128)S(1)}, f32[256,1024]{1,0:T(8,128)S(1)}, f32[8,512]{1,0:T(8,128)S(1)}, f32[8,512]{1,0:T(8,128)S(1)}) custom-call(f32[4,4]{1,0:T(4,128)S(1)} %copy-done.5, bf16[256,1024]{1,0:T(8,128)(2,1)S(1)} %get-tuple-element.88.qt_ref, bf16[1024,256]{1,0:T(8,128)(2,1)S(1)} %get-tuple-element.89.k_ref, ...), custom_call_target="tpu_custom_call" | custom-call | flops 1 | bytes 1 | tf_op jit(solution)/shard_map/own/pallas_call | solution.py:633
  53.7 2.1 %window.1 = (bf16[2048,256]{1,0:T(8,128)(2,1)S(1)}, bf16[256,2048]{1,0:T(8,128)(2,1)S(1)}, bf16[64,256]{1,0:T(8,128)(2,1)S(1)}, bf16[256,64]{1,0:T(8,128)(2,1)S(1)}) custom-call(bf16[1024,256]{1,0:T(8,128)(2,1)S(1)} %get-tuple-element.89.k_ref, bf16[256,1024]{1,0:T(8,128)(2,1)S(1)} %get-tuple-element.90.vt_ref, ...), custom_call_target="tpu_custom_call" | custom-call | flops 1 | bytes 1 | tf_op jit(solution)/shard_map/window/pallas_call | solution.py:652
  55.9 3.4 %rest.2.refs_0_ = bf16[512,256]{1,0:T(8,128)(2,1)S(1)} custom-call(s32[4,8]{1,0:T(4,128)S(1)} %bitcast.1, f32[4,4]{1,0:T(4,128)S(1)} %copy-done.5, bf16[256,1024]{1,0:T(8,128)(2,1)S(1)} %get-tuple-element.88.qt_ref, bf16[2048,256]{1,0:T(8,128)(2,1)S(1)} %get-tuple-element.93.kw_ref, bf16[256,2048]{1,0:T(8,128)(2,1)S(1)} %get-tuple-element.94.vw_ref, ...), custom_call_target="tpu_custom_call" | custom-call | flops 1 | bytes 1 | tf_op jit(solution)/shard_map/rest/pallas_call | solution.py:694
  59.3 0.9 %collective-permute-start.22 = (bf16[512,256]{1,0:T(8,128)(2,1)S(1)}, bf16[512,256]{1,0:T(8,128)(2,1)S(1)}, u32[]{:S(2)}, u32[]{:S(2)}) collective-permute-start(bf16[512,256]{1,0:T(8,128)(2,1)S(1)} %rest.2.refs_0_), channel_id=1, source_target_pairs={{0,2},{2,0},{1,3},{3,1},{4,6},{6,4},{5,7},{7,5},{8,10},{10,8},{9,1... | collective-permute-start | bytes 786440 | tf_op jit(solution)/shard_map/ppermute | solution.py:56
  60.2 3.2 %rest.3.refs_0_ = bf16[512,256]{1,0:T(8,128)(2,1)S(1)} custom-call(s32[4,8]{1,0:T(4,128)S(1)} %bitcast.2, f32[4,4]{1,0:T(4,128)S(1)} %copy-done.5, bf16[256,1024]{1,0:T(8,128)(2,1)S(1)} %get-tuple-element.88.qt_ref, bf16[2048,256]{1,0:T(8,128)(2,1)S(1)} %get-tuple-element.93.kw_ref, bf16[256,2048]{1,0:T(8,128)(2,1)S(1)} %get-tuple-element.94.vw_ref, ...), custom_call_target="tpu_custom_call" | custom-call | flops 1 | bytes 1 | tf_op jit(solution)/shard_map/rest/pallas_call | solution.py:694
  63.3 1.3 %collective-permute-start.23 = (bf16[512,256]{1,0:T(8,128)(2,1)S(1)}, bf16[512,256]{1,0:T(8,128)(2,1)S(1)}, u32[]{:S(2)}, u32[]{:S(2)}) collective-permute-start(bf16[512,256]{1,0:T(8,128)(2,1)S(1)} %rest.3.refs_0_), channel_id=1, source_target_pairs={{0,2},{2,0},{1,3},{3,1},{4,6},{6,4},{5,7},{7,5},{8,10},{10,8},{9,1... | collective-permute-start | bytes 786440 | tf_op jit(solution)/shard_map/ppermute | solution.py:56
  64.6 4.0 %collective-permute-done.22.refs_1_ = bf16[512,256]{1,0:T(8,128)(2,1)S(1)} collective-permute-done((bf16[512,256]{1,0:T(8,128)(2,1)S(1)}, bf16[512,256]{1,0:T(8,128)(2,1)S(1)}, u32[]{:S(2)}, u32[]{:S(2)}) %collective-permute-start.22) | collective-permute-done | bytes 262176 | tf_op jit(solution)/shard_map/ppermute | solution.py:56
  69.1 3.8 %collective-permute-done.23.refs_4_.refs_1_ = bf16[512,256]{1,0:T(8,128)(2,1)S(1)} collective-permute-done((bf16[512,256]{1,0:T(8,128)(2,1)S(1)}, bf16[512,256]{1,0:T(8,128)(2,1)S(1)}, u32[]{:S(2)}, u32[]{:S(2)}) %collective-permute-start.23) | collective-permute-done | bytes 262176 | tf_op jit(solution)/shard_map/ppermute | solution.py:56
  72.9 1.3 %output.2.refs_4_ = bf16[1024,256]{1,0:T(8,128)(2,1)} custom-call(bf16[1024,256]{1,0:T(8,128)(2,1)S(1)} %copy-done, bf16[512,256]{1,0:T(8,128)(2,1)S(1)} %rest.2.refs_0_, bf16[512,256]{1,0:T(8,128)(2,1)S(1)} %collective-permute-done.22.refs_1_, bf16[512,256]{1,0:T(8,128)(2,1)S(1)} %collective-permute-done.26.refs_2_, ...), custom_call_target="tpu_custom_call" | custom-call | flops 1 | bytes 1 | tf_op jit(solution)/shard_map/output/pallas_call | solution.py:679
  74.4 1.3 %output.3 = bf16[1024,256]{1,0:T(8,128)(2,1)} custom-call(bf16[1024,256]{1,0:T(8,128)(2,1)S(1)} %copy-done, bf16[512,256]{1,0:T(8,128)(2,1)S(1)} %rest.3.refs_0_, bf16[512,256]{1,0:T(8,128)(2,1)S(1)} %collective-permute-done.23.refs_4_.refs_1_, bf16[512,256]{1,0:T(8,128)(2,1)S(1)} %collective-permute-done.24.refs_2_, ...), custom_call_target="tpu_custom_call", output_to_operand_aliasing={{}: (5, {})} | custom-call | flops 1 | bytes 1 | tf_op jit(solution)/shard_map/output/pallas_call | solution.py:679
  (57 shorter events, 2.9 us)
Async XLA Ops:
  0.0 12.3 %copy-start.4 = (bf16[1024,256]{1,0:T(8,128)(2,1)S(1)}, bf16[1024,256]{1,0:T(8,128)(2,1)}, u32[]{:S(2)}) copy-start(bf16[1024,256]{1,0:T(8,128)(2,1)} %wk_in.1) | copy-start | bytes 1572868
  0.0 12.3 %copy-start.2 = (bf16[1024,256]{1,0:T(8,128)(2,1)S(1)}, bf16[1024,256]{1,0:T(8,128)(2,1)}, u32[]{:S(2)}) copy-start(bf16[1024,256]{1,0:T(8,128)(2,1)} %wq_ref.1) | copy-start | bytes 1572868
  2.7 26.1 %copy-start.1 = (bf16[128,1024]{1,0:T(8,128)(2,1)S(1)}, bf16[128,1024]{1,0:T(8,128)(2,1)}, u32[]{:S(2)}) copy-start(bf16[128,1024]{1,0:T(8,128)(2,1)} %get-tuple-element.74.refs_10_.refs_14_) | copy-start | bytes 786436
  2.7 12.0 %collective-permute-start = (bf16[144,512]{1,0:T(8,128)(2,1)}, bf16[144,512]{1,0:T(8,128)(2,1)S(1)}, u32[]{:S(2)}, u32[]{:S(2)}) collective-permute-start(bf16[144,512]{1,0:T(8,128)(2,1)} %get-tuple-element.61), channel_id=1, source_target_pairs={{0,28},{1,25},{2,30},{3,27},{4,24},{5,29},{6,26},{7,31},{8,20},{9,... | collective-permute-start | bytes 442376 | tf_op jit(solution)/shard_map/ppermute | solution.py:126
  8.8 10.9 %collective-permute-start.2 = (bf16[144,512]{1,0:T(8,128)(2,1)}, bf16[144,512]{1,0:T(8,128)(2,1)S(1)}, u32[]{:S(2)}, u32[]{:S(2)}) collective-permute-start(bf16[144,512]{1,0:T(8,128)(2,1)} %get-tuple-element.66), channel_id=1, source_target_pairs={{0,12},{1,13},{2,14},{3,15},{4,8},{5,9},{6,10},{7,11},{8,4},{9,5},... | collective-permute-start | bytes 442376 | tf_op jit(solution)/shard_map/ppermute | solution.py:126
  8.8 13.3 %collective-permute-start.3 = (bf16[144,512]{1,0:T(8,128)(2,1)}, bf16[144,512]{1,0:T(8,128)(2,1)S(1)}, u32[]{:S(2)}, u32[]{:S(2)}) collective-permute-start(bf16[144,512]{1,0:T(8,128)(2,1)} %get-tuple-element.67), channel_id=1, source_target_pairs={{0,8},{1,9},{2,10},{3,11},{4,12},{5,13},{6,14},{7,15},{8,0},{9,1},... | collective-permute-start | bytes 442376 | tf_op jit(solution)/shard_map/ppermute | solution.py:126
  10.7 11.3 %collective-permute-start.4 = (bf16[144,512]{1,0:T(8,128)(2,1)}, bf16[144,512]{1,0:T(8,128)(2,1)S(1)}, u32[]{:S(2)}, u32[]{:S(2)}) collective-permute-start(bf16[144,512]{1,0:T(8,128)(2,1)} %get-tuple-element.68), channel_id=1, source_target_pairs={{0,4},{1,5},{2,6},{3,7},{4,0},{5,1},{6,2},{7,3},{8,12},{9,13},{10,... | collective-permute-start | bytes 442376 | tf_op jit(solution)/shard_map/ppermute | solution.py:126
  12.3 11.9 %collective-permute-start.1 = (bf16[144,512]{1,0:T(8,128)(2,1)}, bf16[144,512]{1,0:T(8,128)(2,1)S(1)}, u32[]{:S(2)}, u32[]{:S(2)}) collective-permute-start(bf16[144,512]{1,0:T(8,128)(2,1)} %get-tuple-element.65), channel_id=1, source_target_pairs={{0,20},{1,17},{2,22},{3,19},{4,16},{5,21},{6,18},{7,23},{8,28},{9,... | collective-permute-start | bytes 442376 | tf_op jit(solution)/shard_map/ppermute | solution.py:126
  22.1 5.0 %collective-permute-start.5 = (bf16[128,512]{1,0:T(8,128)(2,1)S(1)}, bf16[128,512]{1,0:T(8,128)(2,1)S(1)}, u32[]{:S(2)}, u32[]{:S(2)}) collective-permute-start(bf16[128,512]{1,0:T(8,128)(2,1)S(1)} %stack.3), channel_id=1, source_target_pairs={{0,2},{2,0},{1,3},{3,1},{4,6},{6,4},{5,7},{7,5},{8,10},{10,8},{9,1... | collective-permute-start | bytes 393224 | tf_op jit(solution)/shard_map/ppermute | solution.py:56
  23.6 3.6 %collective-permute-start.9 = (bf16[144,512]{1,0:T(8,128)(2,1)S(1)}, bf16[144,512]{1,0:T(8,128)(2,1)S(1)}, u32[]{:S(2)}, u32[]{:S(2)}) collective-permute-start(bf16[144,512]{1,0:T(8,128)(2,1)S(1)} %collective-permute-done.2.refs_1_.refs_2_.refs_4_.refs_8_), channel_id=1, source_target_pairs={{0,1},{1,0},{2,3},{3,2},{4,5},{5,4},{6,7},{7,6},{8,9},{9,8},{10,11... | collective-permute-start | bytes 442376 | tf_op jit(solution)/shard_map/ppermute | solution.py:56
  23.6 5.1 %collective-permute-start.10 = (bf16[144,512]{1,0:T(8,128)(2,1)S(1)}, bf16[144,512]{1,0:T(8,128)(2,1)S(1)}, u32[]{:S(2)}, u32[]{:S(2)}) collective-permute-start(bf16[144,512]{1,0:T(8,128)(2,1)S(1)} %collective-permute-done.3.refs_2_.refs_5_.refs_9_), channel_id=1, source_target_pairs={{0,1},{1,0},{2,3},{3,2},{4,5},{5,4},{6,7},{7,6},{8,9},{9,8},{10,11... | collective-permute-start | bytes 442376 | tf_op jit(solution)/shard_map/ppermute | solution.py:56
  24.2 4.6 %collective-permute-start.11 = (bf16[144,512]{1,0:T(8,128)(2,1)S(1)}, bf16[144,512]{1,0:T(8,128)(2,1)S(1)}, u32[]{:S(2)}, u32[]{:S(2)}) collective-permute-start(bf16[144,512]{1,0:T(8,128)(2,1)S(1)} %collective-permute-done.4.refs_3_.refs_6_.refs_10_), channel_id=1, source_target_pairs={{0,1},{1,0},{2,3},{3,2},{4,5},{5,4},{6,7},{7,6},{8,9},{9,8},{10,11... | collective-permute-start | bytes 442376 | tf_op jit(solution)/shard_map/ppermute | solution.py:56
  24.2 4.6 %collective-permute-start.7 = (bf16[144,512]{1,0:T(8,128)(2,1)S(1)}, bf16[144,512]{1,0:T(8,128)(2,1)S(1)}, u32[]{:S(2)}, u32[]{:S(2)}) collective-permute-start(bf16[144,512]{1,0:T(8,128)(2,1)S(1)} %collective-permute-done.refs_0_), channel_id=1, source_target_pairs={{0,1},{1,0},{2,3},{3,2},{4,5},{5,4},{6,7},{7,6},{8,9},{9,8},{10,11... | collective-permute-start | bytes 442376 | tf_op jit(solution)/shard_map/ppermute | solution.py:56
  27.1 1.7 %collective-permute-start.8 = (bf16[128,512]{1,0:T(8,128)(2,1)S(1)}, bf16[128,512]{1,0:T(8,128)(2,1)S(1)}, u32[]{:S(2)}, u32[]{:S(2)}) collective-permute-start(bf16[128,512]{1,0:T(8,128)(2,1)S(1)} %stack.4.refs_1_), channel_id=1, source_target_pairs={{0,1},{1,0},{2,3},{3,2},{4,5},{5,4},{6,7},{7,6},{8,9},{9,8},{10,11... | collective-permute-start | bytes 393224 | tf_op jit(solution)/shard_map/ppermute | solution.py:56
  27.2 6.4 %collective-permute-start.6 = (bf16[128,512]{1,0:T(8,128)(2,1)S(1)}, bf16[128,512]{1,0:T(8,128)(2,1)S(1)}, u32[]{:S(2)}, u32[]{:S(2)}) collective-permute-start(bf16[128,512]{1,0:T(8,128)(2,1)S(1)} %stack.4.refs_1_), channel_id=1, source_target_pairs={{0,2},{2,0},{1,3},{3,1},{4,6},{6,4},{5,7},{7,5},{8,10},{10,8},{9,1... | collective-permute-start | bytes 393224 | tf_op jit(solution)/shard_map/ppermute | solution.py:56
  29.3 8.7 %collective-permute-start.14 = (bf16[512,256]{1,0:T(8,128)(2,1)S(1)}, bf16[512,256]{1,0:T(8,128)(2,1)S(1)}, u32[]{:S(2)}, u32[]{:S(2)}) collective-permute-start(bf16[512,256]{1,0:T(8,128)(2,1)S(1)} %pack.1), channel_id=1, source_target_pairs={{0,4},{4,8},{8,12},{12,16},{16,20},{20,24},{24,28},{1,5},{5,9},{9,... | collective-permute-start | bytes 786440 | tf_op jit(solution)/shard_map/ppermute | solution.py:60
  32.3 1.9 %collective-permute-start.12 = (bf16[128,512]{1,0:T(8,128)(2,1)S(1)}, bf16[128,512]{1,0:T(8,128)(2,1)S(1)}, u32[]{:S(2)}, u32[]{:S(2)}) collective-permute-start(bf16[128,512]{1,0:T(8,128)(2,1)S(1)} %collective-permute-done.5.refs_2_), channel_id=1, source_target_pairs={{0,1},{1,0},{2,3},{3,2},{4,5},{5,4},{6,7},{7,6},{8,9},{9,8},{10,11... | collective-permute-start | bytes 393224 | tf_op jit(solution)/shard_map/ppermute | solution.py:56
  33.6 1.5 %collective-permute-start.13 = (bf16[128,512]{1,0:T(8,128)(2,1)S(1)}, bf16[128,512]{1,0:T(8,128)(2,1)S(1)}, u32[]{:S(2)}, u32[]{:S(2)}) collective-permute-start(bf16[128,512]{1,0:T(8,128)(2,1)S(1)} %collective-permute-done.6.refs_3_), channel_id=1, source_target_pairs={{0,1},{1,0},{2,3},{3,2},{4,5},{5,4},{6,7},{7,6},{8,9},{9,8},{10,11... | collective-permute-start | bytes 393224 | tf_op jit(solution)/shard_map/ppermute | solution.py:56
  38.0 10.5 %collective-permute-start.15 = (bf16[512,256]{1,0:T(8,128)(2,1)S(1)}, bf16[512,256]{1,0:T(8,128)(2,1)S(1)}, u32[]{:S(2)}, u32[]{:S(2)}) collective-permute-start(bf16[512,256]{1,0:T(8,128)(2,1)S(1)} %collective-permute-done.14.refs_0_), channel_id=1, source_target_pairs={{0,2},{2,0},{1,3},{3,1},{4,6},{6,4},{5,7},{7,5},{8,10},{10,8},{9,1... | collective-permute-start | bytes 786440 | tf_op jit(solution)/shard_map/ppermute | solution.py:56
  39.2 7.8 %collective-permute-start.18 = (bf16[48,256]{1,0:T(8,128)(2,1)S(1)}, bf16[48,256]{1,0:T(8,128)(2,1)S(1)}, u32[]{:S(2)}, u32[]{:S(2)}) collective-permute-start(bf16[48,256]{1,0:T(8,128)(2,1)S(1)} %get-tuple-element.83.refs_0_), channel_id=1, source_target_pairs={{0,24},{4,28},{8,16},{12,20},{16,8},{20,12},{24,0},{28,4},{1,25},{... | collective-permute-start | bytes 73736 | tf_op jit(solution)/shard_map/ppermute | solution.py:116
  43.7 4.7 %collective-permute-start.17 = (bf16[48,256]{1,0:T(8,128)(2,1)S(1)}, bf16[48,256]{1,0:T(8,128)(2,1)S(1)}, u32[]{:S(2)}, u32[]{:S(2)}) collective-permute-start(bf16[48,256]{1,0:T(8,128)(2,1)S(1)} %get-tuple-element.83.refs_0_), channel_id=1, source_target_pairs={{0,16},{4,20},{8,24},{12,28},{16,0},{20,4},{24,8},{28,12},{1,17},{... | collective-permute-start | bytes 73736 | tf_op jit(solution)/shard_map/ppermute | solution.py:116
  43.7 4.7 %collective-permute-start.16 = (bf16[48,256]{1,0:T(8,128)(2,1)S(1)}, bf16[48,256]{1,0:T(8,128)(2,1)S(1)}, u32[]{:S(2)}, u32[]{:S(2)}) collective-permute-start(bf16[48,256]{1,0:T(8,128)(2,1)S(1)} %get-tuple-element.83.refs_0_), channel_id=1, source_target_pairs={{0,8},{4,12},{8,0},{12,4},{16,24},{20,28},{24,16},{28,20},{1,9},{5... | collective-permute-start | bytes 73736 | tf_op jit(solution)/shard_map/ppermute | solution.py:116
  46.9 6.5 %collective-permute-start.19 = (bf16[512,256]{1,0:T(8,128)(2,1)S(1)}, bf16[512,256]{1,0:T(8,128)(2,1)S(1)}, u32[]{:S(2)}, u32[]{:S(2)}) collective-permute-start(bf16[512,256]{1,0:T(8,128)(2,1)S(1)} %collective-permute-done.14.refs_0_), channel_id=1, source_target_pairs={{0,1},{1,0},{2,3},{3,2},{4,5},{5,4},{6,7},{7,6},{8,9},{9,8},{10,11... | collective-permute-start | bytes 786440 | tf_op jit(solution)/shard_map/ppermute | solution.py:56
  48.5 5.3 %collective-permute-start.20 = (bf16[512,256]{1,0:T(8,128)(2,1)S(1)}, bf16[512,256]{1,0:T(8,128)(2,1)S(1)}, u32[]{:S(2)}, u32[]{:S(2)}) collective-permute-start(bf16[512,256]{1,0:T(8,128)(2,1)S(1)} %collective-permute-done.15.refs_1_), channel_id=1, source_target_pairs={{0,1},{1,0},{2,3},{3,2},{4,5},{5,4},{6,7},{7,6},{8,9},{9,8},{10,11... | collective-permute-start | bytes 786440 | tf_op jit(solution)/shard_map/ppermute | solution.py:56
  48.5 5.3 %collective-permute-start.21 = (bf16[192,256]{1,0:T(8,128)(2,1)S(1)}, bf16[192,256]{1,0:T(8,128)(2,1)S(1)}, u32[]{:S(2)}, u32[]{:S(2)}) collective-permute-start(bf16[192,256]{1,0:T(8,128)(2,1)S(1)} %stack.5.refs_4_), channel_id=1, source_target_pairs={{0,4},{4,0},{8,12},{12,8},{16,20},{20,16},{24,28},{28,24},{1,5},{5... | collective-permute-start | bytes 294920 | tf_op jit(solution)/shard_map/ppermute | solution.py:116
  59.3 13.6 %copy-start = (bf16[1024,256]{1,0:T(8,128)(2,1)S(1)}, bf16[1024,256]{1,0:T(8,128)(2,1)}, u32[]{:S(2)}) copy-start(bf16[1024,256]{1,0:T(8,128)(2,1)} %w_ref.3) | copy-start | bytes 1572868
  59.3 9.3 %collective-permute-start.22 = (bf16[512,256]{1,0:T(8,128)(2,1)S(1)}, bf16[512,256]{1,0:T(8,128)(2,1)S(1)}, u32[]{:S(2)}, u32[]{:S(2)}) collective-permute-start(bf16[512,256]{1,0:T(8,128)(2,1)S(1)} %rest.2.refs_0_), channel_id=1, source_target_pairs={{0,2},{2,0},{1,3},{3,1},{4,6},{6,4},{5,7},{7,5},{8,10},{10,8},{9,1... | collective-permute-start | bytes 786440 | tf_op jit(solution)/shard_map/ppermute | solution.py:56
  63.3 9.6 %collective-permute-start.23 = (bf16[512,256]{1,0:T(8,128)(2,1)S(1)}, bf16[512,256]{1,0:T(8,128)(2,1)S(1)}, u32[]{:S(2)}, u32[]{:S(2)}) collective-permute-start(bf16[512,256]{1,0:T(8,128)(2,1)S(1)} %rest.3.refs_0_), channel_id=1, source_target_pairs={{0,2},{2,0},{1,3},{3,1},{4,6},{6,4},{5,7},{7,5},{8,10},{10,8},{9,1... | collective-permute-start | bytes 786440 | tf_op jit(solution)/shard_map/ppermute | solution.py:56
  64.6 8.3 %collective-permute-start.26 = (bf16[512,256]{1,0:T(8,128)(2,1)S(1)}, bf16[512,256]{1,0:T(8,128)(2,1)S(1)}, u32[]{:S(2)}, u32[]{:S(2)}) collective-permute-start(bf16[512,256]{1,0:T(8,128)(2,1)S(1)} %rest.2.refs_0_), channel_id=1, source_target_pairs={{0,1},{1,0},{2,3},{3,2},{4,5},{5,4},{6,7},{7,6},{8,9},{9,8},{10,11... | collective-permute-start | bytes 786440 | tf_op jit(solution)/shard_map/ppermute | solution.py:56
  68.6 4.3 %collective-permute-start.27 = (bf16[512,256]{1,0:T(8,128)(2,1)S(1)}, bf16[512,256]{1,0:T(8,128)(2,1)S(1)}, u32[]{:S(2)}, u32[]{:S(2)}) collective-permute-start(bf16[512,256]{1,0:T(8,128)(2,1)S(1)} %collective-permute-done.22.refs_1_), channel_id=1, source_target_pairs={{0,1},{1,0},{2,3},{3,2},{4,5},{5,4},{6,7},{7,6},{8,9},{9,8},{10,11... | collective-permute-start | bytes 786440 | tf_op jit(solution)/shard_map/ppermute | solution.py:56
  68.6 5.7 %collective-permute-start.24 = (bf16[512,256]{1,0:T(8,128)(2,1)S(1)}, bf16[512,256]{1,0:T(8,128)(2,1)S(1)}, u32[]{:S(2)}, u32[]{:S(2)}) collective-permute-start(bf16[512,256]{1,0:T(8,128)(2,1)S(1)} %rest.3.refs_0_), channel_id=1, source_target_pairs={{0,1},{1,0},{2,3},{3,2},{4,5},{5,4},{6,7},{7,6},{8,9},{9,8},{10,11... | collective-permute-start | bytes 786440 | tf_op jit(solution)/shard_map/ppermute | solution.py:56
  72.9 1.5 %collective-permute-start.25 = (bf16[512,256]{1,0:T(8,128)(2,1)S(1)}, bf16[512,256]{1,0:T(8,128)(2,1)S(1)}, u32[]{:S(2)}, u32[]{:S(2)}) collective-permute-start(bf16[512,256]{1,0:T(8,128)(2,1)S(1)} %collective-permute-done.23.refs_4_.refs_1_), channel_id=1, source_target_pairs={{0,1},{1,0},{2,3},{3,2},{4,5},{5,4},{6,7},{7,6},{8,9},{9,8},{10,11... | collective-permute-start | bytes 786440 | tf_op jit(solution)/shard_map/ppermute | solution.py:56
  (5 other events, 44.4 us)

commit v17 on v12

--- a/solution.py
+++ b/solution.py
@@ -563,7 +563,6 @@
     )(*pieces, w_t, w_k, select, f_col)
     if slabs == 8:
         lined = [summ] + [by_distance(summ, d) for d in (2, 4, 6)]
-        comp, *lined = lax.optimization_barrier((comp, *lined))
     comp_before = to_next(comp)
 
     q_t, v_t, keys, near_k, near_vt = pl.pallas_call(

time: 79.9 us -> 74.8 us (0.936)
  the two profiles are of different devices: /device:TPU:9 before, /device:TPU:0 now
where the time goes in v17:
time: 74.8 us; the launch traced here: 74.4 us
  starting transfers between devices  26.5 us (35%)
  Pallas kernels  25.1 us (34%)
  waiting for transfers between devices  22.6 us (30%)
    ppermute x15, waiting for transfers between devices, over_head(): return lax.ppermute(block, 'head', pairs)  12.7 us
    ppermute x5, starting transfers between devices, by_core(): return lax.ppermute(block, ('seq', 'head'), pairs)  9.51 us
    ppermute x15, starting transfers between devices, over_head(): return lax.ppermute(block, 'head', pairs)  7.32 us
    ppermute x5, waiting for transfers between devices, by_core(): return lax.ppermute(block, ('seq', 'head'), pairs)  7.28 us
    ppermute x4, starting transfers between devices, by_distance(): lax.ppermute(block, 'seq', [(i, i ^ distance) for i in range(lax.axis_siz...  6.59 us
    pallas_call x2, Pallas kernels, local(): pl.pallas_call(functools.partial(rest_kernel, first, count), out_shape=sh...  6.32 us
    pallas_call x1, Pallas kernels, local(): pl.pallas_call(own_kernel, out_shape=(shape((group, tok_rows), F32), shap...  3.99 us
    ppermute x1, starting transfers between devices, to_next(): lax.ppermute(block, 'seq', [(i, i + 1) for i in range(lax.axis_size('seq'...  3.04 us
  transfers between devices with their start and end apart: 25, of which 10 were waited for; matrix products, arithmetic and copies ran while one was open for 0% of the time, Pallas kernels for 20%

profile of v17, /device:TPU:0, one launch (start us, length us, event | category | flops | bytes accessed | tf_op | source)
XLA Modules:
  0.0 74.4 jit_solution(2264308586188329085)
XLA Ops:
  0.0 2.7 %send.1 = (bf16[144,512]{1,0:T(8,128)(2,1)}, bf16[144,512]{1,0:T(8,128)(2,1)}, bf16[144,512]{1,0:T(8,128)(2,1)}, bf16[144,512]{1,0:T(8,128)(2,1)}, bf16[144,512]{1,0:T(8,128)(2,1)}, /*index=5*/bf16[128,1024]{1,0:T(8,128)(2,1)}) custom-call(bf16[1024,1024]{1,0:T(8,128)(2,1)} %tokens_ref.1, s32[1,512]{1,0:T(1,128)} %mask_ref.3), custom_call_target="tpu_custom_call" | custom-call | flops 1 | bytes 1 | tf_op jit(solution)/shard_map/send/pallas_call | solution.py:134
  2.7 6.0 %collective-permute-start = (bf16[144,512]{1,0:T(8,128)(2,1)}, bf16[144,512]{1,0:T(8,128)(2,1)S(1)}, u32[]{:S(2)}, u32[]{:S(2)}) collective-permute-start(bf16[144,512]{1,0:T(8,128)(2,1)} %get-tuple-element.52), channel_id=1, source_target_pairs={{0,28},{1,25},{2,30},{3,27},{4,24},{5,29},{6,26},{7,31},{8,20},{9,... | collective-permute-start | bytes 442376 | tf_op jit(solution)/shard_map/ppermute | solution.py:113
  8.8 2.0 %collective-permute-start.3 = (bf16[144,512]{1,0:T(8,128)(2,1)}, bf16[144,512]{1,0:T(8,128)(2,1)S(1)}, u32[]{:S(2)}, u32[]{:S(2)}) collective-permute-start(bf16[144,512]{1,0:T(8,128)(2,1)} %get-tuple-element.58), channel_id=1, source_target_pairs={{0,8},{1,9},{2,10},{3,11},{4,12},{5,13},{6,14},{7,15},{8,0},{9,1},... | collective-permute-start | bytes 442376 | tf_op jit(solution)/shard_map/ppermute | solution.py:113
  10.7 1.5 %collective-permute-start.4 = (bf16[144,512]{1,0:T(8,128)(2,1)}, bf16[144,512]{1,0:T(8,128)(2,1)S(1)}, u32[]{:S(2)}, u32[]{:S(2)}) collective-permute-start(bf16[144,512]{1,0:T(8,128)(2,1)} %get-tuple-element.59), channel_id=1, source_target_pairs={{0,4},{1,5},{2,6},{3,7},{4,0},{5,1},{6,2},{7,3},{8,12},{9,13},{10,... | collective-permute-start | bytes 442376 | tf_op jit(solution)/shard_map/ppermute | solution.py:113
  12.3 2.5 %prepare.1 = (bf16[1024,1024]{1,0:T(8,128)(2,1)S(1)}, bf16[1024,1024]{1,0:T(8,128)(2,1)S(1)}, bf16[672,1024]{1,0:T(8,128)(2,1)S(1)}, f32[160,128]{1,0:T(8,128)S(...) custom-call(s32[1,1024]{1,0:T(1,128)S(1)} %copy-done.8, ...), custom_call_target="tpu_custom_call" | custom-call | flops 1 | bytes 1 | tf_op jit(solution)/shard_map/prepare/pallas_call | solution.py:512
  14.8 4.8 %collective-permute-done.2.refs_1_.refs_2_.refs_8_ = bf16[144,512]{1,0:T(8,128)(2,1)S(1)} collective-permute-done((bf16[144,512]{1,0:T(8,128)(2,1)}, bf16[144,512]{1,0:T(8,128)(2,1)S(1)}, u32[]{:S(2)}, u32[]{:S(2)}) %collective-permute-start.2) | collective-permute-done | bytes 147488 | tf_op jit(solution)/shard_map/ppermute | solution.py:113
  19.6 2.4 %collective-permute-done.3.refs_2_.refs_9_ = bf16[144,512]{1,0:T(8,128)(2,1)S(1)} collective-permute-done((bf16[144,512]{1,0:T(8,128)(2,1)}, bf16[144,512]{1,0:T(8,128)(2,1)S(1)}, u32[]{:S(2)}, u32[]{:S(2)}) %collective-permute-start.3) | collective-permute-done | bytes 147488 | tf_op jit(solution)/shard_map/ppermute | solution.py:113
  22.1 1.6 %collective-permute-start.5 = (bf16[128,512]{1,0:T(8,128)(2,1)S(1)}, bf16[128,512]{1,0:T(8,128)(2,1)S(1)}, u32[]{:S(2)}, u32[]{:S(2)}) collective-permute-start(bf16[128,512]{1,0:T(8,128)(2,1)S(1)} %stack.3), channel_id=1, source_target_pairs={{0,2},{2,0},{1,3},{3,1},{4,6},{6,4},{5,7},{7,5},{8,10},{10,8},{9,1... | collective-permute-start | bytes 393224 | tf_op jit(solution)/shard_map/ppermute | solution.py:56
  23.6 0.5 collective-permute-start.11
  24.2 3.0 %collective-permute-done.5.refs_2_ = bf16[128,512]{1,0:T(8,128)(2,1)S(1)} collective-permute-done((bf16[128,512]{1,0:T(8,128)(2,1)S(1)}, bf16[128,512]{1,0:T(8,128)(2,1)S(1)}, u32[]{:S(2)}, u32[]{:S(2)}) %collective-permute-start.5) | collective-permute-done | bytes 131104 | tf_op jit(solution)/shard_map/ppermute | solution.py:56
  27.1 1.6 %collective-permute-start.6 = (bf16[128,512]{1,0:T(8,128)(2,1)S(1)}, bf16[128,512]{1,0:T(8,128)(2,1)S(1)}, u32[]{:S(2)}, u32[]{:S(2)}) collective-permute-start(bf16[128,512]{1,0:T(8,128)(2,1)S(1)} %stack.4.refs_1_), channel_id=1, source_target_pairs={{0,2},{2,0},{1,3},{3,1},{4,6},{6,4},{5,7},{7,5},{8,10},{10,8},{9,1... | collective-permute-start | bytes 393224 | tf_op jit(solution)/shard_map/ppermute | solution.py:56
  29.2 1.2 %expand.1 = (bf16[1024,512]{1,0:T(8,128)(2,1)S(1)}, bf16[512,1024]{1,0:T(8,128)(2,1)S(1)}, f32[2048,128]{1,0:T(8,128)S(1)}) custom-call(f32[1024,128]{1,0:T(8,128)S(1)} %get-tuple-element.53.seen_ref, bf16[144,512]{1,0:T(8,128)(2,1)S(1)} %collective-permute-done.refs_0_, bf16[144,512]{1,0:T(8,128)(2,1)S(1)} %collective-permute-done.7.refs_1_.refs_4_, ...), custom_call_target="tpu_custom_call" | custom-call | flops 1 | bytes 1 | tf_op jit(solution)/shard_map/expand/pallas_call | solution.py:532
  30.4 1.7 %collective-permute-done.6.refs_3_ = bf16[128,512]{1,0:T(8,128)(2,1)S(1)} collective-permute-done((bf16[128,512]{1,0:T(8,128)(2,1)S(1)}, bf16[128,512]{1,0:T(8,128)(2,1)S(1)}, u32[]{:S(2)}, u32[]{:S(2)}) %collective-permute-start.6) | collective-permute-done | bytes 131104 | tf_op jit(solution)/shard_map/ppermute | solution.py:56
  32.2 0.5 collective-permute-start.10
  32.7 0.8 %collective-permute-done.9.refs_6_ = bf16[128,512]{1,0:T(8,128)(2,1)S(1)} collective-permute-done((bf16[128,512]{1,0:T(8,128)(2,1)S(1)}, bf16[128,512]{1,0:T(8,128)(2,1)S(1)}, u32[]{:S(2)}, u32[]{:S(2)}) %collective-permute-start.9) | collective-permute-done | bytes 131104 | tf_op jit(solution)/shard_map/ppermute | solution.py:56
  33.7 2.1 %project.1 = (bf16[1024,256]{1,0:T(8,128)(2,1)S(1)}, bf16[48,256]{1,0:T(8,128)(2,1)S(1)}, bf16[1024,256]{1,0:T(8,128)(2,1)S(1)}, bf16[256,1024]{1,0:T(8,128)(2,1)S(1)}, bf16[1024,1024]{1,0:T(8,128)(2,1)S(1)}) custom-call(bf16[144,512]{1,0:T(8,128)(2,1)S(1)} %collective-permute-done.refs_0_, bf16[128,512]{1,0:T(8,128)(2,1)S(1)} %stack.4.refs_1_, ...), custom_call_target="tpu_custom_call" | custom-call | flops 1 | bytes 1 | tf_op jit(solution)/shard_map/project/pallas_call | solution.py:549
  35.8 3.0 %collective-permute-start.14 = (bf16[1024,256]{1,0:T(8,128)(2,1)S(1)}, bf16[1024,256]{1,0:T(8,128)(2,1)S(1)}, u32[]{:S(2)}, u32[]{:S(2)}) collective-permute-start(bf16[1024,256]{1,0:T(8,128)(2,1)S(1)} %get-tuple-element.73), channel_id=1, source_target_pairs={{0,4},{4,8},{8,12},{12,16},{16,20},{20,24},{24,28},{1,5},{5,9},{9,... | collective-permute-start | bytes 1572872 | tf_op jit(solution)/shard_map/ppermute | solution.py:60
  38.9 1.9 %collective-permute-start.17 = (bf16[48,256]{1,0:T(8,128)(2,1)S(1)}, bf16[48,256]{1,0:T(8,128)(2,1)S(1)}, u32[]{:S(2)}, u32[]{:S(2)}) collective-permute-start(bf16[48,256]{1,0:T(8,128)(2,1)S(1)} %get-tuple-element.74.refs_0_), channel_id=1, source_target_pairs={{0,24},{4,28},{8,16},{12,20},{16,8},{20,12},{24,0},{28,4},{1,25},{... | collective-permute-start | bytes 73736 | tf_op jit(solution)/shard_map/ppermute | solution.py:103
  40.8 2.5 %collective-permute-start.15 = (bf16[48,256]{1,0:T(8,128)(2,1)S(1)}, bf16[48,256]{1,0:T(8,128)(2,1)S(1)}, u32[]{:S(2)}, u32[]{:S(2)}) collective-permute-start(bf16[48,256]{1,0:T(8,128)(2,1)S(1)} %get-tuple-element.74.refs_0_), channel_id=1, source_target_pairs={{0,8},{4,12},{8,0},{12,4},{16,24},{20,28},{24,16},{28,20},{1,9},{5... | collective-permute-start | bytes 73736 | tf_op jit(solution)/shard_map/ppermute | solution.py:103
  43.3 2.7 %order.1 = (bf16[256,1024]{1,0:T(8,128)(2,1)S(1)}, bf16[256,1024]{1,0:T(8,128)(2,1)S(1)}, bf16[1024,256]{1,0:T(8,128)(2,1)S(1)}, bf16[128,256]{1,0:T(8,128)(2,1)S(1)}, bf16[256,128]{1,0:T(8,128)(2,1)S(1)}) custom-call(bf16[1024,1024]{1,0:T(8,128)(2,1)S(1)} %get-tuple-element.46.p_ref, bf16[1024,1024]{1,0:T(8,128)(2,1)S(1)} %get-tuple-element.47.pt_ref, ...), custom_call_target="tpu_custom_call" | custom-call | flops 1 | bytes 1 | tf_op jit(solution)/shard_map/order/pallas_call | solution.py:568
  46.0 4.0 %own.1 = (f32[256,1024]{1,0:T(8,128)S(1)}, f32[256,1024]{1,0:T(8,128)S(1)}, f32[8,512]{1,0:T(8,128)S(1)}, f32[8,512]{1,0:T(8,128)S(1)}) custom-call(f32[4,4]{1,0:T(4,128)S(1)} %copy-done.5, bf16[256,1024]{1,0:T(8,128)(2,1)S(1)} %get-tuple-element.70.qt_ref, bf16[1024,256]{1,0:T(8,128)(2,1)S(1)} %get-tuple-element.71.k_ref, ...), custom_call_target="tpu_custom_call" | custom-call | flops 1 | bytes 1 | tf_op jit(solution)/shard_map/own/pallas_call | solution.py:584
  50.1 2.1 %collective-permute-start.18 = (bf16[192,256]{1,0:T(8,128)(2,1)S(1)}, bf16[192,256]{1,0:T(8,128)(2,1)S(1)}, u32[]{:S(2)}, u32[]{:S(2)}) collective-permute-start(bf16[192,256]{1,0:T(8,128)(2,1)S(1)} %stack.5.refs_0_), channel_id=1, source_target_pairs={{0,4},{4,0},{8,12},{12,8},{16,20},{20,16},{24,28},{28,24},{1,5},{5... | collective-permute-start | bytes 294920 | tf_op jit(solution)/shard_map/ppermute | solution.py:103
  52.2 2.6 %collective-permute-done.18.refs_1_ = bf16[192,256]{1,0:T(8,128)(2,1)S(1)} collective-permute-done((bf16[192,256]{1,0:T(8,128)(2,1)S(1)}, bf16[192,256]{1,0:T(8,128)(2,1)S(1)}, u32[]{:S(2)}, u32[]{:S(2)}) %collective-permute-start.18) | collective-permute-done | bytes 98336 | tf_op jit(solution)/shard_map/ppermute | solution.py:103
  54.8 0.9 %window.1 = (bf16[2048,256]{1,0:T(8,128)(2,1)S(1)}, bf16[256,2048]{1,0:T(8,128)(2,1)S(1)}, bf16[64,256]{1,0:T(8,128)(2,1)S(1)}, bf16[256,64]{1,0:T(8,128)(2,1)S(1)}) custom-call(bf16[1024,256]{1,0:T(8,128)(2,1)S(1)} %get-tuple-element.71.k_ref, bf16[256,1024]{1,0:T(8,128)(2,1)S(1)} %get-tuple-element.72.vt_ref, ...), custom_call_target="tpu_custom_call" | custom-call | flops 1 | bytes 1 | tf_op jit(solution)/shard_map/window/pallas_call | solution.py:612
  55.8 3.2 %rest.2.refs_0_ = bf16[512,256]{1,0:T(8,128)(2,1)S(1)} custom-call(s32[4,8]{1,0:T(4,128)S(1)} %bitcast.1, f32[4,4]{1,0:T(4,128)S(1)} %copy-done.5, bf16[256,1024]{1,0:T(8,128)(2,1)S(1)} %get-tuple-element.70.qt_ref, bf16[2048,256]{1,0:T(8,128)(2,1)S(1)} %get-tuple-element.78.kw_ref, bf16[256,2048]{1,0:T(8,128)(2,1)S(1)} %get-tuple-element.79.vw_ref, ...), custom_call_target="tpu_custom_call" | custom-call | flops 1 | bytes 1 | tf_op jit(solution)/shard_map/rest/pallas_call | solution.py:654
  58.9 1.5 %collective-permute-start.19 = (bf16[512,256]{1,0:T(8,128)(2,1)S(1)}, bf16[512,256]{1,0:T(8,128)(2,1)S(1)}, u32[]{:S(2)}, u32[]{:S(2)}) collective-permute-start(bf16[512,256]{1,0:T(8,128)(2,1)S(1)} %rest.2.refs_0_), channel_id=1, source_target_pairs={{0,2},{2,0},{1,3},{3,1},{4,6},{6,4},{5,7},{7,5},{8,10},{10,8},{9,1... | collective-permute-start | bytes 786440 | tf_op jit(solution)/shard_map/ppermute | solution.py:56
  60.5 3.2 %rest.3.refs_0_ = bf16[512,256]{1,0:T(8,128)(2,1)S(1)} custom-call(s32[4,8]{1,0:T(4,128)S(1)} %bitcast.2, f32[4,4]{1,0:T(4,128)S(1)} %copy-done.5, bf16[256,1024]{1,0:T(8,128)(2,1)S(1)} %get-tuple-element.70.qt_ref, bf16[2048,256]{1,0:T(8,128)(2,1)S(1)} %get-tuple-element.78.kw_ref, bf16[256,2048]{1,0:T(8,128)(2,1)S(1)} %get-tuple-element.79.vw_ref, ...), custom_call_target="tpu_custom_call" | custom-call | flops 1 | bytes 1 | tf_op jit(solution)/shard_map/rest/pallas_call | solution.py:654
  63.6 0.6 collective-permute-start.20
  64.3 2.9 %collective-permute-done.19.refs_1_ = bf16[512,256]{1,0:T(8,128)(2,1)S(1)} collective-permute-done((bf16[512,256]{1,0:T(8,128)(2,1)S(1)}, bf16[512,256]{1,0:T(8,128)(2,1)S(1)}, u32[]{:S(2)}, u32[]{:S(2)}) %collective-permute-start.19) | collective-permute-done | bytes 262176 | tf_op jit(solution)/shard_map/ppermute | solution.py:56
  67.7 3.9 %collective-permute-done.20.refs_4_.refs_1_ = bf16[512,256]{1,0:T(8,128)(2,1)S(1)} collective-permute-done((bf16[512,256]{1,0:T(8,128)(2,1)S(1)}, bf16[512,256]{1,0:T(8,128)(2,1)S(1)}, u32[]{:S(2)}, u32[]{:S(2)}) %collective-permute-start.20) | collective-permute-done | bytes 262176 | tf_op jit(solution)/shard_map/ppermute | solution.py:56
  71.6 1.3 %output.2.refs_4_ = bf16[1024,256]{1,0:T(8,128)(2,1)} custom-call(bf16[1024,256]{1,0:T(8,128)(2,1)S(1)} %copy-done, bf16[512,256]{1,0:T(8,128)(2,1)S(1)} %rest.2.refs_0_, bf16[512,256]{1,0:T(8,128)(2,1)S(1)} %collective-permute-done.19.refs_1_, bf16[512,256]{1,0:T(8,128)(2,1)S(1)} %collective-permute-done.23.refs_2_, ...), custom_call_target="tpu_custom_call" | custom-call | flops 1 | bytes 1 | tf_op jit(solution)/shard_map/output/pallas_call | solution.py:639
  73.1 1.3 %output.3 = bf16[1024,256]{1,0:T(8,128)(2,1)} custom-call(bf16[1024,256]{1,0:T(8,128)(2,1)S(1)} %copy-done, bf16[512,256]{1,0:T(8,128)(2,1)S(1)} %rest.3.refs_0_, bf16[512,256]{1,0:T(8,128)(2,1)S(1)} %collective-permute-done.20.refs_4_.refs_1_, bf16[512,256]{1,0:T(8,128)(2,1)S(1)} %collective-permute-done.21.refs_2_, ...), custom_call_target="tpu_custom_call", output_to_operand_aliasing={{}: (5, {})} | custom-call | flops 1 | bytes 1 | tf_op jit(solution)/shard_map/output/pallas_call | solution.py:639
  (50 shorter events, 1.5 us)
Async XLA Ops:
  0.0 12.3 %copy-start.6 = (s32[1,512]{1,0:T(1,128)S(1)}, s32[1,512]{1,0:T(1,128)}, u32[]{:S(2)}) copy-start(s32[1,512]{1,0:T(1,128)} %mask_ref.3) | copy-start | bytes 6148
  0.0 12.3 %copy-start.8 = (s32[1,1024]{1,0:T(1,128)S(1)}, s32[1,1024]{1,0:T(1,128)}, u32[]{:S(2)}) copy-start(s32[1,1024]{1,0:T(1,128)} %order_ref.1) | copy-start | bytes 12292
  0.0 12.3 %copy-start.2 = (bf16[1024,256]{1,0:T(8,128)(2,1)S(1)}, bf16[1024,256]{1,0:T(8,128)(2,1)}, u32[]{:S(2)}) copy-start(bf16[1024,256]{1,0:T(8,128)(2,1)} %wv_ref.1) | copy-start | bytes 1572868
  0.0 12.3 %copy-start.3 = (bf16[1024,256]{1,0:T(8,128)(2,1)S(1)}, bf16[1024,256]{1,0:T(8,128)(2,1)}, u32[]{:S(2)}) copy-start(bf16[1024,256]{1,0:T(8,128)(2,1)} %wk_in.1) | copy-start | bytes 1572868
  0.0 12.3 %copy-start.1 = (bf16[1024,256]{1,0:T(8,128)(2,1)S(1)}, bf16[1024,256]{1,0:T(8,128)(2,1)}, u32[]{:S(2)}) copy-start(bf16[1024,256]{1,0:T(8,128)(2,1)} %wq_ref.1) | copy-start | bytes 1572868
  2.7 31.0 %copy-start.4 = (bf16[128,1024]{1,0:T(8,128)(2,1)S(1)}, bf16[128,1024]{1,0:T(8,128)(2,1)}, u32[]{:S(2)}) copy-start(bf16[128,1024]{1,0:T(8,128)(2,1)} %get-tuple-element.66.refs_14_) | copy-start | bytes 786436
  2.7 12.0 %collective-permute-start = (bf16[144,512]{1,0:T(8,128)(2,1)}, bf16[144,512]{1,0:T(8,128)(2,1)S(1)}, u32[]{:S(2)}, u32[]{:S(2)}) collective-permute-start(bf16[144,512]{1,0:T(8,128)(2,1)} %get-tuple-element.52), channel_id=1, source_target_pairs={{0,28},{1,25},{2,30},{3,27},{4,24},{5,29},{6,26},{7,31},{8,20},{9,... | collective-permute-start | bytes 442376 | tf_op jit(solution)/shard_map/ppermute | solution.py:113
  8.8 10.9 %collective-permute-start.2 = (bf16[144,512]{1,0:T(8,128)(2,1)}, bf16[144,512]{1,0:T(8,128)(2,1)S(1)}, u32[]{:S(2)}, u32[]{:S(2)}) collective-permute-start(bf16[144,512]{1,0:T(8,128)(2,1)} %get-tuple-element.57), channel_id=1, source_target_pairs={{0,12},{1,13},{2,14},{3,15},{4,8},{5,9},{6,10},{7,11},{8,4},{9,5},... | collective-permute-start | bytes 442376 | tf_op jit(solution)/shard_map/ppermute | solution.py:113
  8.8 13.3 %collective-permute-start.3 = (bf16[144,512]{1,0:T(8,128)(2,1)}, bf16[144,512]{1,0:T(8,128)(2,1)S(1)}, u32[]{:S(2)}, u32[]{:S(2)}) collective-permute-start(bf16[144,512]{1,0:T(8,128)(2,1)} %get-tuple-element.58), channel_id=1, source_target_pairs={{0,8},{1,9},{2,10},{3,11},{4,12},{5,13},{6,14},{7,15},{8,0},{9,1},... | collective-permute-start | bytes 442376 | tf_op jit(solution)/shard_map/ppermute | solution.py:113
  10.7 11.3 %collective-permute-start.4 = (bf16[144,512]{1,0:T(8,128)(2,1)}, bf16[144,512]{1,0:T(8,128)(2,1)S(1)}, u32[]{:S(2)}, u32[]{:S(2)}) collective-permute-start(bf16[144,512]{1,0:T(8,128)(2,1)} %get-tuple-element.59), channel_id=1, source_target_pairs={{0,4},{1,5},{2,6},{3,7},{4,0},{5,1},{6,2},{7,3},{8,12},{9,13},{10,... | collective-permute-start | bytes 442376 | tf_op jit(solution)/shard_map/ppermute | solution.py:113
  12.3 11.9 %collective-permute-start.1 = (bf16[144,512]{1,0:T(8,128)(2,1)}, bf16[144,512]{1,0:T(8,128)(2,1)S(1)}, u32[]{:S(2)}, u32[]{:S(2)}) collective-permute-start(bf16[144,512]{1,0:T(8,128)(2,1)} %get-tuple-element.56), channel_id=1, source_target_pairs={{0,20},{1,17},{2,22},{3,19},{4,16},{5,21},{6,18},{7,23},{8,28},{9,... | collective-permute-start | bytes 442376 | tf_op jit(solution)/shard_map/ppermute | solution.py:113
  22.1 5.0 %collective-permute-start.5 = (bf16[128,512]{1,0:T(8,128)(2,1)S(1)}, bf16[128,512]{1,0:T(8,128)(2,1)S(1)}, u32[]{:S(2)}, u32[]{:S(2)}) collective-permute-start(bf16[128,512]{1,0:T(8,128)(2,1)S(1)} %stack.3), channel_id=1, source_target_pairs={{0,2},{2,0},{1,3},{3,1},{4,6},{6,4},{5,7},{7,5},{8,10},{10,8},{9,1... | collective-permute-start | bytes 393224 | tf_op jit(solution)/shard_map/ppermute | solution.py:56
  23.6 5.6 %collective-permute-start.7 = (bf16[144,512]{1,0:T(8,128)(2,1)S(1)}, bf16[144,512]{1,0:T(8,128)(2,1)S(1)}, u32[]{:S(2)}, u32[]{:S(2)}) collective-permute-start(bf16[144,512]{1,0:T(8,128)(2,1)S(1)} %collective-permute-done.refs_0_), channel_id=1, source_target_pairs={{0,1},{1,0},{2,3},{3,2},{4,5},{5,4},{6,7},{7,6},{8,9},{9,8},{10,11... | collective-permute-start | bytes 442376 | tf_op jit(solution)/shard_map/ppermute | solution.py:56
  23.6 8.5 %collective-permute-start.11 = (bf16[144,512]{1,0:T(8,128)(2,1)S(1)}, bf16[144,512]{1,0:T(8,128)(2,1)S(1)}, u32[]{:S(2)}, u32[]{:S(2)}) collective-permute-start(bf16[144,512]{1,0:T(8,128)(2,1)S(1)} %collective-permute-done.2.refs_1_.refs_2_.refs_8_), channel_id=1, source_target_pairs={{0,1},{1,0},{2,3},{3,2},{4,5},{5,4},{6,7},{7,6},{8,9},{9,8},{10,11... | collective-permute-start | bytes 442376 | tf_op jit(solution)/shard_map/ppermute | solution.py:56
  27.1 5.0 %collective-permute-start.6 = (bf16[128,512]{1,0:T(8,128)(2,1)S(1)}, bf16[128,512]{1,0:T(8,128)(2,1)S(1)}, u32[]{:S(2)}, u32[]{:S(2)}) collective-permute-start(bf16[128,512]{1,0:T(8,128)(2,1)S(1)} %stack.4.refs_1_), channel_id=1, source_target_pairs={{0,2},{2,0},{1,3},{3,1},{4,6},{6,4},{5,7},{7,5},{8,10},{10,8},{9,1... | collective-permute-start | bytes 393224 | tf_op jit(solution)/shard_map/ppermute | solution.py:56
  28.7 4.0 %collective-permute-start.12 = (bf16[144,512]{1,0:T(8,128)(2,1)S(1)}, bf16[144,512]{1,0:T(8,128)(2,1)S(1)}, u32[]{:S(2)}, u32[]{:S(2)}) collective-permute-start(bf16[144,512]{1,0:T(8,128)(2,1)S(1)} %collective-permute-done.3.refs_2_.refs_9_), channel_id=1, source_target_pairs={{0,1},{1,0},{2,3},{3,2},{4,5},{5,4},{6,7},{7,6},{8,9},{9,8},{10,11... | collective-permute-start | bytes 442376 | tf_op jit(solution)/shard_map/ppermute | solution.py:56
  28.7 4.0 %collective-permute-start.13 = (bf16[144,512]{1,0:T(8,128)(2,1)S(1)}, bf16[144,512]{1,0:T(8,128)(2,1)S(1)}, u32[]{:S(2)}, u32[]{:S(2)}) collective-permute-start(bf16[144,512]{1,0:T(8,128)(2,1)S(1)} %collective-permute-done.4.refs_3_.refs_10_), channel_id=1, source_target_pairs={{0,1},{1,0},{2,3},{3,2},{4,5},{5,4},{6,7},{7,6},{8,9},{9,8},{10,11... | collective-permute-start | bytes 442376 | tf_op jit(solution)/shard_map/ppermute | solution.py:56
  29.2 3.5 %collective-permute-start.8 = (bf16[128,512]{1,0:T(8,128)(2,1)S(1)}, bf16[128,512]{1,0:T(8,128)(2,1)S(1)}, u32[]{:S(2)}, u32[]{:S(2)}) collective-permute-start(bf16[128,512]{1,0:T(8,128)(2,1)S(1)} %stack.4.refs_1_), channel_id=1, source_target_pairs={{0,1},{1,0},{2,3},{3,2},{4,5},{5,4},{6,7},{7,6},{8,9},{9,8},{10,11... | collective-permute-start | bytes 393224 | tf_op jit(solution)/shard_map/ppermute | solution.py:56
  32.2 1.3 %collective-permute-start.9 = (bf16[128,512]{1,0:T(8,128)(2,1)S(1)}, bf16[128,512]{1,0:T(8,128)(2,1)S(1)}, u32[]{:S(2)}, u32[]{:S(2)}) collective-permute-start(bf16[128,512]{1,0:T(8,128)(2,1)S(1)} %collective-permute-done.5.refs_2_), channel_id=1, source_target_pairs={{0,1},{1,0},{2,3},{3,2},{4,5},{5,4},{6,7},{7,6},{8,9},{9,8},{10,11... | collective-permute-start | bytes 393224 | tf_op jit(solution)/shard_map/ppermute | solution.py:56
  32.2 1.5 %collective-permute-start.10 = (bf16[128,512]{1,0:T(8,128)(2,1)S(1)}, bf16[128,512]{1,0:T(8,128)(2,1)S(1)}, u32[]{:S(2)}, u32[]{:S(2)}) collective-permute-start(bf16[128,512]{1,0:T(8,128)(2,1)S(1)} %collective-permute-done.6.refs_3_), channel_id=1, source_target_pairs={{0,1},{1,0},{2,3},{3,2},{4,5},{5,4},{6,7},{7,6},{8,9},{9,8},{10,11... | collective-permute-start | bytes 393224 | tf_op jit(solution)/shard_map/ppermute | solution.py:56
  35.8 19.0 %collective-permute-start.14 = (bf16[1024,256]{1,0:T(8,128)(2,1)S(1)}, bf16[1024,256]{1,0:T(8,128)(2,1)S(1)}, u32[]{:S(2)}, u32[]{:S(2)}) collective-permute-start(bf16[1024,256]{1,0:T(8,128)(2,1)S(1)} %get-tuple-element.73), channel_id=1, source_target_pairs={{0,4},{4,8},{8,12},{12,16},{16,20},{20,24},{24,28},{1,5},{5,9},{9,... | collective-permute-start | bytes 1572872 | tf_op jit(solution)/shard_map/ppermute | solution.py:60
  38.9 11.1 %collective-permute-start.17 = (bf16[48,256]{1,0:T(8,128)(2,1)S(1)}, bf16[48,256]{1,0:T(8,128)(2,1)S(1)}, u32[]{:S(2)}, u32[]{:S(2)}) collective-permute-start(bf16[48,256]{1,0:T(8,128)(2,1)S(1)} %get-tuple-element.74.refs_0_), channel_id=1, source_target_pairs={{0,24},{4,28},{8,16},{12,20},{16,8},{20,12},{24,0},{28,4},{1,25},{... | collective-permute-start | bytes 73736 | tf_op jit(solution)/shard_map/ppermute | solution.py:103
  40.8 9.2 %collective-permute-start.16 = (bf16[48,256]{1,0:T(8,128)(2,1)S(1)}, bf16[48,256]{1,0:T(8,128)(2,1)S(1)}, u32[]{:S(2)}, u32[]{:S(2)}) collective-permute-start(bf16[48,256]{1,0:T(8,128)(2,1)S(1)} %get-tuple-element.74.refs_0_), channel_id=1, source_target_pairs={{0,16},{4,20},{8,24},{12,28},{16,0},{20,4},{24,8},{28,12},{1,17},{... | collective-permute-start | bytes 73736 | tf_op jit(solution)/shard_map/ppermute | solution.py:103
  40.8 9.2 %collective-permute-start.15 = (bf16[48,256]{1,0:T(8,128)(2,1)S(1)}, bf16[48,256]{1,0:T(8,128)(2,1)S(1)}, u32[]{:S(2)}, u32[]{:S(2)}) collective-permute-start(bf16[48,256]{1,0:T(8,128)(2,1)S(1)} %get-tuple-element.74.refs_0_), channel_id=1, source_target_pairs={{0,8},{4,12},{8,0},{12,4},{16,24},{20,28},{24,16},{28,20},{1,9},{5... | collective-permute-start | bytes 73736 | tf_op jit(solution)/shard_map/ppermute | solution.py:103
  50.1 4.7 %collective-permute-start.18 = (bf16[192,256]{1,0:T(8,128)(2,1)S(1)}, bf16[192,256]{1,0:T(8,128)(2,1)S(1)}, u32[]{:S(2)}, u32[]{:S(2)}) collective-permute-start(bf16[192,256]{1,0:T(8,128)(2,1)S(1)} %stack.5.refs_0_), channel_id=1, source_target_pairs={{0,4},{4,0},{8,12},{12,8},{16,20},{20,16},{24,28},{28,24},{1,5},{5... | collective-permute-start | bytes 294920 | tf_op jit(solution)/shard_map/ppermute | solution.py:103
  58.9 12.7 %copy-start = (bf16[1024,256]{1,0:T(8,128)(2,1)S(1)}, bf16[1024,256]{1,0:T(8,128)(2,1)}, u32[]{:S(2)}) copy-start(bf16[1024,256]{1,0:T(8,128)(2,1)} %w_ref.3) | copy-start | bytes 1572868
  58.9 8.2 %collective-permute-start.19 = (bf16[512,256]{1,0:T(8,128)(2,1)S(1)}, bf16[512,256]{1,0:T(8,128)(2,1)S(1)}, u32[]{:S(2)}, u32[]{:S(2)}) collective-permute-start(bf16[512,256]{1,0:T(8,128)(2,1)S(1)} %rest.2.refs_0_), channel_id=1, source_target_pairs={{0,2},{2,0},{1,3},{3,1},{4,6},{6,4},{5,7},{7,5},{8,10},{10,8},{9,1... | collective-permute-start | bytes 786440 | tf_op jit(solution)/shard_map/ppermute | solution.py:56
  63.6 8.0 %collective-permute-start.20 = (bf16[512,256]{1,0:T(8,128)(2,1)S(1)}, bf16[512,256]{1,0:T(8,128)(2,1)S(1)}, u32[]{:S(2)}, u32[]{:S(2)}) collective-permute-start(bf16[512,256]{1,0:T(8,128)(2,1)S(1)} %rest.3.refs_0_), channel_id=1, source_target_pairs={{0,2},{2,0},{1,3},{3,1},{4,6},{6,4},{5,7},{7,5},{8,10},{10,8},{9,1... | collective-permute-start | bytes 786440 | tf_op jit(solution)/shard_map/ppermute | solution.py:56
  64.3 7.3 %collective-permute-start.23 = (bf16[512,256]{1,0:T(8,128)(2,1)S(1)}, bf16[512,256]{1,0:T(8,128)(2,1)S(1)}, u32[]{:S(2)}, u32[]{:S(2)}) collective-permute-start(bf16[512,256]{1,0:T(8,128)(2,1)S(1)} %rest.2.refs_0_), channel_id=1, source_target_pairs={{0,1},{1,0},{2,3},{3,2},{4,5},{5,4},{6,7},{7,6},{8,9},{9,8},{10,11... | collective-permute-start | bytes 786440 | tf_op jit(solution)/shard_map/ppermute | solution.py:56
  67.2 4.4 %collective-permute-start.24 = (bf16[512,256]{1,0:T(8,128)(2,1)S(1)}, bf16[512,256]{1,0:T(8,128)(2,1)S(1)}, u32[]{:S(2)}, u32[]{:S(2)}) collective-permute-start(bf16[512,256]{1,0:T(8,128)(2,1)S(1)} %collective-permute-done.19.refs_1_), channel_id=1, source_target_pairs={{0,1},{1,0},{2,3},{3,2},{4,5},{5,4},{6,7},{7,6},{8,9},{9,8},{10,11... | collective-permute-start | bytes 786440 | tf_op jit(solution)/shard_map/ppermute | solution.py:56
  67.2 5.8 %collective-permute-start.21 = (bf16[512,256]{1,0:T(8,128)(2,1)S(1)}, bf16[512,256]{1,0:T(8,128)(2,1)S(1)}, u32[]{:S(2)}, u32[]{:S(2)}) collective-permute-start(bf16[512,256]{1,0:T(8,128)(2,1)S(1)} %rest.3.refs_0_), channel_id=1, source_target_pairs={{0,1},{1,0},{2,3},{3,2},{4,5},{5,4},{6,7},{7,6},{8,9},{9,8},{10,11... | collective-permute-start | bytes 786440 | tf_op jit(solution)/shard_map/ppermute | solution.py:56
  71.6 1.5 %collective-permute-start.22 = (bf16[512,256]{1,0:T(8,128)(2,1)S(1)}, bf16[512,256]{1,0:T(8,128)(2,1)S(1)}, u32[]{:S(2)}, u32[]{:S(2)}) collective-permute-start(bf16[512,256]{1,0:T(8,128)(2,1)S(1)} %collective-permute-done.20.refs_4_.refs_1_), channel_id=1, source_target_pairs={{0,1},{1,0},{2,3},{3,2},{4,5},{5,4},{6,7},{7,6},{8,9},{9,8},{10,11... | collective-permute-start | bytes 786440 | tf_op jit(solution)/shard_map/ppermute | solution.py:56
  (2 other events, 8.4 us)

commit v18 on v17

--- a/solution.py
+++ b/solution.py
@@ -143,7 +143,7 @@
         ),
         in_specs=vmem_specs(2),
         out_specs=vmem_specs(6),
-        compiler_params=pltpu.CompilerParams(vmem_limit_bytes=60 * 1024 * 1024),
+        compiler_params=pltpu.CompilerParams(vmem_limit_bytes=VMEM_LIMIT),
         cost_estimate=COST,
         name="send",
     )(tokens, mask_ids)

time: 74.8 us -> 74.6 us (level)
  Pallas kernels: 25.1 us -> 22.4 us
  local copies, waits for them, and re-layouts: 0.04 us -> 2.31 us
    pallas_call x1, Pallas kernels: 2.73 us -> 0.07 us  [exchange_tokens(): pl.pallas_call(send_kernel, out_shape=(jax.ShapeDtypeStruct((tall, half),...]
    unnamed x18 -> x20, local copies, waits for them, and re-layouts: 0.04 us -> 2.31 us
where the time goes in v18:
time: 74.6 us; the launch traced here: 74.5 us
  starting transfers between devices  26.5 us (36%)
  waiting for transfers between devices  23 us (31%)
  Pallas kernels  22.4 us (30%)
  local copies, waits for them, and re-layouts  2.31 us (3%)
    ppermute x15, waiting for transfers between devices, over_head(): return lax.ppermute(block, 'head', pairs)  13.2 us
    ppermute x5, starting transfers between devices, by_core(): return lax.ppermute(block, ('seq', 'head'), pairs)  9.56 us
    ppermute x15, starting transfers between devices, over_head(): return lax.ppermute(block, 'head', pairs)  7.32 us
    ppermute x5, waiting for transfers between devices, by_core(): return lax.ppermute(block, ('seq', 'head'), pairs)  7.06 us
    ppermute x4, starting transfers between devices, by_distance(): lax.ppermute(block, 'seq', [(i, i ^ distance) for i in range(lax.axis_siz...  6.59 us
    pallas_call x2, Pallas kernels, local(): pl.pallas_call(functools.partial(rest_kernel, first, count), out_shape=sh...  6.32 us
    pallas_call x1, Pallas kernels, local(): pl.pallas_call(own_kernel, out_shape=(shape((group, tok_rows), F32), shap...  3.99 us
    ppermute x1, starting transfers between devices, to_next(): lax.ppermute(block, 'seq', [(i, i + 1) for i in range(lax.axis_size('seq'...  3.04 us
  transfers between devices with their start and end apart: 25, of which 10 were waited for; matrix products, arithmetic and copies ran while one was open for 0% of the time, Pallas kernels for 20%

profile of v18, /device:TPU:0, one launch (start us, length us, event | category | flops | bytes accessed | tf_op | source)
XLA Modules:
  0.0 74.5 jit_solution(12766973256008597299)
XLA Ops:
  0.0 1.6 %copy-done = bf16[1024,1024]{1,0:T(8,128)(2,1)S(1)} copy-done((bf16[1024,1024]{1,0:T(8,128)(2,1)S(1)}, bf16[1024,1024]{1,0:T(8,128)(2,1)}, u32[]{:S(2)}) %copy-start) | copy-done | bytes 2097176
  1.6 0.7 copy-done.6
  2.4 6.1 %collective-permute-start = (bf16[144,512]{1,0:T(8,128)(2,1)S(1)}, bf16[144,512]{1,0:T(8,128)(2,1)S(1)}, u32[]{:S(2)}, u32[]{:S(2)}) collective-permute-start(bf16[144,512]{1,0:T(8,128)(2,1)S(1)} %get-tuple-element.52), channel_id=1, source_target_pairs={{0,28},{1,25},{2,30},{3,27},{4,24},{5,29},{6,26},{7,31},{8,20},{9,... | collective-permute-start | bytes 442376 | tf_op jit(solution)/shard_map/ppermute | solution.py:113
  8.5 2.0 %collective-permute-start.3 = (bf16[144,512]{1,0:T(8,128)(2,1)S(1)}, bf16[144,512]{1,0:T(8,128)(2,1)S(1)}, u32[]{:S(2)}, u32[]{:S(2)}) collective-permute-start(bf16[144,512]{1,0:T(8,128)(2,1)S(1)} %get-tuple-element.58), channel_id=1, source_target_pairs={{0,8},{1,9},{2,10},{3,11},{4,12},{5,13},{6,14},{7,15},{8,0},{9,1},... | collective-permute-start | bytes 442376 | tf_op jit(solution)/shard_map/ppermute | solution.py:113
  10.4 1.5 %collective-permute-start.4 = (bf16[144,512]{1,0:T(8,128)(2,1)S(1)}, bf16[144,512]{1,0:T(8,128)(2,1)S(1)}, u32[]{:S(2)}, u32[]{:S(2)}) collective-permute-start(bf16[144,512]{1,0:T(8,128)(2,1)S(1)} %get-tuple-element.59), channel_id=1, source_target_pairs={{0,4},{1,5},{2,6},{3,7},{4,0},{5,1},{6,2},{7,3},{8,12},{9,13},{10,... | collective-permute-start | bytes 442376 | tf_op jit(solution)/shard_map/ppermute | solution.py:113
  12.0 2.5 %prepare.1 = (bf16[1024,1024]{1,0:T(8,128)(2,1)S(1)}, bf16[1024,1024]{1,0:T(8,128)(2,1)S(1)}, bf16[672,1024]{1,0:T(8,128)(2,1)S(1)}, f32[160,128]{1,0:T(8,128)S(...) custom-call(s32[1,1024]{1,0:T(1,128)S(1)} %copy-done.9, ...), custom_call_target="tpu_custom_call" | custom-call | flops 1 | bytes 1 | tf_op jit(solution)/shard_map/prepare/pallas_call | solution.py:512
  14.5 4.6 %collective-permute-done.2.refs_1_.refs_2_.refs_8_ = bf16[144,512]{1,0:T(8,128)(2,1)S(1)} collective-permute-done((bf16[144,512]{1,0:T(8,128)(2,1)S(1)}, bf16[144,512]{1,0:T(8,128)(2,1)S(1)}, u32[]{:S(2)}, u32[]{:S(2)}) %collective-permute-start.2) | collective-permute-done | bytes 147488 | tf_op jit(solution)/shard_map/ppermute | solution.py:113
  19.1 2.4 %collective-permute-done.3.refs_2_.refs_9_ = bf16[144,512]{1,0:T(8,128)(2,1)S(1)} collective-permute-done((bf16[144,512]{1,0:T(8,128)(2,1)S(1)}, bf16[144,512]{1,0:T(8,128)(2,1)S(1)}, u32[]{:S(2)}, u32[]{:S(2)}) %collective-permute-start.3) | collective-permute-done | bytes 147488 | tf_op jit(solution)/shard_map/ppermute | solution.py:113
  21.6 1.6 %collective-permute-start.5 = (bf16[128,512]{1,0:T(8,128)(2,1)S(1)}, bf16[128,512]{1,0:T(8,128)(2,1)S(1)}, u32[]{:S(2)}, u32[]{:S(2)}) collective-permute-start(bf16[128,512]{1,0:T(8,128)(2,1)S(1)} %stack.3), channel_id=1, source_target_pairs={{0,2},{2,0},{1,3},{3,1},{4,6},{6,4},{5,7},{7,5},{8,10},{10,8},{9,1... | collective-permute-start | bytes 393224 | tf_op jit(solution)/shard_map/ppermute | solution.py:56
  23.6 3.0 %collective-permute-done.5.refs_2_ = bf16[128,512]{1,0:T(8,128)(2,1)S(1)} collective-permute-done((bf16[128,512]{1,0:T(8,128)(2,1)S(1)}, bf16[128,512]{1,0:T(8,128)(2,1)S(1)}, u32[]{:S(2)}, u32[]{:S(2)}) %collective-permute-start.5) | collective-permute-done | bytes 131104 | tf_op jit(solution)/shard_map/ppermute | solution.py:56
  26.6 1.6 %collective-permute-start.6 = (bf16[128,512]{1,0:T(8,128)(2,1)S(1)}, bf16[128,512]{1,0:T(8,128)(2,1)S(1)}, u32[]{:S(2)}, u32[]{:S(2)}) collective-permute-start(bf16[128,512]{1,0:T(8,128)(2,1)S(1)} %stack.4.refs_1_), channel_id=1, source_target_pairs={{0,2},{2,0},{1,3},{3,1},{4,6},{6,4},{5,7},{7,5},{8,10},{10,8},{9,1... | collective-permute-start | bytes 393224 | tf_op jit(solution)/shard_map/ppermute | solution.py:56
  28.7 1.2 %expand.1 = (bf16[1024,512]{1,0:T(8,128)(2,1)S(1)}, bf16[512,1024]{1,0:T(8,128)(2,1)S(1)}, f32[2048,128]{1,0:T(8,128)S(1)}) custom-call(f32[1024,128]{1,0:T(8,128)S(1)} %get-tuple-element.53.seen_ref, bf16[144,512]{1,0:T(8,128)(2,1)S(1)} %collective-permute-done.refs_0_, bf16[144,512]{1,0:T(8,128)(2,1)S(1)} %collective-permute-done.7.refs_1_.refs_4_, ...), custom_call_target="tpu_custom_call" | custom-call | flops 1 | bytes 1 | tf_op jit(solution)/shard_map/expand/pallas_call | solution.py:532
  29.9 1.7 %collective-permute-done.6.refs_3_ = bf16[128,512]{1,0:T(8,128)(2,1)S(1)} collective-permute-done((bf16[128,512]{1,0:T(8,128)(2,1)S(1)}, bf16[128,512]{1,0:T(8,128)(2,1)S(1)}, u32[]{:S(2)}, u32[]{:S(2)}) %collective-permute-start.6) | collective-permute-done | bytes 131104 | tf_op jit(solution)/shard_map/ppermute | solution.py:56
  31.6 0.5 collective-permute-start.10
  32.2 0.8 %collective-permute-done.9.refs_6_ = bf16[128,512]{1,0:T(8,128)(2,1)S(1)} collective-permute-done((bf16[128,512]{1,0:T(8,128)(2,1)S(1)}, bf16[128,512]{1,0:T(8,128)(2,1)S(1)}, u32[]{:S(2)}, u32[]{:S(2)}) %collective-permute-start.9) | collective-permute-done | bytes 131104 | tf_op jit(solution)/shard_map/ppermute | solution.py:56
  33.2 2.1 %project.1 = (bf16[1024,256]{1,0:T(8,128)(2,1)S(1)}, bf16[48,256]{1,0:T(8,128)(2,1)S(1)}, bf16[1024,256]{1,0:T(8,128)(2,1)S(1)}, bf16[256,1024]{1,0:T(8,128)(2,1)S(1)}, bf16[1024,1024]{1,0:T(8,128)(2,1)S(1)}) custom-call(bf16[144,512]{1,0:T(8,128)(2,1)S(1)} %collective-permute-done.refs_0_, bf16[128,512]{1,0:T(8,128)(2,1)S(1)} %stack.4.refs_1_, ...), custom_call_target="tpu_custom_call" | custom-call | flops 1 | bytes 1 | tf_op jit(solution)/shard_map/project/pallas_call | solution.py:549
  35.3 3.0 %collective-permute-start.14 = (bf16[1024,256]{1,0:T(8,128)(2,1)S(1)}, bf16[1024,256]{1,0:T(8,128)(2,1)S(1)}, u32[]{:S(2)}, u32[]{:S(2)}) collective-permute-start(bf16[1024,256]{1,0:T(8,128)(2,1)S(1)} %get-tuple-element.73), channel_id=1, source_target_pairs={{0,4},{4,8},{8,12},{12,16},{16,20},{20,24},{24,28},{1,5},{5,9},{9,... | collective-permute-start | bytes 1572872 | tf_op jit(solution)/shard_map/ppermute | solution.py:60
  38.3 1.9 %collective-permute-start.17 = (bf16[48,256]{1,0:T(8,128)(2,1)S(1)}, bf16[48,256]{1,0:T(8,128)(2,1)S(1)}, u32[]{:S(2)}, u32[]{:S(2)}) collective-permute-start(bf16[48,256]{1,0:T(8,128)(2,1)S(1)} %get-tuple-element.74.refs_0_), channel_id=1, source_target_pairs={{0,24},{4,28},{8,16},{12,20},{16,8},{20,12},{24,0},{28,4},{1,25},{... | collective-permute-start | bytes 73736 | tf_op jit(solution)/shard_map/ppermute | solution.py:103
  40.3 2.5 %collective-permute-start.15 = (bf16[48,256]{1,0:T(8,128)(2,1)S(1)}, bf16[48,256]{1,0:T(8,128)(2,1)S(1)}, u32[]{:S(2)}, u32[]{:S(2)}) collective-permute-start(bf16[48,256]{1,0:T(8,128)(2,1)S(1)} %get-tuple-element.74.refs_0_), channel_id=1, source_target_pairs={{0,8},{4,12},{8,0},{12,4},{16,24},{20,28},{24,16},{28,20},{1,9},{5... | collective-permute-start | bytes 73736 | tf_op jit(solution)/shard_map/ppermute | solution.py:103
  42.8 2.7 %order.1 = (bf16[256,1024]{1,0:T(8,128)(2,1)S(1)}, bf16[256,1024]{1,0:T(8,128)(2,1)S(1)}, bf16[1024,256]{1,0:T(8,128)(2,1)S(1)}, bf16[128,256]{1,0:T(8,128)(2,1)S(1)}, bf16[256,128]{1,0:T(8,128)(2,1)S(1)}) custom-call(bf16[1024,1024]{1,0:T(8,128)(2,1)S(1)} %get-tuple-element.46.p_ref, bf16[1024,1024]{1,0:T(8,128)(2,1)S(1)} %get-tuple-element.47.pt_ref, ...), custom_call_target="tpu_custom_call" | custom-call | flops 1 | bytes 1 | tf_op jit(solution)/shard_map/order/pallas_call | solution.py:568
  45.5 4.0 %own.1 = (f32[256,1024]{1,0:T(8,128)S(1)}, f32[256,1024]{1,0:T(8,128)S(1)}, f32[8,512]{1,0:T(8,128)S(1)}, f32[8,512]{1,0:T(8,128)S(1)}) custom-call(f32[4,4]{1,0:T(4,128)S(1)} %copy-done.5, bf16[256,1024]{1,0:T(8,128)(2,1)S(1)} %get-tuple-element.70.qt_ref, bf16[1024,256]{1,0:T(8,128)(2,1)S(1)} %get-tuple-element.71.k_ref, ...), custom_call_target="tpu_custom_call" | custom-call | flops 1 | bytes 1 | tf_op jit(solution)/shard_map/own/pallas_call | solution.py:584
  49.5 2.1 %collective-permute-start.18 = (bf16[192,256]{1,0:T(8,128)(2,1)S(1)}, bf16[192,256]{1,0:T(8,128)(2,1)S(1)}, u32[]{:S(2)}, u32[]{:S(2)}) collective-permute-start(bf16[192,256]{1,0:T(8,128)(2,1)S(1)} %stack.5.refs_0_), channel_id=1, source_target_pairs={{0,4},{4,0},{8,12},{12,8},{16,20},{20,16},{24,28},{28,24},{1,5},{5... | collective-permute-start | bytes 294920 | tf_op jit(solution)/shard_map/ppermute | solution.py:103
  51.7 2.7 %collective-permute-done.18.refs_1_ = bf16[192,256]{1,0:T(8,128)(2,1)S(1)} collective-permute-done((bf16[192,256]{1,0:T(8,128)(2,1)S(1)}, bf16[192,256]{1,0:T(8,128)(2,1)S(1)}, u32[]{:S(2)}, u32[]{:S(2)}) %collective-permute-start.18) | collective-permute-done | bytes 98336 | tf_op jit(solution)/shard_map/ppermute | solution.py:103
  54.4 0.9 %window.1 = (bf16[2048,256]{1,0:T(8,128)(2,1)S(1)}, bf16[256,2048]{1,0:T(8,128)(2,1)S(1)}, bf16[64,256]{1,0:T(8,128)(2,1)S(1)}, bf16[256,64]{1,0:T(8,128)(2,1)S(1)}) custom-call(bf16[1024,256]{1,0:T(8,128)(2,1)S(1)} %get-tuple-element.71.k_ref, bf16[256,1024]{1,0:T(8,128)(2,1)S(1)} %get-tuple-element.72.vt_ref, ...), custom_call_target="tpu_custom_call" | custom-call | flops 1 | bytes 1 | tf_op jit(solution)/shard_map/window/pallas_call | solution.py:612
  55.4 3.2 %rest.2.refs_0_ = bf16[512,256]{1,0:T(8,128)(2,1)S(1)} custom-call(s32[4,8]{1,0:T(4,128)S(1)} %bitcast.1, f32[4,4]{1,0:T(4,128)S(1)} %copy-done.5, bf16[256,1024]{1,0:T(8,128)(2,1)S(1)} %get-tuple-element.70.qt_ref, bf16[2048,256]{1,0:T(8,128)(2,1)S(1)} %get-tuple-element.78.kw_ref, bf16[256,2048]{1,0:T(8,128)(2,1)S(1)} %get-tuple-element.79.vw_ref, ...), custom_call_target="tpu_custom_call" | custom-call | flops 1 | bytes 1 | tf_op jit(solution)/shard_map/rest/pallas_call | solution.py:654
  58.5 1.5 %collective-permute-start.19 = (bf16[512,256]{1,0:T(8,128)(2,1)S(1)}, bf16[512,256]{1,0:T(8,128)(2,1)S(1)}, u32[]{:S(2)}, u32[]{:S(2)}) collective-permute-start(bf16[512,256]{1,0:T(8,128)(2,1)S(1)} %rest.2.refs_0_), channel_id=1, source_target_pairs={{0,2},{2,0},{1,3},{3,1},{4,6},{6,4},{5,7},{7,5},{8,10},{10,8},{9,1... | collective-permute-start | bytes 786440 | tf_op jit(solution)/shard_map/ppermute | solution.py:56
  60.0 3.2 %rest.3.refs_0_ = bf16[512,256]{1,0:T(8,128)(2,1)S(1)} custom-call(s32[4,8]{1,0:T(4,128)S(1)} %bitcast.2, f32[4,4]{1,0:T(4,128)S(1)} %copy-done.5, bf16[256,1024]{1,0:T(8,128)(2,1)S(1)} %get-tuple-element.70.qt_ref, bf16[2048,256]{1,0:T(8,128)(2,1)S(1)} %get-tuple-element.78.kw_ref, bf16[256,2048]{1,0:T(8,128)(2,1)S(1)} %get-tuple-element.79.vw_ref, ...), custom_call_target="tpu_custom_call" | custom-call | flops 1 | bytes 1 | tf_op jit(solution)/shard_map/rest/pallas_call | solution.py:654
  63.2 0.7 collective-permute-start.20
  63.9 3.4 %collective-permute-done.19.refs_1_ = bf16[512,256]{1,0:T(8,128)(2,1)S(1)} collective-permute-done((bf16[512,256]{1,0:T(8,128)(2,1)S(1)}, bf16[512,256]{1,0:T(8,128)(2,1)S(1)}, u32[]{:S(2)}, u32[]{:S(2)}) %collective-permute-start.19) | collective-permute-done | bytes 262176 | tf_op jit(solution)/shard_map/ppermute | solution.py:56
  67.7 3.9 %collective-permute-done.20.refs_4_.refs_1_ = bf16[512,256]{1,0:T(8,128)(2,1)S(1)} collective-permute-done((bf16[512,256]{1,0:T(8,128)(2,1)S(1)}, bf16[512,256]{1,0:T(8,128)(2,1)S(1)}, u32[]{:S(2)}, u32[]{:S(2)}) %collective-permute-start.20) | collective-permute-done | bytes 262176 | tf_op jit(solution)/shard_map/ppermute | solution.py:56
  71.7 1.3 %output.2.refs_4_ = bf16[1024,256]{1,0:T(8,128)(2,1)} custom-call(bf16[1024,256]{1,0:T(8,128)(2,1)S(1)} %copy-done.1, bf16[512,256]{1,0:T(8,128)(2,1)S(1)} %rest.2.refs_0_, bf16[512,256]{1,0:T(8,128)(2,1)S(1)} %collective-permute-done.19.refs_1_, bf16[512,256]{1,0:T(8,128)(2,1)S(1)} %collective-permute-done.23.refs_2_, ...), custom_call_target="tpu_custom_call" | custom-call | flops 1 | bytes 1 | tf_op jit(solution)/shard_map/output/pallas_call | solution.py:639
  73.2 1.3 %output.3 = bf16[1024,256]{1,0:T(8,128)(2,1)} custom-call(bf16[1024,256]{1,0:T(8,128)(2,1)S(1)} %copy-done.1, bf16[512,256]{1,0:T(8,128)(2,1)S(1)} %rest.3.refs_0_, bf16[512,256]{1,0:T(8,128)(2,1)S(1)} %collective-permute-done.20.refs_4_.refs_1_, bf16[512,256]{1,0:T(8,128)(2,1)S(1)} %collective-permute-done.21.refs_2_, ...), custom_call_target="tpu_custom_call", output_to_operand_aliasing={{}: (5, {})} | custom-call | flops 1 | bytes 1 | tf_op jit(solution)/shard_map/output/pallas_call | solution.py:639
  (52 shorter events, 2.1 us)
Async XLA Ops:
  2.3 9.7 %copy-start.2 = (bf16[1024,256]{1,0:T(8,128)(2,1)S(1)}, bf16[1024,256]{1,0:T(8,128)(2,1)}, u32[]{:S(2)}) copy-start(bf16[1024,256]{1,0:T(8,128)(2,1)} %wq_ref.1) | copy-start | bytes 1572868
  2.3 9.7 %copy-start.3 = (bf16[1024,256]{1,0:T(8,128)(2,1)S(1)}, bf16[1024,256]{1,0:T(8,128)(2,1)}, u32[]{:S(2)}) copy-start(bf16[1024,256]{1,0:T(8,128)(2,1)} %wv_ref.1) | copy-start | bytes 1572868
  2.3 9.7 %copy-start.4 = (bf16[1024,256]{1,0:T(8,128)(2,1)S(1)}, bf16[1024,256]{1,0:T(8,128)(2,1)}, u32[]{:S(2)}) copy-start(bf16[1024,256]{1,0:T(8,128)(2,1)} %wk_in.1) | copy-start | bytes 1572868
  2.3 9.7 %copy-start.7 = (s32[1,512]{1,0:T(1,128)S(1)}, s32[1,512]{1,0:T(1,128)}, u32[]{:S(2)}) copy-start(s32[1,512]{1,0:T(1,128)} %mask_ref.3) | copy-start | bytes 6148
  2.3 9.7 %copy-start.9 = (s32[1,1024]{1,0:T(1,128)S(1)}, s32[1,1024]{1,0:T(1,128)}, u32[]{:S(2)}) copy-start(s32[1,1024]{1,0:T(1,128)} %order_ref.1) | copy-start | bytes 12292
  2.4 12.1 %collective-permute-start = (bf16[144,512]{1,0:T(8,128)(2,1)S(1)}, bf16[144,512]{1,0:T(8,128)(2,1)S(1)}, u32[]{:S(2)}, u32[]{:S(2)}) collective-permute-start(bf16[144,512]{1,0:T(8,128)(2,1)S(1)} %get-tuple-element.52), channel_id=1, source_target_pairs={{0,28},{1,25},{2,30},{3,27},{4,24},{5,29},{6,26},{7,31},{8,20},{9,... | collective-permute-start | bytes 442376 | tf_op jit(solution)/shard_map/ppermute | solution.py:113
  8.4 10.7 %collective-permute-start.2 = (bf16[144,512]{1,0:T(8,128)(2,1)S(1)}, bf16[144,512]{1,0:T(8,128)(2,1)S(1)}, u32[]{:S(2)}, u32[]{:S(2)}) collective-permute-start(bf16[144,512]{1,0:T(8,128)(2,1)S(1)} %get-tuple-element.57), channel_id=1, source_target_pairs={{0,12},{1,13},{2,14},{3,15},{4,8},{5,9},{6,10},{7,11},{8,4},{9,5},... | collective-permute-start | bytes 442376 | tf_op jit(solution)/shard_map/ppermute | solution.py:113
  8.5 13.1 %collective-permute-start.3 = (bf16[144,512]{1,0:T(8,128)(2,1)S(1)}, bf16[144,512]{1,0:T(8,128)(2,1)S(1)}, u32[]{:S(2)}, u32[]{:S(2)}) collective-permute-start(bf16[144,512]{1,0:T(8,128)(2,1)S(1)} %get-tuple-element.58), channel_id=1, source_target_pairs={{0,8},{1,9},{2,10},{3,11},{4,12},{5,13},{6,14},{7,15},{8,0},{9,1},... | collective-permute-start | bytes 442376 | tf_op jit(solution)/shard_map/ppermute | solution.py:113
  10.4 11.1 %collective-permute-start.4 = (bf16[144,512]{1,0:T(8,128)(2,1)S(1)}, bf16[144,512]{1,0:T(8,128)(2,1)S(1)}, u32[]{:S(2)}, u32[]{:S(2)}) collective-permute-start(bf16[144,512]{1,0:T(8,128)(2,1)S(1)} %get-tuple-element.59), channel_id=1, source_target_pairs={{0,4},{1,5},{2,6},{3,7},{4,0},{5,1},{6,2},{7,3},{8,12},{9,13},{10,... | collective-permute-start | bytes 442376 | tf_op jit(solution)/shard_map/ppermute | solution.py:113
  11.9 11.7 %collective-permute-start.1 = (bf16[144,512]{1,0:T(8,128)(2,1)S(1)}, bf16[144,512]{1,0:T(8,128)(2,1)S(1)}, u32[]{:S(2)}, u32[]{:S(2)}) collective-permute-start(bf16[144,512]{1,0:T(8,128)(2,1)S(1)} %get-tuple-element.56), channel_id=1, source_target_pairs={{0,20},{1,17},{2,22},{3,19},{4,16},{5,21},{6,18},{7,23},{8,28},{9,... | collective-permute-start | bytes 442376 | tf_op jit(solution)/shard_map/ppermute | solution.py:113
  21.6 5.0 %collective-permute-start.5 = (bf16[128,512]{1,0:T(8,128)(2,1)S(1)}, bf16[128,512]{1,0:T(8,128)(2,1)S(1)}, u32[]{:S(2)}, u32[]{:S(2)}) collective-permute-start(bf16[128,512]{1,0:T(8,128)(2,1)S(1)} %stack.3), channel_id=1, source_target_pairs={{0,2},{2,0},{1,3},{3,1},{4,6},{6,4},{5,7},{7,5},{8,10},{10,8},{9,1... | collective-permute-start | bytes 393224 | tf_op jit(solution)/shard_map/ppermute | solution.py:56
  23.1 5.6 %collective-permute-start.7 = (bf16[144,512]{1,0:T(8,128)(2,1)S(1)}, bf16[144,512]{1,0:T(8,128)(2,1)S(1)}, u32[]{:S(2)}, u32[]{:S(2)}) collective-permute-start(bf16[144,512]{1,0:T(8,128)(2,1)S(1)} %collective-permute-done.refs_0_), channel_id=1, source_target_pairs={{0,1},{1,0},{2,3},{3,2},{4,5},{5,4},{6,7},{7,6},{8,9},{9,8},{10,11... | collective-permute-start | bytes 442376 | tf_op jit(solution)/shard_map/ppermute | solution.py:56
  23.1 8.5 %collective-permute-start.11 = (bf16[144,512]{1,0:T(8,128)(2,1)S(1)}, bf16[144,512]{1,0:T(8,128)(2,1)S(1)}, u32[]{:S(2)}, u32[]{:S(2)}) collective-permute-start(bf16[144,512]{1,0:T(8,128)(2,1)S(1)} %collective-permute-done.2.refs_1_.refs_2_.refs_8_), channel_id=1, source_target_pairs={{0,1},{1,0},{2,3},{3,2},{4,5},{5,4},{6,7},{7,6},{8,9},{9,8},{10,11... | collective-permute-start | bytes 442376 | tf_op jit(solution)/shard_map/ppermute | solution.py:56
  26.6 5.0 %collective-permute-start.6 = (bf16[128,512]{1,0:T(8,128)(2,1)S(1)}, bf16[128,512]{1,0:T(8,128)(2,1)S(1)}, u32[]{:S(2)}, u32[]{:S(2)}) collective-permute-start(bf16[128,512]{1,0:T(8,128)(2,1)S(1)} %stack.4.refs_1_), channel_id=1, source_target_pairs={{0,2},{2,0},{1,3},{3,1},{4,6},{6,4},{5,7},{7,5},{8,10},{10,8},{9,1... | collective-permute-start | bytes 393224 | tf_op jit(solution)/shard_map/ppermute | solution.py:56
  28.2 4.0 %collective-permute-start.12 = (bf16[144,512]{1,0:T(8,128)(2,1)S(1)}, bf16[144,512]{1,0:T(8,128)(2,1)S(1)}, u32[]{:S(2)}, u32[]{:S(2)}) collective-permute-start(bf16[144,512]{1,0:T(8,128)(2,1)S(1)} %collective-permute-done.3.refs_2_.refs_9_), channel_id=1, source_target_pairs={{0,1},{1,0},{2,3},{3,2},{4,5},{5,4},{6,7},{7,6},{8,9},{9,8},{10,11... | collective-permute-start | bytes 442376 | tf_op jit(solution)/shard_map/ppermute | solution.py:56
  28.2 4.0 %collective-permute-start.13 = (bf16[144,512]{1,0:T(8,128)(2,1)S(1)}, bf16[144,512]{1,0:T(8,128)(2,1)S(1)}, u32[]{:S(2)}, u32[]{:S(2)}) collective-permute-start(bf16[144,512]{1,0:T(8,128)(2,1)S(1)} %collective-permute-done.4.refs_3_.refs_10_), channel_id=1, source_target_pairs={{0,1},{1,0},{2,3},{3,2},{4,5},{5,4},{6,7},{7,6},{8,9},{9,8},{10,11... | collective-permute-start | bytes 442376 | tf_op jit(solution)/shard_map/ppermute | solution.py:56
  28.7 3.5 %collective-permute-start.8 = (bf16[128,512]{1,0:T(8,128)(2,1)S(1)}, bf16[128,512]{1,0:T(8,128)(2,1)S(1)}, u32[]{:S(2)}, u32[]{:S(2)}) collective-permute-start(bf16[128,512]{1,0:T(8,128)(2,1)S(1)} %stack.4.refs_1_), channel_id=1, source_target_pairs={{0,1},{1,0},{2,3},{3,2},{4,5},{5,4},{6,7},{7,6},{8,9},{9,8},{10,11... | collective-permute-start | bytes 393224 | tf_op jit(solution)/shard_map/ppermute | solution.py:56
  31.6 1.3 %collective-permute-start.9 = (bf16[128,512]{1,0:T(8,128)(2,1)S(1)}, bf16[128,512]{1,0:T(8,128)(2,1)S(1)}, u32[]{:S(2)}, u32[]{:S(2)}) collective-permute-start(bf16[128,512]{1,0:T(8,128)(2,1)S(1)} %collective-permute-done.5.refs_2_), channel_id=1, source_target_pairs={{0,1},{1,0},{2,3},{3,2},{4,5},{5,4},{6,7},{7,6},{8,9},{9,8},{10,11... | collective-permute-start | bytes 393224 | tf_op jit(solution)/shard_map/ppermute | solution.py:56
  31.6 1.5 %collective-permute-start.10 = (bf16[128,512]{1,0:T(8,128)(2,1)S(1)}, bf16[128,512]{1,0:T(8,128)(2,1)S(1)}, u32[]{:S(2)}, u32[]{:S(2)}) collective-permute-start(bf16[128,512]{1,0:T(8,128)(2,1)S(1)} %collective-permute-done.6.refs_3_), channel_id=1, source_target_pairs={{0,1},{1,0},{2,3},{3,2},{4,5},{5,4},{6,7},{7,6},{8,9},{9,8},{10,11... | collective-permute-start | bytes 393224 | tf_op jit(solution)/shard_map/ppermute | solution.py:56
  35.3 19.1 %collective-permute-start.14 = (bf16[1024,256]{1,0:T(8,128)(2,1)S(1)}, bf16[1024,256]{1,0:T(8,128)(2,1)S(1)}, u32[]{:S(2)}, u32[]{:S(2)}) collective-permute-start(bf16[1024,256]{1,0:T(8,128)(2,1)S(1)} %get-tuple-element.73), channel_id=1, source_target_pairs={{0,4},{4,8},{8,12},{12,16},{16,20},{20,24},{24,28},{1,5},{5,9},{9,... | collective-permute-start | bytes 1572872 | tf_op jit(solution)/shard_map/ppermute | solution.py:60
  38.3 11.1 %collective-permute-start.17 = (bf16[48,256]{1,0:T(8,128)(2,1)S(1)}, bf16[48,256]{1,0:T(8,128)(2,1)S(1)}, u32[]{:S(2)}, u32[]{:S(2)}) collective-permute-start(bf16[48,256]{1,0:T(8,128)(2,1)S(1)} %get-tuple-element.74.refs_0_), channel_id=1, source_target_pairs={{0,24},{4,28},{8,16},{12,20},{16,8},{20,12},{24,0},{28,4},{1,25},{... | collective-permute-start | bytes 73736 | tf_op jit(solution)/shard_map/ppermute | solution.py:103
  40.3 9.2 %collective-permute-start.16 = (bf16[48,256]{1,0:T(8,128)(2,1)S(1)}, bf16[48,256]{1,0:T(8,128)(2,1)S(1)}, u32[]{:S(2)}, u32[]{:S(2)}) collective-permute-start(bf16[48,256]{1,0:T(8,128)(2,1)S(1)} %get-tuple-element.74.refs_0_), channel_id=1, source_target_pairs={{0,16},{4,20},{8,24},{12,28},{16,0},{20,4},{24,8},{28,12},{1,17},{... | collective-permute-start | bytes 73736 | tf_op jit(solution)/shard_map/ppermute | solution.py:103
  40.3 9.2 %collective-permute-start.15 = (bf16[48,256]{1,0:T(8,128)(2,1)S(1)}, bf16[48,256]{1,0:T(8,128)(2,1)S(1)}, u32[]{:S(2)}, u32[]{:S(2)}) collective-permute-start(bf16[48,256]{1,0:T(8,128)(2,1)S(1)} %get-tuple-element.74.refs_0_), channel_id=1, source_target_pairs={{0,8},{4,12},{8,0},{12,4},{16,24},{20,28},{24,16},{28,20},{1,9},{5... | collective-permute-start | bytes 73736 | tf_op jit(solution)/shard_map/ppermute | solution.py:103
  49.5 5.9 %copy-start.8 = (s32[8,4]{0,1:T(4,128)S(1)}, s32[8,4]{0,1:T(4,128)}, u32[]{:S(2)}) copy-start(s32[8,4]{0,1:T(4,128)} %param.15) | copy-start | bytes 388
  49.5 4.9 %collective-permute-start.18 = (bf16[192,256]{1,0:T(8,128)(2,1)S(1)}, bf16[192,256]{1,0:T(8,128)(2,1)S(1)}, u32[]{:S(2)}, u32[]{:S(2)}) collective-permute-start(bf16[192,256]{1,0:T(8,128)(2,1)S(1)} %stack.5.refs_0_), channel_id=1, source_target_pairs={{0,4},{4,0},{8,12},{12,8},{16,20},{20,16},{24,28},{28,24},{1,5},{5... | collective-permute-start | bytes 294920 | tf_op jit(solution)/shard_map/ppermute | solution.py:103
  58.5 13.1 %copy-start.1 = (bf16[1024,256]{1,0:T(8,128)(2,1)S(1)}, bf16[1024,256]{1,0:T(8,128)(2,1)}, u32[]{:S(2)}) copy-start(bf16[1024,256]{1,0:T(8,128)(2,1)} %w_ref.3) | copy-start | bytes 1572868
  58.5 8.7 %collective-permute-start.19 = (bf16[512,256]{1,0:T(8,128)(2,1)S(1)}, bf16[512,256]{1,0:T(8,128)(2,1)S(1)}, u32[]{:S(2)}, u32[]{:S(2)}) collective-permute-start(bf16[512,256]{1,0:T(8,128)(2,1)S(1)} %rest.2.refs_0_), channel_id=1, source_target_pairs={{0,2},{2,0},{1,3},{3,1},{4,6},{6,4},{5,7},{7,5},{8,10},{10,8},{9,1... | collective-permute-start | bytes 786440 | tf_op jit(solution)/shard_map/ppermute | solution.py:56
  63.2 8.4 %collective-permute-start.20 = (bf16[512,256]{1,0:T(8,128)(2,1)S(1)}, bf16[512,256]{1,0:T(8,128)(2,1)S(1)}, u32[]{:S(2)}, u32[]{:S(2)}) collective-permute-start(bf16[512,256]{1,0:T(8,128)(2,1)S(1)} %rest.3.refs_0_), channel_id=1, source_target_pairs={{0,2},{2,0},{1,3},{3,1},{4,6},{6,4},{5,7},{7,5},{8,10},{10,8},{9,1... | collective-permute-start | bytes 786440 | tf_op jit(solution)/shard_map/ppermute | solution.py:56
  63.9 7.8 %collective-permute-start.23 = (bf16[512,256]{1,0:T(8,128)(2,1)S(1)}, bf16[512,256]{1,0:T(8,128)(2,1)S(1)}, u32[]{:S(2)}, u32[]{:S(2)}) collective-permute-start(bf16[512,256]{1,0:T(8,128)(2,1)S(1)} %rest.2.refs_0_), channel_id=1, source_target_pairs={{0,1},{1,0},{2,3},{3,2},{4,5},{5,4},{6,7},{7,6},{8,9},{9,8},{10,11... | collective-permute-start | bytes 786440 | tf_op jit(solution)/shard_map/ppermute | solution.py:56
  67.2 4.4 %collective-permute-start.24 = (bf16[512,256]{1,0:T(8,128)(2,1)S(1)}, bf16[512,256]{1,0:T(8,128)(2,1)S(1)}, u32[]{:S(2)}, u32[]{:S(2)}) collective-permute-start(bf16[512,256]{1,0:T(8,128)(2,1)S(1)} %collective-permute-done.19.refs_1_), channel_id=1, source_target_pairs={{0,1},{1,0},{2,3},{3,2},{4,5},{5,4},{6,7},{7,6},{8,9},{9,8},{10,11... | collective-permute-start | bytes 786440 | tf_op jit(solution)/shard_map/ppermute | solution.py:56
  67.2 5.7 %collective-permute-start.21 = (bf16[512,256]{1,0:T(8,128)(2,1)S(1)}, bf16[512,256]{1,0:T(8,128)(2,1)S(1)}, u32[]{:S(2)}, u32[]{:S(2)}) collective-permute-start(bf16[512,256]{1,0:T(8,128)(2,1)S(1)} %rest.3.refs_0_), channel_id=1, source_target_pairs={{0,1},{1,0},{2,3},{3,2},{4,5},{5,4},{6,7},{7,6},{8,9},{9,8},{10,11... | collective-permute-start | bytes 786440 | tf_op jit(solution)/shard_map/ppermute | solution.py:56
  71.6 1.5 %collective-permute-start.22 = (bf16[512,256]{1,0:T(8,128)(2,1)S(1)}, bf16[512,256]{1,0:T(8,128)(2,1)S(1)}, u32[]{:S(2)}, u32[]{:S(2)}) collective-permute-start(bf16[512,256]{1,0:T(8,128)(2,1)S(1)} %collective-permute-done.20.refs_4_.refs_1_), channel_id=1, source_target_pairs={{0,1},{1,0},{2,3},{3,2},{4,5},{5,4},{6,7},{7,6},{8,9},{9,8},{10,11... | collective-permute-start | bytes 786440 | tf_op jit(solution)/shard_map/ppermute | solution.py:56
  (3 other events, 4.9 us)
